TPU v7x, 32 devices: a whole 2x2x4 slice. The times are simulated.
32 devices in a mesh: grp: 4 (over x, core), row: 8 (over z, y).
Axes of the slice: x: 2, y: 2, z: 4, core: 2. Of those that a mesh axis runs over, the one named last changes fastest.
Arguments:
- tokens: bfloat16 [4, 2048, 768], P('grp', 'row'), may hold values from -6 to 6
- cont_lengths: int32 [4, 8], P('grp'), may hold values from 1 to 256, 1024 in all within a row
- cotangent: bfloat16 [4, 2048, 768], P('grp', 'row'), may hold values from -6 to 6
- w_query: bfloat16 [768, 768], P(('grp', 'row')), may hold values from -0.21875 to 0.21875
- w_key: bfloat16 [768, 768], P(('grp', 'row')), may hold values from -0.21875 to 0.21875
- w_value: bfloat16 [768, 768], P(('grp', 'row')), may hold values from -0.21875 to 0.21875
- w_output: bfloat16 [768, 768], P(('grp', 'row')), may hold values from -2.5 to 2.5
- w_inner: bfloat16 [768, 3072], P(('grp', 'row')), may hold values from -0.21875 to 0.21875
- w_outer: bfloat16 [3072, 768], P(('grp', 'row')), may hold values from -0.109375 to 0.109375
- bias_query: bfloat16 [768], P(('grp', 'row')), may hold values from -3 to 3
- bias_value: bfloat16 [768], P(('grp', 'row')), may hold values from -0.59765625 to 0.59765625
- bias_output: bfloat16 [768], P(('grp', 'row')), may hold values from -1.1953125 to 1.1953125
- gain_first: bfloat16 [768], P(('grp', 'row')), may hold values from 0.5 to 1.5
- shift_first: bfloat16 [768], P(('grp', 'row')), may hold values from -1.1953125 to 1.1953125
- bias_inner: bfloat16 [3072], P(('grp', 'row')), may hold values from -1.1953125 to 1.1953125
- bias_outer: bfloat16 [768], P(('grp', 'row')), may hold values from -1.1953125 to 1.1953125
- gain_second: bfloat16 [768], P(('grp', 'row')), may hold values from 0.5 to 1.5
- shift_second: bfloat16 [768], P(('grp', 'row')), may hold values from -1.1953125 to 1.1953125
Outputs:
- layer_out: bfloat16 [4, 2048, 768], P('grp', 'row')
- grad_tokens: bfloat16 [4, 2048, 768], P('grp', 'row')
- grad_w_query: float32 [768, 768], P(('grp', 'row'))
- grad_w_key: float32 [768, 768], P(('grp', 'row'))
- grad_w_value: float32 [768, 768], P(('grp', 'row'))
- grad_w_output: float32 [768, 768], P(('grp', 'row'))
- grad_w_inner: float32 [768, 3072], P(('grp', 'row'))
- grad_w_outer: float32 [3072, 768], P(('grp', 'row'))
- grad_bias_query: float32 [768], P(('grp', 'row'))
- grad_bias_value: float32 [768], P(('grp', 'row'))
- grad_bias_output: float32 [768], P(('grp', 'row'))
- grad_gain_first: float32 [768], P(('grp', 'row'))
- grad_shift_first: float32 [768], P(('grp', 'row'))
- grad_bias_inner: float32 [3072], P(('grp', 'row'))
- grad_bias_outer: float32 [768], P(('grp', 'row'))
- grad_gain_second: float32 [768], P(('grp', 'row'))
- grad_shift_second: float32 [768], P(('grp', 'row'))
Inputs may be any that keep to these rules, and one draw needn't show every extreme that they name: `cont_lengths`: each group's 8 lengths sum to 1024, and the longest of each group is 256.
All inputs are finite; a program needn't handle non-finite values.
Results may differ from a plain program's by a relative error of at most 0.017.
Values may be sent and summed in bfloat16 or wider, within the bound.
No kernel may reach another device: no remote copies, remote signals or barrier semaphores. Data moves between devices by JAX's collectives and lax.ppermute only.
A program may use at most 192 MiB of HBM per device.

v0:
```python
import jax
import jax.numpy as jnp
from jax import lax
from jax.sharding import PartitionSpec as P

HEADS = 12
HDIM = 64
PROMPT = 1024


NORM_EPS = 1e-12
MASK_FILL = -1000000000.0
SQRT_HALF = 0.7071067811865476
INV_ROOT_TAU = 0.3989422804014327


def contract_last(left, right):
    return lax.dot_general(
        left, right, (((1,), (1,)), ((), ())), preferred_element_type=jnp.float32
    )


def contract_rows(left, right):
    return lax.dot_general(
        left, right, (((0,), (0,)), ((), ())), preferred_element_type=jnp.float32
    )


def segment_ids(cont_lengths, prompt_len, group_len):
    ends = jnp.cumsum(cont_lengths, axis=-1)
    places = jnp.arange(group_len, dtype=jnp.int32)
    later = places - prompt_len
    passed = jnp.sum((later[None, :, None] >= ends[:, None, :]).astype(jnp.int32), axis=-1)
    return jnp.where(places[None, :] < prompt_len, 0, 1 + passed)


def norm_forward(hidden, norm_gain, norm_shift):
    average = jnp.mean(hidden, axis=-1, keepdims=True)
    centred = hidden - average
    inverse = lax.rsqrt(jnp.mean(centred * centred, axis=-1, keepdims=True) + NORM_EPS)
    normed = centred * inverse
    return (normed * norm_gain + norm_shift, normed, inverse)


def norm_backward(grad_out, norm_gain, normed, inverse):
    grad_norm = grad_out * norm_gain
    first_term = jnp.mean(grad_norm, axis=-1, keepdims=True)
    second_term = jnp.mean(grad_norm * normed, axis=-1, keepdims=True)
    return inverse * (grad_norm - first_term - normed * second_term)


def gelu_slope(pre_act):
    cumulative = 0.5 * (1.0 + jax.scipy.special.erf(pre_act * SQRT_HALF))
    return cumulative + pre_act * jnp.exp(-0.5 * pre_act * pre_act) * INV_ROOT_TAU


def split_heads(rows_in):
    return rows_in.reshape(rows_in.shape[0], HEADS, HDIM)


def masked_scores(heads_query, heads_key, seg_query, seg_key):
    scores = jnp.einsum("qhd,khd->hqk", heads_query, heads_key, preferred_element_type=jnp.float32)
    allowed = (seg_key[None, :] == 0) | (seg_key[None, :] == seg_query[:, None])
    return jnp.where(allowed[None, :, :], scores, MASK_FILL)


def attend(inputs):
    query_rows, key_rows, value_rows, seg_query, seg_key = inputs
    scores = masked_scores(split_heads(query_rows), split_heads(key_rows), seg_query, seg_key)
    row_peak = jnp.max(scores, axis=-1, keepdims=True)
    exp_scores = jnp.exp(scores - row_peak)
    row_total = jnp.sum(exp_scores, axis=-1, keepdims=True)
    shares_low = (exp_scores / row_total).astype(jnp.bfloat16)
    mixed = jnp.einsum(
        "hqk,khd->qhd", shares_low, split_heads(value_rows), preferred_element_type=jnp.float32
    )
    log_total = (row_peak + jnp.log(row_total))[..., 0]
    return (mixed.reshape(query_rows.shape[0], -1).astype(jnp.bfloat16), log_total)


def attend_back(inputs):
    query_rows, key_rows, value_rows, seg_query, seg_key, log_total, grad_context = inputs
    heads_query = split_heads(query_rows)
    heads_key = split_heads(key_rows)
    heads_value = split_heads(value_rows)
    heads_grad = split_heads(grad_context)
    scores = masked_scores(heads_query, heads_key, seg_query, seg_key)
    shares = jnp.exp(scores - log_total[..., None])
    shares_low = shares.astype(jnp.bfloat16)
    grad_shares = jnp.einsum(
        "qhd,khd->hqk", heads_grad, heads_value, preferred_element_type=jnp.float32
    )
    row_inner = jnp.sum(shares * grad_shares, axis=-1, keepdims=True)
    grad_scores = (shares * (grad_shares - row_inner)).astype(jnp.bfloat16)
    grad_queries = jnp.einsum(
        "hqk,khd->qhd", grad_scores, heads_key, preferred_element_type=jnp.float32
    )
    grad_keys = jnp.einsum(
        "hqk,qhd->khd", grad_scores, heads_query, preferred_element_type=jnp.float32
    )
    grad_values = jnp.einsum(
        "hqk,qhd->khd", shares_low, heads_grad, preferred_element_type=jnp.float32
    )
    return (
        grad_queries.reshape(query_rows.shape[0], -1),
        grad_keys.reshape(key_rows.shape[0], -1),
        grad_values.reshape(key_rows.shape[0], -1),
    )


def per_device(
    tokens,
    cont_lengths,
    cotangent,
    w_query,
    w_key,
    w_value,
    w_output,
    w_inner,
    w_outer,
    bias_query,
    bias_value,
    bias_output,
    gain_first,
    shift_first,
    bias_inner,
    bias_outer,
    gain_second,
    shift_second,
):
    forward_set = (
        lax.all_gather(w_query, ("grp", "row"), axis=0, tiled=True),
        lax.all_gather(w_key, ("grp", "row"), axis=0, tiled=True),
        lax.all_gather(w_value, ("grp", "row"), axis=0, tiled=True),
        lax.all_gather(w_output, ("grp", "row"), axis=0, tiled=True),
        lax.all_gather(w_inner, ("grp", "row"), axis=0, tiled=True),
        lax.all_gather(w_outer, ("grp", "row"), axis=0, tiled=True),
        lax.all_gather(bias_query, ("grp", "row"), axis=0, tiled=True),
        lax.all_gather(bias_value, ("grp", "row"), axis=0, tiled=True),
        lax.all_gather(bias_output, ("grp", "row"), axis=0, tiled=True),
        lax.all_gather(gain_first, ("grp", "row"), axis=0, tiled=True),
        lax.all_gather(shift_first, ("grp", "row"), axis=0, tiled=True),
        lax.all_gather(bias_inner, ("grp", "row"), axis=0, tiled=True),
        lax.all_gather(bias_outer, ("grp", "row"), axis=0, tiled=True),
        lax.all_gather(gain_second, ("grp", "row"), axis=0, tiled=True),
        lax.all_gather(shift_second, ("grp", "row"), axis=0, tiled=True),
    )
    (
        full_query,
        full_key,
        full_value,
        full_output,
        full_inner,
        full_outer,
        full_bias_query,
        full_bias_value,
        full_bias_output,
        full_gain_first,
        full_shift_first,
        full_bias_inner,
        full_bias_outer,
        full_gain_second,
        full_shift_second,
    ) = forward_set
    groups, rows, width = tokens.shape
    count = groups * rows
    scale = HDIM ** (-0.5)
    flat = tokens.reshape(count, width)
    queries = (
        (
            jnp.dot(flat, full_query, preferred_element_type=jnp.float32)
            + full_bias_query.astype(jnp.float32)
        )
        * scale
    ).astype(jnp.bfloat16)
    key_rows = jnp.dot(flat, full_key, preferred_element_type=jnp.float32).astype(jnp.bfloat16)
    value_rows = (
        jnp.dot(flat, full_value, preferred_element_type=jnp.float32)
        + full_bias_value.astype(jnp.float32)
    ).astype(jnp.bfloat16)
    key_all, value_all = (
        lax.all_gather(key_rows.reshape(groups, rows, width), "row", axis=1, tiled=True),
        lax.all_gather(value_rows.reshape(groups, rows, width), "row", axis=1, tiled=True),
    )
    group_len = key_all.shape[1]
    seg_all = segment_ids(cont_lengths, PROMPT, group_len)
    start = lax.axis_index("row") * rows
    seg_own = lax.dynamic_slice_in_dim(seg_all, start, rows, 1)
    query_groups = queries.reshape(groups, rows, width)
    context, log_total = lax.map(attend, (query_groups, key_all, value_all, seg_own, seg_all))
    context_flat = context.reshape(count, width)
    attn_out = jnp.dot(
        context_flat, full_output, preferred_element_type=jnp.float32
    ) + full_bias_output.astype(jnp.float32)
    first, normed_one, inverse_one = norm_forward(
        flat.astype(jnp.float32) + attn_out,
        full_gain_first.astype(jnp.float32),
        full_shift_first.astype(jnp.float32),
    )
    first_low = first.astype(jnp.bfloat16)
    pre_act = jnp.dot(
        first_low, full_inner, preferred_element_type=jnp.float32
    ) + full_bias_inner.astype(jnp.float32)
    activation = jax.nn.gelu(pre_act, approximate=False).astype(jnp.bfloat16)
    ffn_out = jnp.dot(
        activation, full_outer, preferred_element_type=jnp.float32
    ) + full_bias_outer.astype(jnp.float32)
    second, normed_two, inverse_two = norm_forward(
        first + ffn_out, full_gain_second.astype(jnp.float32), full_shift_second.astype(jnp.float32)
    )
    layer_out = second.astype(jnp.bfloat16).reshape(groups, rows, width)
    backward_set = (
        lax.all_gather(w_query, ("grp", "row"), axis=0, tiled=True),
        lax.all_gather(w_key, ("grp", "row"), axis=0, tiled=True),
        lax.all_gather(w_value, ("grp", "row"), axis=0, tiled=True),
        lax.all_gather(w_output, ("grp", "row"), axis=0, tiled=True),
        lax.all_gather(w_inner, ("grp", "row"), axis=0, tiled=True),
        lax.all_gather(w_outer, ("grp", "row"), axis=0, tiled=True),
        lax.all_gather(bias_query, ("grp", "row"), axis=0, tiled=True),
        lax.all_gather(bias_value, ("grp", "row"), axis=0, tiled=True),
        lax.all_gather(bias_output, ("grp", "row"), axis=0, tiled=True),
        lax.all_gather(gain_first, ("grp", "row"), axis=0, tiled=True),
        lax.all_gather(shift_first, ("grp", "row"), axis=0, tiled=True),
        lax.all_gather(bias_inner, ("grp", "row"), axis=0, tiled=True),
        lax.all_gather(bias_outer, ("grp", "row"), axis=0, tiled=True),
        lax.all_gather(gain_second, ("grp", "row"), axis=0, tiled=True),
        lax.all_gather(shift_second, ("grp", "row"), axis=0, tiled=True),
    )
    back_query, back_key, back_value, back_output, back_inner, back_outer = backward_set[:6]
    back_gain_first = backward_set[9].astype(jnp.float32)
    back_gain_second = backward_set[13].astype(jnp.float32)
    grad_out = cotangent.reshape(count, width).astype(jnp.float32)
    grad_gain_second = jnp.sum(grad_out * normed_two, axis=0)
    grad_shift_second = jnp.sum(grad_out, axis=0)
    grad_h2 = norm_backward(grad_out, back_gain_second, normed_two, inverse_two)
    grad_ffn = grad_h2.astype(jnp.bfloat16)
    grad_bias_outer = jnp.sum(grad_ffn.astype(jnp.float32), axis=0)
    grad_w_outer = contract_rows(activation, grad_ffn)
    grad_pre = (contract_last(grad_ffn, back_outer) * gelu_slope(pre_act)).astype(jnp.bfloat16)
    grad_bias_inner = jnp.sum(grad_pre.astype(jnp.float32), axis=0)
    grad_w_inner = contract_rows(first_low, grad_pre)
    grad_first = grad_h2 + contract_last(grad_pre, back_inner)
    grad_gain_first = jnp.sum(grad_first * normed_one, axis=0)
    grad_shift_first = jnp.sum(grad_first, axis=0)
    grad_h1 = norm_backward(grad_first, back_gain_first, normed_one, inverse_one)
    grad_attn = grad_h1.astype(jnp.bfloat16)
    grad_bias_output = jnp.sum(grad_attn.astype(jnp.float32), axis=0)
    grad_w_output = contract_rows(context_flat, grad_attn)
    grad_context = (
        contract_last(grad_attn, back_output).astype(jnp.bfloat16).reshape(groups, rows, width)
    )

    def back_step(unused, inputs):
        grad_queries, grad_keys_all, grad_values_all = attend_back(inputs)
        grad_keys, grad_values = (
            lax.psum_scatter(
                grad_keys_all.astype(jnp.bfloat16), "row", scatter_dimension=0, tiled=True
            ).astype(jnp.float32),
            lax.psum_scatter(
                grad_values_all.astype(jnp.bfloat16), "row", scatter_dimension=0, tiled=True
            ).astype(jnp.float32),
        )
        return (unused, (grad_queries, grad_keys, grad_values))

    _, (grad_queries, grad_keys, grad_values) = lax.scan(
        back_step,
        None,
        (query_groups, key_all, value_all, seg_own, seg_all, log_total, grad_context),
    )
    queries_low = grad_queries.reshape(count, width).astype(jnp.bfloat16)
    keys_low = grad_keys.reshape(count, width).astype(jnp.bfloat16)
    values_low = grad_values.reshape(count, width).astype(jnp.bfloat16)
    grad_w_query = contract_rows(flat, queries_low) * scale
    grad_bias_query = jnp.sum(queries_low.astype(jnp.float32), axis=0) * scale
    grad_w_key = contract_rows(flat, keys_low)
    grad_w_value = contract_rows(flat, values_low)
    grad_bias_value = jnp.sum(values_low.astype(jnp.float32), axis=0)
    grad_inputs = grad_h1 + (
        contract_last(queries_low, back_query) * scale
        + contract_last(keys_low, back_key)
        + contract_last(values_low, back_value)
    )
    grad_tokens = grad_inputs.astype(jnp.bfloat16).reshape(groups, rows, width)
    owned = (
        lax.psum_scatter(grad_w_query, ("grp", "row"), scatter_dimension=0, tiled=True),
        lax.psum_scatter(grad_w_key, ("grp", "row"), scatter_dimension=0, tiled=True),
        lax.psum_scatter(grad_w_value, ("grp", "row"), scatter_dimension=0, tiled=True),
        lax.psum_scatter(grad_w_output, ("grp", "row"), scatter_dimension=0, tiled=True),
        lax.psum_scatter(grad_w_inner, ("grp", "row"), scatter_dimension=0, tiled=True),
        lax.psum_scatter(grad_w_outer, ("grp", "row"), scatter_dimension=0, tiled=True),
        lax.psum_scatter(grad_bias_query, ("grp", "row"), scatter_dimension=0, tiled=True),
        lax.psum_scatter(grad_bias_value, ("grp", "row"), scatter_dimension=0, tiled=True),
        lax.psum_scatter(grad_bias_output, ("grp", "row"), scatter_dimension=0, tiled=True),
        lax.psum_scatter(grad_gain_first, ("grp", "row"), scatter_dimension=0, tiled=True),
        lax.psum_scatter(grad_shift_first, ("grp", "row"), scatter_dimension=0, tiled=True),
        lax.psum_scatter(grad_bias_inner, ("grp", "row"), scatter_dimension=0, tiled=True),
        lax.psum_scatter(grad_bias_outer, ("grp", "row"), scatter_dimension=0, tiled=True),
        lax.psum_scatter(grad_gain_second, ("grp", "row"), scatter_dimension=0, tiled=True),
        lax.psum_scatter(grad_shift_second, ("grp", "row"), scatter_dimension=0, tiled=True),
    )
    return (
        layer_out,
        grad_tokens,
        owned[0],
        owned[1],
        owned[2],
        owned[3],
        owned[4],
        owned[5],
        owned[6],
        owned[7],
        owned[8],
        owned[9],
        owned[10],
        owned[11],
        owned[12],
        owned[13],
        owned[14],
    )


def solution(mesh):
    in_specs = (
        P("grp", "row", None),
        P("grp", None),
        P("grp", "row", None),
        P(("grp", "row"), None),
        P(("grp", "row"), None),
        P(("grp", "row"), None),
        P(("grp", "row"), None),
        P(("grp", "row"), None),
        P(("grp", "row"), None),
        P(("grp", "row")),
        P(("grp", "row")),
        P(("grp", "row")),
        P(("grp", "row")),
        P(("grp", "row")),
        P(("grp", "row")),
        P(("grp", "row")),
        P(("grp", "row")),
        P(("grp", "row")),
    )
    out_specs = (
        P("grp", "row", None),
        P("grp", "row", None),
        P(("grp", "row"), None),
        P(("grp", "row"), None),
        P(("grp", "row"), None),
        P(("grp", "row"), None),
        P(("grp", "row"), None),
        P(("grp", "row"), None),
        P(("grp", "row")),
        P(("grp", "row")),
        P(("grp", "row")),
        P(("grp", "row")),
        P(("grp", "row")),
        P(("grp", "row")),
        P(("grp", "row")),
        P(("grp", "row")),
        P(("grp", "row")),
    )
    return jax.shard_map(
        per_device, mesh=mesh, in_specs=in_specs, out_specs=out_specs, check_vma=False
    )
```

profile of v0, /device:TPU:0, one launch (start us, length us, event | category | flops | bytes accessed | tf_op | source)
XLA Modules:
  0.0 1379.4 jit_solution(11516229698966482481)
XLA Ops:
  17.0 42.4 %all-reduce.19 = (bf16[3072]{0:T(1024)(128)(2,1)S(1)}, bf16[768]{0:T(1024)(128)(2,1)S(1)}, bf16[768]{0:T(1024)(128)(2,1)S(1)}, bf16[768]{0:T(1024)(128)(2,1)S(1)...) all-reduce(bf16[3072]{0:T(1024)(128)(2,1)S(1)} %dynamic-update-slic, ...), channel_id=1, replica_groups=mesh['grp'=4,'row'=8] {'grp','row'}, use_global_device_ids=true, to_apply=%add.5 | all-reduce | flops 9216 | bytes 36864
  59.4 8.6 all-gather.11.cloned.1.call-done
  68.0 2.6 fusion.30
  70.7 53.2 %all-gather.15.cloned.1.call-done = bf16[768,768]{1,0:T(8,128)(2,1)} async-done(((bf16[24,768]{1,0:T(8,128)(2,1)}), bf16[768,768]{1,0:T(8,128)(2,1)}) %all-gather.15.cloned.1.call-update) | async-done | bytes 1179664 | tf_op jit(solution)/shard_map/all_gather | solution.py:133
  123.9 2.6 convolution_convert_fusion.2
  133.8 46.1 %all-gather.13.cloned.1.call-done = bf16[768,768]{1,0:T(8,128)(2,1)} async-done(((bf16[24,768]{1,0:T(8,128)(2,1)}), bf16[768,768]{1,0:T(8,128)(2,1)}) %all-gather.13.cloned.1.call-update) | async-done | bytes 1179664 | tf_op jit(solution)/shard_map/all_gather | solution.py:132
  180.0 1.7 fusion.31
  182.7 59.2 %all-gather.23.cloned.1.call-done = bf16[2048,768]{1,0:T(8,128)(2,1)} async-done(((bf16[256,768]{1,0:T(8,128)(2,1)}), bf16[2048,768]{1,0:T(8,128)(2,1)}) %all-gather.23.cloned.1.call-update) | async-done | bytes 3145744 | tf_op jit(solution)/shard_map/all_gather | solution.py:183
  241.9 4.9 copy.60
  246.8 56.8 %all-gather.25.cloned.1.call-done = bf16[2048,768]{1,0:T(8,128)(2,1)} async-done(((bf16[256,768]{1,0:T(8,128)(2,1)}), bf16[2048,768]{1,0:T(8,128)(2,1)}) %all-gather.25.cloned.1.call-update) | async-done | bytes 3145744 | tf_op jit(solution)/shard_map/all_gather | solution.py:182
  303.6 3.2 copy.62
  306.8 11.4 select_reduce_fusion
  318.2 11.4 fusion
  330.3 12.1 fusion.33
  342.4 16.8 %all-gather.17.cloned.1.call-done = bf16[768,768]{1,0:T(8,128)(2,1)} async-done(((bf16[24,768]{1,0:T(8,128)(2,1)}), bf16[768,768]{1,0:T(8,128)(2,1)}) %all-gather.17.cloned.1.call-update) | async-done | bytes 1179664 | tf_op jit(solution)/shard_map/all_gather | solution.py:135
  359.2 2.0 fusion.65
  363.0 61.7 %all-gather.19.cloned.1.call-done = bf16[768,3072]{1,0:T(8,128)(2,1)} async-done(((bf16[24,3072]{1,0:T(8,128)(2,1)}), bf16[768,3072]{1,0:T(8,128)(2,1)}) %all-gather.19.cloned.1.call-update) | async-done | bytes 4718608 | tf_op jit(solution)/shard_map/all_gather | solution.py:136
  424.7 11.5 fusion.14
  436.2 53.9 %all-gather.21.cloned.1.call-done = bf16[3072,768]{1,0:T(8,128)(2,1)} async-done(((bf16[96,768]{1,0:T(8,128)(2,1)}), bf16[3072,768]{1,0:T(8,128)(2,1)}) %all-gather.21.cloned.1.call-update) | async-done | bytes 4718608 | tf_op jit(solution)/shard_map/all_gather | solution.py:137
  490.2 4.7 fusion.66
  496.1 1.7 convert_reduce_fusion.2
  497.8 3.0 convert_reduce_fusion
  500.9 2.3 multiply_reduce_fusion.1
  506.2 1.9 copy.63
  508.2 12.5 fusion.9
  520.7 19.5 %multiply_reduce_fusion = (f32[12,256]{1,0:T(8,128)}, f32[12,256,2048]{2,1,0:T(8,128)}) fusion(f32[12,256,2048]{2,1,0:T(8,128)} %get-tuple-element.175, f32[12,256]{1,0:T(8,128)S(1)} %log_add_fusion, pred[256,2048]{1,0:T(8,128)(4,1)} %compare_or_fusion, bf16[256,12,64]{0,2,1:T(8,128)(2,1)} %bitcast.111, bf16[2048,12,64]{0,2,1:T(8,128)(2,1)} %bitcast.105), kind=kOutput, calls=%fused_computation.1 | convolution fusion | flops 830469120 | bytes 54419456 | tf_op jit(solution)/shard_map/while/body/eval_jaxpr/qhd,khd->hqk/dot_general | solution.py:90
  540.2 18.0 %multiply_convert_fusion = bf16[12,256,2048]{2,1,0:T(8,128)(2,1)S(1)} fusion(f32[12,256,2048]{2,1,0:T(8,128)} %get-tuple-element.184, f32[12,256,2048]{2,1,0:T(8,128)} %get-tuple-element.175, f32[12,256]{1,0:T(8,128)} %get-tuple-element.183, f32[12,256]{1,0:T(8,128)S(1)} %log_add_fusion, pred[256,2048]{1,0:T(8,128)(4,1)} %compare_or_fusion), kind=kLoop, calls=%fused_computation | loop fusion | flops 31457280 | bytes 63463424 | tf_op jit(solution)/shard_map/while/body/eval_jaxpr/convert_element_type | solution.py:94
  558.3 4.5 convolution_convert_fusion
  563.9 3.1 fusion.53
  567.1 8.7 convert_reduce_fusion.5
  577.0 2.0 copy.67
  579.0 15.7 %reduce-scatter.17.cloned.1.call-done = bf16[256,768]{0,1:T(8,128)(2,1)} async-done(((bf16[2048,768]{0,1:T(8,128)(2,1)}), bf16[256,768]{0,1:T(8,128)(2,1)}) %reduce-scatter.17.cloned.1.call-update) | async-done | bytes 393232 | tf_op jit(solution)/shard_map/while/body/eval_jaxpr/reduce_scatter | solution.py:259
  594.7 1.5 convolution_bitcast_fusion
  596.2 2.0 copy.71
  598.3 74.1 %reduce-scatter.15.cloned.1.call-done = bf16[256,768]{0,1:T(8,128)(2,1)} async-done(((bf16[2048,768]{0,1:T(8,128)(2,1)}), bf16[256,768]{0,1:T(8,128)(2,1)}) %reduce-scatter.15.cloned.1.call-update) | async-done | bytes 393232 | tf_op jit(solution)/shard_map/while/body/eval_jaxpr/reduce_scatter | solution.py:256
  672.4 1.5 convolution_bitcast_fusion.1
  674.0 2.1 copy.69
  677.5 5.2 fusion.61
  684.4 5.1 fusion.56
  691.2 2.7 convolution_multiply_fusion.1
  694.2 40.9 %all-reduce.18 = (f32[768]{0:T(1024)S(1)}, f32[768]{0:T(1024)S(1)}, f32[768]{0:T(1024)S(1)}, f32[768]{0:T(1024)S(1)}, f32[768]{0:T(1024)S(1)}, /*index=5*/f32[30...) all-reduce(f32[768]{0:T(1024)S(1)} %mul.203, ...), channel_id=12, replica_groups=mesh['grp'=4,'row'=8] {'grp','row'}, use_global_device_ids=true, to_apply=%region_22.23.clone | all-reduce | flops 9216 | bytes 73728
  740.3 1.7 convolution_add_fusion.2
  743.3 33.5 %reduce-scatter.19.cloned.1.call-done = f32[24,768]{1,0:T(8,128)} async-done(((f32[768,768]{1,0:T(8,128)}), f32[24,768]{1,0:T(8,128)}) %reduce-scatter.19.cloned.1.call-update) | async-done | bytes 73744 | tf_op jit(solution)/shard_map/reduce_scatter | solution.py:288
  776.8 104.6 %reduce-scatter.25.cloned.1.call-done = f32[24,768]{1,0:T(8,128)} async-done(((f32[768,768]{1,0:T(8,128)}), f32[24,768]{1,0:T(8,128)}) %reduce-scatter.25.cloned.1.call-update) | async-done | bytes 73744
  881.4 103.9 %reduce-scatter.29.cloned.1.call-done = f32[24,768]{1,0:T(8,128)} async-done(((f32[768,768]{1,0:T(8,128)}), f32[24,768]{1,0:T(8,128)}) %reduce-scatter.29.cloned.1.call-update) | async-done | bytes 73744
  985.3 104.6 %reduce-scatter.27.cloned.1.call-done = f32[24,768]{1,0:T(8,128)} async-done(((f32[768,768]{1,0:T(8,128)}), f32[24,768]{1,0:T(8,128)}) %reduce-scatter.27.cloned.1.call-update) | async-done | bytes 73744
  1090.0 140.8 %reduce-scatter.21.cloned.1.call-done = f32[24,3072]{1,0:T(8,128)} async-done(((f32[768,3072]{1,0:T(8,128)}), f32[24,3072]{1,0:T(8,128)}) %reduce-scatter.21.cloned.1.call-update) | async-done | bytes 294928 | tf_op jit(solution)/shard_map/reduce_scatter | solution.py:289
  1230.8 142.0 %reduce-scatter.23.cloned.1.call-done = f32[96,768]{1,0:T(8,128)} async-done(((f32[3072,768]{1,0:T(8,128)}), f32[96,768]{1,0:T(8,128)}) %reduce-scatter.23.cloned.1.call-update) | async-done | bytes 294928 | tf_op jit(solution)/shard_map/reduce_scatter | solution.py:290
  (189 shorter events, 38.6 us)
Async XLA Ops:
  7.2 172.8 %copy-start.8 = (bf16[1,256,768]{2,1,0:T(8,128)(2,1)S(1)}, bf16[1,256,768]{2,1,0:T(8,128)(2,1)}, u32[]{:S(2)}) copy-start(bf16[1,256,768]{2,1,0:T(8,128)(2,1)} %param.18) | copy-start | bytes 1179652
  7.2 121.5 %copy-start.40 = (s32[1,8]{1,0:T(1,128)S(1)}, s32[1,8]{1,0:T(1,128)}, u32[]{:S(2)}) copy-start(s32[1,8]{1,0:T(1,128)} %param.19) | copy-start | bytes 100
  7.2 60.8 %all-gather.11.cloned.1.call-start = ((), (), s32[]{:S(2)}) async-start(), calls=%async_computation.8 | async-start | bytes 1216512 | tf_op jit(solution)/shard_map/all_gather | solution.py:134
  7.9 116.0 %all-gather.15.cloned.1.call-start = ((), (), s32[]{:S(2)}) async-start(), calls=%async_computation.10 | async-start | bytes 1216512 | tf_op jit(solution)/shard_map/all_gather | solution.py:133
  8.7 171.3 %all-gather.13.cloned.1.call-start = ((), (), s32[]{:S(2)}) async-start(), calls=%async_computation.9 | async-start | bytes 1216512 | tf_op jit(solution)/shard_map/all_gather | solution.py:132
  9.4 232.5 %all-gather.23.cloned.1.call-start = ((), (), s32[]{:S(2)}) async-start(), calls=%async_computation.19 | async-start | bytes 3538944 | tf_op jit(solution)/shard_map/all_gather | solution.py:183
  70.7 232.9 %all-gather.25.cloned.1.call-start = ((), (), s32[]{:S(2)}) async-start(), calls=%async_computation.20 | async-start | bytes 3538944 | tf_op jit(solution)/shard_map/all_gather | solution.py:182
  126.6 232.7 %all-gather.17.cloned.1.call-start = ((), (), s32[]{:S(2)}) async-start(), calls=%async_computation.11 | async-start | bytes 1216512 | tf_op jit(solution)/shard_map/all_gather | solution.py:135
  127.2 297.6 %all-gather.19.cloned.1.call-start = ((), (), s32[]{:S(2)}) async-start(), calls=%async_computation.12 | async-start | bytes 4866048 | tf_op jit(solution)/shard_map/all_gather | solution.py:136
  127.9 362.2 %all-gather.21.cloned.1.call-start = ((), (), s32[]{:S(2)}) async-start(), calls=%async_computation.13 | async-start | bytes 4866048 | tf_op jit(solution)/shard_map/all_gather | solution.py:137
  128.7 466.1 %reduce-scatter.17.cloned.1.call-start = ((), (), s32[]{:S(2)}) async-start(), calls=%async_computation.15 | async-start | bytes 3538944 | tf_op jit(solution)/shard_map/while/body/eval_jaxpr/reduce_scatter | solution.py:259
  306.8 11.4 copy-start.1
  318.2 11.4 copy-start.26
  318.2 12.0 copy-start.2
  359.2 3.7 copy-start.27
  359.2 3.7 copy-start.30
  490.2 7.6 slice-start.2
  490.2 4.9 copy-start.13
  490.2 4.9 copy-start.31
  490.2 5.9 copy-start.35
  490.2 7.6 slice-start.3
  494.8 2.9 copy-start.41
  496.1 4.8 slice-start
  497.8 3.1 copy-start.17
  497.8 3.1 copy-start.6
  497.8 3.0 copy-start.24
  497.8 3.0 copy-start.33
  497.8 3.0 copy-start.38
  497.8 3.0 slice-start.1
  500.8 2.3 copy-start.21
  500.9 4.1 copy-start.11
  520.7 151.8 %reduce-scatter.15.cloned.1.call-start = ((), (), s32[]{:S(2)}) async-start(), calls=%async_computation.14 | async-start | bytes 3538944 | tf_op jit(solution)/shard_map/while/body/eval_jaxpr/reduce_scatter | solution.py:256
  540.2 18.1 %copy-start.9 = (bf16[256,768]{0,1:T(8,128)(2,1)S(1)}, bf16[256,768]{0,1:T(8,128)(2,1)}, u32[]{:S(2)}) copy-start(bf16[256,768]{0,1:T(8,128)(2,1)} %copy.61) | copy-start | bytes 1179652
  558.3 5.5 copy-start
  563.8 213.0 %reduce-scatter.19.cloned.1.call-start = ((), (), s32[]{:S(2)}) async-start(), calls=%async_computation.16 | async-start | bytes 2433024 | tf_op jit(solution)/shard_map/reduce_scatter | solution.py:288
  567.0 314.4 %reduce-scatter.25.cloned.1.call-start = ((), (), s32[]{:S(2)}) async-start(), calls=%async_computation.21 | async-start | bytes 2433024
  579.0 406.4 %reduce-scatter.29.cloned.1.call-start = ((), (), s32[]{:S(2)}) async-start(), calls=%async_computation.23 | async-start | bytes 2433024
  598.3 491.7 %reduce-scatter.27.cloned.1.call-start = ((), (), s32[]{:S(2)}) async-start(), calls=%async_computation.22 | async-start | bytes 2433024
  673.9 2.3 copy-start.7
  676.1 554.6 %reduce-scatter.21.cloned.1.call-start = ((), (), s32[]{:S(2)}) async-start(), calls=%async_computation.17 | async-start | bytes 9732096 | tf_op jit(solution)/shard_map/reduce_scatter | solution.py:289
  682.8 690.0 %reduce-scatter.23.cloned.1.call-start = ((), (), s32[]{:S(2)}) async-start(), calls=%async_computation.18 | async-start | bytes 9732096 | tf_op jit(solution)/shard_map/reduce_scatter | solution.py:290
  689.5 4.5 copy-start.12
  689.5 4.6 copy-start.36
  689.5 4.6 copy-start.37
  689.5 50.7 %copy-start.10 = (bf16[768,768]{1,0:T(8,128)(2,1)S(1)}, bf16[768,768]{1,0:T(8,128)(2,1)}, u32[]{:S(2)}) copy-start(bf16[768,768]{1,0:T(8,128)(2,1)} %all-gather.15.cloned.1.call-done) | copy-start | bytes 3538948
  689.6 50.7 %copy-start.20 = (bf16[256,768]{0,1:T(8,128)(2,1)S(1)}, bf16[256,768]{0,1:T(8,128)(2,1)}, u32[]{:S(2)}) copy-start(bf16[256,768]{0,1:T(8,128)(2,1)} %reduce-scatter.15.cloned.1.call-done) | copy-start | bytes 1179652
  690.5 51.5 %copy-start.4 = (f32[256,768]{1,0:T(8,128)S(1)}, f32[256,768]{1,0:T(8,128)}, u32[]{:S(2)}) copy-start(f32[256,768]{1,0:T(8,128)} %copy-done.3) | copy-start | bytes 2359300
  735.0 6.9 copy-start.23
  (14 other events, 20.4 us)
Sparse Core Ops, SparseCore 0:
  11.0 57.0 all-gather.10
  70.9 52.9 all-gather.14
  126.9 53.0 all-gather.12
  182.6 59.3 all-gather.22
  244.5 59.0 all-gather.24
  306.4 52.7 all-gather.16
  362.2 62.5 all-gather.18
  427.6 62.4 all-gather.20
  520.8 73.9 reduce-scatter.16
  598.2 74.1 reduce-scatter.14
  678.3 98.4 reduce-scatter.18
  783.4 98.0 reduce-scatter.24
  887.3 97.9 reduce-scatter.28
  991.9 98.0 reduce-scatter.26
  1096.3 134.4 reduce-scatter.20
  1238.1 134.5 reduce-scatter.22
where the time goes:
time: 1380 us
  waiting for transfers between devices  1080 us (78%)
  matrix products  123 us (9%)
  blocking collectives  83.2 us (6%)
  other arithmetic  40 us (3%)
  local copies, waits for them, and re-layouts  38 us (3%)
  between operations  14.8 us (1%)
    unnamed x19, waiting for transfers between devices  317 us
    reduce_scatter x1, waiting for transfers between devices, per_device(): lax.psum_scatter(grad_w_outer, ('grp', 'row'), scatter_dimension=0, tiled...  142 us
    reduce_scatter x1, waiting for transfers between devices, per_device(): lax.psum_scatter(grad_w_inner, ('grp', 'row'), scatter_dimension=0, tiled...  141 us
    unnamed x2, blocking collectives  83.2 us
    reduce_scatter x1, waiting for transfers between devices, back_step(): lax.psum_scatter(grad_keys_all.astype(jnp.bfloat16), 'row', scatter_dimen...  74.1 us
    all_gather x1, waiting for transfers between devices, per_device(): lax.all_gather(w_inner, ('grp', 'row'), axis=0, tiled=True)  61.7 us
    all_gather x1, waiting for transfers between devices, per_device(): lax.all_gather(value_rows.reshape(groups, rows, width), 'row', axis=1, ti...  59.2 us
    all_gather x1, waiting for transfers between devices, per_device(): lax.all_gather(key_rows.reshape(groups, rows, width), 'row', axis=1, tile...  56.8 us
  transfers between devices with their start and end apart: 16, of which 16 were waited for; matrix products, arithmetic and copies ran while one was open for 12% of the time, Pallas kernels for 0%

commit v1 on v0

v1 whole, which is shorter than its diff:
```python
import jax
import jax.numpy as jnp
import numpy as np
from jax import lax
from jax.sharding import PartitionSpec as P

HEADS = 12
HDIM = 64
PROMPT = 1024
CONT_MOST = 256
BF = jnp.bfloat16
F32 = jnp.float32

NORM_EPS = 1e-12
MASK_FILL = -1000000000.0
SQRT_HALF = 0.7071067811865476
INV_ROOT_TAU = 0.3989422804014327
AXES = ("grp", "row")


def mm(left, right):
    return jnp.dot(left, right, preferred_element_type=F32)


def contract_last(left, right):
    return lax.dot_general(left, right, (((1,), (1,)), ((), ())), preferred_element_type=F32)


def contract_rows(left, right):
    return lax.dot_general(left, right, (((0,), (0,)), ((), ())), preferred_element_type=F32)


def segment_ids(lengths, group_len):
    ends = jnp.cumsum(lengths)
    places = jnp.arange(group_len, dtype=jnp.int32)
    passed = jnp.sum(((places - PROMPT)[:, None] >= ends[None, :]).astype(jnp.int32), axis=-1)
    return jnp.where(places < PROMPT, 0, 1 + passed)


def norm_forward(hidden, gain, shift):
    average = jnp.mean(hidden, axis=-1, keepdims=True)
    centred = hidden - average
    inverse = lax.rsqrt(jnp.mean(centred * centred, axis=-1, keepdims=True) + NORM_EPS)
    normed = centred * inverse
    return normed * gain + shift, normed, inverse


def norm_backward(grad_out, gain, normed, inverse):
    grad_norm = grad_out * gain
    one = jnp.mean(grad_norm, axis=-1, keepdims=True)
    two = jnp.mean(grad_norm * normed, axis=-1, keepdims=True)
    return inverse * (grad_norm - one - normed * two)


def gelu_slope(pre_act):
    cumulative = 0.5 * (1.0 + jax.scipy.special.erf(pre_act * SQRT_HALF))
    return cumulative + pre_act * jnp.exp(-0.5 * pre_act * pre_act) * INV_ROOT_TAU


def split_heads(rows_in):
    return rows_in.reshape(rows_in.shape[0], HEADS, HDIM)


class Plan:
    def __init__(self, grp, row):
        self.grp, self.row, self.count = grp, row, grp * row
        self.y = row // 4
        bits = lambda base, size: [base << i for i in range(size.bit_length() - 1)]
        ys, zs = bits(1, self.y), bits(self.y, 4)
        core, xs = bits(row, 2), bits(2 * row, grp // 2)
        self.orders = (tuple(zs + ys + xs + core), tuple(zs + xs + ys + core))

    def swap(self, value, mask):
        return lax.ppermute(value, AXES, [(i, i ^ mask) for i in range(self.count)])

    def send(self, value, moves):
        pairs = [(g * self.row + a, g * self.row + b) for g in range(self.grp) for a, b in moves]
        return lax.ppermute(value, AXES, pairs)

    def me(self):
        return lax.axis_index("grp") * self.row + lax.axis_index("row")

    def gather(self, value, order):
        held, masks = value[None], [0]
        for bit in order:
            held = jnp.concatenate([held, self.swap(held, bit)], 0)
            masks = masks + [m ^ bit for m in masks]
        slot = np.zeros(self.count, np.int32)
        for j, m in enumerate(masks):
            slot[m] = j
        places = jnp.asarray(slot)[self.me() ^ jnp.arange(self.count)]
        return jnp.take(held, places, axis=0, mode="clip")


def token_blocks(plan, own, rows):
    if plan.row != 8:
        every = lax.all_gather(own, "row", axis=0, tiled=True)
        start = jnp.maximum(lax.axis_index("row") * rows - CONT_MOST, 0)
        padded = jnp.concatenate([every, jnp.zeros((CONT_MOST, own.shape[1]), own.dtype)], 0)
        near = lax.dynamic_slice_in_dim(padded, start, rows + 2 * CONT_MOST, 0)
        return jnp.concatenate([every[:PROMPT], near], 0)
    row = lax.axis_index("row")
    across = plan.send(own, [(0, 4), (1, 5), (2, 6), (3, 7)])
    same = jnp.where(row < 4, own, across)
    beside = plan.swap(own, 1)
    diagonal = plan.send(own, [(5, 6), (6, 5)])
    other = plan.swap(same, 2)
    same_y = plan.swap(same, 1)
    other_y = plan.swap(other, 1)
    return jnp.concatenate([same, other, same_y, other_y, own, beside, diagonal], 0)


def near_segments(plan, segments, rows):
    row = lax.axis_index("row")
    if plan.row != 8:
        start = jnp.maximum(row * rows - CONT_MOST, 0)
        padded = jnp.concatenate([segments, jnp.full((CONT_MOST,), -1, jnp.int32)], 0)
        near = lax.dynamic_slice_in_dim(padded, start, rows + 2 * CONT_MOST, 0)
        return jnp.where((near == 0) | (row * rows < PROMPT), -1, near)
    pieces = []
    for block, valid in (
        (row, row >= 4),
        (row ^ 1, row >= 4),
        (11 - row, (row == 5) | (row == 6)),
    ):
        block = jnp.clip(block, 0, 7)
        ids = lax.dynamic_slice_in_dim(segments, block * rows, rows, 0)
        pieces.append(jnp.where(valid, ids, -1))
    return jnp.concatenate(pieces, 0)


def token_return(plan, parts, rows):
    if plan.row != 8:
        row = lax.axis_index("row")
        start = jnp.maximum(row * rows - CONT_MOST, 0)
        whole = jnp.zeros((plan.row * rows + CONT_MOST, parts.shape[1]), F32)
        whole = whole.at[:PROMPT].set(parts[:PROMPT])
        near = lax.dynamic_slice_in_dim(whole, start, rows + 2 * CONT_MOST, 0) + parts[PROMPT:]
        whole = lax.dynamic_update_slice_in_dim(whole, near, start, 0)
        return lax.psum_scatter(whole[: plan.row * rows], "row", scatter_dimension=0, tiled=True)
    row = lax.axis_index("row")
    same, other, same_y, other_y, own, beside, diagonal = [
        parts[i * rows : (i + 1) * rows] for i in range(7)
    ]
    low = lambda v: v.astype(BF)
    wide = lambda v: v.astype(F32)
    other = other + wide(plan.swap(low(other_y), 1))
    same = same + wide(plan.swap(low(same_y), 1))
    own = own + wide(plan.swap(low(beside), 1))
    own = own + wide(plan.send(low(diagonal), [(5, 6), (6, 5)]))
    same = same + wide(plan.swap(low(other), 2))
    back = plan.send(low(same), [(4, 0), (5, 1), (6, 2), (7, 3)])
    return jnp.where(row < 4, same + wide(back), own)


def attend(queries, keys, values, allowed):
    scores = jnp.einsum(
        "qhd,khd->hqk", split_heads(queries), split_heads(keys), preferred_element_type=F32
    )
    scores = jnp.where(allowed[None], scores, MASK_FILL)
    peak = jnp.max(scores, axis=-1, keepdims=True)
    grown = jnp.exp(scores - peak)
    total = jnp.sum(grown, axis=-1, keepdims=True)
    shares = (grown / total).astype(BF)
    mixed = jnp.einsum("hqk,khd->qhd", shares, split_heads(values), preferred_element_type=F32)
    return mixed.reshape(queries.shape).astype(BF), peak + jnp.log(total)


def attend_back(queries, keys, values, allowed, log_total, grad_context):
    hq, hk, hv, hg = [split_heads(v) for v in (queries, keys, values, grad_context)]
    scores = jnp.einsum("qhd,khd->hqk", hq, hk, preferred_element_type=F32)
    scores = jnp.where(allowed[None], scores, MASK_FILL)
    shares = jnp.exp(scores - log_total)
    grad_shares = jnp.einsum("qhd,khd->hqk", hg, hv, preferred_element_type=F32)
    inner = jnp.sum(shares * grad_shares, axis=-1, keepdims=True)
    grad_scores = (shares * (grad_shares - inner)).astype(BF)
    grad_queries = jnp.einsum("hqk,khd->qhd", grad_scores, hk, preferred_element_type=F32)
    grad_keys = jnp.einsum("hqk,qhd->khd", grad_scores, hq, preferred_element_type=F32)
    grad_values = jnp.einsum("hqk,qhd->khd", shares.astype(BF), hg, preferred_element_type=F32)
    return (
        grad_queries.reshape(queries.shape).astype(BF),
        grad_keys.reshape(keys.shape).astype(BF),
        grad_values.reshape(keys.shape).astype(BF),
    )


def solution(mesh):
    plan = Plan(mesh.shape["grp"], mesh.shape["row"])

    def per_device(
        tokens, cont_lengths, cotangent, w_query, w_key, w_value, w_output, w_inner, w_outer,
        bias_query, bias_value, bias_output, gain_first, shift_first, bias_inner, bias_outer,
        gain_second, shift_second,
    ):
        count = plan.count
        _, rows, width = tokens.shape
        step = w_query.shape[0]
        wide = w_inner.shape[1] // width
        row = lax.axis_index("row")
        scale = HDIM ** (-0.5)
        own = tokens[0]

        vectors = (
            bias_query, bias_value, bias_output, gain_first, shift_first, bias_outer, gain_second,
            shift_second, bias_inner,
        )
        line = jnp.concatenate(vectors)
        small = len(vectors) - 1
        line = jnp.pad(line, (0, width - line.shape[0]))[None]
        line = jnp.pad(line, ((0, 7), (0, 0)))
        pack_a = jnp.concatenate([w_query, line], 0)
        pack_b = jnp.concatenate([w_key, w_value], 0)
        got_a = plan.gather(pack_a, plan.orders[0])
        got_b = plan.gather(pack_b, plan.orders[1])
        blocks = token_blocks(plan, own, rows)

        inner_rows = w_inner.reshape(step, wide, width).transpose(1, 0, 2).reshape(-1, width)
        pack_c = jnp.concatenate([w_output, inner_rows, w_outer], 0)
        got_c = lax.all_gather(pack_c, AXES, axis=0, tiled=True).reshape(count, -1, width)

        full_query = got_a[:, :step].reshape(width, width)
        lines = got_a[:, step]
        table = lines[:, : small * step].reshape(count, small, step).transpose(1, 0, 2)
        table = table.reshape(small, width).astype(F32)
        v_bq, v_bv, v_bo, v_g1, v_s1, v_bout, v_g2, v_s2 = [table[i] for i in range(small)]
        v_bin = lines[:, small * step : (small + wide) * step].reshape(-1).astype(F32)
        full_key = got_b[:, :step].reshape(width, width)
        full_value = got_b[:, step : 2 * step].reshape(width, width)

        queries = ((mm(own, full_query) + v_bq) * scale).astype(BF)
        keys = mm(blocks, full_key).astype(BF)
        values = (mm(blocks, full_value) + v_bv).astype(BF)

        segments = segment_ids(cont_lengths[0], plan.row * rows)
        seg_own = lax.dynamic_slice_in_dim(segments, row * rows, rows, 0)
        near = near_segments(plan, segments, rows)
        allowed = jnp.concatenate(
            [
                jnp.ones((rows, PROMPT), jnp.bool_),
                near[None, :] == seg_own[:, None],
            ],
            1,
        )
        context, log_total = attend(queries, keys, values, allowed)

        full_output = got_c[:, :step].reshape(width, width)
        full_inner = got_c[:, step : step * (1 + wide)].reshape(count, wide, step, width)
        full_inner = full_inner.transpose(0, 2, 1, 3).reshape(width, wide * width)
        full_outer = got_c[:, step * (1 + wide) :].reshape(wide * width, width)

        attn_out = mm(context, full_output) + v_bo
        first, normed_one, inverse_one = norm_forward(own.astype(F32) + attn_out, v_g1, v_s1)
        first_low = first.astype(BF)
        pre_act = mm(first_low, full_inner) + v_bin
        activation = jax.nn.gelu(pre_act, approximate=False).astype(BF)
        ffn_out = mm(activation, full_outer) + v_bout
        second, normed_two, inverse_two = norm_forward(first + ffn_out, v_g2, v_s2)
        layer_out = second.astype(BF)

        grad_out = cotangent[0].astype(F32)
        d_gain_second = jnp.sum(grad_out * normed_two, axis=0)
        d_shift_second = jnp.sum(grad_out, axis=0)
        grad_h2 = norm_backward(grad_out, v_g2, normed_two, inverse_two)
        grad_ffn = grad_h2.astype(BF)
        d_bias_outer = jnp.sum(grad_ffn.astype(F32), axis=0)
        d_outer = contract_rows(activation, grad_ffn).astype(BF)
        grad_pre = (contract_last(grad_ffn, full_outer) * gelu_slope(pre_act)).astype(BF)
        d_bias_inner = jnp.sum(grad_pre.astype(F32), axis=0)
        d_inner = contract_rows(first_low, grad_pre).astype(BF)
        grad_first = grad_h2 + contract_last(grad_pre, full_inner)
        d_gain_first = jnp.sum(grad_first * normed_one, axis=0)
        d_shift_first = jnp.sum(grad_first, axis=0)
        grad_h1 = norm_backward(grad_first, v_g1, normed_one, inverse_one)
        grad_attn = grad_h1.astype(BF)
        d_bias_output = jnp.sum(grad_attn.astype(F32), axis=0)
        d_output = contract_rows(context, grad_attn).astype(BF)
        grad_context = contract_last(grad_attn, full_output).astype(BF)

        def scatter(pieces):
            whole = jnp.concatenate(pieces, 1)
            depth = whole.shape[1]
            flat = whole.reshape(count * depth, width)
            return lax.psum_scatter(flat, AXES, scatter_dimension=0, tiled=True).astype(F32)

        by_owner = lambda grad: grad.reshape(count, step, width)
        sums_c = scatter(
            [
                by_owner(d_output),
                d_inner.reshape(count, step, wide, width)
                .transpose(0, 2, 1, 3)
                .reshape(count, wide * step, width),
                d_outer.reshape(count, wide * step, width),
            ]
        )

        grad_queries, grad_keys, grad_values = attend_back(
            queries, keys, values, allowed, log_total, grad_context
        )
        d_query = (contract_rows(own, grad_queries) * scale).astype(BF)
        d_bias_query = jnp.sum(grad_queries.astype(F32), axis=0) * scale
        d_key = contract_rows(blocks, grad_keys).astype(BF)
        d_value = contract_rows(blocks, grad_values).astype(BF)
        d_bias_value = jnp.sum(grad_values.astype(F32), axis=0)
        shared = contract_last(grad_keys, full_key) + contract_last(grad_values, full_value)
        returned = token_return(plan, shared, rows)
        grad_tokens = grad_h1 + contract_last(grad_queries, full_query) * scale + returned

        d_table = jnp.stack(
            [d_bias_query, d_bias_value, d_bias_output, d_gain_first, d_shift_first, d_bias_outer,
             d_gain_second, d_shift_second]
        )
        d_lines = jnp.concatenate(
            [
                d_table.reshape(small, count, step).transpose(1, 0, 2).reshape(count, -1),
                d_bias_inner.reshape(count, wide * step),
            ],
            1,
        )
        d_lines = jnp.pad(d_lines, ((0, 0), (0, width - d_lines.shape[1]))).astype(BF)
        d_lines = jnp.pad(d_lines[:, None], ((0, 0), (0, 7), (0, 0)))
        sums_a = scatter([by_owner(d_query), by_owner(d_key), by_owner(d_value), d_lines])

        o_line = sums_a[3 * step]
        o_small = [o_line[i * step : (i + 1) * step] for i in range(small)]
        o_bin = o_line[small * step : (small + wide) * step]
        o_inner = sums_c[step : step * (1 + wide)].reshape(wide, step, width)
        o_inner = o_inner.transpose(1, 0, 2).reshape(step, wide * width)
        return (
            layer_out[None],
            grad_tokens.astype(BF)[None],
            sums_a[:step],
            sums_a[step : 2 * step],
            sums_a[2 * step : 3 * step],
            sums_c[:step],
            o_inner,
            sums_c[step * (1 + wide) :],
            o_small[0],
            o_small[1],
            o_small[2],
            o_small[3],
            o_small[4],
            o_bin,
            o_small[5],
            o_small[6],
            o_small[7],
        )

    split = P("grp", "row", None)
    owned2, owned1 = P(AXES, None), P(AXES)
    in_specs = (split, P("grp", None), split) + (owned2,) * 6 + (owned1,) * 9
    out_specs = (split, split) + (owned2,) * 6 + (owned1,) * 9
    return jax.shard_map(
        per_device, mesh=mesh, in_specs=in_specs, out_specs=out_specs, check_vma=False
    )
```

time: 1380 us -> 572 us (0.41)
  waiting for transfers between devices: 1080 us -> 274 us
  blocking collectives: 83.2 us -> 0 us
  local copies, waits for them, and re-layouts: 38 us -> 93.4 us
  starting transfers between devices: 0.64 us -> 35.7 us
  matrix products: 123 us -> 101 us
    all_gather x8 -> x1, waiting for transfers between devices: 357 us -> 0.02 us  [per_device(): lax.all_gather(pack_c, AXES, axis=0, tiled=True).reshape(count, -1, width)]
    unnamed x19 -> x3, waiting for transfers between devices: 317 us -> 0.05 us
    reduce_scatter x5 -> x2, waiting for transfers between devices: 406 us -> 178 us  [scatter(): lax.psum_scatter(flat, AXES, scatter_dimension=0, tiled=True).astype(F32)]
    ppermute x0 -> x22, waiting for transfers between devices: none -> 96.2 us  [the longest x18 59.8 us: swap(): return lax.ppermute(value, AXES, [(i, i ^ mask) for i in range(self.count)])]
    unnamed x2 -> x0, blocking collectives: 83.2 us -> none
    ppermute x0 -> x22, starting transfers between devices: none -> 35.6 us  [the longest x18 26.9 us: swap(): return lax.ppermute(value, AXES, [(i, i ^ mask) for i in range(self.count)])]
    dot_general x12, matrix products: 93.8 us -> 68.4 us  [the longest x6 17.8 us: mm(): return jnp.dot(left, right, preferred_element_type=F32)]
    reshape x0 -> x6, local copies, waits for them, and re-layouts: none -> 17.4 us  [the longest x2 13.4 us: per_device(): d_inner.reshape(count, step, wide, width).transpose(0, 2, 1, 3)]
  transfers between devices with their start and end apart: 16 -> 25, of which waited for: 16 -> 13; matrix products, arithmetic and copies ran while one was open for 12% -> 18% of each run, Pallas kernels for 0% -> 0%
where the time goes in v1:
time: 572 us; the launch traced here: 562 us
  waiting for transfers between devices  274 us (48%)
  matrix products  101 us (18%)
  local copies, waits for them, and re-layouts  93.4 us (16%)
  other arithmetic  43.3 us (8%)
  starting transfers between devices  35.7 us (6%)
  between operations  15.1 us (3%)
    reduce_scatter x2, waiting for transfers between devices, scatter(): lax.psum_scatter(flat, AXES, scatter_dimension=0, tiled=True).astype(F32)  178 us
    ppermute x18, waiting for transfers between devices, swap(): return lax.ppermute(value, AXES, [(i, i ^ mask) for i in range(self.count)])  59.8 us
    ppermute x4, waiting for transfers between devices, send(): return lax.ppermute(value, AXES, pairs)  36.4 us
    ppermute x18, starting transfers between devices, swap(): return lax.ppermute(value, AXES, [(i, i ^ mask) for i in range(self.count)])  26.9 us
    unnamed x95, local copies, waits for them, and re-layouts  22.4 us
    dot_general x6, matrix products, mm(): return jnp.dot(left, right, preferred_element_type=F32)  17.8 us
    dot_general x6, matrix products, contract_rows(): lax.dot_general(left, right, (((0,), (0,)), ((), ())), preferred_element_...  17.4 us
    dot_general x1, matrix products, attend_back(): grad_shares = jnp.einsum('qhd,khd->hqk', hg, hv, preferred_element_type=F32)  16.2 us
  transfers between devices with their start and end apart: 25, of which 13 were waited for; matrix products, arithmetic and copies ran while one was open for 18% of the time, Pallas kernels for 0%

profile of v1, /device:TPU:0, one launch (start us, length us, event | category | flops | bytes accessed | tf_op | source)
XLA Modules:
  0.0 562.5 jit_solution(2380386424197938883)
XLA Ops:
  9.9 6.1 %collective-permute-start = (bf16[256,768]{1,0:T(8,128)(2,1)}, bf16[256,768]{1,0:T(8,128)(2,1)S(1)}, u32[]{:S(2)}, u32[]{:S(2)}) collective-permute-start(bf16[256,768]{1,0:T(8,128)(2,1)} %bitcast.169), channel_id=1, source_target_pairs={{0,4},{1,5},{2,6},{3,7},{8,12},{9,13},{10,14},{11,15},{16,20},{17,... | collective-permute-start | bytes 1179656 | tf_op jit(solution)/shard_map/ppermute | solution.py:78
  20.0 6.1 %concatenate.78 = bf16[288]{0:T(512)(128)(2,1)S(1)} concatenate(bf16[24]{0:T(256)(128)(2,1)} %param.29, bf16[24]{0:T(256)(128)(2,1)} %param.30, bf16[24]{0:T(256)(128)(2,1)} %param.31, bf16[24]{0:T(256)(128)(2,1)} %param.32, bf16[24]{0:T(256)(128)(2,1)} %param.33, bf16[24]{0:T(256)(128)(2,1)} %param.35, bf16[24]{0:T(256)(128)(2,1)} %param.36, bf16[24]{0:T(256)(128)(2,1)} %param.37, ...), dimensions={0} | concatenate | bytes 1152 | tf_op jit(solution)/shard_map/concatenate | solution.py:207
  35.8 3.0 collective-permute-start.7
  39.5 6.5 %collective-permute-done.12 = bf16[2,32,768]{2,1,0:T(8,128)(2,1)S(1)} collective-permute-done((bf16[2,32,768]{2,1,0:T(8,128)(2,1)S(1)}, bf16[2,32,768]{2,1,0:T(8,128)(2,1)S(1)}, u32[]{:S(2)}, u32[]{:S(2)}) %collective-permute-start.12) | collective-permute-done | bytes 98336 | tf_op jit(solution)/shard_map/ppermute | solution.py:74
  49.8 3.8 collective-permute-done.13
  55.4 6.5 %collective-permute-start.1 = (bf16[256,768]{1,0:T(8,128)(2,1)S(1)}, bf16[256,768]{1,0:T(8,128)(2,1)S(1)}, u32[]{:S(2)}, u32[]{:S(2)}) collective-permute-start(bf16[256,768]{1,0:T(8,128)(2,1)S(1)} %get-tuple-element.37), channel_id=1, source_target_pairs={{0,2},{1,3},{2,0},{3,1},{4,6},{5,7},{6,4},{7,5},{8,10},{9,11},{10,... | collective-permute-start | bytes 1179656 | tf_op jit(solution)/shard_map/ppermute | solution.py:74
  66.6 7.8 %collective-permute-done.14 = bf16[8,32,768]{2,1,0:T(8,128)(2,1)S(1)} collective-permute-done((bf16[8,32,768]{2,1,0:T(8,128)(2,1)S(1)}, bf16[8,32,768]{2,1,0:T(8,128)(2,1)S(1)}, u32[]{:S(2)}, u32[]{:S(2)}) %collective-permute-start.14) | collective-permute-done | bytes 393248 | tf_op jit(solution)/shard_map/ppermute | solution.py:74
  75.1 3.1 collective-permute-start.3
  79.2 11.2 %collective-permute-done.9 = bf16[8,48,768]{2,1,0:T(8,128)(2,1)S(1)} collective-permute-done((bf16[8,48,768]{2,1,0:T(8,128)(2,1)S(1)}, bf16[8,48,768]{2,1,0:T(8,128)(2,1)S(1)}, u32[]{:S(2)}, u32[]{:S(2)}) %collective-permute-start.9) | collective-permute-done | bytes 589856 | tf_op jit(solution)/shard_map/ppermute | solution.py:74
  91.5 13.7 %collective-permute-done.3 = bf16[256,768]{1,0:T(8,128)(2,1)S(1)} collective-permute-done((bf16[256,768]{1,0:T(8,128)(2,1)S(1)}, bf16[256,768]{1,0:T(8,128)(2,1)S(1)}, u32[]{:S(2)}, u32[]{:S(2)}) %collective-permute-start.3) | collective-permute-done | bytes 393248 | tf_op jit(solution)/shard_map/ppermute | solution.py:74
  107.9 2.1 gather_fusion.3
  114.3 2.5 fusion.33
  116.8 2.4 constant_dynamic-update-slice_fusion.12
  119.2 2.5 gather_fusion.1
  124.3 2.4 convolution_convert_fusion.3
  126.8 4.6 select_reduce_fusion
  131.4 5.5 fusion
  137.0 3.1 copy-done
  140.1 2.4 add_convert_fusion
  144.1 10.2 %fusion.35 = bf16[12,64,256]{2,1,0:T(8,128)(2,1)S(1)} fusion(bf16[1792,12,64]{0,2,1:T(8,128)(2,1)S(1)} %bitcast.192, f32[12,256,1792]{2,1,0:T(8,128)} %copy-done, f32[12,256]{1,0:T(8,128)S(1)} %fusion, f32[12,256]{1,0:T(8,128)S(1)} %get-tuple-element.84, pred[256,1792]{1,0:T(8,128)(4,1)S(1)} %concatenate.86), kind=kOutput, calls=%fused_computation.74 | convolution fusion | flops 726859776 | bytes 25649152 | tf_op jit(solution)/shard_map/hqk,khd->qhd/dot_general | solution.py:165
  155.8 6.6 %fusion.70 = (bf16[32,96,768]{2,1,0:T(8,128)(2,1)}, bf16[32,96,768]{2,1,0:T(8,128)(2,1)S(1)}) fusion(bf16[32,216,768]{2,1,0:T(8,128)(2,1)} %bitcast.168), kind=kLoop, calls=%fused_computation.216 | loop fusion | bytes 18874368 | tf_op jit(solution)/shard_map/slice | solution.py:249
  163.3 2.3 copy.55
  166.8 8.3 %fusion.16 = (bf16[256,3072]{1,0:T(8,128)(2,1)S(1)}, f32[256,3072]{1,0:T(8,128)S(1)}) fusion(f32[3072]{0:T(1024)S(1)} %copy-done.32, bf16[768,3072]{1,0:T(8,128)(2,1)S(1)} %bitcast.174, f32[256,768]{1,0:T(8,128)S(1)} %get-tuple-element.87, f32[768]{0:T(1024)S(1)} %add.204, f32[768]{0:T(1024)S(1)} %mul.192, f32[256]{0:T(256)S(1)} %add_rsqrt_fusion.1, ...), kind=kOutput, calls=%fused_computation.35 | convolution fusion | flops 1260847104 | bytes 10244096 | tf_op jit(solution)/shard_map/dot_general | solution.py:22
  176.9 1.7 fusion.43
  179.5 3.0 fusion.79
  182.5 2.3 multiply_reduce_fusion.1
  188.1 16.2 %multiply_reduce_fusion = (f32[12,256]{1,0:T(8,128)S(1)}, f32[12,256,1792]{2,1,0:T(8,128)}) fusion(f32[12,256,1792]{2,1,0:T(8,128)} %copy-done, f32[12,256]{1,0:T(8,128)S(1)} %log_add_fusion, pred[256,1792]{1,0:T(8,128)(4,1)S(1)} %concatenate.86, bf16[256,12,64]{0,2,1:T(8,128)(2,1)S(1)} %bitcast.186, bf16[1792,12,64]{0,2,1:T(8,128)(2,1)} %bitcast.193), kind=kOutput, calls=%fused_computation.5 | convolution fusion | flops 726660096 | bytes 47669248 | tf_op jit(solution)/shard_map/qhd,khd->hqk/dot_general | solution.py:174
  204.3 11.6 %bitcast_reduce_fusion = (bf16[12,64]{1,0:T(8,128)(2,1)}, bf16[12,64,1792]{2,1,0:T(8,128)(2,1)}) fusion(bf16[256,12,64]{0,2,1:T(8,128)(2,1)S(1)} %bitcast.187, f32[12,256,1792]{2,1,0:T(8,128)} %copy-done, f32[12,256]{1,0:T(8,128)S(1)} %log_add_fusion, pred[256,1792]{1,0:T(8,128)(4,1)S(1)} %concatenate.86), kind=kOutput, calls=%fused_computation.55 | convolution fusion | flops 723909888 | bytes 25638400 | tf_op jit(solution)/shard_map/hqk,qhd->khd/dot_general | solution.py:179
  215.9 15.1 %multiply_convert_fusion = bf16[12,256,1792]{2,1,0:T(8,128)(2,1)S(1)} fusion(f32[12,256,1792]{2,1,0:T(8,128)} %get-tuple-element.94, f32[12,256,1792]{2,1,0:T(8,128)} %copy-done, f32[12,256]{1,0:T(8,128)S(1)} %get-tuple-element.93, f32[12,256]{1,0:T(8,128)S(1)} %log_add_fusion, pred[256,1792]{1,0:T(8,128)(4,1)S(1)} %concatenate.86), kind=kLoop, calls=%fused_computation.4 | loop fusion | flops 27525120 | bytes 55533568 | tf_op jit(solution)/shard_map/convert_element_type | solution.py:176
  230.9 2.0 convolution_convert_fusion.2
  233.0 5.9 %convert_reduce_fusion = (f32[12,64]{1,0:T(8,128)S(1)}, bf16[12,64,256]{2,1,0:T(8,128)(2,1)}) fusion(bf16[1792,12,64]{0,2,1:T(8,128)(2,1)} %bitcast.160, bf16[12,256,1792]{2,1,0:T(8,128)(2,1)S(1)} %multiply_convert_fusion), kind=kOutput, calls=%fused_computation.93 | convolution fusion | flops 705232128 | bytes 14158848 | tf_op jit(solution)/shard_map/hqk,khd->qhd/dot_general | solution.py:177
  238.9 5.3 convolution_convert_fusion.6
  244.3 3.4 convolution_convert_fusion.5
  272.0 3.4 fusion.9
  276.1 5.1 convolution_convert_fusion.1
  281.2 10.0 %reshape.333 = bf16[32,24,4,768]{3,2,1,0:T(4,128)(2,1)} reshape(bf16[768,3072]{1,0:T(8,128)(2,1)} %convolution_convert_fusion.1) | data formatting | bytes 9437184 | tf_op jit(solution)/shard_map/reshape | solution.py:289
  291.2 3.4 copy.59
  297.5 5.0 pad_maximum_fusion
  302.5 4.7 fusion.80
  307.2 2.4 fusion.78
  309.8 2.0 collective-permute-start.17
  311.9 10.0 %collective-permute-done.17 = bf16[256,768]{1,0:T(8,128)(2,1)S(1)} collective-permute-done((bf16[256,768]{1,0:T(8,128)(2,1)S(1)}, bf16[256,768]{1,0:T(8,128)(2,1)S(1)}, u32[]{:S(2)}, u32[]{:S(2)}) %collective-permute-start.17) | collective-permute-done | bytes 393248 | tf_op jit(solution)/shard_map/ppermute | solution.py:74
  322.1 2.0 collective-permute-start.20
  324.7 3.3 collective-permute-done.16
  328.1 1.8 collective-permute-done.18
  332.3 36.3 %collective-permute-done.19 = bf16[256,768]{1,0:T(8,128)(2,1)S(1)} collective-permute-done((bf16[256,768]{1,0:T(8,128)(2,1)S(1)}, bf16[256,768]{1,0:T(8,128)(2,1)S(1)}, u32[]{:S(2)}, u32[]{:S(2)}) %collective-permute-start.19) | collective-permute-done | bytes 393248 | tf_op jit(solution)/shard_map/ppermute | solution.py:78
  370.1 34.6 %reduce-scatter.3.cloned.1.call-done = bf16[80,768]{1,0:T(8,128)(2,1)} async-done(((bf16[2560,768]{1,0:T(8,128)(2,1)}), bf16[80,768]{1,0:T(8,128)(2,1)}) %reduce-scatter.3.cloned.1.call-update) | async-done | bytes 122896 | tf_op jit(solution)/shard_map/reduce_scatter | solution.py:283
  408.3 143.3 %reduce-scatter.5.cloned.1.call-done = bf16[216,768]{1,0:T(8,128)(2,1)} async-done(((bf16[6912,768]{1,0:T(8,128)(2,1)}), bf16[216,768]{1,0:T(8,128)(2,1)}) %reduce-scatter.5.cloned.1.call-update) | async-done | bytes 331792 | tf_op jit(solution)/shard_map/reduce_scatter | solution.py:283
  (226 shorter events, 90.6 us)
Async XLA Ops:
  7.2 27.0 %copy-start.13 = (bf16[1,256,768]{2,1,0:T(8,128)(2,1)S(1)}, bf16[1,256,768]{2,1,0:T(8,128)(2,1)}, u32[]{:S(2)}) copy-start(bf16[1,256,768]{2,1,0:T(8,128)(2,1)} %param.22) | copy-start | bytes 1179652
  7.2 147.1 %all-gather.2.cloned.1.call-start = ((), (), s32[]{:S(2)}) async-start(), calls=%async_computation.2 | async-start | bytes 10948608 | tf_op jit(solution)/shard_map/all_gather | solution.py:219
  9.9 45.4 %copy-start.4 = (bf16[1,256,768]{2,1,0:T(8,128)(2,1)S(1)}, bf16[1,256,768]{2,1,0:T(8,128)(2,1)}, u32[]{:S(2)}) copy-start(bf16[1,256,768]{2,1,0:T(8,128)(2,1)} %param.20) | copy-start | bytes 1179652
  9.9 394.8 %reduce-scatter.3.cloned.1.call-start = ((), (), s32[]{:S(2)}) async-start(), calls=%async_computation.3 | async-start | bytes 4055040 | tf_op jit(solution)/shard_map/reduce_scatter | solution.py:283
  9.9 45.3 %collective-permute-start = (bf16[256,768]{1,0:T(8,128)(2,1)}, bf16[256,768]{1,0:T(8,128)(2,1)S(1)}, u32[]{:S(2)}, u32[]{:S(2)}) collective-permute-start(bf16[256,768]{1,0:T(8,128)(2,1)} %bitcast.169), channel_id=1, source_target_pairs={{0,4},{1,5},{2,6},{3,7},{8,12},{9,13},{10,14},{11,15},{16,20},{17,... | collective-permute-start | bytes 1179656 | tf_op jit(solution)/shard_map/ppermute | solution.py:78
  16.1 89.3 %collective-permute-start.4 = (bf16[256,768]{1,0:T(8,128)(2,1)}, bf16[256,768]{1,0:T(8,128)(2,1)S(1)}, u32[]{:S(2)}, u32[]{:S(2)}) collective-permute-start(bf16[256,768]{1,0:T(8,128)(2,1)} %bitcast.170), channel_id=1, source_target_pairs={{0,1},{1,0},{2,3},{3,2},{4,5},{5,4},{6,7},{7,6},{8,9},{9,8},{10,11... | collective-permute-start | bytes 1179656 | tf_op jit(solution)/shard_map/ppermute | solution.py:74
  18.4 17.4 %collective-permute-start.6 = (bf16[1,48,768]{2,1,0:T(8,128)(2,1)S(1)}, bf16[1,48,768]{2,1,0:T(8,128)(2,1)S(1)}, u32[]{:S(2)}, u32[]{:S(2)}) collective-permute-start(bf16[1,48,768]{2,1,0:T(8,128)(2,1)S(1)} %maximum_bitcast_fusion), channel_id=1, source_target_pairs={{0,2},{1,3},{2,0},{3,1},{4,6},{5,7},{6,4},{7,5},{8,10},{9,11},{10,... | collective-permute-start | bytes 221192 | tf_op jit(solution)/shard_map/ppermute | solution.py:74
  26.9 8.2 %collective-permute-start.11 = (bf16[1,32,768]{2,1,0:T(8,128)(2,1)S(1)}, bf16[1,32,768]{2,1,0:T(8,128)(2,1)S(1)}, u32[]{:S(2)}, u32[]{:S(2)}) collective-permute-start(bf16[1,32,768]{2,1,0:T(8,128)(2,1)S(1)} %fusion.55), channel_id=1, source_target_pairs={{0,2},{1,3},{2,0},{3,1},{4,6},{5,7},{6,4},{7,5},{8,10},{9,11},{10,... | collective-permute-start | bytes 147464 | tf_op jit(solution)/shard_map/ppermute | solution.py:74
  35.1 10.9 %collective-permute-start.12 = (bf16[2,32,768]{2,1,0:T(8,128)(2,1)S(1)}, bf16[2,32,768]{2,1,0:T(8,128)(2,1)S(1)}, u32[]{:S(2)}, u32[]{:S(2)}) collective-permute-start(bf16[2,32,768]{2,1,0:T(8,128)(2,1)S(1)} %pad_maximum_fusion.7), channel_id=1, source_target_pairs={{0,4},{1,5},{2,6},{3,7},{4,0},{5,1},{6,2},{7,3},{8,12},{9,13},{10,... | collective-permute-start | bytes 294920 | tf_op jit(solution)/shard_map/ppermute | solution.py:74
  35.8 12.4 %collective-permute-start.7 = (bf16[2,48,768]{2,1,0:T(8,128)(2,1)S(1)}, bf16[2,48,768]{2,1,0:T(8,128)(2,1)S(1)}, u32[]{:S(2)}, u32[]{:S(2)}) collective-permute-start(bf16[2,48,768]{2,1,0:T(8,128)(2,1)S(1)} %pad_maximum_fusion.6), channel_id=1, source_target_pairs={{0,4},{1,5},{2,6},{3,7},{4,0},{5,1},{6,2},{7,3},{8,12},{9,13},{10,... | collective-permute-start | bytes 442376 | tf_op jit(solution)/shard_map/ppermute | solution.py:74
  46.0 7.6 %collective-permute-start.13 = (bf16[4,32,768]{2,1,0:T(8,128)(2,1)S(1)}, bf16[4,32,768]{2,1,0:T(8,128)(2,1)S(1)}, u32[]{:S(2)}, u32[]{:S(2)}) collective-permute-start(bf16[4,32,768]{2,1,0:T(8,128)(2,1)S(1)} %pad_maximum_fusion.5), channel_id=1, source_target_pairs={{0,1},{1,0},{2,3},{3,2},{4,5},{5,4},{6,7},{7,6},{8,9},{9,8},{10,11... | collective-permute-start | bytes 589832 | tf_op jit(solution)/shard_map/ppermute | solution.py:74
  47.6 17.5 %copy-start.34 = (bf16[16,32,768]{2,1,0:T(8,128)(2,1)S(1)}, bf16[16,32,768]{2,1,0:T(8,128)(2,1)}, u32[]{:S(2)}) copy-start(bf16[16,32,768]{2,1,0:T(8,128)(2,1)} %get-tuple-element.70) | copy-start | bytes 2359300
  48.3 15.9 %collective-permute-start.8 = (bf16[4,48,768]{2,1,0:T(8,128)(2,1)S(1)}, bf16[4,48,768]{2,1,0:T(8,128)(2,1)S(1)}, u32[]{:S(2)}, u32[]{:S(2)}) collective-permute-start(bf16[4,48,768]{2,1,0:T(8,128)(2,1)S(1)} %pad_maximum_fusion.4), channel_id=1, source_target_pairs={{0,16},{1,17},{2,18},{3,19},{4,20},{5,21},{6,22},{7,23},{8,24},{9,... | collective-permute-start | bytes 884744 | tf_op jit(solution)/shard_map/ppermute | solution.py:74
  53.7 20.7 %collective-permute-start.14 = (bf16[8,32,768]{2,1,0:T(8,128)(2,1)S(1)}, bf16[8,32,768]{2,1,0:T(8,128)(2,1)S(1)}, u32[]{:S(2)}, u32[]{:S(2)}) collective-permute-start(bf16[8,32,768]{2,1,0:T(8,128)(2,1)S(1)} %pad_maximum_fusion.2), channel_id=1, source_target_pairs={{0,16},{1,17},{2,18},{3,19},{4,20},{5,21},{6,22},{7,23},{8,24},{9,... | collective-permute-start | bytes 1179656 | tf_op jit(solution)/shard_map/ppermute | solution.py:74
  55.4 19.7 %collective-permute-start.1 = (bf16[256,768]{1,0:T(8,128)(2,1)S(1)}, bf16[256,768]{1,0:T(8,128)(2,1)S(1)}, u32[]{:S(2)}, u32[]{:S(2)}) collective-permute-start(bf16[256,768]{1,0:T(8,128)(2,1)S(1)} %get-tuple-element.37), channel_id=1, source_target_pairs={{0,2},{1,3},{2,0},{3,1},{4,6},{5,7},{6,4},{7,5},{8,10},{9,11},{10,... | collective-permute-start | bytes 1179656 | tf_op jit(solution)/shard_map/ppermute | solution.py:74
  62.6 16.4 %collective-permute-start.2 = (bf16[256,768]{1,0:T(8,128)(2,1)S(1)}, bf16[256,768]{1,0:T(8,128)(2,1)S(1)}, u32[]{:S(2)}, u32[]{:S(2)}) collective-permute-start(bf16[256,768]{1,0:T(8,128)(2,1)S(1)} %get-tuple-element.37), channel_id=1, source_target_pairs={{0,1},{1,0},{2,3},{3,2},{4,5},{5,4},{6,7},{7,6},{8,9},{9,8},{10,11... | collective-permute-start | bytes 1179656 | tf_op jit(solution)/shard_map/ppermute | solution.py:74
  64.3 26.1 %collective-permute-start.9 = (bf16[8,48,768]{2,1,0:T(8,128)(2,1)S(1)}, bf16[8,48,768]{2,1,0:T(8,128)(2,1)S(1)}, u32[]{:S(2)}, u32[]{:S(2)}) collective-permute-start(bf16[8,48,768]{2,1,0:T(8,128)(2,1)S(1)} %pad_maximum_fusion.1), channel_id=1, source_target_pairs={{0,1},{1,0},{2,3},{3,2},{4,5},{5,4},{6,7},{7,6},{8,9},{9,8},{10,11... | collective-permute-start | bytes 1769480 | tf_op jit(solution)/shard_map/ppermute | solution.py:74
  74.4 31.0 %collective-permute-start.5 = (bf16[256,768]{1,0:T(8,128)(2,1)S(1)}, bf16[256,768]{1,0:T(8,128)(2,1)S(1)}, u32[]{:S(2)}, u32[]{:S(2)}) collective-permute-start(bf16[256,768]{1,0:T(8,128)(2,1)S(1)} %bitcast.171), channel_id=1, source_target_pairs={{5,6},{6,5},{13,14},{14,13},{21,22},{22,21},{29,30},{30,29}} | collective-permute-start | bytes 1179656 | tf_op jit(solution)/shard_map/ppermute | solution.py:78
  75.1 30.1 %collective-permute-start.3 = (bf16[256,768]{1,0:T(8,128)(2,1)S(1)}, bf16[256,768]{1,0:T(8,128)(2,1)S(1)}, u32[]{:S(2)}, u32[]{:S(2)}) collective-permute-start(bf16[256,768]{1,0:T(8,128)(2,1)S(1)} %collective-permute-done.1), channel_id=1, source_target_pairs={{0,1},{1,0},{2,3},{3,2},{4,5},{5,4},{6,7},{7,6},{8,9},{9,8},{10,11... | collective-permute-start | bytes 1179656 | tf_op jit(solution)/shard_map/ppermute | solution.py:74
  79.1 26.3 %collective-permute-start.15 = (bf16[16,32,768]{2,1,0:T(8,128)(2,1)S(1)}, bf16[16,32,768]{2,1,0:T(8,128)(2,1)S(1)}, u32[]{:S(2)}, u32[]{:S(2)}) collective-permute-start(bf16[16,32,768]{2,1,0:T(8,128)(2,1)S(1)} %get-tuple-element.49), channel_id=1, source_target_pairs={{0,8},{1,9},{2,10},{3,11},{4,12},{5,13},{6,14},{7,15},{8,0},{9,1},... | collective-permute-start | bytes 2359304 | tf_op jit(solution)/shard_map/ppermute | solution.py:74
  91.5 25.3 %collective-permute-start.10 = (bf16[16,48,768]{2,1,0:T(8,128)(2,1)}, bf16[16,48,768]{2,1,0:T(8,128)(2,1)}, u32[]{:S(2)}, u32[]{:S(2)}) collective-permute-start(bf16[16,48,768]{2,1,0:T(8,128)(2,1)} %get-tuple-element.47), channel_id=1, source_target_pairs={{0,8},{1,9},{2,10},{3,11},{4,12},{5,13},{6,14},{7,15},{8,0},{9,1},... | collective-permute-start | bytes 3538952 | tf_op jit(solution)/shard_map/ppermute | solution.py:74
  126.8 4.6 copy-start.1
  131.4 8.7 %copy-start = (f32[12,256,1792]{2,1,0:T(8,128)}, f32[12,256,1792]{2,1,0:T(8,128)S(1)}, u32[]{:S(2)}) copy-start(f32[12,256,1792]{2,1,0:T(8,128)S(1)} %get-tuple-element.85) | copy-start | bytes 66060292
  131.4 8.7 %copy-start.22 = (bf16[32,24,768]{2,1,0:T(8,128)(2,1)S(1)}, bf16[32,24,768]{2,1,0:T(8,128)(2,1)}, u32[]{:S(2)}) copy-start(bf16[32,24,768]{2,1,0:T(8,128)(2,1)} %get-tuple-element.45) | copy-start | bytes 3538948
  131.4 8.7 %copy-start.25 = (bf16[1792,768]{1,0:T(8,128)(2,1)S(1)}, bf16[1792,768]{1,0:T(8,128)(2,1)}, u32[]{:S(2)}) copy-start(bf16[1792,768]{1,0:T(8,128)(2,1)} %copy-done.23) | copy-start | bytes 8257540
  154.3 8.2 %copy-start.19 = (bf16[12,64,256]{2,1,0:T(8,128)(2,1)}, bf16[12,64,256]{2,1,0:T(8,128)(2,1)S(1)}, u32[]{:S(2)}) copy-start(bf16[12,64,256]{2,1,0:T(8,128)(2,1)S(1)} %fusion.35) | copy-start | bytes 1179652
  155.8 6.6 %copy-start.5 = (bf16[1,256,768]{2,1,0:T(8,128)(2,1)S(1)}, bf16[1,256,768]{2,1,0:T(8,128)(2,1)}, u32[]{:S(2)}) copy-start(bf16[1,256,768]{2,1,0:T(8,128)(2,1)} %param.20) | copy-start | bytes 1179652
  155.8 6.6 %copy-start.29 = (f32[768]{0:T(1024)S(1)}, f32[768]{0:T(1024)}, u32[]{:S(2)}) copy-start(f32[768]{0:T(1024)} %add.199) | copy-start | bytes 9220
  163.1 21.7 %copy-start.27 = (f32[256]{0:T(256)}, f32[256]{0:T(256)S(1)}, u32[]{:S(2)}) copy-start(f32[256]{0:T(256)S(1)} %broadcast_multiply_fusion.5) | copy-start | bytes 3076
  163.3 21.5 %copy-start.30 = (f32[256]{0:T(256)}, f32[256]{0:T(256)S(1)}, u32[]{:S(2)}) copy-start(f32[256]{0:T(256)S(1)} %add_rsqrt_fusion.1) | copy-start | bytes 3076
  165.7 9.4 %slice-start = ((s8[4718592]{0:T(1024)(128)(4,1)}), s8[4194304]{0:T(1024)(128)(4,1)S(1)}, s32[]{:S(2)}) async-start(s8[4718592]{0:T(1024)(128)(4,1)} %bitcast.178), calls=%async_computation.5 | async-start | bytes 8388608
  166.8 8.3 %slice-start.1 = ((s8[4718592]{0:T(1024)(128)(4,1)}), s8[524288]{0:T(1024)(128)(4,1)S(1)}, s32[]{:S(2)}) async-start(s8[4718592]{0:T(1024)(128)(4,1)} %bitcast.178), calls=%async_computation.6 | async-start | bytes 1048576
  166.8 8.3 %copy-start.33 = (f32[768]{0:T(1024)S(1)}, f32[768]{0:T(1024)}, u32[]{:S(2)}) copy-start(f32[768]{0:T(1024)} %add.209) | copy-start | bytes 9220
  185.7 18.6 %copy-start.2 = (f32[256,768]{1,0:T(8,128)}, f32[256,768]{1,0:T(8,128)S(1)}, u32[]{:S(2)}) copy-start(f32[256,768]{1,0:T(8,128)S(1)} %get-tuple-element.35) | copy-start | bytes 2359300
  215.9 15.1 %copy-start.9 = (bf16[768,256]{1,0:T(8,128)(2,1)S(1)}, bf16[768,256]{1,0:T(8,128)(2,1)}, u32[]{:S(2)}) copy-start(bf16[768,256]{1,0:T(8,128)(2,1)} %fusion.33) | copy-start | bytes 1179652
  238.9 5.3 copy-start.17
  238.9 5.3 copy-start.26
  275.4 276.2 %reduce-scatter.5.cloned.1.call-start = ((), (), s32[]{:S(2)}) async-start(), calls=%async_computation.4 | async-start | bytes 10948608 | tf_op jit(solution)/shard_map/reduce_scatter | solution.py:283
  291.2 3.9 copy-start.16
  302.5 4.7 copy-start.7
  309.7 59.0 %copy-start.8 = (bf16[32,24,768]{2,1,0:T(8,128)(2,1)S(1)}, bf16[32,24,768]{2,1,0:T(8,128)(2,1)}, u32[]{:S(2)}) copy-start(bf16[32,24,768]{2,1,0:T(8,128)(2,1)} %slice.226) | copy-start | bytes 3538948
  309.7 59.0 %copy-start.10 = (bf16[12,64,256]{2,1,0:T(8,128)(2,1)S(1)}, bf16[12,64,256]{2,1,0:T(8,128)(2,1)}, u32[]{:S(2)}) copy-start(bf16[12,64,256]{2,1,0:T(8,128)(2,1)} %get-tuple-element.100) | copy-start | bytes 1179652
  309.8 12.1 %collective-permute-start.17 = (bf16[256,768]{1,0:T(8,128)(2,1)S(1)}, bf16[256,768]{1,0:T(8,128)(2,1)S(1)}, u32[]{:S(2)}, u32[]{:S(2)}) collective-permute-start(bf16[256,768]{1,0:T(8,128)(2,1)S(1)} %get-tuple-element.43), channel_id=1, source_target_pairs={{0,1},{1,0},{2,3},{3,2},{4,5},{5,4},{6,7},{7,6},{8,9},{9,8},{10,11... | collective-permute-start | bytes 1179656 | tf_op jit(solution)/shard_map/ppermute | solution.py:74
  311.8 16.3 %collective-permute-start.16 = (bf16[256,768]{1,0:T(8,128)(2,1)S(1)}, bf16[256,768]{1,0:T(8,128)(2,1)S(1)}, u32[]{:S(2)}, u32[]{:S(2)}) collective-permute-start(bf16[256,768]{1,0:T(8,128)(2,1)S(1)} %get-tuple-element.40), channel_id=1, source_target_pairs={{0,1},{1,0},{2,3},{3,2},{4,5},{5,4},{6,7},{7,6},{8,9},{9,8},{10,11... | collective-permute-start | bytes 1179656 | tf_op jit(solution)/shard_map/ppermute | solution.py:74
  322.0 7.8 %collective-permute-start.18 = (bf16[256,768]{1,0:T(8,128)(2,1)S(1)}, bf16[256,768]{1,0:T(8,128)(2,1)S(1)}, u32[]{:S(2)}, u32[]{:S(2)}) collective-permute-start(bf16[256,768]{1,0:T(8,128)(2,1)S(1)} %fusion.46), channel_id=1, source_target_pairs={{0,2},{1,3},{2,0},{3,1},{4,6},{5,7},{6,4},{7,5},{8,10},{9,11},{10,... | collective-permute-start | bytes 1179656 | tf_op jit(solution)/shard_map/ppermute | solution.py:74
  322.1 10.2 %collective-permute-start.20 = (bf16[256,768]{1,0:T(8,128)(2,1)S(1)}, bf16[256,768]{1,0:T(8,128)(2,1)S(1)}, u32[]{:S(2)}, u32[]{:S(2)}) collective-permute-start(bf16[256,768]{1,0:T(8,128)(2,1)S(1)} %get-tuple-element.42), channel_id=1, source_target_pairs={{0,1},{1,0},{2,3},{3,2},{4,5},{5,4},{6,7},{7,6},{8,9},{9,8},{10,11... | collective-permute-start | bytes 1179656 | tf_op jit(solution)/shard_map/ppermute | solution.py:74
  324.1 8.2 %collective-permute-start.21 = (bf16[256,768]{1,0:T(8,128)(2,1)S(1)}, bf16[256,768]{1,0:T(8,128)(2,1)S(1)}, u32[]{:S(2)}, u32[]{:S(2)}) collective-permute-start(bf16[256,768]{1,0:T(8,128)(2,1)S(1)} %get-tuple-element.41), channel_id=1, source_target_pairs={{5,6},{6,5},{13,14},{14,13},{21,22},{22,21},{29,30},{30,29}} | collective-permute-start | bytes 1179656 | tf_op jit(solution)/shard_map/ppermute | solution.py:78
  330.0 38.7 %collective-permute-start.19 = (bf16[256,768]{1,0:T(8,128)(2,1)S(1)}, bf16[256,768]{1,0:T(8,128)(2,1)S(1)}, u32[]{:S(2)}, u32[]{:S(2)}) collective-permute-start(bf16[256,768]{1,0:T(8,128)(2,1)S(1)} %fusion.50), channel_id=1, source_target_pairs={{4,0},{5,1},{6,2},{7,3},{12,8},{13,9},{14,10},{15,11},{20,16},{21,... | collective-permute-start | bytes 1179656 | tf_op jit(solution)/shard_map/ppermute | solution.py:78
  (14 other events, 28.7 us)
Sparse Core Ops, SparseCore 0:
  11.5 117.7 all-gather.1
  275.5 129.1 reduce-scatter.2
  410.8 140.8 reduce-scatter.4

commit v2 on v1

--- a/solution.py
+++ b/solution.py
@@ -69,6 +69,9 @@
         ys, zs = bits(1, self.y), bits(self.y, 4)
         core, xs = bits(row, 2), bits(2 * row, grp // 2)
         self.orders = (tuple(zs + ys + xs + core), tuple(zs + xs + ys + core))
+        flat = [ys + xs] if len(ys + xs) == 2 else [ys, xs]
+        self.scatter_stages = [core] + flat + [zs]
+        self.bits = (grp * row).bit_length() - 1
 
     def swap(self, value, mask):
         return lax.ppermute(value, AXES, [(i, i ^ mask) for i in range(self.count)])
@@ -90,6 +93,35 @@
             slot[m] = j
         places = jnp.asarray(slot)[self.me() ^ jnp.arange(self.count)]
         return jnp.take(held, places, axis=0, mode="clip")
+
+
+    def scatter(self, value):
+        me = self.me()
+        rest = value.shape[1:]
+        left = [1 << i for i in reversed(range(self.bits))]
+        value = value.astype(BF).reshape([2] * self.bits + list(rest))
+        for stage in self.scatter_stages:
+
+            def part(array, mask):
+                for bit in stage:
+                    axis = at.index(bit)
+                    place = ((me ^ mask) // bit) & 1
+                    array = lax.dynamic_slice_in_dim(array, place, 1, axis)
+                return array
+
+            at = left
+            masks = [0]
+            for bit in stage:
+                masks = masks + [m ^ bit for m in masks]
+            total = part(value, 0).astype(F32)
+            for mask in masks[1:]:
+                total = total + self.swap(part(value, mask), mask).astype(F32)
+            left = [b for b in left if b not in stage]
+            shape = [2] * len(left) + list(rest)
+            value = total.reshape(shape)
+            if left:
+                value = value.astype(BF)
+        return value
 
 
 def token_blocks(plan, own, rows):
@@ -276,30 +308,18 @@
         d_output = contract_rows(context, grad_attn).astype(BF)
         grad_context = contract_last(grad_attn, full_output).astype(BF)
 
-        def scatter(pieces):
-            whole = jnp.concatenate(pieces, 1)
-            depth = whole.shape[1]
-            flat = whole.reshape(count * depth, width)
-            return lax.psum_scatter(flat, AXES, scatter_dimension=0, tiled=True).astype(F32)
-
-        by_owner = lambda grad: grad.reshape(count, step, width)
-        sums_c = scatter(
-            [
-                by_owner(d_output),
-                d_inner.reshape(count, step, wide, width)
-                .transpose(0, 2, 1, 3)
-                .reshape(count, wide * step, width),
-                d_outer.reshape(count, wide * step, width),
-            ]
-        )
+        by_owner = lambda grad: grad.reshape(count, step, -1)
+        o_outer = plan.scatter(d_outer.reshape(count, wide * step, width))
+        o_inner = plan.scatter(by_owner(d_inner))
+        o_output = plan.scatter(by_owner(d_output))
 
         grad_queries, grad_keys, grad_values = attend_back(
             queries, keys, values, allowed, log_total, grad_context
         )
         d_query = (contract_rows(own, grad_queries) * scale).astype(BF)
         d_bias_query = jnp.sum(grad_queries.astype(F32), axis=0) * scale
-        d_key = contract_rows(blocks, grad_keys).astype(BF)
-        d_value = contract_rows(blocks, grad_values).astype(BF)
+        both = jnp.concatenate([grad_keys, grad_values], 1)
+        d_both = contract_rows(blocks, both).astype(BF)
         d_bias_value = jnp.sum(grad_values.astype(F32), axis=0)
         shared = contract_last(grad_keys, full_key) + contract_last(grad_values, full_value)
         returned = token_return(plan, shared, rows)
@@ -318,22 +338,21 @@
         )
         d_lines = jnp.pad(d_lines, ((0, 0), (0, width - d_lines.shape[1]))).astype(BF)
         d_lines = jnp.pad(d_lines[:, None], ((0, 0), (0, 7), (0, 0)))
-        sums_a = scatter([by_owner(d_query), by_owner(d_key), by_owner(d_value), d_lines])
-
-        o_line = sums_a[3 * step]
+        o_query = plan.scatter(jnp.concatenate([by_owner(d_query), d_lines], 1))
+        o_both = plan.scatter(by_owner(d_both))
+
+        o_line = o_query[step]
         o_small = [o_line[i * step : (i + 1) * step] for i in range(small)]
         o_bin = o_line[small * step : (small + wide) * step]
-        o_inner = sums_c[step : step * (1 + wide)].reshape(wide, step, width)
-        o_inner = o_inner.transpose(1, 0, 2).reshape(step, wide * width)
         return (
             layer_out[None],
             grad_tokens.astype(BF)[None],
-            sums_a[:step],
-            sums_a[step : 2 * step],
-            sums_a[2 * step : 3 * step],
-            sums_c[:step],
+            o_query[:step],
+            o_both[:, :width],
+            o_both[:, width:],
+            o_output,
             o_inner,
-            sums_c[step * (1 + wide) :],
+            o_outer,
             o_small[0],
             o_small[1],
             o_small[2],

time: 572 us -> 475 us (0.83)
  waiting for transfers between devices: 274 us -> 131 us
  starting transfers between devices: 35.7 us -> 92 us
  local copies, waits for them, and re-layouts: 93.4 us -> 86 us
    reduce_scatter x2 -> x0, waiting for transfers between devices: 178 us -> none  [scatter(): lax.psum_scatter(flat, AXES, scatter_dimension=0, tiled=True).astype(F32)]
    ppermute x18 -> x53, waiting for transfers between devices: 59.8 us -> 124 us  [swap(): return lax.ppermute(value, AXES, [(i, i ^ mask) for i in range(self.count)])]
    ppermute x18 -> x53, starting transfers between devices: 26.9 us -> 83.2 us  [swap(): return lax.ppermute(value, AXES, [(i, i ^ mask) for i in range(self.count)])]
    ppermute x4, waiting for transfers between devices: 36.4 us -> 7.19 us  [send(): return lax.ppermute(value, AXES, pairs)]
    reshape x3 -> x0, local copies, waits for them, and re-layouts: 14.1 us -> none  [the longest x2 13.4 us: per_device(): d_inner.reshape(count, step, wide, width).transpose(0, 2, 1, 3)]
    concatenate x2 -> x1, other arithmetic: 8.37 us -> 0.19 us  [per_device(): o_query = plan.scatter(jnp.concatenate([by_owner(d_query), d_lines], 1))]
    unnamed x95 -> x110, local copies, waits for them, and re-layouts: 22.4 us -> 29.6 us
    dynamic_slice x0 -> x14, local copies, waits for them, and re-layouts: none -> 6.48 us  [part(): array = lax.dynamic_slice_in_dim(array, place, 1, axis)]
  transfers between devices with their start and end apart: 25 -> 58, of which waited for: 13 -> 26; matrix products, arithmetic and copies ran while one was open for 18% -> 24% of each run, Pallas kernels for 0% -> 0%
where the time goes in v2:
time: 475 us; the launch traced here: 465 us
  waiting for transfers between devices  131 us (28%)
  matrix products  99.6 us (21%)
  starting transfers between devices  92 us (19%)
  local copies, waits for them, and re-layouts  86 us (18%)
  other arithmetic  40.7 us (9%)
  between operations  15.7 us (3%)
    ppermute x53, waiting for transfers between devices, swap(): return lax.ppermute(value, AXES, [(i, i ^ mask) for i in range(self.count)])  124 us
    ppermute x53, starting transfers between devices, swap(): return lax.ppermute(value, AXES, [(i, i ^ mask) for i in range(self.count)])  83.2 us
    unnamed x110, local copies, waits for them, and re-layouts  29.6 us
    dot_general x6, matrix products, mm(): return jnp.dot(left, right, preferred_element_type=F32)  17.9 us
    dot_general x1, matrix products, attend_back(): grad_shares = jnp.einsum('qhd,khd->hqk', hg, hv, preferred_element_type=F32)  16.1 us
    dot_general x5, matrix products, contract_rows(): lax.dot_general(left, right, (((0,), (0,)), ((), ())), preferred_element_...  15.4 us
    convert_element_type x1, other arithmetic, attend_back(): grad_scores = (shares * (grad_shares - inner)).astype(BF)  15 us
    dot_general x6, matrix products, contract_last(): lax.dot_general(left, right, (((1,), (1,)), ((), ())), preferred_element_...  14.5 us
  transfers between devices with their start and end apart: 58, of which 26 were waited for; matrix products, arithmetic and copies ran while one was open for 24% of the time, Pallas kernels for 0%

profile of v2, /device:TPU:0, one launch (start us, length us, event | category | flops | bytes accessed | tf_op | source)
XLA Modules:
  0.0 465.1 jit_solution(2385143185412695710)
XLA Ops:
  9.9 6.0 %collective-permute-start = (bf16[256,768]{1,0:T(8,128)(2,1)}, bf16[256,768]{1,0:T(8,128)(2,1)S(1)}, u32[]{:S(2)}, u32[]{:S(2)}) collective-permute-start(bf16[256,768]{1,0:T(8,128)(2,1)} %bitcast.259), channel_id=1, source_target_pairs={{0,4},{1,5},{2,6},{3,7},{8,12},{9,13},{10,14},{11,15},{16,20},{17,... | collective-permute-start | bytes 1179656 | tf_op jit(solution)/shard_map/ppermute | solution.py:81
  17.5 6.1 %concatenate.83 = bf16[288]{0:T(512)(128)(2,1)S(1)} concatenate(bf16[24]{0:T(256)(128)(2,1)} %param.29, bf16[24]{0:T(256)(128)(2,1)} %param.30, bf16[24]{0:T(256)(128)(2,1)} %param.31, bf16[24]{0:T(256)(128)(2,1)} %param.32, bf16[24]{0:T(256)(128)(2,1)} %param.33, bf16[24]{0:T(256)(128)(2,1)} %param.35, bf16[24]{0:T(256)(128)(2,1)} %param.36, bf16[24]{0:T(256)(128)(2,1)} %param.37, ...), dimensions={0} | concatenate | bytes 1152 | tf_op jit(solution)/shard_map/concatenate | solution.py:239
  34.6 3.0 collective-permute-start.7
  38.2 7.7 %collective-permute-done.12 = bf16[2,32,768]{2,1,0:T(8,128)(2,1)S(1)} collective-permute-done((bf16[2,32,768]{2,1,0:T(8,128)(2,1)S(1)}, bf16[2,32,768]{2,1,0:T(8,128)(2,1)S(1)}, u32[]{:S(2)}, u32[]{:S(2)}) %collective-permute-start.12) | collective-permute-done | bytes 98336 | tf_op jit(solution)/shard_map/ppermute | solution.py:77
  49.8 3.4 collective-permute-done.13
  54.6 7.1 %collective-permute-start.1 = (bf16[256,768]{1,0:T(8,128)(2,1)S(1)}, bf16[256,768]{1,0:T(8,128)(2,1)S(1)}, u32[]{:S(2)}, u32[]{:S(2)}) collective-permute-start(bf16[256,768]{1,0:T(8,128)(2,1)S(1)} %get-tuple-element.37), channel_id=1, source_target_pairs={{0,2},{1,3},{2,0},{3,1},{4,6},{5,7},{6,4},{7,5},{8,10},{9,11},{10,... | collective-permute-start | bytes 1179656 | tf_op jit(solution)/shard_map/ppermute | solution.py:77
  66.7 7.8 %collective-permute-done.14 = bf16[8,32,768]{2,1,0:T(8,128)(2,1)S(1)} collective-permute-done((bf16[8,32,768]{2,1,0:T(8,128)(2,1)S(1)}, bf16[8,32,768]{2,1,0:T(8,128)(2,1)S(1)}, u32[]{:S(2)}, u32[]{:S(2)}) %collective-permute-start.14) | collective-permute-done | bytes 393248 | tf_op jit(solution)/shard_map/ppermute | solution.py:77
  75.2 3.0 collective-permute-start.3
  79.2 11.6 %collective-permute-done.9 = bf16[8,48,768]{2,1,0:T(8,128)(2,1)S(1)} collective-permute-done((bf16[8,48,768]{2,1,0:T(8,128)(2,1)S(1)}, bf16[8,48,768]{2,1,0:T(8,128)(2,1)S(1)}, u32[]{:S(2)}, u32[]{:S(2)}) %collective-permute-start.9) | collective-permute-done | bytes 589856 | tf_op jit(solution)/shard_map/ppermute | solution.py:77
  91.9 13.6 %collective-permute-done.3 = bf16[256,768]{1,0:T(8,128)(2,1)S(1)} collective-permute-done((bf16[256,768]{1,0:T(8,128)(2,1)S(1)}, bf16[256,768]{1,0:T(8,128)(2,1)S(1)}, u32[]{:S(2)}, u32[]{:S(2)}) %collective-permute-start.3) | collective-permute-done | bytes 393248 | tf_op jit(solution)/shard_map/ppermute | solution.py:77
  113.7 2.6 fusion.38
  123.5 2.4 convolution_convert_fusion.3
  126.0 4.6 select_reduce_fusion
  130.6 5.7 %fusion = f32[12,256]{1,0:T(8,128)S(1)} fusion(f32[12,256,1792]{2,1,0:T(8,128)S(1)} %get-tuple-element.122, f32[12,256]{1,0:T(8,128)S(1)} %get-tuple-element.121, pred[256,1792]{1,0:T(8,128)(4,1)S(1)} %concatenate.91), kind=kLoop, calls=%fused_computation.9 | loop fusion | flops 16512000 | bytes 22503424 | tf_op jit(solution)/shard_map/reduce_sum | solution.py:195
  136.3 3.0 copy-done
  143.3 10.2 %fusion.40 = bf16[12,64,256]{2,1,0:T(8,128)(2,1)S(1)} fusion(bf16[1792,12,64]{0,2,1:T(8,128)(2,1)S(1)} %bitcast.282, f32[12,256,1792]{2,1,0:T(8,128)} %copy-done, f32[12,256]{1,0:T(8,128)S(1)} %fusion, f32[12,256]{1,0:T(8,128)S(1)} %get-tuple-element.121, pred[256,1792]{1,0:T(8,128)(4,1)S(1)} %concatenate.91), kind=kOutput, calls=%fused_computation.81 | convolution fusion | flops 726859776 | bytes 25649152 | tf_op jit(solution)/shard_map/hqk,khd->qhd/dot_general | solution.py:197
  155.0 6.6 %fusion.107 = (bf16[32,96,768]{2,1,0:T(8,128)(2,1)}, bf16[32,96,768]{2,1,0:T(8,128)(2,1)S(1)}) fusion(bf16[32,216,768]{2,1,0:T(8,128)(2,1)} %bitcast.258), kind=kLoop, calls=%fused_computation.305 | loop fusion | bytes 18874368 | tf_op jit(solution)/shard_map/slice | solution.py:281
  165.9 8.3 %fusion.21 = (bf16[256,3072]{1,0:T(8,128)(2,1)S(1)}, f32[256,3072]{1,0:T(8,128)S(1)}) fusion(f32[3072]{0:T(1024)S(1)} %reshape.400, bf16[768,3072]{1,0:T(8,128)(2,1)S(1)} %bitcast.264, f32[256,768]{1,0:T(8,128)S(1)} %get-tuple-element.124, f32[768]{0:T(1024)S(1)} %add.654, f32[768]{0:T(1024)S(1)} %mul.197, f32[256]{0:T(256)S(1)} %add_rsqrt_fusion.1, ...), kind=kOutput, calls=%fused_computation.38 | convolution fusion | flops 1260847104 | bytes 10244096 | tf_op jit(solution)/shard_map/dot_general | solution.py:22
  178.7 3.6 convolution_convert_fusion
  182.3 3.0 fusion.115
  185.3 3.7 convolution_convert_fusion.1
  194.3 16.1 %multiply_reduce_fusion = (f32[12,256]{1,0:T(8,128)S(1)}, f32[12,256,1792]{2,1,0:T(8,128)}) fusion(f32[12,256,1792]{2,1,0:T(8,128)} %copy-done, f32[12,256]{1,0:T(8,128)S(1)} %log_add_fusion, pred[256,1792]{1,0:T(8,128)(4,1)S(1)} %concatenate.91, bf16[256,12,64]{0,2,1:T(8,128)(2,1)S(1)} %bitcast.276, bf16[1792,12,64]{0,2,1:T(8,128)(2,1)} %bitcast.283), kind=kOutput, calls=%fused_computation.5 | convolution fusion | flops 726660096 | bytes 47669248 | tf_op jit(solution)/shard_map/qhd,khd->hqk/dot_general | solution.py:206
  210.4 12.0 %bitcast_reduce_fusion = (bf16[12,64]{1,0:T(8,128)(2,1)}, bf16[12,64,1792]{2,1,0:T(8,128)(2,1)}) fusion(bf16[256,12,64]{0,2,1:T(8,128)(2,1)S(1)} %bitcast.277, f32[12,256,1792]{2,1,0:T(8,128)} %copy-done, f32[12,256]{1,0:T(8,128)S(1)} %log_add_fusion, pred[256,1792]{1,0:T(8,128)(4,1)S(1)} %concatenate.91), kind=kOutput, calls=%fused_computation.58 | convolution fusion | flops 723909888 | bytes 25638400 | tf_op jit(solution)/shard_map/hqk,qhd->khd/dot_general | solution.py:211
  222.4 15.0 %multiply_convert_fusion = bf16[12,256,1792]{2,1,0:T(8,128)(2,1)S(1)} fusion(f32[12,256,1792]{2,1,0:T(8,128)} %get-tuple-element.131, f32[12,256,1792]{2,1,0:T(8,128)} %copy-done, f32[12,256]{1,0:T(8,128)S(1)} %get-tuple-element.130, f32[12,256]{1,0:T(8,128)S(1)} %log_add_fusion, pred[256,1792]{1,0:T(8,128)(4,1)S(1)} %concatenate.91), kind=kLoop, calls=%fused_computation.4 | loop fusion | flops 27525120 | bytes 55533568 | tf_op jit(solution)/shard_map/convert_element_type | solution.py:208
  237.4 3.6 convolution_convert_fusion.2
  241.0 5.3 %convert_reduce_fusion = (f32[12,64]{1,0:T(8,128)S(1)}, bf16[12,64,256]{2,1,0:T(8,128)(2,1)S(1)}) fusion(bf16[1792,12,64]{0,2,1:T(8,128)(2,1)} %bitcast.252, bf16[12,256,1792]{2,1,0:T(8,128)(2,1)S(1)} %multiply_convert_fusion), kind=kOutput, calls=%fused_computation.111 | convolution fusion | flops 705232128 | bytes 14158848 | tf_op jit(solution)/shard_map/hqk,khd->qhd/dot_general | solution.py:209
  255.5 4.8 %fusion.116 = f32[1792,768]{1,0:T(8,128)} fusion(bf16[1792,768]{0,1:T(8,128)(2,1)S(1)} %bitcast.280, bf16[768,768]{1,0:T(8,128)(2,1)S(1)} %bitcast.289), kind=kOutput, calls=%fused_computation.314 | convolution fusion | flops 2113929216 | bytes 9437184 | tf_op jit(solution)/shard_map/dot_general | solution.py:26
  260.3 6.1 %fusion.13 = bf16[768,1536]{1,0:T(8,128)(2,1)S(1)} fusion(bf16[1792,768]{1,0:T(8,128)(2,1)S(1)} %copy-done.33, bf16[1792,768]{0,1:T(8,128)(2,1)S(1)} %bitcast.281, bf16[1792,768]{0,1:T(8,128)(2,1)S(1)} %bitcast.246), kind=kOutput, calls=%fused_computation.33 | convolution fusion | flops 4240048128 | bytes 10616832 | tf_op jit(solution)/shard_map/dot_general | solution.py:30
  294.3 2.4 fusion.114
  302.0 2.5 collective-permute-done.37
  309.3 15.7 %collective-permute-start.41 = (bf16[1,1,24,768]{3,2,1,0:T(8,128)(2,1)S(1)}, bf16[1,1,24,768]{3,2,1,0:T(8,128)(2,1)S(1)}, u32[]{:S(2)}, u32[]{:S(2)}) collective-permute-start(bf16[1,1,24,768]{3,2,1,0:T(8,128)(2,1)S(1)} %get-tuple-element.94), channel_id=1, source_target_pairs={{0,4},{1,5},{2,6},{3,7},{4,0},{5,1},{6,2},{7,3},{8,12},{9,13},{10,... | collective-permute-start | bytes 110600 | tf_op jit(solution)/shard_map/ppermute | solution.py:77
  331.5 4.3 collective-permute-done.23
  335.8 2.6 collective-permute-start.25
  339.1 3.4 collective-permute-done.25
  344.8 7.6 %collective-permute-start.27 = (bf16[1,1,32,768]{3,2,1,0:T(8,128)(2,1)S(1)}, bf16[1,1,32,768]{3,2,1,0:T(8,128)(2,1)S(1)}, u32[]{:S(2)}, u32[]{:S(2)}) collective-permute-start(bf16[1,1,32,768]{3,2,1,0:T(8,128)(2,1)S(1)} %get-tuple-element.89), channel_id=1, source_target_pairs={{0,4},{1,5},{2,6},{3,7},{4,0},{5,1},{6,2},{7,3},{8,12},{9,13},{10,... | collective-permute-start | bytes 147464 | tf_op jit(solution)/shard_map/ppermute | solution.py:77
  354.5 3.8 collective-permute-done.28
  365.5 9.9 %collective-permute-done.30 = bf16[1,2,2,1,24,1536]{5,4,3,2,1,0:T(8,128)(2,1)S(1)} collective-permute-done((bf16[1,2,2,1,24,1536]{5,4,3,2,1,0:T(8,128)(2,1)S(1)}, bf16[1,2,2,1,24,1536]{5,4,3,2,1,0:T(8,128)(2,1)S(1)}, u32[]{:S(2)}, u32[]{:S(2)}) %collective-permute-start.30) | collective-permute-done | bytes 294944 | tf_op jit(solution)/shard_map/ppermute | solution.py:77
  379.4 3.8 collective-permute-done.20
  383.1 6.8 %collective-permute-start.34 = (bf16[1,1,24,1536]{3,2,1,0:T(8,128)(2,1)S(1)}, bf16[1,1,24,1536]{3,2,1,0:T(8,128)(2,1)S(1)}, u32[]{:S(2)}, u32[]{:S(2)}) collective-permute-start(bf16[1,1,24,1536]{3,2,1,0:T(8,128)(2,1)S(1)} %get-tuple-element.84), channel_id=1, source_target_pairs={{0,4},{1,5},{2,6},{3,7},{4,0},{5,1},{6,2},{7,3},{8,12},{9,13},{10,... | collective-permute-start | bytes 221192 | tf_op jit(solution)/shard_map/ppermute | solution.py:77
  390.0 7.2 %collective-permute-done.19 = bf16[256,768]{1,0:T(8,128)(2,1)S(1)} collective-permute-done((bf16[256,768]{1,0:T(8,128)(2,1)S(1)}, bf16[256,768]{1,0:T(8,128)(2,1)S(1)}, u32[]{:S(2)}, u32[]{:S(2)}) %collective-permute-start.19) | collective-permute-done | bytes 393248 | tf_op jit(solution)/shard_map/ppermute | solution.py:81
  398.7 4.6 collective-permute-done.35
  405.1 2.7 collective-permute-start.53
  409.8 11.2 %collective-permute-done.51 = bf16[1,2,2,1,96,768]{5,4,3,2,1,0:T(8,128)(2,1)S(1)} collective-permute-done((bf16[1,2,2,1,96,768]{5,4,3,2,1,0:T(8,128)(2,1)S(1)}, bf16[1,2,2,1,96,768]{5,4,3,2,1,0:T(8,128)(2,1)S(1)}, u32[]{:S(2)}, u32[]{:S(2)}) %collective-permute-start.51) | collective-permute-done | bytes 589856 | tf_op jit(solution)/shard_map/ppermute | solution.py:77
  422.0 12.8 %collective-permute-done.53 = bf16[1,2,2,1,96,768]{5,4,3,2,1,0:T(8,128)(2,1)S(1)} collective-permute-done((bf16[1,2,2,1,96,768]{5,4,3,2,1,0:T(8,128)(2,1)S(1)}, bf16[1,2,2,1,96,768]{5,4,3,2,1,0:T(8,128)(2,1)S(1)}, u32[]{:S(2)}, u32[]{:S(2)}) %collective-permute-start.53) | collective-permute-done | bytes 589856 | tf_op jit(solution)/shard_map/ppermute | solution.py:77
  435.7 4.2 collective-permute-done.44
  440.1 7.4 %collective-permute-done.46 = bf16[1,2,2,1,24,3072]{5,4,3,2,1,0:T(8,128)(2,1)S(1)} collective-permute-done((bf16[1,2,2,1,24,3072]{5,4,3,2,1,0:T(8,128)(2,1)S(1)}, bf16[1,2,2,1,24,3072]{5,4,3,2,1,0:T(8,128)(2,1)S(1)}, u32[]{:S(2)}, u32[]{:S(2)}) %collective-permute-start.46) | collective-permute-done | bytes 589856 | tf_op jit(solution)/shard_map/ppermute | solution.py:77
  448.3 4.0 collective-permute-start.49
  454.6 2.7 collective-permute-done.48
  (330 shorter events, 143.8 us)
Async XLA Ops:
  7.2 146.3 %all-gather.2.cloned.1.call-start = ((), (), s32[]{:S(2)}) async-start(), calls=%async_computation | async-start | bytes 10948608 | tf_op jit(solution)/shard_map/all_gather | solution.py:251
  9.9 44.6 %collective-permute-start = (bf16[256,768]{1,0:T(8,128)(2,1)}, bf16[256,768]{1,0:T(8,128)(2,1)S(1)}, u32[]{:S(2)}, u32[]{:S(2)}) collective-permute-start(bf16[256,768]{1,0:T(8,128)(2,1)} %bitcast.259), channel_id=1, source_target_pairs={{0,4},{1,5},{2,6},{3,7},{8,12},{9,13},{10,14},{11,15},{16,20},{17,... | collective-permute-start | bytes 1179656 | tf_op jit(solution)/shard_map/ppermute | solution.py:81
  15.9 89.6 %collective-permute-start.4 = (bf16[256,768]{1,0:T(8,128)(2,1)}, bf16[256,768]{1,0:T(8,128)(2,1)}, u32[]{:S(2)}, u32[]{:S(2)}) collective-permute-start(bf16[256,768]{1,0:T(8,128)(2,1)} %bitcast.260), channel_id=1, source_target_pairs={{0,1},{1,0},{2,3},{3,2},{4,5},{5,4},{6,7},{7,6},{8,9},{9,8},{10,11... | collective-permute-start | bytes 1179656 | tf_op jit(solution)/shard_map/ppermute | solution.py:77
  24.4 9.4 %collective-permute-start.11 = (bf16[1,32,768]{2,1,0:T(8,128)(2,1)S(1)}, bf16[1,32,768]{2,1,0:T(8,128)(2,1)S(1)}, u32[]{:S(2)}, u32[]{:S(2)}) collective-permute-start(bf16[1,32,768]{2,1,0:T(8,128)(2,1)S(1)} %fusion.91), channel_id=1, source_target_pairs={{0,2},{1,3},{2,0},{3,1},{4,6},{5,7},{6,4},{7,5},{8,10},{9,11},{10,... | collective-permute-start | bytes 147464 | tf_op jit(solution)/shard_map/ppermute | solution.py:77
  33.8 12.1 %collective-permute-start.12 = (bf16[2,32,768]{2,1,0:T(8,128)(2,1)S(1)}, bf16[2,32,768]{2,1,0:T(8,128)(2,1)S(1)}, u32[]{:S(2)}, u32[]{:S(2)}) collective-permute-start(bf16[2,32,768]{2,1,0:T(8,128)(2,1)S(1)} %pad_maximum_fusion.6), channel_id=1, source_target_pairs={{0,4},{1,5},{2,6},{3,7},{4,0},{5,1},{6,2},{7,3},{8,12},{9,13},{10,... | collective-permute-start | bytes 294920 | tf_op jit(solution)/shard_map/ppermute | solution.py:77
  34.6 13.7 %collective-permute-start.7 = (bf16[2,48,768]{2,1,0:T(8,128)(2,1)S(1)}, bf16[2,48,768]{2,1,0:T(8,128)(2,1)S(1)}, u32[]{:S(2)}, u32[]{:S(2)}) collective-permute-start(bf16[2,48,768]{2,1,0:T(8,128)(2,1)S(1)} %pad_maximum_fusion.5), channel_id=1, source_target_pairs={{0,4},{1,5},{2,6},{3,7},{4,0},{5,1},{6,2},{7,3},{8,12},{9,13},{10,... | collective-permute-start | bytes 442376 | tf_op jit(solution)/shard_map/ppermute | solution.py:77
  48.3 16.1 %collective-permute-start.8 = (bf16[4,48,768]{2,1,0:T(8,128)(2,1)S(1)}, bf16[4,48,768]{2,1,0:T(8,128)(2,1)S(1)}, u32[]{:S(2)}, u32[]{:S(2)}) collective-permute-start(bf16[4,48,768]{2,1,0:T(8,128)(2,1)S(1)} %pad_maximum_fusion.3), channel_id=1, source_target_pairs={{0,16},{1,17},{2,18},{3,19},{4,20},{5,21},{6,22},{7,23},{8,24},{9,... | collective-permute-start | bytes 884744 | tf_op jit(solution)/shard_map/ppermute | solution.py:77
  53.3 21.2 %collective-permute-start.14 = (bf16[8,32,768]{2,1,0:T(8,128)(2,1)S(1)}, bf16[8,32,768]{2,1,0:T(8,128)(2,1)S(1)}, u32[]{:S(2)}, u32[]{:S(2)}) collective-permute-start(bf16[8,32,768]{2,1,0:T(8,128)(2,1)S(1)} %pad_maximum_fusion.1), channel_id=1, source_target_pairs={{0,16},{1,17},{2,18},{3,19},{4,20},{5,21},{6,22},{7,23},{8,24},{9,... | collective-permute-start | bytes 1179656 | tf_op jit(solution)/shard_map/ppermute | solution.py:77
  54.6 20.6 %collective-permute-start.1 = (bf16[256,768]{1,0:T(8,128)(2,1)S(1)}, bf16[256,768]{1,0:T(8,128)(2,1)S(1)}, u32[]{:S(2)}, u32[]{:S(2)}) collective-permute-start(bf16[256,768]{1,0:T(8,128)(2,1)S(1)} %get-tuple-element.37), channel_id=1, source_target_pairs={{0,2},{1,3},{2,0},{3,1},{4,6},{5,7},{6,4},{7,5},{8,10},{9,11},{10,... | collective-permute-start | bytes 1179656 | tf_op jit(solution)/shard_map/ppermute | solution.py:77
  62.5 16.6 %collective-permute-start.2 = (bf16[256,768]{1,0:T(8,128)(2,1)S(1)}, bf16[256,768]{1,0:T(8,128)(2,1)S(1)}, u32[]{:S(2)}, u32[]{:S(2)}) collective-permute-start(bf16[256,768]{1,0:T(8,128)(2,1)S(1)} %get-tuple-element.37), channel_id=1, source_target_pairs={{0,1},{1,0},{2,3},{3,2},{4,5},{5,4},{6,7},{7,6},{8,9},{9,8},{10,11... | collective-permute-start | bytes 1179656 | tf_op jit(solution)/shard_map/ppermute | solution.py:77
  64.4 26.3 %collective-permute-start.9 = (bf16[8,48,768]{2,1,0:T(8,128)(2,1)S(1)}, bf16[8,48,768]{2,1,0:T(8,128)(2,1)S(1)}, u32[]{:S(2)}, u32[]{:S(2)}) collective-permute-start(bf16[8,48,768]{2,1,0:T(8,128)(2,1)S(1)} %pad_maximum_fusion), channel_id=1, source_target_pairs={{0,1},{1,0},{2,3},{3,2},{4,5},{5,4},{6,7},{7,6},{8,9},{9,8},{10,11... | collective-permute-start | bytes 1769480 | tf_op jit(solution)/shard_map/ppermute | solution.py:77
  74.5 32.0 %collective-permute-start.5 = (bf16[256,768]{1,0:T(8,128)(2,1)S(1)}, bf16[256,768]{1,0:T(8,128)(2,1)S(1)}, u32[]{:S(2)}, u32[]{:S(2)}) collective-permute-start(bf16[256,768]{1,0:T(8,128)(2,1)S(1)} %bitcast.261), channel_id=1, source_target_pairs={{5,6},{6,5},{13,14},{14,13},{21,22},{22,21},{29,30},{30,29}} | collective-permute-start | bytes 1179656 | tf_op jit(solution)/shard_map/ppermute | solution.py:81
  75.2 30.2 %collective-permute-start.3 = (bf16[256,768]{1,0:T(8,128)(2,1)S(1)}, bf16[256,768]{1,0:T(8,128)(2,1)S(1)}, u32[]{:S(2)}, u32[]{:S(2)}) collective-permute-start(bf16[256,768]{1,0:T(8,128)(2,1)S(1)} %collective-permute-done.1), channel_id=1, source_target_pairs={{0,1},{1,0},{2,3},{3,2},{4,5},{5,4},{6,7},{7,6},{8,9},{9,8},{10,11... | collective-permute-start | bytes 1179656 | tf_op jit(solution)/shard_map/ppermute | solution.py:77
  79.1 27.5 %collective-permute-start.15 = (bf16[16,32,768]{2,1,0:T(8,128)(2,1)S(1)}, bf16[16,32,768]{2,1,0:T(8,128)(2,1)S(1)}, u32[]{:S(2)}, u32[]{:S(2)}) collective-permute-start(bf16[16,32,768]{2,1,0:T(8,128)(2,1)S(1)} %get-tuple-element.80), channel_id=1, source_target_pairs={{0,8},{1,9},{2,10},{3,11},{4,12},{5,13},{6,14},{7,15},{8,0},{9,1},... | collective-permute-start | bytes 2359304 | tf_op jit(solution)/shard_map/ppermute | solution.py:77
  91.9 24.4 %collective-permute-start.10 = (bf16[16,48,768]{2,1,0:T(8,128)(2,1)}, bf16[16,48,768]{2,1,0:T(8,128)(2,1)}, u32[]{:S(2)}, u32[]{:S(2)}) collective-permute-start(bf16[16,48,768]{2,1,0:T(8,128)(2,1)} %get-tuple-element.78), channel_id=1, source_target_pairs={{0,8},{1,9},{2,10},{3,11},{4,12},{5,13},{6,14},{7,15},{8,0},{9,1},... | collective-permute-start | bytes 3538952 | tf_op jit(solution)/shard_map/ppermute | solution.py:77
  255.3 41.4 %collective-permute-start.36 = (bf16[2,1,2,2,2,24,768]{6,5,3,2,4,1,0:T(8,128)(2,1)}, bf16[2,1,2,2,2,24,768]{6,5,3,2,4,1,0:T(8,128)(2,1)}, u32[]{:S(2)}, u32[]{:S(2)}) collective-permute-start(bf16[2,1,2,2,2,24,768]{6,5,3,2,4,1,0:T(8,128)(2,1)} %copy.100), channel_id=1, source_target_pairs={{0,8},{1,9},{2,10},{3,11},{4,12},{5,13},{6,14},{7,15},{8,0},{9,1},... | collective-permute-start | bytes 1769480 | tf_op jit(solution)/shard_map/ppermute | solution.py:77
  268.8 90.2 %collective-permute-start.29 = (bf16[2,1,2,2,2,24,1536]{6,5,3,2,4,1,0:T(8,128)(2,1)}, bf16[2,1,2,2,2,24,1536]{6,5,3,2,4,1,0:T(8,128)(2,1)}, u32[]{:S(2)}, u32[]{:S(2)}) collective-permute-start(bf16[2,1,2,2,2,24,1536]{6,5,3,2,4,1,0:T(8,128)(2,1)} %copy.98), channel_id=1, source_target_pairs={{0,8},{1,9},{2,10},{3,11},{4,12},{5,13},{6,14},{7,15},{8,0},{9,1},... | collective-permute-start | bytes 3538952 | tf_op jit(solution)/shard_map/ppermute | solution.py:77
  292.1 32.8 %collective-permute-start.22 = (bf16[2,1,2,2,2,32,768]{6,5,3,2,4,1,0:T(8,128)(2,1)S(1)}, bf16[2,1,2,2,2,32,768]{6,5,3,2,4,1,0:T(8,128)(2,1)S(1)}, u32[]{:S(2)}, u32[]{:S(2)}) collective-permute-start(bf16[2,1,2,2,2,32,768]{6,5,3,2,4,1,0:T(8,128)(2,1)S(1)} %copy.96), channel_id=1, source_target_pairs={{0,8},{1,9},{2,10},{3,11},{4,12},{5,13},{6,14},{7,15},{8,0},{9,1},... | collective-permute-start | bytes 2359304 | tf_op jit(solution)/shard_map/ppermute | solution.py:77
  300.4 8.7 %collective-permute-start.39 = (bf16[1,2,2,1,24,768]{5,4,3,2,1,0:T(8,128)(2,1)S(1)}, bf16[1,2,2,1,24,768]{5,4,3,2,1,0:T(8,128)(2,1)S(1)}, u32[]{:S(2)}, u32[]{:S(2)}) collective-permute-start(bf16[1,2,2,1,24,768]{5,4,3,2,1,0:T(8,128)(2,1)S(1)} %get-tuple-element.76), channel_id=1, source_target_pairs={{0,17},{1,16},{2,19},{3,18},{4,21},{5,20},{6,23},{7,22},{8,25},{9,... | collective-permute-start | bytes 442376 | tf_op jit(solution)/shard_map/ppermute | solution.py:77
  304.5 22.1 %collective-permute-start.17 = (bf16[256,768]{1,0:T(8,128)(2,1)S(1)}, bf16[256,768]{1,0:T(8,128)(2,1)S(1)}, u32[]{:S(2)}, u32[]{:S(2)}) collective-permute-start(bf16[256,768]{1,0:T(8,128)(2,1)S(1)} %get-tuple-element.47), channel_id=1, source_target_pairs={{0,1},{1,0},{2,3},{3,2},{4,5},{5,4},{6,7},{7,6},{8,9},{9,8},{10,11... | collective-permute-start | bytes 1179656 | tf_op jit(solution)/shard_map/ppermute | solution.py:77
  309.2 19.3 %collective-permute-start.40 = (bf16[1,1,24,768]{3,2,1,0:T(8,128)(2,1)S(1)}, bf16[1,1,24,768]{3,2,1,0:T(8,128)(2,1)S(1)}, u32[]{:S(2)}, u32[]{:S(2)}) collective-permute-start(bf16[1,1,24,768]{3,2,1,0:T(8,128)(2,1)S(1)} %get-tuple-element.92), channel_id=1, source_target_pairs={{0,2},{1,3},{2,0},{3,1},{4,6},{5,7},{6,4},{7,5},{8,10},{9,11},{10,... | collective-permute-start | bytes 110600 | tf_op jit(solution)/shard_map/ppermute | solution.py:77
  309.3 19.6 %collective-permute-start.41 = (bf16[1,1,24,768]{3,2,1,0:T(8,128)(2,1)S(1)}, bf16[1,1,24,768]{3,2,1,0:T(8,128)(2,1)S(1)}, u32[]{:S(2)}, u32[]{:S(2)}) collective-permute-start(bf16[1,1,24,768]{3,2,1,0:T(8,128)(2,1)S(1)} %get-tuple-element.94), channel_id=1, source_target_pairs={{0,4},{1,5},{2,6},{3,7},{4,0},{5,1},{6,2},{7,3},{8,12},{9,13},{10,... | collective-permute-start | bytes 110600 | tf_op jit(solution)/shard_map/ppermute | solution.py:77
  326.6 9.2 %collective-permute-start.23 = (bf16[1,2,2,1,32,768]{5,4,3,2,1,0:T(8,128)(2,1)S(1)}, bf16[1,2,2,1,32,768]{5,4,3,2,1,0:T(8,128)(2,1)S(1)}, u32[]{:S(2)}, u32[]{:S(2)}) collective-permute-start(bf16[1,2,2,1,32,768]{5,4,3,2,1,0:T(8,128)(2,1)S(1)} %get-tuple-element.66), channel_id=1, source_target_pairs={{0,1},{1,0},{2,3},{3,2},{4,5},{5,4},{6,7},{7,6},{8,9},{9,8},{10,11... | collective-permute-start | bytes 589832 | tf_op jit(solution)/shard_map/ppermute | solution.py:77
  328.5 16.3 %collective-permute-start.16 = (bf16[256,768]{1,0:T(8,128)(2,1)S(1)}, bf16[256,768]{1,0:T(8,128)(2,1)S(1)}, u32[]{:S(2)}, u32[]{:S(2)}) collective-permute-start(bf16[256,768]{1,0:T(8,128)(2,1)S(1)} %get-tuple-element.44), channel_id=1, source_target_pairs={{0,1},{1,0},{2,3},{3,2},{4,5},{5,4},{6,7},{7,6},{8,9},{9,8},{10,11... | collective-permute-start | bytes 1179656 | tf_op jit(solution)/shard_map/ppermute | solution.py:77
  328.9 23.6 %collective-permute-start.18 = (bf16[256,768]{1,0:T(8,128)(2,1)S(1)}, bf16[256,768]{1,0:T(8,128)(2,1)S(1)}, u32[]{:S(2)}, u32[]{:S(2)}) collective-permute-start(bf16[256,768]{1,0:T(8,128)(2,1)S(1)} %fusion.59), channel_id=1, source_target_pairs={{0,2},{1,3},{2,0},{3,1},{4,6},{5,7},{6,4},{7,5},{8,10},{9,11},{10,... | collective-permute-start | bytes 1179656 | tf_op jit(solution)/shard_map/ppermute | solution.py:77
  330.8 8.3 %collective-permute-start.24 = (bf16[1,2,2,1,32,768]{5,4,3,2,1,0:T(8,128)(2,1)S(1)}, bf16[1,2,2,1,32,768]{5,4,3,2,1,0:T(8,128)(2,1)S(1)}, u32[]{:S(2)}, u32[]{:S(2)}) collective-permute-start(bf16[1,2,2,1,32,768]{5,4,3,2,1,0:T(8,128)(2,1)S(1)} %get-tuple-element.68), channel_id=1, source_target_pairs={{0,16},{1,17},{2,18},{3,19},{4,20},{5,21},{6,22},{7,23},{8,24},{9,... | collective-permute-start | bytes 589832 | tf_op jit(solution)/shard_map/ppermute | solution.py:77
  339.1 64.3 %collective-permute-start.50 = (bf16[2,1,2,2,2,96,768]{6,5,3,2,4,1,0:T(8,128)(2,1)S(1)}, bf16[2,1,2,2,2,96,768]{6,5,3,2,4,1,0:T(8,128)(2,1)S(1)}, u32[]{:S(2)}, u32[]{:S(2)}) collective-permute-start(bf16[2,1,2,2,2,96,768]{6,5,3,2,4,1,0:T(8,128)(2,1)S(1)} %copy-done.21), channel_id=1, source_target_pairs={{0,8},{1,9},{2,10},{3,11},{4,12},{5,13},{6,14},{7,15},{8,0},{9,1},... | collective-permute-start | bytes 7077896 | tf_op jit(solution)/shard_map/ppermute | solution.py:77
  342.7 9.9 %collective-permute-start.26 = (bf16[1,1,32,768]{3,2,1,0:T(8,128)(2,1)S(1)}, bf16[1,1,32,768]{3,2,1,0:T(8,128)(2,1)S(1)}, u32[]{:S(2)}, u32[]{:S(2)}) collective-permute-start(bf16[1,1,32,768]{3,2,1,0:T(8,128)(2,1)S(1)} %get-tuple-element.87), channel_id=1, source_target_pairs={{0,2},{1,3},{2,0},{3,1},{4,6},{5,7},{6,4},{7,5},{8,10},{9,11},{10,... | collective-permute-start | bytes 147464 | tf_op jit(solution)/shard_map/ppermute | solution.py:77
  344.8 9.7 %collective-permute-start.27 = (bf16[1,1,32,768]{3,2,1,0:T(8,128)(2,1)S(1)}, bf16[1,1,32,768]{3,2,1,0:T(8,128)(2,1)S(1)}, u32[]{:S(2)}, u32[]{:S(2)}) collective-permute-start(bf16[1,1,32,768]{3,2,1,0:T(8,128)(2,1)S(1)} %get-tuple-element.89), channel_id=1, source_target_pairs={{0,4},{1,5},{2,6},{3,7},{4,0},{5,1},{6,2},{7,3},{8,12},{9,13},{10,... | collective-permute-start | bytes 147464 | tf_op jit(solution)/shard_map/ppermute | solution.py:77
  352.6 55.2 %collective-permute-start.43 = (bf16[2,1,2,2,2,24,3072]{6,5,3,2,4,1,0:T(8,128)(2,1)S(1)}, bf16[2,1,2,2,2,24,3072]{6,5,3,2,4,1,0:T(8,128)(2,1)S(1)}, u32[]{:S(2)}, u32[]{:S(2)}) collective-permute-start(bf16[2,1,2,2,2,24,3072]{6,5,3,2,4,1,0:T(8,128)(2,1)S(1)} %copy-done.20), channel_id=1, source_target_pairs={{0,8},{1,9},{2,10},{3,11},{4,12},{5,13},{6,14},{7,15},{8,0},{9,1},... | collective-permute-start | bytes 7077896 | tf_op jit(solution)/shard_map/ppermute | solution.py:77
  360.7 14.7 %collective-permute-start.30 = (bf16[1,2,2,1,24,1536]{5,4,3,2,1,0:T(8,128)(2,1)S(1)}, bf16[1,2,2,1,24,1536]{5,4,3,2,1,0:T(8,128)(2,1)S(1)}, u32[]{:S(2)}, u32[]{:S(2)}) collective-permute-start(bf16[1,2,2,1,24,1536]{5,4,3,2,1,0:T(8,128)(2,1)S(1)} %get-tuple-element.62), channel_id=1, source_target_pairs={{0,1},{1,0},{2,3},{3,2},{4,5},{5,4},{6,7},{7,6},{8,9},{9,8},{10,11... | collective-permute-start | bytes 884744 | tf_op jit(solution)/shard_map/ppermute | solution.py:77
  362.0 14.9 %collective-permute-start.31 = (bf16[1,2,2,1,24,1536]{5,4,3,2,1,0:T(8,128)(2,1)S(1)}, bf16[1,2,2,1,24,1536]{5,4,3,2,1,0:T(8,128)(2,1)S(1)}, u32[]{:S(2)}, u32[]{:S(2)}) collective-permute-start(bf16[1,2,2,1,24,1536]{5,4,3,2,1,0:T(8,128)(2,1)S(1)} %get-tuple-element.64), channel_id=1, source_target_pairs={{0,16},{1,17},{2,18},{3,19},{4,20},{5,21},{6,22},{7,23},{8,24},{9,... | collective-permute-start | bytes 884744 | tf_op jit(solution)/shard_map/ppermute | solution.py:77
  362.7 14.9 %collective-permute-start.32 = (bf16[1,2,2,1,24,1536]{5,4,3,2,1,0:T(8,128)(2,1)S(1)}, bf16[1,2,2,1,24,1536]{5,4,3,2,1,0:T(8,128)(2,1)S(1)}, u32[]{:S(2)}, u32[]{:S(2)}) collective-permute-start(bf16[1,2,2,1,24,1536]{5,4,3,2,1,0:T(8,128)(2,1)S(1)} %get-tuple-element.63), channel_id=1, source_target_pairs={{0,17},{1,16},{2,19},{3,18},{4,21},{5,20},{6,23},{7,22},{8,25},{9,... | collective-permute-start | bytes 884744 | tf_op jit(solution)/shard_map/ppermute | solution.py:77
  375.4 7.8 %collective-permute-start.20 = (bf16[256,768]{1,0:T(8,128)(2,1)S(1)}, bf16[256,768]{1,0:T(8,128)(2,1)S(1)}, u32[]{:S(2)}, u32[]{:S(2)}) collective-permute-start(bf16[256,768]{1,0:T(8,128)(2,1)S(1)} %get-tuple-element.46), channel_id=1, source_target_pairs={{0,1},{1,0},{2,3},{3,2},{4,5},{5,4},{6,7},{7,6},{8,9},{9,8},{10,11... | collective-permute-start | bytes 1179656 | tf_op jit(solution)/shard_map/ppermute | solution.py:77
  377.7 19.5 %collective-permute-start.19 = (bf16[256,768]{1,0:T(8,128)(2,1)S(1)}, bf16[256,768]{1,0:T(8,128)(2,1)S(1)}, u32[]{:S(2)}, u32[]{:S(2)}) collective-permute-start(bf16[256,768]{1,0:T(8,128)(2,1)S(1)} %fusion.78), channel_id=1, source_target_pairs={{4,0},{5,1},{6,2},{7,3},{12,8},{13,9},{14,10},{15,11},{20,16},{21,... | collective-permute-start | bytes 1179656 | tf_op jit(solution)/shard_map/ppermute | solution.py:81
  383.1 15.5 %collective-permute-start.33 = (bf16[1,1,24,1536]{3,2,1,0:T(8,128)(2,1)S(1)}, bf16[1,1,24,1536]{3,2,1,0:T(8,128)(2,1)S(1)}, u32[]{:S(2)}, u32[]{:S(2)}) collective-permute-start(bf16[1,1,24,1536]{3,2,1,0:T(8,128)(2,1)S(1)} %get-tuple-element.82), channel_id=1, source_target_pairs={{0,2},{1,3},{2,0},{3,1},{4,6},{5,7},{6,4},{7,5},{8,10},{9,11},{10,... | collective-permute-start | bytes 221192 | tf_op jit(solution)/shard_map/ppermute | solution.py:77
  383.1 15.5 %collective-permute-start.34 = (bf16[1,1,24,1536]{3,2,1,0:T(8,128)(2,1)S(1)}, bf16[1,1,24,1536]{3,2,1,0:T(8,128)(2,1)S(1)}, u32[]{:S(2)}, u32[]{:S(2)}) collective-permute-start(bf16[1,1,24,1536]{3,2,1,0:T(8,128)(2,1)S(1)} %get-tuple-element.84), channel_id=1, source_target_pairs={{0,4},{1,5},{2,6},{3,7},{4,0},{5,1},{6,2},{7,3},{8,12},{9,13},{10,... | collective-permute-start | bytes 221192 | tf_op jit(solution)/shard_map/ppermute | solution.py:77
  404.3 16.7 %collective-permute-start.51 = (bf16[1,2,2,1,96,768]{5,4,3,2,1,0:T(8,128)(2,1)S(1)}, bf16[1,2,2,1,96,768]{5,4,3,2,1,0:T(8,128)(2,1)S(1)}, u32[]{:S(2)}, u32[]{:S(2)}) collective-permute-start(bf16[1,2,2,1,96,768]{5,4,3,2,1,0:T(8,128)(2,1)S(1)} %get-tuple-element.48), channel_id=1, source_target_pairs={{0,1},{1,0},{2,3},{3,2},{4,5},{5,4},{6,7},{7,6},{8,9},{9,8},{10,11... | collective-permute-start | bytes 1769480 | tf_op jit(solution)/shard_map/ppermute | solution.py:77
  404.4 17.7 %collective-permute-start.52 = (bf16[1,2,2,1,96,768]{5,4,3,2,1,0:T(8,128)(2,1)S(1)}, bf16[1,2,2,1,96,768]{5,4,3,2,1,0:T(8,128)(2,1)S(1)}, u32[]{:S(2)}, u32[]{:S(2)}) collective-permute-start(bf16[1,2,2,1,96,768]{5,4,3,2,1,0:T(8,128)(2,1)S(1)} %get-tuple-element.50), channel_id=1, source_target_pairs={{0,16},{1,17},{2,18},{3,19},{4,20},{5,21},{6,22},{7,23},{8,24},{9,... | collective-permute-start | bytes 1769480 | tf_op jit(solution)/shard_map/ppermute | solution.py:77
  405.1 29.7 %collective-permute-start.53 = (bf16[1,2,2,1,96,768]{5,4,3,2,1,0:T(8,128)(2,1)S(1)}, bf16[1,2,2,1,96,768]{5,4,3,2,1,0:T(8,128)(2,1)S(1)}, u32[]{:S(2)}, u32[]{:S(2)}) collective-permute-start(bf16[1,2,2,1,96,768]{5,4,3,2,1,0:T(8,128)(2,1)S(1)} %get-tuple-element.49), channel_id=1, source_target_pairs={{0,17},{1,16},{2,19},{3,18},{4,21},{5,20},{6,23},{7,22},{8,25},{9,... | collective-permute-start | bytes 1769480 | tf_op jit(solution)/shard_map/ppermute | solution.py:77
  408.9 31.0 %collective-permute-start.44 = (bf16[1,2,2,1,24,3072]{5,4,3,2,1,0:T(8,128)(2,1)S(1)}, bf16[1,2,2,1,24,3072]{5,4,3,2,1,0:T(8,128)(2,1)S(1)}, u32[]{:S(2)}, u32[]{:S(2)}) collective-permute-start(bf16[1,2,2,1,24,3072]{5,4,3,2,1,0:T(8,128)(2,1)S(1)} %get-tuple-element.51), channel_id=1, source_target_pairs={{0,1},{1,0},{2,3},{3,2},{4,5},{5,4},{6,7},{7,6},{8,9},{9,8},{10,11... | collective-permute-start | bytes 1769480 | tf_op jit(solution)/shard_map/ppermute | solution.py:77
  409.1 31.0 %collective-permute-start.45 = (bf16[1,2,2,1,24,3072]{5,4,3,2,1,0:T(8,128)(2,1)S(1)}, bf16[1,2,2,1,24,3072]{5,4,3,2,1,0:T(8,128)(2,1)S(1)}, u32[]{:S(2)}, u32[]{:S(2)}) collective-permute-start(bf16[1,2,2,1,24,3072]{5,4,3,2,1,0:T(8,128)(2,1)S(1)} %get-tuple-element.53), channel_id=1, source_target_pairs={{0,16},{1,17},{2,18},{3,19},{4,20},{5,21},{6,22},{7,23},{8,24},{9,... | collective-permute-start | bytes 1769480 | tf_op jit(solution)/shard_map/ppermute | solution.py:77
  420.9 26.6 %collective-permute-start.46 = (bf16[1,2,2,1,24,3072]{5,4,3,2,1,0:T(8,128)(2,1)S(1)}, bf16[1,2,2,1,24,3072]{5,4,3,2,1,0:T(8,128)(2,1)S(1)}, u32[]{:S(2)}, u32[]{:S(2)}) collective-permute-start(bf16[1,2,2,1,24,3072]{5,4,3,2,1,0:T(8,128)(2,1)S(1)} %get-tuple-element.52), channel_id=1, source_target_pairs={{0,17},{1,16},{2,19},{3,18},{4,21},{5,20},{6,23},{7,22},{8,25},{9,... | collective-permute-start | bytes 1769480 | tf_op jit(solution)/shard_map/ppermute | solution.py:77
  435.2 13.1 %collective-permute-start.54 = (bf16[1,1,96,768]{3,2,1,0:T(8,128)(2,1)S(1)}, bf16[1,1,96,768]{3,2,1,0:T(8,128)(2,1)S(1)}, u32[]{:S(2)}, u32[]{:S(2)}) collective-permute-start(bf16[1,1,96,768]{3,2,1,0:T(8,128)(2,1)S(1)} %get-tuple-element.69), channel_id=1, source_target_pairs={{0,2},{1,3},{2,0},{3,1},{4,6},{5,7},{6,4},{7,5},{8,10},{9,11},{10,... | collective-permute-start | bytes 442376 | tf_op jit(solution)/shard_map/ppermute | solution.py:77
  435.3 17.1 %collective-permute-start.55 = (bf16[1,1,96,768]{3,2,1,0:T(8,128)(2,1)S(1)}, bf16[1,1,96,768]{3,2,1,0:T(8,128)(2,1)S(1)}, u32[]{:S(2)}, u32[]{:S(2)}) collective-permute-start(bf16[1,1,96,768]{3,2,1,0:T(8,128)(2,1)S(1)} %get-tuple-element.71), channel_id=1, source_target_pairs={{0,4},{1,5},{2,6},{3,7},{4,0},{5,1},{6,2},{7,3},{8,12},{9,13},{10,... | collective-permute-start | bytes 442376 | tf_op jit(solution)/shard_map/ppermute | solution.py:77
  439.9 12.5 %collective-permute-start.56 = (bf16[1,1,96,768]{3,2,1,0:T(8,128)(2,1)S(1)}, bf16[1,1,96,768]{3,2,1,0:T(8,128)(2,1)S(1)}, u32[]{:S(2)}, u32[]{:S(2)}) collective-permute-start(bf16[1,1,96,768]{3,2,1,0:T(8,128)(2,1)S(1)} %get-tuple-element.70), channel_id=1, source_target_pairs={{0,6},{1,7},{2,4},{3,5},{4,2},{5,3},{6,0},{7,1},{8,14},{9,15},{10,... | collective-permute-start | bytes 442376 | tf_op jit(solution)/shard_map/ppermute | solution.py:77
  448.0 9.3 %collective-permute-start.48 = (bf16[1,1,24,3072]{3,2,1,0:T(8,128)(2,1)S(1)}, bf16[1,1,24,3072]{3,2,1,0:T(8,128)(2,1)S(1)}, u32[]{:S(2)}, u32[]{:S(2)}) collective-permute-start(bf16[1,1,24,3072]{3,2,1,0:T(8,128)(2,1)S(1)} %get-tuple-element.74), channel_id=1, source_target_pairs={{0,4},{1,5},{2,6},{3,7},{4,0},{5,1},{6,2},{7,3},{8,12},{9,13},{10,... | collective-permute-start | bytes 442376 | tf_op jit(solution)/shard_map/ppermute | solution.py:77
  448.3 9.0 %collective-permute-start.49 = (bf16[1,1,24,3072]{3,2,1,0:T(8,128)(2,1)S(1)}, bf16[1,1,24,3072]{3,2,1,0:T(8,128)(2,1)S(1)}, u32[]{:S(2)}, u32[]{:S(2)}) collective-permute-start(bf16[1,1,24,3072]{3,2,1,0:T(8,128)(2,1)S(1)} %get-tuple-element.73), channel_id=1, source_target_pairs={{0,6},{1,7},{2,4},{3,5},{4,2},{5,3},{6,0},{7,1},{8,14},{9,15},{10,... | collective-permute-start | bytes 442376 | tf_op jit(solution)/shard_map/ppermute | solution.py:77
  (52 other events, 602.9 us)
Sparse Core Ops, SparseCore 0:
  11.6 117.7 all-gather.1

commit v3 on v2

v3 whole, which is shorter than its diff:
```python
import functools

import jax
import jax.numpy as jnp
import numpy as np
from jax import lax
from jax.experimental import pallas as pl
from jax.experimental.pallas import tpu as pltpu
from jax.sharding import PartitionSpec as P

HEADS = 12
HDIM = 64
PROMPT = 1024
CONT_MOST = 256
BF = jnp.bfloat16
F32 = jnp.float32

NORM_EPS = 1e-12
MASK_FILL = -1000000000.0
SQRT_HALF = 0.7071067811865476
INV_ROOT_TAU = 0.3989422804014327
AXES = ("grp", "row")


def mm(left, right):
    return jnp.dot(left, right, preferred_element_type=F32)


def segment_ids(lengths, group_len):
    ends = jnp.cumsum(lengths)
    places = jnp.arange(group_len, dtype=jnp.int32)
    passed = jnp.sum(((places - PROMPT)[:, None] >= ends[None, :]).astype(jnp.int32), axis=-1)
    return jnp.where(places < PROMPT, 0, 1 + passed)


class Plan:
    def __init__(self, grp, row):
        self.grp, self.row, self.count = grp, row, grp * row
        self.y = row // 4
        bits = lambda base, size: [base << i for i in range(size.bit_length() - 1)]
        ys, zs = bits(1, self.y), bits(self.y, 4)
        core, xs = bits(row, 2), bits(2 * row, grp // 2)
        self.orders = (tuple(zs + ys + xs + core), tuple(zs + xs + ys + core))
        flat = [ys + xs] if len(ys + xs) == 2 else [ys, xs]
        self.scatter_stages = [core] + flat + [zs]
        self.bits = (grp * row).bit_length() - 1

    def swap(self, value, mask):
        return lax.ppermute(value, AXES, [(i, i ^ mask) for i in range(self.count)])

    def send(self, value, moves):
        pairs = [(g * self.row + a, g * self.row + b) for g in range(self.grp) for a, b in moves]
        return lax.ppermute(value, AXES, pairs)

    def me(self):
        return lax.axis_index("grp") * self.row + lax.axis_index("row")

    def gather(self, value, order):
        held, masks = value[None], [0]
        for bit in order:
            held = jnp.concatenate([held, self.swap(held, bit)], 0)
            masks = masks + [m ^ bit for m in masks]
        slot = np.zeros(self.count, np.int32)
        for j, m in enumerate(masks):
            slot[m] = j
        places = jnp.asarray(slot)[self.me() ^ jnp.arange(self.count)]
        return jnp.take(held, places, axis=0, mode="clip")


    def scatter(self, value, before=0):
        me = self.me()
        lead, rest = value.shape[:before], value.shape[before + 1 :]
        left = [1 << i for i in reversed(range(self.bits))]
        value = value.astype(BF).reshape(list(lead) + [2] * self.bits + list(rest))
        for stage in self.scatter_stages:

            def part(array, mask):
                for bit in stage:
                    axis = before + at.index(bit)
                    place = ((me ^ mask) // bit) & 1
                    array = lax.dynamic_slice_in_dim(array, place, 1, axis)
                return array

            at = left
            masks = [0]
            for bit in stage:
                masks = masks + [m ^ bit for m in masks]
            total = part(value, 0).astype(F32)
            for mask in masks[1:]:
                total = total + self.swap(part(value, mask), mask).astype(F32)
            left = [b for b in left if b not in stage]
            shape = list(lead) + [2] * len(left) + list(rest)
            value = total.reshape(shape)
            if left:
                value = value.astype(BF)
        return value


def token_blocks(plan, own, rows):
    row = lax.axis_index("row")
    if plan.row != 8:
        every = lax.all_gather(own, "row", axis=0, tiled=True)
        start = jnp.maximum(row * rows - CONT_MOST, 0)
        padded = jnp.concatenate([every, jnp.zeros((CONT_MOST, own.shape[1]), own.dtype)], 0)
        near = lax.dynamic_slice_in_dim(padded, start, rows + 2 * CONT_MOST, 0)
        every = jnp.concatenate([every[:PROMPT], near], 0)
        spots = [every[i : i + rows] for i in range(0, every.shape[0], rows)]
        return spots, jnp.where(row * rows < PROMPT, 0, near.shape[0] // rows)
    across = plan.send(own, [(0, 4), (1, 5), (2, 6), (3, 7)])
    same = jnp.where(row < 4, own, across)
    beside = plan.swap(own, 1)
    diagonal = plan.send(own, [(5, 6), (6, 5)])
    other = plan.swap(same, 2)
    same_y = plan.swap(same, 1)
    other_y = plan.swap(other, 1)
    near = jnp.where(row < 4, 0, jnp.where((row == 5) | (row == 6), 3, 2))
    return [same, other, same_y, other_y, own, beside, diagonal], near


def near_segments(plan, segments, rows):
    row = lax.axis_index("row")
    if plan.row != 8:
        start = jnp.maximum(row * rows - CONT_MOST, 0)
        padded = jnp.concatenate([segments, jnp.full((CONT_MOST,), -1, jnp.int32)], 0)
        near = lax.dynamic_slice_in_dim(padded, start, rows + 2 * CONT_MOST, 0)
        return jnp.where((near == 0) | (row * rows < PROMPT), -1, near)
    pieces = []
    for block, valid in (
        (row, row >= 4),
        (row ^ 1, row >= 4),
        (11 - row, (row == 5) | (row == 6)),
    ):
        block = jnp.clip(block, 0, 7)
        ids = lax.dynamic_slice_in_dim(segments, block * rows, rows, 0)
        pieces.append(jnp.where(valid, ids, -1))
    return jnp.concatenate(pieces, 0)


def token_return(plan, parts, rows):
    row = lax.axis_index("row")
    if plan.row != 8:
        parts = parts.reshape(-1, parts.shape[-1]).astype(F32)
        start = jnp.maximum(row * rows - CONT_MOST, 0)
        whole = jnp.zeros((plan.row * rows + CONT_MOST, parts.shape[1]), F32)
        whole = whole.at[:PROMPT].set(parts[:PROMPT])
        near = jnp.where(row * rows < PROMPT, 0, parts[PROMPT:])
        near = lax.dynamic_slice_in_dim(whole, start, rows + 2 * CONT_MOST, 0) + near
        whole = lax.dynamic_update_slice_in_dim(whole, near, start, 0)
        return lax.psum_scatter(whole[: plan.row * rows], "row", scatter_dimension=0, tiled=True)
    same, other, same_y, other_y, own, beside, diagonal = [parts[i] for i in range(7)]
    low = lambda v: v.astype(BF)
    wide = lambda v: v.astype(F32)
    other = wide(other) + wide(plan.swap(other_y, 1))
    same = wide(same) + wide(plan.swap(same_y, 1))
    own = wide(own) + wide(plan.swap(beside, 1))
    own = own + wide(plan.send(diagonal, [(5, 6), (6, 5)]))
    same = same + wide(plan.swap(low(other), 2))
    back = plan.send(low(same), [(4, 0), (5, 1), (6, 2), (7, 3)])
    return jnp.where(row < 4, same + wide(back), own)


def heads_mask(lanes, head):
    lane = lax.broadcasted_iota(jnp.int32, lanes, 1)
    return (lane >= head * HDIM) & (lane < (head + 1) * HDIM)


def nt(left, right):
    return lax.dot_general(left, right, (((1,), (1,)), ((), ())), preferred_element_type=F32)


def tn(left, right):
    return lax.dot_general(left, right, (((0,), (0,)), ((), ())), preferred_element_type=F32)


def attention_kernel(blocks, first, rows, *refs):
    spots = refs[:blocks]
    (near_ref, own_ref, wq_ref, wk_ref, wv_ref, bq_ref, bv_ref, segq_ref, segk_ref,
     q_ref, k_ref, v_ref, ctx_ref, lse_ref, x_ref, s_ref, sems) = refs[blocks:]
    near = near_ref[0]

    @pl.when(pl.program_id(0) == 0)
    def _():
        copies = [
            pltpu.make_async_copy(spot, x_ref.at[pl.ds(i * rows, rows)], sems.at[i])
            for i, spot in enumerate(spots)
        ]
        for copy in copies:
            copy.start()
        for copy in copies:
            copy.wait()

    queries = (mm(own_ref[...], wq_ref[...]) + bq_ref[...]) * (HDIM**-0.5)
    q_ref[...] = queries.astype(BF)

    @pl.loop(0, first + near)
    def _(b):
        here = pl.ds(pl.multiple_of(b * rows, rows), rows)
        x = x_ref[here, :]
        k_ref[here, :] = mm(x, wk_ref[...]).astype(BF)
        v_ref[here, :] = (mm(x, wv_ref[...]) + bv_ref[...]).astype(BF)

    width = q_ref.shape[1]
    heads = width // HDIM
    q = q_ref[...]
    parts = [jnp.where(heads_mask(q.shape, h), q, 0) for h in range(heads)]

    def scores(b, peaks, masked):
        here = pl.ds(pl.multiple_of(b * rows, rows), rows)
        k = k_ref[here, :]
        out = []
        for h in range(heads):
            s = nt(k, parts[h])
            if masked:
                side = pl.ds(pl.multiple_of((b - first) * rows, rows), rows)
                s = jnp.where(segk_ref[side, :] == segq_ref[...], s, MASK_FILL)
            s_ref[h, here, :] = s
            out.append(jnp.maximum(peaks[h], jnp.max(s, axis=0, keepdims=True)))
        return tuple(out)

    peaks = tuple(jnp.full((1, rows), MASK_FILL, F32) for _ in range(heads))
    peaks = lax.fori_loop(0, first, lambda b, c: scores(b, c, False), peaks)
    peaks = lax.fori_loop(first, first + near, lambda b, c: scores(b, c, True), peaks)

    def mix(b, carry):
        totals, mixed = carry
        here = pl.ds(pl.multiple_of(b * rows, rows), rows)
        vt = v_ref[here, :].T
        new_totals, new_mixed = [], []
        for h in range(heads):
            p = jnp.exp(s_ref[h, here, :] - peaks[h])
            new_totals.append(totals[h] + jnp.sum(p, axis=0, keepdims=True))
            new_mixed.append(mixed[h] + mm(vt[h * HDIM : (h + 1) * HDIM], p.astype(BF)))
        return tuple(new_totals), tuple(new_mixed)

    zero = (
        tuple(jnp.zeros((1, rows), F32) for _ in range(heads)),
        tuple(jnp.zeros((HDIM, rows), F32) for _ in range(heads)),
    )
    totals, mixed = lax.fori_loop(0, first + near, mix, zero)
    whole = jnp.concatenate([mixed[h] / totals[h] for h in range(heads)], 0)
    ctx_ref[...] = whole.T.astype(BF)
    for h in range(heads):
        lse_ref[0, h : h + 1, :] = peaks[h] + jnp.log(totals[h])


def attention_call(spots, first, near, own, wq, wk, wv, bq, bv, segq, segk):
    rows, width = own.shape
    blocks = len(spots)
    tall = blocks * rows
    part = 256
    steps = width // part
    heads = part // HDIM
    cols = lambda depth: pl.BlockSpec((depth, part), lambda g: (0, g))
    flops = 2 * tall * width * width * 2 + 4 * tall * rows * width * 4
    return pl.pallas_call(
        functools.partial(attention_kernel, blocks, first, rows),
        grid=(steps,),
        in_specs=[pl.BlockSpec(memory_space=pl.ANY)] * blocks
        + [
            pl.BlockSpec(memory_space=pltpu.SMEM),
            pl.BlockSpec((rows, width), lambda g: (0, 0)),
            cols(width), cols(width), cols(width), cols(1), cols(1),
            pl.BlockSpec((1, rows), lambda g: (0, 0)),
            pl.BlockSpec(segk.shape, lambda g: (0, 0)),
        ],
        out_specs=[
            cols(rows), cols(tall), cols(tall), cols(rows),
            pl.BlockSpec((1, 8, rows), lambda g: (g, 0, 0)),
        ],
        out_shape=[
            jax.ShapeDtypeStruct((rows, width), BF),
            jax.ShapeDtypeStruct((tall, width), BF),
            jax.ShapeDtypeStruct((tall, width), BF),
            jax.ShapeDtypeStruct((rows, width), BF),
            jax.ShapeDtypeStruct((steps, 8, rows), F32),
        ],
        scratch_shapes=[
            pltpu.VMEM((tall, width), BF),
            pltpu.VMEM((heads, tall, rows), F32),
            pltpu.SemaphoreType.DMA((blocks,)),
        ],
        compiler_params=pltpu.CompilerParams(vmem_limit_bytes=60 * 2**20),
        cost_estimate=pl.CostEstimate(
            flops=flops, bytes_accessed=12 * 2**20, transcendentals=tall * rows * 12
        ),
        name="attention",
    )(*spots, near, own, wq, wk, wv, bq, bv, segq, segk)


def middle_kernel(wide, ctx_ref, own_ref, cot_ref, wo_ref, wi_ref, wu_ref, vec_ref, bin_ref,
                  out_ref, h1_ref, gctx_ref, dwo_ref, dwi_ref, dwu_ref, sums_ref, sbin_ref,
                  first_ref, n1_ref, inv_ref, low_ref, pre_ref, cdf_ref, act_ref, acc_ref,
                  gffn_ref, glow_ref):
    step = pl.program_id(0)
    width = ctx_ref.shape[1]
    vec = lambda i: vec_ref[i : i + 1, :]
    mean = lambda v: jnp.sum(v, axis=-1, keepdims=True) * (1.0 / width)
    down = lambda v: jnp.sum(v, axis=0, keepdims=True)

    @pl.when(step == 0)
    def _():
        hidden = own_ref[...].astype(F32) + mm(ctx_ref[...], wo_ref[...]) + vec(0)
        centred = hidden - mean(hidden)
        inverse = lax.rsqrt(mean(centred * centred) + NORM_EPS)
        normed = centred * inverse
        n1_ref[...] = normed
        inv_ref[...] = inverse
        first = normed * vec(1) + vec(2)
        first_ref[...] = first
        low_ref[...] = first.astype(BF)

    @pl.when(step < wide)
    def _():
        chunk = pl.ds(pl.multiple_of(step * width, width), width)
        pre = mm(low_ref[...], wi_ref[0]) + bin_ref[pl.ds(step, 1), :]
        cdf = 0.5 * (1.0 + lax.erf(pre * SQRT_HALF))
        act = (pre * cdf).astype(BF)
        pre_ref[:, chunk] = pre
        cdf_ref[:, chunk] = cdf
        act_ref[:, chunk] = act
        more = mm(act, wu_ref[...])

        @pl.when(step == 0)
        def _():
            acc_ref[...] = more

        @pl.when(step > 0)
        def _():
            acc_ref[...] += more

    @pl.when(step == wide - 1)
    def _():
        hidden = first_ref[...] + acc_ref[...] + vec(3)
        centred = hidden - mean(hidden)
        inverse = lax.rsqrt(mean(centred * centred) + NORM_EPS)
        normed = centred * inverse
        out_ref[...] = (normed * vec(4) + vec(5)).astype(BF)
        grad = cot_ref[...].astype(F32)
        sums_ref[0:1, :] = down(grad * normed)
        sums_ref[1:2, :] = down(grad)
        e = grad * vec(4)
        back = inverse * (e - mean(e) - normed * mean(e * normed))
        gffn_ref[...] = back
        low = back.astype(BF)
        glow_ref[...] = low
        sums_ref[2:3, :] = down(low.astype(F32))

    @pl.when(step >= wide)
    def _():
        at = 2 * wide - 1 - step
        chunk = pl.ds(pl.multiple_of(at * width, width), width)
        pre = pre_ref[:, chunk]
        slope = cdf_ref[:, chunk] + pre * jnp.exp(-0.5 * pre * pre) * INV_ROOT_TAU
        low = glow_ref[...]
        grad = (nt(low, wu_ref[...]) * slope).astype(BF)
        sbin_ref[pl.ds(at, 1), :] = down(grad.astype(F32))
        dwu_ref[...] = tn(act_ref[:, chunk], low).astype(BF)
        dwi_ref[0] = tn(low_ref[...], grad).astype(BF)
        gffn_ref[...] += nt(grad, wi_ref[0])

    @pl.when(step == 2 * wide - 1)
    def _():
        grad = gffn_ref[...]
        normed = n1_ref[...]
        sums_ref[3:4, :] = down(grad * normed)
        sums_ref[4:5, :] = down(grad)
        e = grad * vec(1)
        back = inv_ref[...] * (e - mean(e) - normed * mean(e * normed))
        h1_ref[...] = back
        low = back.astype(BF)
        sums_ref[5:6, :] = down(low.astype(F32))
        sums_ref[6:8, :] = jnp.zeros((2, width), F32)
        dwo_ref[...] = tn(ctx_ref[...], low).astype(BF)
        gctx_ref[...] = nt(low, wo_ref[...]).astype(BF)


def middle_call(ctx, own, cot, wo, wi, wu, vec, b_inner):
    rows, width = own.shape
    wide = wi.shape[0]
    whole = lambda shape: pl.BlockSpec(shape, lambda s: (0,) * len(shape))
    at = lambda s: jnp.where(s < wide, s, 2 * wide - 1 - s)
    back = lambda s: jnp.where(s < wide, wide - 1, 2 * wide - 1 - s)
    shape = jax.ShapeDtypeStruct
    return pl.pallas_call(
        functools.partial(middle_kernel, wide),
        grid=(2 * wide,),
        in_specs=[
            whole((rows, width)), whole((rows, width)), whole((rows, width)), whole((width, width)),
            pl.BlockSpec((1, width, width), lambda s: (at(s), 0, 0)),
            pl.BlockSpec((width, width), lambda s: (at(s), 0)),
            whole((8, width)), whole((8, width)),
        ],
        out_specs=[
            whole((rows, width)), whole((rows, width)), whole((rows, width)), whole((width, width)),
            pl.BlockSpec((1, width, width), lambda s: (back(s), 0, 0)),
            pl.BlockSpec((width, width), lambda s: (back(s), 0)),
            whole((8, width)), whole((8, width)),
        ],
        out_shape=[
            shape((rows, width), BF), shape((rows, width), F32), shape((rows, width), BF),
            shape((width, width), BF), shape((wide, width, width), BF),
            shape((wide * width, width), BF), shape((8, width), F32), shape((8, width), F32),
        ],
        scratch_shapes=[
            pltpu.VMEM((rows, width), F32), pltpu.VMEM((rows, width), F32), pltpu.VMEM((rows, 1), F32),
            pltpu.VMEM((rows, width), BF), pltpu.VMEM((rows, wide * width), F32),
            pltpu.VMEM((rows, wide * width), F32), pltpu.VMEM((rows, wide * width), BF),
            pltpu.VMEM((rows, width), F32), pltpu.VMEM((rows, width), F32),
            pltpu.VMEM((rows, width), BF),
        ],
        compiler_params=pltpu.CompilerParams(vmem_limit_bytes=60 * 2**20),
        cost_estimate=pl.CostEstimate(
            flops=2 * rows * width * width * (6 * wide + 3), bytes_accessed=32 * 2**20,
            transcendentals=2 * rows * width * wide,
        ),
        name="middle",
    )(ctx, own, cot, wo, wi, wu, vec, b_inner)


def back_kernel(blocks, first, rows, *refs):
    spots = refs[:blocks]
    (near_ref, own_ref, gctx_ref, ctx_ref, q_ref, k_ref, v_ref, lse_ref, wq_ref, wk_ref, wv_ref,
     segq_ref, segk_ref, h1_ref, dw_ref, gx_ref, gown_ref, sums_ref,
     x_ref, dk_ref, dv_ref, acc_ref, keep_ref, sems) = refs[blocks:]
    near = near_ref[0]
    step = pl.program_id(0)

    @pl.when(step == 0)
    def _():
        copies = [
            pltpu.make_async_copy(spot, x_ref.at[pl.ds(i * rows, rows)], sems.at[i])
            for i, spot in enumerate(spots)
        ]
        for copy in copies:
            copy.start()
        for copy in copies:
            copy.wait()
        acc_ref[...] = jnp.zeros_like(acc_ref)
        keep_ref[...] = h1_ref[...]

    q, g = q_ref[...], gctx_ref[...]
    part = q.shape[1]
    heads = part // HDIM
    masks = [heads_mask(q.shape, h) for h in range(heads)]
    q_parts = [jnp.where(m, q, 0) for m in masks]
    g_parts = [jnp.where(m, g, 0) for m in masks]
    product = (g.astype(F32) * ctx_ref[...].astype(F32)).T
    inner = [
        jnp.sum(product[h * HDIM : (h + 1) * HDIM], axis=0, keepdims=True) for h in range(heads)
    ]

    def one(b, dq, masked):
        here = pl.ds(pl.multiple_of(b * rows, rows), rows)
        k, v = k_ref[here, :], v_ref[here, :]
        kt = k.T
        if masked:
            side = pl.ds(pl.multiple_of((b - first) * rows, rows), rows)
            allowed = segk_ref[side, :] == segq_ref[...]
        dk = jnp.zeros((rows, part), F32)
        dv = jnp.zeros((rows, part), F32)
        out = []
        for h in range(heads):
            s = nt(k, q_parts[h])
            if masked:
                s = jnp.where(allowed, s, MASK_FILL)
            p = jnp.exp(s - lse_ref[0, h : h + 1, :])
            dp = nt(v, g_parts[h])
            ds = (p * (dp - inner[h])).astype(BF)
            dv = dv + mm(p.astype(BF), g_parts[h])
            dk = dk + mm(ds, q_parts[h])
            out.append(dq[h] + mm(kt[h * HDIM : (h + 1) * HDIM], ds))
        dk_ref[here, :] = dk.astype(BF)
        dv_ref[here, :] = dv.astype(BF)
        return tuple(out)

    dq = tuple(jnp.zeros((HDIM, rows), F32) for _ in range(heads))
    dq = lax.fori_loop(0, first, lambda b, c: one(b, c, False), dq)
    dq = lax.fori_loop(first, first + near, lambda b, c: one(b, c, True), dq)
    dq_low = jnp.concatenate(dq, 0).T.astype(BF)
    scale = HDIM**-0.5
    keep_ref[...] += nt(dq_low, wq_ref[...]) * scale
    dw_ref[:, 0:part] = (tn(own_ref[...], dq_low) * scale).astype(BF)
    sums_ref[0:1, :] = jnp.sum(dq_low.astype(F32), axis=0, keepdims=True) * scale

    def products(b, carry):
        here = pl.ds(pl.multiple_of(b * rows, rows), rows)
        dk, dv, x = dk_ref[here, :], dv_ref[here, :], x_ref[here, :]
        acc_ref[here, :] += nt(dk, wk_ref[...]) + nt(dv, wv_ref[...])
        wk, wv, bv = carry
        bv = bv + jnp.sum(dv.astype(F32), axis=0, keepdims=True)
        return wk + tn(x, dk), wv + tn(x, dv), bv

    width = x_ref.shape[1]
    zero = jnp.zeros((width, part), F32)
    wk, wv, bv = lax.fori_loop(0, first + near, products, (zero, zero, jnp.zeros((1, part), F32)))
    dw_ref[:, part : 2 * part] = wk.astype(BF)
    dw_ref[:, 2 * part :] = wv.astype(BF)
    sums_ref[1:2, :] = bv
    sums_ref[2:8, :] = jnp.zeros((6, part), F32)

    @pl.when(step == pl.num_programs(0) - 1)
    def _():
        gown_ref[...] = keep_ref[...]
        for b in range(blocks):
            gx_ref[b] = acc_ref[b * rows : (b + 1) * rows, :].astype(BF)


def back_call(spots, first, near, own, gctx, ctx, q, k, v, lse, wq, wk, wv, segq, segk, h1):
    rows, width = own.shape
    blocks = len(spots)
    tall = blocks * rows
    part = 256
    steps = width // part
    cols = lambda depth: pl.BlockSpec((depth, part), lambda g: (0, g))
    whole = lambda shape: pl.BlockSpec(shape, lambda g: (0,) * len(shape))
    flops = 2 * tall * width * width * 4 + 10 * tall * rows * width * 4
    shape = jax.ShapeDtypeStruct
    return pl.pallas_call(
        functools.partial(back_kernel, blocks, first, rows),
        grid=(steps,),
        in_specs=[pl.BlockSpec(memory_space=pl.ANY)] * blocks
        + [
            pl.BlockSpec(memory_space=pltpu.SMEM),
            whole((rows, width)),
            cols(rows), cols(rows), cols(rows), cols(tall), cols(tall),
            pl.BlockSpec((1, 8, rows), lambda g: (g, 0, 0)),
            cols(width), cols(width), cols(width),
            whole((1, rows)), whole(segk.shape), whole((rows, width)),
        ],
        out_specs=[
            pl.BlockSpec((width, 3 * part), lambda g: (0, g)),
            whole((blocks, rows, width)), whole((rows, width)), cols(8),
        ],
        out_shape=[
            shape((width, 3 * width), BF), shape((blocks, rows, width), BF),
            shape((rows, width), F32), shape((8, width), F32),
        ],
        scratch_shapes=[
            pltpu.VMEM((tall, width), BF), pltpu.VMEM((tall, part), BF), pltpu.VMEM((tall, part), BF),
            pltpu.VMEM((tall, width), F32), pltpu.VMEM((rows, width), F32),
            pltpu.SemaphoreType.DMA((blocks,)),
        ],
        compiler_params=pltpu.CompilerParams(vmem_limit_bytes=60 * 2**20),
        cost_estimate=pl.CostEstimate(
            flops=flops, bytes_accessed=24 * 2**20, transcendentals=tall * rows * 12
        ),
        name="attention_back",
    )(*spots, near, own, gctx, ctx, q, k, v, lse, wq, wk, wv, segq, segk, h1)


def solution(mesh):
    plan = Plan(mesh.shape["grp"], mesh.shape["row"])

    def per_device(
        tokens, cont_lengths, cotangent, w_query, w_key, w_value, w_output, w_inner, w_outer,
        bias_query, bias_value, bias_output, gain_first, shift_first, bias_inner, bias_outer,
        gain_second, shift_second,
    ):
        count = plan.count
        _, rows, width = tokens.shape
        step = w_query.shape[0]
        wide = w_inner.shape[1] // width
        row = lax.axis_index("row")
        scale = HDIM ** (-0.5)
        own = tokens[0]

        vectors = (
            bias_query, bias_value, bias_output, gain_first, shift_first, bias_outer, gain_second,
            shift_second, bias_inner,
        )
        line = jnp.concatenate(vectors)
        small = len(vectors) - 1
        line = jnp.pad(line, (0, width - line.shape[0]))[None]
        line = jnp.pad(line, ((0, 7), (0, 0)))
        pack_a = jnp.concatenate([w_query, line], 0)
        pack_b = jnp.concatenate([w_key, w_value], 0)
        got_a = plan.gather(pack_a, plan.orders[0])
        got_b = plan.gather(pack_b, plan.orders[1])
        spots, near = token_blocks(plan, own, rows)
        first_near = PROMPT // rows

        inner_rows = w_inner.reshape(step, wide, width).transpose(1, 0, 2).reshape(-1, width)
        pack_c = jnp.concatenate([w_output, inner_rows, w_outer], 0)
        got_c = lax.all_gather(pack_c, AXES, axis=0, tiled=True).reshape(count, -1, width)

        full_query = got_a[:, :step].reshape(width, width)
        lines = got_a[:, step]
        table = lines[:, : small * step].reshape(count, small, step).transpose(1, 0, 2)
        table = table.reshape(small, width).astype(F32)
        v_bin = lines[:, small * step : (small + wide) * step].reshape(wide, width).astype(F32)
        v_bin = jnp.pad(v_bin, ((0, 8 - wide), (0, 0)))
        full_key = got_b[:, :step].reshape(width, width)
        full_value = got_b[:, step : 2 * step].reshape(width, width)

        segments = segment_ids(cont_lengths[0], plan.row * rows)
        seg_own = lax.dynamic_slice_in_dim(segments, row * rows, rows, 0)[None, :]
        seg_near = near_segments(plan, segments, rows)[:, None]
        near = near.astype(jnp.int32).reshape(1)

        queries, keys, values, context, log_total = attention_call(
            spots, first_near, near, own, full_query, full_key, full_value, table[0:1], table[1:2],
            seg_own, seg_near,
        )

        full_output = got_c[:, :step].reshape(width, width)
        full_inner = got_c[:, step : step * (1 + wide)].reshape(count, wide, step, width)
        full_inner = full_inner.transpose(1, 0, 2, 3).reshape(wide, width, width)
        full_outer = got_c[:, step * (1 + wide) :].reshape(wide * width, width)
        vec = jnp.concatenate([table[2:], jnp.zeros((2, width), F32)], 0)
        layer_out, grad_h1, grad_context, d_output, d_inner, d_outer, sums, sums_bin = middle_call(
            context, own, cotangent[0], full_output, full_inner, full_outer, vec, v_bin
        )
        by_owner = lambda grad: grad.reshape(count, step, -1)
        o_outer = plan.scatter(d_outer.reshape(count, wide * step, width))
        o_inner = plan.scatter(d_inner.reshape(wide, count, step, width), 1)
        o_output = plan.scatter(by_owner(d_output))

        d_qkv, shared, grad_own, sums_qkv = back_call(
            spots, first_near, near, own, grad_context, context, queries, keys, values, log_total,
            full_query, full_key, full_value, seg_own, seg_near, grad_h1,
        )
        grad_tokens = grad_own + token_return(plan, shared, rows)

        order = (5, 3, 4, 2, 0, 1)
        d_table = jnp.concatenate([sums_qkv[:2]] + [sums[i : i + 1] for i in order], 0)
        d_lines = jnp.concatenate(
            [
                d_table.reshape(small, count, step).transpose(1, 0, 2).reshape(count, -1),
                sums_bin[:wide].reshape(count, wide * step),
            ],
            1,
        )
        d_lines = jnp.pad(d_lines, ((0, 0), (0, width - d_lines.shape[1])))[:, None]
        o_line = plan.scatter(jnp.pad(d_lines, ((0, 0), (0, 7), (0, 0))))[0]
        parts = 3 * width // 768
        o_qkv = plan.scatter(by_owner(d_qkv)).reshape(step, parts, 3, width // parts)

        o_small = [o_line[i * step : (i + 1) * step] for i in range(small)]
        o_bin = o_line[small * step : (small + wide) * step]
        return (
            layer_out[None],
            grad_tokens.astype(BF)[None],
            o_qkv[:, :, 0].reshape(step, width),
            o_qkv[:, :, 1].reshape(step, width),
            o_qkv[:, :, 2].reshape(step, width),
            o_output,
            o_inner.transpose(1, 0, 2).reshape(step, wide * width),
            o_outer,
            o_small[0],
            o_small[1],
            o_small[2],
            o_small[3],
            o_small[4],
            o_bin,
            o_small[5],
            o_small[6],
            o_small[7],
        )

    split = P("grp", "row", None)
    owned2, owned1 = P(AXES, None), P(AXES)
    in_specs = (split, P("grp", None), split) + (owned2,) * 6 + (owned1,) * 9
    out_specs = (split, split) + (owned2,) * 6 + (owned1,) * 9
    return jax.shard_map(
        per_device, mesh=mesh, in_specs=in_specs, out_specs=out_specs, check_vma=False
    )
```

time: 475 us -> 425 us (0.89); the launches traced: 465 us -> 423 us
  matrix products: 99.6 us -> 0 us
  Pallas kernels: 0 us -> 74.1 us
  starting transfers between devices: 92 us -> 125 us
  local copies, waits for them, and re-layouts: 86 us -> 60.4 us
  other arithmetic: 40.7 us -> 22.3 us
    dot_general x23 -> x0, matrix products: 99.6 us -> none  [the longest x6 17.9 us: mm(): return jnp.dot(left, right, preferred_element_type=F32)]
    pallas_call x0 -> x3, Pallas kernels: none -> 74.1 us  [the longest x1 35.5 us: back_call(): pl.pallas_call(functools.partial(back_kernel, blocks, first, rows), grid=...]
    ppermute x53, starting transfers between devices: 83.2 us -> 115 us  [swap(): return lax.ppermute(value, AXES, [(i, i ^ mask) for i in range(self.count)])]
    unnamed x110 -> x46, local copies, waits for them, and re-layouts: 29.6 us -> 8.47 us
    convert_element_type x2 -> x0, other arithmetic: 15.1 us -> none  [the longest x1 15 us: attend_back(): grad_scores = (shares * (grad_shares - inner)).astype(BF)]
    reduce_sum x7 -> x0, other arithmetic: 9.73 us -> none  [the longest x1 5.67 us: attend(): total = jnp.sum(grown, axis=-1, keepdims=True)]
    another operation x8 -> x1, local copies, waits for them, and re-layouts: 8.94 us -> 0.12 us  [per_device(): plan.scatter(by_owner(d_qkv)).reshape(step, parts, 3, width // parts)]
    ppermute x4, waiting for transfers between devices: 7.19 us -> 0.01 us  [send(): return lax.ppermute(value, AXES, pairs)]
  transfers between devices with their start and end apart: 58 -> 58, of which waited for: 26 -> 29; matrix products, arithmetic and copies ran while one was open for 24% -> 15% of each run, Pallas kernels for 0% -> 5%
where the time goes in v3:
time: 425 us; the launch traced here: 423 us
  waiting for transfers between devices  127 us (30%)
  starting transfers between devices  125 us (29%)
  Pallas kernels  74.1 us (17%)
  local copies, waits for them, and re-layouts  60.4 us (14%)
  other arithmetic  22.3 us (5%)
  between operations  14.7 us (3%)
    ppermute x53, waiting for transfers between devices, swap(): return lax.ppermute(value, AXES, [(i, i ^ mask) for i in range(self.count)])  127 us
    ppermute x53, starting transfers between devices, swap(): return lax.ppermute(value, AXES, [(i, i ^ mask) for i in range(self.count)])  115 us
    pallas_call x1, Pallas kernels, back_call(): pl.pallas_call(functools.partial(back_kernel, blocks, first, rows), grid=...  35.5 us
    pallas_call x1, Pallas kernels, middle_call(): pl.pallas_call(functools.partial(middle_kernel, wide), grid=(2 * wide,),...  19.5 us
    pallas_call x1, Pallas kernels, attention_call(): pl.pallas_call(functools.partial(attention_kernel, blocks, first, rows),...  19.1 us
    ppermute x4, starting transfers between devices, send(): return lax.ppermute(value, AXES, pairs)  10.1 us
  transfers between devices with their start and end apart: 58, of which 29 were waited for; matrix products, arithmetic and copies ran while one was open for 15% of the time, Pallas kernels for 5%

profile of v3, /device:TPU:0, one launch (start us, length us, event | category | flops | bytes accessed | tf_op | source)
XLA Modules:
  0.0 423.2 jit_solution(7962778741782450448)
XLA Ops:
  9.8 6.7 %collective-permute-start = (bf16[256,768]{1,0:T(8,128)(2,1)}, bf16[256,768]{1,0:T(8,128)(2,1)}, u32[]{:S(2)}, u32[]{:S(2)}) collective-permute-start(bf16[256,768]{1,0:T(8,128)(2,1)} %bitcast.225), channel_id=1, source_target_pairs={{0,4},{1,5},{2,6},{3,7},{8,12},{9,13},{10,14},{11,15},{16,20},{17,... | collective-permute-start | bytes 1179656 | tf_op jit(solution)/shard_map/ppermute | solution.py:53
  19.5 6.1 %concatenate.65 = bf16[288]{0:T(512)(128)(2,1)S(1)} concatenate(bf16[24]{0:T(256)(128)(2,1)} %param.29, bf16[24]{0:T(256)(128)(2,1)} %param.30, bf16[24]{0:T(256)(128)(2,1)} %param.31, bf16[24]{0:T(256)(128)(2,1)} %param.32, bf16[24]{0:T(256)(128)(2,1)} %param.33, bf16[24]{0:T(256)(128)(2,1)} %param.35, bf16[24]{0:T(256)(128)(2,1)} %param.36, bf16[24]{0:T(256)(128)(2,1)} %param.37, ...), dimensions={0} | concatenate | bytes 1152 | tf_op jit(solution)/shard_map/concatenate | solution.py:571
  34.3 4.7 %collective-permute-start.12 = (bf16[2,48,768]{2,1,0:T(8,128)(2,1)S(1)}, bf16[2,48,768]{2,1,0:T(8,128)(2,1)S(1)}, u32[]{:S(2)}, u32[]{:S(2)}) collective-permute-start(bf16[2,48,768]{2,1,0:T(8,128)(2,1)S(1)} %pad_maximum_fusion.5), channel_id=1, source_target_pairs={{0,4},{1,5},{2,6},{3,7},{4,0},{5,1},{6,2},{7,3},{8,12},{9,13},{10,... | collective-permute-start | bytes 442376 | tf_op jit(solution)/shard_map/ppermute | solution.py:49
  39.7 6.5 %collective-permute-done.7 = bf16[2,32,768]{2,1,0:T(8,128)(2,1)S(1)} collective-permute-done((bf16[2,32,768]{2,1,0:T(8,128)(2,1)S(1)}, bf16[2,32,768]{2,1,0:T(8,128)(2,1)S(1)}, u32[]{:S(2)}, u32[]{:S(2)}) %collective-permute-start.7) | collective-permute-done | bytes 98336 | tf_op jit(solution)/shard_map/ppermute | solution.py:49
  46.1 7.9 %collective-permute-start.8 = (bf16[4,32,768]{2,1,0:T(8,128)(2,1)S(1)}, bf16[4,32,768]{2,1,0:T(8,128)(2,1)S(1)}, u32[]{:S(2)}, u32[]{:S(2)}) collective-permute-start(bf16[4,32,768]{2,1,0:T(8,128)(2,1)S(1)} %pad_maximum_fusion.4), channel_id=1, source_target_pairs={{0,1},{1,0},{2,3},{3,2},{4,5},{5,4},{6,7},{7,6},{8,9},{9,8},{10,11... | collective-permute-start | bytes 589832 | tf_op jit(solution)/shard_map/ppermute | solution.py:49
  57.0 3.7 collective-permute-done.8
  62.2 8.0 %collective-permute-done.13 = bf16[4,48,768]{2,1,0:T(8,128)(2,1)S(1)} collective-permute-done((bf16[4,48,768]{2,1,0:T(8,128)(2,1)S(1)}, bf16[4,48,768]{2,1,0:T(8,128)(2,1)S(1)}, u32[]{:S(2)}, u32[]{:S(2)}) %collective-permute-start.13) | collective-permute-done | bytes 294944 | tf_op jit(solution)/shard_map/ppermute | solution.py:49
  70.3 3.2 collective-permute-start.14
  77.4 3.9 collective-permute-done.14
  83.2 2.3 collective-permute-start.1
  89.4 27.2 %collective-permute-done.1.refs_1_ = bf16[256,768]{1,0:T(8,128)(2,1)} collective-permute-done((bf16[256,768]{1,0:T(8,128)(2,1)}, bf16[256,768]{1,0:T(8,128)(2,1)}, u32[]{:S(2)}, u32[]{:S(2)}) %collective-permute-start.1) | collective-permute-done | bytes 393248 | tf_op jit(solution)/shard_map/ppermute | solution.py:49
  116.6 1.8 collective-permute-start.2
  118.7 2.1 constant_dynamic-update-slice_fusion.5
  120.8 2.1 gather_fusion.1
  128.2 2.4 gather_fusion.3
  132.2 4.3 %collective-permute-done.3.refs_3_ = bf16[256,768]{1,0:T(8,128)(2,1)} collective-permute-done((bf16[256,768]{1,0:T(8,128)(2,1)}, bf16[256,768]{1,0:T(8,128)(2,1)}, u32[]{:S(2)}, u32[]{:S(2)}) %collective-permute-start.3) | collective-permute-done | bytes 393248 | tf_op jit(solution)/shard_map/ppermute | solution.py:49
  136.5 19.1 %attention.1 = (bf16[256,768]{1,0:T(8,128)(2,1)}, bf16[1792,768]{1,0:T(8,128)(2,1)}, bf16[1792,768]{1,0:T(8,128)(2,1)}, bf16[256,768]{1,0:T(8,128)(2,1)}, f32[3,8,256]{2,1,0:T(8,128)}) custom-call(bf16[256,768]{1,0:T(8,128)(2,1)} %broadcast_select_fusion.refs_0_, bf16[256,768]{1,0:T(8,128)(2,1)} %collective-permute-done.1.refs_1_, ...), custom_call_target="tpu_custom_call" | custom-call | flops 9865003008 | bytes 12582912 | tf_op jit(solution)/shard_map/attention/pallas_call | solution.py:255
  155.6 2.4 slice.232
  158.0 6.5 %fusion.48 = (bf16[32,96,768]{2,1,0:T(8,128)(2,1)}, bf16[32,96,768]{2,1,0:T(8,128)(2,1)S(1)}) fusion(bf16[32,216,768]{2,1,0:T(8,128)(2,1)} %bitcast.201), kind=kLoop, calls=%fused_computation.178 | loop fusion | bytes 18874368 | tf_op jit(solution)/shard_map/slice | solution.py:608
  164.5 2.4 copy.79
  166.9 19.5 %middle.1 = (bf16[256,768]{1,0:T(8,128)(2,1)}, f32[256,768]{1,0:T(8,128)}, bf16[256,768]{1,0:T(8,128)(2,1)}, bf16[768,768]{1,0:T(8,128)(2,1)}, bf16[4,768,768]{2...) custom-call(bf16[256,768]{1,0:T(8,128)(2,1)} %get-tuple-element.34.ctx_ref.refs_10_, ...), custom_call_target="tpu_custom_call" | custom-call | flops 8153726976 | bytes 33554432 | tf_op jit(solution)/shard_map/middle/pallas_call | solution.py:384
  188.4 35.5 %attention_back.1 = (bf16[768,2304]{1,0:T(8,128)(2,1)}, bf16[7,256,768]{2,1,0:T(8,128)(2,1)}, f32[256,768]{1,0:T(8,128)}, f32[8,768]{1,0:T(8,128)}) custom-call(bf16[256,768]{1,0:T(8,128)(2,1)} %broadcast_select_fusion.refs_0_, bf16[256,768]{1,0:T(8,128)(2,1)} %collective-permute-done.1.refs_1_, bf16[256,768]{1,0:T(8,128)(2,1)} %collective-permute-done.2.refs_2_, ...), custom_call_target="tpu_custom_call" | custom-call | flops 22548578304 | bytes 25165824 | tf_op jit(solution)/shard_map/attention_back/pallas_call | solution.py:518
  223.9 2.7 slice_bitcast_fusion.3
  226.6 1.7 collective-permute-start.17
  239.5 1.7 collective-permute-start.51
  243.7 32.1 %collective-permute-start.56 = (bf16[1,1,8,768]{3,2,1,0:T(8,128)(2,1)S(1)}, bf16[1,1,8,768]{3,2,1,0:T(8,128)(2,1)S(1)}, u32[]{:S(2)}, u32[]{:S(2)}) collective-permute-start(bf16[1,1,8,768]{3,2,1,0:T(8,128)(2,1)S(1)} %get-tuple-element.114), channel_id=1, source_target_pairs={{0,6},{1,7},{2,4},{3,5},{4,2},{5,3},{6,0},{7,1},{8,14},{9,15},{10,... | collective-permute-start | bytes 36872 | tf_op jit(solution)/shard_map/ppermute | solution.py:49
  277.9 2.4 collective-permute-done.55
  284.7 4.2 collective-permute-done.32
  291.1 2.9 collective-permute-done.30
  294.5 3.0 collective-permute-start.35
  299.7 3.8 collective-permute-done.20
  303.5 8.7 %collective-permute-start.34 = (bf16[1,1,24,768]{3,2,1,0:T(8,128)(2,1)S(1)}, bf16[1,1,24,768]{3,2,1,0:T(8,128)(2,1)S(1)}, u32[]{:S(2)}, u32[]{:S(2)}) collective-permute-start(bf16[1,1,24,768]{3,2,1,0:T(8,128)(2,1)S(1)} %get-tuple-element.104), channel_id=1, source_target_pairs={{0,4},{1,5},{2,6},{3,7},{4,0},{5,1},{6,2},{7,3},{8,12},{9,13},{10,... | collective-permute-start | bytes 110600 | tf_op jit(solution)/shard_map/ppermute | solution.py:49
  312.3 3.3 collective-permute-start.33
  315.6 6.6 %collective-permute-done.34 = bf16[1,1,24,768]{3,2,1,0:T(8,128)(2,1)S(1)} collective-permute-done((bf16[1,1,24,768]{3,2,1,0:T(8,128)(2,1)S(1)}, bf16[1,1,24,768]{3,2,1,0:T(8,128)(2,1)S(1)}, u32[]{:S(2)}, u32[]{:S(2)}) %collective-permute-start.34) | collective-permute-done | bytes 36896 | tf_op jit(solution)/shard_map/ppermute | solution.py:49
  323.8 1.9 collective-permute-start.23
  327.6 8.7 %collective-permute-done.25 = bf16[1,2,2,1,24,2304]{5,4,3,2,1,0:T(8,128)(2,1)S(1)} collective-permute-done((bf16[1,2,2,1,24,2304]{5,4,3,2,1,0:T(8,128)(2,1)S(1)}, bf16[1,2,2,1,24,2304]{5,4,3,2,1,0:T(8,128)(2,1)S(1)}, u32[]{:S(2)}, u32[]{:S(2)}) %collective-permute-start.25) | collective-permute-done | bytes 442400 | tf_op jit(solution)/shard_map/ppermute | solution.py:49
  336.3 6.7 %collective-permute-done.24 = bf16[1,2,2,1,24,2304]{5,4,3,2,1,0:T(8,128)(2,1)S(1)} collective-permute-done((bf16[1,2,2,1,24,2304]{5,4,3,2,1,0:T(8,128)(2,1)S(1)}, bf16[1,2,2,1,24,2304]{5,4,3,2,1,0:T(8,128)(2,1)S(1)}, u32[]{:S(2)}, u32[]{:S(2)}) %collective-permute-start.24) | collective-permute-done | bytes 442400 | tf_op jit(solution)/shard_map/ppermute | solution.py:49
  347.8 4.3 %collective-permute-start.26 = (bf16[1,1,24,2304]{3,2,1,0:T(8,128)(2,1)S(1)}, bf16[1,1,24,2304]{3,2,1,0:T(8,128)(2,1)S(1)}, u32[]{:S(2)}, u32[]{:S(2)}) collective-permute-start(bf16[1,1,24,2304]{3,2,1,0:T(8,128)(2,1)S(1)} %get-tuple-element.90), channel_id=1, source_target_pairs={{0,2},{1,3},{2,0},{3,1},{4,6},{5,7},{6,4},{7,5},{8,10},{9,11},{10,... | collective-permute-start | bytes 331784 | tf_op jit(solution)/shard_map/ppermute | solution.py:49
  357.6 2.1 collective-permute-start.46
  361.0 2.6 collective-permute-done.39
  367.0 8.4 %collective-permute-done.38 = bf16[4,1,2,2,1,24,768]{6,5,3,2,0,4,1:T(8,128)(2,1)} collective-permute-done((bf16[4,1,2,2,1,24,768]{6,5,3,2,0,4,1:T(8,128)(2,1)}, bf16[4,1,2,2,1,24,768]{6,5,3,2,0,4,1:T(8,128)(2,1)}, u32[]{:S(2)}, u32[]{:S(2)}) %collective-permute-start.38) | collective-permute-done | bytes 589856 | tf_op jit(solution)/shard_map/ppermute | solution.py:49
  376.2 1.7 fusion.5
  378.0 8.5 %collective-permute-start.42 = (bf16[4,1,1,24,768]{4,3,0,2,1:T(8,128)(2,1)S(1)}, bf16[4,1,1,24,768]{4,3,0,2,1:T(8,128)(2,1)S(1)}, u32[]{:S(2)}, u32[]{:S(2)}) collective-permute-start(bf16[4,1,1,24,768]{4,3,0,2,1:T(8,128)(2,1)S(1)} %get-tuple-element.83), channel_id=1, source_target_pairs={{0,6},{1,7},{2,4},{3,5},{4,2},{5,3},{6,0},{7,1},{8,14},{9,15},{10,... | collective-permute-start | bytes 442376 | tf_op jit(solution)/shard_map/ppermute | solution.py:49
  388.9 10.3 %collective-permute-done.45 = bf16[1,2,2,1,96,768]{5,4,3,2,1,0:T(8,128)(2,1)} collective-permute-done((bf16[1,2,2,1,96,768]{5,4,3,2,1,0:T(8,128)(2,1)}, bf16[1,2,2,1,96,768]{5,4,3,2,1,0:T(8,128)(2,1)}, u32[]{:S(2)}, u32[]{:S(2)}) %collective-permute-start.45) | collective-permute-done | bytes 589856 | tf_op jit(solution)/shard_map/ppermute | solution.py:49
  400.5 1.9 fusion.2
  402.6 4.3 %collective-permute-start.47 = (bf16[1,1,96,768]{3,2,1,0:T(8,128)(2,1)S(1)}, bf16[1,1,96,768]{3,2,1,0:T(8,128)(2,1)S(1)}, u32[]{:S(2)}, u32[]{:S(2)}) collective-permute-start(bf16[1,1,96,768]{3,2,1,0:T(8,128)(2,1)S(1)} %get-tuple-element.79), channel_id=1, source_target_pairs={{0,2},{1,3},{2,0},{3,1},{4,6},{5,7},{6,4},{7,5},{8,10},{9,11},{10,... | collective-permute-start | bytes 442376 | tf_op jit(solution)/shard_map/ppermute | solution.py:49
  407.7 3.4 collective-permute-done.49
  411.1 4.5 %collective-permute-done.48 = bf16[1,1,96,768]{3,2,1,0:T(8,128)(2,1)S(1)} collective-permute-done((bf16[1,1,96,768]{3,2,1,0:T(8,128)(2,1)S(1)}, bf16[1,1,96,768]{3,2,1,0:T(8,128)(2,1)S(1)}, u32[]{:S(2)}, u32[]{:S(2)}) %collective-permute-start.48) | collective-permute-done | bytes 147488 | tf_op jit(solution)/shard_map/ppermute | solution.py:49
  (224 shorter events, 87.7 us)
Async XLA Ops:
  7.2 148.4 %all-gather.2.cloned.1.call-start = ((), (), s32[]{:S(2)}) async-start(), calls=%async_computation | async-start | bytes 10948608 | tf_op jit(solution)/shard_map/all_gather | solution.py:584
  9.8 72.4 %collective-permute-start = (bf16[256,768]{1,0:T(8,128)(2,1)}, bf16[256,768]{1,0:T(8,128)(2,1)}, u32[]{:S(2)}, u32[]{:S(2)}) collective-permute-start(bf16[256,768]{1,0:T(8,128)(2,1)} %bitcast.225), channel_id=1, source_target_pairs={{0,4},{1,5},{2,6},{3,7},{8,12},{9,13},{10,14},{11,15},{16,20},{17,... | collective-permute-start | bytes 1179656 | tf_op jit(solution)/shard_map/ppermute | solution.py:53
  16.6 115.6 %collective-permute-start.4 = (bf16[256,768]{1,0:T(8,128)(2,1)}, bf16[256,768]{1,0:T(8,128)(2,1)}, u32[]{:S(2)}, u32[]{:S(2)}) collective-permute-start(bf16[256,768]{1,0:T(8,128)(2,1)} %bitcast.226), channel_id=1, source_target_pairs={{0,1},{1,0},{2,3},{3,2},{4,5},{5,4},{6,7},{7,6},{8,9},{9,8},{10,11... | collective-permute-start | bytes 1179656 | tf_op jit(solution)/shard_map/ppermute | solution.py:49
  18.1 114.1 %collective-permute-start.5 = (bf16[256,768]{1,0:T(8,128)(2,1)}, bf16[256,768]{1,0:T(8,128)(2,1)}, u32[]{:S(2)}, u32[]{:S(2)}) collective-permute-start(bf16[256,768]{1,0:T(8,128)(2,1)} %bitcast.227), channel_id=1, source_target_pairs={{5,6},{6,5},{13,14},{14,13},{21,22},{22,21},{29,30},{30,29}} | collective-permute-start | bytes 1179656 | tf_op jit(solution)/shard_map/ppermute | solution.py:53
  33.0 13.1 %collective-permute-start.7 = (bf16[2,32,768]{2,1,0:T(8,128)(2,1)S(1)}, bf16[2,32,768]{2,1,0:T(8,128)(2,1)S(1)}, u32[]{:S(2)}, u32[]{:S(2)}) collective-permute-start(bf16[2,32,768]{2,1,0:T(8,128)(2,1)S(1)} %pad_maximum_fusion.6), channel_id=1, source_target_pairs={{0,4},{1,5},{2,6},{3,7},{4,0},{5,1},{6,2},{7,3},{8,12},{9,13},{10,... | collective-permute-start | bytes 294920 | tf_op jit(solution)/shard_map/ppermute | solution.py:49
  34.3 19.7 %collective-permute-start.12 = (bf16[2,48,768]{2,1,0:T(8,128)(2,1)S(1)}, bf16[2,48,768]{2,1,0:T(8,128)(2,1)S(1)}, u32[]{:S(2)}, u32[]{:S(2)}) collective-permute-start(bf16[2,48,768]{2,1,0:T(8,128)(2,1)S(1)} %pad_maximum_fusion.5), channel_id=1, source_target_pairs={{0,4},{1,5},{2,6},{3,7},{4,0},{5,1},{6,2},{7,3},{8,12},{9,13},{10,... | collective-permute-start | bytes 442376 | tf_op jit(solution)/shard_map/ppermute | solution.py:49
  46.1 14.5 %collective-permute-start.8 = (bf16[4,32,768]{2,1,0:T(8,128)(2,1)S(1)}, bf16[4,32,768]{2,1,0:T(8,128)(2,1)S(1)}, u32[]{:S(2)}, u32[]{:S(2)}) collective-permute-start(bf16[4,32,768]{2,1,0:T(8,128)(2,1)S(1)} %pad_maximum_fusion.4), channel_id=1, source_target_pairs={{0,1},{1,0},{2,3},{3,2},{4,5},{5,4},{6,7},{7,6},{8,9},{9,8},{10,11... | collective-permute-start | bytes 589832 | tf_op jit(solution)/shard_map/ppermute | solution.py:49
  54.1 16.1 %collective-permute-start.13 = (bf16[4,48,768]{2,1,0:T(8,128)(2,1)S(1)}, bf16[4,48,768]{2,1,0:T(8,128)(2,1)S(1)}, u32[]{:S(2)}, u32[]{:S(2)}) collective-permute-start(bf16[4,48,768]{2,1,0:T(8,128)(2,1)S(1)} %pad_maximum_fusion.3), channel_id=1, source_target_pairs={{0,16},{1,17},{2,18},{3,19},{4,20},{5,21},{6,22},{7,23},{8,24},{9,... | collective-permute-start | bytes 884744 | tf_op jit(solution)/shard_map/ppermute | solution.py:49
  60.7 15.7 %collective-permute-start.9 = (bf16[8,32,768]{2,1,0:T(8,128)(2,1)S(1)}, bf16[8,32,768]{2,1,0:T(8,128)(2,1)S(1)}, u32[]{:S(2)}, u32[]{:S(2)}) collective-permute-start(bf16[8,32,768]{2,1,0:T(8,128)(2,1)S(1)} %pad_maximum_fusion.1), channel_id=1, source_target_pairs={{0,16},{1,17},{2,18},{3,19},{4,20},{5,21},{6,22},{7,23},{8,24},{9,... | collective-permute-start | bytes 1179656 | tf_op jit(solution)/shard_map/ppermute | solution.py:49
  70.3 11.0 %collective-permute-start.14 = (bf16[8,48,768]{2,1,0:T(8,128)(2,1)S(1)}, bf16[8,48,768]{2,1,0:T(8,128)(2,1)S(1)}, u32[]{:S(2)}, u32[]{:S(2)}) collective-permute-start(bf16[8,48,768]{2,1,0:T(8,128)(2,1)S(1)} %pad_maximum_fusion), channel_id=1, source_target_pairs={{0,1},{1,0},{2,3},{3,2},{4,5},{5,4},{6,7},{7,6},{8,9},{9,8},{10,11... | collective-permute-start | bytes 1769480 | tf_op jit(solution)/shard_map/ppermute | solution.py:49
  77.4 41.0 %collective-permute-start.10 = (bf16[16,32,768]{2,1,0:T(8,128)(2,1)}, bf16[16,32,768]{2,1,0:T(8,128)(2,1)}, u32[]{:S(2)}, u32[]{:S(2)}) collective-permute-start(bf16[16,32,768]{2,1,0:T(8,128)(2,1)} %get-tuple-element.93), channel_id=1, source_target_pairs={{0,8},{1,9},{2,10},{3,11},{4,12},{5,13},{6,14},{7,15},{8,0},{9,1},... | collective-permute-start | bytes 2359304 | tf_op jit(solution)/shard_map/ppermute | solution.py:49
  82.2 44.9 %collective-permute-start.15 = (bf16[16,48,768]{2,1,0:T(8,128)(2,1)}, bf16[16,48,768]{2,1,0:T(8,128)(2,1)S(1)}, u32[]{:S(2)}, u32[]{:S(2)}) collective-permute-start(bf16[16,48,768]{2,1,0:T(8,128)(2,1)} %get-tuple-element.88), channel_id=1, source_target_pairs={{0,8},{1,9},{2,10},{3,11},{4,12},{5,13},{6,14},{7,15},{8,0},{9,1},... | collective-permute-start | bytes 3538952 | tf_op jit(solution)/shard_map/ppermute | solution.py:49
  83.2 33.5 %collective-permute-start.1 = (bf16[256,768]{1,0:T(8,128)(2,1)}, bf16[256,768]{1,0:T(8,128)(2,1)}, u32[]{:S(2)}, u32[]{:S(2)}) collective-permute-start(bf16[256,768]{1,0:T(8,128)(2,1)} %broadcast_select_fusion.refs_0_), channel_id=1, source_target_pairs={{0,2},{1,3},{2,0},{3,1},{4,6},{5,7},{6,4},{7,5},{8,10},{9,11},{10,... | collective-permute-start | bytes 1179656 | tf_op jit(solution)/shard_map/ppermute | solution.py:49
  116.6 15.5 %collective-permute-start.2 = (bf16[256,768]{1,0:T(8,128)(2,1)}, bf16[256,768]{1,0:T(8,128)(2,1)}, u32[]{:S(2)}, u32[]{:S(2)}) collective-permute-start(bf16[256,768]{1,0:T(8,128)(2,1)} %broadcast_select_fusion.refs_0_), channel_id=1, source_target_pairs={{0,1},{1,0},{2,3},{3,2},{4,5},{5,4},{6,7},{7,6},{8,9},{9,8},{10,11... | collective-permute-start | bytes 1179656 | tf_op jit(solution)/shard_map/ppermute | solution.py:49
  118.4 18.1 %collective-permute-start.3 = (bf16[256,768]{1,0:T(8,128)(2,1)}, bf16[256,768]{1,0:T(8,128)(2,1)}, u32[]{:S(2)}, u32[]{:S(2)}) collective-permute-start(bf16[256,768]{1,0:T(8,128)(2,1)} %collective-permute-done.1.refs_1_), channel_id=1, source_target_pairs={{0,1},{1,0},{2,3},{3,2},{4,5},{5,4},{6,7},{7,6},{8,9},{9,8},{10,11... | collective-permute-start | bytes 1179656 | tf_op jit(solution)/shard_map/ppermute | solution.py:49
  226.6 55.6 %collective-permute-start.17 = (bf16[256,768]{1,0:T(8,128)(2,1)}, bf16[256,768]{1,0:T(8,128)(2,1)}, u32[]{:S(2)}, u32[]{:S(2)}) collective-permute-start(bf16[256,768]{1,0:T(8,128)(2,1)} %get-tuple-element.65), channel_id=1, source_target_pairs={{0,1},{1,0},{2,3},{3,2},{4,5},{5,4},{6,7},{7,6},{8,9},{9,8},{10,11... | collective-permute-start | bytes 1179656 | tf_op jit(solution)/shard_map/ppermute | solution.py:49
  237.0 44.0 %collective-permute-start.29 = (bf16[2,1,2,2,2,24,768]{6,5,3,2,4,1,0:T(8,128)(2,1)S(1)}, bf16[2,1,2,2,2,24,768]{6,5,3,2,4,1,0:T(8,128)(2,1)S(1)}, u32[]{:S(2)}, u32[]{:S(2)}) collective-permute-start(bf16[2,1,2,2,2,24,768]{6,5,3,2,4,1,0:T(8,128)(2,1)S(1)} %copy.95), channel_id=1, source_target_pairs={{0,8},{1,9},{2,10},{3,11},{4,12},{5,13},{6,14},{7,15},{8,0},{9,1},... | collective-permute-start | bytes 1769480 | tf_op jit(solution)/shard_map/ppermute | solution.py:49
  243.7 33.9 %collective-permute-start.56 = (bf16[1,1,8,768]{3,2,1,0:T(8,128)(2,1)S(1)}, bf16[1,1,8,768]{3,2,1,0:T(8,128)(2,1)S(1)}, u32[]{:S(2)}, u32[]{:S(2)}) collective-permute-start(bf16[1,1,8,768]{3,2,1,0:T(8,128)(2,1)S(1)} %get-tuple-element.114), channel_id=1, source_target_pairs={{0,6},{1,7},{2,4},{3,5},{4,2},{5,3},{6,0},{7,1},{8,14},{9,15},{10,... | collective-permute-start | bytes 36872 | tf_op jit(solution)/shard_map/ppermute | solution.py:49
  277.7 16.7 %collective-permute-start.16 = (bf16[256,768]{1,0:T(8,128)(2,1)S(1)}, bf16[256,768]{1,0:T(8,128)(2,1)S(1)}, u32[]{:S(2)}, u32[]{:S(2)}) collective-permute-start(bf16[256,768]{1,0:T(8,128)(2,1)S(1)} %copy-done.10), channel_id=1, source_target_pairs={{0,1},{1,0},{2,3},{3,2},{4,5},{5,4},{6,7},{7,6},{8,9},{9,8},{10,11... | collective-permute-start | bytes 1179656 | tf_op jit(solution)/shard_map/ppermute | solution.py:49
  280.4 17.4 %collective-permute-start.22 = (bf16[2,1,2,2,2,24,2304]{6,5,3,2,4,1,0:T(8,128)(2,1)S(1)}, bf16[2,1,2,2,2,24,2304]{6,5,3,2,4,1,0:T(8,128)(2,1)S(1)}, u32[]{:S(2)}, u32[]{:S(2)}) collective-permute-start(bf16[2,1,2,2,2,24,2304]{6,5,3,2,4,1,0:T(8,128)(2,1)S(1)} %copy.93), channel_id=1, source_target_pairs={{0,8},{1,9},{2,10},{3,11},{4,12},{5,13},{6,14},{7,15},{8,0},{9,1},... | collective-permute-start | bytes 5308424 | tf_op jit(solution)/shard_map/ppermute | solution.py:49
  281.2 7.7 %collective-permute-start.32 = (bf16[1,2,2,1,24,768]{5,4,3,2,1,0:T(8,128)(2,1)S(1)}, bf16[1,2,2,1,24,768]{5,4,3,2,1,0:T(8,128)(2,1)S(1)}, u32[]{:S(2)}, u32[]{:S(2)}) collective-permute-start(bf16[1,2,2,1,24,768]{5,4,3,2,1,0:T(8,128)(2,1)S(1)} %get-tuple-element.86), channel_id=1, source_target_pairs={{0,17},{1,16},{2,19},{3,18},{4,21},{5,20},{6,23},{7,22},{8,25},{9,... | collective-permute-start | bytes 442376 | tf_op jit(solution)/shard_map/ppermute | solution.py:49
  283.2 11.3 %collective-permute-start.18 = (bf16[256,768]{1,0:T(8,128)(2,1)S(1)}, bf16[256,768]{1,0:T(8,128)(2,1)S(1)}, u32[]{:S(2)}, u32[]{:S(2)}) collective-permute-start(bf16[256,768]{1,0:T(8,128)(2,1)S(1)} %fusion.13), channel_id=1, source_target_pairs={{0,2},{1,3},{2,0},{3,1},{4,6},{5,7},{6,4},{7,5},{8,10},{9,11},{10,... | collective-permute-start | bytes 1179656 | tf_op jit(solution)/shard_map/ppermute | solution.py:49
  290.4 9.1 %collective-permute-start.21 = (bf16[256,768]{1,0:T(8,128)(2,1)S(1)}, bf16[256,768]{1,0:T(8,128)(2,1)S(1)}, u32[]{:S(2)}, u32[]{:S(2)}) collective-permute-start(bf16[256,768]{1,0:T(8,128)(2,1)S(1)} %copy-done.9), channel_id=1, source_target_pairs={{5,6},{6,5},{13,14},{14,13},{21,22},{22,21},{29,30},{30,29}} | collective-permute-start | bytes 1179656 | tf_op jit(solution)/shard_map/ppermute | solution.py:53
  294.0 9.5 %collective-permute-start.20 = (bf16[256,768]{1,0:T(8,128)(2,1)S(1)}, bf16[256,768]{1,0:T(8,128)(2,1)S(1)}, u32[]{:S(2)}, u32[]{:S(2)}) collective-permute-start(bf16[256,768]{1,0:T(8,128)(2,1)S(1)} %copy-done.8), channel_id=1, source_target_pairs={{0,1},{1,0},{2,3},{3,2},{4,5},{5,4},{6,7},{7,6},{8,9},{9,8},{10,11... | collective-permute-start | bytes 1179656 | tf_op jit(solution)/shard_map/ppermute | solution.py:49
  294.4 50.2 %collective-permute-start.36 = (bf16[4,2,1,2,2,2,24,768]{7,6,5,4,3,2,1,0:T(8,128)(2,1)S(1)}, bf16[4,2,1,2,2,2,24,768]{7,6,5,4,3,2,1,0:T(8,128)(2,1)S(1)}, u32[]{:S(2)}, u32[]{:S(2)}) collective-permute-start(bf16[4,2,1,2,2,2,24,768]{7,6,5,4,3,2,1,0:T(8,128)(2,1)S(1)} %constant_dynamic-slice_fusion.7), channel_id=1, source_target_pairs={{0,8},{1,9},{2,10},{3,11},{4,12},{5,13},{6,14},{7,15},{8,0},{9,1},... | collective-permute-start | bytes 7077896 | tf_op jit(solution)/shard_map/ppermute | solution.py:49
  294.5 17.7 %collective-permute-start.35 = (bf16[1,1,24,768]{3,2,1,0:T(8,128)(2,1)S(1)}, bf16[1,1,24,768]{3,2,1,0:T(8,128)(2,1)S(1)}, u32[]{:S(2)}, u32[]{:S(2)}) collective-permute-start(bf16[1,1,24,768]{3,2,1,0:T(8,128)(2,1)S(1)} %get-tuple-element.103), channel_id=1, source_target_pairs={{0,6},{1,7},{2,4},{3,5},{4,2},{5,3},{6,0},{7,1},{8,14},{9,15},{10,... | collective-permute-start | bytes 110600 | tf_op jit(solution)/shard_map/ppermute | solution.py:49
  297.8 26.1 %collective-permute-start.19 = (bf16[256,768]{1,0:T(8,128)(2,1)S(1)}, bf16[256,768]{1,0:T(8,128)(2,1)S(1)}, u32[]{:S(2)}, u32[]{:S(2)}) collective-permute-start(bf16[256,768]{1,0:T(8,128)(2,1)S(1)} %fusion.15), channel_id=1, source_target_pairs={{4,0},{5,1},{6,2},{7,3},{12,8},{13,9},{14,10},{15,11},{20,16},{21,... | collective-permute-start | bytes 1179656 | tf_op jit(solution)/shard_map/ppermute | solution.py:53
  299.5 52.5 %collective-permute-start.43 = (bf16[2,1,2,2,2,96,768]{6,5,3,2,4,1,0:T(8,128)(2,1)S(1)}, bf16[2,1,2,2,2,96,768]{6,5,3,2,4,1,0:T(8,128)(2,1)S(1)}, u32[]{:S(2)}, u32[]{:S(2)}) collective-permute-start(bf16[2,1,2,2,2,96,768]{6,5,3,2,4,1,0:T(8,128)(2,1)S(1)} %copy.97), channel_id=1, source_target_pairs={{0,8},{1,9},{2,10},{3,11},{4,12},{5,13},{6,14},{7,15},{8,0},{9,1},... | collective-permute-start | bytes 7077896 | tf_op jit(solution)/shard_map/ppermute | solution.py:49
  303.5 18.7 %collective-permute-start.34 = (bf16[1,1,24,768]{3,2,1,0:T(8,128)(2,1)S(1)}, bf16[1,1,24,768]{3,2,1,0:T(8,128)(2,1)S(1)}, u32[]{:S(2)}, u32[]{:S(2)}) collective-permute-start(bf16[1,1,24,768]{3,2,1,0:T(8,128)(2,1)S(1)} %get-tuple-element.104), channel_id=1, source_target_pairs={{0,4},{1,5},{2,6},{3,7},{4,0},{5,1},{6,2},{7,3},{8,12},{9,13},{10,... | collective-permute-start | bytes 110600 | tf_op jit(solution)/shard_map/ppermute | solution.py:49
  312.3 10.5 %collective-permute-start.33 = (bf16[1,1,24,768]{3,2,1,0:T(8,128)(2,1)S(1)}, bf16[1,1,24,768]{3,2,1,0:T(8,128)(2,1)S(1)}, u32[]{:S(2)}, u32[]{:S(2)}) collective-permute-start(bf16[1,1,24,768]{3,2,1,0:T(8,128)(2,1)S(1)} %get-tuple-element.102), channel_id=1, source_target_pairs={{0,2},{1,3},{2,0},{3,1},{4,6},{5,7},{6,4},{7,5},{8,10},{9,11},{10,... | collective-permute-start | bytes 110600 | tf_op jit(solution)/shard_map/ppermute | solution.py:49
  322.3 14.0 %collective-permute-start.25 = (bf16[1,2,2,1,24,2304]{5,4,3,2,1,0:T(8,128)(2,1)S(1)}, bf16[1,2,2,1,24,2304]{5,4,3,2,1,0:T(8,128)(2,1)S(1)}, u32[]{:S(2)}, u32[]{:S(2)}) collective-permute-start(bf16[1,2,2,1,24,2304]{5,4,3,2,1,0:T(8,128)(2,1)S(1)} %get-tuple-element.75), channel_id=1, source_target_pairs={{0,17},{1,16},{2,19},{3,18},{4,21},{5,20},{6,23},{7,22},{8,25},{9,... | collective-permute-start | bytes 1327112 | tf_op jit(solution)/shard_map/ppermute | solution.py:49
  322.7 20.3 %collective-permute-start.24 = (bf16[1,2,2,1,24,2304]{5,4,3,2,1,0:T(8,128)(2,1)S(1)}, bf16[1,2,2,1,24,2304]{5,4,3,2,1,0:T(8,128)(2,1)S(1)}, u32[]{:S(2)}, u32[]{:S(2)}) collective-permute-start(bf16[1,2,2,1,24,2304]{5,4,3,2,1,0:T(8,128)(2,1)S(1)} %get-tuple-element.76), channel_id=1, source_target_pairs={{0,16},{1,17},{2,18},{3,19},{4,20},{5,21},{6,22},{7,23},{8,24},{9,... | collective-permute-start | bytes 1327112 | tf_op jit(solution)/shard_map/ppermute | solution.py:49
  323.8 20.6 %collective-permute-start.23 = (bf16[1,2,2,1,24,2304]{5,4,3,2,1,0:T(8,128)(2,1)S(1)}, bf16[1,2,2,1,24,2304]{5,4,3,2,1,0:T(8,128)(2,1)S(1)}, u32[]{:S(2)}, u32[]{:S(2)}) collective-permute-start(bf16[1,2,2,1,24,2304]{5,4,3,2,1,0:T(8,128)(2,1)S(1)} %get-tuple-element.74), channel_id=1, source_target_pairs={{0,1},{1,0},{2,3},{3,2},{4,5},{5,4},{6,7},{7,6},{8,9},{9,8},{10,11... | collective-permute-start | bytes 1327112 | tf_op jit(solution)/shard_map/ppermute | solution.py:49
  346.3 17.2 %collective-permute-start.39 = (bf16[4,1,2,2,1,24,768]{6,5,3,2,0,4,1:T(8,128)(2,1)S(1)}, bf16[4,1,2,2,1,24,768]{6,5,3,2,0,4,1:T(8,128)(2,1)}, u32[]{:S(2)}, u32[]{:S(2)}) collective-permute-start(bf16[4,1,2,2,1,24,768]{6,5,3,2,0,4,1:T(8,128)(2,1)S(1)} %get-tuple-element.70), channel_id=1, source_target_pairs={{0,17},{1,16},{2,19},{3,18},{4,21},{5,20},{6,23},{7,22},{8,25},{9,... | collective-permute-start | bytes 1769480 | tf_op jit(solution)/shard_map/ppermute | solution.py:49
  347.6 7.9 %collective-permute-start.28 = (bf16[1,1,24,2304]{3,2,1,0:T(8,128)(2,1)S(1)}, bf16[1,1,24,2304]{3,2,1,0:T(8,128)(2,1)S(1)}, u32[]{:S(2)}, u32[]{:S(2)}) collective-permute-start(bf16[1,1,24,2304]{3,2,1,0:T(8,128)(2,1)S(1)} %get-tuple-element.91), channel_id=1, source_target_pairs={{0,6},{1,7},{2,4},{3,5},{4,2},{5,3},{6,0},{7,1},{8,14},{9,15},{10,... | collective-permute-start | bytes 331784 | tf_op jit(solution)/shard_map/ppermute | solution.py:49
  347.7 9.9 %collective-permute-start.27 = (bf16[1,1,24,2304]{3,2,1,0:T(8,128)(2,1)S(1)}, bf16[1,1,24,2304]{3,2,1,0:T(8,128)(2,1)S(1)}, u32[]{:S(2)}, u32[]{:S(2)}) collective-permute-start(bf16[1,1,24,2304]{3,2,1,0:T(8,128)(2,1)S(1)} %get-tuple-element.92), channel_id=1, source_target_pairs={{0,4},{1,5},{2,6},{3,7},{4,0},{5,1},{6,2},{7,3},{8,12},{9,13},{10,... | collective-permute-start | bytes 331784 | tf_op jit(solution)/shard_map/ppermute | solution.py:49
  347.8 12.0 %collective-permute-start.26 = (bf16[1,1,24,2304]{3,2,1,0:T(8,128)(2,1)S(1)}, bf16[1,1,24,2304]{3,2,1,0:T(8,128)(2,1)S(1)}, u32[]{:S(2)}, u32[]{:S(2)}) collective-permute-start(bf16[1,1,24,2304]{3,2,1,0:T(8,128)(2,1)S(1)} %get-tuple-element.90), channel_id=1, source_target_pairs={{0,2},{1,3},{2,0},{3,1},{4,6},{5,7},{6,4},{7,5},{8,10},{9,11},{10,... | collective-permute-start | bytes 331784 | tf_op jit(solution)/shard_map/ppermute | solution.py:49
  352.1 23.3 %collective-permute-start.38 = (bf16[4,1,2,2,1,24,768]{6,5,3,2,0,4,1:T(8,128)(2,1)}, bf16[4,1,2,2,1,24,768]{6,5,3,2,0,4,1:T(8,128)(2,1)}, u32[]{:S(2)}, u32[]{:S(2)}) collective-permute-start(bf16[4,1,2,2,1,24,768]{6,5,3,2,0,4,1:T(8,128)(2,1)} %get-tuple-element.71), channel_id=1, source_target_pairs={{0,16},{1,17},{2,18},{3,19},{4,20},{5,21},{6,22},{7,23},{8,24},{9,... | collective-permute-start | bytes 1769480 | tf_op jit(solution)/shard_map/ppermute | solution.py:49
  355.5 20.7 %collective-permute-start.37 = (bf16[4,1,2,2,1,24,768]{6,5,3,2,0,4,1:T(8,128)(2,1)S(1)}, bf16[4,1,2,2,1,24,768]{6,5,3,2,0,4,1:T(8,128)(2,1)}, u32[]{:S(2)}, u32[]{:S(2)}) collective-permute-start(bf16[4,1,2,2,1,24,768]{6,5,3,2,0,4,1:T(8,128)(2,1)S(1)} %get-tuple-element.69), channel_id=1, source_target_pairs={{0,1},{1,0},{2,3},{3,2},{4,5},{5,4},{6,7},{7,6},{8,9},{9,8},{10,11... | collective-permute-start | bytes 1769480 | tf_op jit(solution)/shard_map/ppermute | solution.py:49
  357.6 31.2 %collective-permute-start.46 = (bf16[1,2,2,1,96,768]{5,4,3,2,1,0:T(8,128)(2,1)}, bf16[1,2,2,1,96,768]{5,4,3,2,1,0:T(8,128)(2,1)}, u32[]{:S(2)}, u32[]{:S(2)}) collective-permute-start(bf16[1,2,2,1,96,768]{5,4,3,2,1,0:T(8,128)(2,1)} %get-tuple-element.67), channel_id=1, source_target_pairs={{0,17},{1,16},{2,19},{3,18},{4,21},{5,20},{6,23},{7,22},{8,25},{9,... | collective-permute-start | bytes 1769480 | tf_op jit(solution)/shard_map/ppermute | solution.py:49
  359.7 39.4 %collective-permute-start.45 = (bf16[1,2,2,1,96,768]{5,4,3,2,1,0:T(8,128)(2,1)}, bf16[1,2,2,1,96,768]{5,4,3,2,1,0:T(8,128)(2,1)}, u32[]{:S(2)}, u32[]{:S(2)}) collective-permute-start(bf16[1,2,2,1,96,768]{5,4,3,2,1,0:T(8,128)(2,1)} %get-tuple-element.68), channel_id=1, source_target_pairs={{0,16},{1,17},{2,18},{3,19},{4,20},{5,21},{6,22},{7,23},{8,24},{9,... | collective-permute-start | bytes 1769480 | tf_op jit(solution)/shard_map/ppermute | solution.py:49
  363.5 36.9 %collective-permute-start.44 = (bf16[1,2,2,1,96,768]{5,4,3,2,1,0:T(8,128)(2,1)}, bf16[1,2,2,1,96,768]{5,4,3,2,1,0:T(8,128)(2,1)}, u32[]{:S(2)}, u32[]{:S(2)}) collective-permute-start(bf16[1,2,2,1,96,768]{5,4,3,2,1,0:T(8,128)(2,1)} %get-tuple-element.66), channel_id=1, source_target_pairs={{0,1},{1,0},{2,3},{3,2},{4,5},{5,4},{6,7},{7,6},{8,9},{9,8},{10,11... | collective-permute-start | bytes 1769480 | tf_op jit(solution)/shard_map/ppermute | solution.py:49
  378.0 24.6 %collective-permute-start.42 = (bf16[4,1,1,24,768]{4,3,0,2,1:T(8,128)(2,1)S(1)}, bf16[4,1,1,24,768]{4,3,0,2,1:T(8,128)(2,1)S(1)}, u32[]{:S(2)}, u32[]{:S(2)}) collective-permute-start(bf16[4,1,1,24,768]{4,3,0,2,1:T(8,128)(2,1)S(1)} %get-tuple-element.83), channel_id=1, source_target_pairs={{0,6},{1,7},{2,4},{3,5},{4,2},{5,3},{6,0},{7,1},{8,14},{9,15},{10,... | collective-permute-start | bytes 442376 | tf_op jit(solution)/shard_map/ppermute | solution.py:49
  386.5 20.4 %collective-permute-start.41 = (bf16[4,1,1,24,768]{4,3,0,2,1:T(8,128)(2,1)S(1)}, bf16[4,1,1,24,768]{4,3,0,2,1:T(8,128)(2,1)S(1)}, u32[]{:S(2)}, u32[]{:S(2)}) collective-permute-start(bf16[4,1,1,24,768]{4,3,0,2,1:T(8,128)(2,1)S(1)} %get-tuple-element.84), channel_id=1, source_target_pairs={{0,4},{1,5},{2,6},{3,7},{4,0},{5,1},{6,2},{7,3},{8,12},{9,13},{10,... | collective-permute-start | bytes 442376 | tf_op jit(solution)/shard_map/ppermute | solution.py:49
  388.9 18.0 %collective-permute-start.40 = (bf16[4,1,1,24,768]{4,3,0,2,1:T(8,128)(2,1)S(1)}, bf16[4,1,1,24,768]{4,3,0,2,1:T(8,128)(2,1)S(1)}, u32[]{:S(2)}, u32[]{:S(2)}) collective-permute-start(bf16[4,1,1,24,768]{4,3,0,2,1:T(8,128)(2,1)S(1)} %get-tuple-element.82), channel_id=1, source_target_pairs={{0,2},{1,3},{2,0},{3,1},{4,6},{5,7},{6,4},{7,5},{8,10},{9,11},{10,... | collective-permute-start | bytes 442376 | tf_op jit(solution)/shard_map/ppermute | solution.py:49
  402.4 8.7 %collective-permute-start.49 = (bf16[1,1,96,768]{3,2,1,0:T(8,128)(2,1)S(1)}, bf16[1,1,96,768]{3,2,1,0:T(8,128)(2,1)S(1)}, u32[]{:S(2)}, u32[]{:S(2)}) collective-permute-start(bf16[1,1,96,768]{3,2,1,0:T(8,128)(2,1)S(1)} %get-tuple-element.80), channel_id=1, source_target_pairs={{0,6},{1,7},{2,4},{3,5},{4,2},{5,3},{6,0},{7,1},{8,14},{9,15},{10,... | collective-permute-start | bytes 442376 | tf_op jit(solution)/shard_map/ppermute | solution.py:49
  402.5 13.1 %collective-permute-start.48 = (bf16[1,1,96,768]{3,2,1,0:T(8,128)(2,1)S(1)}, bf16[1,1,96,768]{3,2,1,0:T(8,128)(2,1)S(1)}, u32[]{:S(2)}, u32[]{:S(2)}) collective-permute-start(bf16[1,1,96,768]{3,2,1,0:T(8,128)(2,1)S(1)} %get-tuple-element.81), channel_id=1, source_target_pairs={{0,4},{1,5},{2,6},{3,7},{4,0},{5,1},{6,2},{7,3},{8,12},{9,13},{10,... | collective-permute-start | bytes 442376 | tf_op jit(solution)/shard_map/ppermute | solution.py:49
  402.6 13.0 %collective-permute-start.47 = (bf16[1,1,96,768]{3,2,1,0:T(8,128)(2,1)S(1)}, bf16[1,1,96,768]{3,2,1,0:T(8,128)(2,1)S(1)}, u32[]{:S(2)}, u32[]{:S(2)}) collective-permute-start(bf16[1,1,96,768]{3,2,1,0:T(8,128)(2,1)S(1)} %get-tuple-element.79), channel_id=1, source_target_pairs={{0,2},{1,3},{2,0},{3,1},{4,6},{5,7},{6,4},{7,5},{8,10},{9,11},{10,... | collective-permute-start | bytes 442376 | tf_op jit(solution)/shard_map/ppermute | solution.py:49
  (26 other events, 258.5 us)
Sparse Core Ops, SparseCore 0:
  11.5 111.7 all-gather.1

commit v4 on v3

v4 whole, which is shorter than its diff:
```python
import functools

import jax
import jax.numpy as jnp
import numpy as np
from jax import lax
from jax.experimental import pallas as pl
from jax.experimental.pallas import tpu as pltpu
from jax.sharding import PartitionSpec as P

HEADS = 12
HDIM = 64
PROMPT = 1024
CONT_MOST = 256
BF = jnp.bfloat16
F32 = jnp.float32

NORM_EPS = 1e-12
MASK_FILL = -1000000000.0
SQRT_HALF = 0.7071067811865476
INV_ROOT_TAU = 0.3989422804014327
AXES = ("grp", "row")


def mm(left, right):
    return jnp.dot(left, right, preferred_element_type=F32)


def segment_ids(lengths, group_len):
    ends = jnp.cumsum(lengths)
    places = jnp.arange(group_len, dtype=jnp.int32)
    passed = jnp.sum(((places - PROMPT)[:, None] >= ends[None, :]).astype(jnp.int32), axis=-1)
    return jnp.where(places < PROMPT, 0, 1 + passed)


class Plan:
    def __init__(self, grp, row):
        self.grp, self.row, self.count = grp, row, grp * row
        y = row // 4
        bits = lambda base, size: [base << i for i in range(size.bit_length() - 1)]
        self.y, self.z = bits(1, y), bits(y, 4)
        self.core, self.x = bits(row, 2), bits(2 * row, grp // 2)
        self.bits = self.count.bit_length() - 1

    def swap(self, value, mask):
        return lax.ppermute(value, AXES, [(i, i ^ mask) for i in range(self.count)])

    def send(self, value, moves):
        pairs = [(g * self.row + a, g * self.row + b) for g in range(self.grp) for a, b in moves]
        return lax.ppermute(value, AXES, pairs)

    def me(self):
        return lax.axis_index("grp") * self.row + lax.axis_index("row")


def combos(stage):
    masks = [0]
    for bit in stage:
        masks = masks + [m ^ bit for m in masks]
    return masks


class Gather:
    def __init__(self, plan, value):
        self.plan, self.held, self.masks = plan, value[None], [0]

    def stage(self, bits):
        masks = combos(bits)
        self.held = jnp.concatenate(
            [self.held] + [self.plan.swap(self.held, m) for m in masks[1:]], 0
        )
        self.masks = [m ^ k for k in masks for m in self.masks]

    def ordered(self):
        slot = np.zeros(self.plan.count, np.int32)
        for j, m in enumerate(self.masks):
            slot[m] = j
        places = jnp.asarray(slot)[self.plan.me() ^ jnp.arange(self.plan.count)]
        return jnp.take(self.held, places, axis=0, mode="clip")


class Reduce:
    def __init__(self, plan, value, before=0):
        self.plan, self.before = plan, before
        self.lead, self.rest = list(value.shape[:before]), list(value.shape[before + 1 :])
        self.left = [1 << i for i in reversed(range(plan.bits))]
        self.value = value.astype(BF).reshape(self.lead + [2] * plan.bits + self.rest)

    def stage(self, bits):
        me, value = self.plan.me(), self.value

        def part(mask):
            array = value
            for bit in bits:
                place = ((me ^ mask) // bit) & 1
                axis = self.before + self.left.index(bit)
                array = lax.dynamic_slice_in_dim(array, place, 1, axis)
            return array

        total = part(0).astype(F32)
        for mask in combos(bits)[1:]:
            total = total + self.plan.swap(part(mask), mask).astype(F32)
        self.left = [b for b in self.left if b not in bits]
        value = total.reshape(self.lead + [2] * len(self.left) + self.rest)
        self.value = value.astype(BF) if self.left else value


def tie(*values):
    return lax.optimization_barrier(values)


class Tokens:
    def __init__(self, plan, own):
        self.plan, self.own = plan, own
        self.rows = own.shape[0]
        self.ready = plan.row == 8

    def stage_one(self):
        if self.ready:
            plan, own = self.plan, self.own
            across = plan.send(own, [(0, 4), (1, 5), (2, 6), (3, 7)])
            self.same = jnp.where(lax.axis_index("row") < 4, own, across)
            self.beside = plan.swap(own, 1)
            return [self.same, self.beside]
        return []

    def stage_two(self):
        if self.ready:
            plan = self.plan
            self.other = plan.swap(self.same, 2)
            self.same_y = plan.swap(self.same, 1)
            self.diagonal = plan.send(self.own, [(5, 6), (6, 5)])
            return [self.other, self.same_y, self.diagonal]
        return []

    def stage_three(self):
        if self.ready:
            self.other_y = self.plan.swap(self.other, 1)

    def spots(self):
        row, rows, own = lax.axis_index("row"), self.rows, self.own
        if self.ready:
            near = jnp.where(row < 4, 0, jnp.where((row == 5) | (row == 6), 3, 2))
            return [
                self.same, self.other, self.same_y, self.other_y, own, self.beside, self.diagonal,
            ], near
        every = lax.all_gather(own, "row", axis=0, tiled=True)
        start = jnp.maximum(row * rows - CONT_MOST, 0)
        padded = jnp.concatenate([every, jnp.zeros((CONT_MOST, own.shape[1]), own.dtype)], 0)
        near = lax.dynamic_slice_in_dim(padded, start, rows + 2 * CONT_MOST, 0)
        every = jnp.concatenate([every[:PROMPT], near], 0)
        spots = [every[i : i + rows] for i in range(0, every.shape[0], rows)]
        return spots, jnp.where(row * rows < PROMPT, 0, near.shape[0] // rows)


def near_segments(plan, segments, rows):
    row = lax.axis_index("row")
    if plan.row != 8:
        start = jnp.maximum(row * rows - CONT_MOST, 0)
        padded = jnp.concatenate([segments, jnp.full((CONT_MOST,), -1, jnp.int32)], 0)
        near = lax.dynamic_slice_in_dim(padded, start, rows + 2 * CONT_MOST, 0)
        return jnp.where((near == 0) | (row * rows < PROMPT), -1, near)
    pieces = []
    for block, valid in (
        (row, row >= 4),
        (row ^ 1, row >= 4),
        (11 - row, (row == 5) | (row == 6)),
    ):
        block = jnp.clip(block, 0, 7)
        ids = lax.dynamic_slice_in_dim(segments, block * rows, rows, 0)
        pieces.append(jnp.where(valid, ids, -1))
    return jnp.concatenate(pieces, 0)


class Return:
    def __init__(self, plan, rows):
        self.plan, self.rows = plan, rows

    def prompt_one(self, parts):
        self.prompt = self.same = parts
        if self.plan.row == 8:
            same, other, same_y, other_y = [parts[i].astype(F32) for i in range(4)]
            self.other = (other + self.plan.swap(parts[3], 1).astype(F32)).astype(BF)
            self.same = same + self.plan.swap(parts[2], 1).astype(F32)

    def prompt_two(self):
        if self.plan.row == 8:
            self.same = self.same + self.plan.swap(self.other, 2).astype(F32)

    def prompt_three(self):
        if self.plan.row == 8:
            back = self.plan.send(self.same.astype(BF), [(4, 0), (5, 1), (6, 2), (7, 3)])
            self.same = self.same + back.astype(F32)

    def near(self, parts):
        self.around = parts
        if self.plan.row == 8:
            own = parts[0].astype(F32) + self.plan.swap(parts[1], 1).astype(F32)
            self.own = own + self.plan.send(parts[2], [(5, 6), (6, 5)]).astype(F32)

    def total(self):
        row, rows = lax.axis_index("row"), self.rows
        if self.plan.row == 8:
            return jnp.where(row < 4, self.same, self.own)
        around = self.around.reshape(-1, self.around.shape[-1]).astype(F32)
        start = jnp.maximum(row * rows - CONT_MOST, 0)
        whole = jnp.zeros((self.plan.row * rows + CONT_MOST, around.shape[1]), F32)
        whole = whole.at[:PROMPT].set(self.prompt.reshape(PROMPT, -1).astype(F32))
        near = jnp.where(row * rows < PROMPT, 0, around)
        near = lax.dynamic_slice_in_dim(whole, start, rows + 2 * CONT_MOST, 0) + near
        whole = lax.dynamic_update_slice_in_dim(whole, near, start, 0)
        return lax.psum_scatter(whole[: self.plan.row * rows], "row", scatter_dimension=0, tiled=True)


def heads_mask(lanes, head):
    lane = lax.broadcasted_iota(jnp.int32, lanes, 1)
    return (lane >= head * HDIM) & (lane < (head + 1) * HDIM)


def nt(left, right):
    return lax.dot_general(left, right, (((1,), (1,)), ((), ())), preferred_element_type=F32)


def tn(left, right):
    return lax.dot_general(left, right, (((0,), (0,)), ((), ())), preferred_element_type=F32)


def attention_kernel(blocks, first, rows, *refs):
    spots = refs[:blocks]
    (near_ref, own_ref, wq_ref, wk_ref, wv_ref, bq_ref, bv_ref, segq_ref, segk_ref,
     q_ref, kp_ref, vp_ref, kn_ref, vn_ref, ctx_ref, lse_ref, x_ref, s_ref, sems) = refs[blocks:]
    near = near_ref[0]
    at = lambda b: pl.ds(pl.multiple_of(b * rows, rows), rows)

    @pl.when(pl.program_id(0) == 0)
    def _():
        copies = [
            pltpu.make_async_copy(spot, x_ref.at[pl.ds(i * rows, rows)], sems.at[i])
            for i, spot in enumerate(spots)
        ]
        for copy in copies:
            copy.start()
        for copy in copies:
            copy.wait()

    queries = (mm(own_ref[...], wq_ref[...]) + bq_ref[...]) * (HDIM**-0.5)
    q_ref[...] = queries.astype(BF)

    def project(b, k_ref, v_ref, side):
        x = x_ref[at(b), :]
        k_ref[at(side), :] = mm(x, wk_ref[...]).astype(BF)
        v_ref[at(side), :] = (mm(x, wv_ref[...]) + bv_ref[...]).astype(BF)

    @pl.loop(0, first)
    def _(b):
        project(b, kp_ref, vp_ref, b)

    @pl.loop(0, near)
    def _(b):
        project(first + b, kn_ref, vn_ref, b)

    width = q_ref.shape[1]
    heads = width // HDIM
    q = q_ref[...]
    parts = [jnp.where(heads_mask(q.shape, h), q, 0) for h in range(heads)]

    def scores(b, peaks, k_ref, base):
        k = k_ref[at(b), :]
        out = []
        for h in range(heads):
            s = nt(k, parts[h])
            if base:
                s = jnp.where(segk_ref[at(b), :] == segq_ref[...], s, MASK_FILL)
            s_ref[h, at(base + b), :] = s
            out.append(jnp.maximum(peaks[h], jnp.max(s, axis=0, keepdims=True)))
        return tuple(out)

    peaks = tuple(jnp.full((1, rows), MASK_FILL, F32) for _ in range(heads))
    peaks = lax.fori_loop(0, first, lambda b, c: scores(b, c, kp_ref, 0), peaks)
    peaks = lax.fori_loop(0, near, lambda b, c: scores(b, c, kn_ref, first), peaks)

    def mix(b, carry, v_ref, base):
        totals, mixed = carry
        vt = v_ref[at(b), :].T
        new_totals, new_mixed = [], []
        for h in range(heads):
            p = jnp.exp(s_ref[h, at(base + b), :] - peaks[h])
            new_totals.append(totals[h] + jnp.sum(p, axis=0, keepdims=True))
            new_mixed.append(mixed[h] + mm(vt[h * HDIM : (h + 1) * HDIM], p.astype(BF)))
        return tuple(new_totals), tuple(new_mixed)

    zero = (
        tuple(jnp.zeros((1, rows), F32) for _ in range(heads)),
        tuple(jnp.zeros((HDIM, rows), F32) for _ in range(heads)),
    )
    carry = lax.fori_loop(0, first, lambda b, c: mix(b, c, vp_ref, 0), zero)
    totals, mixed = lax.fori_loop(0, near, lambda b, c: mix(b, c, vn_ref, first), carry)
    whole = jnp.concatenate([mixed[h] / totals[h] for h in range(heads)], 0)
    ctx_ref[...] = whole.T.astype(BF)
    for h in range(heads):
        lse_ref[0, h : h + 1, :] = peaks[h] + jnp.log(totals[h])


def attention_call(spots, first, near, own, wq, wk, wv, bq, bv, segq, segk):
    rows, width = own.shape
    blocks = len(spots)
    tall = blocks * rows
    part = 256
    steps = width // part
    heads = part // HDIM
    cols = lambda depth: pl.BlockSpec((depth, part), lambda g: (0, g))
    flops = 2 * tall * width * width * 2 + 4 * tall * rows * width * 4
    return pl.pallas_call(
        functools.partial(attention_kernel, blocks, first, rows),
        grid=(steps,),
        in_specs=[pl.BlockSpec(memory_space=pl.ANY)] * blocks
        + [
            pl.BlockSpec(memory_space=pltpu.SMEM),
            pl.BlockSpec((rows, width), lambda g: (0, 0)),
            cols(width), cols(width), cols(width), cols(1), cols(1),
            pl.BlockSpec((1, rows), lambda g: (0, 0)),
            pl.BlockSpec(segk.shape, lambda g: (0, 0)),
        ],
        out_specs=[
            cols(rows), cols(PROMPT), cols(PROMPT), cols(tall - PROMPT), cols(tall - PROMPT),
            cols(rows), pl.BlockSpec((1, 8, rows), lambda g: (g, 0, 0)),
        ],
        out_shape=[
            jax.ShapeDtypeStruct((rows, width), BF),
            jax.ShapeDtypeStruct((PROMPT, width), BF),
            jax.ShapeDtypeStruct((PROMPT, width), BF),
            jax.ShapeDtypeStruct((tall - PROMPT, width), BF),
            jax.ShapeDtypeStruct((tall - PROMPT, width), BF),
            jax.ShapeDtypeStruct((rows, width), BF),
            jax.ShapeDtypeStruct((steps, 8, rows), F32),
        ],
        scratch_shapes=[
            pltpu.VMEM((tall, width), BF),
            pltpu.VMEM((heads, tall, rows), F32),
            pltpu.SemaphoreType.DMA((blocks,)),
        ],
        compiler_params=pltpu.CompilerParams(vmem_limit_bytes=60 * 2**20),
        cost_estimate=pl.CostEstimate(
            flops=flops, bytes_accessed=12 * 2**20, transcendentals=tall * rows * 12
        ),
        name="attention",
    )(*spots, near, own, wq, wk, wv, bq, bv, segq, segk)


def middle_kernel(wide, ctx_ref, own_ref, cot_ref, wo_ref, wi_ref, wu_ref, vec_ref, bin_ref,
                  out_ref, h1_ref, gctx_ref, dwo_ref, dwi_ref, dwu_ref, sums_ref, sbin_ref,
                  first_ref, n1_ref, inv_ref, low_ref, pre_ref, cdf_ref, act_ref, acc_ref,
                  gffn_ref, glow_ref):
    step = pl.program_id(0)
    width = ctx_ref.shape[1]
    square = lambda ref: ref[...].reshape(width, width)
    vec = lambda i: vec_ref[i : i + 1, :]
    mean = lambda v: jnp.sum(v, axis=-1, keepdims=True) * (1.0 / width)
    down = lambda v: jnp.sum(v, axis=0, keepdims=True)

    @pl.when(step == 0)
    def _():
        hidden = own_ref[...].astype(F32) + mm(ctx_ref[...], square(wo_ref)) + vec(0)
        centred = hidden - mean(hidden)
        inverse = lax.rsqrt(mean(centred * centred) + NORM_EPS)
        normed = centred * inverse
        n1_ref[...] = normed
        inv_ref[...] = inverse
        first = normed * vec(1) + vec(2)
        first_ref[...] = first
        low_ref[...] = first.astype(BF)

    @pl.when(step < wide)
    def _():
        chunk = pl.ds(pl.multiple_of(step * width, width), width)
        pre = mm(low_ref[...], square(wi_ref)) + bin_ref[pl.ds(step, 1), :]
        cdf = 0.5 * (1.0 + lax.erf(pre * SQRT_HALF))
        act = (pre * cdf).astype(BF)
        pre_ref[:, chunk] = pre
        cdf_ref[:, chunk] = cdf
        act_ref[:, chunk] = act
        more = mm(act, square(wu_ref))

        @pl.when(step == 0)
        def _():
            acc_ref[...] = more

        @pl.when(step > 0)
        def _():
            acc_ref[...] += more

    @pl.when(step == wide - 1)
    def _():
        hidden = first_ref[...] + acc_ref[...] + vec(3)
        centred = hidden - mean(hidden)
        inverse = lax.rsqrt(mean(centred * centred) + NORM_EPS)
        normed = centred * inverse
        out_ref[...] = (normed * vec(4) + vec(5)).astype(BF)
        grad = cot_ref[...].astype(F32)
        sums_ref[0:1, :] = down(grad * normed)
        sums_ref[1:2, :] = down(grad)
        e = grad * vec(4)
        back = inverse * (e - mean(e) - normed * mean(e * normed))
        gffn_ref[...] = back
        low = back.astype(BF)
        glow_ref[...] = low
        sums_ref[2:3, :] = down(low.astype(F32))

    @pl.when(step >= wide)
    def _():
        at = 2 * wide - 1 - step
        chunk = pl.ds(pl.multiple_of(at * width, width), width)
        pre = pre_ref[:, chunk]
        slope = cdf_ref[:, chunk] + pre * jnp.exp(-0.5 * pre * pre) * INV_ROOT_TAU
        low = glow_ref[...]
        grad = (nt(low, square(wu_ref)) * slope).astype(BF)
        sbin_ref[pl.ds(at, 1), :] = down(grad.astype(F32))
        dwu_ref[...] = tn(act_ref[:, chunk], low).astype(BF)
        dwi_ref[0] = tn(low_ref[...], grad).astype(BF)
        gffn_ref[...] += nt(grad, square(wi_ref))

    @pl.when(step == 2 * wide - 1)
    def _():
        grad = gffn_ref[...]
        normed = n1_ref[...]
        sums_ref[3:4, :] = down(grad * normed)
        sums_ref[4:5, :] = down(grad)
        e = grad * vec(1)
        back = inv_ref[...] * (e - mean(e) - normed * mean(e * normed))
        h1_ref[...] = back
        low = back.astype(BF)
        sums_ref[5:6, :] = down(low.astype(F32))
        sums_ref[6:8, :] = jnp.zeros((2, width), F32)
        dwo_ref[...] = tn(ctx_ref[...], low).astype(BF)
        gctx_ref[...] = nt(low, square(wo_ref)).astype(BF)


def middle_call(ctx, own, cot, got, vec, b_inner):
    rows, width = own.shape
    owners = got.shape[0]
    each = width // owners
    wide = got.shape[1] // each // 2
    whole = lambda shape: pl.BlockSpec(shape, lambda s: (0,) * len(shape))
    at = lambda s: jnp.where(s < wide, s, 2 * wide - 1 - s)
    back = lambda s: jnp.where(s < wide, wide - 1, 2 * wide - 1 - s)
    shape = jax.ShapeDtypeStruct
    return pl.pallas_call(
        functools.partial(middle_kernel, wide),
        grid=(2 * wide,),
        in_specs=[
            whole((rows, width)), whole((rows, width)), whole((rows, width)),
            pl.BlockSpec((owners, each, width), lambda s: (0, wide, 0)),
            pl.BlockSpec((owners, each, width), lambda s: (0, wide + 1 + at(s), 0)),
            pl.BlockSpec((owners // wide, wide * each, width), lambda s: (at(s), 0, 0)),
            whole((8, width)), whole((8, width)),
        ],
        out_specs=[
            whole((rows, width)), whole((rows, width)), whole((rows, width)), whole((width, width)),
            pl.BlockSpec((1, width, width), lambda s: (back(s), 0, 0)),
            pl.BlockSpec((width, width), lambda s: (back(s), 0)),
            whole((8, width)), whole((8, width)),
        ],
        out_shape=[
            shape((rows, width), BF), shape((rows, width), F32), shape((rows, width), BF),
            shape((width, width), BF), shape((wide, width, width), BF),
            shape((wide * width, width), BF), shape((8, width), F32), shape((8, width), F32),
        ],
        scratch_shapes=[
            pltpu.VMEM((rows, width), F32), pltpu.VMEM((rows, width), F32), pltpu.VMEM((rows, 1), F32),
            pltpu.VMEM((rows, width), BF), pltpu.VMEM((rows, wide * width), F32),
            pltpu.VMEM((rows, wide * width), F32), pltpu.VMEM((rows, wide * width), BF),
            pltpu.VMEM((rows, width), F32), pltpu.VMEM((rows, width), F32),
            pltpu.VMEM((rows, width), BF),
        ],
        compiler_params=pltpu.CompilerParams(vmem_limit_bytes=60 * 2**20),
        cost_estimate=pl.CostEstimate(
            flops=2 * rows * width * width * (6 * wide + 3), bytes_accessed=32 * 2**20,
            transcendentals=2 * rows * width * wide,
        ),
        name="middle",
    )(ctx, own, cot, got, got, got, vec, b_inner)


def back_kernel(rows, bound, *refs):
    (near_ref, gctx_ref, ctx_ref, q_ref, k_ref, v_ref, lse_ref, segq_ref, segk_ref, dq0_ref,
     dk_ref, dv_ref, dq_ref) = refs
    q, g = q_ref[...], gctx_ref[...]
    part = q.shape[1]
    heads = part // HDIM
    masks = [heads_mask(q.shape, h) for h in range(heads)]
    q_parts = [jnp.where(m, q, 0) for m in masks]
    g_parts = [jnp.where(m, g, 0) for m in masks]
    product = (g.astype(F32) * ctx_ref[...].astype(F32)).T
    inner = [
        jnp.sum(product[h * HDIM : (h + 1) * HDIM], axis=0, keepdims=True) for h in range(heads)
    ]

    def one(b, dq):
        here = pl.ds(pl.multiple_of(b * rows, rows), rows)
        k, v = k_ref[here, :], v_ref[here, :]
        kt = k.T
        if bound is None:
            allowed = segk_ref[here, :] == segq_ref[...]
        dk = jnp.zeros((rows, part), F32)
        dv = jnp.zeros((rows, part), F32)
        out = []
        for h in range(heads):
            s = nt(k, q_parts[h])
            if bound is None:
                s = jnp.where(allowed, s, MASK_FILL)
            p = jnp.exp(s - lse_ref[0, h : h + 1, :])
            dp = nt(v, g_parts[h])
            ds = (p * (dp - inner[h])).astype(BF)
            dv = dv + mm(p.astype(BF), g_parts[h])
            dk = dk + mm(ds, q_parts[h])
            out.append(dq[h] + mm(kt[h * HDIM : (h + 1) * HDIM], ds))
        dk_ref[here, :] = dk.astype(BF)
        dv_ref[here, :] = dv.astype(BF)
        return tuple(out)

    dq = tuple(dq0_ref[h * HDIM : (h + 1) * HDIM, :] for h in range(heads))
    dq = lax.fori_loop(0, near_ref[0] if bound is None else bound, one, dq)
    dq_ref[...] = jnp.concatenate(dq, 0)


def back_call(start, steps, bound, near, gctx, ctx, q, k, v, lse, segq, segk, dq0):
    rows = q.shape[0]
    tall = k.shape[0]
    part = 256
    cols = lambda depth: pl.BlockSpec((depth, part), lambda g: (0, start + g))
    mine = lambda depth: pl.BlockSpec((depth, part), lambda g: (0, g))
    whole = lambda shape: pl.BlockSpec(shape, lambda g: (0,) * len(shape))
    shape = jax.ShapeDtypeStruct
    return pl.pallas_call(
        functools.partial(back_kernel, rows, bound),
        grid=(steps,),
        in_specs=[
            pl.BlockSpec(memory_space=pltpu.SMEM),
            cols(rows), cols(rows), cols(rows), cols(tall), cols(tall),
            pl.BlockSpec((1, 8, rows), lambda g: (start + g, 0, 0)),
            whole((1, rows)), whole(segk.shape),
            pl.BlockSpec((part, rows), lambda g: (g, 0)),
        ],
        out_specs=[mine(tall), mine(tall), pl.BlockSpec((part, rows), lambda g: (g, 0))],
        out_shape=[
            shape((tall, steps * part), BF), shape((tall, steps * part), BF),
            shape((steps * part, rows), F32),
        ],
        compiler_params=pltpu.CompilerParams(vmem_limit_bytes=60 * 2**20),
        cost_estimate=pl.CostEstimate(
            flops=2 * 10 * 2 * tall * rows * part * steps * 2,
            bytes_accessed=8 * tall * part * steps, transcendentals=tall * rows * 4 * steps,
        ),
        name="attention_back",
    )(near, gctx, ctx, q, k, v, lse, segq, segk, dq0)


def product_kernel(rows, bound, near_ref, dk_ref, dv_ref, wk_ref, wv_ref, gx_ref):
    @pl.when((pl.program_id(0) < near_ref[0]) | (bound is not None))
    def _():
        gx_ref[0] = (nt(dk_ref[...], wk_ref[...]) + nt(dv_ref[...], wv_ref[...])).astype(BF)


def product_call(bound, near, dk, dv, wk, wv, rows):
    tall, width = dk.shape
    whole = lambda shape: pl.BlockSpec(shape, lambda b: (0,) * len(shape))
    return pl.pallas_call(
        functools.partial(product_kernel, rows, bound),
        grid=(tall // rows,),
        in_specs=[
            pl.BlockSpec(memory_space=pltpu.SMEM),
            pl.BlockSpec((rows, width), lambda b: (b, 0)),
            pl.BlockSpec((rows, width), lambda b: (b, 0)),
            whole((width, width)), whole((width, width)),
        ],
        out_specs=pl.BlockSpec((1, rows, width), lambda b: (b, 0, 0)),
        out_shape=jax.ShapeDtypeStruct((tall // rows, rows, width), BF),
        compiler_params=pltpu.CompilerParams(vmem_limit_bytes=60 * 2**20),
        cost_estimate=pl.CostEstimate(
            flops=4 * tall * width * width, bytes_accessed=6 * tall * width, transcendentals=0
        ),
        name="token_product",
    )(near, dk, dv, wk, wv)


def weight_kernel(blocks, first, rows, *refs):
    spots = refs[:blocks]
    (near_ref, own_ref, dq_ref, wq_ref, h1_ref, dkp_ref, dvp_ref, dkn_ref, dvn_ref,
     dwq_ref, dwkv_ref, gown_ref, sums_ref, x_ref, sems) = refs[blocks:]
    at = lambda b: pl.ds(pl.multiple_of(b * rows, rows), rows)
    step = pl.program_id(0)

    @pl.when(step == 0)
    def _():
        copies = [
            pltpu.make_async_copy(spot, x_ref.at[pl.ds(i * rows, rows)], sems.at[i])
            for i, spot in enumerate(spots)
        ]
        for copy in copies:
            copy.start()
        for copy in copies:
            copy.wait()
        gown_ref[...] = h1_ref[...]

    scale = HDIM**-0.5
    dq = dq_ref[...].T.astype(BF)
    part = dq.shape[1]
    gown_ref[...] += nt(dq, wq_ref[...]) * scale
    dwq_ref[...] = (tn(own_ref[...], dq) * scale).astype(BF)
    sums_ref[0:1, :] = jnp.sum(dq.astype(F32), axis=0, keepdims=True) * scale

    def products(b, carry, dk_ref, dv_ref, base):
        dk, dv, x = dk_ref[at(b), :], dv_ref[at(b), :], x_ref[at(base + b), :]
        wk, wv, bv = carry
        bv = bv + jnp.sum(dv.astype(F32), axis=0, keepdims=True)
        return wk + tn(x, dk), wv + tn(x, dv), bv

    width = x_ref.shape[1]
    zero = jnp.zeros((width, part), F32)
    carry = (zero, zero, jnp.zeros((1, part), F32))
    carry = lax.fori_loop(0, first, lambda b, c: products(b, c, dkp_ref, dvp_ref, 0), carry)
    carry = lax.fori_loop(0, near_ref[0], lambda b, c: products(b, c, dkn_ref, dvn_ref, first), carry)
    wk, wv, bv = carry
    dwkv_ref[:, :part] = wk.astype(BF)
    dwkv_ref[:, part:] = wv.astype(BF)
    sums_ref[1:2, :] = bv
    sums_ref[2:8, :] = jnp.zeros((6, part), F32)


def weight_call(spots, first, near, own, dq, wq, h1, dkp, dvp, dkn, dvn):
    rows, width = own.shape
    blocks = len(spots)
    tall = blocks * rows
    part = 256
    steps = width // part
    cols = lambda depth, size=part: pl.BlockSpec((depth, size), lambda g: (0, g))
    whole = lambda shape: pl.BlockSpec(shape, lambda g: (0,) * len(shape))
    shape = jax.ShapeDtypeStruct
    return pl.pallas_call(
        functools.partial(weight_kernel, blocks, first, rows),
        grid=(steps,),
        in_specs=[pl.BlockSpec(memory_space=pl.ANY)] * blocks
        + [
            pl.BlockSpec(memory_space=pltpu.SMEM),
            whole((rows, width)), pl.BlockSpec((part, rows), lambda g: (g, 0)), cols(width),
            whole((rows, width)), cols(PROMPT), cols(PROMPT), cols(tall - PROMPT), cols(tall - PROMPT),
        ],
        out_specs=[cols(width), cols(width, 2 * part), whole((rows, width)), cols(8)],
        out_shape=[
            shape((width, width), BF), shape((width, 2 * width), BF), shape((rows, width), F32),
            shape((8, width), F32),
        ],
        scratch_shapes=[pltpu.VMEM((tall, width), BF), pltpu.SemaphoreType.DMA((blocks,))],
        compiler_params=pltpu.CompilerParams(vmem_limit_bytes=60 * 2**20),
        cost_estimate=pl.CostEstimate(
            flops=4 * tall * width * width, bytes_accessed=12 * tall * width, transcendentals=0
        ),
        name="weight_product",
    )(*spots, near, own, dq, wq, h1, dkp, dvp, dkn, dvn)


def solution(mesh):
    plan = Plan(mesh.shape["grp"], mesh.shape["row"])

    def per_device(
        tokens, cont_lengths, cotangent, w_query, w_key, w_value, w_output, w_inner, w_outer,
        bias_query, bias_value, bias_output, gain_first, shift_first, bias_inner, bias_outer,
        gain_second, shift_second,
    ):
        count = plan.count
        _, rows, width = tokens.shape
        step = w_query.shape[0]
        wide = w_inner.shape[1] // width
        row = lax.axis_index("row")
        scale = HDIM ** (-0.5)
        own = tokens[0]

        vectors = (
            bias_query, bias_value, bias_output, gain_first, shift_first, bias_outer, gain_second,
            shift_second, bias_inner,
        )
        line = jnp.concatenate(vectors)
        small = len(vectors) - 1
        line = jnp.pad(line, (0, width - line.shape[0]))[None]
        line = jnp.pad(line, ((0, 7), (0, 0)))
        inner_rows = w_inner.reshape(step, wide, width).transpose(1, 0, 2).reshape(-1, width)
        pack_c = jnp.concatenate([w_outer, w_output, inner_rows], 0)
        got_c = lax.all_gather(pack_c, AXES, axis=0, tiled=True).reshape(count, -1, width)

        gather = Gather(plan, jnp.concatenate([w_query, w_key, w_value, line], 0))
        exchange = Tokens(plan, own)
        gather.stage(plan.z)
        gather.held, *seen = tie(gather.held, *exchange.stage_one())
        if seen:
            exchange.same, exchange.beside = seen
        gather.stage(plan.y)
        gather.held, *seen = tie(gather.held, *exchange.stage_two())
        if seen:
            exchange.other, exchange.same_y, exchange.diagonal = seen
        gather.stage(plan.x)
        exchange.stage_three()
        gather.stage(plan.core)
        got_a = gather.ordered()
        spots, near = exchange.spots()
        first_near = PROMPT // rows

        full_query, full_key, full_value = [
            got_a[:, i * step : (i + 1) * step].reshape(width, width) for i in range(3)
        ]
        lines = got_a[:, 3 * step]
        table = lines[:, : small * step].reshape(count, small, step).transpose(1, 0, 2)
        table = table.reshape(small, width).astype(F32)
        v_bin = lines[:, small * step : (small + wide) * step].reshape(wide, width).astype(F32)
        v_bin = jnp.pad(v_bin, ((0, 8 - wide), (0, 0)))
        segments = segment_ids(cont_lengths[0], plan.row * rows)
        seg_own = lax.dynamic_slice_in_dim(segments, row * rows, rows, 0)[None, :]
        seg_near = near_segments(plan, segments, rows)[:, None]
        near = near.astype(jnp.int32).reshape(1)

        queries, keys_p, values_p, keys_n, values_n, context, log_total = attention_call(
            spots, first_near, near, own, full_query, full_key, full_value, table[0:1], table[1:2],
            seg_own, seg_near,
        )

        if step % 8:
            cuts = [wide * step, (wide + 1) * step]
            outer, output, inner = jnp.split(got_c, cuts, axis=1)
            inner = inner.reshape(count, wide, step, width).transpose(1, 0, 2, 3)
            inner = inner.reshape(wide, 32, width // 32, width).transpose(1, 0, 2, 3)
            got_c = jnp.concatenate(
                [v.reshape(32, -1, width) for v in (outer, output, inner)], 1
            )
        vec = jnp.concatenate([table[2:], jnp.zeros((2, width), F32)], 0)
        layer_out, grad_h1, grad_context, d_output, d_inner, d_outer, sums, sums_bin = middle_call(
            context, own, cotangent[0], got_c, vec, v_bin
        )
        by_owner = lambda grad: grad.reshape(count, step, -1)
        r_outer = Reduce(plan, d_outer.reshape(count, wide * step, width))
        r_inner = Reduce(plan, d_inner.reshape(wide, count, step, width), 1)
        r_output = Reduce(plan, by_owner(d_output))
        big = (r_outer, r_inner, r_output)

        def hold(*values):
            tied = tie(*[r.value for r in big], *values)
            for r, value in zip(big, tied):
                r.value = value
            return tied[len(big) :]

        part = 256
        none = jnp.zeros((part, rows), F32)
        back = lambda start, gctx: back_call(
            start, 1, first_near, near, gctx, context, queries, keys_p, values_p, log_total,
            seg_own, seg_near, none,
        )
        heads_p = [back(0, grad_context)]
        for r in big:
            r.stage(plan.core)
        (grad_context,) = hold(grad_context)
        r_outer.stage(plan.x)
        r_inner.stage(plan.y)
        r_output.stage(plan.x)
        heads_p += [back(i, grad_context) for i in range(1, width // part)]
        dkp, dvp, dqp = [
            jnp.concatenate([h[i] for h in heads_p], 1 if i < 2 else 0) for i in range(3)
        ]
        shared_p = product_call(first_near, near, dkp, dvp, full_key, full_value, rows)
        grad_context, dqp, shared_p = hold(grad_context, dqp, shared_p)
        returned = Return(plan, rows)
        returned.prompt_one(shared_p)
        r_outer.stage(plan.y)
        r_inner.stage(plan.x)
        r_output.stage(plan.y)
        dkn, dvn, dq = back_call(
            0, width // part, None, near, grad_context, context, queries, keys_n, values_n, log_total,
            seg_own, seg_near, dqp,
        )
        shared_n = product_call(None, near, dkn, dvn, full_key, full_value, rows)
        d_query, d_both, grad_own, sums_qkv = weight_call(
            spots, first_near, near, own, dq, full_query, grad_h1, dkp, dvp, dkn, dvn
        )
        returned.prompt_two()
        d_query, d_both, shared_n, returned.same = hold(d_query, d_both, shared_n, returned.same)
        returned.prompt_three()
        returned.near(shared_n)
        for r in big:
            r.stage(plan.z)
        o_outer, o_inner, o_output = [r.value.reshape(r.lead + r.rest) for r in big]
        grad_tokens = grad_own + returned.total()

        order = (5, 3, 4, 2, 0, 1)
        d_table = jnp.concatenate([sums_qkv[:2]] + [sums[i : i + 1] for i in order], 0)
        d_lines = jnp.concatenate(
            [
                d_table.reshape(small, count, step).transpose(1, 0, 2).reshape(count, -1),
                sums_bin[:wide].reshape(count, wide * step),
            ],
            1,
        )
        d_lines = jnp.pad(d_lines, ((0, 0), (0, width - d_lines.shape[1])))[:, None].astype(BF)
        d_lines = jnp.pad(d_lines, ((0, 0), (0, 7), (0, 0)))
        r_query = Reduce(plan, jnp.concatenate([by_owner(d_query), d_lines], 1))
        r_both = Reduce(plan, by_owner(d_both))
        for one, two in ((plan.core, plan.core), (plan.x, plan.y), (plan.y, plan.x), (plan.z, plan.z)):
            r_query.stage(one)
            r_both.stage(two)
        o_query = r_query.value
        o_line = o_query[step]
        o_both = r_both.value.reshape(step, width // part, 2, part)

        o_small = [o_line[i * step : (i + 1) * step] for i in range(small)]
        o_bin = o_line[small * step : (small + wide) * step]
        return (
            layer_out[None],
            grad_tokens.astype(BF)[None],
            o_query[:step],
            o_both[:, :, 0].reshape(step, width),
            o_both[:, :, 1].reshape(step, width),
            o_output,
            o_inner.transpose(1, 0, 2).reshape(step, wide * width),
            o_outer,
            o_small[0],
            o_small[1],
            o_small[2],
            o_small[3],
            o_small[4],
            o_bin,
            o_small[5],
            o_small[6],
            o_small[7],
        )

    split = P("grp", "row", None)
    owned2, owned1 = P(AXES, None), P(AXES)
    in_specs = (split, P("grp", None), split) + (owned2,) * 6 + (owned1,) * 9
    out_specs = (split, split) + (owned2,) * 6 + (owned1,) * 9
    return jax.shard_map(
        per_device, mesh=mesh, in_specs=in_specs, out_specs=out_specs, check_vma=False
    )
```

time: 425 us -> 437 us (1.028)
  starting transfers between devices: 125 us -> 104 us
  Pallas kernels: 74.1 us -> 92.7 us
  other arithmetic: 22.3 us -> 32 us
  waiting for transfers between devices: 127 us -> 132 us
    ppermute x53 -> x44, starting transfers between devices: 115 us -> 95.5 us  [swap(): return lax.ppermute(value, AXES, [(i, i ^ mask) for i in range(self.count)])]
    pallas_call x1 -> x7, Pallas kernels: 35.5 us -> 54.1 us  [the longest x4 28.7 us: back_call(): pl.pallas_call(functools.partial(back_kernel, rows, bound), grid=(steps,)...]
    convert_element_type x12 -> x18, other arithmetic: 7.29 us -> 17.9 us  [the longest x15 16.6 us: stage(): self.value = value.astype(BF) if self.left else value]
    dynamic_slice x15 -> x19, local copies, waits for them, and re-layouts: 3.58 us -> 13.4 us  [part(): array = lax.dynamic_slice_in_dim(array, place, 1, axis)]
    slice x6 -> x4, local copies, waits for them, and re-layouts: 12.3 us -> 6 us  [the longest x1 3.9 us: per_device(): got_a[:, i * step:(i + 1) * step].reshape(width, width)]
    concatenate x7, other arithmetic: 1.85 us -> 7.91 us  [the longest x4 5.08 us: stage(): jnp.concatenate([self.held] + [self.plan.swap(self.held, m) for m in mask...]
    unnamed x46 -> x80, local copies, waits for them, and re-layouts: 8.47 us -> 14.1 us
    ppermute x53 -> x44, waiting for transfers between devices: 127 us -> 131 us  [swap(): return lax.ppermute(value, AXES, [(i, i ^ mask) for i in range(self.count)])]
  transfers between devices with their start and end apart: 58 -> 49, of which waited for: 29 -> 16; matrix products, arithmetic and copies ran while one was open for 15% -> 16% of each run, Pallas kernels for 5% -> 13%
where the time goes in v4:
time: 437 us; the launch traced here: 435 us
  waiting for transfers between devices  132 us (30%)
  starting transfers between devices  104 us (24%)
  Pallas kernels  92.7 us (21%)
  local copies, waits for them, and re-layouts  59.2 us (14%)
  other arithmetic  32 us (7%)
  between operations  14.9 us (3%)
    ppermute x44, waiting for transfers between devices, swap(): return lax.ppermute(value, AXES, [(i, i ^ mask) for i in range(self.count)])  131 us
    ppermute x44, starting transfers between devices, swap(): return lax.ppermute(value, AXES, [(i, i ^ mask) for i in range(self.count)])  95.5 us
    pallas_call x4, Pallas kernels, back_call(): pl.pallas_call(functools.partial(back_kernel, rows, bound), grid=(steps,)...  28.7 us
    pallas_call x1, Pallas kernels, middle_call(): pl.pallas_call(functools.partial(middle_kernel, wide), grid=(2 * wide,),...  19.7 us
    pallas_call x1, Pallas kernels, attention_call(): pl.pallas_call(functools.partial(attention_kernel, blocks, first, rows),...  18.9 us
    convert_element_type x15, other arithmetic, stage(): self.value = value.astype(BF) if self.left else value  16.6 us
    pallas_call x1, Pallas kernels, weight_call(): pl.pallas_call(functools.partial(weight_kernel, blocks, first, rows), gri...  14.9 us
    unnamed x80, local copies, waits for them, and re-layouts  14.1 us
  transfers between devices with their start and end apart: 49, of which 16 were waited for; matrix products, arithmetic and copies ran while one was open for 16% of the time, Pallas kernels for 13%

profile of v4, /device:TPU:0, one launch (start us, length us, event | category | flops | bytes accessed | tf_op | source)
XLA Modules:
  0.0 435.3 jit_solution(17849089028995420284)
XLA Ops:
  8.2 1.7 pad_maximum_fusion.5
  9.9 6.0 %collective-permute-start.3 = (bf16[256,768]{1,0:T(8,128)(2,1)}, bf16[256,768]{1,0:T(8,128)(2,1)S(1)}, u32[]{:S(2)}, u32[]{:S(2)}) collective-permute-start(bf16[256,768]{1,0:T(8,128)(2,1)} %bitcast.154), channel_id=1, source_target_pairs={{0,4},{1,5},{2,6},{3,7},{8,12},{9,13},{10,14},{11,15},{16,20},{17,... | collective-permute-start | bytes 1179656 | tf_op jit(solution)/shard_map/ppermute | solution.py:50
  15.9 6.1 %concatenate.54 = bf16[288]{0:T(512)(128)(2,1)S(1)} concatenate(bf16[24]{0:T(256)(128)(2,1)} %param.28, bf16[24]{0:T(256)(128)(2,1)} %param.29, bf16[24]{0:T(256)(128)(2,1)} %param.30, bf16[24]{0:T(256)(128)(2,1)} %param.31, bf16[24]{0:T(256)(128)(2,1)} %param.32, bf16[24]{0:T(256)(128)(2,1)} %param.34, bf16[24]{0:T(256)(128)(2,1)} %param.35, bf16[24]{0:T(256)(128)(2,1)} %param.36, ...), dimensions={0} | concatenate | bytes 1152 | tf_op jit(solution)/shard_map/concatenate | solution.py:682
  22.8 1.6 collective-permute-start
  24.5 2.8 collective-permute-start.2
  28.8 2.9 collective-permute-done
  31.7 9.8 %collective-permute-done.1 = bf16[1,80,768]{2,1,0:T(8,128)(2,1)S(1)} collective-permute-done((bf16[1,80,768]{2,1,0:T(8,128)(2,1)S(1)}, bf16[1,80,768]{2,1,0:T(8,128)(2,1)S(1)}, u32[]{:S(2)}, u32[]{:S(2)}) %collective-permute-start.1) | collective-permute-done | bytes 122912 | tf_op jit(solution)/shard_map/ppermute | solution.py:46
  43.8 15.5 %collective-permute-start.6 = (bf16[256,768]{1,0:T(8,128)(2,1)S(1)}, bf16[256,768]{1,0:T(8,128)(2,1)S(1)}, u32[]{:S(2)}, u32[]{:S(2)}) collective-permute-start(bf16[256,768]{1,0:T(8,128)(2,1)S(1)} %broadcast_select_fusion.refs_0_), channel_id=1, source_target_pairs={{0,2},{1,3},{2,0},{3,1},{4,6},{5,7},{6,4},{7,5},{8,10},{9,11},{10,... | collective-permute-start | bytes 1179656 | tf_op jit(solution)/shard_map/ppermute | solution.py:46
  59.8 14.3 %collective-permute-done.6.refs_1_ = bf16[256,768]{1,0:T(8,128)(2,1)S(1)} collective-permute-done((bf16[256,768]{1,0:T(8,128)(2,1)S(1)}, bf16[256,768]{1,0:T(8,128)(2,1)S(1)}, u32[]{:S(2)}, u32[]{:S(2)}) %collective-permute-start.6) | collective-permute-done | bytes 393248 | tf_op jit(solution)/shard_map/ppermute | solution.py:46
  76.7 41.0 %collective-permute-done.10 = bf16[8,80,768]{2,1,0:T(8,128)(2,1)S(1)} collective-permute-done((bf16[8,80,768]{2,1,0:T(8,128)(2,1)S(1)}, bf16[8,80,768]{2,1,0:T(8,128)(2,1)S(1)}, u32[]{:S(2)}, u32[]{:S(2)}) %collective-permute-start.10) | collective-permute-done | bytes 983072 | tf_op jit(solution)/shard_map/ppermute | solution.py:46
  123.6 3.5 pad_maximum_fusion
  127.1 4.8 %gather_fusion.1 = bf16[32,80,768]{2,1,0:T(8,128)(2,1)} fusion(bf16[32,80,768]{2,1,0:T(8,128)(2,1)} %pad_maximum_fusion, s32[1024]{0:T(1024)S(1)} %pad_clamp_fusion), kind=kCustom, calls=%fused_computation.1 | custom fusion | bytes 7864448 | tf_op jit(solution)/shard_map/jit(_take)/gather | solution.py:79
  136.1 3.9 fusion.34
  140.7 18.9 %attention.1 = (bf16[256,768]{1,0:T(8,128)(2,1)}, bf16[1024,768]{1,0:T(8,128)(2,1)}, bf16[1024,768]{1,0:T(8,128)(2,1)}, bf16[768,768]{1,0:T(8,128)(2,1)}, bf16[7...) custom-call(bf16[256,768]{1,0:T(8,128)(2,1)} %copy-done.16, bf16[256,768]{1,0:T(8,128)(2,1)} %copy-done.30, ...), custom_call_target="tpu_custom_call" | custom-call | flops 9865003008 | bytes 12582912 | tf_op jit(solution)/shard_map/attention/pallas_call | solution.py:313
  159.6 19.7 %middle.1 = (bf16[256,768]{1,0:T(8,128)(2,1)}, f32[256,768]{1,0:T(8,128)}, bf16[256,768]{1,0:T(8,128)(2,1)}, bf16[768,768]{1,0:T(8,128)(2,1)}, bf16[4,768,768]{2...) custom-call(bf16[256,768]{1,0:T(8,128)(2,1)} %get-tuple-element.79.ctx_ref.refs_2_, ...), custom_call_target="tpu_custom_call" | custom-call | flops 8153726976 | bytes 33554432 | tf_op jit(solution)/shard_map/middle/pallas_call | solution.py:447
  179.4 3.3 constant_dynamic-slice_fusion.19
  182.7 2.8 constant_dynamic-slice_fusion.21
  190.4 7.8 %attention_back.4 = (bf16[1024,256]{1,0:T(8,128)(2,1)}, bf16[1024,256]{1,0:T(8,128)(2,1)}, f32[256,256]{1,0:T(8,128)}) custom-call(s32[1]{0:T(128)} %bitcast.2.refs_7_.refs_0_.near_ref, bf16[256,768]{1,0:T(8,128)(2,1)} %get-tuple-element.102.refs_1_, bf16[256,768]{1,0:T(8,128)(2,1)} %get-tuple-element.79.ctx_ref.refs_2_, ...), custom_call_target="tpu_custom_call" | custom-call | flops 5368709120 | bytes 2097152 | tf_op jit(solution)/shard_map/attention_back/pallas_call | solution.py:534
  198.2 1.9 constant_dynamic-update-slice_fusion.5
  202.8 1.9 constant_dynamic-update-slice_fusion.2
  208.0 4.6 %fusion.1 = bf16[4,2,2,2,2,24,768]{6,5,4,3,2,1,0:T(8,128)(2,1)} fusion(bf16[4,2,1,2,2,2,24,768]{7,6,5,4,3,2,1,0:T(8,128)(2,1)} %collective-permute-done.13, bf16[4,2,2,2,2,2,24,768]{7,6,5,4,3,2,1,0:T(8,128)(2,1)} %bitcast.151, s32[]{:T(128)S(6)} %select_n.292), kind=kLoop, calls=%fused_computation.6 | loop fusion | flops 4718592 | bytes 7077892 | tf_op jit(solution)/shard_map/convert_element_type | solution.py:105
  212.6 3.8 fusion
  216.3 7.8 %attention_back.5 = (bf16[1024,256]{1,0:T(8,128)(2,1)}, bf16[1024,256]{1,0:T(8,128)(2,1)}, f32[256,256]{1,0:T(8,128)}) custom-call(s32[1]{0:T(128)} %bitcast.2.refs_7_.refs_0_.near_ref, bf16[256,768]{1,0:T(8,128)(2,1)} %get-tuple-element.102.refs_1_, bf16[256,768]{1,0:T(8,128)(2,1)} %get-tuple-element.79.ctx_ref.refs_2_, ...), custom_call_target="tpu_custom_call" | custom-call | flops 5368709120 | bytes 2097152 | tf_op jit(solution)/shard_map/attention_back/pallas_call | solution.py:534
  224.1 7.8 %attention_back.6 = (bf16[1024,256]{1,0:T(8,128)(2,1)}, bf16[1024,256]{1,0:T(8,128)(2,1)}, f32[256,256]{1,0:T(8,128)}) custom-call(s32[1]{0:T(128)} %bitcast.2.refs_7_.refs_0_.near_ref, bf16[256,768]{1,0:T(8,128)(2,1)} %get-tuple-element.102.refs_1_, bf16[256,768]{1,0:T(8,128)(2,1)} %get-tuple-element.79.ctx_ref.refs_2_, ...), custom_call_target="tpu_custom_call" | custom-call | flops 5368709120 | bytes 2097152 | tf_op jit(solution)/shard_map/attention_back/pallas_call | solution.py:534
  231.9 2.5 constant_dynamic-slice_fusion.16
  241.9 6.4 %token_product.2 = bf16[4,256,768]{2,1,0:T(8,128)(2,1)} custom-call(s32[1]{0:T(128)} %bitcast.2.refs_7_.refs_0_.near_ref, bf16[1024,768]{1,0:T(8,128)(2,1)} %get-tuple-element.177.dk_ref.refs_12_, bf16[1024,768]{1,0:T(8,128)(2,1)} %copy-done.21, bf16[768,768]{1,0:T(8,128)(2,1)} %bitcast.167, bf16[768,768]{1,0:T(8,128)(2,1)} %bitcast.164), custom_call_target="tpu_custom_call" | custom-call | flops 2415919104 | bytes 4718592 | tf_op jit(solution)/shard_map/token_product/pallas_call | solution.py:567
  248.3 21.1 %collective-permute-done.17 = bf16[1,2,2,2,24,768]{5,4,2,1,3,0:T(8,128)(2,1)S(1)} collective-permute-done((bf16[1,2,2,2,24,768]{5,4,2,1,3,0:T(8,128)(2,1)S(1)}, bf16[1,2,2,2,24,768]{5,4,2,1,3,0:T(8,128)(2,1)S(1)}, u32[]{:S(2)}, u32[]{:S(2)}) %collective-permute-start.17) | collective-permute-done | bytes 294944 | tf_op jit(solution)/shard_map/ppermute | solution.py:46
  269.4 1.9 fusion.2
  271.4 1.7 fusion.3
  281.0 5.3 %attention_back.7 = (bf16[768,768]{1,0:T(8,128)(2,1)}, bf16[768,768]{1,0:T(8,128)(2,1)}, f32[768,256]{1,0:T(8,128)}) custom-call(s32[1]{0:T(128)} %bitcast.2.refs_7_.refs_0_.near_ref, bf16[256,768]{1,0:T(8,128)(2,1)} %get-tuple-element.102.refs_1_, bf16[256,768]{1,0:T(8,128)(2,1)} %get-tuple-element.79.ctx_ref.refs_2_, ...), custom_call_target="tpu_custom_call" | custom-call | flops 12079595520 | bytes 4718592 | tf_op jit(solution)/shard_map/attention_back/pallas_call | solution.py:534
  286.3 14.9 %weight_product.1 = (bf16[768,768]{1,0:T(8,128)(2,1)}, bf16[768,1536]{1,0:T(8,128)(2,1)}, f32[256,768]{1,0:T(8,128)}, f32[8,768]{1,0:T(8,128)}) custom-call(bf16[256,768]{1,0:T(8,128)(2,1)} %copy-done.16, bf16[256,768]{1,0:T(8,128)(2,1)} %copy-done.30, bf16[256,768]{1,0:T(8,128)(2,1)} %copy-done.31, bf16[256,768]{1,0:T(8,128)(2,1)} %copy-done.32, ...), custom_call_target="tpu_custom_call" | custom-call | flops 4227858432 | bytes 16515072 | tf_op jit(solution)/shard_map/weight_product/pallas_call | solution.py:639
  302.6 4.2 token_product.3
  308.0 2.8 collective-permute-start.23
  313.2 5.1 %collective-permute-done.23 = bf16[256,768]{1,0:T(8,128)(2,1)S(1)} collective-permute-done((bf16[256,768]{1,0:T(8,128)(2,1)S(1)}, bf16[256,768]{1,0:T(8,128)(2,1)S(1)}, u32[]{:S(2)}, u32[]{:S(2)}) %collective-permute-start.23) | collective-permute-done | bytes 393248 | tf_op jit(solution)/shard_map/ppermute | solution.py:46
  319.6 1.8 collective-permute-start.45
  321.7 29.3 %collective-permute-start.40 = (bf16[1,1,24,768]{3,2,1,0:T(8,128)(2,1)S(1)}, bf16[1,1,24,768]{3,2,1,0:T(8,128)(2,1)S(1)}, u32[]{:S(2)}, u32[]{:S(2)}) collective-permute-start(bf16[1,1,24,768]{3,2,1,0:T(8,128)(2,1)S(1)} %get-tuple-element.160), channel_id=1, source_target_pairs={{0,4},{1,5},{2,6},{3,7},{4,0},{5,1},{6,2},{7,3},{8,12},{9,13},{10,... | collective-permute-start | bytes 110600 | tf_op jit(solution)/shard_map/ppermute | solution.py:46
  355.3 2.6 collective-permute-start.43
  361.7 1.9 collective-permute-start.46
  363.6 9.9 %collective-permute-done.43 = bf16[4,1,1,24,768]{4,3,2,1,0:T(8,128)(2,1)S(1)} collective-permute-done((bf16[4,1,1,24,768]{4,3,2,1,0:T(8,128)(2,1)S(1)}, bf16[4,1,1,24,768]{4,3,2,1,0:T(8,128)(2,1)S(1)}, u32[]{:S(2)}, u32[]{:S(2)}) %collective-permute-start.43) | collective-permute-done | bytes 147488 | tf_op jit(solution)/shard_map/ppermute | solution.py:46
  373.5 2.6 collective-permute-start.47
  378.0 3.2 collective-permute-done.46
  386.7 7.5 %collective-permute-done.29 = bf16[2,2,1,32,768]{4,3,2,1,0:T(8,128)(2,1)S(1)} collective-permute-done((bf16[2,2,1,32,768]{4,3,2,1,0:T(8,128)(2,1)S(1)}, bf16[2,2,1,32,768]{4,3,2,1,0:T(8,128)(2,1)S(1)}, u32[]{:S(2)}, u32[]{:S(2)}) %collective-permute-start.29) | collective-permute-done | bytes 196640 | tf_op jit(solution)/shard_map/ppermute | solution.py:46
  394.3 8.0 %collective-permute-start.31 = (bf16[1,1,32,768]{3,2,1,0:T(8,128)(2,1)S(1)}, bf16[1,1,32,768]{3,2,1,0:T(8,128)(2,1)S(1)}, u32[]{:S(2)}, u32[]{:S(2)}) collective-permute-start(bf16[1,1,32,768]{3,2,1,0:T(8,128)(2,1)S(1)} %get-tuple-element.157), channel_id=1, source_target_pairs={{0,4},{1,5},{2,6},{3,7},{4,0},{5,1},{6,2},{7,3},{8,12},{9,13},{10,... | collective-permute-start | bytes 147464 | tf_op jit(solution)/shard_map/ppermute | solution.py:46
  405.3 3.0 collective-permute-done.32
  410.4 4.8 %collective-permute-done.35 = bf16[1,2,2,24,1536]{4,3,2,1,0:T(8,128)(2,1)S(1)} collective-permute-done((bf16[1,2,2,24,1536]{4,3,2,1,0:T(8,128)(2,1)S(1)}, bf16[1,2,2,24,1536]{4,3,2,1,0:T(8,128)(2,1)S(1)}, u32[]{:S(2)}, u32[]{:S(2)}) %collective-permute-start.35) | collective-permute-done | bytes 294944 | tf_op jit(solution)/shard_map/ppermute | solution.py:46
  415.5 5.0 %collective-permute-start.37 = (bf16[1,1,24,1536]{3,2,1,0:T(8,128)(2,1)S(1)}, bf16[1,1,24,1536]{3,2,1,0:T(8,128)(2,1)S(1)}, u32[]{:S(2)}, u32[]{:S(2)}) collective-permute-start(bf16[1,1,24,1536]{3,2,1,0:T(8,128)(2,1)S(1)} %get-tuple-element.154), channel_id=1, source_target_pairs={{0,4},{1,5},{2,6},{3,7},{4,0},{5,1},{6,2},{7,3},{8,12},{9,13},{10,... | collective-permute-start | bytes 221192 | tf_op jit(solution)/shard_map/ppermute | solution.py:46
  421.0 3.1 collective-permute-done.37
  424.1 2.5 collective-permute-done.38
  (244 shorter events, 75.3 us)
Async XLA Ops:
  7.2 152.4 %all-gather.2.cloned.1.call-start = ((), (), s32[]{:S(2)}) async-start(), calls=%async_computation | async-start | bytes 10948608 | tf_op jit(solution)/shard_map/all_gather | solution.py:688
  9.9 31.7 %collective-permute-start.3 = (bf16[256,768]{1,0:T(8,128)(2,1)}, bf16[256,768]{1,0:T(8,128)(2,1)S(1)}, u32[]{:S(2)}, u32[]{:S(2)}) collective-permute-start(bf16[256,768]{1,0:T(8,128)(2,1)} %bitcast.154), channel_id=1, source_target_pairs={{0,4},{1,5},{2,6},{3,7},{8,12},{9,13},{10,14},{11,15},{16,20},{17,... | collective-permute-start | bytes 1179656 | tf_op jit(solution)/shard_map/ppermute | solution.py:50
  22.8 8.9 %collective-permute-start = (bf16[1,80,768]{2,1,0:T(8,128)(2,1)S(1)}, bf16[1,80,768]{2,1,0:T(8,128)(2,1)S(1)}, u32[]{:S(2)}, u32[]{:S(2)}) collective-permute-start(bf16[1,80,768]{2,1,0:T(8,128)(2,1)S(1)} %fusion.26), channel_id=1, source_target_pairs={{0,2},{1,3},{2,0},{3,1},{4,6},{5,7},{6,4},{7,5},{8,10},{9,11},{10,... | collective-permute-start | bytes 368648 | tf_op jit(solution)/shard_map/ppermute | solution.py:46
  24.5 17.0 %collective-permute-start.1 = (bf16[1,80,768]{2,1,0:T(8,128)(2,1)S(1)}, bf16[1,80,768]{2,1,0:T(8,128)(2,1)S(1)}, u32[]{:S(2)}, u32[]{:S(2)}) collective-permute-start(bf16[1,80,768]{2,1,0:T(8,128)(2,1)S(1)} %fusion.26), channel_id=1, source_target_pairs={{0,4},{1,5},{2,6},{3,7},{4,0},{5,1},{6,2},{7,3},{8,12},{9,13},{10,... | collective-permute-start | bytes 368648 | tf_op jit(solution)/shard_map/ppermute | solution.py:46
  24.5 17.0 %collective-permute-start.2 = (bf16[1,80,768]{2,1,0:T(8,128)(2,1)S(1)}, bf16[1,80,768]{2,1,0:T(8,128)(2,1)S(1)}, u32[]{:S(2)}, u32[]{:S(2)}) collective-permute-start(bf16[1,80,768]{2,1,0:T(8,128)(2,1)S(1)} %fusion.26), channel_id=1, source_target_pairs={{0,6},{1,7},{2,4},{3,5},{4,2},{5,3},{6,0},{7,1},{8,14},{9,15},{10,... | collective-permute-start | bytes 368648 | tf_op jit(solution)/shard_map/ppermute | solution.py:46
  27.3 14.4 %collective-permute-start.4 = (bf16[256,768]{1,0:T(8,128)(2,1)}, bf16[256,768]{1,0:T(8,128)(2,1)S(1)}, u32[]{:S(2)}, u32[]{:S(2)}) collective-permute-start(bf16[256,768]{1,0:T(8,128)(2,1)} %bitcast.155), channel_id=1, source_target_pairs={{0,1},{1,0},{2,3},{3,2},{4,5},{5,4},{6,7},{7,6},{8,9},{9,8},{10,11... | collective-permute-start | bytes 1179656 | tf_op jit(solution)/shard_map/ppermute | solution.py:46
  41.7 18.0 %collective-permute-start.5 = (bf16[4,80,768]{2,1,0:T(8,128)(2,1)S(1)}, bf16[4,80,768]{2,1,0:T(8,128)(2,1)S(1)}, u32[]{:S(2)}, u32[]{:S(2)}) collective-permute-start(bf16[4,80,768]{2,1,0:T(8,128)(2,1)S(1)} %pad_maximum_fusion.4), channel_id=1, source_target_pairs={{0,1},{1,0},{2,3},{3,2},{4,5},{5,4},{6,7},{7,6},{8,9},{9,8},{10,11... | collective-permute-start | bytes 1474568 | tf_op jit(solution)/shard_map/ppermute | solution.py:46
  43.1 16.7 %collective-permute-start.8 = (bf16[256,768]{1,0:T(8,128)(2,1)S(1)}, bf16[256,768]{1,0:T(8,128)(2,1)S(1)}, u32[]{:S(2)}, u32[]{:S(2)}) collective-permute-start(bf16[256,768]{1,0:T(8,128)(2,1)S(1)} %bitcast.161), channel_id=1, source_target_pairs={{5,6},{6,5},{13,14},{14,13},{21,22},{22,21},{29,30},{30,29}} | collective-permute-start | bytes 1179656 | tf_op jit(solution)/shard_map/ppermute | solution.py:50
  43.8 30.4 %collective-permute-start.6 = (bf16[256,768]{1,0:T(8,128)(2,1)S(1)}, bf16[256,768]{1,0:T(8,128)(2,1)S(1)}, u32[]{:S(2)}, u32[]{:S(2)}) collective-permute-start(bf16[256,768]{1,0:T(8,128)(2,1)S(1)} %broadcast_select_fusion.refs_0_), channel_id=1, source_target_pairs={{0,2},{1,3},{2,0},{3,1},{4,6},{5,7},{6,4},{7,5},{8,10},{9,11},{10,... | collective-permute-start | bytes 1179656 | tf_op jit(solution)/shard_map/ppermute | solution.py:46
  59.3 15.6 %collective-permute-start.7 = (bf16[256,768]{1,0:T(8,128)(2,1)S(1)}, bf16[256,768]{1,0:T(8,128)(2,1)S(1)}, u32[]{:S(2)}, u32[]{:S(2)}) collective-permute-start(bf16[256,768]{1,0:T(8,128)(2,1)S(1)} %broadcast_select_fusion.refs_0_), channel_id=1, source_target_pairs={{0,1},{1,0},{2,3},{3,2},{4,5},{5,4},{6,7},{7,6},{8,9},{9,8},{10,11... | collective-permute-start | bytes 1179656 | tf_op jit(solution)/shard_map/ppermute | solution.py:46
  75.7 42.1 %collective-permute-start.10 = (bf16[8,80,768]{2,1,0:T(8,128)(2,1)S(1)}, bf16[8,80,768]{2,1,0:T(8,128)(2,1)S(1)}, u32[]{:S(2)}, u32[]{:S(2)}) collective-permute-start(bf16[8,80,768]{2,1,0:T(8,128)(2,1)S(1)} %pad_maximum_fusion.2), channel_id=1, source_target_pairs={{0,16},{1,17},{2,18},{3,19},{4,20},{5,21},{6,22},{7,23},{8,24},{9,... | collective-permute-start | bytes 2949128 | tf_op jit(solution)/shard_map/ppermute | solution.py:46
  121.9 18.0 %collective-permute-start.9 = (bf16[256,768]{1,0:T(8,128)(2,1)}, bf16[256,768]{1,0:T(8,128)(2,1)S(1)}, u32[]{:S(2)}, u32[]{:S(2)}) collective-permute-start(bf16[256,768]{1,0:T(8,128)(2,1)} %copy-done.30), channel_id=1, source_target_pairs={{0,1},{1,0},{2,3},{3,2},{4,5},{5,4},{6,7},{7,6},{8,9},{9,8},{10,11... | collective-permute-start | bytes 1179656 | tf_op jit(solution)/shard_map/ppermute | solution.py:46
  182.7 25.3 %collective-permute-start.13 = (bf16[4,2,1,2,2,2,24,768]{7,6,5,4,3,2,1,0:T(8,128)(2,1)}, bf16[4,2,1,2,2,2,24,768]{7,6,5,4,3,2,1,0:T(8,128)(2,1)}, u32[]{:S(2)}, u32[]{:S(2)}) collective-permute-start(bf16[4,2,1,2,2,2,24,768]{7,6,5,4,3,2,1,0:T(8,128)(2,1)} %constant_dynamic-slice_fusion.19), channel_id=1, source_target_pairs={{0,8},{1,9},{2,10},{3,11},{4,12},{5,13},{6,14},{7,15},{8,0},{9,1},... | collective-permute-start | bytes 7077896 | tf_op jit(solution)/shard_map/ppermute | solution.py:46
  187.0 25.6 %collective-permute-start.12 = (bf16[2,1,2,2,2,96,768]{6,5,3,2,4,0,1:T(8,128)(2,1)}, bf16[2,1,2,2,2,96,768]{6,5,3,2,4,0,1:T(8,128)(2,1)}, u32[]{:S(2)}, u32[]{:S(2)}) collective-permute-start(bf16[2,1,2,2,2,96,768]{6,5,3,2,4,0,1:T(8,128)(2,1)} %copy.104), channel_id=1, source_target_pairs={{0,8},{1,9},{2,10},{3,11},{4,12},{5,13},{6,14},{7,15},{8,0},{9,1},... | collective-permute-start | bytes 7077896 | tf_op jit(solution)/shard_map/ppermute | solution.py:46
  189.7 16.2 %collective-permute-start.14 = (bf16[2,1,2,2,2,24,768]{6,5,3,2,4,0,1:T(8,128)(2,1)}, bf16[2,1,2,2,2,24,768]{6,5,3,2,4,0,1:T(8,128)(2,1)S(1)}, u32[]{:S(2)}, u32[]{:S(2)}) collective-permute-start(bf16[2,1,2,2,2,24,768]{6,5,3,2,4,0,1:T(8,128)(2,1)} %copy.106), channel_id=1, source_target_pairs={{0,8},{1,9},{2,10},{3,11},{4,12},{5,13},{6,14},{7,15},{8,0},{9,1},... | collective-permute-start | bytes 1769480 | tf_op jit(solution)/shard_map/ppermute | solution.py:46
  234.4 35.0 %collective-permute-start.15 = (bf16[1,2,2,2,96,768]{5,4,2,1,3,0:T(8,128)(2,1)}, bf16[1,2,2,2,96,768]{5,4,2,1,3,0:T(8,128)(2,1)}, u32[]{:S(2)}, u32[]{:S(2)}) collective-permute-start(bf16[1,2,2,2,96,768]{5,4,2,1,3,0:T(8,128)(2,1)} %constant_dynamic-slice_fusion.16), channel_id=1, source_target_pairs={{0,16},{1,17},{2,18},{3,19},{4,20},{5,21},{6,22},{7,23},{8,24},{9,... | collective-permute-start | bytes 3538952 | tf_op jit(solution)/shard_map/ppermute | solution.py:46
  235.5 33.9 %collective-permute-start.17 = (bf16[1,2,2,2,24,768]{5,4,2,1,3,0:T(8,128)(2,1)S(1)}, bf16[1,2,2,2,24,768]{5,4,2,1,3,0:T(8,128)(2,1)S(1)}, u32[]{:S(2)}, u32[]{:S(2)}) collective-permute-start(bf16[1,2,2,2,24,768]{5,4,2,1,3,0:T(8,128)(2,1)S(1)} %constant_dynamic-slice_fusion.14), channel_id=1, source_target_pairs={{0,16},{1,17},{2,18},{3,19},{4,20},{5,21},{6,22},{7,23},{8,24},{9,... | collective-permute-start | bytes 884744 | tf_op jit(solution)/shard_map/ppermute | solution.py:46
  237.7 33.7 %collective-permute-start.16 = (bf16[4,2,2,2,1,24,768]{6,5,4,3,2,1,0:T(8,128)(2,1)}, bf16[4,2,2,2,1,24,768]{6,5,4,3,2,1,0:T(8,128)(2,1)}, u32[]{:S(2)}, u32[]{:S(2)}) collective-permute-start(bf16[4,2,2,2,1,24,768]{6,5,4,3,2,1,0:T(8,128)(2,1)} %constant_dynamic-slice_fusion.15), channel_id=1, source_target_pairs={{0,1},{1,0},{2,3},{3,2},{4,5},{5,4},{6,7},{7,6},{8,9},{9,8},{10,11... | collective-permute-start | bytes 3538952 | tf_op jit(solution)/shard_map/ppermute | solution.py:46
  274.1 32.7 %collective-permute-start.22 = (bf16[256,768]{1,0:T(8,128)(2,1)}, bf16[256,768]{1,0:T(8,128)(2,1)}, u32[]{:S(2)}, u32[]{:S(2)}) collective-permute-start(bf16[256,768]{1,0:T(8,128)(2,1)} %get-tuple-element.141), channel_id=1, source_target_pairs={{0,1},{1,0},{2,3},{3,2},{4,5},{5,4},{6,7},{7,6},{8,9},{9,8},{10,11... | collective-permute-start | bytes 1179656 | tf_op jit(solution)/shard_map/ppermute | solution.py:46
  274.9 38.3 %collective-permute-start.21 = (bf16[256,768]{1,0:T(8,128)(2,1)}, bf16[256,768]{1,0:T(8,128)(2,1)}, u32[]{:S(2)}, u32[]{:S(2)}) collective-permute-start(bf16[256,768]{1,0:T(8,128)(2,1)} %get-tuple-element.140), channel_id=1, source_target_pairs={{0,1},{1,0},{2,3},{3,2},{4,5},{5,4},{6,7},{7,6},{8,9},{9,8},{10,11... | collective-permute-start | bytes 1179656 | tf_op jit(solution)/shard_map/ppermute | solution.py:46
  276.2 30.6 %collective-permute-start.20 = (bf16[2,2,1,24,768]{4,3,1,0,2:T(8,128)(2,1)S(1)}, bf16[2,2,1,24,768]{4,3,1,0,2:T(8,128)(2,1)S(1)}, u32[]{:S(2)}, u32[]{:S(2)}) collective-permute-start(bf16[2,2,1,24,768]{4,3,1,0,2:T(8,128)(2,1)S(1)} %constant_dynamic-slice_fusion.11), channel_id=1, source_target_pairs={{0,1},{1,0},{2,3},{3,2},{4,5},{5,4},{6,7},{7,6},{8,9},{9,8},{10,11... | collective-permute-start | bytes 442376 | tf_op jit(solution)/shard_map/ppermute | solution.py:46
  277.9 32.9 %collective-permute-start.19 = (bf16[4,1,2,2,24,768]{5,4,3,2,1,0:T(8,128)(2,1)}, bf16[4,1,2,2,24,768]{5,4,3,2,1,0:T(8,128)(2,1)}, u32[]{:S(2)}, u32[]{:S(2)}) collective-permute-start(bf16[4,1,2,2,24,768]{5,4,3,2,1,0:T(8,128)(2,1)} %constant_dynamic-slice_fusion.12), channel_id=1, source_target_pairs={{0,16},{1,17},{2,18},{3,19},{4,20},{5,21},{6,22},{7,23},{8,24},{9,... | collective-permute-start | bytes 1769480 | tf_op jit(solution)/shard_map/ppermute | solution.py:46
  280.0 32.0 %collective-permute-start.18 = (bf16[2,2,1,96,768]{4,3,1,0,2:T(8,128)(2,1)}, bf16[2,2,1,96,768]{4,3,1,0,2:T(8,128)(2,1)}, u32[]{:S(2)}, u32[]{:S(2)}) collective-permute-start(bf16[2,2,1,96,768]{4,3,1,0,2:T(8,128)(2,1)} %constant_dynamic-slice_fusion.13), channel_id=1, source_target_pairs={{0,1},{1,0},{2,3},{3,2},{4,5},{5,4},{6,7},{7,6},{8,9},{9,8},{10,11... | collective-permute-start | bytes 1769480 | tf_op jit(solution)/shard_map/ppermute | solution.py:46
  308.0 10.3 %collective-permute-start.23 = (bf16[256,768]{1,0:T(8,128)(2,1)S(1)}, bf16[256,768]{1,0:T(8,128)(2,1)S(1)}, u32[]{:S(2)}, u32[]{:S(2)}) collective-permute-start(bf16[256,768]{1,0:T(8,128)(2,1)S(1)} %fusion.12), channel_id=1, source_target_pairs={{0,2},{1,3},{2,0},{3,1},{4,6},{5,7},{6,4},{7,5},{8,10},{9,11},{10,... | collective-permute-start | bytes 1179656 | tf_op jit(solution)/shard_map/ppermute | solution.py:46
  319.6 58.5 %collective-permute-start.45 = (bf16[1,1,96,768]{3,2,1,0:T(8,128)(2,1)S(1)}, bf16[1,1,96,768]{3,2,1,0:T(8,128)(2,1)S(1)}, u32[]{:S(2)}, u32[]{:S(2)}) collective-permute-start(bf16[1,1,96,768]{3,2,1,0:T(8,128)(2,1)S(1)} %get-tuple-element.146), channel_id=1, source_target_pairs={{0,2},{1,3},{2,0},{3,1},{4,6},{5,7},{6,4},{7,5},{8,10},{9,11},{10,... | collective-permute-start | bytes 442376 | tf_op jit(solution)/shard_map/ppermute | solution.py:46
  321.4 33.3 %collective-permute-start.39 = (bf16[1,1,24,768]{3,2,1,0:T(8,128)(2,1)S(1)}, bf16[1,1,24,768]{3,2,1,0:T(8,128)(2,1)S(1)}, u32[]{:S(2)}, u32[]{:S(2)}) collective-permute-start(bf16[1,1,24,768]{3,2,1,0:T(8,128)(2,1)S(1)} %get-tuple-element.158), channel_id=1, source_target_pairs={{0,2},{1,3},{2,0},{3,1},{4,6},{5,7},{6,4},{7,5},{8,10},{9,11},{10,... | collective-permute-start | bytes 110600 | tf_op jit(solution)/shard_map/ppermute | solution.py:46
  321.7 33.6 %collective-permute-start.40 = (bf16[1,1,24,768]{3,2,1,0:T(8,128)(2,1)S(1)}, bf16[1,1,24,768]{3,2,1,0:T(8,128)(2,1)S(1)}, u32[]{:S(2)}, u32[]{:S(2)}) collective-permute-start(bf16[1,1,24,768]{3,2,1,0:T(8,128)(2,1)S(1)} %get-tuple-element.160), channel_id=1, source_target_pairs={{0,4},{1,5},{2,6},{3,7},{4,0},{5,1},{6,2},{7,3},{8,12},{9,13},{10,... | collective-permute-start | bytes 110600 | tf_op jit(solution)/shard_map/ppermute | solution.py:46
  351.0 6.9 %collective-permute-start.41 = (bf16[1,1,24,768]{3,2,1,0:T(8,128)(2,1)S(1)}, bf16[1,1,24,768]{3,2,1,0:T(8,128)(2,1)S(1)}, u32[]{:S(2)}, u32[]{:S(2)}) collective-permute-start(bf16[1,1,24,768]{3,2,1,0:T(8,128)(2,1)S(1)} %get-tuple-element.159), channel_id=1, source_target_pairs={{0,6},{1,7},{2,4},{3,5},{4,2},{5,3},{6,0},{7,1},{8,14},{9,15},{10,... | collective-permute-start | bytes 110600 | tf_op jit(solution)/shard_map/ppermute | solution.py:46
  352.4 7.4 %collective-permute-start.27 = (bf16[2,1,2,2,2,32,768]{6,5,3,2,4,1,0:T(8,128)(2,1)S(1)}, bf16[2,1,2,2,2,32,768]{6,5,3,2,4,1,0:T(8,128)(2,1)S(1)}, u32[]{:S(2)}, u32[]{:S(2)}) collective-permute-start(bf16[2,1,2,2,2,32,768]{6,5,3,2,4,1,0:T(8,128)(2,1)S(1)} %copy.108), channel_id=1, source_target_pairs={{0,8},{1,9},{2,10},{3,11},{4,12},{5,13},{6,14},{7,15},{8,0},{9,1},... | collective-permute-start | bytes 2359304 | tf_op jit(solution)/shard_map/ppermute | solution.py:46
  354.7 7.0 %collective-permute-start.42 = (bf16[4,1,1,24,768]{4,3,2,1,0:T(8,128)(2,1)S(1)}, bf16[4,1,1,24,768]{4,3,2,1,0:T(8,128)(2,1)S(1)}, u32[]{:S(2)}, u32[]{:S(2)}) collective-permute-start(bf16[4,1,1,24,768]{4,3,2,1,0:T(8,128)(2,1)S(1)} %get-tuple-element.149), channel_id=1, source_target_pairs={{0,2},{1,3},{2,0},{3,1},{4,6},{5,7},{6,4},{7,5},{8,10},{9,11},{10,... | collective-permute-start | bytes 442376 | tf_op jit(solution)/shard_map/ppermute | solution.py:46
  355.3 18.2 %collective-permute-start.43 = (bf16[4,1,1,24,768]{4,3,2,1,0:T(8,128)(2,1)S(1)}, bf16[4,1,1,24,768]{4,3,2,1,0:T(8,128)(2,1)S(1)}, u32[]{:S(2)}, u32[]{:S(2)}) collective-permute-start(bf16[4,1,1,24,768]{4,3,2,1,0:T(8,128)(2,1)S(1)} %get-tuple-element.151), channel_id=1, source_target_pairs={{0,4},{1,5},{2,6},{3,7},{4,0},{5,1},{6,2},{7,3},{8,12},{9,13},{10,... | collective-permute-start | bytes 442376 | tf_op jit(solution)/shard_map/ppermute | solution.py:46
  358.0 18.1 %collective-permute-start.44 = (bf16[4,1,1,24,768]{4,3,2,1,0:T(8,128)(2,1)S(1)}, bf16[4,1,1,24,768]{4,3,2,1,0:T(8,128)(2,1)S(1)}, u32[]{:S(2)}, u32[]{:S(2)}) collective-permute-start(bf16[4,1,1,24,768]{4,3,2,1,0:T(8,128)(2,1)S(1)} %get-tuple-element.150), channel_id=1, source_target_pairs={{0,6},{1,7},{2,4},{3,5},{4,2},{5,3},{6,0},{7,1},{8,14},{9,15},{10,... | collective-permute-start | bytes 442376 | tf_op jit(solution)/shard_map/ppermute | solution.py:46
  359.8 25.7 %collective-permute-start.33 = (bf16[2,1,2,2,2,24,1536]{6,5,3,2,0,4,1:T(8,128)(2,1)S(1)}, bf16[2,1,2,2,2,24,1536]{6,5,3,2,0,4,1:T(8,128)(2,1)S(1)}, u32[]{:S(2)}, u32[]{:S(2)}) collective-permute-start(bf16[2,1,2,2,2,24,1536]{6,5,3,2,0,4,1:T(8,128)(2,1)S(1)} %copy.110), channel_id=1, source_target_pairs={{0,8},{1,9},{2,10},{3,11},{4,12},{5,13},{6,14},{7,15},{8,0},{9,1},... | collective-permute-start | bytes 3538952 | tf_op jit(solution)/shard_map/ppermute | solution.py:46
  361.7 19.5 %collective-permute-start.46 = (bf16[1,1,96,768]{3,2,1,0:T(8,128)(2,1)S(1)}, bf16[1,1,96,768]{3,2,1,0:T(8,128)(2,1)S(1)}, u32[]{:S(2)}, u32[]{:S(2)}) collective-permute-start(bf16[1,1,96,768]{3,2,1,0:T(8,128)(2,1)S(1)} %get-tuple-element.148), channel_id=1, source_target_pairs={{0,4},{1,5},{2,6},{3,7},{4,0},{5,1},{6,2},{7,3},{8,12},{9,13},{10,... | collective-permute-start | bytes 442376 | tf_op jit(solution)/shard_map/ppermute | solution.py:46
  373.5 8.4 %collective-permute-start.47 = (bf16[1,1,96,768]{3,2,1,0:T(8,128)(2,1)S(1)}, bf16[1,1,96,768]{3,2,1,0:T(8,128)(2,1)S(1)}, u32[]{:S(2)}, u32[]{:S(2)}) collective-permute-start(bf16[1,1,96,768]{3,2,1,0:T(8,128)(2,1)S(1)} %get-tuple-element.147), channel_id=1, source_target_pairs={{0,6},{1,7},{2,4},{3,5},{4,2},{5,3},{6,0},{7,1},{8,14},{9,15},{10,... | collective-permute-start | bytes 442376 | tf_op jit(solution)/shard_map/ppermute | solution.py:46
  376.1 7.9 %collective-permute-start.28 = (bf16[1,2,2,2,32,768]{5,4,2,1,3,0:T(8,128)(2,1)S(1)}, bf16[1,2,2,2,32,768]{5,4,2,1,3,0:T(8,128)(2,1)S(1)}, u32[]{:S(2)}, u32[]{:S(2)}) collective-permute-start(bf16[1,2,2,2,32,768]{5,4,2,1,3,0:T(8,128)(2,1)S(1)} %dynamic-slice_bitcast_fusion.1), channel_id=1, source_target_pairs={{0,16},{1,17},{2,18},{3,19},{4,20},{5,21},{6,22},{7,23},{8,24},{9,... | collective-permute-start | bytes 1179656 | tf_op jit(solution)/shard_map/ppermute | solution.py:46
  378.0 16.3 %collective-permute-start.25 = (bf16[256,768]{1,0:T(8,128)(2,1)S(1)}, bf16[256,768]{1,0:T(8,128)(2,1)S(1)}, u32[]{:S(2)}, u32[]{:S(2)}) collective-permute-start(bf16[256,768]{1,0:T(8,128)(2,1)S(1)} %get-tuple-element.142), channel_id=1, source_target_pairs={{0,1},{1,0},{2,3},{3,2},{4,5},{5,4},{6,7},{7,6},{8,9},{9,8},{10,11... | collective-permute-start | bytes 1179656 | tf_op jit(solution)/shard_map/ppermute | solution.py:46
  381.2 21.2 %collective-permute-start.26 = (bf16[256,768]{1,0:T(8,128)(2,1)S(1)}, bf16[256,768]{1,0:T(8,128)(2,1)S(1)}, u32[]{:S(2)}, u32[]{:S(2)}) collective-permute-start(bf16[256,768]{1,0:T(8,128)(2,1)S(1)} %get-tuple-element.143), channel_id=1, source_target_pairs={{5,6},{6,5},{13,14},{14,13},{21,22},{22,21},{29,30},{30,29}} | collective-permute-start | bytes 1179656 | tf_op jit(solution)/shard_map/ppermute | solution.py:50
  381.9 22.3 %collective-permute-start.24 = (bf16[256,768]{1,0:T(8,128)(2,1)S(1)}, bf16[256,768]{1,0:T(8,128)(2,1)S(1)}, u32[]{:S(2)}, u32[]{:S(2)}) collective-permute-start(bf16[256,768]{1,0:T(8,128)(2,1)S(1)} %convert_element_type.371), channel_id=1, source_target_pairs={{4,0},{5,1},{6,2},{7,3},{12,8},{13,9},{14,10},{15,11},{20,16},{21,... | collective-permute-start | bytes 1179656 | tf_op jit(solution)/shard_map/ppermute | solution.py:50
  384.1 10.0 %collective-permute-start.29 = (bf16[2,2,1,32,768]{4,3,2,1,0:T(8,128)(2,1)S(1)}, bf16[2,2,1,32,768]{4,3,2,1,0:T(8,128)(2,1)S(1)}, u32[]{:S(2)}, u32[]{:S(2)}) collective-permute-start(bf16[2,2,1,32,768]{4,3,2,1,0:T(8,128)(2,1)S(1)} %dynamic-slice_bitcast_fusion.3), channel_id=1, source_target_pairs={{0,1},{1,0},{2,3},{3,2},{4,5},{5,4},{6,7},{7,6},{8,9},{9,8},{10,11... | collective-permute-start | bytes 589832 | tf_op jit(solution)/shard_map/ppermute | solution.py:46
  385.9 22.3 %collective-permute-start.34 = (bf16[2,2,2,1,24,1536]{5,4,2,1,3,0:T(8,128)(2,1)S(1)}, bf16[2,2,2,1,24,1536]{5,4,2,1,3,0:T(8,128)(2,1)S(1)}, u32[]{:S(2)}, u32[]{:S(2)}) collective-permute-start(bf16[2,2,2,1,24,1536]{5,4,2,1,3,0:T(8,128)(2,1)S(1)} %dynamic-slice_bitcast_fusion), channel_id=1, source_target_pairs={{0,1},{1,0},{2,3},{3,2},{4,5},{5,4},{6,7},{7,6},{8,9},{9,8},{10,11... | collective-permute-start | bytes 1769480 | tf_op jit(solution)/shard_map/ppermute | solution.py:46
  394.2 11.0 %collective-permute-start.30 = (bf16[1,1,32,768]{3,2,1,0:T(8,128)(2,1)S(1)}, bf16[1,1,32,768]{3,2,1,0:T(8,128)(2,1)S(1)}, u32[]{:S(2)}, u32[]{:S(2)}) collective-permute-start(bf16[1,1,32,768]{3,2,1,0:T(8,128)(2,1)S(1)} %get-tuple-element.155), channel_id=1, source_target_pairs={{0,2},{1,3},{2,0},{3,1},{4,6},{5,7},{6,4},{7,5},{8,10},{9,11},{10,... | collective-permute-start | bytes 147464 | tf_op jit(solution)/shard_map/ppermute | solution.py:46
  394.3 10.9 %collective-permute-start.31 = (bf16[1,1,32,768]{3,2,1,0:T(8,128)(2,1)S(1)}, bf16[1,1,32,768]{3,2,1,0:T(8,128)(2,1)S(1)}, u32[]{:S(2)}, u32[]{:S(2)}) collective-permute-start(bf16[1,1,32,768]{3,2,1,0:T(8,128)(2,1)S(1)} %get-tuple-element.157), channel_id=1, source_target_pairs={{0,4},{1,5},{2,6},{3,7},{4,0},{5,1},{6,2},{7,3},{8,12},{9,13},{10,... | collective-permute-start | bytes 147464 | tf_op jit(solution)/shard_map/ppermute | solution.py:46
  402.3 5.9 %collective-permute-start.32 = (bf16[1,1,32,768]{3,2,1,0:T(8,128)(2,1)S(1)}, bf16[1,1,32,768]{3,2,1,0:T(8,128)(2,1)S(1)}, u32[]{:S(2)}, u32[]{:S(2)}) collective-permute-start(bf16[1,1,32,768]{3,2,1,0:T(8,128)(2,1)S(1)} %get-tuple-element.156), channel_id=1, source_target_pairs={{0,6},{1,7},{2,4},{3,5},{4,2},{5,3},{6,0},{7,1},{8,14},{9,15},{10,... | collective-permute-start | bytes 147464 | tf_op jit(solution)/shard_map/ppermute | solution.py:46
  408.5 6.8 %collective-permute-start.35 = (bf16[1,2,2,24,1536]{4,3,2,1,0:T(8,128)(2,1)S(1)}, bf16[1,2,2,24,1536]{4,3,2,1,0:T(8,128)(2,1)S(1)}, u32[]{:S(2)}, u32[]{:S(2)}) collective-permute-start(bf16[1,2,2,24,1536]{4,3,2,1,0:T(8,128)(2,1)S(1)} %dynamic-slice_bitcast_fusion.2), channel_id=1, source_target_pairs={{0,16},{1,17},{2,18},{3,19},{4,20},{5,21},{6,22},{7,23},{8,24},{9,... | collective-permute-start | bytes 884744 | tf_op jit(solution)/shard_map/ppermute | solution.py:46
  415.4 5.6 %collective-permute-start.36 = (bf16[1,1,24,1536]{3,2,1,0:T(8,128)(2,1)S(1)}, bf16[1,1,24,1536]{3,2,1,0:T(8,128)(2,1)S(1)}, u32[]{:S(2)}, u32[]{:S(2)}) collective-permute-start(bf16[1,1,24,1536]{3,2,1,0:T(8,128)(2,1)S(1)} %get-tuple-element.152), channel_id=1, source_target_pairs={{0,2},{1,3},{2,0},{3,1},{4,6},{5,7},{6,4},{7,5},{8,10},{9,11},{10,... | collective-permute-start | bytes 221192 | tf_op jit(solution)/shard_map/ppermute | solution.py:46
  415.5 8.6 %collective-permute-start.37 = (bf16[1,1,24,1536]{3,2,1,0:T(8,128)(2,1)S(1)}, bf16[1,1,24,1536]{3,2,1,0:T(8,128)(2,1)S(1)}, u32[]{:S(2)}, u32[]{:S(2)}) collective-permute-start(bf16[1,1,24,1536]{3,2,1,0:T(8,128)(2,1)S(1)} %get-tuple-element.154), channel_id=1, source_target_pairs={{0,4},{1,5},{2,6},{3,7},{4,0},{5,1},{6,2},{7,3},{8,12},{9,13},{10,... | collective-permute-start | bytes 221192 | tf_op jit(solution)/shard_map/ppermute | solution.py:46
  420.4 6.2 %collective-permute-start.38 = (bf16[1,1,24,1536]{3,2,1,0:T(8,128)(2,1)S(1)}, bf16[1,1,24,1536]{3,2,1,0:T(8,128)(2,1)S(1)}, u32[]{:S(2)}, u32[]{:S(2)}) collective-permute-start(bf16[1,1,24,1536]{3,2,1,0:T(8,128)(2,1)S(1)} %get-tuple-element.153), channel_id=1, source_target_pairs={{0,6},{1,7},{2,4},{3,5},{4,2},{5,3},{6,0},{7,1},{8,14},{9,15},{10,... | collective-permute-start | bytes 221192 | tf_op jit(solution)/shard_map/ppermute | solution.py:46
  (35 other events, 569.8 us)
Sparse Core Ops, SparseCore 0:
  11.5 116.0 all-gather.1

commit v5 on v4

--- a/solution.py
+++ b/solution.py
@@ -20,6 +20,8 @@
 SQRT_HALF = 0.7071067811865476
 INV_ROOT_TAU = 0.3989422804014327
 AXES = ("grp", "row")
+WIDE = 4
+WO, WI, WQ, WK, WV = 4, 5, 9, 10, 11
 
 
 def mm(left, right):
@@ -53,56 +55,30 @@
         return lax.axis_index("grp") * self.row + lax.axis_index("row")
 
 
-def combos(stage):
-    masks = [0]
-    for bit in stage:
-        masks = masks + [m ^ bit for m in masks]
-    return masks
-
-
-class Gather:
-    def __init__(self, plan, value):
-        self.plan, self.held, self.masks = plan, value[None], [0]
-
-    def stage(self, bits):
-        masks = combos(bits)
-        self.held = jnp.concatenate(
-            [self.held] + [self.plan.swap(self.held, m) for m in masks[1:]], 0
-        )
-        self.masks = [m ^ k for k in masks for m in self.masks]
-
-    def ordered(self):
-        slot = np.zeros(self.plan.count, np.int32)
-        for j, m in enumerate(self.masks):
-            slot[m] = j
-        places = jnp.asarray(slot)[self.plan.me() ^ jnp.arange(self.plan.count)]
-        return jnp.take(self.held, places, axis=0, mode="clip")
-
-
 class Reduce:
-    def __init__(self, plan, value, before=0):
-        self.plan, self.before = plan, before
-        self.lead, self.rest = list(value.shape[:before]), list(value.shape[before + 1 :])
-        self.left = [1 << i for i in reversed(range(plan.bits))]
-        self.value = value.astype(BF).reshape(self.lead + [2] * plan.bits + self.rest)
-
-    def stage(self, bits):
-        me, value = self.plan.me(), self.value
-
-        def part(mask):
-            array = value
-            for bit in bits:
-                place = ((me ^ mask) // bit) & 1
-                axis = self.before + self.left.index(bit)
-                array = lax.dynamic_slice_in_dim(array, place, 1, axis)
-            return array
-
-        total = part(0).astype(F32)
-        for mask in combos(bits)[1:]:
-            total = total + self.plan.swap(part(mask), mask).astype(F32)
-        self.left = [b for b in self.left if b not in bits]
-        value = total.reshape(self.lead + [2] * len(self.left) + self.rest)
-        self.value = value.astype(BF) if self.left else value
+    def __init__(self, plan, terms, left=None):
+        self.plan, self.terms = plan, list(terms)
+        self.left = left or [1 << i for i in reversed(range(plan.bits))]
+
+    def cut(self, term, bit, place):
+        at = self.left.index(bit)
+        high, low = 1 << at, 1 << (len(self.left) - at - 1)
+        _, rows, width = term.shape
+        term = term.reshape(high, 2, low * rows, width)
+        return lax.dynamic_slice_in_dim(term, place, 1, 1).reshape(high * low, rows, width)
+
+    def total(self, terms):
+        return sum([t.astype(F32) for t in terms[1:]], terms[0].astype(F32))
+
+    def stage(self, bit):
+        place = (self.plan.me() // bit) & 1
+        away = self.total([self.cut(t, bit, 1 - place) for t in self.terms]).astype(BF)
+        here = [self.cut(t, bit, place) for t in self.terms]
+        self.left = [b for b in self.left if b != bit]
+        self.terms = here + [self.plan.swap(away, bit)]
+
+    def result(self):
+        return self.total(self.terms)[0]
 
 
 def tie(*values):
@@ -231,6 +207,8 @@
      q_ref, kp_ref, vp_ref, kn_ref, vn_ref, ctx_ref, lse_ref, x_ref, s_ref, sems) = refs[blocks:]
     near = near_ref[0]
     at = lambda b: pl.ds(pl.multiple_of(b * rows, rows), rows)
+    depth = own_ref.shape[1]
+    wq, wk, wv = [ref[...].reshape(depth, -1) for ref in (wq_ref, wk_ref, wv_ref)]
 
     @pl.when(pl.program_id(0) == 0)
     def _():
@@ -243,13 +221,13 @@
         for copy in copies:
             copy.wait()
 
-    queries = (mm(own_ref[...], wq_ref[...]) + bq_ref[...]) * (HDIM**-0.5)
+    queries = (mm(own_ref[...], wq) + bq_ref[...]) * (HDIM**-0.5)
     q_ref[...] = queries.astype(BF)
 
     def project(b, k_ref, v_ref, side):
         x = x_ref[at(b), :]
-        k_ref[at(side), :] = mm(x, wk_ref[...]).astype(BF)
-        v_ref[at(side), :] = (mm(x, wv_ref[...]) + bv_ref[...]).astype(BF)
+        k_ref[at(side), :] = mm(x, wk).astype(BF)
+        v_ref[at(side), :] = (mm(x, wv) + bv_ref[...]).astype(BF)
 
     @pl.loop(0, first)
     def _(b):
@@ -301,7 +279,7 @@
         lse_ref[0, h : h + 1, :] = peaks[h] + jnp.log(totals[h])
 
 
-def attention_call(spots, first, near, own, wq, wk, wv, bq, bv, segq, segk):
+def attention_call(spots, first, near, own, got, bq, bv, segq, segk):
     rows, width = own.shape
     blocks = len(spots)
     tall = blocks * rows
@@ -310,6 +288,8 @@
     heads = part // HDIM
     cols = lambda depth: pl.BlockSpec((depth, part), lambda g: (0, g))
     flops = 2 * tall * width * width * 2 + 4 * tall * rows * width * 4
+    owners, each = got.shape[0], width // got.shape[0]
+    weight = lambda place: pl.BlockSpec((owners, each, part), lambda g: (0, place, g))
     return pl.pallas_call(
         functools.partial(attention_kernel, blocks, first, rows),
         grid=(steps,),
@@ -317,7 +297,7 @@
         + [
             pl.BlockSpec(memory_space=pltpu.SMEM),
             pl.BlockSpec((rows, width), lambda g: (0, 0)),
-            cols(width), cols(width), cols(width), cols(1), cols(1),
+            weight(WQ), weight(WK), weight(WV), cols(1), cols(1),
             pl.BlockSpec((1, rows), lambda g: (0, 0)),
             pl.BlockSpec(segk.shape, lambda g: (0, 0)),
         ],
@@ -344,19 +324,51 @@
             flops=flops, bytes_accessed=12 * 2**20, transcendentals=tall * rows * 12
         ),
         name="attention",
-    )(*spots, near, own, wq, wk, wv, bq, bv, segq, segk)
-
-
-def middle_kernel(wide, ctx_ref, own_ref, cot_ref, wo_ref, wi_ref, wu_ref, vec_ref, bin_ref,
-                  out_ref, h1_ref, gctx_ref, dwo_ref, dwi_ref, dwu_ref, sums_ref, sbin_ref,
+    )(*spots, near, own, got, got, got, bq, bv, segq, segk)
+
+
+def halves(value, runs, core):
+    depth = value.shape[0] // runs
+    pick = lambda first: jnp.concatenate(
+        [value[i * depth : (i + 1) * depth] for i in range(first, runs, 2)], 0
+    )
+    even, odd = pick(0), pick(1)
+    return jnp.where(core == 0, odd, even), jnp.where(core == 0, even, odd)
+
+
+def middle_kernel(wide, runs, core_ref, ctx_ref, own_ref, cot_ref, wo_ref, wi_ref, wu_ref, vec_ref, bin_ref,
+                  out_ref, h1_ref, gctx_ref, a_send, a_keep, b_send, b_keep, sums_ref, sbin_ref,
                   first_ref, n1_ref, inv_ref, low_ref, pre_ref, cdf_ref, act_ref, acc_ref,
-                  gffn_ref, glow_ref):
+                  gffn_ref, glow_ref, out_buf, wo_buf, sems):
     step = pl.program_id(0)
     width = ctx_ref.shape[1]
     square = lambda ref: ref[...].reshape(width, width)
     vec = lambda i: vec_ref[i : i + 1, :]
     mean = lambda v: jnp.sum(v, axis=-1, keepdims=True) * (1.0 / width)
     down = lambda v: jnp.sum(v, axis=0, keepdims=True)
+    core = core_ref[0]
+    owners = wi_ref.shape[0]
+    each = width // owners
+    run = owners // runs
+
+    def put(source, runs_here, base, top, sem, act):
+        size = source.shape[0] // runs_here
+        for i in range(runs_here):
+            number = base + i
+            place = pl.ds(number // 2 * run, run)
+            rows_here = source.shape[1]
+
+            @pl.when(number % 2 == core)
+            def _():
+                act(pltpu.make_async_copy(
+                    source.at[pl.ds(i * size, size)], a_keep.at[place, pl.ds(top, rows_here)], sem.at[i]
+                ))
+
+            @pl.when(number % 2 != core)
+            def _():
+                act(pltpu.make_async_copy(
+                    source.at[pl.ds(i * size, size)], a_send.at[place, pl.ds(top, rows_here)], sem.at[i]
+                ))
 
     @pl.when(step == 0)
     def _():
@@ -415,8 +427,22 @@
         low = glow_ref[...]
         grad = (nt(low, square(wu_ref)) * slope).astype(BF)
         sbin_ref[pl.ds(at, 1), :] = down(grad.astype(F32))
-        dwu_ref[...] = tn(act_ref[:, chunk], low).astype(BF)
-        dwi_ref[0] = tn(low_ref[...], grad).astype(BF)
+        turn = step % 2
+        chunk_runs = runs // wide
+        outer = lambda which, at, act: put(
+            out_buf.at[which], chunk_runs, at * chunk_runs, 0, sems.at[which], act
+        )
+
+        @pl.when(step >= wide + 2)
+        def _():
+            outer(turn, at + 2, lambda c: c.wait())
+
+        d_outer = tn(act_ref[:, chunk], low).astype(BF)
+        out_buf[turn] = d_outer.reshape(owners // wide, wide * each, width)
+        outer(turn, at, lambda c: c.start())
+        away, here = halves(tn(low_ref[...], grad).astype(BF), runs, core)
+        b_send[...] = away.reshape(owners // 2, each, width)
+        b_keep[...] = here.reshape(owners // 2, each, width)
         gffn_ref[...] += nt(grad, square(wi_ref))
 
     @pl.when(step == 2 * wide - 1)
@@ -430,40 +456,52 @@
         h1_ref[...] = back
         low = back.astype(BF)
         sums_ref[5:6, :] = down(low.astype(F32))
-        sums_ref[6:8, :] = jnp.zeros((2, width), F32)
-        dwo_ref[...] = tn(ctx_ref[...], low).astype(BF)
-        gctx_ref[...] = nt(low, square(wo_ref)).astype(BF)
-
-
-def middle_call(ctx, own, cot, got, vec, b_inner):
+        wo_buf[...] = tn(ctx_ref[...], low).astype(BF).reshape(owners, each, width)
+        put(wo_buf, runs, 0, wide * each, sems.at[2], lambda c: c.start())
+        gctx = nt(low, square(wo_ref)).astype(BF)
+        gctx_ref[...] = gctx
+        sums_ref[6:7, :] = down(gctx.astype(F32))
+        sums_ref[7:8, :] = jnp.zeros((1, width), F32)
+        chunk_runs = runs // wide
+        for at in (1, 0):
+            put(out_buf.at[(2 * wide - 1 - at) % 2], chunk_runs, at * chunk_runs, 0,
+                sems.at[(2 * wide - 1 - at) % 2], lambda c: c.wait())
+        put(wo_buf, runs, 0, wide * each, sems.at[2], lambda c: c.wait())
+
+
+def middle_call(ctx, own, cot, got, vec, b_inner, core, runs):
     rows, width = own.shape
     owners = got.shape[0]
     each = width // owners
-    wide = got.shape[1] // each // 2
+    wide = WIDE
+    half = owners // 2
     whole = lambda shape: pl.BlockSpec(shape, lambda s: (0,) * len(shape))
     at = lambda s: jnp.where(s < wide, s, 2 * wide - 1 - s)
     back = lambda s: jnp.where(s < wide, wide - 1, 2 * wide - 1 - s)
     shape = jax.ShapeDtypeStruct
     return pl.pallas_call(
-        functools.partial(middle_kernel, wide),
+        functools.partial(middle_kernel, wide, runs),
         grid=(2 * wide,),
         in_specs=[
+            pl.BlockSpec(memory_space=pltpu.SMEM),
             whole((rows, width)), whole((rows, width)), whole((rows, width)),
-            pl.BlockSpec((owners, each, width), lambda s: (0, wide, 0)),
-            pl.BlockSpec((owners, each, width), lambda s: (0, wide + 1 + at(s), 0)),
+            pl.BlockSpec((owners, each, width), lambda s: (0, WO, 0)),
+            pl.BlockSpec((owners, each, width), lambda s: (0, WI + at(s), 0)),
             pl.BlockSpec((owners // wide, wide * each, width), lambda s: (at(s), 0, 0)),
             whole((8, width)), whole((8, width)),
         ],
         out_specs=[
-            whole((rows, width)), whole((rows, width)), whole((rows, width)), whole((width, width)),
-            pl.BlockSpec((1, width, width), lambda s: (back(s), 0, 0)),
-            pl.BlockSpec((width, width), lambda s: (back(s), 0)),
+            whole((rows, width)), whole((rows, width)), whole((rows, width)),
+            pl.BlockSpec(memory_space=pl.ANY), pl.BlockSpec(memory_space=pl.ANY),
+            pl.BlockSpec((half, each, width), lambda s: (0, back(s), 0)),
+            pl.BlockSpec((half, each, width), lambda s: (0, back(s), 0)),
             whole((8, width)), whole((8, width)),
         ],
         out_shape=[
             shape((rows, width), BF), shape((rows, width), F32), shape((rows, width), BF),
-            shape((width, width), BF), shape((wide, width, width), BF),
-            shape((wide * width, width), BF), shape((8, width), F32), shape((8, width), F32),
+            shape((half, (wide + 1) * each, width), BF), shape((half, (wide + 1) * each, width), BF),
+            shape((half, wide * each, width), BF), shape((half, wide * each, width), BF),
+            shape((8, width), F32), shape((8, width), F32),
         ],
         scratch_shapes=[
             pltpu.VMEM((rows, width), F32), pltpu.VMEM((rows, width), F32), pltpu.VMEM((rows, 1), F32),
@@ -471,6 +509,8 @@
             pltpu.VMEM((rows, wide * width), F32), pltpu.VMEM((rows, wide * width), BF),
             pltpu.VMEM((rows, width), F32), pltpu.VMEM((rows, width), F32),
             pltpu.VMEM((rows, width), BF),
+            pltpu.VMEM((2, owners // wide, wide * each, width), BF),
+            pltpu.VMEM((owners, each, width), BF), pltpu.SemaphoreType.DMA((3, runs)),
         ],
         compiler_params=pltpu.CompilerParams(vmem_limit_bytes=60 * 2**20),
         cost_estimate=pl.CostEstimate(
@@ -478,12 +518,12 @@
             transcendentals=2 * rows * width * wide,
         ),
         name="middle",
-    )(ctx, own, cot, got, got, got, vec, b_inner)
-
-
-def back_kernel(rows, bound, *refs):
-    (near_ref, gctx_ref, ctx_ref, q_ref, k_ref, v_ref, lse_ref, segq_ref, segk_ref, dq0_ref,
-     dk_ref, dv_ref, dq_ref) = refs
+    )(core, ctx, own, cot, got, got, got, vec, b_inner)
+
+
+def back_kernel(rows, bound, started, *refs):
+    near_ref, gctx_ref, ctx_ref, q_ref, k_ref, v_ref, lse_ref, segq_ref, segk_ref = refs[:9]
+    dk_ref, dv_ref, dq_ref = refs[-3:]
     q, g = q_ref[...], gctx_ref[...]
     part = q.shape[1]
     heads = part // HDIM
@@ -518,52 +558,57 @@
         dv_ref[here, :] = dv.astype(BF)
         return tuple(out)
 
-    dq = tuple(dq0_ref[h * HDIM : (h + 1) * HDIM, :] for h in range(heads))
+    if started:
+        dq = tuple(refs[9][h * HDIM : (h + 1) * HDIM, :] for h in range(heads))
+    else:
+        dq = tuple(jnp.zeros((HDIM, rows), F32) for _ in range(heads))
     dq = lax.fori_loop(0, near_ref[0] if bound is None else bound, one, dq)
     dq_ref[...] = jnp.concatenate(dq, 0)
 
 
-def back_call(start, steps, bound, near, gctx, ctx, q, k, v, lse, segq, segk, dq0):
-    rows = q.shape[0]
+def back_call(start, steps, bound, near, gctx, ctx, q, k, v, lse, segq, segk, dq0=None, into=None):
+    rows, width = q.shape
     tall = k.shape[0]
     part = 256
     cols = lambda depth: pl.BlockSpec((depth, part), lambda g: (0, start + g))
-    mine = lambda depth: pl.BlockSpec((depth, part), lambda g: (0, g))
     whole = lambda shape: pl.BlockSpec(shape, lambda g: (0,) * len(shape))
+    down = pl.BlockSpec((part, rows), lambda g: (start + g, 0))
     shape = jax.ShapeDtypeStruct
+    extra = ([dq0] if dq0 is not None else []) + list(into or [])
+    specs = ([down] if dq0 is not None else []) + [pl.BlockSpec(memory_space=pl.ANY)] * len(into or [])
     return pl.pallas_call(
-        functools.partial(back_kernel, rows, bound),
+        functools.partial(back_kernel, rows, bound, dq0 is not None),
         grid=(steps,),
         in_specs=[
             pl.BlockSpec(memory_space=pltpu.SMEM),
             cols(rows), cols(rows), cols(rows), cols(tall), cols(tall),
             pl.BlockSpec((1, 8, rows), lambda g: (start + g, 0, 0)),
             whole((1, rows)), whole(segk.shape),
-            pl.BlockSpec((part, rows), lambda g: (g, 0)),
-        ],
-        out_specs=[mine(tall), mine(tall), pl.BlockSpec((part, rows), lambda g: (g, 0))],
-        out_shape=[
-            shape((tall, steps * part), BF), shape((tall, steps * part), BF),
-            shape((steps * part, rows), F32),
-        ],
+        ] + specs,
+        out_specs=[cols(tall), cols(tall), down],
+        out_shape=[shape((tall, width), BF), shape((tall, width), BF), shape((width, rows), F32)],
+        input_output_aliases={9 + i: i for i in range(3)} if into else {},
         compiler_params=pltpu.CompilerParams(vmem_limit_bytes=60 * 2**20),
         cost_estimate=pl.CostEstimate(
             flops=2 * 10 * 2 * tall * rows * part * steps * 2,
             bytes_accessed=8 * tall * part * steps, transcendentals=tall * rows * 4 * steps,
         ),
         name="attention_back",
-    )(near, gctx, ctx, q, k, v, lse, segq, segk, dq0)
+    )(near, gctx, ctx, q, k, v, lse, segq, segk, *extra)
 
 
 def product_kernel(rows, bound, near_ref, dk_ref, dv_ref, wk_ref, wv_ref, gx_ref):
     @pl.when((pl.program_id(0) < near_ref[0]) | (bound is not None))
     def _():
-        gx_ref[0] = (nt(dk_ref[...], wk_ref[...]) + nt(dv_ref[...], wv_ref[...])).astype(BF)
-
-
-def product_call(bound, near, dk, dv, wk, wv, rows):
+        width = dk_ref.shape[1]
+        wk, wv = wk_ref[...].reshape(width, width), wv_ref[...].reshape(width, width)
+        gx_ref[0] = (nt(dk_ref[...], wk) + nt(dv_ref[...], wv)).astype(BF)
+
+
+def product_call(bound, near, dk, dv, got, rows):
     tall, width = dk.shape
-    whole = lambda shape: pl.BlockSpec(shape, lambda b: (0,) * len(shape))
+    owners, each = got.shape[0], width // got.shape[0]
+    weight = lambda place: pl.BlockSpec((owners, each, width), lambda b: (0, place, 0))
     return pl.pallas_call(
         functools.partial(product_kernel, rows, bound),
         grid=(tall // rows,),
@@ -571,7 +616,7 @@
             pl.BlockSpec(memory_space=pltpu.SMEM),
             pl.BlockSpec((rows, width), lambda b: (b, 0)),
             pl.BlockSpec((rows, width), lambda b: (b, 0)),
-            whole((width, width)), whole((width, width)),
+            weight(WK), weight(WV),
         ],
         out_specs=pl.BlockSpec((1, rows, width), lambda b: (b, 0, 0)),
         out_shape=jax.ShapeDtypeStruct((tall // rows, rows, width), BF),
@@ -580,13 +625,14 @@
             flops=4 * tall * width * width, bytes_accessed=6 * tall * width, transcendentals=0
         ),
         name="token_product",
-    )(near, dk, dv, wk, wv)
-
-
-def weight_kernel(blocks, first, rows, *refs):
+    )(near, dk, dv, got, got)
+
+
+def weight_kernel(blocks, first, rows, runs, *refs):
     spots = refs[:blocks]
-    (near_ref, own_ref, dq_ref, wq_ref, h1_ref, dkp_ref, dvp_ref, dkn_ref, dvn_ref,
-     dwq_ref, dwkv_ref, gown_ref, sums_ref, x_ref, sems) = refs[blocks:]
+    (near_ref, core_ref, own_ref, dq_ref, wq_ref, h1_ref, dkp_ref, dvp_ref, dkn_ref, dvn_ref,
+     q_send, q_keep, kv_send, kv_keep, gown_ref, sums_ref, x_ref, sems) = refs[blocks:]
+    core = core_ref[0]
     at = lambda b: pl.ds(pl.multiple_of(b * rows, rows), rows)
     step = pl.program_id(0)
 
@@ -605,29 +651,31 @@
     scale = HDIM**-0.5
     dq = dq_ref[...].T.astype(BF)
     part = dq.shape[1]
-    gown_ref[...] += nt(dq, wq_ref[...]) * scale
-    dwq_ref[...] = (tn(own_ref[...], dq) * scale).astype(BF)
+    width = x_ref.shape[1]
+    gown_ref[...] += nt(dq, wq_ref[...].reshape(width, part)) * scale
+    away, here = halves((tn(own_ref[...], dq) * scale).astype(BF), runs, core)
+    q_send[...] = away.reshape(q_send.shape)
+    q_keep[...] = here.reshape(q_send.shape)
     sums_ref[0:1, :] = jnp.sum(dq.astype(F32), axis=0, keepdims=True) * scale
 
     def products(b, carry, dk_ref, dv_ref, base):
         dk, dv, x = dk_ref[at(b), :], dv_ref[at(b), :], x_ref[at(base + b), :]
-        wk, wv, bv = carry
-        bv = bv + jnp.sum(dv.astype(F32), axis=0, keepdims=True)
-        return wk + tn(x, dk), wv + tn(x, dv), bv
-
-    width = x_ref.shape[1]
+        wk, wv = carry
+        return wk + tn(x, dk), wv + tn(x, dv)
+
     zero = jnp.zeros((width, part), F32)
-    carry = (zero, zero, jnp.zeros((1, part), F32))
+    carry = (zero, zero)
     carry = lax.fori_loop(0, first, lambda b, c: products(b, c, dkp_ref, dvp_ref, 0), carry)
     carry = lax.fori_loop(0, near_ref[0], lambda b, c: products(b, c, dkn_ref, dvn_ref, first), carry)
-    wk, wv, bv = carry
-    dwkv_ref[:, :part] = wk.astype(BF)
-    dwkv_ref[:, part:] = wv.astype(BF)
-    sums_ref[1:2, :] = bv
-    sums_ref[2:8, :] = jnp.zeros((6, part), F32)
-
-
-def weight_call(spots, first, near, own, dq, wq, h1, dkp, dvp, dkn, dvn):
+    for i, grad in enumerate(carry):
+        away, here = halves(grad.astype(BF), runs, core)
+        shape = kv_send.shape[:2] + (part,)
+        kv_send[:, :, i * part : (i + 1) * part] = away.reshape(shape)
+        kv_keep[:, :, i * part : (i + 1) * part] = here.reshape(shape)
+    sums_ref[1:8, :] = jnp.zeros((7, part), F32)
+
+
+def weight_call(spots, first, near, own, dq, got, h1, dkp, dvp, dkn, dvn, core, runs):
     rows, width = own.shape
     blocks = len(spots)
     tall = blocks * rows
@@ -636,19 +684,27 @@
     cols = lambda depth, size=part: pl.BlockSpec((depth, size), lambda g: (0, g))
     whole = lambda shape: pl.BlockSpec(shape, lambda g: (0,) * len(shape))
     shape = jax.ShapeDtypeStruct
+    owners, each = got.shape[0], width // got.shape[0]
+    half = owners // 2
+    slab = lambda size: pl.BlockSpec((half, each, size), lambda g: (0, 0, g))
     return pl.pallas_call(
-        functools.partial(weight_kernel, blocks, first, rows),
+        functools.partial(weight_kernel, blocks, first, rows, runs),
         grid=(steps,),
         in_specs=[pl.BlockSpec(memory_space=pl.ANY)] * blocks
         + [
             pl.BlockSpec(memory_space=pltpu.SMEM),
-            whole((rows, width)), pl.BlockSpec((part, rows), lambda g: (g, 0)), cols(width),
+            pl.BlockSpec(memory_space=pltpu.SMEM),
+            whole((rows, width)), pl.BlockSpec((part, rows), lambda g: (g, 0)),
+            pl.BlockSpec((owners, each, part), lambda g: (0, WQ, g)),
             whole((rows, width)), cols(PROMPT), cols(PROMPT), cols(tall - PROMPT), cols(tall - PROMPT),
         ],
-        out_specs=[cols(width), cols(width, 2 * part), whole((rows, width)), cols(8)],
+        out_specs=[
+            slab(part), slab(part), slab(2 * part), slab(2 * part), whole((rows, width)), cols(8),
+        ],
         out_shape=[
-            shape((width, width), BF), shape((width, 2 * width), BF), shape((rows, width), F32),
-            shape((8, width), F32),
+            shape((half, each, width), BF), shape((half, each, width), BF),
+            shape((half, each, 2 * width), BF), shape((half, each, 2 * width), BF),
+            shape((rows, width), F32), shape((8, width), F32),
         ],
         scratch_shapes=[pltpu.VMEM((tall, width), BF), pltpu.SemaphoreType.DMA((blocks,))],
         compiler_params=pltpu.CompilerParams(vmem_limit_bytes=60 * 2**20),
@@ -656,7 +712,17 @@
             flops=4 * tall * width * width, bytes_accessed=12 * tall * width, transcendentals=0
         ),
         name="weight_product",
-    )(*spots, near, own, dq, wq, h1, dkp, dvp, dkn, dvn)
+    )(*spots, near, core, own, dq, got, h1, dkp, dvp, dkn, dvn)
+
+
+def real_owners(half, count, step, width):
+    split = count // 32
+    take = lambda v, n: v.reshape(16, n, split, step, width).transpose(0, 2, 1, 3, 4)
+    outer, rest = half[:, : 4 * split * step], half[:, 4 * split * step :]
+    if rest.shape[1]:
+        pieces = [outer.reshape(16 * split, 4 * step, width), rest.reshape(16 * split, step, width)]
+        return jnp.concatenate(pieces, 1)
+    return take(outer, 4).reshape(16 * split, 4 * step, width)
 
 
 def solution(mesh):
@@ -679,35 +745,38 @@
             bias_query, bias_value, bias_output, gain_first, shift_first, bias_outer, gain_second,
             shift_second, bias_inner,
         )
-        line = jnp.concatenate(vectors)
         small = len(vectors) - 1
-        line = jnp.pad(line, (0, width - line.shape[0]))[None]
-        line = jnp.pad(line, ((0, 7), (0, 0)))
-        inner_rows = w_inner.reshape(step, wide, width).transpose(1, 0, 2).reshape(-1, width)
-        pack_c = jnp.concatenate([w_outer, w_output, inner_rows], 0)
-        got_c = lax.all_gather(pack_c, AXES, axis=0, tiled=True).reshape(count, -1, width)
-
-        gather = Gather(plan, jnp.concatenate([w_query, w_key, w_value, line], 0))
+        line, place = 0, 0
+        for vector in vectors:
+            size = vector.shape[0]
+            line = line + jnp.pad(vector, (place, width - place - size))
+            place += size
+        line = jnp.pad(line[None], ((0, 7), (0, 0)))
+        inner_rows = [w_inner[:, i * width : (i + 1) * width] for i in range(wide)]
+        pack = jnp.concatenate([w_outer, w_output, *inner_rows, w_query, w_key, w_value, line], 0)
+        got = lax.all_gather(pack, AXES, axis=0, tiled=True).reshape(count, -1, width)
+        lines = got[:, 12 * step]
+        if step % 8:
+            cuts = [wide * step, (wide + 1) * step, (2 * wide + 1) * step, 12 * step]
+            outer, output, inner, rest, _ = jnp.split(got, cuts, axis=1)
+            apart = lambda v, n: v.reshape(count, n, step, width).transpose(1, 0, 2, 3)
+            inner, rest = [
+                v.reshape(v.shape[0], 32, width // 32, width).transpose(1, 0, 2, 3)
+                for v in (apart(inner, wide), apart(rest, 3))
+            ]
+            got = jnp.concatenate(
+                [v.reshape(32, -1, width) for v in (outer, output, inner, rest)], 1
+            )
+        runs = plan.grp
+        core = (lax.axis_index("grp") % 2).astype(jnp.int32).reshape(1)
+
         exchange = Tokens(plan, own)
-        gather.stage(plan.z)
-        gather.held, *seen = tie(gather.held, *exchange.stage_one())
-        if seen:
-            exchange.same, exchange.beside = seen
-        gather.stage(plan.y)
-        gather.held, *seen = tie(gather.held, *exchange.stage_two())
-        if seen:
-            exchange.other, exchange.same_y, exchange.diagonal = seen
-        gather.stage(plan.x)
+        exchange.stage_one()
+        exchange.stage_two()
         exchange.stage_three()
-        gather.stage(plan.core)
-        got_a = gather.ordered()
         spots, near = exchange.spots()
         first_near = PROMPT // rows
 
-        full_query, full_key, full_value = [
-            got_a[:, i * step : (i + 1) * step].reshape(width, width) for i in range(3)
-        ]
-        lines = got_a[:, 3 * step]
         table = lines[:, : small * step].reshape(count, small, step).transpose(1, 0, 2)
         table = table.reshape(small, width).astype(F32)
         v_bin = lines[:, small * step : (small + wide) * step].reshape(wide, width).astype(F32)
@@ -718,77 +787,68 @@
         near = near.astype(jnp.int32).reshape(1)
 
         queries, keys_p, values_p, keys_n, values_n, context, log_total = attention_call(
-            spots, first_near, near, own, full_query, full_key, full_value, table[0:1], table[1:2],
-            seg_own, seg_near,
+            spots, first_near, near, own, got, table[0:1], table[1:2], seg_own, seg_near
         )
-
+        vec = jnp.concatenate([table[2:], jnp.zeros((2, width), F32)], 0)
+        layer_out, grad_h1, grad_context, a_send, a_keep, b_send, b_keep, sums, sums_bin = middle_call(
+            context, own, cotangent[0], got, vec, v_bin, core, runs
+        )
         if step % 8:
-            cuts = [wide * step, (wide + 1) * step]
-            outer, output, inner = jnp.split(got_c, cuts, axis=1)
-            inner = inner.reshape(count, wide, step, width).transpose(1, 0, 2, 3)
-            inner = inner.reshape(wide, 32, width // 32, width).transpose(1, 0, 2, 3)
-            got_c = jnp.concatenate(
-                [v.reshape(32, -1, width) for v in (outer, output, inner)], 1
-            )
-        vec = jnp.concatenate([table[2:], jnp.zeros((2, width), F32)], 0)
-        layer_out, grad_h1, grad_context, d_output, d_inner, d_outer, sums, sums_bin = middle_call(
-            context, own, cotangent[0], got_c, vec, v_bin
+            a_send, a_keep, b_send, b_keep = [
+                real_owners(v, count, step, width) for v in (a_send, a_keep, b_send, b_keep)
+            ]
+        core_bit = plan.core[0]
+        left = [1 << i for i in reversed(range(plan.bits)) if 1 << i != core_bit]
+        back = lambda start, gctx, into: back_call(
+            start, 1, first_near, near, gctx, context, queries, keys_p, values_p, log_total,
+            seg_own, seg_near, None, into,
         )
-        by_owner = lambda grad: grad.reshape(count, step, -1)
-        r_outer = Reduce(plan, d_outer.reshape(count, wide * step, width))
-        r_inner = Reduce(plan, d_inner.reshape(wide, count, step, width), 1)
-        r_output = Reduce(plan, by_owner(d_output))
-        big = (r_outer, r_inner, r_output)
+        parts = width // 256
+        a_got, b_got = plan.swap(a_send, core_bit), plan.swap(b_send, core_bit)
+        into = back(0, grad_context, None)
+        a_keep, a_got, b_keep, b_got, grad_context = tie(a_keep, a_got, b_keep, b_got, grad_context)
+        r_a, r_b = Reduce(plan, [a_keep, a_got], left), Reduce(plan, [b_keep, b_got], left)
+
+        def stages(reduce, bits):
+            for bit in bits:
+                reduce.stage(bit)
 
         def hold(*values):
-            tied = tie(*[r.value for r in big], *values)
-            for r, value in zip(big, tied):
-                r.value = value
-            return tied[len(big) :]
-
-        part = 256
-        none = jnp.zeros((part, rows), F32)
-        back = lambda start, gctx: back_call(
-            start, 1, first_near, near, gctx, context, queries, keys_p, values_p, log_total,
-            seg_own, seg_near, none,
-        )
-        heads_p = [back(0, grad_context)]
-        for r in big:
-            r.stage(plan.core)
-        (grad_context,) = hold(grad_context)
-        r_outer.stage(plan.x)
-        r_inner.stage(plan.y)
-        r_output.stage(plan.x)
-        heads_p += [back(i, grad_context) for i in range(1, width // part)]
-        dkp, dvp, dqp = [
-            jnp.concatenate([h[i] for h in heads_p], 1 if i < 2 else 0) for i in range(3)
-        ]
-        shared_p = product_call(first_near, near, dkp, dvp, full_key, full_value, rows)
-        grad_context, dqp, shared_p = hold(grad_context, dqp, shared_p)
+            n, m = len(r_a.terms), len(r_b.terms)
+            tied = tie(*r_a.terms, *r_b.terms, *values)
+            r_a.terms, r_b.terms = list(tied[:n]), list(tied[n : n + m])
+            return tied[n + m :]
+
+        stages(r_a, plan.x)
+        stages(r_b, plan.y)
+        for i in range(1, parts):
+            into = back(i, grad_context, into)
+        dkp, dvp, dqp = into
+        shared_p = product_call(first_near, near, dkp, dvp, got, rows)
         returned = Return(plan, rows)
         returned.prompt_one(shared_p)
-        r_outer.stage(plan.y)
-        r_inner.stage(plan.x)
-        r_output.stage(plan.y)
         dkn, dvn, dq = back_call(
-            0, width // part, None, near, grad_context, context, queries, keys_n, values_n, log_total,
+            0, parts, None, near, grad_context, context, queries, keys_n, values_n, log_total,
             seg_own, seg_near, dqp,
         )
-        shared_n = product_call(None, near, dkn, dvn, full_key, full_value, rows)
-        d_query, d_both, grad_own, sums_qkv = weight_call(
-            spots, first_near, near, own, dq, full_query, grad_h1, dkp, dvp, dkn, dvn
+        dkn, dvn, dq = hold(dkn, dvn, dq)
+        stages(r_a, plan.y)
+        stages(r_b, plan.x)
+        shared_n = product_call(None, near, dkn, dvn, got, rows)
+        returned.near(shared_n)
+        returned.prompt_two()
+        q_send, q_keep, kv_send, kv_keep, grad_own, sums_qkv = weight_call(
+            spots, first_near, near, own, dq, got, grad_h1, dkp, dvp, dkn, dvn, core, runs
         )
-        returned.prompt_two()
-        d_query, d_both, shared_n, returned.same = hold(d_query, d_both, shared_n, returned.same)
+        q_send, q_keep, kv_send, kv_keep = hold(q_send, q_keep, kv_send, kv_keep)
         returned.prompt_three()
-        returned.near(shared_n)
-        for r in big:
-            r.stage(plan.z)
-        o_outer, o_inner, o_output = [r.value.reshape(r.lead + r.rest) for r in big]
+        stages(r_a, plan.z[::-1])
+        stages(r_b, plan.z[::-1])
+        o_a, o_b = r_a.result(), r_b.result()
         grad_tokens = grad_own + returned.total()
 
-        order = (5, 3, 4, 2, 0, 1)
-        d_table = jnp.concatenate([sums_qkv[:2]] + [sums[i : i + 1] for i in order], 0)
+        order = (6, 5, 3, 4, 2, 0, 1)
+        d_table = jnp.concatenate([sums_qkv[:1]] + [sums[i : i + 1] for i in order], 0)
         d_lines = jnp.concatenate(
             [
                 d_table.reshape(small, count, step).transpose(1, 0, 2).reshape(count, -1),
@@ -798,14 +858,21 @@
         )
         d_lines = jnp.pad(d_lines, ((0, 0), (0, width - d_lines.shape[1])))[:, None].astype(BF)
         d_lines = jnp.pad(d_lines, ((0, 0), (0, 7), (0, 0)))
-        r_query = Reduce(plan, jnp.concatenate([by_owner(d_query), d_lines], 1))
-        r_both = Reduce(plan, by_owner(d_both))
-        for one, two in ((plan.core, plan.core), (plan.x, plan.y), (plan.y, plan.x), (plan.z, plan.z)):
-            r_query.stage(one)
-            r_both.stage(two)
-        o_query = r_query.value
+        place = core[0]
+        pick = Reduce(plan, [])
+        if step % 8:
+            q_send, q_keep, kv_send, kv_keep = [
+                v.reshape(count // 2, step, -1) for v in (q_send, q_keep, kv_send, kv_keep)
+            ]
+        q_send = jnp.concatenate([q_send, pick.cut(d_lines, core_bit, 1 - place)], 1)
+        q_keep = jnp.concatenate([q_keep, pick.cut(d_lines, core_bit, place)], 1)
+        r_q = Reduce(plan, [q_keep, plan.swap(q_send, core_bit)], left)
+        r_kv = Reduce(plan, [kv_keep, plan.swap(kv_send, core_bit)], left)
+        stages(r_q, plan.x + plan.y + plan.z[::-1])
+        stages(r_kv, plan.y + plan.x + plan.z[::-1])
+        o_query = r_q.result()
         o_line = o_query[step]
-        o_both = r_both.value.reshape(step, width // part, 2, part)
+        o_both = r_kv.result().reshape(step, parts, 2, width // parts)
 
         o_small = [o_line[i * step : (i + 1) * step] for i in range(small)]
         o_bin = o_line[small * step : (small + wide) * step]
@@ -815,9 +882,9 @@
             o_query[:step],
             o_both[:, :, 0].reshape(step, width),
             o_both[:, :, 1].reshape(step, width),
-            o_output,
-            o_inner.transpose(1, 0, 2).reshape(step, wide * width),
-            o_outer,
+            o_a[wide * step :],
+            o_b.reshape(wide, step, width).transpose(1, 0, 2).reshape(step, wide * width),
+            o_a[: wide * step],
             o_small[0],
             o_small[1],
             o_small[2],

time: 437 us -> 438 us (level)
  waiting for transfers between devices: 132 us -> 199 us
  starting transfers between devices: 104 us -> 72.2 us
  local copies, waits for them, and re-layouts: 59.2 us -> 38.5 us
  other arithmetic: 32 us -> 18.3 us
    all_gather x1, waiting for transfers between devices: 0.02 us -> 74.2 us  [per_device(): lax.all_gather(pack, AXES, axis=0, tiled=True).reshape(count, -1, width)]
    ppermute x44 -> x28, starting transfers between devices: 95.5 us -> 63.3 us  [swap(): return lax.ppermute(value, AXES, [(i, i ^ mask) for i in range(self.count)])]
    ppermute x44 -> x28, waiting for transfers between devices: 131 us -> 116 us  [swap(): return lax.ppermute(value, AXES, [(i, i ^ mask) for i in range(self.count)])]
    concatenate x7 -> x2, other arithmetic: 7.91 us -> 0.15 us  [the longest x1 0.08 us: per_device(): jnp.concatenate([q_send, pick.cut(d_lines, core_bit, 1 - place)], 1)]
    dynamic_slice x19 -> x26, local copies, waits for them, and re-layouts: 13.4 us -> 5.69 us  [cut(): lax.dynamic_slice_in_dim(term, place, 1, 1).reshape(high * low, rows, width)]
    ppermute x4, waiting for transfers between devices: 1.57 us -> 8.77 us  [send(): return lax.ppermute(value, AXES, pairs)]
    concatenate x3 -> x2, local copies, waits for them, and re-layouts: 7.12 us -> 0.05 us  [the longest x1 0.04 us: per_device(): jnp.concatenate([sums_qkv[:1]] + [sums[i:i + 1] for i in order], 0)]
    convert_element_type x15 -> x12, other arithmetic: 16.6 us -> 9.98 us  [stage(): self.total([self.cut(t, bit, 1 - place) for t in self.terms]).astype(BF)]
  transfers between devices with their start and end apart: 49 -> 33, of which waited for: 16 -> 18; matrix products, arithmetic and copies ran while one was open for 16% -> 8% of each run, Pallas kernels for 13% -> 12%
where the time goes in v5:
time: 438 us; the launch traced here: 436 us
  waiting for transfers between devices  199 us (45%)
  Pallas kernels  93.7 us (21%)
  starting transfers between devices  72.2 us (16%)
  local copies, waits for them, and re-layouts  38.5 us (9%)
  other arithmetic  18.3 us (4%)
  between operations  14.8 us (3%)
    ppermute x28, waiting for transfers between devices, swap(): return lax.ppermute(value, AXES, [(i, i ^ mask) for i in range(self.count)])  116 us
    all_gather x1, waiting for transfers between devices, per_device(): lax.all_gather(pack, AXES, axis=0, tiled=True).reshape(count, -1, width)  74.2 us
    ppermute x28, starting transfers between devices, swap(): return lax.ppermute(value, AXES, [(i, i ^ mask) for i in range(self.count)])  63.3 us
    pallas_call x4, Pallas kernels, back_call(): pl.pallas_call(functools.partial(back_kernel, rows, bound, dq0 is not Non...  28.6 us
    pallas_call x1, Pallas kernels, middle_call(): pl.pallas_call(functools.partial(middle_kernel, wide, runs), grid=(2 * wi...  20.8 us
    pallas_call x1, Pallas kernels, attention_call(): pl.pallas_call(functools.partial(attention_kernel, blocks, first, rows),...  18.9 us
    pallas_call x1, Pallas kernels, weight_call(): pl.pallas_call(functools.partial(weight_kernel, blocks, first, rows, runs...  14.6 us
    unnamed x65, local copies, waits for them, and re-layouts  13.7 us
  transfers between devices with their start and end apart: 33, of which 18 were waited for; matrix products, arithmetic and copies ran while one was open for 8% of the time, Pallas kernels for 12%

profile of v5, /device:TPU:0, one launch (start us, length us, event | category | flops | bytes accessed | tf_op | source)
XLA Modules:
  0.0 436.3 jit_solution(13741518481637221134)
XLA Ops:
  16.1 6.0 %collective-permute-start = (bf16[256,768]{1,0:T(8,128)(2,1)}, bf16[256,768]{1,0:T(8,128)(2,1)S(1)}, u32[]{:S(2)}, u32[]{:S(2)}) collective-permute-start(bf16[256,768]{1,0:T(8,128)(2,1)} %bitcast.207), channel_id=1, source_target_pairs={{0,4},{1,5},{2,6},{3,7},{8,12},{9,13},{10,14},{11,15},{16,20},{17,... | collective-permute-start | bytes 1179656 | tf_op jit(solution)/shard_map/ppermute | solution.py:52
  22.8 1.6 collective-permute-start.4
  25.3 8.8 %collective-permute-done = bf16[256,768]{1,0:T(8,128)(2,1)S(1)} collective-permute-done((bf16[256,768]{1,0:T(8,128)(2,1)}, bf16[256,768]{1,0:T(8,128)(2,1)S(1)}, u32[]{:S(2)}, u32[]{:S(2)}) %collective-permute-start) | collective-permute-done | bytes 393248 | tf_op jit(solution)/shard_map/ppermute | solution.py:52
  34.1 16.4 %collective-permute-start.1 = (bf16[256,768]{1,0:T(8,128)(2,1)S(1)}, bf16[256,768]{1,0:T(8,128)(2,1)S(1)}, u32[]{:S(2)}, u32[]{:S(2)}) collective-permute-start(bf16[256,768]{1,0:T(8,128)(2,1)S(1)} %broadcast_select_fusion.refs_0_), channel_id=1, source_target_pairs={{0,2},{1,3},{2,0},{3,1},{4,6},{5,7},{6,4},{7,5},{8,10},{9,11},{10,... | collective-permute-start | bytes 1179656 | tf_op jit(solution)/shard_map/ppermute | solution.py:48
  52.1 1.5 collective-permute-start.2
  53.6 7.3 %collective-permute-done.1.refs_1_ = bf16[256,768]{1,0:T(8,128)(2,1)S(1)} collective-permute-done((bf16[256,768]{1,0:T(8,128)(2,1)S(1)}, bf16[256,768]{1,0:T(8,128)(2,1)S(1)}, u32[]{:S(2)}, u32[]{:S(2)}) %collective-permute-start.1) | collective-permute-done | bytes 393248 | tf_op jit(solution)/shard_map/ppermute | solution.py:48
  62.2 74.2 %all-gather.2.cloned.1.call-done = bf16[9472,768]{1,0:T(8,128)(2,1)} async-done(((bf16[296,768]{1,0:T(8,128)(2,1)}), bf16[9472,768]{1,0:T(8,128)(2,1)}) %all-gather.2.cloned.1.call-update) | async-done | bytes 14549008 | tf_op jit(solution)/shard_map/all_gather | solution.py:757
  141.7 18.9 %attention.1 = (bf16[256,768]{1,0:T(8,128)(2,1)}, bf16[1024,768]{1,0:T(8,128)(2,1)}, bf16[1024,768]{1,0:T(8,128)(2,1)}, bf16[768,768]{1,0:T(8,128)(2,1)}, bf16[7...) custom-call(bf16[256,768]{1,0:T(8,128)(2,1)} %copy-done.4, bf16[256,768]{1,0:T(8,128)(2,1)} %copy-done.14, ...), custom_call_target="tpu_custom_call" | custom-call | flops 9865003008 | bytes 12582912 | tf_op jit(solution)/shard_map/attention/pallas_call | solution.py:293
  160.7 20.8 %middle.1 = (bf16[256,768]{1,0:T(8,128)(2,1)}, f32[256,768]{1,0:T(8,128)}, bf16[256,768]{1,0:T(8,128)(2,1)}, bf16[16,120,768]{2,1,0:T(8,128)(2,1)}, bf16[16,120,...) custom-call(s32[1]{0:T(128)} %bitcast.core_ref.refs_8_, ...), custom_call_target="tpu_custom_call" | custom-call | flops 8153726976 | bytes 33554432 | tf_op jit(solution)/shard_map/middle/pallas_call | solution.py:482
  183.6 7.8 %attention_back.4 = (bf16[1024,768]{1,0:T(8,128)(2,1)}, bf16[1024,768]{1,0:T(8,128)(2,1)}, f32[768,256]{1,0:T(8,128)}) custom-call(s32[1]{0:T(128)} %bitcast.2.refs_7_.refs_0_.near_ref, bf16[256,768]{1,0:T(8,128)(2,1)} %get-tuple-element.88.refs_1_, bf16[256,768]{1,0:T(8,128)(2,1)} %get-tuple-element.77.ctx_ref.refs_2_, ...), custom_call_target="tpu_custom_call" | custom-call | flops 5368709120 | bytes 2097152 | tf_op jit(solution)/shard_map/attention_back/pallas_call | solution.py:579
  191.4 4.0 fusion
  195.5 1.5 collective-permute-start.9
  196.9 1.5 add_convert_fusion
  199.0 7.8 %attention_back.5 = (bf16[1024,768]{1,0:T(8,128)(2,1)}, bf16[1024,768]{1,0:T(8,128)(2,1)}, f32[768,256]{1,0:T(8,128)}) custom-call(s32[1]{0:T(128)} %bitcast.2.refs_7_.refs_0_.near_ref, bf16[256,768]{1,0:T(8,128)(2,1)} %get-tuple-element.88.refs_1_, ...), custom_call_target="tpu_custom_call", output_to_operand_aliasing={{0}: (9, {}), {1}: (10, {}), {2}: (11, {})} | custom-call | flops 5368709120 | bytes 2097152 | tf_op jit(solution)/shard_map/attention_back/pallas_call | solution.py:579
  206.8 7.7 %attention_back.6 = (bf16[1024,768]{1,0:T(8,128)(2,1)}, bf16[1024,768]{1,0:T(8,128)(2,1)}, f32[768,256]{1,0:T(8,128)}) custom-call(s32[1]{0:T(128)} %bitcast.2.refs_7_.refs_0_.near_ref, bf16[256,768]{1,0:T(8,128)(2,1)} %get-tuple-element.88.refs_1_, ...), custom_call_target="tpu_custom_call", output_to_operand_aliasing={{0}: (9, {}), {1}: (10, {}), {2}: (11, {})} | custom-call | flops 5368709120 | bytes 2097152 | tf_op jit(solution)/shard_map/attention_back/pallas_call | solution.py:579
  214.5 6.6 %token_product.2 = bf16[4,256,768]{2,1,0:T(8,128)(2,1)} custom-call(s32[1]{0:T(128)} %bitcast.2.refs_7_.refs_0_.near_ref, bf16[1024,768]{1,0:T(8,128)(2,1)} %get-tuple-element.107.refs_13_.dk_ref, bf16[1024,768]{1,0:T(8,128)(2,1)} %get-tuple-element.108.refs_14_.dv_ref, bf16[32,296,768]{2,1,0:T(8,128)(2,1)} %bitcast.202, bf16[32,296,768]{2,1,0:T(8,128)(2,1)} %bitcast.203), custom_call_target="tpu_custom_call" | custom-call | flops 2415919104 | bytes 4718592 | tf_op jit(solution)/shard_map/token_product/pallas_call | solution.py:612
  222.3 1.5 collective-permute-start.10
  224.4 5.3 %attention_back.7 = (bf16[768,768]{1,0:T(8,128)(2,1)}, bf16[768,768]{1,0:T(8,128)(2,1)}, f32[768,256]{1,0:T(8,128)}) custom-call(s32[1]{0:T(128)} %bitcast.2.refs_7_.refs_0_.near_ref, bf16[256,768]{1,0:T(8,128)(2,1)} %get-tuple-element.88.refs_1_, bf16[256,768]{1,0:T(8,128)(2,1)} %get-tuple-element.77.ctx_ref.refs_2_, ...), custom_call_target="tpu_custom_call" | custom-call | flops 12079595520 | bytes 4718592 | tf_op jit(solution)/shard_map/attention_back/pallas_call | solution.py:579
  229.7 1.5 dynamic-slice_bitcast_fusion.1
  231.2 10.3 %collective-permute-done.11 = bf16[256,768]{1,0:T(8,128)(2,1)S(1)} collective-permute-done((bf16[256,768]{1,0:T(8,128)(2,1)S(1)}, bf16[256,768]{1,0:T(8,128)(2,1)S(1)}, u32[]{:S(2)}, u32[]{:S(2)}) %collective-permute-start.11) | collective-permute-done | bytes 393248 | tf_op jit(solution)/shard_map/ppermute | solution.py:48
  242.3 1.5 dynamic-slice_bitcast_fusion
  243.8 1.3 constant_dynamic-slice_fusion.32
  246.2 5.3 %collective-permute-done.12 = bf16[256,768]{1,0:T(8,128)(2,1)S(1)} collective-permute-done((bf16[256,768]{1,0:T(8,128)(2,1)S(1)}, bf16[256,768]{1,0:T(8,128)(2,1)S(1)}, u32[]{:S(2)}, u32[]{:S(2)}) %collective-permute-start.12) | collective-permute-done | bytes 393248 | tf_op jit(solution)/shard_map/ppermute | solution.py:48
  255.5 2.2 add_convert_fusion.4
  257.7 1.9 constant_dynamic-slice_fusion.28
  259.6 4.1 token_product.3
  263.7 14.6 %weight_product.1 = (bf16[16,24,768]{2,1,0:T(8,128)(2,1)}, bf16[16,24,768]{2,1,0:T(8,128)(2,1)}, bf16[16,24,1536]{2,1,0:T(8,128)(2,1)}, bf16[16,24,1536]{2,1,0:T...) custom-call(bf16[256,768]{1,0:T(8,128)(2,1)} %copy-done.4, bf16[256,768]{1,0:T(8,128)(2,1)} %copy-done.14, ...), custom_call_target="tpu_custom_call" | custom-call | flops 4227858432 | bytes 16515072 | tf_op jit(solution)/shard_map/weight_product/pallas_call | solution.py:690
  280.9 1.3 dynamic-slice_bitcast_fusion.4
  282.5 1.5 fusion.7
  284.0 1.5 collective-permute-start.16
  287.3 1.6 collective-permute-start.17
  290.3 18.5 %collective-permute-done.14 = bf16[256,768]{1,0:T(8,128)(2,1)S(1)} collective-permute-done((bf16[256,768]{1,0:T(8,128)(2,1)S(1)}, bf16[256,768]{1,0:T(8,128)(2,1)S(1)}, u32[]{:S(2)}, u32[]{:S(2)}) %collective-permute-start.14) | collective-permute-done | bytes 393248 | tf_op jit(solution)/shard_map/ppermute | solution.py:48
  308.8 2.3 fusion.10
  311.4 26.7 %collective-permute-start.30 = (bf16[2,96,768]{2,1,0:T(8,128)(2,1)S(1)}, bf16[2,96,768]{2,1,0:T(8,128)(2,1)S(1)}, u32[]{:S(2)}, u32[]{:S(2)}) collective-permute-start(bf16[2,96,768]{2,1,0:T(8,128)(2,1)S(1)} %bitcast.324), channel_id=1, source_target_pairs={{0,4},{1,5},{2,6},{3,7},{4,0},{5,1},{6,2},{7,3},{8,12},{9,13},{10,... | collective-permute-start | bytes 884744 | tf_op jit(solution)/shard_map/ppermute | solution.py:48
  340.6 17.2 %collective-permute-done.30 = bf16[2,96,768]{2,1,0:T(8,128)(2,1)S(1)} collective-permute-done((bf16[2,96,768]{2,1,0:T(8,128)(2,1)S(1)}, bf16[2,96,768]{2,1,0:T(8,128)(2,1)S(1)}, u32[]{:S(2)}, u32[]{:S(2)}) %collective-permute-start.30) | collective-permute-done | bytes 294944 | tf_op jit(solution)/shard_map/ppermute | solution.py:48
  358.7 6.3 %collective-permute-done.28 = bf16[2,120,768]{2,1,0:T(8,128)(2,1)S(1)} collective-permute-done((bf16[2,120,768]{2,1,0:T(8,128)(2,1)S(1)}, bf16[2,120,768]{2,1,0:T(8,128)(2,1)S(1)}, u32[]{:S(2)}, u32[]{:S(2)}) %collective-permute-start.28) | collective-permute-done | bytes 368672 | tf_op jit(solution)/shard_map/ppermute | solution.py:48
  365.6 2.6 collective-permute-done.31
  369.1 3.0 collective-permute-done.29
  374.1 10.1 %collective-permute-done.19 = bf16[8,32,768]{2,1,0:T(8,128)(2,1)S(1)} collective-permute-done((bf16[8,32,768]{2,1,0:T(8,128)(2,1)S(1)}, bf16[8,32,768]{2,1,0:T(8,128)(2,1)S(1)}, u32[]{:S(2)}, u32[]{:S(2)}) %collective-permute-start.19) | collective-permute-done | bytes 393248 | tf_op jit(solution)/shard_map/ppermute | solution.py:48
  384.8 5.5 %collective-permute-done.20 = bf16[4,32,768]{2,1,0:T(8,128)(2,1)S(1)} collective-permute-done((bf16[4,32,768]{2,1,0:T(8,128)(2,1)S(1)}, bf16[4,32,768]{2,1,0:T(8,128)(2,1)S(1)}, u32[]{:S(2)}, u32[]{:S(2)}) %collective-permute-start.20) | collective-permute-done | bytes 196640 | tf_op jit(solution)/shard_map/ppermute | solution.py:48
  390.3 1.4 collective-permute-start.21
  391.7 5.2 %collective-permute-done.21 = bf16[2,32,768]{2,1,0:T(8,128)(2,1)S(1)} collective-permute-done((bf16[2,32,768]{2,1,0:T(8,128)(2,1)S(1)}, bf16[2,32,768]{2,1,0:T(8,128)(2,1)S(1)}, u32[]{:S(2)}, u32[]{:S(2)}) %collective-permute-start.21) | collective-permute-done | bytes 98336 | tf_op jit(solution)/shard_map/ppermute | solution.py:48
  397.4 3.7 collective-permute-done.22
  402.4 6.1 %collective-permute-done.24 = bf16[8,24,1536]{2,1,0:T(8,128)(2,1)S(1)} collective-permute-done((bf16[8,24,1536]{2,1,0:T(8,128)(2,1)S(1)}, bf16[8,24,1536]{2,1,0:T(8,128)(2,1)S(1)}, u32[]{:S(2)}, u32[]{:S(2)}) %collective-permute-start.24) | collective-permute-done | bytes 589856 | tf_op jit(solution)/shard_map/ppermute | solution.py:48
  409.2 6.2 %collective-permute-done.25 = bf16[4,24,1536]{2,1,0:T(8,128)(2,1)S(1)} collective-permute-done((bf16[4,24,1536]{2,1,0:T(8,128)(2,1)S(1)}, bf16[4,24,1536]{2,1,0:T(8,128)(2,1)S(1)}, u32[]{:S(2)}, u32[]{:S(2)}) %collective-permute-start.25) | collective-permute-done | bytes 294944 | tf_op jit(solution)/shard_map/ppermute | solution.py:48
  415.5 2.5 collective-permute-start.26
  418.0 5.2 %collective-permute-done.26 = bf16[2,24,1536]{2,1,0:T(8,128)(2,1)S(1)} collective-permute-done((bf16[2,24,1536]{2,1,0:T(8,128)(2,1)S(1)}, bf16[2,24,1536]{2,1,0:T(8,128)(2,1)S(1)}, u32[]{:S(2)}, u32[]{:S(2)}) %collective-permute-start.26) | collective-permute-done | bytes 147488 | tf_op jit(solution)/shard_map/ppermute | solution.py:48
  424.1 3.5 collective-permute-done.27
  (195 shorter events, 48.0 us)
Async XLA Ops:
  7.2 26.9 %copy-start = (bf16[1,256,768]{2,1,0:T(8,128)(2,1)S(1)}, bf16[1,256,768]{2,1,0:T(8,128)(2,1)}, u32[]{:S(2)}) copy-start(bf16[1,256,768]{2,1,0:T(8,128)(2,1)} %param.18) | copy-start | bytes 1179652
  7.2 129.2 %all-gather.2.cloned.1.call-start = ((), (), s32[]{:S(2)}) async-start(), calls=%async_computation | async-start | bytes 15003648 | tf_op jit(solution)/shard_map/all_gather | solution.py:757
  16.1 17.9 %collective-permute-start = (bf16[256,768]{1,0:T(8,128)(2,1)}, bf16[256,768]{1,0:T(8,128)(2,1)S(1)}, u32[]{:S(2)}, u32[]{:S(2)}) collective-permute-start(bf16[256,768]{1,0:T(8,128)(2,1)} %bitcast.207), channel_id=1, source_target_pairs={{0,4},{1,5},{2,6},{3,7},{8,12},{9,13},{10,14},{11,15},{16,20},{17,... | collective-permute-start | bytes 1179656 | tf_op jit(solution)/shard_map/ppermute | solution.py:52
  22.1 118.5 %collective-permute-start.5 = (bf16[256,768]{1,0:T(8,128)(2,1)}, bf16[256,768]{1,0:T(8,128)(2,1)S(1)}, u32[]{:S(2)}, u32[]{:S(2)}) collective-permute-start(bf16[256,768]{1,0:T(8,128)(2,1)} %bitcast.208), channel_id=1, source_target_pairs={{5,6},{6,5},{13,14},{14,13},{21,22},{22,21},{29,30},{30,29}} | collective-permute-start | bytes 1179656 | tf_op jit(solution)/shard_map/ppermute | solution.py:52
  22.8 117.8 %collective-permute-start.4 = (bf16[256,768]{1,0:T(8,128)(2,1)}, bf16[256,768]{1,0:T(8,128)(2,1)S(1)}, u32[]{:S(2)}, u32[]{:S(2)}) collective-permute-start(bf16[256,768]{1,0:T(8,128)(2,1)} %bitcast.209), channel_id=1, source_target_pairs={{0,1},{1,0},{2,3},{3,2},{4,5},{5,4},{6,7},{7,6},{8,9},{9,8},{10,11... | collective-permute-start | bytes 1179656 | tf_op jit(solution)/shard_map/ppermute | solution.py:48
  34.1 106.5 %copy-start.4 = (bf16[256,768]{1,0:T(8,128)(2,1)}, bf16[256,768]{1,0:T(8,128)(2,1)S(1)}, u32[]{:S(2)}) copy-start(bf16[256,768]{1,0:T(8,128)(2,1)S(1)} %broadcast_select_fusion.refs_0_) | copy-start | bytes 1179652
  34.1 26.8 %collective-permute-start.1 = (bf16[256,768]{1,0:T(8,128)(2,1)S(1)}, bf16[256,768]{1,0:T(8,128)(2,1)S(1)}, u32[]{:S(2)}, u32[]{:S(2)}) collective-permute-start(bf16[256,768]{1,0:T(8,128)(2,1)S(1)} %broadcast_select_fusion.refs_0_), channel_id=1, source_target_pairs={{0,2},{1,3},{2,0},{3,1},{4,6},{5,7},{6,4},{7,5},{8,10},{9,11},{10,... | collective-permute-start | bytes 1179656 | tf_op jit(solution)/shard_map/ppermute | solution.py:48
  52.1 88.5 %collective-permute-start.2 = (bf16[256,768]{1,0:T(8,128)(2,1)S(1)}, bf16[256,768]{1,0:T(8,128)(2,1)S(1)}, u32[]{:S(2)}, u32[]{:S(2)}) collective-permute-start(bf16[256,768]{1,0:T(8,128)(2,1)S(1)} %broadcast_select_fusion.refs_0_), channel_id=1, source_target_pairs={{0,1},{1,0},{2,3},{3,2},{4,5},{5,4},{6,7},{7,6},{8,9},{9,8},{10,11... | collective-permute-start | bytes 1179656 | tf_op jit(solution)/shard_map/ppermute | solution.py:48
  60.9 79.7 %copy-start.14 = (bf16[256,768]{1,0:T(8,128)(2,1)}, bf16[256,768]{1,0:T(8,128)(2,1)S(1)}, u32[]{:S(2)}) copy-start(bf16[256,768]{1,0:T(8,128)(2,1)S(1)} %collective-permute-done.1.refs_1_) | copy-start | bytes 1179652
  60.9 79.6 %collective-permute-start.3 = (bf16[256,768]{1,0:T(8,128)(2,1)S(1)}, bf16[256,768]{1,0:T(8,128)(2,1)S(1)}, u32[]{:S(2)}, u32[]{:S(2)}) collective-permute-start(bf16[256,768]{1,0:T(8,128)(2,1)S(1)} %collective-permute-done.1.refs_1_), channel_id=1, source_target_pairs={{0,1},{1,0},{2,3},{3,2},{4,5},{5,4},{6,7},{7,6},{8,9},{9,8},{10,11... | collective-permute-start | bytes 1179656 | tf_op jit(solution)/shard_map/ppermute | solution.py:48
  181.4 10.0 %collective-permute-start.6 = (bf16[16,120,768]{2,1,0:T(8,128)(2,1)}, bf16[16,120,768]{2,1,0:T(8,128)(2,1)S(1)}, u32[]{:S(2)}, u32[]{:S(2)}) collective-permute-start(bf16[16,120,768]{2,1,0:T(8,128)(2,1)} %get-tuple-element.80), channel_id=1, source_target_pairs={{0,8},{1,9},{2,10},{3,11},{4,12},{5,13},{6,14},{7,15},{8,0},{9,1},... | collective-permute-start | bytes 8847368 | tf_op jit(solution)/shard_map/ppermute | solution.py:48
  181.7 9.6 %collective-permute-start.7 = (bf16[16,96,768]{2,1,0:T(8,128)(2,1)}, bf16[16,96,768]{2,1,0:T(8,128)(2,1)}, u32[]{:S(2)}, u32[]{:S(2)}) collective-permute-start(bf16[16,96,768]{2,1,0:T(8,128)(2,1)} %get-tuple-element.82), channel_id=1, source_target_pairs={{0,8},{1,9},{2,10},{3,11},{4,12},{5,13},{6,14},{7,15},{8,0},{9,1},... | collective-permute-start | bytes 7077896 | tf_op jit(solution)/shard_map/ppermute | solution.py:48
  191.4 5.5 %copy-start.7 = (bf16[16,120,768]{2,1,0:T(8,128)(2,1)}, bf16[16,120,768]{2,1,0:T(8,128)(2,1)S(1)}, u32[]{:S(2)}) copy-start(bf16[16,120,768]{2,1,0:T(8,128)(2,1)S(1)} %collective-permute-done.6) | copy-start | bytes 8847364
  191.4 5.5 %copy-start.5 = (bf16[16,120,768]{2,1,0:T(8,128)(2,1)S(1)}, bf16[16,120,768]{2,1,0:T(8,128)(2,1)}, u32[]{:S(2)}) copy-start(bf16[16,120,768]{2,1,0:T(8,128)(2,1)} %get-tuple-element.84) | copy-start | bytes 8847364
  195.5 58.3 %collective-permute-start.9 = (bf16[8,96,768]{2,1,0:T(8,128)(2,1)}, bf16[8,96,768]{2,1,0:T(8,128)(2,1)}, u32[]{:S(2)}, u32[]{:S(2)}) collective-permute-start(bf16[8,96,768]{2,1,0:T(8,128)(2,1)} %fusion), channel_id=1, source_target_pairs={{0,1},{1,0},{2,3},{3,2},{4,5},{5,4},{6,7},{7,6},{8,9},{9,8},{10,11... | collective-permute-start | bytes 3538952 | tf_op jit(solution)/shard_map/ppermute | solution.py:48
  198.5 55.3 %collective-permute-start.8 = (bf16[8,120,768]{2,1,0:T(8,128)(2,1)}, bf16[8,120,768]{2,1,0:T(8,128)(2,1)}, u32[]{:S(2)}, u32[]{:S(2)}) collective-permute-start(bf16[8,120,768]{2,1,0:T(8,128)(2,1)} %bitcast.14), channel_id=1, source_target_pairs={{0,16},{1,17},{2,18},{3,19},{4,20},{5,21},{6,22},{7,23},{8,24},{9,... | collective-permute-start | bytes 4423688 | tf_op jit(solution)/shard_map/ppermute | solution.py:48
  222.3 23.9 %collective-permute-start.10 = (bf16[256,768]{1,0:T(8,128)(2,1)S(1)}, bf16[256,768]{1,0:T(8,128)(2,1)S(1)}, u32[]{:S(2)}, u32[]{:S(2)}) collective-permute-start(bf16[256,768]{1,0:T(8,128)(2,1)S(1)} %get-tuple-element.141), channel_id=1, source_target_pairs={{0,1},{1,0},{2,3},{3,2},{4,5},{5,4},{6,7},{7,6},{8,9},{9,8},{10,11... | collective-permute-start | bytes 1179656 | tf_op jit(solution)/shard_map/ppermute | solution.py:48
  223.8 17.8 %collective-permute-start.11 = (bf16[256,768]{1,0:T(8,128)(2,1)S(1)}, bf16[256,768]{1,0:T(8,128)(2,1)S(1)}, u32[]{:S(2)}, u32[]{:S(2)}) collective-permute-start(bf16[256,768]{1,0:T(8,128)(2,1)S(1)} %get-tuple-element.142), channel_id=1, source_target_pairs={{0,1},{1,0},{2,3},{3,2},{4,5},{5,4},{6,7},{7,6},{8,9},{9,8},{10,11... | collective-permute-start | bytes 1179656 | tf_op jit(solution)/shard_map/ppermute | solution.py:48
  229.7 11.8 %copy-start.1 = (bf16[4,256,768]{2,1,0:T(8,128)(2,1)S(1)}, bf16[4,256,768]{2,1,0:T(8,128)(2,1)}, u32[]{:S(2)}) copy-start(bf16[4,256,768]{2,1,0:T(8,128)(2,1)} %token_product.2) | copy-start | bytes 4718596
  241.6 9.9 %collective-permute-start.12 = (bf16[256,768]{1,0:T(8,128)(2,1)S(1)}, bf16[256,768]{1,0:T(8,128)(2,1)S(1)}, u32[]{:S(2)}, u32[]{:S(2)}) collective-permute-start(bf16[256,768]{1,0:T(8,128)(2,1)S(1)} %fusion.5), channel_id=1, source_target_pairs={{0,2},{1,3},{2,0},{3,1},{4,6},{5,7},{6,4},{7,5},{8,10},{9,11},{10,... | collective-permute-start | bytes 1179656 | tf_op jit(solution)/shard_map/ppermute | solution.py:48
  243.8 2.4 copy-start.8
  251.5 4.0 copy-start.17
  252.5 37.8 %collective-permute-start.13 = (bf16[256,768]{1,0:T(8,128)(2,1)}, bf16[256,768]{1,0:T(8,128)(2,1)}, u32[]{:S(2)}, u32[]{:S(2)}) collective-permute-start(bf16[256,768]{1,0:T(8,128)(2,1)} %fusion.9), channel_id=1, source_target_pairs={{4,0},{5,1},{6,2},{7,3},{12,8},{13,9},{14,10},{15,11},{20,16},{21,... | collective-permute-start | bytes 1179656 | tf_op jit(solution)/shard_map/ppermute | solution.py:52
  282.5 3.0 copy-start.3
  284.0 3.3 copy-start.24
  284.0 27.1 %collective-permute-start.16 = (bf16[4,120,768]{2,1,0:T(8,128)(2,1)S(1)}, bf16[4,120,768]{2,1,0:T(8,128)(2,1)S(1)}, u32[]{:S(2)}, u32[]{:S(2)}) collective-permute-start(bf16[4,120,768]{2,1,0:T(8,128)(2,1)S(1)} %fusion.7), channel_id=1, source_target_pairs={{0,1},{1,0},{2,3},{3,2},{4,5},{5,4},{6,7},{7,6},{8,9},{9,8},{10,11... | collective-permute-start | bytes 2211848 | tf_op jit(solution)/shard_map/ppermute | solution.py:48
  285.6 23.2 %collective-permute-start.14 = (bf16[256,768]{1,0:T(8,128)(2,1)S(1)}, bf16[256,768]{1,0:T(8,128)(2,1)S(1)}, u32[]{:S(2)}, u32[]{:S(2)}) collective-permute-start(bf16[256,768]{1,0:T(8,128)(2,1)S(1)} %get-tuple-element.143), channel_id=1, source_target_pairs={{0,1},{1,0},{2,3},{3,2},{4,5},{5,4},{6,7},{7,6},{8,9},{9,8},{10,11... | collective-permute-start | bytes 1179656 | tf_op jit(solution)/shard_map/ppermute | solution.py:48
  286.2 22.6 %collective-permute-start.15 = (bf16[256,768]{1,0:T(8,128)(2,1)S(1)}, bf16[256,768]{1,0:T(8,128)(2,1)S(1)}, u32[]{:S(2)}, u32[]{:S(2)}) collective-permute-start(bf16[256,768]{1,0:T(8,128)(2,1)S(1)} %get-tuple-element.144), channel_id=1, source_target_pairs={{5,6},{6,5},{13,14},{14,13},{21,22},{22,21},{29,30},{30,29}} | collective-permute-start | bytes 1179656 | tf_op jit(solution)/shard_map/ppermute | solution.py:52
  287.3 23.8 %collective-permute-start.17 = (bf16[4,96,768]{2,1,0:T(8,128)(2,1)S(1)}, bf16[4,96,768]{2,1,0:T(8,128)(2,1)S(1)}, u32[]{:S(2)}, u32[]{:S(2)}) collective-permute-start(bf16[4,96,768]{2,1,0:T(8,128)(2,1)S(1)} %bitcast.293), channel_id=1, source_target_pairs={{0,16},{1,17},{2,18},{3,19},{4,20},{5,21},{6,22},{7,23},{8,24},{9,... | collective-permute-start | bytes 1769480 | tf_op jit(solution)/shard_map/ppermute | solution.py:48
  289.0 19.8 %copy-start.18 = (bf16[256,768]{1,0:T(8,128)(2,1)S(1)}, bf16[256,768]{1,0:T(8,128)(2,1)}, u32[]{:S(2)}) copy-start(bf16[256,768]{1,0:T(8,128)(2,1)} %copy-done.17) | copy-start | bytes 1179652
  289.0 19.8 %copy-start.21 = (f32[256,768]{1,0:T(8,128)S(1)}, f32[256,768]{1,0:T(8,128)}, u32[]{:S(2)}) copy-start(f32[256,768]{1,0:T(8,128)} %get-tuple-element.111) | copy-start | bytes 2359300
  308.8 2.3 copy-start.10
  308.8 2.4 copy-start.9
  311.4 46.4 %collective-permute-start.30 = (bf16[2,96,768]{2,1,0:T(8,128)(2,1)S(1)}, bf16[2,96,768]{2,1,0:T(8,128)(2,1)S(1)}, u32[]{:S(2)}, u32[]{:S(2)}) collective-permute-start(bf16[2,96,768]{2,1,0:T(8,128)(2,1)S(1)} %bitcast.324), channel_id=1, source_target_pairs={{0,4},{1,5},{2,6},{3,7},{4,0},{5,1},{6,2},{7,3},{8,12},{9,13},{10,... | collective-permute-start | bytes 884744 | tf_op jit(solution)/shard_map/ppermute | solution.py:48
  338.3 26.7 %collective-permute-start.28 = (bf16[2,120,768]{2,1,0:T(8,128)(2,1)S(1)}, bf16[2,120,768]{2,1,0:T(8,128)(2,1)S(1)}, u32[]{:S(2)}, u32[]{:S(2)}) collective-permute-start(bf16[2,120,768]{2,1,0:T(8,128)(2,1)S(1)} %bitcast.320), channel_id=1, source_target_pairs={{0,4},{1,5},{2,6},{3,7},{4,0},{5,1},{6,2},{7,3},{8,12},{9,13},{10,... | collective-permute-start | bytes 1105928 | tf_op jit(solution)/shard_map/ppermute | solution.py:48
  340.6 17.7 %copy-start.25 = (bf16[16,24,1536]{2,1,0:T(8,128)(2,1)S(1)}, bf16[16,24,1536]{2,1,0:T(8,128)(2,1)}, u32[]{:S(2)}) copy-start(bf16[16,24,1536]{2,1,0:T(8,128)(2,1)} %get-tuple-element.128) | copy-start | bytes 3538948
  357.9 10.3 %collective-permute-start.31 = (bf16[1,96,768]{2,1,0:T(8,128)(2,1)S(1)}, bf16[1,96,768]{2,1,0:T(8,128)(2,1)S(1)}, u32[]{:S(2)}, u32[]{:S(2)}) collective-permute-start(bf16[1,96,768]{2,1,0:T(8,128)(2,1)S(1)} %fusion.13), channel_id=1, source_target_pairs={{0,2},{1,3},{2,0},{3,1},{4,6},{5,7},{6,4},{7,5},{8,10},{9,11},{10,... | collective-permute-start | bytes 442376 | tf_op jit(solution)/shard_map/ppermute | solution.py:48
  358.1 15.5 %collective-permute-start.18 = (bf16[16,32,768]{2,1,0:T(8,128)(2,1)S(1)}, bf16[16,32,768]{2,1,0:T(8,128)(2,1)S(1)}, u32[]{:S(2)}, u32[]{:S(2)}) collective-permute-start(bf16[16,32,768]{2,1,0:T(8,128)(2,1)S(1)} %pad_maximum_fusion.1), channel_id=1, source_target_pairs={{0,8},{1,9},{2,10},{3,11},{4,12},{5,13},{6,14},{7,15},{8,0},{9,1},... | collective-permute-start | bytes 2359304 | tf_op jit(solution)/shard_map/ppermute | solution.py:48
  358.2 26.0 %collective-permute-start.23 = (bf16[16,24,1536]{2,1,0:T(8,128)(2,1)S(1)}, bf16[16,24,1536]{2,1,0:T(8,128)(2,1)S(1)}, u32[]{:S(2)}, u32[]{:S(2)}) collective-permute-start(bf16[16,24,1536]{2,1,0:T(8,128)(2,1)S(1)} %copy-done.25), channel_id=1, source_target_pairs={{0,8},{1,9},{2,10},{3,11},{4,12},{5,13},{6,14},{7,15},{8,0},{9,1},... | collective-permute-start | bytes 3538952 | tf_op jit(solution)/shard_map/ppermute | solution.py:48
  365.2 6.9 %collective-permute-start.29 = (bf16[1,120,768]{2,1,0:T(8,128)(2,1)S(1)}, bf16[1,120,768]{2,1,0:T(8,128)(2,1)S(1)}, u32[]{:S(2)}, u32[]{:S(2)}) collective-permute-start(bf16[1,120,768]{2,1,0:T(8,128)(2,1)S(1)} %fusion.11), channel_id=1, source_target_pairs={{0,2},{1,3},{2,0},{3,1},{4,6},{5,7},{6,4},{7,5},{8,10},{9,11},{10,... | collective-permute-start | bytes 552968 | tf_op jit(solution)/shard_map/ppermute | solution.py:48
  373.7 10.4 %collective-permute-start.19 = (bf16[8,32,768]{2,1,0:T(8,128)(2,1)S(1)}, bf16[8,32,768]{2,1,0:T(8,128)(2,1)S(1)}, u32[]{:S(2)}, u32[]{:S(2)}) collective-permute-start(bf16[8,32,768]{2,1,0:T(8,128)(2,1)S(1)} %bitcast.317), channel_id=1, source_target_pairs={{0,16},{1,17},{2,18},{3,19},{4,20},{5,21},{6,22},{7,23},{8,24},{9,... | collective-permute-start | bytes 1179656 | tf_op jit(solution)/shard_map/ppermute | solution.py:48
  384.5 5.7 %collective-permute-start.20 = (bf16[4,32,768]{2,1,0:T(8,128)(2,1)S(1)}, bf16[4,32,768]{2,1,0:T(8,128)(2,1)S(1)}, u32[]{:S(2)}, u32[]{:S(2)}) collective-permute-start(bf16[4,32,768]{2,1,0:T(8,128)(2,1)S(1)} %fusion.15), channel_id=1, source_target_pairs={{0,1},{1,0},{2,3},{3,2},{4,5},{5,4},{6,7},{7,6},{8,9},{9,8},{10,11... | collective-permute-start | bytes 589832 | tf_op jit(solution)/shard_map/ppermute | solution.py:48
  390.3 6.6 %collective-permute-start.21 = (bf16[2,32,768]{2,1,0:T(8,128)(2,1)S(1)}, bf16[2,32,768]{2,1,0:T(8,128)(2,1)S(1)}, u32[]{:S(2)}, u32[]{:S(2)}) collective-permute-start(bf16[2,32,768]{2,1,0:T(8,128)(2,1)S(1)} %bitcast.332), channel_id=1, source_target_pairs={{0,4},{1,5},{2,6},{3,7},{4,0},{5,1},{6,2},{7,3},{8,12},{9,13},{10,... | collective-permute-start | bytes 294920 | tf_op jit(solution)/shard_map/ppermute | solution.py:48
  396.9 4.2 collective-permute-start.22
  397.1 11.4 %collective-permute-start.24 = (bf16[8,24,1536]{2,1,0:T(8,128)(2,1)S(1)}, bf16[8,24,1536]{2,1,0:T(8,128)(2,1)S(1)}, u32[]{:S(2)}, u32[]{:S(2)}) collective-permute-start(bf16[8,24,1536]{2,1,0:T(8,128)(2,1)S(1)} %fusion.8), channel_id=1, source_target_pairs={{0,1},{1,0},{2,3},{3,2},{4,5},{5,4},{6,7},{7,6},{8,9},{9,8},{10,11... | collective-permute-start | bytes 1769480 | tf_op jit(solution)/shard_map/ppermute | solution.py:48
  408.6 6.8 %collective-permute-start.25 = (bf16[4,24,1536]{2,1,0:T(8,128)(2,1)S(1)}, bf16[4,24,1536]{2,1,0:T(8,128)(2,1)S(1)}, u32[]{:S(2)}, u32[]{:S(2)}) collective-permute-start(bf16[4,24,1536]{2,1,0:T(8,128)(2,1)S(1)} %bitcast.325), channel_id=1, source_target_pairs={{0,16},{1,17},{2,18},{3,19},{4,20},{5,21},{6,22},{7,23},{8,24},{9,... | collective-permute-start | bytes 884744 | tf_op jit(solution)/shard_map/ppermute | solution.py:48
  415.5 7.7 %collective-permute-start.26 = (bf16[2,24,1536]{2,1,0:T(8,128)(2,1)S(1)}, bf16[2,24,1536]{2,1,0:T(8,128)(2,1)S(1)}, u32[]{:S(2)}, u32[]{:S(2)}) collective-permute-start(bf16[2,24,1536]{2,1,0:T(8,128)(2,1)S(1)} %bitcast.329), channel_id=1, source_target_pairs={{0,4},{1,5},{2,6},{3,7},{4,0},{5,1},{6,2},{7,3},{8,12},{9,13},{10,... | collective-permute-start | bytes 442376 | tf_op jit(solution)/shard_map/ppermute | solution.py:48
  423.2 4.4 %collective-permute-start.27 = (bf16[1,24,1536]{2,1,0:T(8,128)(2,1)S(1)}, bf16[1,24,1536]{2,1,0:T(8,128)(2,1)S(1)}, u32[]{:S(2)}, u32[]{:S(2)}) collective-permute-start(bf16[1,24,1536]{2,1,0:T(8,128)(2,1)S(1)} %fusion.16), channel_id=1, source_target_pairs={{0,2},{1,3},{2,0},{3,1},{4,6},{5,7},{6,4},{7,5},{8,10},{9,11},{10,... | collective-permute-start | bytes 221192 | tf_op jit(solution)/shard_map/ppermute | solution.py:48
  (11 other events, 14.5 us)
Sparse Core Ops, SparseCore 0:
  16.2 120.0 all-gather.1

commit v6 on v5

--- a/solution.py
+++ b/solution.py
@@ -153,7 +153,7 @@
         self.plan, self.rows = plan, rows
 
     def prompt_one(self, parts):
-        self.prompt = self.same = parts
+        self.prompt = self.same = self.own = self.back = parts
         if self.plan.row == 8:
             same, other, same_y, other_y = [parts[i].astype(F32) for i in range(4)]
             self.other = (other + self.plan.swap(parts[3], 1).astype(F32)).astype(BF)
@@ -165,8 +165,7 @@
 
     def prompt_three(self):
         if self.plan.row == 8:
-            back = self.plan.send(self.same.astype(BF), [(4, 0), (5, 1), (6, 2), (7, 3)])
-            self.same = self.same + back.astype(F32)
+            self.back = self.plan.send(self.same.astype(BF), [(4, 0), (5, 1), (6, 2), (7, 3)])
 
     def near(self, parts):
         self.around = parts
@@ -177,7 +176,7 @@
     def total(self):
         row, rows = lax.axis_index("row"), self.rows
         if self.plan.row == 8:
-            return jnp.where(row < 4, self.same, self.own)
+            return jnp.where(row < 4, self.same + self.back.astype(F32), self.own)
         around = self.around.reshape(-1, self.around.shape[-1]).astype(F32)
         start = jnp.maximum(row * rows - CONT_MOST, 0)
         whole = jnp.zeros((self.plan.row * rows + CONT_MOST, around.shape[1]), F32)
@@ -336,39 +335,32 @@
     return jnp.where(core == 0, odd, even), jnp.where(core == 0, even, odd)
 
 
-def middle_kernel(wide, runs, core_ref, ctx_ref, own_ref, cot_ref, wo_ref, wi_ref, wu_ref, vec_ref, bin_ref,
-                  out_ref, h1_ref, gctx_ref, a_send, a_keep, b_send, b_keep, sums_ref, sbin_ref,
+def middle_kernel(wide, ctx_ref, own_ref, cot_ref, wo_ref, wi_ref, wu_ref, vec_ref, bin_ref,
+                  out_ref, h1_ref, gctx_ref, grads, sums_ref, sbin_ref,
                   first_ref, n1_ref, inv_ref, low_ref, pre_ref, cdf_ref, act_ref, acc_ref,
-                  gffn_ref, glow_ref, out_buf, wo_buf, sems):
+                  gffn_ref, glow_ref, out_buf, in_buf, wo_buf, sems):
     step = pl.program_id(0)
     width = ctx_ref.shape[1]
     square = lambda ref: ref[...].reshape(width, width)
     vec = lambda i: vec_ref[i : i + 1, :]
     mean = lambda v: jnp.sum(v, axis=-1, keepdims=True) * (1.0 / width)
     down = lambda v: jnp.sum(v, axis=0, keepdims=True)
-    core = core_ref[0]
     owners = wi_ref.shape[0]
     each = width // owners
-    run = owners // runs
-
-    def put(source, runs_here, base, top, sem, act):
-        size = source.shape[0] // runs_here
-        for i in range(runs_here):
-            number = base + i
-            place = pl.ds(number // 2 * run, run)
-            rows_here = source.shape[1]
-
-            @pl.when(number % 2 == core)
-            def _():
-                act(pltpu.make_async_copy(
-                    source.at[pl.ds(i * size, size)], a_keep.at[place, pl.ds(top, rows_here)], sem.at[i]
-                ))
-
-            @pl.when(number % 2 != core)
-            def _():
-                act(pltpu.make_async_copy(
-                    source.at[pl.ds(i * size, size)], a_send.at[place, pl.ds(top, rows_here)], sem.at[i]
-                ))
+    some = owners // wide
+
+    def outer(at):
+        turn = (2 * wide - 1 - at) % 2
+        place = grads.at[pl.ds(at * some, some), pl.ds(0, wide * each)]
+        return pltpu.make_async_copy(out_buf.at[turn], place, sems.at[turn])
+
+    def inner(at):
+        turn = (2 * wide - 1 - at) % 2
+        place = grads.at[:, pl.ds((wide + 1 + at) * each, each)]
+        return pltpu.make_async_copy(in_buf.at[turn], place, sems.at[2 + turn])
+
+    def output():
+        return pltpu.make_async_copy(wo_buf, grads.at[:, pl.ds(wide * each, each)], sems.at[4])
 
     @pl.when(step == 0)
     def _():
@@ -428,21 +420,16 @@
         grad = (nt(low, square(wu_ref)) * slope).astype(BF)
         sbin_ref[pl.ds(at, 1), :] = down(grad.astype(F32))
         turn = step % 2
-        chunk_runs = runs // wide
-        outer = lambda which, at, act: put(
-            out_buf.at[which], chunk_runs, at * chunk_runs, 0, sems.at[which], act
-        )
 
         @pl.when(step >= wide + 2)
         def _():
-            outer(turn, at + 2, lambda c: c.wait())
-
-        d_outer = tn(act_ref[:, chunk], low).astype(BF)
-        out_buf[turn] = d_outer.reshape(owners // wide, wide * each, width)
-        outer(turn, at, lambda c: c.start())
-        away, here = halves(tn(low_ref[...], grad).astype(BF), runs, core)
-        b_send[...] = away.reshape(owners // 2, each, width)
-        b_keep[...] = here.reshape(owners // 2, each, width)
+            outer(at + 2).wait()
+            inner(at + 2).wait()
+
+        out_buf[turn] = tn(act_ref[:, chunk], low).astype(BF).reshape(some, wide * each, width)
+        outer(at).start()
+        in_buf[turn] = tn(low_ref[...], grad).astype(BF).reshape(owners, each, width)
+        inner(at).start()
         gffn_ref[...] += nt(grad, square(wi_ref))
 
     @pl.when(step == 2 * wide - 1)
@@ -457,33 +444,29 @@
         low = back.astype(BF)
         sums_ref[5:6, :] = down(low.astype(F32))
         wo_buf[...] = tn(ctx_ref[...], low).astype(BF).reshape(owners, each, width)
-        put(wo_buf, runs, 0, wide * each, sems.at[2], lambda c: c.start())
+        output().start()
         gctx = nt(low, square(wo_ref)).astype(BF)
         gctx_ref[...] = gctx
         sums_ref[6:7, :] = down(gctx.astype(F32))
         sums_ref[7:8, :] = jnp.zeros((1, width), F32)
-        chunk_runs = runs // wide
         for at in (1, 0):
-            put(out_buf.at[(2 * wide - 1 - at) % 2], chunk_runs, at * chunk_runs, 0,
-                sems.at[(2 * wide - 1 - at) % 2], lambda c: c.wait())
-        put(wo_buf, runs, 0, wide * each, sems.at[2], lambda c: c.wait())
-
-
-def middle_call(ctx, own, cot, got, vec, b_inner, core, runs):
+            outer(at).wait()
+            inner(at).wait()
+        output().wait()
+
+
+def middle_call(ctx, own, cot, got, vec, b_inner):
     rows, width = own.shape
     owners = got.shape[0]
     each = width // owners
     wide = WIDE
-    half = owners // 2
     whole = lambda shape: pl.BlockSpec(shape, lambda s: (0,) * len(shape))
     at = lambda s: jnp.where(s < wide, s, 2 * wide - 1 - s)
-    back = lambda s: jnp.where(s < wide, wide - 1, 2 * wide - 1 - s)
     shape = jax.ShapeDtypeStruct
     return pl.pallas_call(
-        functools.partial(middle_kernel, wide, runs),
+        functools.partial(middle_kernel, wide),
         grid=(2 * wide,),
         in_specs=[
-            pl.BlockSpec(memory_space=pltpu.SMEM),
             whole((rows, width)), whole((rows, width)), whole((rows, width)),
             pl.BlockSpec((owners, each, width), lambda s: (0, WO, 0)),
             pl.BlockSpec((owners, each, width), lambda s: (0, WI + at(s), 0)),
@@ -492,15 +475,12 @@
         ],
         out_specs=[
             whole((rows, width)), whole((rows, width)), whole((rows, width)),
-            pl.BlockSpec(memory_space=pl.ANY), pl.BlockSpec(memory_space=pl.ANY),
-            pl.BlockSpec((half, each, width), lambda s: (0, back(s), 0)),
-            pl.BlockSpec((half, each, width), lambda s: (0, back(s), 0)),
+            pl.BlockSpec(memory_space=pl.ANY),
             whole((8, width)), whole((8, width)),
         ],
         out_shape=[
             shape((rows, width), BF), shape((rows, width), F32), shape((rows, width), BF),
-            shape((half, (wide + 1) * each, width), BF), shape((half, (wide + 1) * each, width), BF),
-            shape((half, wide * each, width), BF), shape((half, wide * each, width), BF),
+            shape((owners, (2 * wide + 1) * each, width), BF),
             shape((8, width), F32), shape((8, width), F32),
         ],
         scratch_shapes=[
@@ -510,7 +490,8 @@
             pltpu.VMEM((rows, width), F32), pltpu.VMEM((rows, width), F32),
             pltpu.VMEM((rows, width), BF),
             pltpu.VMEM((2, owners // wide, wide * each, width), BF),
-            pltpu.VMEM((owners, each, width), BF), pltpu.SemaphoreType.DMA((3, runs)),
+            pltpu.VMEM((2, owners, each, width), BF),
+            pltpu.VMEM((owners, each, width), BF), pltpu.SemaphoreType.DMA((5,)),
         ],
         compiler_params=pltpu.CompilerParams(vmem_limit_bytes=60 * 2**20),
         cost_estimate=pl.CostEstimate(
@@ -518,7 +499,7 @@
             transcendentals=2 * rows * width * wide,
         ),
         name="middle",
-    )(core, ctx, own, cot, got, got, got, vec, b_inner)
+    )(ctx, own, cot, got, got, got, vec, b_inner)
 
 
 def back_kernel(rows, bound, started, *refs):
@@ -715,14 +696,11 @@
     )(*spots, near, core, own, dq, got, h1, dkp, dvp, dkn, dvn)
 
 
-def real_owners(half, count, step, width):
+def real_owners(grads, count, step, width):
     split = count // 32
-    take = lambda v, n: v.reshape(16, n, split, step, width).transpose(0, 2, 1, 3, 4)
-    outer, rest = half[:, : 4 * split * step], half[:, 4 * split * step :]
-    if rest.shape[1]:
-        pieces = [outer.reshape(16 * split, 4 * step, width), rest.reshape(16 * split, step, width)]
-        return jnp.concatenate(pieces, 1)
-    return take(outer, 4).reshape(16 * split, 4 * step, width)
+    take = lambda v: v.reshape(32, -1, split, step, width).transpose(0, 2, 1, 3, 4).reshape(count, -1, width)
+    outer, rest = grads[:, : 4 * split * step], grads[:, 4 * split * step :]
+    return jnp.concatenate([outer.reshape(count, 4 * step, width), take(rest)], 1)
 
 
 def solution(mesh):
@@ -790,40 +768,21 @@
             spots, first_near, near, own, got, table[0:1], table[1:2], seg_own, seg_near
         )
         vec = jnp.concatenate([table[2:], jnp.zeros((2, width), F32)], 0)
-        layer_out, grad_h1, grad_context, a_send, a_keep, b_send, b_keep, sums, sums_bin = middle_call(
-            context, own, cotangent[0], got, vec, v_bin, core, runs
+        layer_out, grad_h1, grad_context, grads, sums, sums_bin = middle_call(
+            context, own, cotangent[0], got, vec, v_bin
         )
         if step % 8:
-            a_send, a_keep, b_send, b_keep = [
-                real_owners(v, count, step, width) for v in (a_send, a_keep, b_send, b_keep)
-            ]
+            grads = real_owners(grads, count, step, width)
+        o_ab = lax.psum_scatter(
+            grads.reshape(-1, width), AXES, scatter_dimension=0, tiled=True
+        ).astype(F32)
         core_bit = plan.core[0]
         left = [1 << i for i in reversed(range(plan.bits)) if 1 << i != core_bit]
-        back = lambda start, gctx, into: back_call(
-            start, 1, first_near, near, gctx, context, queries, keys_p, values_p, log_total,
-            seg_own, seg_near, None, into,
+        parts = width // 256
+        dkp, dvp, dqp = back_call(
+            0, parts, first_near, near, grad_context, context, queries, keys_p, values_p, log_total,
+            seg_own, seg_near,
         )
-        parts = width // 256
-        a_got, b_got = plan.swap(a_send, core_bit), plan.swap(b_send, core_bit)
-        into = back(0, grad_context, None)
-        a_keep, a_got, b_keep, b_got, grad_context = tie(a_keep, a_got, b_keep, b_got, grad_context)
-        r_a, r_b = Reduce(plan, [a_keep, a_got], left), Reduce(plan, [b_keep, b_got], left)
-
-        def stages(reduce, bits):
-            for bit in bits:
-                reduce.stage(bit)
-
-        def hold(*values):
-            n, m = len(r_a.terms), len(r_b.terms)
-            tied = tie(*r_a.terms, *r_b.terms, *values)
-            r_a.terms, r_b.terms = list(tied[:n]), list(tied[n : n + m])
-            return tied[n + m :]
-
-        stages(r_a, plan.x)
-        stages(r_b, plan.y)
-        for i in range(1, parts):
-            into = back(i, grad_context, into)
-        dkp, dvp, dqp = into
         shared_p = product_call(first_near, near, dkp, dvp, got, rows)
         returned = Return(plan, rows)
         returned.prompt_one(shared_p)
@@ -831,21 +790,17 @@
             0, parts, None, near, grad_context, context, queries, keys_n, values_n, log_total,
             seg_own, seg_near, dqp,
         )
-        dkn, dvn, dq = hold(dkn, dvn, dq)
-        stages(r_a, plan.y)
-        stages(r_b, plan.x)
         shared_n = product_call(None, near, dkn, dvn, got, rows)
+        returned.same, shared_n, dq = tie(returned.same, shared_n, dq)
+        returned.prompt_two()
         returned.near(shared_n)
-        returned.prompt_two()
         q_send, q_keep, kv_send, kv_keep, grad_own, sums_qkv = weight_call(
             spots, first_near, near, own, dq, got, grad_h1, dkp, dvp, dkn, dvn, core, runs
         )
-        q_send, q_keep, kv_send, kv_keep = hold(q_send, q_keep, kv_send, kv_keep)
+        q_send, q_keep, kv_send, kv_keep, returned.same, returned.own = tie(
+            q_send, q_keep, kv_send, kv_keep, returned.same, returned.own
+        )
         returned.prompt_three()
-        stages(r_a, plan.z[::-1])
-        stages(r_b, plan.z[::-1])
-        o_a, o_b = r_a.result(), r_b.result()
-        grad_tokens = grad_own + returned.total()
 
         order = (6, 5, 3, 4, 2, 0, 1)
         d_table = jnp.concatenate([sums_qkv[:1]] + [sums[i : i + 1] for i in order], 0)
@@ -868,8 +823,16 @@
         q_keep = jnp.concatenate([q_keep, pick.cut(d_lines, core_bit, place)], 1)
         r_q = Reduce(plan, [q_keep, plan.swap(q_send, core_bit)], left)
         r_kv = Reduce(plan, [kv_keep, plan.swap(kv_send, core_bit)], left)
-        stages(r_q, plan.x + plan.y + plan.z[::-1])
-        stages(r_kv, plan.y + plan.x + plan.z[::-1])
+        for one, two in zip(plan.x + plan.y + plan.z[::-1], plan.y + plan.x + plan.z[::-1]):
+            n = len(r_q.terms)
+            if one == plan.z[0]:
+                *tied, returned.back = tie(*r_q.terms, *r_kv.terms, returned.back)
+            else:
+                tied = tie(*r_q.terms, *r_kv.terms)
+            r_q.terms, r_kv.terms = list(tied[:n]), list(tied[n:])
+            r_q.stage(one)
+            r_kv.stage(two)
+        grad_tokens = grad_own + returned.total()
         o_query = r_q.result()
         o_line = o_query[step]
         o_both = r_kv.result().reshape(step, parts, 2, width // parts)
@@ -882,9 +845,9 @@
             o_query[:step],
             o_both[:, :, 0].reshape(step, width),
             o_both[:, :, 1].reshape(step, width),
-            o_a[wide * step :],
-            o_b.reshape(wide, step, width).transpose(1, 0, 2).reshape(step, wide * width),
-            o_a[: wide * step],
+            o_ab[wide * step : (wide + 1) * step],
+            jnp.concatenate([o_ab[i * step : (i + 1) * step] for i in range(wide + 1, 2 * wide + 1)], 1),
+            o_ab[: wide * step],
             o_small[0],
             o_small[1],
             o_small[2],

time: 438 us -> 372 us (0.85)
  waiting for transfers between devices: 199 us -> 149 us
  local copies, waits for them, and re-layouts: 38.5 us -> 25.5 us
  starting transfers between devices: 72.2 us -> 81.5 us
  other arithmetic: 18.3 us -> 10.7 us
  Pallas kernels: 93.7 us -> 89 us
    ppermute x28 -> x18, waiting for transfers between devices: 116 us -> 53.9 us  [swap(): return lax.ppermute(value, AXES, [(i, i ^ mask) for i in range(self.count)])]
    ppermute x28 -> x18, starting transfers between devices: 63.3 us -> 72.7 us  [swap(): return lax.ppermute(value, AXES, [(i, i ^ mask) for i in range(self.count)])]
    reduce_scatter x0 -> x1, waiting for transfers between devices: none -> 8.77 us  [per_device(): lax.psum_scatter(grads.reshape(-1, width), AXES, scatter_dimension=0, til...]
    convert_element_type x12 -> x6, other arithmetic: 9.98 us -> 1.51 us  [stage(): self.total([self.cut(t, bit, 1 - place) for t in self.terms]).astype(BF)]
    reshape x5 -> x4, local copies, waits for them, and re-layouts: 5.54 us -> 0.14 us  [cut(): lax.dynamic_slice_in_dim(term, place, 1, 1).reshape(high * low, rows, width)]
    dynamic_slice x26 -> x13, local copies, waits for them, and re-layouts: 5.69 us -> 1.3 us  [cut(): lax.dynamic_slice_in_dim(term, place, 1, 1).reshape(high * low, rows, width)]
    pallas_call x4 -> x2, Pallas kernels: 28.6 us -> 24.3 us  [back_call(): pl.pallas_call(functools.partial(back_kernel, rows, bound, dq0 is not Non...]
    unnamed x65 -> x53, local copies, waits for them, and re-layouts: 13.7 us -> 11.2 us
  transfers between devices with their start and end apart: 33 -> 24, of which waited for: 18 -> 12; matrix products, arithmetic and copies ran while one was open for 8% -> 6% of each run, Pallas kernels for 12% -> 14%
where the time goes in v6:
time: 372 us; the launch traced here: 370 us
  waiting for transfers between devices  149 us (40%)
  Pallas kernels  89 us (24%)
  starting transfers between devices  81.5 us (22%)
  local copies, waits for them, and re-layouts  25.5 us (7%)
  between operations  14.7 us (4%)
  other arithmetic  10.7 us (3%)
    all_gather x1, waiting for transfers between devices, per_device(): lax.all_gather(pack, AXES, axis=0, tiled=True).reshape(count, -1, width)  77.1 us
    ppermute x18, starting transfers between devices, swap(): return lax.ppermute(value, AXES, [(i, i ^ mask) for i in range(self.count)])  72.7 us
    ppermute x18, waiting for transfers between devices, swap(): return lax.ppermute(value, AXES, [(i, i ^ mask) for i in range(self.count)])  53.9 us
    pallas_call x2, Pallas kernels, back_call(): pl.pallas_call(functools.partial(back_kernel, rows, bound, dq0 is not Non...  24.3 us
    pallas_call x1, Pallas kernels, middle_call(): pl.pallas_call(functools.partial(middle_kernel, wide), grid=(2 * wide,),...  19.9 us
    pallas_call x1, Pallas kernels, attention_call(): pl.pallas_call(functools.partial(attention_kernel, blocks, first, rows),...  18.9 us
    pallas_call x1, Pallas kernels, weight_call(): pl.pallas_call(functools.partial(weight_kernel, blocks, first, rows, runs...  14.9 us
    unnamed x53, local copies, waits for them, and re-layouts  11.2 us
  transfers between devices with their start and end apart: 24, of which 12 were waited for; matrix products, arithmetic and copies ran while one was open for 6% of the time, Pallas kernels for 14%

profile of v6, /device:TPU:0, one launch (start us, length us, event | category | flops | bytes accessed | tf_op | source)
XLA Modules:
  0.0 370.2 jit_solution(8898703871300267219)
XLA Ops:
  7.3 1.0 constant_dynamic-update-slice_fusion.5
  8.2 0.8 constant_dynamic-update-slice_fusion.4
  9.0 0.8 slice_dynamic-update-slice_fusion.3
  9.8 0.8 slice_dynamic-update-slice_fusion.2
  10.5 0.8 slice_dynamic-update-slice_fusion.1
  12.1 0.9 pad_add_fusion.1
  13.0 0.8 constant_dynamic-update-slice_fusion.3
  14.5 0.8 constant_dynamic-update-slice_fusion.1
  16.1 6.0 %collective-permute-start = (bf16[256,768]{1,0:T(8,128)(2,1)S(1)}, bf16[256,768]{1,0:T(8,128)(2,1)S(1)}, u32[]{:S(2)}, u32[]{:S(2)}) collective-permute-start(bf16[256,768]{1,0:T(8,128)(2,1)S(1)} %bitcast.134), channel_id=1, source_target_pairs={{0,4},{1,5},{2,6},{3,7},{8,12},{9,13},{10,14},{11,15},{16,20},{17,... | collective-permute-start | bytes 1179656 | tf_op jit(solution)/shard_map/ppermute | solution.py:52
  22.1 1.6 collective-permute-start.4
  24.7 8.9 %collective-permute-done = bf16[256,768]{1,0:T(8,128)(2,1)S(1)} collective-permute-done((bf16[256,768]{1,0:T(8,128)(2,1)S(1)}, bf16[256,768]{1,0:T(8,128)(2,1)S(1)}, u32[]{:S(2)}, u32[]{:S(2)}) %collective-permute-start) | collective-permute-done | bytes 393248 | tf_op jit(solution)/shard_map/ppermute | solution.py:52
  33.7 16.5 %collective-permute-start.1 = (bf16[256,768]{1,0:T(8,128)(2,1)S(1)}, bf16[256,768]{1,0:T(8,128)(2,1)S(1)}, u32[]{:S(2)}, u32[]{:S(2)}) collective-permute-start(bf16[256,768]{1,0:T(8,128)(2,1)S(1)} %broadcast_select_fusion.refs_0_), channel_id=1, source_target_pairs={{0,2},{1,3},{2,0},{3,1},{4,6},{5,7},{6,4},{7,5},{8,10},{9,11},{10,... | collective-permute-start | bytes 1179656 | tf_op jit(solution)/shard_map/ppermute | solution.py:48
  50.9 0.9 broadcast_in_dim.36.refs_15_.refs_8_
  51.8 1.5 collective-permute-start.2
  53.3 6.2 %collective-permute-done.1.refs_1_ = bf16[256,768]{1,0:T(8,128)(2,1)S(1)} collective-permute-done((bf16[256,768]{1,0:T(8,128)(2,1)S(1)}, bf16[256,768]{1,0:T(8,128)(2,1)S(1)}, u32[]{:S(2)}, u32[]{:S(2)}) %collective-permute-start.1) | collective-permute-done | bytes 393248 | tf_op jit(solution)/shard_map/ppermute | solution.py:48
  59.5 1.5 collective-permute-start.3
  61.0 77.1 %all-gather.2.cloned.1.call-done = bf16[9472,768]{1,0:T(8,128)(2,1)} async-done(((bf16[296,768]{1,0:T(8,128)(2,1)}), bf16[9472,768]{1,0:T(8,128)(2,1)}) %all-gather.2.cloned.1.call-update) | async-done | bytes 14549008 | tf_op jit(solution)/shard_map/all_gather | solution.py:735
  138.2 1.0 slice.242
  143.5 18.9 %attention.1 = (bf16[256,768]{1,0:T(8,128)(2,1)}, bf16[1024,768]{1,0:T(8,128)(2,1)}, bf16[1024,768]{1,0:T(8,128)(2,1)}, bf16[768,768]{1,0:T(8,128)(2,1)}, bf16[7...) custom-call(bf16[256,768]{1,0:T(8,128)(2,1)} %copy-done.3, bf16[256,768]{1,0:T(8,128)(2,1)} %copy-done.7, ...), custom_call_target="tpu_custom_call" | custom-call | flops 9865003008 | bytes 12582912 | tf_op jit(solution)/shard_map/attention/pallas_call | solution.py:292
  162.4 19.9 %middle.1 = (bf16[256,768]{1,0:T(8,128)(2,1)}, f32[256,768]{1,0:T(8,128)}, bf16[256,768]{1,0:T(8,128)(2,1)}, bf16[32,216,768]{2,1,0:T(8,128)(2,1)}, f32[8,768]{1,0:T(8,128)}, /*index=5*/f32[8,768]{1,0:T(8,128)}) custom-call(bf16[256,768]{1,0:T(8,128)(2,1)} %get-tuple-element.80.ctx_ref.refs_2_, bf16[256,768]{1,0:T(8,128)(2,1)} %bitcast.131, ...), custom_call_target="tpu_custom_call" | custom-call | flops 8153726976 | bytes 33554432 | tf_op jit(solution)/shard_map/middle/pallas_call | solution.py:466
  182.3 18.6 %attention_back.2 = (bf16[1024,768]{1,0:T(8,128)(2,1)}, bf16[1024,768]{1,0:T(8,128)(2,1)}, f32[768,256]{1,0:T(8,128)}) custom-call(s32[1]{0:T(128)} %bitcast.1.refs_7_.refs_0_.near_ref, bf16[256,768]{1,0:T(8,128)(2,1)} %get-tuple-element.82.refs_1_, bf16[256,768]{1,0:T(8,128)(2,1)} %get-tuple-element.80.ctx_ref.refs_2_, ...), custom_call_target="tpu_custom_call" | custom-call | flops 16106127360 | bytes 6291456 | tf_op jit(solution)/shard_map/attention_back/pallas_call | solution.py:560
  201.0 6.7 %token_product.2 = bf16[4,256,768]{2,1,0:T(8,128)(2,1)} custom-call(s32[1]{0:T(128)} %bitcast.1.refs_7_.refs_0_.near_ref, bf16[1024,768]{1,0:T(8,128)(2,1)} %get-tuple-element.87.dk_ref.refs_13_, bf16[1024,768]{1,0:T(8,128)(2,1)} %get-tuple-element.88.dv_ref.refs_14_, bf16[32,296,768]{2,1,0:T(8,128)(2,1)} %bitcast.124, bf16[32,296,768]{2,1,0:T(8,128)(2,1)} %bitcast.125), custom_call_target="tpu_custom_call" | custom-call | flops 2415919104 | bytes 4718592 | tf_op jit(solution)/shard_map/token_product/pallas_call | solution.py:593
  207.6 1.2 slice_bitcast_fusion
  208.9 1.6 collective-permute-start.6
  210.9 5.6 %attention_back.3 = (bf16[768,768]{1,0:T(8,128)(2,1)}, bf16[768,768]{1,0:T(8,128)(2,1)}, f32[768,256]{1,0:T(8,128)}) custom-call(s32[1]{0:T(128)} %bitcast.1.refs_7_.refs_0_.near_ref, bf16[256,768]{1,0:T(8,128)(2,1)} %get-tuple-element.82.refs_1_, bf16[256,768]{1,0:T(8,128)(2,1)} %get-tuple-element.80.ctx_ref.refs_2_, ...), custom_call_target="tpu_custom_call" | custom-call | flops 12079595520 | bytes 4718592 | tf_op jit(solution)/shard_map/attention_back/pallas_call | solution.py:560
  216.6 4.4 %token_product.3 = bf16[3,256,768]{2,1,0:T(8,128)(2,1)} custom-call(s32[1]{0:T(128)} %bitcast.1.refs_7_.refs_0_.near_ref, bf16[768,768]{1,0:T(8,128)(2,1)} %get-tuple-element.92.dk_ref.refs_15_, bf16[768,768]{1,0:T(8,128)(2,1)} %get-tuple-element.93.dv_ref.refs_16_, bf16[32,296,768]{2,1,0:T(8,128)(2,1)} %bitcast.126, bf16[32,296,768]{2,1,0:T(8,128)(2,1)} %bitcast.127), custom_call_target="tpu_custom_call" | custom-call | flops 1811939328 | bytes 3538944 | tf_op jit(solution)/shard_map/token_product/pallas_call | solution.py:593
  222.4 6.3 %collective-permute-done.7 = bf16[256,768]{1,0:T(8,128)(2,1)} collective-permute-done((bf16[256,768]{1,0:T(8,128)(2,1)S(1)}, bf16[256,768]{1,0:T(8,128)(2,1)}, u32[]{:S(2)}, u32[]{:S(2)}) %collective-permute-start.7) | collective-permute-done | bytes 393248 | tf_op jit(solution)/shard_map/ppermute | solution.py:48
  228.7 1.3 fusion.1
  230.8 1.6 collective-permute-start.9
  232.9 14.9 %weight_product.1 = (bf16[16,24,768]{2,1,0:T(8,128)(2,1)}, bf16[16,24,768]{2,1,0:T(8,128)(2,1)}, bf16[16,24,1536]{2,1,0:T(8,128)(2,1)}, bf16[16,24,1536]{2,1,0:T...) custom-call(bf16[256,768]{1,0:T(8,128)(2,1)} %copy-done.3, bf16[256,768]{1,0:T(8,128)(2,1)} %copy-done.7, ...), custom_call_target="tpu_custom_call" | custom-call | flops 4227858432 | bytes 16515072 | tf_op jit(solution)/shard_map/weight_product/pallas_call | solution.py:671
  247.8 2.0 fusion
  252.2 1.2 pad_maximum_fusion.1
  254.0 1.4 collective-permute-start.19
  256.8 1.1 add_convert_fusion.2
  257.9 1.5 collective-permute-start.13
  259.5 1.0 constant_dynamic-slice_fusion.11
  260.6 8.5 %collective-permute-done.13 = bf16[8,32,768]{2,1,0:T(8,128)(2,1)S(1)} collective-permute-done((bf16[8,32,768]{2,1,0:T(8,128)(2,1)S(1)}, bf16[8,32,768]{2,1,0:T(8,128)(2,1)S(1)}, u32[]{:S(2)}, u32[]{:S(2)}) %collective-permute-start.13) | collective-permute-done | bytes 393248 | tf_op jit(solution)/shard_map/ppermute | solution.py:48
  269.1 2.8 collective-permute-done.14
  272.8 1.4 collective-permute-start.15
  274.4 6.0 %collective-permute-done.15 = bf16[4,32,768]{2,1,0:T(8,128)(2,1)S(1)} collective-permute-done((bf16[4,32,768]{2,1,0:T(8,128)(2,1)S(1)}, bf16[4,32,768]{2,1,0:T(8,128)(2,1)S(1)}, u32[]{:S(2)}, u32[]{:S(2)}) %collective-permute-start.15) | collective-permute-done | bytes 196640 | tf_op jit(solution)/shard_map/ppermute | solution.py:48
  280.4 5.2 %collective-permute-done.16 = bf16[4,24,1536]{2,1,0:T(8,128)(2,1)S(1)} collective-permute-done((bf16[4,24,1536]{2,1,0:T(8,128)(2,1)S(1)}, bf16[4,24,1536]{2,1,0:T(8,128)(2,1)S(1)}, u32[]{:S(2)}, u32[]{:S(2)}) %collective-permute-start.16) | collective-permute-done | bytes 294944 | tf_op jit(solution)/shard_map/ppermute | solution.py:48
  285.7 40.1 %collective-permute-start.18 = (bf16[2,24,1536]{2,1,0:T(8,128)(2,1)S(1)}, bf16[2,24,1536]{2,1,0:T(8,128)(2,1)S(1)}, u32[]{:S(2)}, u32[]{:S(2)}) collective-permute-start(bf16[2,24,1536]{2,1,0:T(8,128)(2,1)S(1)} %bitcast.199), channel_id=1, source_target_pairs={{0,4},{1,5},{2,6},{3,7},{4,0},{5,1},{6,2},{7,3},{8,12},{9,13},{10,... | collective-permute-start | bytes 442376 | tf_op jit(solution)/shard_map/ppermute | solution.py:48
  326.2 16.6 %collective-permute-done.17 = bf16[2,32,768]{2,1,0:T(8,128)(2,1)S(1)} collective-permute-done((bf16[2,32,768]{2,1,0:T(8,128)(2,1)S(1)}, bf16[2,32,768]{2,1,0:T(8,128)(2,1)S(1)}, u32[]{:S(2)}, u32[]{:S(2)}) %collective-permute-start.17) | collective-permute-done | bytes 98336 | tf_op jit(solution)/shard_map/ppermute | solution.py:48
  343.0 2.1 collective-permute-start.20
  345.0 0.9 fusion.3
  346.0 1.8 collective-permute-done.20
  351.5 8.8 %reduce-scatter.2.cloned.1.call-done = bf16[216,768]{1,0:T(8,128)(2,1)} async-done(((bf16[6912,768]{1,0:T(8,128)(2,1)}), bf16[216,768]{1,0:T(8,128)(2,1)}) %reduce-scatter.2.cloned.1.call-update) | async-done | bytes 331792 | tf_op jit(solution)/shard_map/reduce_scatter | solution.py:776
  360.3 1.5 fusion.9
  (142 shorter events, 22.6 us)
Async XLA Ops:
  7.2 9.0 %copy-start = (bf16[1,256,768]{2,1,0:T(8,128)(2,1)S(1)}, bf16[1,256,768]{2,1,0:T(8,128)(2,1)}, u32[]{:S(2)}) copy-start(bf16[1,256,768]{2,1,0:T(8,128)(2,1)} %param.18) | copy-start | bytes 1179652
  7.2 17.2 %copy-start.19 = (s32[1,8]{1,0:T(1,128)S(1)}, s32[1,8]{1,0:T(1,128)}, u32[]{:S(2)}) copy-start(s32[1,8]{1,0:T(1,128)} %param.19) | copy-start | bytes 100
  7.2 130.9 %all-gather.2.cloned.1.call-start = ((), (), s32[]{:S(2)}) async-start(), calls=%async_computation.1 | async-start | bytes 15003648 | tf_op jit(solution)/shard_map/all_gather | solution.py:735
  15.3 0.8 copy-start.12
  16.1 344.2 %reduce-scatter.2.cloned.1.call-start = ((), (), s32[]{:S(2)}) async-start(), calls=%async_computation.2 | async-start | bytes 10948608 | tf_op jit(solution)/shard_map/reduce_scatter | solution.py:776
  16.1 17.5 %collective-permute-start = (bf16[256,768]{1,0:T(8,128)(2,1)S(1)}, bf16[256,768]{1,0:T(8,128)(2,1)S(1)}, u32[]{:S(2)}, u32[]{:S(2)}) collective-permute-start(bf16[256,768]{1,0:T(8,128)(2,1)S(1)} %bitcast.134), channel_id=1, source_target_pairs={{0,4},{1,5},{2,6},{3,7},{8,12},{9,13},{10,14},{11,15},{16,20},{17,... | collective-permute-start | bytes 1179656 | tf_op jit(solution)/shard_map/ppermute | solution.py:52
  22.1 120.2 %collective-permute-start.4 = (bf16[256,768]{1,0:T(8,128)(2,1)S(1)}, bf16[256,768]{1,0:T(8,128)(2,1)S(1)}, u32[]{:S(2)}, u32[]{:S(2)}) collective-permute-start(bf16[256,768]{1,0:T(8,128)(2,1)S(1)} %bitcast.135), channel_id=1, source_target_pairs={{0,1},{1,0},{2,3},{3,2},{4,5},{5,4},{6,7},{7,6},{8,9},{9,8},{10,11... | collective-permute-start | bytes 1179656 | tf_op jit(solution)/shard_map/ppermute | solution.py:48
  23.7 118.6 %collective-permute-start.5 = (bf16[256,768]{1,0:T(8,128)(2,1)S(1)}, bf16[256,768]{1,0:T(8,128)(2,1)S(1)}, u32[]{:S(2)}, u32[]{:S(2)}) collective-permute-start(bf16[256,768]{1,0:T(8,128)(2,1)S(1)} %bitcast.136), channel_id=1, source_target_pairs={{5,6},{6,5},{13,14},{14,13},{21,22},{22,21},{29,30},{30,29}} | collective-permute-start | bytes 1179656 | tf_op jit(solution)/shard_map/ppermute | solution.py:52
  33.7 108.7 %copy-start.3 = (bf16[256,768]{1,0:T(8,128)(2,1)}, bf16[256,768]{1,0:T(8,128)(2,1)S(1)}, u32[]{:S(2)}) copy-start(bf16[256,768]{1,0:T(8,128)(2,1)S(1)} %broadcast_select_fusion.refs_0_) | copy-start | bytes 1179652
  33.7 25.8 %collective-permute-start.1 = (bf16[256,768]{1,0:T(8,128)(2,1)S(1)}, bf16[256,768]{1,0:T(8,128)(2,1)S(1)}, u32[]{:S(2)}, u32[]{:S(2)}) collective-permute-start(bf16[256,768]{1,0:T(8,128)(2,1)S(1)} %broadcast_select_fusion.refs_0_), channel_id=1, source_target_pairs={{0,2},{1,3},{2,0},{3,1},{4,6},{5,7},{6,4},{7,5},{8,10},{9,11},{10,... | collective-permute-start | bytes 1179656 | tf_op jit(solution)/shard_map/ppermute | solution.py:48
  51.8 90.5 %collective-permute-start.2 = (bf16[256,768]{1,0:T(8,128)(2,1)S(1)}, bf16[256,768]{1,0:T(8,128)(2,1)S(1)}, u32[]{:S(2)}, u32[]{:S(2)}) collective-permute-start(bf16[256,768]{1,0:T(8,128)(2,1)S(1)} %broadcast_select_fusion.refs_0_), channel_id=1, source_target_pairs={{0,1},{1,0},{2,3},{3,2},{4,5},{5,4},{6,7},{7,6},{8,9},{9,8},{10,11... | collective-permute-start | bytes 1179656 | tf_op jit(solution)/shard_map/ppermute | solution.py:48
  59.5 82.9 %copy-start.7 = (bf16[256,768]{1,0:T(8,128)(2,1)}, bf16[256,768]{1,0:T(8,128)(2,1)S(1)}, u32[]{:S(2)}) copy-start(bf16[256,768]{1,0:T(8,128)(2,1)S(1)} %collective-permute-done.1.refs_1_) | copy-start | bytes 1179652
  59.5 82.8 %collective-permute-start.3 = (bf16[256,768]{1,0:T(8,128)(2,1)S(1)}, bf16[256,768]{1,0:T(8,128)(2,1)S(1)}, u32[]{:S(2)}, u32[]{:S(2)}) collective-permute-start(bf16[256,768]{1,0:T(8,128)(2,1)S(1)} %collective-permute-done.1.refs_1_), channel_id=1, source_target_pairs={{0,1},{1,0},{2,3},{3,2},{4,5},{5,4},{6,7},{7,6},{8,9},{9,8},{10,11... | collective-permute-start | bytes 1179656 | tf_op jit(solution)/shard_map/ppermute | solution.py:48
  142.3 0.7 copy-start.5
  142.3 0.9 copy-start.6
  142.3 1.0 copy-start.8
  142.4 1.1 copy-start.9
  207.6 3.3 copy-start.16
  208.9 12.8 %collective-permute-start.6 = (bf16[256,768]{1,0:T(8,128)(2,1)S(1)}, bf16[256,768]{1,0:T(8,128)(2,1)S(1)}, u32[]{:S(2)}, u32[]{:S(2)}) collective-permute-start(bf16[256,768]{1,0:T(8,128)(2,1)S(1)} %get-tuple-element.150), channel_id=1, source_target_pairs={{0,1},{1,0},{2,3},{3,2},{4,5},{5,4},{6,7},{7,6},{8,9},{9,8},{10,11... | collective-permute-start | bytes 1179656 | tf_op jit(solution)/shard_map/ppermute | solution.py:48
  210.4 18.3 %collective-permute-start.7 = (bf16[256,768]{1,0:T(8,128)(2,1)S(1)}, bf16[256,768]{1,0:T(8,128)(2,1)}, u32[]{:S(2)}, u32[]{:S(2)}) collective-permute-start(bf16[256,768]{1,0:T(8,128)(2,1)S(1)} %get-tuple-element.149), channel_id=1, source_target_pairs={{0,1},{1,0},{2,3},{3,2},{4,5},{5,4},{6,7},{7,6},{8,9},{9,8},{10,11... | collective-permute-start | bytes 1179656 | tf_op jit(solution)/shard_map/ppermute | solution.py:48
  216.6 12.1 %copy-start.1 = (bf16[4,256,768]{2,1,0:T(8,128)(2,1)S(1)}, bf16[4,256,768]{2,1,0:T(8,128)(2,1)}, u32[]{:S(2)}) copy-start(bf16[4,256,768]{2,1,0:T(8,128)(2,1)} %token_product.2) | copy-start | bytes 4718596
  221.6 8.4 %copy-start.2 = (bf16[3,256,768]{2,1,0:T(8,128)(2,1)S(1)}, bf16[3,256,768]{2,1,0:T(8,128)(2,1)}, u32[]{:S(2)}) copy-start(bf16[3,256,768]{2,1,0:T(8,128)(2,1)} %token_product.3) | copy-start | bytes 3538948
  221.6 0.8 copy-start.15
  230.1 17.7 %collective-permute-start.10 = (bf16[256,768]{1,0:T(8,128)(2,1)S(1)}, bf16[256,768]{1,0:T(8,128)(2,1)S(1)}, u32[]{:S(2)}, u32[]{:S(2)}) collective-permute-start(bf16[256,768]{1,0:T(8,128)(2,1)S(1)} %get-tuple-element.152), channel_id=1, source_target_pairs={{5,6},{6,5},{13,14},{14,13},{21,22},{22,21},{29,30},{30,29}} | collective-permute-start | bytes 1179656 | tf_op jit(solution)/shard_map/ppermute | solution.py:52
  230.8 17.0 %collective-permute-start.9 = (bf16[256,768]{1,0:T(8,128)(2,1)S(1)}, bf16[256,768]{1,0:T(8,128)(2,1)}, u32[]{:S(2)}, u32[]{:S(2)}) collective-permute-start(bf16[256,768]{1,0:T(8,128)(2,1)S(1)} %get-tuple-element.151), channel_id=1, source_target_pairs={{0,1},{1,0},{2,3},{3,2},{4,5},{5,4},{6,7},{7,6},{8,9},{9,8},{10,11... | collective-permute-start | bytes 1179656 | tf_op jit(solution)/shard_map/ppermute | solution.py:48
  232.4 17.4 %collective-permute-start.8 = (bf16[256,768]{1,0:T(8,128)(2,1)S(1)}, bf16[256,768]{1,0:T(8,128)(2,1)S(1)}, u32[]{:S(2)}, u32[]{:S(2)}) collective-permute-start(bf16[256,768]{1,0:T(8,128)(2,1)S(1)} %get-tuple-element.147), channel_id=1, source_target_pairs={{0,2},{1,3},{2,0},{3,1},{4,6},{5,7},{6,4},{7,5},{8,10},{9,11},{10,... | collective-permute-start | bytes 1179656 | tf_op jit(solution)/shard_map/ppermute | solution.py:48
  249.8 1.8 copy-start.17
  249.8 1.8 copy-start.18
  249.9 6.1 %collective-permute-start.12 = (bf16[16,24,1536]{2,1,0:T(8,128)(2,1)}, bf16[16,24,1536]{2,1,0:T(8,128)(2,1)S(1)}, u32[]{:S(2)}, u32[]{:S(2)}) collective-permute-start(bf16[16,24,1536]{2,1,0:T(8,128)(2,1)} %get-tuple-element.111), channel_id=1, source_target_pairs={{0,8},{1,9},{2,10},{3,11},{4,12},{5,13},{6,14},{7,15},{8,0},{9,1},... | collective-permute-start | bytes 3538952 | tf_op jit(solution)/shard_map/ppermute | solution.py:48
  252.2 3.3 copy-start.14
  253.4 2.6 collective-permute-start.11
  254.0 2.0 copy-start.11
  254.0 72.1 %collective-permute-start.19 = (bf16[256,768]{1,0:T(8,128)(2,1)S(1)}, bf16[256,768]{1,0:T(8,128)(2,1)S(1)}, u32[]{:S(2)}, u32[]{:S(2)}) collective-permute-start(bf16[256,768]{1,0:T(8,128)(2,1)S(1)} %convert_element_type.353), channel_id=1, source_target_pairs={{4,0},{5,1},{6,2},{7,3},{12,8},{13,9},{14,10},{15,11},{20,16},{21,... | collective-permute-start | bytes 1179656 | tf_op jit(solution)/shard_map/ppermute | solution.py:52
  256.2 15.7 %collective-permute-start.14 = (bf16[8,24,1536]{2,1,0:T(8,128)(2,1)S(1)}, bf16[8,24,1536]{2,1,0:T(8,128)(2,1)S(1)}, u32[]{:S(2)}, u32[]{:S(2)}) collective-permute-start(bf16[8,24,1536]{2,1,0:T(8,128)(2,1)S(1)} %fusion.2), channel_id=1, source_target_pairs={{0,1},{1,0},{2,3},{3,2},{4,5},{5,4},{6,7},{7,6},{8,9},{9,8},{10,11... | collective-permute-start | bytes 1769480 | tf_op jit(solution)/shard_map/ppermute | solution.py:48
  257.9 11.2 %collective-permute-start.13 = (bf16[8,32,768]{2,1,0:T(8,128)(2,1)S(1)}, bf16[8,32,768]{2,1,0:T(8,128)(2,1)S(1)}, u32[]{:S(2)}, u32[]{:S(2)}) collective-permute-start(bf16[8,32,768]{2,1,0:T(8,128)(2,1)S(1)} %bitcast.190), channel_id=1, source_target_pairs={{0,16},{1,17},{2,18},{3,19},{4,20},{5,21},{6,22},{7,23},{8,24},{9,... | collective-permute-start | bytes 1179656 | tf_op jit(solution)/shard_map/ppermute | solution.py:48
  272.0 13.6 %collective-permute-start.16 = (bf16[4,24,1536]{2,1,0:T(8,128)(2,1)S(1)}, bf16[4,24,1536]{2,1,0:T(8,128)(2,1)S(1)}, u32[]{:S(2)}, u32[]{:S(2)}) collective-permute-start(bf16[4,24,1536]{2,1,0:T(8,128)(2,1)S(1)} %bitcast.195), channel_id=1, source_target_pairs={{0,16},{1,17},{2,18},{3,19},{4,20},{5,21},{6,22},{7,23},{8,24},{9,... | collective-permute-start | bytes 884744 | tf_op jit(solution)/shard_map/ppermute | solution.py:48
  272.8 7.6 %collective-permute-start.15 = (bf16[4,32,768]{2,1,0:T(8,128)(2,1)S(1)}, bf16[4,32,768]{2,1,0:T(8,128)(2,1)S(1)}, u32[]{:S(2)}, u32[]{:S(2)}) collective-permute-start(bf16[4,32,768]{2,1,0:T(8,128)(2,1)S(1)} %fusion.4), channel_id=1, source_target_pairs={{0,1},{1,0},{2,3},{3,2},{4,5},{5,4},{6,7},{7,6},{8,9},{9,8},{10,11... | collective-permute-start | bytes 589832 | tf_op jit(solution)/shard_map/ppermute | solution.py:48
  285.7 57.1 %collective-permute-start.18 = (bf16[2,24,1536]{2,1,0:T(8,128)(2,1)S(1)}, bf16[2,24,1536]{2,1,0:T(8,128)(2,1)S(1)}, u32[]{:S(2)}, u32[]{:S(2)}) collective-permute-start(bf16[2,24,1536]{2,1,0:T(8,128)(2,1)S(1)} %bitcast.199), channel_id=1, source_target_pairs={{0,4},{1,5},{2,6},{3,7},{4,0},{5,1},{6,2},{7,3},{8,12},{9,13},{10,... | collective-permute-start | bytes 442376 | tf_op jit(solution)/shard_map/ppermute | solution.py:48
  325.9 19.2 %copy-start.4 = (f32[256,768]{1,0:T(8,128)S(1)}, f32[256,768]{1,0:T(8,128)}, u32[]{:S(2)}) copy-start(f32[256,768]{1,0:T(8,128)} %fusion) | copy-start | bytes 2359300
  325.9 19.2 %copy-start.13 = (f32[256,768]{1,0:T(8,128)S(1)}, f32[256,768]{1,0:T(8,128)}, u32[]{:S(2)}) copy-start(f32[256,768]{1,0:T(8,128)} %get-tuple-element.97) | copy-start | bytes 2359300
  326.1 16.7 %collective-permute-start.17 = (bf16[2,32,768]{2,1,0:T(8,128)(2,1)S(1)}, bf16[2,32,768]{2,1,0:T(8,128)(2,1)S(1)}, u32[]{:S(2)}, u32[]{:S(2)}) collective-permute-start(bf16[2,32,768]{2,1,0:T(8,128)(2,1)S(1)} %bitcast.202), channel_id=1, source_target_pairs={{0,4},{1,5},{2,6},{3,7},{4,0},{5,1},{6,2},{7,3},{8,12},{9,13},{10,... | collective-permute-start | bytes 294920 | tf_op jit(solution)/shard_map/ppermute | solution.py:48
  342.8 6.8 %collective-permute-start.21 = (bf16[1,24,1536]{2,1,0:T(8,128)(2,1)S(1)}, bf16[1,24,1536]{2,1,0:T(8,128)(2,1)S(1)}, u32[]{:S(2)}, u32[]{:S(2)}) collective-permute-start(bf16[1,24,1536]{2,1,0:T(8,128)(2,1)S(1)} %add_convert_fusion.7), channel_id=1, source_target_pairs={{0,2},{1,3},{2,0},{3,1},{4,6},{5,7},{6,4},{7,5},{8,10},{9,11},{10,... | collective-permute-start | bytes 221192 | tf_op jit(solution)/shard_map/ppermute | solution.py:48
  343.0 4.8 %collective-permute-start.20 = (bf16[1,32,768]{2,1,0:T(8,128)(2,1)S(1)}, bf16[1,32,768]{2,1,0:T(8,128)(2,1)S(1)}, u32[]{:S(2)}, u32[]{:S(2)}) collective-permute-start(bf16[1,32,768]{2,1,0:T(8,128)(2,1)S(1)} %add_convert_fusion.8), channel_id=1, source_target_pairs={{0,2},{1,3},{2,0},{3,1},{4,6},{5,7},{6,4},{7,5},{8,10},{9,11},{10,... | collective-permute-start | bytes 147464 | tf_op jit(solution)/shard_map/ppermute | solution.py:48
  360.3 2.3 copy-start.10
Sparse Core Ops, SparseCore 0:
  16.2 121.8 all-gather.1
  182.4 177.8 reduce-scatter.1

commit v7 on v6

--- a/solution.py
+++ b/solution.py
@@ -21,7 +21,8 @@
 INV_ROOT_TAU = 0.3989422804014327
 AXES = ("grp", "row")
 WIDE = 4
-WO, WI, WQ, WK, WV = 4, 5, 9, 10, 11
+WO, WI = 4, 5
+WQ, WK, WV = 0, 1, 2
 
 
 def mm(left, right):
@@ -200,14 +201,57 @@
     return lax.dot_general(left, right, (((0,), (0,)), ((), ())), preferred_element_type=F32)
 
 
-def attention_kernel(blocks, first, rows, *refs):
+def pack_kernel(wo_ref, wi_ref, wu_ref, wq_ref, wk_ref, wv_ref, line_ref, early_ref, late_ref):
+    step, width = wo_ref.shape
+    early_ref[:step, :] = wq_ref[...]
+    early_ref[step : step + 8, :] = line_ref[:8, :]
+    early_ref[step + 8 : 2 * step + 8, :] = wk_ref[...]
+    early_ref[2 * step + 8 :, :] = wv_ref[...]
+    late_ref[: WIDE * step, :] = wu_ref[...]
+    late_ref[WO * step : WI * step, :] = wo_ref[...]
+    for i in range(WIDE):
+        late_ref[(WI + i) * step : (WI + i + 1) * step, :] = wi_ref[:, i * width : (i + 1) * width]
+    late_ref[(WI + WIDE) * step :, :] = line_ref[8:, :]
+
+
+def pack_call(w_output, w_inner, w_outer, w_query, w_key, w_value, line):
+    step, width = w_output.shape
+    shape = lambda rows: jax.ShapeDtypeStruct((rows, width), BF)
+    return pl.pallas_call(
+        pack_kernel, out_shape=[shape(3 * step + 8), shape((WI + WIDE) * step + 8)], name="pack"
+    )(w_output, w_inner, w_outer, w_query, w_key, w_value, line)
+
+
+def attention_kernel(blocks, first, rows, places, *refs):
     spots = refs[:blocks]
-    (near_ref, own_ref, wq_ref, wk_ref, wv_ref, bq_ref, bv_ref, segq_ref, segk_ref,
-     q_ref, kp_ref, vp_ref, kn_ref, vn_ref, ctx_ref, lse_ref, x_ref, s_ref, sems) = refs[blocks:]
+    (near_ref, me_ref, own_ref, a0_ref, a1_ref, b0_ref, b1_ref, segq_ref, segk_ref,
+     w_ref, q_ref, kp_ref, vp_ref, kn_ref, vn_ref, ctx_ref, lse_ref,
+     x_ref, s_ref, line_ref, bias_ref, sems, w_sems) = refs[blocks:]
     near = near_ref[0]
     at = lambda b: pl.ds(pl.multiple_of(b * rows, rows), rows)
     depth = own_ref.shape[1]
-    wq, wk, wv = [ref[...].reshape(depth, -1) for ref in (wq_ref, wk_ref, wv_ref)]
+    owners = w_ref.shape[0]
+    each = depth // owners
+    part = q_ref.shape[1]
+
+    def weights(act):
+        @pl.loop(0, owners)
+        def _(e):
+            away = e ^ me_ref[0]
+            for (bits, half), (zero, one), parts in (
+                (places[0], (a0_ref, a1_ref), ((0, each, w_ref, 0), (each, 8, line_ref, 0))),
+                (places[1], (b0_ref, b1_ref), ((0, 2 * each, w_ref, each),)),
+            ):
+                j = sum([((away // bit) & 1) * weight for bit, weight in bits])
+                for which, source in enumerate((zero, one)):
+
+                    @pl.when(((away // half) & 1) == which)
+                    def _():
+                        for k, (top, size, target, base) in enumerate(parts):
+                            act(pltpu.make_async_copy(
+                                source.at[j, pl.ds(top, size)], target.at[e, pl.ds(base, size)],
+                                w_sems.at[2 * k if zero is a0_ref else 1, e],
+                            ))
 
     @pl.when(pl.program_id(0) == 0)
     def _():
@@ -215,18 +259,32 @@
             pltpu.make_async_copy(spot, x_ref.at[pl.ds(i * rows, rows)], sems.at[i])
             for i, spot in enumerate(spots)
         ]
+        weights(lambda c: c.start())
         for copy in copies:
             copy.start()
+        weights(lambda c: c.wait())
         for copy in copies:
             copy.wait()
-
-    queries = (mm(own_ref[...], wq) + bq_ref[...]) * (HDIM**-0.5)
+        line = line_ref[:, 0, :128]
+        place = lax.broadcasted_iota(jnp.int32, (128, depth), 0)
+        lane = lax.broadcasted_iota(jnp.int32, (128, depth), 1)
+        mine = lax.broadcasted_iota(jnp.int32, (owners, depth), 0)
+        mine = mine == lax.broadcasted_iota(jnp.int32, (owners, depth), 1) // each
+        for i in range(2):
+            spread = mm(line, jnp.where(place == lane % each + i * each, 1.0, 0.0).astype(BF))
+            bias_ref[i : i + 1, :] = jnp.sum(jnp.where(mine, spread, 0.0), axis=0, keepdims=True)
+
+    lanes = pl.ds(pl.multiple_of(pl.program_id(0) * part, part), part)
+    wq, wk, wv = [
+        w_ref[:, i * each : (i + 1) * each, lanes].reshape(depth, part) for i in (WQ, WK, WV)
+    ]
+    queries = (mm(own_ref[...], wq) + bias_ref[0:1, lanes]) * (HDIM**-0.5)
     q_ref[...] = queries.astype(BF)
 
     def project(b, k_ref, v_ref, side):
         x = x_ref[at(b), :]
         k_ref[at(side), :] = mm(x, wk).astype(BF)
-        v_ref[at(side), :] = (mm(x, wv) + bv_ref[...]).astype(BF)
+        v_ref[at(side), :] = (mm(x, wv) + bias_ref[1:2, lanes]).astype(BF)
 
     @pl.loop(0, first)
     def _(b):
@@ -278,7 +336,7 @@
         lse_ref[0, h : h + 1, :] = peaks[h] + jnp.log(totals[h])
 
 
-def attention_call(spots, first, near, own, got, bq, bv, segq, segk):
+def attention_call(spots, first, near, me, own, pieces, places, segq, segk):
     rows, width = own.shape
     blocks = len(spots)
     tall = blocks * rows
@@ -287,24 +345,27 @@
     heads = part // HDIM
     cols = lambda depth: pl.BlockSpec((depth, part), lambda g: (0, g))
     flops = 2 * tall * width * width * 2 + 4 * tall * rows * width * 4
-    owners, each = got.shape[0], width // got.shape[0]
-    weight = lambda place: pl.BlockSpec((owners, each, part), lambda g: (0, place, g))
+    owners = 2 * pieces[0].shape[0]
+    each = width // owners
     return pl.pallas_call(
-        functools.partial(attention_kernel, blocks, first, rows),
+        functools.partial(attention_kernel, blocks, first, rows, places),
         grid=(steps,),
         in_specs=[pl.BlockSpec(memory_space=pl.ANY)] * blocks
         + [
             pl.BlockSpec(memory_space=pltpu.SMEM),
+            pl.BlockSpec(memory_space=pltpu.SMEM),
             pl.BlockSpec((rows, width), lambda g: (0, 0)),
-            weight(WQ), weight(WK), weight(WV), cols(1), cols(1),
+        ] + [pl.BlockSpec(memory_space=pl.ANY)] * 4 + [
             pl.BlockSpec((1, rows), lambda g: (0, 0)),
             pl.BlockSpec(segk.shape, lambda g: (0, 0)),
         ],
         out_specs=[
+            pl.BlockSpec((owners, 3 * each, width), lambda g: (0, 0, 0)),
             cols(rows), cols(PROMPT), cols(PROMPT), cols(tall - PROMPT), cols(tall - PROMPT),
             cols(rows), pl.BlockSpec((1, 8, rows), lambda g: (g, 0, 0)),
         ],
         out_shape=[
+            jax.ShapeDtypeStruct((owners, 3 * each, width), BF),
             jax.ShapeDtypeStruct((rows, width), BF),
             jax.ShapeDtypeStruct((PROMPT, width), BF),
             jax.ShapeDtypeStruct((PROMPT, width), BF),
@@ -316,14 +377,17 @@
         scratch_shapes=[
             pltpu.VMEM((tall, width), BF),
             pltpu.VMEM((heads, tall, rows), F32),
+            pltpu.VMEM((owners, 8, width), BF),
+            pltpu.VMEM((8, width), F32),
             pltpu.SemaphoreType.DMA((blocks,)),
+            pltpu.SemaphoreType.DMA((3, owners)),
         ],
         compiler_params=pltpu.CompilerParams(vmem_limit_bytes=60 * 2**20),
         cost_estimate=pl.CostEstimate(
             flops=flops, bytes_accessed=12 * 2**20, transcendentals=tall * rows * 12
         ),
         name="attention",
-    )(*spots, near, own, got, got, got, bq, bv, segq, segk)
+    )(*spots, near, me, own, *pieces, segq, segk)
 
 
 def halves(value, runs, core):
@@ -715,43 +779,79 @@
         _, rows, width = tokens.shape
         step = w_query.shape[0]
         wide = w_inner.shape[1] // width
-        row = lax.axis_index("row")
-        scale = HDIM ** (-0.5)
         own = tokens[0]
 
-        vectors = (
-            bias_query, bias_value, bias_output, gain_first, shift_first, bias_outer, gain_second,
-            shift_second, bias_inner,
-        )
-        small = len(vectors) - 1
-        line, place = 0, 0
-        for vector in vectors:
-            size = vector.shape[0]
-            line = line + jnp.pad(vector, (place, width - place - size))
-            place += size
-        line = jnp.pad(line[None], ((0, 7), (0, 0)))
-        inner_rows = [w_inner[:, i * width : (i + 1) * width] for i in range(wide)]
-        pack = jnp.concatenate([w_outer, w_output, *inner_rows, w_query, w_key, w_value, line], 0)
-        got = lax.all_gather(pack, AXES, axis=0, tiled=True).reshape(count, -1, width)
-        lines = got[:, 12 * step]
-        if step % 8:
+        early = (bias_query, bias_value)
+        late = (bias_output, gain_first, shift_first, bias_outer, gain_second, shift_second, bias_inner)
+        small = len(late) - 1
+
+        def in_line(vectors):
+            line, place = 0, 0
+            for vector in vectors:
+                size = vector.shape[0]
+                line = line + jnp.pad(vector, (place, width - place - size))
+                place += size
+            return jnp.pad(line[None], ((0, 7), (0, 0)))
+
+        line = jnp.concatenate([in_line(early), in_line(late)], 0)
+        runs = plan.grp
+        grp, row = lax.axis_index("grp"), lax.axis_index("row")
+        core = (grp % 2).astype(jnp.int32).reshape(1)
+        exchange = Tokens(plan, own)
+        squares = (w_query, w_key, w_value)
+        if step % 8 == 0:
+            first_pack, pack = pack_call(w_output, w_inner, w_outer, *squares, line)
+            got = lax.all_gather(pack, AXES, axis=0, tiled=True).reshape(count, -1, width)
+            lines = got[:, (WI + WIDE) * step]
+
+            def swaps(value, bits):
+                masks = [0]
+                for bit in bits:
+                    masks = masks + [m ^ bit for m in masks]
+                return [plan.swap(value, m) for m in masks[1:]]
+
+            def stage(held, bit):
+                return jnp.concatenate([held, plan.swap(held, bit)], 0)
+
+            away = swaps(first_pack, plan.z)
+            *away, same, beside = tie(*away, *exchange.stage_one())
+            exchange.same, exchange.beside = same, beside
+            cut = step + 8
+            one = jnp.stack([v[:cut] for v in (first_pack, *away)])
+            two = jnp.stack([v[cut:] for v in (first_pack, *away)])
+            one, two = stage(one, plan.y[0]), stage(two, plan.x[0])
+            one, two, *seen = tie(one, two, *exchange.stage_two())
+            exchange.other, exchange.same_y, exchange.diagonal = seen
+            one, two = stage(one, plan.x[0]), stage(two, plan.y[0])
+            exchange.stage_three()
+            one, two, exchange.other_y = tie(one, two, exchange.other_y)
+            pieces = [one, plan.swap(one, plan.core[0]), two, plan.swap(two, plan.core[0])]
+            order = lambda *bits: ([(bit, 1 << i) for i, bit in enumerate(bits)], plan.core[0])
+            places = (
+                order(*plan.z, plan.y[0], plan.x[0]),
+                order(*plan.z, plan.x[0], plan.y[0]),
+            )
+            me = plan.me().astype(jnp.int32).reshape(1)
+        else:
+            inner_rows = [w_inner[:, i * width : (i + 1) * width] for i in range(wide)]
+            pack = jnp.concatenate([w_outer, w_output, *inner_rows, *squares, line], 0)
+            got = lax.all_gather(pack, AXES, axis=0, tiled=True).reshape(count, -1, width)
+            lines = got[:, 12 * step + 8]
             cuts = [wide * step, (wide + 1) * step, (2 * wide + 1) * step, 12 * step]
-            outer, output, inner, rest, _ = jnp.split(got, cuts, axis=1)
+            outer, output, inner, rest, marks = jnp.split(got, cuts, axis=1)
             apart = lambda v, n: v.reshape(count, n, step, width).transpose(1, 0, 2, 3)
             inner, rest = [
                 v.reshape(v.shape[0], 32, width // 32, width).transpose(1, 0, 2, 3)
                 for v in (apart(inner, wide), apart(rest, 3))
             ]
-            got = jnp.concatenate(
-                [v.reshape(32, -1, width) for v in (outer, output, inner, rest)], 1
-            )
-        runs = plan.grp
-        core = (lax.axis_index("grp") % 2).astype(jnp.int32).reshape(1)
-
-        exchange = Tokens(plan, own)
-        exchange.stage_one()
-        exchange.stage_two()
-        exchange.stage_three()
+            got = jnp.concatenate([v.reshape(32, -1, width) for v in (outer, output, inner)], 1)
+            pairs = marks[:, 0, : 2 * step].reshape(32, count // 32, 2, step).transpose(0, 2, 1, 3)
+            pairs = jnp.pad(pairs.reshape(32, 1, -1), ((0, 0), (0, 7), (0, width - 2 * width // 32)))
+            one = jnp.concatenate([rest[:, 0], pairs], 1)
+            two = rest[:, 1:].reshape(32, -1, width)
+            pieces = [one[:16], one[16:], two[:16], two[16:]]
+            places = (([(1, 1), (2, 2), (4, 4), (8, 8)], 16),) * 2
+            me = jnp.zeros((1,), jnp.int32)
         spots, near = exchange.spots()
         first_near = PROMPT // rows
 
@@ -764,10 +864,10 @@
         seg_near = near_segments(plan, segments, rows)[:, None]
         near = near.astype(jnp.int32).reshape(1)
 
-        queries, keys_p, values_p, keys_n, values_n, context, log_total = attention_call(
-            spots, first_near, near, own, got, table[0:1], table[1:2], seg_own, seg_near
+        squares, queries, keys_p, values_p, keys_n, values_n, context, log_total = attention_call(
+            spots, first_near, near, me, own, pieces, places, seg_own, seg_near
         )
-        vec = jnp.concatenate([table[2:], jnp.zeros((2, width), F32)], 0)
+        vec = jnp.concatenate([table, jnp.zeros((2, width), F32)], 0)
         layer_out, grad_h1, grad_context, grads, sums, sums_bin = middle_call(
             context, own, cotangent[0], got, vec, v_bin
         )
@@ -783,19 +883,19 @@
             0, parts, first_near, near, grad_context, context, queries, keys_p, values_p, log_total,
             seg_own, seg_near,
         )
-        shared_p = product_call(first_near, near, dkp, dvp, got, rows)
+        shared_p = product_call(first_near, near, dkp, dvp, squares, rows)
         returned = Return(plan, rows)
         returned.prompt_one(shared_p)
         dkn, dvn, dq = back_call(
             0, parts, None, near, grad_context, context, queries, keys_n, values_n, log_total,
             seg_own, seg_near, dqp,
         )
-        shared_n = product_call(None, near, dkn, dvn, got, rows)
+        shared_n = product_call(None, near, dkn, dvn, squares, rows)
         returned.same, shared_n, dq = tie(returned.same, shared_n, dq)
         returned.prompt_two()
         returned.near(shared_n)
         q_send, q_keep, kv_send, kv_keep, grad_own, sums_qkv = weight_call(
-            spots, first_near, near, own, dq, got, grad_h1, dkp, dvp, dkn, dvn, core, runs
+            spots, first_near, near, own, dq, squares, grad_h1, dkp, dvp, dkn, dvn, core, runs
         )
         q_send, q_keep, kv_send, kv_keep, returned.same, returned.own = tie(
             q_send, q_keep, kv_send, kv_keep, returned.same, returned.own
@@ -803,6 +903,7 @@
         returned.prompt_three()
 
         order = (6, 5, 3, 4, 2, 0, 1)
+        small = len(early) + len(late) - 1
         d_table = jnp.concatenate([sums_qkv[:1]] + [sums[i : i + 1] for i in order], 0)
         d_lines = jnp.concatenate(
             [

time: 372 us -> 367 us (0.987)
  waiting for transfers between devices: 149 us -> 126 us
  starting transfers between devices: 81.5 us -> 99.8 us
  local copies, waits for them, and re-layouts: 25.5 us -> 19.1 us
  Pallas kernels: 89 us -> 94.1 us
    all_gather x1, waiting for transfers between devices: 77.1 us -> 0.02 us  [per_device(): lax.all_gather(pack, AXES, axis=0, tiled=True).reshape(count, -1, width)]
    ppermute x18 -> x27, waiting for transfers between devices: 53.9 us -> 105 us  [swap(): return lax.ppermute(value, AXES, [(i, i ^ mask) for i in range(self.count)])]
    ppermute x18 -> x27, starting transfers between devices: 72.7 us -> 92.3 us  [swap(): return lax.ppermute(value, AXES, [(i, i ^ mask) for i in range(self.count)])]
    unnamed x53 -> x56, local copies, waits for them, and re-layouts: 11.2 us -> 4.97 us
    pallas_call x1 -> x2, Pallas kernels: 18.9 us -> 24 us  [the longest x1 22.1 us: attention_call(): pl.pallas_call(functools.partial(attention_kernel, blocks, first, rows, p...]
  transfers between devices with their start and end apart: 24 -> 33, of which waited for: 12 -> 17; matrix products, arithmetic and copies ran while one was open for 6% -> 6% of each run, Pallas kernels for 14% -> 20%
where the time goes in v7:
time: 367 us; the launch traced here: 366 us
  waiting for transfers between devices  126 us (34%)
  starting transfers between devices  99.8 us (27%)
  Pallas kernels  94.1 us (26%)
  local copies, waits for them, and re-layouts  19.1 us (5%)
  between operations  14.8 us (4%)
  other arithmetic  12.4 us (3%)
    ppermute x27, waiting for transfers between devices, swap(): return lax.ppermute(value, AXES, [(i, i ^ mask) for i in range(self.count)])  105 us
    ppermute x27, starting transfers between devices, swap(): return lax.ppermute(value, AXES, [(i, i ^ mask) for i in range(self.count)])  92.3 us
    pallas_call x2, Pallas kernels, back_call(): pl.pallas_call(functools.partial(back_kernel, rows, bound, dq0 is not Non...  24.2 us
    pallas_call x1, Pallas kernels, attention_call(): pl.pallas_call(functools.partial(attention_kernel, blocks, first, rows, p...  22.1 us
    pallas_call x1, Pallas kernels, middle_call(): pl.pallas_call(functools.partial(middle_kernel, wide), grid=(2 * wide,),...  19.8 us
    pallas_call x1, Pallas kernels, weight_call(): pl.pallas_call(functools.partial(weight_kernel, blocks, first, rows, runs...  15.2 us
    ppermute x4, waiting for transfers between devices, send(): return lax.ppermute(value, AXES, pairs)  12.6 us
    pallas_call x2, Pallas kernels, product_call(): pl.pallas_call(functools.partial(product_kernel, rows, bound), grid=(tall...  10.9 us
  transfers between devices with their start and end apart: 33, of which 17 were waited for; matrix products, arithmetic and copies ran while one was open for 6% of the time, Pallas kernels for 20%

profile of v7, /device:TPU:0, one launch (start us, length us, event | category | flops | bytes accessed | tf_op | source)
XLA Modules:
  0.0 366.3 jit_solution(9500218524680081911)
XLA Ops:
  9.5 1.8 pack.1
  11.4 3.1 collective-permute-start
  14.5 2.6 collective-permute-start.1
  17.1 3.8 %collective-permute-start.3 = (bf16[256,768]{1,0:T(8,128)(2,1)}, bf16[256,768]{1,0:T(8,128)(2,1)S(1)}, u32[]{:S(2)}, u32[]{:S(2)}) collective-permute-start(bf16[256,768]{1,0:T(8,128)(2,1)} %bitcast.163), channel_id=1, source_target_pairs={{0,4},{1,5},{2,6},{3,7},{8,12},{9,13},{10,14},{11,15},{16,20},{17,... | collective-permute-start | bytes 1179656 | tf_op jit(solution)/shard_map/ppermute | solution.py:53
  20.9 1.6 collective-permute-start.4
  25.9 12.6 %collective-permute-done.3 = bf16[256,768]{1,0:T(8,128)(2,1)S(1)} collective-permute-done((bf16[256,768]{1,0:T(8,128)(2,1)}, bf16[256,768]{1,0:T(8,128)(2,1)S(1)}, u32[]{:S(2)}, u32[]{:S(2)}) %collective-permute-start.3) | collective-permute-done | bytes 393248 | tf_op jit(solution)/shard_map/ppermute | solution.py:53
  39.3 16.1 %collective-permute-start.7 = (bf16[256,768]{1,0:T(8,128)(2,1)S(1)}, bf16[256,768]{1,0:T(8,128)(2,1)S(1)}, u32[]{:S(2)}, u32[]{:S(2)}) collective-permute-start(bf16[256,768]{1,0:T(8,128)(2,1)S(1)} %broadcast_select_fusion.refs_0_), channel_id=1, source_target_pairs={{0,2},{1,3},{2,0},{3,1},{4,6},{5,7},{6,4},{7,5},{8,10},{9,11},{10,... | collective-permute-start | bytes 1179656 | tf_op jit(solution)/shard_map/ppermute | solution.py:49
  55.4 1.2 collective-permute-start.8
  56.7 1.6 collective-permute-start.6
  58.9 10.8 %collective-permute-done.5 = bf16[4,32,768]{2,1,0:T(8,128)(2,1)S(1)} collective-permute-done((bf16[4,32,768]{2,1,0:T(8,128)(2,1)S(1)}, bf16[4,32,768]{2,1,0:T(8,128)(2,1)S(1)}, u32[]{:S(2)}, u32[]{:S(2)}) %collective-permute-start.5) | collective-permute-done | bytes 196640 | tf_op jit(solution)/shard_map/ppermute | solution.py:49
  69.7 5.6 %collective-permute-done.7.refs_1_ = bf16[256,768]{1,0:T(8,128)(2,1)S(1)} collective-permute-done((bf16[256,768]{1,0:T(8,128)(2,1)S(1)}, bf16[256,768]{1,0:T(8,128)(2,1)S(1)}, u32[]{:S(2)}, u32[]{:S(2)}) %collective-permute-start.7) | collective-permute-done | bytes 393248 | tf_op jit(solution)/shard_map/ppermute | solution.py:49
  75.3 1.1 collective-permute-start.11
  76.4 1.9 collective-permute-start.10
  78.9 12.0 %collective-permute-done.10 = bf16[8,32,768]{2,1,0:T(8,128)(2,1)S(1)} collective-permute-done((bf16[8,32,768]{2,1,0:T(8,128)(2,1)S(1)}, bf16[8,32,768]{2,1,0:T(8,128)(2,1)S(1)}, u32[]{:S(2)}, u32[]{:S(2)}) %collective-permute-start.10) | collective-permute-done | bytes 393248 | tf_op jit(solution)/shard_map/ppermute | solution.py:49
  91.0 7.2 %collective-permute-done.11 = bf16[8,48,768]{2,1,0:T(8,128)(2,1)S(1)} collective-permute-done((bf16[8,48,768]{2,1,0:T(8,128)(2,1)S(1)}, bf16[8,48,768]{2,1,0:T(8,128)(2,1)S(1)}, u32[]{:S(2)}, u32[]{:S(2)}) %collective-permute-start.11) | collective-permute-done | bytes 589856 | tf_op jit(solution)/shard_map/ppermute | solution.py:49
  98.4 13.9 %collective-permute-done.12.refs_3_ = bf16[256,768]{1,0:T(8,128)(2,1)S(1)} collective-permute-done((bf16[256,768]{1,0:T(8,128)(2,1)S(1)}, bf16[256,768]{1,0:T(8,128)(2,1)S(1)}, u32[]{:S(2)}, u32[]{:S(2)}) %collective-permute-start.12) | collective-permute-done | bytes 393248 | tf_op jit(solution)/shard_map/ppermute | solution.py:49
  114.7 1.4 collective-permute-done.13.refs_11_
  117.3 22.1 %attention.1 = (bf16[32,72,768]{2,1,0:T(8,128)(2,1)}, bf16[256,768]{1,0:T(8,128)(2,1)}, bf16[1024,768]{1,0:T(8,128)(2,1)}, bf16[1024,768]{1,0:T(8,128)(2,1)}, bf...) custom-call(bf16[256,768]{1,0:T(8,128)(2,1)} %copy-done.10, ...), custom_call_target="tpu_custom_call" | custom-call | flops 9865003008 | bytes 12582912 | tf_op jit(solution)/shard_map/attention/pallas_call | solution.py:350
  139.4 1.1 slice.234
  141.7 19.8 %middle.1 = (bf16[256,768]{1,0:T(8,128)(2,1)}, f32[256,768]{1,0:T(8,128)}, bf16[256,768]{1,0:T(8,128)(2,1)}, bf16[32,216,768]{2,1,0:T(8,128)(2,1)}, f32[8,768]{1,0:T(8,128)}, /*index=5*/f32[8,768]{1,0:T(8,128)}) custom-call(bf16[256,768]{1,0:T(8,128)(2,1)} %get-tuple-element.110.ctx_ref.refs_2_, bf16[256,768]{1,0:T(8,128)(2,1)} %bitcast.167, ...), custom_call_target="tpu_custom_call" | custom-call | flops 8153726976 | bytes 33554432 | tf_op jit(solution)/shard_map/middle/pallas_call | solution.py:530
  161.5 18.6 %attention_back.2 = (bf16[1024,768]{1,0:T(8,128)(2,1)}, bf16[1024,768]{1,0:T(8,128)(2,1)}, f32[768,256]{1,0:T(8,128)}) custom-call(s32[1]{0:T(128)} %bitcast.9.refs_7_.refs_0_.near_ref, bf16[256,768]{1,0:T(8,128)(2,1)} %get-tuple-element.113.refs_1_, bf16[256,768]{1,0:T(8,128)(2,1)} %get-tuple-element.110.ctx_ref.refs_2_, ...), custom_call_target="tpu_custom_call" | custom-call | flops 16106127360 | bytes 6291456 | tf_op jit(solution)/shard_map/attention_back/pallas_call | solution.py:624
  180.1 6.5 %token_product.2 = bf16[4,256,768]{2,1,0:T(8,128)(2,1)} custom-call(s32[1]{0:T(128)} %bitcast.9.refs_7_.refs_0_.near_ref, bf16[1024,768]{1,0:T(8,128)(2,1)} %get-tuple-element.118.dk_ref.refs_13_, bf16[1024,768]{1,0:T(8,128)(2,1)} %get-tuple-element.119.dv_ref.refs_14_, bf16[32,72,768]{2,1,0:T(8,128)(2,1)} %get-tuple-element.120.wk_ref.wv_ref.refs_11_, ...), custom_call_target="tpu_custom_call" | custom-call | flops 2415919104 | bytes 4718592 | tf_op jit(solution)/shard_map/token_product/pallas_call | solution.py:657
  186.6 1.2 slice_bitcast_fusion
  187.8 2.0 collective-permute-start.15
  189.9 5.6 %attention_back.3 = (bf16[768,768]{1,0:T(8,128)(2,1)}, bf16[768,768]{1,0:T(8,128)(2,1)}, f32[768,256]{1,0:T(8,128)}) custom-call(s32[1]{0:T(128)} %bitcast.9.refs_7_.refs_0_.near_ref, bf16[256,768]{1,0:T(8,128)(2,1)} %get-tuple-element.113.refs_1_, bf16[256,768]{1,0:T(8,128)(2,1)} %get-tuple-element.110.ctx_ref.refs_2_, ...), custom_call_target="tpu_custom_call" | custom-call | flops 12079595520 | bytes 4718592 | tf_op jit(solution)/shard_map/attention_back/pallas_call | solution.py:624
  195.5 4.5 %token_product.3 = bf16[3,256,768]{2,1,0:T(8,128)(2,1)} custom-call(s32[1]{0:T(128)} %bitcast.9.refs_7_.refs_0_.near_ref, bf16[768,768]{1,0:T(8,128)(2,1)} %get-tuple-element.124.dk_ref.refs_15_, bf16[768,768]{1,0:T(8,128)(2,1)} %get-tuple-element.125.dv_ref.refs_16_, bf16[32,72,768]{2,1,0:T(8,128)(2,1)} %get-tuple-element.120.wk_ref.wv_ref.refs_11_, ...), custom_call_target="tpu_custom_call" | custom-call | flops 1811939328 | bytes 3538944 | tf_op jit(solution)/shard_map/token_product/pallas_call | solution.py:657
  201.3 6.3 %collective-permute-done.16 = bf16[256,768]{1,0:T(8,128)(2,1)} collective-permute-done((bf16[256,768]{1,0:T(8,128)(2,1)S(1)}, bf16[256,768]{1,0:T(8,128)(2,1)}, u32[]{:S(2)}, u32[]{:S(2)}) %collective-permute-start.16) | collective-permute-done | bytes 393248 | tf_op jit(solution)/shard_map/ppermute | solution.py:49
  207.6 1.3 fusion.1
  209.0 1.8 collective-permute-start.18
  210.8 1.4 collective-permute-start.19
  212.2 15.2 %weight_product.1 = (bf16[16,24,768]{2,1,0:T(8,128)(2,1)}, bf16[16,24,768]{2,1,0:T(8,128)(2,1)}, bf16[16,24,1536]{2,1,0:T(8,128)(2,1)}, bf16[16,24,1536]{2,1,0:T...) custom-call(bf16[256,768]{1,0:T(8,128)(2,1)} %copy-done.10, bf16[256,768]{1,0:T(8,128)(2,1)} %copy-done.18, ...), custom_call_target="tpu_custom_call" | custom-call | flops 4227858432 | bytes 16515072 | tf_op jit(solution)/shard_map/weight_product/pallas_call | solution.py:735
  227.5 2.0 fusion
  231.8 1.2 pad_maximum_fusion.3
  233.6 1.4 collective-permute-start.28
  235.8 1.4 collective-permute-start.23
  237.2 1.2 add_convert_fusion.2
  238.4 2.0 collective-permute-start.22
  241.6 16.1 %collective-permute-done.22 = bf16[8,32,768]{2,1,0:T(8,128)(2,1)S(1)} collective-permute-done((bf16[8,32,768]{2,1,0:T(8,128)(2,1)S(1)}, bf16[8,32,768]{2,1,0:T(8,128)(2,1)S(1)}, u32[]{:S(2)}, u32[]{:S(2)}) %collective-permute-start.22) | collective-permute-done | bytes 393248 | tf_op jit(solution)/shard_map/ppermute | solution.py:49
  257.8 3.2 collective-permute-done.23
  261.1 2.6 collective-permute-start.25
  264.5 5.7 %collective-permute-done.24 = bf16[4,32,768]{2,1,0:T(8,128)(2,1)S(1)} collective-permute-done((bf16[4,32,768]{2,1,0:T(8,128)(2,1)S(1)}, bf16[4,32,768]{2,1,0:T(8,128)(2,1)S(1)}, u32[]{:S(2)}, u32[]{:S(2)}) %collective-permute-start.24) | collective-permute-done | bytes 196640 | tf_op jit(solution)/shard_map/ppermute | solution.py:49
  270.2 2.3 collective-permute-done.25
  272.7 48.2 %collective-permute-start.27 = (bf16[2,24,1536]{2,1,0:T(8,128)(2,1)S(1)}, bf16[2,24,1536]{2,1,0:T(8,128)(2,1)S(1)}, u32[]{:S(2)}, u32[]{:S(2)}) collective-permute-start(bf16[2,24,1536]{2,1,0:T(8,128)(2,1)S(1)} %bitcast.224), channel_id=1, source_target_pairs={{0,4},{1,5},{2,6},{3,7},{4,0},{5,1},{6,2},{7,3},{8,12},{9,13},{10,... | collective-permute-start | bytes 442376 | tf_op jit(solution)/shard_map/ppermute | solution.py:49
  321.2 18.0 %collective-permute-done.26 = bf16[2,32,768]{2,1,0:T(8,128)(2,1)S(1)} collective-permute-done((bf16[2,32,768]{2,1,0:T(8,128)(2,1)S(1)}, bf16[2,32,768]{2,1,0:T(8,128)(2,1)S(1)}, u32[]{:S(2)}, u32[]{:S(2)}) %collective-permute-start.26) | collective-permute-done | bytes 98336 | tf_op jit(solution)/shard_map/ppermute | solution.py:49
  339.4 2.1 collective-permute-start.29
  342.4 2.2 collective-permute-done.29
  348.3 8.1 %reduce-scatter.2.cloned.1.call-done = bf16[216,768]{1,0:T(8,128)(2,1)} async-done(((bf16[6912,768]{1,0:T(8,128)(2,1)}), bf16[216,768]{1,0:T(8,128)(2,1)}) %reduce-scatter.2.cloned.1.call-update) | async-done | bytes 331792 | tf_op jit(solution)/shard_map/reduce_scatter | solution.py:876
  356.5 1.5 fusion.12
  (175 shorter events, 26.6 us)
Async XLA Ops:
  7.2 31.3 %copy-start.3 = (bf16[1,256,768]{2,1,0:T(8,128)(2,1)S(1)}, bf16[1,256,768]{2,1,0:T(8,128)(2,1)}, u32[]{:S(2)}) copy-start(bf16[1,256,768]{2,1,0:T(8,128)(2,1)} %param.18) | copy-start | bytes 1179652
  7.2 132.2 %all-gather.2.cloned.1.call-start = ((), (), s32[]{:S(2)}) async-start(), calls=%async_computation.1 | async-start | bytes 11354112 | tf_op jit(solution)/shard_map/all_gather | solution.py:804
  11.3 345.1 %reduce-scatter.2.cloned.1.call-start = ((), (), s32[]{:S(2)}) async-start(), calls=%async_computation.2 | async-start | bytes 10948608 | tf_op jit(solution)/shard_map/reduce_scatter | solution.py:876
  11.4 27.9 %collective-permute-start = (bf16[80,768]{1,0:T(8,128)(2,1)}, bf16[80,768]{1,0:T(8,128)(2,1)S(1)}, u32[]{:S(2)}, u32[]{:S(2)}) collective-permute-start(bf16[80,768]{1,0:T(8,128)(2,1)} %get-tuple-element.96), channel_id=1, source_target_pairs={{0,2},{1,3},{2,0},{3,1},{4,6},{5,7},{6,4},{7,5},{8,10},{9,11},{10,... | collective-permute-start | bytes 368648 | tf_op jit(solution)/shard_map/ppermute | solution.py:49
  14.5 24.8 %collective-permute-start.1 = (bf16[80,768]{1,0:T(8,128)(2,1)}, bf16[80,768]{1,0:T(8,128)(2,1)S(1)}, u32[]{:S(2)}, u32[]{:S(2)}) collective-permute-start(bf16[80,768]{1,0:T(8,128)(2,1)} %get-tuple-element.96), channel_id=1, source_target_pairs={{0,4},{1,5},{2,6},{3,7},{4,0},{5,1},{6,2},{7,3},{8,12},{9,13},{10,... | collective-permute-start | bytes 368648 | tf_op jit(solution)/shard_map/ppermute | solution.py:49
  17.1 22.2 %collective-permute-start.2 = (bf16[80,768]{1,0:T(8,128)(2,1)}, bf16[80,768]{1,0:T(8,128)(2,1)S(1)}, u32[]{:S(2)}, u32[]{:S(2)}) collective-permute-start(bf16[80,768]{1,0:T(8,128)(2,1)} %get-tuple-element.96), channel_id=1, source_target_pairs={{0,6},{1,7},{2,4},{3,5},{4,2},{5,3},{6,0},{7,1},{8,14},{9,15},{10,... | collective-permute-start | bytes 368648 | tf_op jit(solution)/shard_map/ppermute | solution.py:49
  17.1 21.4 %collective-permute-start.3 = (bf16[256,768]{1,0:T(8,128)(2,1)}, bf16[256,768]{1,0:T(8,128)(2,1)S(1)}, u32[]{:S(2)}, u32[]{:S(2)}) collective-permute-start(bf16[256,768]{1,0:T(8,128)(2,1)} %bitcast.163), channel_id=1, source_target_pairs={{0,4},{1,5},{2,6},{3,7},{8,12},{9,13},{10,14},{11,15},{16,20},{17,... | collective-permute-start | bytes 1179656 | tf_op jit(solution)/shard_map/ppermute | solution.py:53
  20.9 18.4 %collective-permute-start.4 = (bf16[256,768]{1,0:T(8,128)(2,1)}, bf16[256,768]{1,0:T(8,128)(2,1)S(1)}, u32[]{:S(2)}, u32[]{:S(2)}) collective-permute-start(bf16[256,768]{1,0:T(8,128)(2,1)} %bitcast.164), channel_id=1, source_target_pairs={{0,1},{1,0},{2,3},{3,2},{4,5},{5,4},{6,7},{7,6},{8,9},{9,8},{10,11... | collective-permute-start | bytes 1179656 | tf_op jit(solution)/shard_map/ppermute | solution.py:49
  38.5 31.2 %collective-permute-start.9 = (bf16[256,768]{1,0:T(8,128)(2,1)S(1)}, bf16[256,768]{1,0:T(8,128)(2,1)S(1)}, u32[]{:S(2)}, u32[]{:S(2)}) collective-permute-start(bf16[256,768]{1,0:T(8,128)(2,1)S(1)} %bitcast.170), channel_id=1, source_target_pairs={{5,6},{6,5},{13,14},{14,13},{21,22},{22,21},{29,30},{30,29}} | collective-permute-start | bytes 1179656 | tf_op jit(solution)/shard_map/ppermute | solution.py:53
  39.2 19.7 %copy-start.10 = (bf16[256,768]{1,0:T(8,128)(2,1)}, bf16[256,768]{1,0:T(8,128)(2,1)S(1)}, u32[]{:S(2)}) copy-start(bf16[256,768]{1,0:T(8,128)(2,1)S(1)} %broadcast_select_fusion.refs_0_) | copy-start | bytes 1179652
  39.3 19.0 %copy-start.16 = (bf16[256,768]{1,0:T(8,128)(2,1)}, bf16[256,768]{1,0:T(8,128)(2,1)S(1)}, u32[]{:S(2)}) copy-start(bf16[256,768]{1,0:T(8,128)(2,1)S(1)} %collective-permute-done.4.refs_5_) | copy-start | bytes 1179652
  39.3 36.0 %collective-permute-start.7 = (bf16[256,768]{1,0:T(8,128)(2,1)S(1)}, bf16[256,768]{1,0:T(8,128)(2,1)S(1)}, u32[]{:S(2)}, u32[]{:S(2)}) collective-permute-start(bf16[256,768]{1,0:T(8,128)(2,1)S(1)} %broadcast_select_fusion.refs_0_), channel_id=1, source_target_pairs={{0,2},{1,3},{2,0},{3,1},{4,6},{5,7},{6,4},{7,5},{8,10},{9,11},{10,... | collective-permute-start | bytes 1179656 | tf_op jit(solution)/shard_map/ppermute | solution.py:49
  55.4 19.9 %collective-permute-start.8 = (bf16[256,768]{1,0:T(8,128)(2,1)S(1)}, bf16[256,768]{1,0:T(8,128)(2,1)S(1)}, u32[]{:S(2)}, u32[]{:S(2)}) collective-permute-start(bf16[256,768]{1,0:T(8,128)(2,1)S(1)} %broadcast_select_fusion.refs_0_), channel_id=1, source_target_pairs={{0,1},{1,0},{2,3},{3,2},{4,5},{5,4},{6,7},{7,6},{8,9},{9,8},{10,11... | collective-permute-start | bytes 1179656 | tf_op jit(solution)/shard_map/ppermute | solution.py:49
  56.7 13.0 %collective-permute-start.6 = (bf16[4,48,768]{2,1,0:T(8,128)(2,1)S(1)}, bf16[4,48,768]{2,1,0:T(8,128)(2,1)S(1)}, u32[]{:S(2)}, u32[]{:S(2)}) collective-permute-start(bf16[4,48,768]{2,1,0:T(8,128)(2,1)S(1)} %pad_maximum_fusion.4), channel_id=1, source_target_pairs={{0,16},{1,17},{2,18},{3,19},{4,20},{5,21},{6,22},{7,23},{8,24},{9,... | collective-permute-start | bytes 884744 | tf_op jit(solution)/shard_map/ppermute | solution.py:49
  58.3 11.3 %collective-permute-start.5 = (bf16[4,32,768]{2,1,0:T(8,128)(2,1)S(1)}, bf16[4,32,768]{2,1,0:T(8,128)(2,1)S(1)}, u32[]{:S(2)}, u32[]{:S(2)}) collective-permute-start(bf16[4,32,768]{2,1,0:T(8,128)(2,1)S(1)} %pad_maximum_fusion.6), channel_id=1, source_target_pairs={{0,1},{1,0},{2,3},{3,2},{4,5},{5,4},{6,7},{7,6},{8,9},{9,8},{10,11... | collective-permute-start | bytes 589832 | tf_op jit(solution)/shard_map/ppermute | solution.py:49
  69.7 28.6 %copy-start.17 = (bf16[256,768]{1,0:T(8,128)(2,1)}, bf16[256,768]{1,0:T(8,128)(2,1)S(1)}, u32[]{:S(2)}) copy-start(bf16[256,768]{1,0:T(8,128)(2,1)S(1)} %collective-permute-done.9.refs_6_) | copy-start | bytes 1179652
  75.3 23.1 %copy-start.18 = (bf16[256,768]{1,0:T(8,128)(2,1)}, bf16[256,768]{1,0:T(8,128)(2,1)S(1)}, u32[]{:S(2)}) copy-start(bf16[256,768]{1,0:T(8,128)(2,1)S(1)} %collective-permute-done.7.refs_1_) | copy-start | bytes 1179652
  75.3 3.6 copy-start.19
  75.3 22.9 %collective-permute-start.11 = (bf16[8,48,768]{2,1,0:T(8,128)(2,1)S(1)}, bf16[8,48,768]{2,1,0:T(8,128)(2,1)S(1)}, u32[]{:S(2)}, u32[]{:S(2)}) collective-permute-start(bf16[8,48,768]{2,1,0:T(8,128)(2,1)S(1)} %constant_dynamic-update-slice_fusion.5), channel_id=1, source_target_pairs={{0,1},{1,0},{2,3},{3,2},{4,5},{5,4},{6,7},{7,6},{8,9},{9,8},{10,11... | collective-permute-start | bytes 1769480 | tf_op jit(solution)/shard_map/ppermute | solution.py:49
  76.4 14.5 %collective-permute-start.10 = (bf16[8,32,768]{2,1,0:T(8,128)(2,1)S(1)}, bf16[8,32,768]{2,1,0:T(8,128)(2,1)S(1)}, u32[]{:S(2)}, u32[]{:S(2)}) collective-permute-start(bf16[8,32,768]{2,1,0:T(8,128)(2,1)S(1)} %constant_dynamic-update-slice_fusion), channel_id=1, source_target_pairs={{0,16},{1,17},{2,18},{3,19},{4,20},{5,21},{6,22},{7,23},{8,24},{9,... | collective-permute-start | bytes 1179656 | tf_op jit(solution)/shard_map/ppermute | solution.py:49
  78.3 33.9 %collective-permute-start.12 = (bf16[256,768]{1,0:T(8,128)(2,1)S(1)}, bf16[256,768]{1,0:T(8,128)(2,1)S(1)}, u32[]{:S(2)}, u32[]{:S(2)}) collective-permute-start(bf16[256,768]{1,0:T(8,128)(2,1)S(1)} %collective-permute-done.7.refs_1_), channel_id=1, source_target_pairs={{0,1},{1,0},{2,3},{3,2},{4,5},{5,4},{6,7},{7,6},{8,9},{9,8},{10,11... | collective-permute-start | bytes 1179656 | tf_op jit(solution)/shard_map/ppermute | solution.py:49
  91.0 21.8 %copy-start.7 = (bf16[16,32,768]{2,1,0:T(8,128)(2,1)}, bf16[16,32,768]{2,1,0:T(8,128)(2,1)S(1)}, u32[]{:S(2)}) copy-start(bf16[16,32,768]{2,1,0:T(8,128)(2,1)S(1)} %pad_maximum_fusion.1.refs_10_) | copy-start | bytes 2359300
  91.0 21.8 %copy-start.21 = (s32[1,8]{1,0:T(1,128)S(1)}, s32[1,8]{1,0:T(1,128)}, u32[]{:S(2)}) copy-start(s32[1,8]{1,0:T(1,128)} %param.19) | copy-start | bytes 100
  98.4 17.9 %copy-start.5 = (bf16[16,48,768]{2,1,0:T(8,128)(2,1)}, bf16[16,48,768]{2,1,0:T(8,128)(2,1)S(1)}, u32[]{:S(2)}) copy-start(bf16[16,48,768]{2,1,0:T(8,128)(2,1)S(1)} %pad_maximum_fusion.refs_12_) | copy-start | bytes 3538948
  112.3 4.0 %copy-start.20 = (bf16[256,768]{1,0:T(8,128)(2,1)}, bf16[256,768]{1,0:T(8,128)(2,1)S(1)}, u32[]{:S(2)}) copy-start(bf16[256,768]{1,0:T(8,128)(2,1)S(1)} %collective-permute-done.12.refs_3_) | copy-start | bytes 1179652
  112.3 4.0 %collective-permute-start.14 = (bf16[16,48,768]{2,1,0:T(8,128)(2,1)S(1)}, bf16[16,48,768]{2,1,0:T(8,128)(2,1)S(1)}, u32[]{:S(2)}, u32[]{:S(2)}) collective-permute-start(bf16[16,48,768]{2,1,0:T(8,128)(2,1)S(1)} %pad_maximum_fusion.refs_12_), channel_id=1, source_target_pairs={{0,8},{1,9},{2,10},{3,11},{4,12},{5,13},{6,14},{7,15},{8,0},{9,1},... | collective-permute-start | bytes 3538952 | tf_op jit(solution)/shard_map/ppermute | solution.py:49
  112.3 3.8 %collective-permute-start.13 = (bf16[16,32,768]{2,1,0:T(8,128)(2,1)S(1)}, bf16[16,32,768]{2,1,0:T(8,128)(2,1)}, u32[]{:S(2)}, u32[]{:S(2)}) collective-permute-start(bf16[16,32,768]{2,1,0:T(8,128)(2,1)S(1)} %pad_maximum_fusion.1.refs_10_), channel_id=1, source_target_pairs={{0,8},{1,9},{2,10},{3,11},{4,12},{5,13},{6,14},{7,15},{8,0},{9,1},... | collective-permute-start | bytes 2359304 | tf_op jit(solution)/shard_map/ppermute | solution.py:49
  186.6 3.3 copy-start.12
  187.8 12.8 %collective-permute-start.15 = (bf16[256,768]{1,0:T(8,128)(2,1)S(1)}, bf16[256,768]{1,0:T(8,128)(2,1)S(1)}, u32[]{:S(2)}, u32[]{:S(2)}) collective-permute-start(bf16[256,768]{1,0:T(8,128)(2,1)S(1)} %get-tuple-element.180), channel_id=1, source_target_pairs={{0,1},{1,0},{2,3},{3,2},{4,5},{5,4},{6,7},{7,6},{8,9},{9,8},{10,11... | collective-permute-start | bytes 1179656 | tf_op jit(solution)/shard_map/ppermute | solution.py:49
  189.7 17.9 %collective-permute-start.16 = (bf16[256,768]{1,0:T(8,128)(2,1)S(1)}, bf16[256,768]{1,0:T(8,128)(2,1)}, u32[]{:S(2)}, u32[]{:S(2)}) collective-permute-start(bf16[256,768]{1,0:T(8,128)(2,1)S(1)} %get-tuple-element.179), channel_id=1, source_target_pairs={{0,1},{1,0},{2,3},{3,2},{4,5},{5,4},{6,7},{7,6},{8,9},{9,8},{10,11... | collective-permute-start | bytes 1179656 | tf_op jit(solution)/shard_map/ppermute | solution.py:49
  195.5 12.2 %copy-start = (bf16[4,256,768]{2,1,0:T(8,128)(2,1)S(1)}, bf16[4,256,768]{2,1,0:T(8,128)(2,1)}, u32[]{:S(2)}) copy-start(bf16[4,256,768]{2,1,0:T(8,128)(2,1)} %token_product.2) | copy-start | bytes 4718596
  200.5 8.4 %copy-start.1 = (bf16[3,256,768]{2,1,0:T(8,128)(2,1)S(1)}, bf16[3,256,768]{2,1,0:T(8,128)(2,1)}, u32[]{:S(2)}) copy-start(bf16[3,256,768]{2,1,0:T(8,128)(2,1)} %token_product.3) | copy-start | bytes 3538948
  209.0 18.4 %collective-permute-start.18 = (bf16[256,768]{1,0:T(8,128)(2,1)S(1)}, bf16[256,768]{1,0:T(8,128)(2,1)S(1)}, u32[]{:S(2)}, u32[]{:S(2)}) collective-permute-start(bf16[256,768]{1,0:T(8,128)(2,1)S(1)} %get-tuple-element.181), channel_id=1, source_target_pairs={{0,1},{1,0},{2,3},{3,2},{4,5},{5,4},{6,7},{7,6},{8,9},{9,8},{10,11... | collective-permute-start | bytes 1179656 | tf_op jit(solution)/shard_map/ppermute | solution.py:49
  210.8 16.6 %collective-permute-start.19 = (bf16[256,768]{1,0:T(8,128)(2,1)S(1)}, bf16[256,768]{1,0:T(8,128)(2,1)}, u32[]{:S(2)}, u32[]{:S(2)}) collective-permute-start(bf16[256,768]{1,0:T(8,128)(2,1)S(1)} %get-tuple-element.182), channel_id=1, source_target_pairs={{5,6},{6,5},{13,14},{14,13},{21,22},{22,21},{29,30},{30,29}} | collective-permute-start | bytes 1179656 | tf_op jit(solution)/shard_map/ppermute | solution.py:53
  212.2 17.2 %collective-permute-start.17 = (bf16[256,768]{1,0:T(8,128)(2,1)S(1)}, bf16[256,768]{1,0:T(8,128)(2,1)S(1)}, u32[]{:S(2)}, u32[]{:S(2)}) collective-permute-start(bf16[256,768]{1,0:T(8,128)(2,1)S(1)} %get-tuple-element.177), channel_id=1, source_target_pairs={{0,2},{1,3},{2,0},{3,1},{4,6},{5,7},{6,4},{7,5},{8,10},{9,11},{10,... | collective-permute-start | bytes 1179656 | tf_op jit(solution)/shard_map/ppermute | solution.py:49
  229.5 6.1 %collective-permute-start.21 = (bf16[16,24,1536]{2,1,0:T(8,128)(2,1)}, bf16[16,24,1536]{2,1,0:T(8,128)(2,1)S(1)}, u32[]{:S(2)}, u32[]{:S(2)}) collective-permute-start(bf16[16,24,1536]{2,1,0:T(8,128)(2,1)} %get-tuple-element.143), channel_id=1, source_target_pairs={{0,8},{1,9},{2,10},{3,11},{4,12},{5,13},{6,14},{7,15},{8,0},{9,1},... | collective-permute-start | bytes 3538952 | tf_op jit(solution)/shard_map/ppermute | solution.py:49
  233.0 2.6 collective-permute-start.20
  233.6 87.6 %collective-permute-start.28 = (bf16[256,768]{1,0:T(8,128)(2,1)S(1)}, bf16[256,768]{1,0:T(8,128)(2,1)S(1)}, u32[]{:S(2)}, u32[]{:S(2)}) collective-permute-start(bf16[256,768]{1,0:T(8,128)(2,1)S(1)} %convert_element_type.352), channel_id=1, source_target_pairs={{4,0},{5,1},{6,2},{7,3},{12,8},{13,9},{14,10},{15,11},{20,16},{21,... | collective-permute-start | bytes 1179656 | tf_op jit(solution)/shard_map/ppermute | solution.py:53
  235.8 25.2 %collective-permute-start.23 = (bf16[8,24,1536]{2,1,0:T(8,128)(2,1)S(1)}, bf16[8,24,1536]{2,1,0:T(8,128)(2,1)S(1)}, u32[]{:S(2)}, u32[]{:S(2)}) collective-permute-start(bf16[8,24,1536]{2,1,0:T(8,128)(2,1)S(1)} %fusion.2), channel_id=1, source_target_pairs={{0,1},{1,0},{2,3},{3,2},{4,5},{5,4},{6,7},{7,6},{8,9},{9,8},{10,11... | collective-permute-start | bytes 1769480 | tf_op jit(solution)/shard_map/ppermute | solution.py:49
  238.4 19.3 %collective-permute-start.22 = (bf16[8,32,768]{2,1,0:T(8,128)(2,1)S(1)}, bf16[8,32,768]{2,1,0:T(8,128)(2,1)S(1)}, u32[]{:S(2)}, u32[]{:S(2)}) collective-permute-start(bf16[8,32,768]{2,1,0:T(8,128)(2,1)S(1)} %bitcast.215), channel_id=1, source_target_pairs={{0,16},{1,17},{2,18},{3,19},{4,20},{5,21},{6,22},{7,23},{8,24},{9,... | collective-permute-start | bytes 1179656 | tf_op jit(solution)/shard_map/ppermute | solution.py:49
  261.1 11.5 %collective-permute-start.25 = (bf16[4,24,1536]{2,1,0:T(8,128)(2,1)S(1)}, bf16[4,24,1536]{2,1,0:T(8,128)(2,1)S(1)}, u32[]{:S(2)}, u32[]{:S(2)}) collective-permute-start(bf16[4,24,1536]{2,1,0:T(8,128)(2,1)S(1)} %bitcast.220), channel_id=1, source_target_pairs={{0,16},{1,17},{2,18},{3,19},{4,20},{5,21},{6,22},{7,23},{8,24},{9,... | collective-permute-start | bytes 884744 | tf_op jit(solution)/shard_map/ppermute | solution.py:49
  263.7 6.5 %collective-permute-start.24 = (bf16[4,32,768]{2,1,0:T(8,128)(2,1)S(1)}, bf16[4,32,768]{2,1,0:T(8,128)(2,1)S(1)}, u32[]{:S(2)}, u32[]{:S(2)}) collective-permute-start(bf16[4,32,768]{2,1,0:T(8,128)(2,1)S(1)} %fusion.4), channel_id=1, source_target_pairs={{0,1},{1,0},{2,3},{3,2},{4,5},{5,4},{6,7},{7,6},{8,9},{9,8},{10,11... | collective-permute-start | bytes 589832 | tf_op jit(solution)/shard_map/ppermute | solution.py:49
  272.7 66.5 %collective-permute-start.27 = (bf16[2,24,1536]{2,1,0:T(8,128)(2,1)S(1)}, bf16[2,24,1536]{2,1,0:T(8,128)(2,1)S(1)}, u32[]{:S(2)}, u32[]{:S(2)}) collective-permute-start(bf16[2,24,1536]{2,1,0:T(8,128)(2,1)S(1)} %bitcast.224), channel_id=1, source_target_pairs={{0,4},{1,5},{2,6},{3,7},{4,0},{5,1},{6,2},{7,3},{8,12},{9,13},{10,... | collective-permute-start | bytes 442376 | tf_op jit(solution)/shard_map/ppermute | solution.py:49
  320.9 20.5 %copy-start.2 = (f32[256,768]{1,0:T(8,128)S(1)}, f32[256,768]{1,0:T(8,128)}, u32[]{:S(2)}) copy-start(f32[256,768]{1,0:T(8,128)} %fusion) | copy-start | bytes 2359300
  320.9 20.5 %copy-start.8 = (f32[256,768]{1,0:T(8,128)S(1)}, f32[256,768]{1,0:T(8,128)}, u32[]{:S(2)}) copy-start(f32[256,768]{1,0:T(8,128)} %get-tuple-element.129) | copy-start | bytes 2359300
  321.1 18.1 %collective-permute-start.26 = (bf16[2,32,768]{2,1,0:T(8,128)(2,1)S(1)}, bf16[2,32,768]{2,1,0:T(8,128)(2,1)S(1)}, u32[]{:S(2)}, u32[]{:S(2)}) collective-permute-start(bf16[2,32,768]{2,1,0:T(8,128)(2,1)S(1)} %bitcast.228), channel_id=1, source_target_pairs={{0,4},{1,5},{2,6},{3,7},{4,0},{5,1},{6,2},{7,3},{8,12},{9,13},{10,... | collective-permute-start | bytes 294920 | tf_op jit(solution)/shard_map/ppermute | solution.py:49
  339.2 7.2 %collective-permute-start.30 = (bf16[1,24,1536]{2,1,0:T(8,128)(2,1)S(1)}, bf16[1,24,1536]{2,1,0:T(8,128)(2,1)S(1)}, u32[]{:S(2)}, u32[]{:S(2)}) collective-permute-start(bf16[1,24,1536]{2,1,0:T(8,128)(2,1)S(1)} %add_convert_fusion.7), channel_id=1, source_target_pairs={{0,2},{1,3},{2,0},{3,1},{4,6},{5,7},{6,4},{7,5},{8,10},{9,11},{10,... | collective-permute-start | bytes 221192 | tf_op jit(solution)/shard_map/ppermute | solution.py:49
  339.4 5.2 %collective-permute-start.29 = (bf16[1,32,768]{2,1,0:T(8,128)(2,1)S(1)}, bf16[1,32,768]{2,1,0:T(8,128)(2,1)S(1)}, u32[]{:S(2)}, u32[]{:S(2)}) collective-permute-start(bf16[1,32,768]{2,1,0:T(8,128)(2,1)S(1)} %add_convert_fusion.8), channel_id=1, source_target_pairs={{0,2},{1,3},{2,0},{3,1},{4,6},{5,7},{6,4},{7,5},{8,10},{9,11},{10,... | collective-permute-start | bytes 147464 | tf_op jit(solution)/shard_map/ppermute | solution.py:49
  (7 other events, 12.9 us)
Sparse Core Ops, SparseCore 0:
  11.5 126.9 all-gather.1
  161.6 194.7 reduce-scatter.1

commit v8 on v7

--- a/solution.py
+++ b/solution.py
@@ -6,6 +6,7 @@
 from jax import lax
 from jax.experimental import pallas as pl
 from jax.experimental.pallas import tpu as pltpu
+from jax.sharding import Mesh
 from jax.sharding import PartitionSpec as P
 
 HEADS = 12
@@ -19,7 +20,8 @@
 MASK_FILL = -1000000000.0
 SQRT_HALF = 0.7071067811865476
 INV_ROOT_TAU = 0.3989422804014327
-AXES = ("grp", "row")
+AXES = ("x", "core", "z", "y")
+GRP, ROW = AXES[:2], AXES[2:]
 WIDE = 4
 WO, WI = 4, 5
 WQ, WK, WV = 0, 1, 2
@@ -53,7 +55,7 @@
         return lax.ppermute(value, AXES, pairs)
 
     def me(self):
-        return lax.axis_index("grp") * self.row + lax.axis_index("row")
+        return lax.axis_index(AXES)
 
 
 class Reduce:
@@ -96,7 +98,7 @@
         if self.ready:
             plan, own = self.plan, self.own
             across = plan.send(own, [(0, 4), (1, 5), (2, 6), (3, 7)])
-            self.same = jnp.where(lax.axis_index("row") < 4, own, across)
+            self.same = jnp.where(lax.axis_index(ROW) < 4, own, across)
             self.beside = plan.swap(own, 1)
             return [self.same, self.beside]
         return []
@@ -115,13 +117,13 @@
             self.other_y = self.plan.swap(self.other, 1)
 
     def spots(self):
-        row, rows, own = lax.axis_index("row"), self.rows, self.own
+        row, rows, own = lax.axis_index(ROW), self.rows, self.own
         if self.ready:
             near = jnp.where(row < 4, 0, jnp.where((row == 5) | (row == 6), 3, 2))
             return [
                 self.same, self.other, self.same_y, self.other_y, own, self.beside, self.diagonal,
             ], near
-        every = lax.all_gather(own, "row", axis=0, tiled=True)
+        every = lax.all_gather(own, ROW, axis=0, tiled=True)
         start = jnp.maximum(row * rows - CONT_MOST, 0)
         padded = jnp.concatenate([every, jnp.zeros((CONT_MOST, own.shape[1]), own.dtype)], 0)
         near = lax.dynamic_slice_in_dim(padded, start, rows + 2 * CONT_MOST, 0)
@@ -131,7 +133,7 @@
 
 
 def near_segments(plan, segments, rows):
-    row = lax.axis_index("row")
+    row = lax.axis_index(ROW)
     if plan.row != 8:
         start = jnp.maximum(row * rows - CONT_MOST, 0)
         padded = jnp.concatenate([segments, jnp.full((CONT_MOST,), -1, jnp.int32)], 0)
@@ -175,7 +177,7 @@
             self.own = own + self.plan.send(parts[2], [(5, 6), (6, 5)]).astype(F32)
 
     def total(self):
-        row, rows = lax.axis_index("row"), self.rows
+        row, rows = lax.axis_index(ROW), self.rows
         if self.plan.row == 8:
             return jnp.where(row < 4, self.same + self.back.astype(F32), self.own)
         around = self.around.reshape(-1, self.around.shape[-1]).astype(F32)
@@ -185,7 +187,7 @@
         near = jnp.where(row * rows < PROMPT, 0, around)
         near = lax.dynamic_slice_in_dim(whole, start, rows + 2 * CONT_MOST, 0) + near
         whole = lax.dynamic_update_slice_in_dim(whole, near, start, 0)
-        return lax.psum_scatter(whole[: self.plan.row * rows], "row", scatter_dimension=0, tiled=True)
+        return lax.psum_scatter(whole[: self.plan.row * rows], ROW, scatter_dimension=0, tiled=True)
 
 
 def heads_mask(lanes, head):
@@ -399,7 +401,7 @@
     return jnp.where(core == 0, odd, even), jnp.where(core == 0, even, odd)
 
 
-def middle_kernel(wide, ctx_ref, own_ref, cot_ref, wo_ref, wi_ref, wu_ref, vec_ref, bin_ref,
+def middle_kernel(wide, mapped, ctx_ref, own_ref, cot_ref, wo_ref, wi_ref, wu_ref, vec_ref, bin_ref,
                   out_ref, h1_ref, gctx_ref, grads, sums_ref, sbin_ref,
                   first_ref, n1_ref, inv_ref, low_ref, pre_ref, cdf_ref, act_ref, acc_ref,
                   gffn_ref, glow_ref, out_buf, in_buf, wo_buf, sems):
@@ -413,18 +415,43 @@
     each = width // owners
     some = owners // wide
 
+    def slot(group, i):
+        return group % 2 * 16 + group // 2 * 8 + i % 2 * 4 + i // 2 if mapped else group * 8 + i
+
     def outer(at):
         turn = (2 * wide - 1 - at) % 2
-        place = grads.at[pl.ds(at * some, some), pl.ds(0, wide * each)]
-        return pltpu.make_async_copy(out_buf.at[turn], place, sems.at[turn])
+        return [
+            pltpu.make_async_copy(
+                out_buf.at[turn, i], grads.at[slot(at, i), pl.ds(0, wide * each)], sems.at[turn, i]
+            )
+            for i in range(some)
+        ]
 
     def inner(at):
         turn = (2 * wide - 1 - at) % 2
-        place = grads.at[:, pl.ds((wide + 1 + at) * each, each)]
-        return pltpu.make_async_copy(in_buf.at[turn], place, sems.at[2 + turn])
+        top = pl.multiple_of((wide + 1 + at) * each, each)
+        return [
+            pltpu.make_async_copy(
+                in_buf.at[turn, e], grads.at[slot(e // 8, e % 8), pl.ds(top, each)], sems.at[2 + turn, e]
+            )
+            for e in range(owners)
+        ]
 
     def output():
-        return pltpu.make_async_copy(wo_buf, grads.at[:, pl.ds(wide * each, each)], sems.at[4])
+        return [
+            pltpu.make_async_copy(
+                wo_buf.at[e], grads.at[slot(e // 8, e % 8), pl.ds(wide * each, each)], sems.at[4, e]
+            )
+            for e in range(owners)
+        ]
+
+    def start(copies):
+        for copy in copies:
+            copy.start()
+
+    def wait(copies):
+        for copy in copies:
+            copy.wait()
 
     @pl.when(step == 0)
     def _():
@@ -487,13 +514,12 @@
 
         @pl.when(step >= wide + 2)
         def _():
-            outer(at + 2).wait()
-            inner(at + 2).wait()
+            wait(outer(at + 2) + inner(at + 2))
 
         out_buf[turn] = tn(act_ref[:, chunk], low).astype(BF).reshape(some, wide * each, width)
-        outer(at).start()
+        start(outer(at))
         in_buf[turn] = tn(low_ref[...], grad).astype(BF).reshape(owners, each, width)
-        inner(at).start()
+        start(inner(at))
         gffn_ref[...] += nt(grad, square(wi_ref))
 
     @pl.when(step == 2 * wide - 1)
@@ -508,18 +534,15 @@
         low = back.astype(BF)
         sums_ref[5:6, :] = down(low.astype(F32))
         wo_buf[...] = tn(ctx_ref[...], low).astype(BF).reshape(owners, each, width)
-        output().start()
+        start(output())
         gctx = nt(low, square(wo_ref)).astype(BF)
         gctx_ref[...] = gctx
         sums_ref[6:7, :] = down(gctx.astype(F32))
         sums_ref[7:8, :] = jnp.zeros((1, width), F32)
-        for at in (1, 0):
-            outer(at).wait()
-            inner(at).wait()
-        output().wait()
-
-
-def middle_call(ctx, own, cot, got, vec, b_inner):
+        wait(outer(1) + inner(1) + outer(0) + inner(0) + output())
+
+
+def middle_call(ctx, own, cot, got, vec, b_inner, mapped):
     rows, width = own.shape
     owners = got.shape[0]
     each = width // owners
@@ -528,7 +551,7 @@
     at = lambda s: jnp.where(s < wide, s, 2 * wide - 1 - s)
     shape = jax.ShapeDtypeStruct
     return pl.pallas_call(
-        functools.partial(middle_kernel, wide),
+        functools.partial(middle_kernel, wide, mapped),
         grid=(2 * wide,),
         in_specs=[
             whole((rows, width)), whole((rows, width)), whole((rows, width)),
@@ -555,7 +578,7 @@
             pltpu.VMEM((rows, width), BF),
             pltpu.VMEM((2, owners // wide, wide * each, width), BF),
             pltpu.VMEM((2, owners, each, width), BF),
-            pltpu.VMEM((owners, each, width), BF), pltpu.SemaphoreType.DMA((5,)),
+            pltpu.VMEM((owners, each, width), BF), pltpu.SemaphoreType.DMA((5, owners)),
         ],
         compiler_params=pltpu.CompilerParams(vmem_limit_bytes=60 * 2**20),
         cost_estimate=pl.CostEstimate(
@@ -769,6 +792,7 @@
 
 def solution(mesh):
     plan = Plan(mesh.shape["grp"], mesh.shape["row"])
+    fine = Mesh(mesh.devices.reshape(plan.grp // 2, 2, 4, plan.row // 4), AXES)
 
     def per_device(
         tokens, cont_lengths, cotangent, w_query, w_key, w_value, w_output, w_inner, w_outer,
@@ -795,8 +819,8 @@
 
         line = jnp.concatenate([in_line(early), in_line(late)], 0)
         runs = plan.grp
-        grp, row = lax.axis_index("grp"), lax.axis_index("row")
-        core = (grp % 2).astype(jnp.int32).reshape(1)
+        row = lax.axis_index(ROW)
+        core = lax.axis_index("core").astype(jnp.int32).reshape(1)
         exchange = Tokens(plan, own)
         squares = (w_query, w_key, w_value)
         if step % 8 == 0:
@@ -869,13 +893,14 @@
         )
         vec = jnp.concatenate([table, jnp.zeros((2, width), F32)], 0)
         layer_out, grad_h1, grad_context, grads, sums, sums_bin = middle_call(
-            context, own, cotangent[0], got, vec, v_bin
+            context, own, cotangent[0], got, vec, v_bin, step % 8 == 0
         )
         if step % 8:
             grads = real_owners(grads, count, step, width)
-        o_ab = lax.psum_scatter(
-            grads.reshape(-1, width), AXES, scatter_dimension=0, tiled=True
-        ).astype(F32)
+            grads = grads.reshape(plan.grp // 2, 2, 4, plan.row // 4, -1, width)
+            grads = grads.transpose(1, 0, 3, 2, 4, 5).reshape(count, -1, width)
+        level = lambda value, axes: lax.psum_scatter(value, axes, scatter_dimension=0, tiled=True)
+        grads = level(grads, "core")
         core_bit = plan.core[0]
         left = [1 << i for i in reversed(range(plan.bits)) if 1 << i != core_bit]
         parts = width // 256
@@ -883,6 +908,8 @@
             0, parts, first_near, near, grad_context, context, queries, keys_p, values_p, log_total,
             seg_own, seg_near,
         )
+        grads, dkp, dvp, dqp = tie(grads, dkp, dvp, dqp)
+        grads = level(grads, ("x", "y"))
         shared_p = product_call(first_near, near, dkp, dvp, squares, rows)
         returned = Return(plan, rows)
         returned.prompt_one(shared_p)
@@ -890,16 +917,15 @@
             0, parts, None, near, grad_context, context, queries, keys_n, values_n, log_total,
             seg_own, seg_near, dqp,
         )
-        shared_n = product_call(None, near, dkn, dvn, squares, rows)
-        returned.same, shared_n, dq = tie(returned.same, shared_n, dq)
+        returned.same, dkn, dvn, dq = tie(returned.same, dkn, dvn, dq)
         returned.prompt_two()
-        returned.near(shared_n)
         q_send, q_keep, kv_send, kv_keep, grad_own, sums_qkv = weight_call(
             spots, first_near, near, own, dq, squares, grad_h1, dkp, dvp, dkn, dvn, core, runs
         )
-        q_send, q_keep, kv_send, kv_keep, returned.same, returned.own = tie(
-            q_send, q_keep, kv_send, kv_keep, returned.same, returned.own
+        q_send, q_keep, kv_send, kv_keep, returned.same, dkn, dvn = tie(
+            q_send, q_keep, kv_send, kv_keep, returned.same, dkn, dvn
         )
+        shared_n = product_call(None, near, dkn, dvn, squares, rows)
         returned.prompt_three()
 
         order = (6, 5, 3, 4, 2, 0, 1)
@@ -926,13 +952,21 @@
         r_kv = Reduce(plan, [kv_keep, plan.swap(kv_send, core_bit)], left)
         for one, two in zip(plan.x + plan.y + plan.z[::-1], plan.y + plan.x + plan.z[::-1]):
             n = len(r_q.terms)
-            if one == plan.z[0]:
-                *tied, returned.back = tie(*r_q.terms, *r_kv.terms, returned.back)
+            held = [*r_q.terms, *r_kv.terms]
+            if one == plan.x[0]:
+                *held, shared_n = tie(*held, shared_n)
+                returned.near(shared_n)
+            elif one == plan.y[0]:
+                *held, returned.own = tie(*held, returned.own)
+            elif one == plan.z[-1]:
+                *held, grads = tie(*held, grads)
+                grads = level(grads, "z")
             else:
-                tied = tie(*r_q.terms, *r_kv.terms)
-            r_q.terms, r_kv.terms = list(tied[:n]), list(tied[n:])
+                *held, returned.back = tie(*held, returned.back)
+            r_q.terms, r_kv.terms = held[:n], held[n:]
             r_q.stage(one)
             r_kv.stage(two)
+        o_ab = grads.reshape(-1, width).astype(F32)
         grad_tokens = grad_own + returned.total()
         o_query = r_q.result()
         o_line = o_query[step]
@@ -960,10 +994,10 @@
             o_small[7],
         )
 
-    split = P("grp", "row", None)
+    split = P(GRP, ROW, None)
     owned2, owned1 = P(AXES, None), P(AXES)
-    in_specs = (split, P("grp", None), split) + (owned2,) * 6 + (owned1,) * 9
+    in_specs = (split, P(GRP, None), split) + (owned2,) * 6 + (owned1,) * 9
     out_specs = (split, split) + (owned2,) * 6 + (owned1,) * 9
     return jax.shard_map(
-        per_device, mesh=mesh, in_specs=in_specs, out_specs=out_specs, check_vma=False
+        per_device, mesh=fine, in_specs=in_specs, out_specs=out_specs, check_vma=False
     )

time: 367 us -> 377 us (1.027)
  waiting for transfers between devices: 126 us -> 168 us
  starting transfers between devices: 99.8 us -> 64.8 us
    ppermute x27, starting transfers between devices: 92.3 us -> 58 us  [swap(): return lax.ppermute(value, AXES, [(i, i ^ mask) for i in range(self.count)])]
    ppermute x27, waiting for transfers between devices: 105 us -> 131 us  [swap(): return lax.ppermute(value, AXES, [(i, i ^ mask) for i in range(self.count)])]
    reduce_scatter x1 -> x3, waiting for transfers between devices: 8.12 us -> 24.6 us  [per_device(): lax.psum_scatter(value, axes, scatter_dimension=0, tiled=True)]
  transfers between devices with their start and end apart: 33 -> 35, of which waited for: 17 -> 18; matrix products, arithmetic and copies ran while one was open for 6% -> 6% of each run, Pallas kernels for 20% -> 19%
where the time goes in v8:
time: 377 us; the launch traced here: 376 us
  waiting for transfers between devices  168 us (45%)
  Pallas kernels  95.1 us (25%)
  starting transfers between devices  64.8 us (17%)
  local copies, waits for them, and re-layouts  20 us (5%)
  between operations  14.5 us (4%)
  other arithmetic  13.1 us (3%)
    ppermute x27, waiting for transfers between devices, swap(): return lax.ppermute(value, AXES, [(i, i ^ mask) for i in range(self.count)])  131 us
    ppermute x27, starting transfers between devices, swap(): return lax.ppermute(value, AXES, [(i, i ^ mask) for i in range(self.count)])  58 us
    reduce_scatter x3, waiting for transfers between devices, per_device(): lax.psum_scatter(value, axes, scatter_dimension=0, tiled=True)  24.6 us
    pallas_call x2, Pallas kernels, back_call(): pl.pallas_call(functools.partial(back_kernel, rows, bound, dq0 is not Non...  24.2 us
    pallas_call x1, Pallas kernels, attention_call(): pl.pallas_call(functools.partial(attention_kernel, blocks, first, rows, p...  22.2 us
    pallas_call x1, Pallas kernels, middle_call(): pl.pallas_call(functools.partial(middle_kernel, wide, mapped), grid=(2 *...  21.6 us
    pallas_call x1, Pallas kernels, weight_call(): pl.pallas_call(functools.partial(weight_kernel, blocks, first, rows, runs...  14.7 us
    ppermute x4, waiting for transfers between devices, send(): return lax.ppermute(value, AXES, pairs)  12.6 us
  transfers between devices with their start and end apart: 35, of which 18 were waited for; matrix products, arithmetic and copies ran while one was open for 6% of the time, Pallas kernels for 19%

profile of v8, /device:TPU:0, one launch (start us, length us, event | category | flops | bytes accessed | tf_op | source)
XLA Modules:
  0.0 375.6 jit_solution(326610684404153566)
XLA Ops:
  9.5 1.8 pack.1
  11.4 3.1 collective-permute-start
  14.5 2.6 collective-permute-start.1
  17.1 3.8 %collective-permute-start.3 = (bf16[256,768]{1,0:T(8,128)(2,1)}, bf16[256,768]{1,0:T(8,128)(2,1)S(1)}, u32[]{:S(2)}, u32[]{:S(2)}) collective-permute-start(bf16[256,768]{1,0:T(8,128)(2,1)} %bitcast.173), channel_id=1, source_target_pairs={{0,4},{1,5},{2,6},{3,7},{8,12},{9,13},{10,14},{11,15},{16,20},{17,... | collective-permute-start | bytes 1179656 | tf_op jit(solution)/shard_map/ppermute | solution.py:55
  20.9 1.6 collective-permute-start.4
  25.9 12.6 %collective-permute-done.3 = bf16[256,768]{1,0:T(8,128)(2,1)S(1)} collective-permute-done((bf16[256,768]{1,0:T(8,128)(2,1)}, bf16[256,768]{1,0:T(8,128)(2,1)S(1)}, u32[]{:S(2)}, u32[]{:S(2)}) %collective-permute-start.3) | collective-permute-done | bytes 393248 | tf_op jit(solution)/shard_map/ppermute | solution.py:55
  39.3 16.1 %collective-permute-start.7 = (bf16[256,768]{1,0:T(8,128)(2,1)S(1)}, bf16[256,768]{1,0:T(8,128)(2,1)S(1)}, u32[]{:S(2)}, u32[]{:S(2)}) collective-permute-start(bf16[256,768]{1,0:T(8,128)(2,1)S(1)} %broadcast_select_fusion.refs_0_), channel_id=1, source_target_pairs={{0,2},{1,3},{2,0},{3,1},{4,6},{5,7},{6,4},{7,5},{8,10},{9,11},{10,... | collective-permute-start | bytes 1179656 | tf_op jit(solution)/shard_map/ppermute | solution.py:51
  55.4 1.2 collective-permute-start.8
  56.7 1.6 collective-permute-start.6
  58.9 10.8 %collective-permute-done.5 = bf16[4,32,768]{2,1,0:T(8,128)(2,1)S(1)} collective-permute-done((bf16[4,32,768]{2,1,0:T(8,128)(2,1)S(1)}, bf16[4,32,768]{2,1,0:T(8,128)(2,1)S(1)}, u32[]{:S(2)}, u32[]{:S(2)}) %collective-permute-start.5) | collective-permute-done | bytes 196640 | tf_op jit(solution)/shard_map/ppermute | solution.py:51
  69.7 5.6 %collective-permute-done.7.refs_1_ = bf16[256,768]{1,0:T(8,128)(2,1)S(1)} collective-permute-done((bf16[256,768]{1,0:T(8,128)(2,1)S(1)}, bf16[256,768]{1,0:T(8,128)(2,1)S(1)}, u32[]{:S(2)}, u32[]{:S(2)}) %collective-permute-start.7) | collective-permute-done | bytes 393248 | tf_op jit(solution)/shard_map/ppermute | solution.py:51
  75.3 1.1 collective-permute-start.11
  76.4 1.9 collective-permute-start.10
  78.9 12.0 %collective-permute-done.10 = bf16[8,32,768]{2,1,0:T(8,128)(2,1)S(1)} collective-permute-done((bf16[8,32,768]{2,1,0:T(8,128)(2,1)S(1)}, bf16[8,32,768]{2,1,0:T(8,128)(2,1)S(1)}, u32[]{:S(2)}, u32[]{:S(2)}) %collective-permute-start.10) | collective-permute-done | bytes 393248 | tf_op jit(solution)/shard_map/ppermute | solution.py:51
  91.0 7.2 %collective-permute-done.11 = bf16[8,48,768]{2,1,0:T(8,128)(2,1)S(1)} collective-permute-done((bf16[8,48,768]{2,1,0:T(8,128)(2,1)S(1)}, bf16[8,48,768]{2,1,0:T(8,128)(2,1)S(1)}, u32[]{:S(2)}, u32[]{:S(2)}) %collective-permute-start.11) | collective-permute-done | bytes 589856 | tf_op jit(solution)/shard_map/ppermute | solution.py:51
  98.4 13.9 %collective-permute-done.12.refs_3_ = bf16[256,768]{1,0:T(8,128)(2,1)S(1)} collective-permute-done((bf16[256,768]{1,0:T(8,128)(2,1)S(1)}, bf16[256,768]{1,0:T(8,128)(2,1)S(1)}, u32[]{:S(2)}, u32[]{:S(2)}) %collective-permute-start.12) | collective-permute-done | bytes 393248 | tf_op jit(solution)/shard_map/ppermute | solution.py:51
  114.7 1.4 collective-permute-done.13.refs_11_
  117.3 22.2 %attention.1 = (bf16[32,72,768]{2,1,0:T(8,128)(2,1)}, bf16[256,768]{1,0:T(8,128)(2,1)}, bf16[1024,768]{1,0:T(8,128)(2,1)}, bf16[1024,768]{1,0:T(8,128)(2,1)}, bf...) custom-call(bf16[256,768]{1,0:T(8,128)(2,1)} %copy-done.7, ...), custom_call_target="tpu_custom_call" | custom-call | flops 9865003008 | bytes 12582912 | tf_op jit(solution)/shard_map/attention/pallas_call | solution.py:352
  139.5 1.1 slice.258
  141.7 21.6 %middle.1 = (bf16[256,768]{1,0:T(8,128)(2,1)}, f32[256,768]{1,0:T(8,128)}, bf16[256,768]{1,0:T(8,128)(2,1)}, bf16[32,216,768]{2,1,0:T(8,128)(2,1)}, f32[8,768]{1,0:T(8,128)}, /*index=5*/f32[8,768]{1,0:T(8,128)}) custom-call(bf16[256,768]{1,0:T(8,128)(2,1)} %get-tuple-element.119.ctx_ref.refs_2_, bf16[256,768]{1,0:T(8,128)(2,1)} %bitcast.177, ...), custom_call_target="tpu_custom_call" | custom-call | flops 8153726976 | bytes 33554432 | tf_op jit(solution)/shard_map/middle/pallas_call | solution.py:553
  163.6 18.6 %attention_back.2 = (bf16[1024,768]{1,0:T(8,128)(2,1)}, bf16[1024,768]{1,0:T(8,128)(2,1)}, f32[768,256]{1,0:T(8,128)}) custom-call(s32[1]{0:T(128)} %bitcast.9.refs_7_.refs_0_.near_ref, bf16[256,768]{1,0:T(8,128)(2,1)} %get-tuple-element.123.refs_1_, bf16[256,768]{1,0:T(8,128)(2,1)} %get-tuple-element.119.ctx_ref.refs_2_, ...), custom_call_target="tpu_custom_call" | custom-call | flops 16106127360 | bytes 6291456 | tf_op jit(solution)/shard_map/attention_back/pallas_call | solution.py:647
  182.2 23.9 %reduce-scatter.4.cloned.1.call-done = bf16[16,216,768]{2,1,0:T(8,128)(2,1)} async-done(((bf16[32,216,768]{2,1,0:T(8,128)(2,1)}), bf16[16,216,768]{2,1,0:T(8,128)(2,1)}) %reduce-scatter.4.cloned.1.call-update) | async-done | bytes 5308432 | tf_op jit(solution)/shard_map/reduce_scatter | solution.py:902
  207.5 6.4 %token_product.2 = bf16[4,256,768]{2,1,0:T(8,128)(2,1)} custom-call(s32[1]{0:T(128)} %bitcast.9.refs_7_.refs_0_.near_ref, bf16[1024,768]{1,0:T(8,128)(2,1)} %get-tuple-element.131.dk_ref.refs_13_, bf16[1024,768]{1,0:T(8,128)(2,1)} %get-tuple-element.132.dv_ref.refs_14_, bf16[32,72,768]{2,1,0:T(8,128)(2,1)} %get-tuple-element.133.wk_ref.wv_ref.refs_11_, ...), custom_call_target="tpu_custom_call" | custom-call | flops 2415919104 | bytes 4718592 | tf_op jit(solution)/shard_map/token_product/pallas_call | solution.py:680
  213.9 1.2 slice_bitcast_fusion
  215.1 1.9 collective-permute-start.15
  217.2 5.6 %attention_back.3 = (bf16[768,768]{1,0:T(8,128)(2,1)}, bf16[768,768]{1,0:T(8,128)(2,1)}, f32[768,256]{1,0:T(8,128)}) custom-call(s32[1]{0:T(128)} %bitcast.9.refs_7_.refs_0_.near_ref, bf16[256,768]{1,0:T(8,128)(2,1)} %get-tuple-element.123.refs_1_, bf16[256,768]{1,0:T(8,128)(2,1)} %get-tuple-element.119.ctx_ref.refs_2_, ...), custom_call_target="tpu_custom_call" | custom-call | flops 12079595520 | bytes 4718592 | tf_op jit(solution)/shard_map/attention_back/pallas_call | solution.py:647
  222.8 12.2 %collective-permute-done.15 = bf16[256,768]{1,0:T(8,128)(2,1)S(1)} collective-permute-done((bf16[256,768]{1,0:T(8,128)(2,1)S(1)}, bf16[256,768]{1,0:T(8,128)(2,1)S(1)}, u32[]{:S(2)}, u32[]{:S(2)}) %collective-permute-start.15) | collective-permute-done | bytes 393248 | tf_op jit(solution)/shard_map/ppermute | solution.py:51
  234.9 16.2 %collective-permute-done.16 = bf16[256,768]{1,0:T(8,128)(2,1)S(1)} collective-permute-done((bf16[256,768]{1,0:T(8,128)(2,1)S(1)}, bf16[256,768]{1,0:T(8,128)(2,1)S(1)}, u32[]{:S(2)}, u32[]{:S(2)}) %collective-permute-start.16) | collective-permute-done | bytes 393248 | tf_op jit(solution)/shard_map/ppermute | solution.py:51
  251.3 2.2 collective-permute-start.17
  253.5 14.7 %weight_product.1 = (bf16[16,24,768]{2,1,0:T(8,128)(2,1)}, bf16[16,24,768]{2,1,0:T(8,128)(2,1)}, bf16[16,24,1536]{2,1,0:T(8,128)(2,1)}, bf16[16,24,1536]{2,1,0:T...) custom-call(bf16[256,768]{1,0:T(8,128)(2,1)} %copy-done.7, bf16[256,768]{1,0:T(8,128)(2,1)} %copy-done.14, ...), custom_call_target="tpu_custom_call" | custom-call | flops 4227858432 | bytes 16515072 | tf_op jit(solution)/shard_map/weight_product/pallas_call | solution.py:758
  272.7 1.3 collective-permute-start.28
  274.0 1.3 pad_maximum_fusion.2
  275.3 4.1 %token_product.3 = bf16[3,256,768]{2,1,0:T(8,128)(2,1)} custom-call(s32[1]{0:T(128)} %bitcast.9.refs_7_.refs_0_.near_ref, bf16[768,768]{1,0:T(8,128)(2,1)} %get-tuple-element.158.refs_15_.dk_ref, bf16[768,768]{1,0:T(8,128)(2,1)} %get-tuple-element.159.refs_16_.dv_ref, bf16[32,72,768]{2,1,0:T(8,128)(2,1)} %get-tuple-element.133.wk_ref.wv_ref.refs_11_, ...), custom_call_target="tpu_custom_call" | custom-call | flops 1811939328 | bytes 3538944 | tf_op jit(solution)/shard_map/token_product/pallas_call | solution.py:680
  279.4 1.3 slice_bitcast_fusion.5
  280.7 1.8 collective-permute-start.22
  283.7 1.1 add_convert_fusion.2
  284.8 1.6 collective-permute-start.20
  286.4 1.0 constant_dynamic-slice_fusion.11
  287.5 8.9 %collective-permute-done.22 = bf16[256,768]{1,0:T(8,128)(2,1)S(1)} collective-permute-done((bf16[256,768]{1,0:T(8,128)(2,1)S(1)}, bf16[256,768]{1,0:T(8,128)(2,1)S(1)}, u32[]{:S(2)}, u32[]{:S(2)}) %collective-permute-start.22) | collective-permute-done | bytes 393248 | tf_op jit(solution)/shard_map/ppermute | solution.py:51
  296.4 1.1 fusion
  297.6 11.2 %collective-permute-done.21 = bf16[8,24,1536]{2,1,0:T(8,128)(2,1)S(1)} collective-permute-done((bf16[8,24,1536]{2,1,0:T(8,128)(2,1)S(1)}, bf16[8,24,1536]{2,1,0:T(8,128)(2,1)S(1)}, u32[]{:S(2)}, u32[]{:S(2)}) %collective-permute-start.21) | collective-permute-done | bytes 589856 | tf_op jit(solution)/shard_map/ppermute | solution.py:51
  308.9 1.6 collective-permute-start.25
  311.3 5.6 %collective-permute-done.24 = bf16[4,32,768]{2,1,0:T(8,128)(2,1)S(1)} collective-permute-done((bf16[4,32,768]{2,1,0:T(8,128)(2,1)S(1)}, bf16[4,32,768]{2,1,0:T(8,128)(2,1)S(1)}, u32[]{:S(2)}, u32[]{:S(2)}) %collective-permute-start.24) | collective-permute-done | bytes 196640 | tf_op jit(solution)/shard_map/ppermute | solution.py:51
  318.0 13.2 %collective-permute-start.27 = (bf16[2,24,1536]{2,1,0:T(8,128)(2,1)S(1)}, bf16[2,24,1536]{2,1,0:T(8,128)(2,1)S(1)}, u32[]{:S(2)}, u32[]{:S(2)}) collective-permute-start(bf16[2,24,1536]{2,1,0:T(8,128)(2,1)S(1)} %bitcast.234), channel_id=1, source_target_pairs={{0,4},{1,5},{2,6},{3,7},{4,0},{5,1},{6,2},{7,3},{8,12},{9,13},{10,... | collective-permute-start | bytes 442376 | tf_op jit(solution)/shard_map/ppermute | solution.py:51
  331.3 17.7 %collective-permute-done.26 = bf16[2,32,768]{2,1,0:T(8,128)(2,1)S(1)} collective-permute-done((bf16[2,32,768]{2,1,0:T(8,128)(2,1)S(1)}, bf16[2,32,768]{2,1,0:T(8,128)(2,1)S(1)}, u32[]{:S(2)}, u32[]{:S(2)}) %collective-permute-start.26) | collective-permute-done | bytes 98336 | tf_op jit(solution)/shard_map/ppermute | solution.py:51
  349.1 3.2 collective-permute-start.30
  352.4 1.9 fusion.3
  354.3 7.1 %collective-permute-done.29 = bf16[1,32,768]{2,1,0:T(8,128)(2,1)S(1)} collective-permute-done((bf16[1,32,768]{2,1,0:T(8,128)(2,1)S(1)}, bf16[1,32,768]{2,1,0:T(8,128)(2,1)S(1)}, u32[]{:S(2)}, u32[]{:S(2)}) %collective-permute-start.29) | collective-permute-done | bytes 49184 | tf_op jit(solution)/shard_map/ppermute | solution.py:51
  (174 shorter events, 30.2 us)
Async XLA Ops:
  7.2 31.3 %copy-start.1 = (bf16[1,256,768]{2,1,0:T(8,128)(2,1)S(1)}, bf16[1,256,768]{2,1,0:T(8,128)(2,1)}, u32[]{:S(2)}) copy-start(bf16[1,256,768]{2,1,0:T(8,128)(2,1)} %param.18) | copy-start | bytes 1179652
  7.2 132.2 %all-gather.2.cloned.1.call-start = ((), (), s32[]{:S(2)}) async-start(), calls=%async_computation.3 | async-start | bytes 11354112 | tf_op jit(solution)/shard_map/all_gather | solution.py:828
  11.3 194.8 %reduce-scatter.4.cloned.1.call-start = ((), (), s32[]{:S(2)}) async-start(), calls=%async_computation.4 | async-start | bytes 15925248 | tf_op jit(solution)/shard_map/reduce_scatter | solution.py:902
  11.4 27.9 %collective-permute-start = (bf16[80,768]{1,0:T(8,128)(2,1)}, bf16[80,768]{1,0:T(8,128)(2,1)S(1)}, u32[]{:S(2)}, u32[]{:S(2)}) collective-permute-start(bf16[80,768]{1,0:T(8,128)(2,1)} %get-tuple-element.105), channel_id=1, source_target_pairs={{0,2},{1,3},{2,0},{3,1},{4,6},{5,7},{6,4},{7,5},{8,10},{9,11},{10,... | collective-permute-start | bytes 368648 | tf_op jit(solution)/shard_map/ppermute | solution.py:51
  14.5 24.8 %collective-permute-start.1 = (bf16[80,768]{1,0:T(8,128)(2,1)}, bf16[80,768]{1,0:T(8,128)(2,1)S(1)}, u32[]{:S(2)}, u32[]{:S(2)}) collective-permute-start(bf16[80,768]{1,0:T(8,128)(2,1)} %get-tuple-element.105), channel_id=1, source_target_pairs={{0,4},{1,5},{2,6},{3,7},{4,0},{5,1},{6,2},{7,3},{8,12},{9,13},{10,... | collective-permute-start | bytes 368648 | tf_op jit(solution)/shard_map/ppermute | solution.py:51
  17.1 22.2 %collective-permute-start.2 = (bf16[80,768]{1,0:T(8,128)(2,1)}, bf16[80,768]{1,0:T(8,128)(2,1)S(1)}, u32[]{:S(2)}, u32[]{:S(2)}) collective-permute-start(bf16[80,768]{1,0:T(8,128)(2,1)} %get-tuple-element.105), channel_id=1, source_target_pairs={{0,6},{1,7},{2,4},{3,5},{4,2},{5,3},{6,0},{7,1},{8,14},{9,15},{10,... | collective-permute-start | bytes 368648 | tf_op jit(solution)/shard_map/ppermute | solution.py:51
  17.1 21.4 %collective-permute-start.3 = (bf16[256,768]{1,0:T(8,128)(2,1)}, bf16[256,768]{1,0:T(8,128)(2,1)S(1)}, u32[]{:S(2)}, u32[]{:S(2)}) collective-permute-start(bf16[256,768]{1,0:T(8,128)(2,1)} %bitcast.173), channel_id=1, source_target_pairs={{0,4},{1,5},{2,6},{3,7},{8,12},{9,13},{10,14},{11,15},{16,20},{17,... | collective-permute-start | bytes 1179656 | tf_op jit(solution)/shard_map/ppermute | solution.py:55
  20.9 18.4 %collective-permute-start.4 = (bf16[256,768]{1,0:T(8,128)(2,1)}, bf16[256,768]{1,0:T(8,128)(2,1)S(1)}, u32[]{:S(2)}, u32[]{:S(2)}) collective-permute-start(bf16[256,768]{1,0:T(8,128)(2,1)} %bitcast.174), channel_id=1, source_target_pairs={{0,1},{1,0},{2,3},{3,2},{4,5},{5,4},{6,7},{7,6},{8,9},{9,8},{10,11... | collective-permute-start | bytes 1179656 | tf_op jit(solution)/shard_map/ppermute | solution.py:51
  38.5 31.2 %collective-permute-start.9 = (bf16[256,768]{1,0:T(8,128)(2,1)S(1)}, bf16[256,768]{1,0:T(8,128)(2,1)S(1)}, u32[]{:S(2)}, u32[]{:S(2)}) collective-permute-start(bf16[256,768]{1,0:T(8,128)(2,1)S(1)} %bitcast.180), channel_id=1, source_target_pairs={{5,6},{6,5},{13,14},{14,13},{21,22},{22,21},{29,30},{30,29}} | collective-permute-start | bytes 1179656 | tf_op jit(solution)/shard_map/ppermute | solution.py:55
  39.2 19.7 %copy-start.7 = (bf16[256,768]{1,0:T(8,128)(2,1)}, bf16[256,768]{1,0:T(8,128)(2,1)S(1)}, u32[]{:S(2)}) copy-start(bf16[256,768]{1,0:T(8,128)(2,1)S(1)} %broadcast_select_fusion.refs_0_) | copy-start | bytes 1179652
  39.3 19.0 %copy-start.12 = (bf16[256,768]{1,0:T(8,128)(2,1)}, bf16[256,768]{1,0:T(8,128)(2,1)S(1)}, u32[]{:S(2)}) copy-start(bf16[256,768]{1,0:T(8,128)(2,1)S(1)} %collective-permute-done.4.refs_5_) | copy-start | bytes 1179652
  39.3 36.0 %collective-permute-start.7 = (bf16[256,768]{1,0:T(8,128)(2,1)S(1)}, bf16[256,768]{1,0:T(8,128)(2,1)S(1)}, u32[]{:S(2)}, u32[]{:S(2)}) collective-permute-start(bf16[256,768]{1,0:T(8,128)(2,1)S(1)} %broadcast_select_fusion.refs_0_), channel_id=1, source_target_pairs={{0,2},{1,3},{2,0},{3,1},{4,6},{5,7},{6,4},{7,5},{8,10},{9,11},{10,... | collective-permute-start | bytes 1179656 | tf_op jit(solution)/shard_map/ppermute | solution.py:51
  55.4 19.9 %collective-permute-start.8 = (bf16[256,768]{1,0:T(8,128)(2,1)S(1)}, bf16[256,768]{1,0:T(8,128)(2,1)S(1)}, u32[]{:S(2)}, u32[]{:S(2)}) collective-permute-start(bf16[256,768]{1,0:T(8,128)(2,1)S(1)} %broadcast_select_fusion.refs_0_), channel_id=1, source_target_pairs={{0,1},{1,0},{2,3},{3,2},{4,5},{5,4},{6,7},{7,6},{8,9},{9,8},{10,11... | collective-permute-start | bytes 1179656 | tf_op jit(solution)/shard_map/ppermute | solution.py:51
  56.7 13.0 %collective-permute-start.6 = (bf16[4,48,768]{2,1,0:T(8,128)(2,1)S(1)}, bf16[4,48,768]{2,1,0:T(8,128)(2,1)S(1)}, u32[]{:S(2)}, u32[]{:S(2)}) collective-permute-start(bf16[4,48,768]{2,1,0:T(8,128)(2,1)S(1)} %pad_maximum_fusion.4), channel_id=1, source_target_pairs={{0,16},{1,17},{2,18},{3,19},{4,20},{5,21},{6,22},{7,23},{8,24},{9,... | collective-permute-start | bytes 884744 | tf_op jit(solution)/shard_map/ppermute | solution.py:51
  58.3 11.3 %collective-permute-start.5 = (bf16[4,32,768]{2,1,0:T(8,128)(2,1)S(1)}, bf16[4,32,768]{2,1,0:T(8,128)(2,1)S(1)}, u32[]{:S(2)}, u32[]{:S(2)}) collective-permute-start(bf16[4,32,768]{2,1,0:T(8,128)(2,1)S(1)} %pad_maximum_fusion.6), channel_id=1, source_target_pairs={{0,1},{1,0},{2,3},{3,2},{4,5},{5,4},{6,7},{7,6},{8,9},{9,8},{10,11... | collective-permute-start | bytes 589832 | tf_op jit(solution)/shard_map/ppermute | solution.py:51
  69.7 28.6 %copy-start.13 = (bf16[256,768]{1,0:T(8,128)(2,1)}, bf16[256,768]{1,0:T(8,128)(2,1)S(1)}, u32[]{:S(2)}) copy-start(bf16[256,768]{1,0:T(8,128)(2,1)S(1)} %collective-permute-done.9.refs_6_) | copy-start | bytes 1179652
  75.3 23.1 %copy-start.14 = (bf16[256,768]{1,0:T(8,128)(2,1)}, bf16[256,768]{1,0:T(8,128)(2,1)S(1)}, u32[]{:S(2)}) copy-start(bf16[256,768]{1,0:T(8,128)(2,1)S(1)} %collective-permute-done.7.refs_1_) | copy-start | bytes 1179652
  75.3 3.6 copy-start.15
  75.3 22.9 %collective-permute-start.11 = (bf16[8,48,768]{2,1,0:T(8,128)(2,1)S(1)}, bf16[8,48,768]{2,1,0:T(8,128)(2,1)S(1)}, u32[]{:S(2)}, u32[]{:S(2)}) collective-permute-start(bf16[8,48,768]{2,1,0:T(8,128)(2,1)S(1)} %constant_dynamic-update-slice_fusion.5), channel_id=1, source_target_pairs={{0,1},{1,0},{2,3},{3,2},{4,5},{5,4},{6,7},{7,6},{8,9},{9,8},{10,11... | collective-permute-start | bytes 1769480 | tf_op jit(solution)/shard_map/ppermute | solution.py:51
  76.4 14.5 %collective-permute-start.10 = (bf16[8,32,768]{2,1,0:T(8,128)(2,1)S(1)}, bf16[8,32,768]{2,1,0:T(8,128)(2,1)S(1)}, u32[]{:S(2)}, u32[]{:S(2)}) collective-permute-start(bf16[8,32,768]{2,1,0:T(8,128)(2,1)S(1)} %constant_dynamic-update-slice_fusion), channel_id=1, source_target_pairs={{0,16},{1,17},{2,18},{3,19},{4,20},{5,21},{6,22},{7,23},{8,24},{9,... | collective-permute-start | bytes 1179656 | tf_op jit(solution)/shard_map/ppermute | solution.py:51
  78.3 33.9 %collective-permute-start.12 = (bf16[256,768]{1,0:T(8,128)(2,1)S(1)}, bf16[256,768]{1,0:T(8,128)(2,1)S(1)}, u32[]{:S(2)}, u32[]{:S(2)}) collective-permute-start(bf16[256,768]{1,0:T(8,128)(2,1)S(1)} %collective-permute-done.7.refs_1_), channel_id=1, source_target_pairs={{0,1},{1,0},{2,3},{3,2},{4,5},{5,4},{6,7},{7,6},{8,9},{9,8},{10,11... | collective-permute-start | bytes 1179656 | tf_op jit(solution)/shard_map/ppermute | solution.py:51
  91.0 21.8 %copy-start.4 = (bf16[16,32,768]{2,1,0:T(8,128)(2,1)}, bf16[16,32,768]{2,1,0:T(8,128)(2,1)S(1)}, u32[]{:S(2)}) copy-start(bf16[16,32,768]{2,1,0:T(8,128)(2,1)S(1)} %pad_maximum_fusion.1.refs_10_) | copy-start | bytes 2359300
  91.0 21.8 %copy-start.17 = (s32[1,8]{1,0:T(1,128)S(1)}, s32[1,8]{1,0:T(1,128)}, u32[]{:S(2)}) copy-start(s32[1,8]{1,0:T(1,128)} %param.19) | copy-start | bytes 100
  98.4 17.9 %copy-start.2 = (bf16[16,48,768]{2,1,0:T(8,128)(2,1)}, bf16[16,48,768]{2,1,0:T(8,128)(2,1)S(1)}, u32[]{:S(2)}) copy-start(bf16[16,48,768]{2,1,0:T(8,128)(2,1)S(1)} %pad_maximum_fusion.refs_12_) | copy-start | bytes 3538948
  112.3 4.0 %copy-start.16 = (bf16[256,768]{1,0:T(8,128)(2,1)}, bf16[256,768]{1,0:T(8,128)(2,1)S(1)}, u32[]{:S(2)}) copy-start(bf16[256,768]{1,0:T(8,128)(2,1)S(1)} %collective-permute-done.12.refs_3_) | copy-start | bytes 1179652
  112.3 4.0 %collective-permute-start.14 = (bf16[16,48,768]{2,1,0:T(8,128)(2,1)S(1)}, bf16[16,48,768]{2,1,0:T(8,128)(2,1)S(1)}, u32[]{:S(2)}, u32[]{:S(2)}) collective-permute-start(bf16[16,48,768]{2,1,0:T(8,128)(2,1)S(1)} %pad_maximum_fusion.refs_12_), channel_id=1, source_target_pairs={{0,8},{1,9},{2,10},{3,11},{4,12},{5,13},{6,14},{7,15},{8,0},{9,1},... | collective-permute-start | bytes 3538952 | tf_op jit(solution)/shard_map/ppermute | solution.py:51
  112.3 3.8 %collective-permute-start.13 = (bf16[16,32,768]{2,1,0:T(8,128)(2,1)S(1)}, bf16[16,32,768]{2,1,0:T(8,128)(2,1)}, u32[]{:S(2)}, u32[]{:S(2)}) collective-permute-start(bf16[16,32,768]{2,1,0:T(8,128)(2,1)S(1)} %pad_maximum_fusion.1.refs_10_), channel_id=1, source_target_pairs={{0,8},{1,9},{2,10},{3,11},{4,12},{5,13},{6,14},{7,15},{8,0},{9,1},... | collective-permute-start | bytes 2359304 | tf_op jit(solution)/shard_map/ppermute | solution.py:51
  163.3 154.4 %reduce-scatter.6.cloned.1.call-start = ((), (), s32[]{:S(2)}) async-start(), calls=%async_computation.5 | async-start | bytes 6635520 | tf_op jit(solution)/shard_map/reduce_scatter | solution.py:902
  206.2 159.7 %reduce-scatter.8.cloned.1.call-start = ((), (), s32[]{:S(2)}) async-start(), calls=%async_computation.6 | async-start | bytes 1658880 | tf_op jit(solution)/shard_map/reduce_scatter | solution.py:902
  215.1 19.8 %collective-permute-start.15 = (bf16[256,768]{1,0:T(8,128)(2,1)S(1)}, bf16[256,768]{1,0:T(8,128)(2,1)S(1)}, u32[]{:S(2)}, u32[]{:S(2)}) collective-permute-start(bf16[256,768]{1,0:T(8,128)(2,1)S(1)} %get-tuple-element.198), channel_id=1, source_target_pairs={{0,1},{1,0},{2,3},{3,2},{4,5},{5,4},{6,7},{7,6},{8,9},{9,8},{10,11... | collective-permute-start | bytes 1179656 | tf_op jit(solution)/shard_map/ppermute | solution.py:51
  217.0 34.2 %collective-permute-start.16 = (bf16[256,768]{1,0:T(8,128)(2,1)S(1)}, bf16[256,768]{1,0:T(8,128)(2,1)S(1)}, u32[]{:S(2)}, u32[]{:S(2)}) collective-permute-start(bf16[256,768]{1,0:T(8,128)(2,1)S(1)} %get-tuple-element.197), channel_id=1, source_target_pairs={{0,1},{1,0},{2,3},{3,2},{4,5},{5,4},{6,7},{7,6},{8,9},{9,8},{10,11... | collective-permute-start | bytes 1179656 | tf_op jit(solution)/shard_map/ppermute | solution.py:51
  217.2 34.0 %copy-start = (bf16[4,256,768]{2,1,0:T(8,128)(2,1)S(1)}, bf16[4,256,768]{2,1,0:T(8,128)(2,1)}, u32[]{:S(2)}) copy-start(bf16[4,256,768]{2,1,0:T(8,128)(2,1)} %token_product.2) | copy-start | bytes 4718596
  251.3 16.9 %collective-permute-start.17 = (bf16[256,768]{1,0:T(8,128)(2,1)S(1)}, bf16[256,768]{1,0:T(8,128)(2,1)S(1)}, u32[]{:S(2)}, u32[]{:S(2)}) collective-permute-start(bf16[256,768]{1,0:T(8,128)(2,1)S(1)} %get-tuple-element.195), channel_id=1, source_target_pairs={{0,2},{1,3},{2,0},{3,1},{4,6},{5,7},{6,4},{7,5},{8,10},{9,11},{10,... | collective-permute-start | bytes 1179656 | tf_op jit(solution)/shard_map/ppermute | solution.py:51
  268.4 11.0 %collective-permute-start.19 = (bf16[16,24,1536]{2,1,0:T(8,128)(2,1)}, bf16[16,24,1536]{2,1,0:T(8,128)(2,1)S(1)}, u32[]{:S(2)}, u32[]{:S(2)}) collective-permute-start(bf16[16,24,1536]{2,1,0:T(8,128)(2,1)} %get-tuple-element.157), channel_id=1, source_target_pairs={{0,8},{1,9},{2,10},{3,11},{4,12},{5,13},{6,14},{7,15},{8,0},{9,1},... | collective-permute-start | bytes 3538952 | tf_op jit(solution)/shard_map/ppermute | solution.py:51
  271.4 7.9 %collective-permute-start.18 = (bf16[16,32,768]{2,1,0:T(8,128)(2,1)S(1)}, bf16[16,32,768]{2,1,0:T(8,128)(2,1)}, u32[]{:S(2)}, u32[]{:S(2)}) collective-permute-start(bf16[16,32,768]{2,1,0:T(8,128)(2,1)S(1)} %pad_maximum_fusion.3), channel_id=1, source_target_pairs={{0,8},{1,9},{2,10},{3,11},{4,12},{5,13},{6,14},{7,15},{8,0},{9,1},... | collective-permute-start | bytes 2359304 | tf_op jit(solution)/shard_map/ppermute | solution.py:51
  272.7 58.6 %collective-permute-start.28 = (bf16[256,768]{1,0:T(8,128)(2,1)}, bf16[256,768]{1,0:T(8,128)(2,1)}, u32[]{:S(2)}, u32[]{:S(2)}) collective-permute-start(bf16[256,768]{1,0:T(8,128)(2,1)} %convert_element_type.353), channel_id=1, source_target_pairs={{4,0},{5,1},{6,2},{7,3},{12,8},{13,9},{14,10},{15,11},{20,16},{21,... | collective-permute-start | bytes 1179656 | tf_op jit(solution)/shard_map/ppermute | solution.py:55
  279.4 3.8 copy-start.3
  280.7 15.8 %collective-permute-start.22 = (bf16[256,768]{1,0:T(8,128)(2,1)S(1)}, bf16[256,768]{1,0:T(8,128)(2,1)S(1)}, u32[]{:S(2)}, u32[]{:S(2)}) collective-permute-start(bf16[256,768]{1,0:T(8,128)(2,1)S(1)} %get-tuple-element.199), channel_id=1, source_target_pairs={{0,1},{1,0},{2,3},{3,2},{4,5},{5,4},{6,7},{7,6},{8,9},{9,8},{10,11... | collective-permute-start | bytes 1179656 | tf_op jit(solution)/shard_map/ppermute | solution.py:51
  282.5 14.0 %collective-permute-start.23 = (bf16[256,768]{1,0:T(8,128)(2,1)S(1)}, bf16[256,768]{1,0:T(8,128)(2,1)S(1)}, u32[]{:S(2)}, u32[]{:S(2)}) collective-permute-start(bf16[256,768]{1,0:T(8,128)(2,1)S(1)} %get-tuple-element.200), channel_id=1, source_target_pairs={{5,6},{6,5},{13,14},{14,13},{21,22},{22,21},{29,30},{30,29}} | collective-permute-start | bytes 1179656 | tf_op jit(solution)/shard_map/ppermute | solution.py:55
  283.3 25.5 %collective-permute-start.21 = (bf16[8,24,1536]{2,1,0:T(8,128)(2,1)S(1)}, bf16[8,24,1536]{2,1,0:T(8,128)(2,1)S(1)}, u32[]{:S(2)}, u32[]{:S(2)}) collective-permute-start(bf16[8,24,1536]{2,1,0:T(8,128)(2,1)S(1)} %fusion.2), channel_id=1, source_target_pairs={{0,1},{1,0},{2,3},{3,2},{4,5},{5,4},{6,7},{7,6},{8,9},{9,8},{10,11... | collective-permute-start | bytes 1769480 | tf_op jit(solution)/shard_map/ppermute | solution.py:51
  284.8 12.8 %collective-permute-start.20 = (bf16[8,32,768]{2,1,0:T(8,128)(2,1)S(1)}, bf16[8,32,768]{2,1,0:T(8,128)(2,1)S(1)}, u32[]{:S(2)}, u32[]{:S(2)}) collective-permute-start(bf16[8,32,768]{2,1,0:T(8,128)(2,1)S(1)} %bitcast.225), channel_id=1, source_target_pairs={{0,16},{1,17},{2,18},{3,19},{4,20},{5,21},{6,22},{7,23},{8,24},{9,... | collective-permute-start | bytes 1179656 | tf_op jit(solution)/shard_map/ppermute | solution.py:51
  308.9 8.8 %collective-permute-start.25 = (bf16[4,24,1536]{2,1,0:T(8,128)(2,1)S(1)}, bf16[4,24,1536]{2,1,0:T(8,128)(2,1)S(1)}, u32[]{:S(2)}, u32[]{:S(2)}) collective-permute-start(bf16[4,24,1536]{2,1,0:T(8,128)(2,1)S(1)} %bitcast.230), channel_id=1, source_target_pairs={{0,16},{1,17},{2,18},{3,19},{4,20},{5,21},{6,22},{7,23},{8,24},{9,... | collective-permute-start | bytes 884744 | tf_op jit(solution)/shard_map/ppermute | solution.py:51
  310.5 6.4 %collective-permute-start.24 = (bf16[4,32,768]{2,1,0:T(8,128)(2,1)S(1)}, bf16[4,32,768]{2,1,0:T(8,128)(2,1)S(1)}, u32[]{:S(2)}, u32[]{:S(2)}) collective-permute-start(bf16[4,32,768]{2,1,0:T(8,128)(2,1)S(1)} %fusion.4), channel_id=1, source_target_pairs={{0,1},{1,0},{2,3},{3,2},{4,5},{5,4},{6,7},{7,6},{8,9},{9,8},{10,11... | collective-permute-start | bytes 589832 | tf_op jit(solution)/shard_map/ppermute | solution.py:51
  317.9 34.5 %copy-start.5 = (f32[256,768]{1,0:T(8,128)S(1)}, f32[256,768]{1,0:T(8,128)}, u32[]{:S(2)}) copy-start(f32[256,768]{1,0:T(8,128)} %get-tuple-element.144) | copy-start | bytes 2359300
  318.0 31.1 %collective-permute-start.27 = (bf16[2,24,1536]{2,1,0:T(8,128)(2,1)S(1)}, bf16[2,24,1536]{2,1,0:T(8,128)(2,1)S(1)}, u32[]{:S(2)}, u32[]{:S(2)}) collective-permute-start(bf16[2,24,1536]{2,1,0:T(8,128)(2,1)S(1)} %bitcast.234), channel_id=1, source_target_pairs={{0,4},{1,5},{2,6},{3,7},{4,0},{5,1},{6,2},{7,3},{8,12},{9,13},{10,... | collective-permute-start | bytes 442376 | tf_op jit(solution)/shard_map/ppermute | solution.py:51
  331.2 17.8 %collective-permute-start.26 = (bf16[2,32,768]{2,1,0:T(8,128)(2,1)S(1)}, bf16[2,32,768]{2,1,0:T(8,128)(2,1)S(1)}, u32[]{:S(2)}, u32[]{:S(2)}) collective-permute-start(bf16[2,32,768]{2,1,0:T(8,128)(2,1)S(1)} %bitcast.238), channel_id=1, source_target_pairs={{0,4},{1,5},{2,6},{3,7},{4,0},{5,1},{6,2},{7,3},{8,12},{9,13},{10,... | collective-permute-start | bytes 294920 | tf_op jit(solution)/shard_map/ppermute | solution.py:51
  349.1 14.2 %collective-permute-start.30 = (bf16[1,24,1536]{2,1,0:T(8,128)(2,1)S(1)}, bf16[1,24,1536]{2,1,0:T(8,128)(2,1)S(1)}, u32[]{:S(2)}, u32[]{:S(2)}) collective-permute-start(bf16[1,24,1536]{2,1,0:T(8,128)(2,1)S(1)} %add_convert_fusion.7), channel_id=1, source_target_pairs={{0,2},{1,3},{2,0},{3,1},{4,6},{5,7},{6,4},{7,5},{8,10},{9,11},{10,... | collective-permute-start | bytes 221192 | tf_op jit(solution)/shard_map/ppermute | solution.py:51
  352.3 9.1 %collective-permute-start.29 = (bf16[1,32,768]{2,1,0:T(8,128)(2,1)S(1)}, bf16[1,32,768]{2,1,0:T(8,128)(2,1)S(1)}, u32[]{:S(2)}, u32[]{:S(2)}) collective-permute-start(bf16[1,32,768]{2,1,0:T(8,128)(2,1)S(1)} %add_convert_fusion.8), channel_id=1, source_target_pairs={{0,2},{1,3},{2,0},{3,1},{4,6},{5,7},{6,4},{7,5},{8,10},{9,11},{10,... | collective-permute-start | bytes 147464 | tf_op jit(solution)/shard_map/ppermute | solution.py:51
  (5 other events, 8.4 us)
Sparse Core Ops, SparseCore 0:
  11.5 126.9 all-gather.1
  163.5 42.6 reduce-scatter.3
  209.4 84.1 reduce-scatter.5
  317.9 47.9 reduce-scatter.7

commit v9 on v8

--- a/solution.py
+++ b/solution.py
@@ -843,17 +843,17 @@
             cut = step + 8
             one = jnp.stack([v[:cut] for v in (first_pack, *away)])
             two = jnp.stack([v[cut:] for v in (first_pack, *away)])
-            one, two = stage(one, plan.y[0]), stage(two, plan.x[0])
+            one, two = stage(one, plan.x[0]), stage(two, plan.y[0])
             one, two, *seen = tie(one, two, *exchange.stage_two())
             exchange.other, exchange.same_y, exchange.diagonal = seen
-            one, two = stage(one, plan.x[0]), stage(two, plan.y[0])
+            one, two = stage(one, plan.y[0]), stage(two, plan.x[0])
             exchange.stage_three()
             one, two, exchange.other_y = tie(one, two, exchange.other_y)
             pieces = [one, plan.swap(one, plan.core[0]), two, plan.swap(two, plan.core[0])]
             order = lambda *bits: ([(bit, 1 << i) for i, bit in enumerate(bits)], plan.core[0])
             places = (
+                order(*plan.z, plan.x[0], plan.y[0]),
                 order(*plan.z, plan.y[0], plan.x[0]),
-                order(*plan.z, plan.x[0], plan.y[0]),
             )
             me = plan.me().astype(jnp.int32).reshape(1)
         else:
@@ -917,16 +917,14 @@
             0, parts, None, near, grad_context, context, queries, keys_n, values_n, log_total,
             seg_own, seg_near, dqp,
         )
-        returned.same, dkn, dvn, dq = tie(returned.same, dkn, dvn, dq)
-        returned.prompt_two()
         q_send, q_keep, kv_send, kv_keep, grad_own, sums_qkv = weight_call(
             spots, first_near, near, own, dq, squares, grad_h1, dkp, dvp, dkn, dvn, core, runs
         )
         q_send, q_keep, kv_send, kv_keep, returned.same, dkn, dvn = tie(
             q_send, q_keep, kv_send, kv_keep, returned.same, dkn, dvn
         )
+        returned.prompt_two()
         shared_n = product_call(None, near, dkn, dvn, squares, rows)
-        returned.prompt_three()
 
         order = (6, 5, 3, 4, 2, 0, 1)
         small = len(early) + len(late) - 1
@@ -954,13 +952,14 @@
             n = len(r_q.terms)
             held = [*r_q.terms, *r_kv.terms]
             if one == plan.x[0]:
-                *held, shared_n = tie(*held, shared_n)
+                *held, shared_n, returned.same = tie(*held, shared_n, returned.same)
                 returned.near(shared_n)
+                returned.prompt_three()
             elif one == plan.y[0]:
-                *held, returned.own = tie(*held, returned.own)
+                *held, grads, returned.own = tie(*held, grads, returned.own)
+                grads = level(grads, "z")
             elif one == plan.z[-1]:
-                *held, grads = tie(*held, grads)
-                grads = level(grads, "z")
+                held = tie(*held)
             else:
                 *held, returned.back = tie(*held, returned.back)
             r_q.terms, r_kv.terms = held[:n], held[n:]

time: 377 us -> 370 us (0.981)
  waiting for transfers between devices: 168 us -> 157 us
    ppermute x27, waiting for transfers between devices: 131 us -> 122 us  [swap(): return lax.ppermute(value, AXES, [(i, i ^ mask) for i in range(self.count)])]
  transfers between devices with their start and end apart: 35 -> 35, of which waited for: 18 -> 18; matrix products, arithmetic and copies ran while one was open for 6% -> 7% of each run, Pallas kernels for 19% -> 19%
where the time goes in v9:
time: 370 us; the launch traced here: 368 us
  waiting for transfers between devices  157 us (42%)
  Pallas kernels  95.3 us (26%)
  starting transfers between devices  64.4 us (17%)
  local copies, waits for them, and re-layouts  20.8 us (6%)
  other arithmetic  16.6 us (4%)
  between operations  14.5 us (4%)
    ppermute x27, waiting for transfers between devices, swap(): return lax.ppermute(value, AXES, [(i, i ^ mask) for i in range(self.count)])  122 us
    ppermute x27, starting transfers between devices, swap(): return lax.ppermute(value, AXES, [(i, i ^ mask) for i in range(self.count)])  57.6 us
    pallas_call x2, Pallas kernels, back_call(): pl.pallas_call(functools.partial(back_kernel, rows, bound, dq0 is not Non...  24.1 us
    pallas_call x1, Pallas kernels, attention_call(): pl.pallas_call(functools.partial(attention_kernel, blocks, first, rows, p...  22.3 us
    reduce_scatter x3, waiting for transfers between devices, per_device(): lax.psum_scatter(value, axes, scatter_dimension=0, tiled=True)  21.8 us
    pallas_call x1, Pallas kernels, middle_call(): pl.pallas_call(functools.partial(middle_kernel, wide, mapped), grid=(2 *...  21.7 us
    pallas_call x1, Pallas kernels, weight_call(): pl.pallas_call(functools.partial(weight_kernel, blocks, first, rows, runs...  14.8 us
    ppermute x4, waiting for transfers between devices, send(): return lax.ppermute(value, AXES, pairs)  12.6 us
  transfers between devices with their start and end apart: 35, of which 18 were waited for; matrix products, arithmetic and copies ran while one was open for 7% of the time, Pallas kernels for 19%

profile of v9, /device:TPU:0, one launch (start us, length us, event | category | flops | bytes accessed | tf_op | source)
XLA Modules:
  0.0 368.2 jit_solution(1043350692406479409)
XLA Ops:
  9.5 1.8 pack.1
  11.4 3.1 collective-permute-start
  14.5 2.6 collective-permute-start.1
  17.1 3.8 %collective-permute-start.3 = (bf16[256,768]{1,0:T(8,128)(2,1)}, bf16[256,768]{1,0:T(8,128)(2,1)S(1)}, u32[]{:S(2)}, u32[]{:S(2)}) collective-permute-start(bf16[256,768]{1,0:T(8,128)(2,1)} %bitcast.173), channel_id=1, source_target_pairs={{0,4},{1,5},{2,6},{3,7},{8,12},{9,13},{10,14},{11,15},{16,20},{17,... | collective-permute-start | bytes 1179656 | tf_op jit(solution)/shard_map/ppermute | solution.py:55
  20.9 1.6 collective-permute-start.4
  25.9 12.6 %collective-permute-done.3 = bf16[256,768]{1,0:T(8,128)(2,1)S(1)} collective-permute-done((bf16[256,768]{1,0:T(8,128)(2,1)}, bf16[256,768]{1,0:T(8,128)(2,1)S(1)}, u32[]{:S(2)}, u32[]{:S(2)}) %collective-permute-start.3) | collective-permute-done | bytes 393248 | tf_op jit(solution)/shard_map/ppermute | solution.py:55
  39.3 16.1 %collective-permute-start.7 = (bf16[256,768]{1,0:T(8,128)(2,1)S(1)}, bf16[256,768]{1,0:T(8,128)(2,1)S(1)}, u32[]{:S(2)}, u32[]{:S(2)}) collective-permute-start(bf16[256,768]{1,0:T(8,128)(2,1)S(1)} %broadcast_select_fusion.refs_0_), channel_id=1, source_target_pairs={{0,2},{1,3},{2,0},{3,1},{4,6},{5,7},{6,4},{7,5},{8,10},{9,11},{10,... | collective-permute-start | bytes 1179656 | tf_op jit(solution)/shard_map/ppermute | solution.py:51
  55.4 1.2 collective-permute-start.8
  57.6 1.2 collective-permute-start.5
  58.9 7.3 %collective-permute-done.5 = bf16[4,32,768]{2,1,0:T(8,128)(2,1)S(1)} collective-permute-done((bf16[4,32,768]{2,1,0:T(8,128)(2,1)S(1)}, bf16[4,32,768]{2,1,0:T(8,128)(2,1)S(1)}, u32[]{:S(2)}, u32[]{:S(2)}) %collective-permute-start.5) | collective-permute-done | bytes 196640 | tf_op jit(solution)/shard_map/ppermute | solution.py:51
  66.2 5.6 %collective-permute-done.6 = bf16[4,48,768]{2,1,0:T(8,128)(2,1)S(1)} collective-permute-done((bf16[4,48,768]{2,1,0:T(8,128)(2,1)S(1)}, bf16[4,48,768]{2,1,0:T(8,128)(2,1)S(1)}, u32[]{:S(2)}, u32[]{:S(2)}) %collective-permute-start.6) | collective-permute-done | bytes 294944 | tf_op jit(solution)/shard_map/ppermute | solution.py:51
  71.8 3.5 collective-permute-done.7.refs_1_
  76.2 1.5 collective-permute-start.11
  77.6 1.5 collective-permute-start.10
  79.7 14.8 %collective-permute-done.10 = bf16[8,32,768]{2,1,0:T(8,128)(2,1)S(1)} collective-permute-done((bf16[8,32,768]{2,1,0:T(8,128)(2,1)S(1)}, bf16[8,32,768]{2,1,0:T(8,128)(2,1)S(1)}, u32[]{:S(2)}, u32[]{:S(2)}) %collective-permute-start.10) | collective-permute-done | bytes 393248 | tf_op jit(solution)/shard_map/ppermute | solution.py:51
  94.6 3.9 %collective-permute-done.11 = bf16[8,48,768]{2,1,0:T(8,128)(2,1)S(1)} collective-permute-done((bf16[8,48,768]{2,1,0:T(8,128)(2,1)S(1)}, bf16[8,48,768]{2,1,0:T(8,128)(2,1)S(1)}, u32[]{:S(2)}, u32[]{:S(2)}) %collective-permute-start.11) | collective-permute-done | bytes 589856 | tf_op jit(solution)/shard_map/ppermute | solution.py:51
  98.6 10.9 %collective-permute-done.12.refs_3_ = bf16[256,768]{1,0:T(8,128)(2,1)S(1)} collective-permute-done((bf16[256,768]{1,0:T(8,128)(2,1)S(1)}, bf16[256,768]{1,0:T(8,128)(2,1)S(1)}, u32[]{:S(2)}, u32[]{:S(2)}) %collective-permute-start.12) | collective-permute-done | bytes 393248 | tf_op jit(solution)/shard_map/ppermute | solution.py:51
  111.9 1.3 collective-permute-done.13.refs_11_
  114.6 22.3 %attention.1 = (bf16[32,72,768]{2,1,0:T(8,128)(2,1)}, bf16[256,768]{1,0:T(8,128)(2,1)}, bf16[1024,768]{1,0:T(8,128)(2,1)}, bf16[1024,768]{1,0:T(8,128)(2,1)}, bf...) custom-call(bf16[256,768]{1,0:T(8,128)(2,1)} %copy-done.8, ...), custom_call_target="tpu_custom_call" | custom-call | flops 9865003008 | bytes 12582912 | tf_op jit(solution)/shard_map/attention/pallas_call | solution.py:352
  139.2 21.7 %middle.1 = (bf16[256,768]{1,0:T(8,128)(2,1)}, f32[256,768]{1,0:T(8,128)}, bf16[256,768]{1,0:T(8,128)(2,1)}, bf16[32,216,768]{2,1,0:T(8,128)(2,1)}, f32[8,768]{1,0:T(8,128)}, /*index=5*/f32[8,768]{1,0:T(8,128)}) custom-call(bf16[256,768]{1,0:T(8,128)(2,1)} %get-tuple-element.116.ctx_ref.refs_2_, bf16[256,768]{1,0:T(8,128)(2,1)} %bitcast.177, ...), custom_call_target="tpu_custom_call" | custom-call | flops 8153726976 | bytes 33554432 | tf_op jit(solution)/shard_map/middle/pallas_call | solution.py:553
  161.1 18.6 %attention_back.2 = (bf16[1024,768]{1,0:T(8,128)(2,1)}, bf16[1024,768]{1,0:T(8,128)(2,1)}, f32[768,256]{1,0:T(8,128)}) custom-call(s32[1]{0:T(128)} %bitcast.9.refs_7_.refs_0_.near_ref, bf16[256,768]{1,0:T(8,128)(2,1)} %get-tuple-element.119.refs_1_, bf16[256,768]{1,0:T(8,128)(2,1)} %get-tuple-element.116.ctx_ref.refs_2_, ...), custom_call_target="tpu_custom_call" | custom-call | flops 16106127360 | bytes 6291456 | tf_op jit(solution)/shard_map/attention_back/pallas_call | solution.py:647
  179.7 21.8 %reduce-scatter.4.cloned.1.call-done = bf16[16,216,768]{2,1,0:T(8,128)(2,1)} async-done(((bf16[32,216,768]{2,1,0:T(8,128)(2,1)}), bf16[16,216,768]{2,1,0:T(8,128)(2,1)}) %reduce-scatter.4.cloned.1.call-update) | async-done | bytes 5308432 | tf_op jit(solution)/shard_map/reduce_scatter | solution.py:902
  202.8 6.5 %token_product.2 = bf16[4,256,768]{2,1,0:T(8,128)(2,1)} custom-call(s32[1]{0:T(128)} %bitcast.9.refs_7_.refs_0_.near_ref, bf16[1024,768]{1,0:T(8,128)(2,1)} %get-tuple-element.134.refs_13_.dk_ref, bf16[1024,768]{1,0:T(8,128)(2,1)} %get-tuple-element.135.refs_14_.dv_ref, bf16[32,72,768]{2,1,0:T(8,128)(2,1)} %get-tuple-element.132.refs_11_.wk_ref.wv_ref, ...), custom_call_target="tpu_custom_call" | custom-call | flops 2415919104 | bytes 4718592 | tf_op jit(solution)/shard_map/token_product/pallas_call | solution.py:680
  209.3 1.2 slice_bitcast_fusion
  210.4 1.9 collective-permute-start.15
  212.5 5.6 %attention_back.3 = (bf16[768,768]{1,0:T(8,128)(2,1)}, bf16[768,768]{1,0:T(8,128)(2,1)}, f32[768,256]{1,0:T(8,128)}) custom-call(s32[1]{0:T(128)} %bitcast.9.refs_7_.refs_0_.near_ref, bf16[256,768]{1,0:T(8,128)(2,1)} %get-tuple-element.119.refs_1_, bf16[256,768]{1,0:T(8,128)(2,1)} %get-tuple-element.116.ctx_ref.refs_2_, ...), custom_call_target="tpu_custom_call" | custom-call | flops 12079595520 | bytes 4718592 | tf_op jit(solution)/shard_map/attention_back/pallas_call | solution.py:647
  218.1 14.8 %weight_product.1 = (bf16[16,24,768]{2,1,0:T(8,128)(2,1)}, bf16[16,24,768]{2,1,0:T(8,128)(2,1)}, bf16[16,24,1536]{2,1,0:T(8,128)(2,1)}, bf16[16,24,1536]{2,1,0:T...) custom-call(bf16[256,768]{1,0:T(8,128)(2,1)} %copy-done.8, bf16[256,768]{1,0:T(8,128)(2,1)} %copy-done.15, ...), custom_call_target="tpu_custom_call" | custom-call | flops 4227858432 | bytes 16515072 | tf_op jit(solution)/shard_map/weight_product/pallas_call | solution.py:758
  232.9 13.6 %collective-permute-done.18 = bf16[256,768]{1,0:T(8,128)(2,1)S(1)} collective-permute-done((bf16[256,768]{1,0:T(8,128)(2,1)S(1)}, bf16[256,768]{1,0:T(8,128)(2,1)S(1)}, u32[]{:S(2)}, u32[]{:S(2)}) %collective-permute-start.18) | collective-permute-done | bytes 393248 | tf_op jit(solution)/shard_map/ppermute | solution.py:51
  251.2 2.1 collective-permute-start.19
  253.3 1.1 pad_maximum_fusion.2
  254.5 4.1 %token_product.3 = bf16[3,256,768]{2,1,0:T(8,128)(2,1)} custom-call(s32[1]{0:T(128)} %bitcast.9.refs_7_.refs_0_.near_ref, bf16[768,768]{1,0:T(8,128)(2,1)} %get-tuple-element.150.refs_15_.dk_ref, bf16[768,768]{1,0:T(8,128)(2,1)} %get-tuple-element.151.refs_16_.dv_ref, bf16[32,72,768]{2,1,0:T(8,128)(2,1)} %get-tuple-element.132.refs_11_.wk_ref.wv_ref, ...), custom_call_target="tpu_custom_call" | custom-call | flops 1811939328 | bytes 3538944 | tf_op jit(solution)/shard_map/token_product/pallas_call | solution.py:680
  258.6 4.4 %collective-permute-done.19 = bf16[256,768]{1,0:T(8,128)(2,1)} collective-permute-done((bf16[256,768]{1,0:T(8,128)(2,1)}, bf16[256,768]{1,0:T(8,128)(2,1)}, u32[]{:S(2)}, u32[]{:S(2)}) %collective-permute-start.19) | collective-permute-done | bytes 393248 | tf_op jit(solution)/shard_map/ppermute | solution.py:51
  263.0 1.1 convert_add_fusion.3
  264.1 2.1 collective-permute-start.22
  267.6 1.1 add_convert_fusion.2
  268.7 1.5 collective-permute-start.20
  272.0 1.3 collective-permute-start.28
  273.4 10.3 %collective-permute-done.22 = bf16[256,768]{1,0:T(8,128)(2,1)S(1)} collective-permute-done((bf16[256,768]{1,0:T(8,128)(2,1)S(1)}, bf16[256,768]{1,0:T(8,128)(2,1)S(1)}, u32[]{:S(2)}, u32[]{:S(2)}) %collective-permute-start.22) | collective-permute-done | bytes 393248 | tf_op jit(solution)/shard_map/ppermute | solution.py:51
  283.9 4.6 %collective-permute-done.20 = bf16[8,32,768]{2,1,0:T(8,128)(2,1)} collective-permute-done((bf16[8,32,768]{2,1,0:T(8,128)(2,1)S(1)}, bf16[8,32,768]{2,1,0:T(8,128)(2,1)}, u32[]{:S(2)}, u32[]{:S(2)}) %collective-permute-start.20) | collective-permute-done | bytes 393248 | tf_op jit(solution)/shard_map/ppermute | solution.py:51
  288.5 13.2 %collective-permute-done.21 = bf16[8,24,1536]{2,1,0:T(8,128)(2,1)} collective-permute-done((bf16[8,24,1536]{2,1,0:T(8,128)(2,1)S(1)}, bf16[8,24,1536]{2,1,0:T(8,128)(2,1)}, u32[]{:S(2)}, u32[]{:S(2)}) %collective-permute-start.21) | collective-permute-done | bytes 589856 | tf_op jit(solution)/shard_map/ppermute | solution.py:51
  301.8 1.1 add_convert_fusion.3
  302.9 1.5 collective-permute-start.25
  306.4 1.8 collective-permute-start.24
  309.2 2.9 collective-permute-done.24
  312.3 12.6 %collective-permute-start.27 = (bf16[2,24,1536]{2,1,0:T(8,128)(2,1)S(1)}, bf16[2,24,1536]{2,1,0:T(8,128)(2,1)S(1)}, u32[]{:S(2)}, u32[]{:S(2)}) collective-permute-start(bf16[2,24,1536]{2,1,0:T(8,128)(2,1)S(1)} %bitcast.230), channel_id=1, source_target_pairs={{0,4},{1,5},{2,6},{3,7},{4,0},{5,1},{6,2},{7,3},{8,12},{9,13},{10,... | collective-permute-start | bytes 442376 | tf_op jit(solution)/shard_map/ppermute | solution.py:51
  325.2 24.5 %collective-permute-done.26 = bf16[2,32,768]{2,1,0:T(8,128)(2,1)S(1)} collective-permute-done((bf16[2,32,768]{2,1,0:T(8,128)(2,1)S(1)}, bf16[2,32,768]{2,1,0:T(8,128)(2,1)S(1)}, u32[]{:S(2)}, u32[]{:S(2)}) %collective-permute-start.26) | collective-permute-done | bytes 98336 | tf_op jit(solution)/shard_map/ppermute | solution.py:51
  350.0 2.1 collective-permute-start.29
  352.0 1.9 fusion.3
  (176 shorter events, 36.3 us)
Async XLA Ops:
  7.2 31.3 %copy-start.2 = (bf16[1,256,768]{2,1,0:T(8,128)(2,1)S(1)}, bf16[1,256,768]{2,1,0:T(8,128)(2,1)}, u32[]{:S(2)}) copy-start(bf16[1,256,768]{2,1,0:T(8,128)(2,1)} %param.18) | copy-start | bytes 1179652
  7.2 129.8 %all-gather.2.cloned.1.call-start = ((), (), s32[]{:S(2)}) async-start(), calls=%async_computation.3 | async-start | bytes 11354112 | tf_op jit(solution)/shard_map/all_gather | solution.py:828
  11.3 190.1 %reduce-scatter.4.cloned.1.call-start = ((), (), s32[]{:S(2)}) async-start(), calls=%async_computation.4 | async-start | bytes 15925248 | tf_op jit(solution)/shard_map/reduce_scatter | solution.py:902
  11.4 27.8 %collective-permute-start = (bf16[80,768]{1,0:T(8,128)(2,1)}, bf16[80,768]{1,0:T(8,128)(2,1)S(1)}, u32[]{:S(2)}, u32[]{:S(2)}) collective-permute-start(bf16[80,768]{1,0:T(8,128)(2,1)} %get-tuple-element.102), channel_id=1, source_target_pairs={{0,2},{1,3},{2,0},{3,1},{4,6},{5,7},{6,4},{7,5},{8,10},{9,11},{10,... | collective-permute-start | bytes 368648 | tf_op jit(solution)/shard_map/ppermute | solution.py:51
  14.5 24.8 %collective-permute-start.1 = (bf16[80,768]{1,0:T(8,128)(2,1)}, bf16[80,768]{1,0:T(8,128)(2,1)S(1)}, u32[]{:S(2)}, u32[]{:S(2)}) collective-permute-start(bf16[80,768]{1,0:T(8,128)(2,1)} %get-tuple-element.102), channel_id=1, source_target_pairs={{0,4},{1,5},{2,6},{3,7},{4,0},{5,1},{6,2},{7,3},{8,12},{9,13},{10,... | collective-permute-start | bytes 368648 | tf_op jit(solution)/shard_map/ppermute | solution.py:51
  17.1 22.2 %collective-permute-start.2 = (bf16[80,768]{1,0:T(8,128)(2,1)}, bf16[80,768]{1,0:T(8,128)(2,1)S(1)}, u32[]{:S(2)}, u32[]{:S(2)}) collective-permute-start(bf16[80,768]{1,0:T(8,128)(2,1)} %get-tuple-element.102), channel_id=1, source_target_pairs={{0,6},{1,7},{2,4},{3,5},{4,2},{5,3},{6,0},{7,1},{8,14},{9,15},{10,... | collective-permute-start | bytes 368648 | tf_op jit(solution)/shard_map/ppermute | solution.py:51
  17.1 21.4 %collective-permute-start.3 = (bf16[256,768]{1,0:T(8,128)(2,1)}, bf16[256,768]{1,0:T(8,128)(2,1)S(1)}, u32[]{:S(2)}, u32[]{:S(2)}) collective-permute-start(bf16[256,768]{1,0:T(8,128)(2,1)} %bitcast.173), channel_id=1, source_target_pairs={{0,4},{1,5},{2,6},{3,7},{8,12},{9,13},{10,14},{11,15},{16,20},{17,... | collective-permute-start | bytes 1179656 | tf_op jit(solution)/shard_map/ppermute | solution.py:55
  20.9 18.4 %collective-permute-start.4 = (bf16[256,768]{1,0:T(8,128)(2,1)}, bf16[256,768]{1,0:T(8,128)(2,1)S(1)}, u32[]{:S(2)}, u32[]{:S(2)}) collective-permute-start(bf16[256,768]{1,0:T(8,128)(2,1)} %bitcast.174), channel_id=1, source_target_pairs={{0,1},{1,0},{2,3},{3,2},{4,5},{5,4},{6,7},{7,6},{8,9},{9,8},{10,11... | collective-permute-start | bytes 1179656 | tf_op jit(solution)/shard_map/ppermute | solution.py:51
  38.5 33.3 %collective-permute-start.9 = (bf16[256,768]{1,0:T(8,128)(2,1)S(1)}, bf16[256,768]{1,0:T(8,128)(2,1)S(1)}, u32[]{:S(2)}, u32[]{:S(2)}) collective-permute-start(bf16[256,768]{1,0:T(8,128)(2,1)S(1)} %bitcast.180), channel_id=1, source_target_pairs={{5,6},{6,5},{13,14},{14,13},{21,22},{22,21},{29,30},{30,29}} | collective-permute-start | bytes 1179656 | tf_op jit(solution)/shard_map/ppermute | solution.py:55
  39.2 19.6 %copy-start.8 = (bf16[256,768]{1,0:T(8,128)(2,1)}, bf16[256,768]{1,0:T(8,128)(2,1)S(1)}, u32[]{:S(2)}) copy-start(bf16[256,768]{1,0:T(8,128)(2,1)S(1)} %broadcast_select_fusion.refs_0_) | copy-start | bytes 1179652
  39.3 19.6 %copy-start.13 = (bf16[256,768]{1,0:T(8,128)(2,1)}, bf16[256,768]{1,0:T(8,128)(2,1)S(1)}, u32[]{:S(2)}) copy-start(bf16[256,768]{1,0:T(8,128)(2,1)S(1)} %collective-permute-done.4.refs_5_) | copy-start | bytes 1179652
  39.3 36.0 %collective-permute-start.7 = (bf16[256,768]{1,0:T(8,128)(2,1)S(1)}, bf16[256,768]{1,0:T(8,128)(2,1)S(1)}, u32[]{:S(2)}, u32[]{:S(2)}) collective-permute-start(bf16[256,768]{1,0:T(8,128)(2,1)S(1)} %broadcast_select_fusion.refs_0_), channel_id=1, source_target_pairs={{0,2},{1,3},{2,0},{3,1},{4,6},{5,7},{6,4},{7,5},{8,10},{9,11},{10,... | collective-permute-start | bytes 1179656 | tf_op jit(solution)/shard_map/ppermute | solution.py:51
  55.4 19.9 %collective-permute-start.8 = (bf16[256,768]{1,0:T(8,128)(2,1)S(1)}, bf16[256,768]{1,0:T(8,128)(2,1)S(1)}, u32[]{:S(2)}, u32[]{:S(2)}) collective-permute-start(bf16[256,768]{1,0:T(8,128)(2,1)S(1)} %broadcast_select_fusion.refs_0_), channel_id=1, source_target_pairs={{0,1},{1,0},{2,3},{3,2},{4,5},{5,4},{6,7},{7,6},{8,9},{9,8},{10,11... | collective-permute-start | bytes 1179656 | tf_op jit(solution)/shard_map/ppermute | solution.py:51
  56.7 15.1 %collective-permute-start.6 = (bf16[4,48,768]{2,1,0:T(8,128)(2,1)S(1)}, bf16[4,48,768]{2,1,0:T(8,128)(2,1)S(1)}, u32[]{:S(2)}, u32[]{:S(2)}) collective-permute-start(bf16[4,48,768]{2,1,0:T(8,128)(2,1)S(1)} %pad_maximum_fusion.4), channel_id=1, source_target_pairs={{0,1},{1,0},{2,3},{3,2},{4,5},{5,4},{6,7},{7,6},{8,9},{9,8},{10,11... | collective-permute-start | bytes 884744 | tf_op jit(solution)/shard_map/ppermute | solution.py:51
  57.6 8.6 %collective-permute-start.5 = (bf16[4,32,768]{2,1,0:T(8,128)(2,1)S(1)}, bf16[4,32,768]{2,1,0:T(8,128)(2,1)S(1)}, u32[]{:S(2)}, u32[]{:S(2)}) collective-permute-start(bf16[4,32,768]{2,1,0:T(8,128)(2,1)S(1)} %pad_maximum_fusion.6), channel_id=1, source_target_pairs={{0,16},{1,17},{2,18},{3,19},{4,20},{5,21},{6,22},{7,23},{8,24},{9,... | collective-permute-start | bytes 589832 | tf_op jit(solution)/shard_map/ppermute | solution.py:51
  71.8 26.7 %copy-start.14 = (bf16[256,768]{1,0:T(8,128)(2,1)}, bf16[256,768]{1,0:T(8,128)(2,1)S(1)}, u32[]{:S(2)}) copy-start(bf16[256,768]{1,0:T(8,128)(2,1)S(1)} %collective-permute-done.9.refs_6_) | copy-start | bytes 1179652
  75.3 23.2 %copy-start.15 = (bf16[256,768]{1,0:T(8,128)(2,1)}, bf16[256,768]{1,0:T(8,128)(2,1)S(1)}, u32[]{:S(2)}) copy-start(bf16[256,768]{1,0:T(8,128)(2,1)S(1)} %collective-permute-done.7.refs_1_) | copy-start | bytes 1179652
  76.2 22.3 %collective-permute-start.11 = (bf16[8,48,768]{2,1,0:T(8,128)(2,1)S(1)}, bf16[8,48,768]{2,1,0:T(8,128)(2,1)S(1)}, u32[]{:S(2)}, u32[]{:S(2)}) collective-permute-start(bf16[8,48,768]{2,1,0:T(8,128)(2,1)S(1)} %constant_dynamic-update-slice_fusion.5), channel_id=1, source_target_pairs={{0,16},{1,17},{2,18},{3,19},{4,20},{5,21},{6,22},{7,23},{8,24},{9,... | collective-permute-start | bytes 1769480 | tf_op jit(solution)/shard_map/ppermute | solution.py:51
  77.6 16.8 %collective-permute-start.10 = (bf16[8,32,768]{2,1,0:T(8,128)(2,1)S(1)}, bf16[8,32,768]{2,1,0:T(8,128)(2,1)S(1)}, u32[]{:S(2)}, u32[]{:S(2)}) collective-permute-start(bf16[8,32,768]{2,1,0:T(8,128)(2,1)S(1)} %constant_dynamic-update-slice_fusion), channel_id=1, source_target_pairs={{0,1},{1,0},{2,3},{3,2},{4,5},{5,4},{6,7},{7,6},{8,9},{9,8},{10,11... | collective-permute-start | bytes 1179656 | tf_op jit(solution)/shard_map/ppermute | solution.py:51
  79.1 30.4 %collective-permute-start.12 = (bf16[256,768]{1,0:T(8,128)(2,1)S(1)}, bf16[256,768]{1,0:T(8,128)(2,1)S(1)}, u32[]{:S(2)}, u32[]{:S(2)}) collective-permute-start(bf16[256,768]{1,0:T(8,128)(2,1)S(1)} %collective-permute-done.7.refs_1_), channel_id=1, source_target_pairs={{0,1},{1,0},{2,3},{3,2},{4,5},{5,4},{6,7},{7,6},{8,9},{9,8},{10,11... | collective-permute-start | bytes 1179656 | tf_op jit(solution)/shard_map/ppermute | solution.py:51
  94.5 15.5 %copy-start.5 = (bf16[16,32,768]{2,1,0:T(8,128)(2,1)}, bf16[16,32,768]{2,1,0:T(8,128)(2,1)S(1)}, u32[]{:S(2)}) copy-start(bf16[16,32,768]{2,1,0:T(8,128)(2,1)S(1)} %pad_maximum_fusion.1.refs_10_) | copy-start | bytes 2359300
  94.6 15.4 %copy-start.18 = (s32[1,8]{1,0:T(1,128)S(1)}, s32[1,8]{1,0:T(1,128)}, u32[]{:S(2)}) copy-start(s32[1,8]{1,0:T(1,128)} %param.19) | copy-start | bytes 100
  98.6 15.1 %copy-start.3 = (bf16[16,48,768]{2,1,0:T(8,128)(2,1)}, bf16[16,48,768]{2,1,0:T(8,128)(2,1)S(1)}, u32[]{:S(2)}) copy-start(bf16[16,48,768]{2,1,0:T(8,128)(2,1)S(1)} %pad_maximum_fusion.refs_12_) | copy-start | bytes 3538948
  109.5 4.1 %collective-permute-start.14 = (bf16[16,48,768]{2,1,0:T(8,128)(2,1)S(1)}, bf16[16,48,768]{2,1,0:T(8,128)(2,1)S(1)}, u32[]{:S(2)}, u32[]{:S(2)}) collective-permute-start(bf16[16,48,768]{2,1,0:T(8,128)(2,1)S(1)} %pad_maximum_fusion.refs_12_), channel_id=1, source_target_pairs={{0,8},{1,9},{2,10},{3,11},{4,12},{5,13},{6,14},{7,15},{8,0},{9,1},... | collective-permute-start | bytes 3538952 | tf_op jit(solution)/shard_map/ppermute | solution.py:51
  109.5 3.7 %collective-permute-start.13 = (bf16[16,32,768]{2,1,0:T(8,128)(2,1)S(1)}, bf16[16,32,768]{2,1,0:T(8,128)(2,1)}, u32[]{:S(2)}, u32[]{:S(2)}) collective-permute-start(bf16[16,32,768]{2,1,0:T(8,128)(2,1)S(1)} %pad_maximum_fusion.1.refs_10_), channel_id=1, source_target_pairs={{0,8},{1,9},{2,10},{3,11},{4,12},{5,13},{6,14},{7,15},{8,0},{9,1},... | collective-permute-start | bytes 2359304 | tf_op jit(solution)/shard_map/ppermute | solution.py:51
  160.9 140.8 %reduce-scatter.6.cloned.1.call-start = ((), (), s32[]{:S(2)}) async-start(), calls=%async_computation.5 | async-start | bytes 6635520 | tf_op jit(solution)/shard_map/reduce_scatter | solution.py:902
  201.5 157.0 %reduce-scatter.8.cloned.1.call-start = ((), (), s32[]{:S(2)}) async-start(), calls=%async_computation.6 | async-start | bytes 1658880 | tf_op jit(solution)/shard_map/reduce_scatter | solution.py:902
  210.4 22.4 %collective-permute-start.15 = (bf16[256,768]{1,0:T(8,128)(2,1)S(1)}, bf16[256,768]{1,0:T(8,128)(2,1)S(1)}, u32[]{:S(2)}, u32[]{:S(2)}) collective-permute-start(bf16[256,768]{1,0:T(8,128)(2,1)S(1)} %get-tuple-element.192), channel_id=1, source_target_pairs={{0,1},{1,0},{2,3},{3,2},{4,5},{5,4},{6,7},{7,6},{8,9},{9,8},{10,11... | collective-permute-start | bytes 1179656 | tf_op jit(solution)/shard_map/ppermute | solution.py:51
  212.3 34.2 %collective-permute-start.18 = (bf16[256,768]{1,0:T(8,128)(2,1)S(1)}, bf16[256,768]{1,0:T(8,128)(2,1)S(1)}, u32[]{:S(2)}, u32[]{:S(2)}) collective-permute-start(bf16[256,768]{1,0:T(8,128)(2,1)S(1)} %get-tuple-element.191), channel_id=1, source_target_pairs={{0,1},{1,0},{2,3},{3,2},{4,5},{5,4},{6,7},{7,6},{8,9},{9,8},{10,11... | collective-permute-start | bytes 1179656 | tf_op jit(solution)/shard_map/ppermute | solution.py:51
  218.1 28.4 %copy-start = (bf16[4,256,768]{2,1,0:T(8,128)(2,1)S(1)}, bf16[4,256,768]{2,1,0:T(8,128)(2,1)}, u32[]{:S(2)}) copy-start(bf16[4,256,768]{2,1,0:T(8,128)(2,1)} %token_product.2) | copy-start | bytes 4718596
  232.9 16.2 %copy-start.10 = (bf16[1,768]{1,0:T(2,128)(2,1)S(1)}, bf16[1,768]{1,0:T(2,128)(2,1)}, u32[]{:S(2)}) copy-start(bf16[1,768]{1,0:T(2,128)(2,1)} %get-tuple-element.213) | copy-start | bytes 4612
  232.9 16.2 %copy-start.11 = (bf16[1,768]{1,0:T(2,128)(2,1)S(1)}, bf16[1,768]{1,0:T(2,128)(2,1)}, u32[]{:S(2)}) copy-start(bf16[1,768]{1,0:T(2,128)(2,1)} %get-tuple-element.214) | copy-start | bytes 4612
  247.4 16.6 %collective-permute-start.17 = (bf16[16,24,1536]{2,1,0:T(8,128)(2,1)}, bf16[16,24,1536]{2,1,0:T(8,128)(2,1)S(1)}, u32[]{:S(2)}, u32[]{:S(2)}) collective-permute-start(bf16[16,24,1536]{2,1,0:T(8,128)(2,1)} %get-tuple-element.149), channel_id=1, source_target_pairs={{0,8},{1,9},{2,10},{3,11},{4,12},{5,13},{6,14},{7,15},{8,0},{9,1},... | collective-permute-start | bytes 3538952 | tf_op jit(solution)/shard_map/ppermute | solution.py:51
  250.7 13.3 %collective-permute-start.16 = (bf16[16,32,768]{2,1,0:T(8,128)(2,1)}, bf16[16,32,768]{2,1,0:T(8,128)(2,1)}, u32[]{:S(2)}, u32[]{:S(2)}) collective-permute-start(bf16[16,32,768]{2,1,0:T(8,128)(2,1)} %pad_maximum_fusion.3), channel_id=1, source_target_pairs={{0,8},{1,9},{2,10},{3,11},{4,12},{5,13},{6,14},{7,15},{8,0},{9,1},... | collective-permute-start | bytes 2359304 | tf_op jit(solution)/shard_map/ppermute | solution.py:51
  251.2 11.8 %collective-permute-start.19 = (bf16[256,768]{1,0:T(8,128)(2,1)}, bf16[256,768]{1,0:T(8,128)(2,1)}, u32[]{:S(2)}, u32[]{:S(2)}) collective-permute-start(bf16[256,768]{1,0:T(8,128)(2,1)} %get-tuple-element.189), channel_id=1, source_target_pairs={{0,2},{1,3},{2,0},{3,1},{4,6},{5,7},{6,4},{7,5},{8,10},{9,11},{10,... | collective-permute-start | bytes 1179656 | tf_op jit(solution)/shard_map/ppermute | solution.py:51
  258.6 5.5 %copy-start.1 = (bf16[3,256,768]{2,1,0:T(8,128)(2,1)S(1)}, bf16[3,256,768]{2,1,0:T(8,128)(2,1)}, u32[]{:S(2)}) copy-start(bf16[3,256,768]{2,1,0:T(8,128)(2,1)} %token_product.3) | copy-start | bytes 3538948
  264.1 19.6 %collective-permute-start.22 = (bf16[256,768]{1,0:T(8,128)(2,1)S(1)}, bf16[256,768]{1,0:T(8,128)(2,1)S(1)}, u32[]{:S(2)}, u32[]{:S(2)}) collective-permute-start(bf16[256,768]{1,0:T(8,128)(2,1)S(1)} %get-tuple-element.193), channel_id=1, source_target_pairs={{0,1},{1,0},{2,3},{3,2},{4,5},{5,4},{6,7},{7,6},{8,9},{9,8},{10,11... | collective-permute-start | bytes 1179656 | tf_op jit(solution)/shard_map/ppermute | solution.py:51
  266.3 17.5 %collective-permute-start.23 = (bf16[256,768]{1,0:T(8,128)(2,1)S(1)}, bf16[256,768]{1,0:T(8,128)(2,1)S(1)}, u32[]{:S(2)}, u32[]{:S(2)}) collective-permute-start(bf16[256,768]{1,0:T(8,128)(2,1)S(1)} %get-tuple-element.194), channel_id=1, source_target_pairs={{5,6},{6,5},{13,14},{14,13},{21,22},{22,21},{29,30},{30,29}} | collective-permute-start | bytes 1179656 | tf_op jit(solution)/shard_map/ppermute | solution.py:55
  267.1 34.6 %collective-permute-start.21 = (bf16[8,24,1536]{2,1,0:T(8,128)(2,1)S(1)}, bf16[8,24,1536]{2,1,0:T(8,128)(2,1)}, u32[]{:S(2)}, u32[]{:S(2)}) collective-permute-start(bf16[8,24,1536]{2,1,0:T(8,128)(2,1)S(1)} %fusion.2), channel_id=1, source_target_pairs={{0,1},{1,0},{2,3},{3,2},{4,5},{5,4},{6,7},{7,6},{8,9},{9,8},{10,11... | collective-permute-start | bytes 1769480 | tf_op jit(solution)/shard_map/ppermute | solution.py:51
  268.7 19.9 %collective-permute-start.20 = (bf16[8,32,768]{2,1,0:T(8,128)(2,1)S(1)}, bf16[8,32,768]{2,1,0:T(8,128)(2,1)}, u32[]{:S(2)}, u32[]{:S(2)}) collective-permute-start(bf16[8,32,768]{2,1,0:T(8,128)(2,1)S(1)} %bitcast.221), channel_id=1, source_target_pairs={{0,16},{1,17},{2,18},{3,19},{4,20},{5,21},{6,22},{7,23},{8,24},{9,... | collective-permute-start | bytes 1179656 | tf_op jit(solution)/shard_map/ppermute | solution.py:51
  272.0 53.2 %collective-permute-start.28 = (bf16[256,768]{1,0:T(8,128)(2,1)}, bf16[256,768]{1,0:T(8,128)(2,1)}, u32[]{:S(2)}, u32[]{:S(2)}) collective-permute-start(bf16[256,768]{1,0:T(8,128)(2,1)} %convert_element_type.353), channel_id=1, source_target_pairs={{4,0},{5,1},{6,2},{7,3},{12,8},{13,9},{14,10},{15,11},{20,16},{21,... | collective-permute-start | bytes 1179656 | tf_op jit(solution)/shard_map/ppermute | solution.py:55
  302.9 9.2 %collective-permute-start.25 = (bf16[4,24,1536]{2,1,0:T(8,128)(2,1)S(1)}, bf16[4,24,1536]{2,1,0:T(8,128)(2,1)S(1)}, u32[]{:S(2)}, u32[]{:S(2)}) collective-permute-start(bf16[4,24,1536]{2,1,0:T(8,128)(2,1)S(1)} %bitcast.226), channel_id=1, source_target_pairs={{0,16},{1,17},{2,18},{3,19},{4,20},{5,21},{6,22},{7,23},{8,24},{9,... | collective-permute-start | bytes 884744 | tf_op jit(solution)/shard_map/ppermute | solution.py:51
  306.4 5.7 %collective-permute-start.24 = (bf16[4,32,768]{2,1,0:T(8,128)(2,1)S(1)}, bf16[4,32,768]{2,1,0:T(8,128)(2,1)S(1)}, u32[]{:S(2)}, u32[]{:S(2)}) collective-permute-start(bf16[4,32,768]{2,1,0:T(8,128)(2,1)S(1)} %fusion.4), channel_id=1, source_target_pairs={{0,1},{1,0},{2,3},{3,2},{4,5},{5,4},{6,7},{7,6},{8,9},{9,8},{10,11... | collective-permute-start | bytes 589832 | tf_op jit(solution)/shard_map/ppermute | solution.py:51
  312.3 39.7 %copy-start.6 = (f32[256,768]{1,0:T(8,128)S(1)}, f32[256,768]{1,0:T(8,128)}, u32[]{:S(2)}) copy-start(f32[256,768]{1,0:T(8,128)} %get-tuple-element.138) | copy-start | bytes 2359300
  312.3 37.4 %collective-permute-start.27 = (bf16[2,24,1536]{2,1,0:T(8,128)(2,1)S(1)}, bf16[2,24,1536]{2,1,0:T(8,128)(2,1)S(1)}, u32[]{:S(2)}, u32[]{:S(2)}) collective-permute-start(bf16[2,24,1536]{2,1,0:T(8,128)(2,1)S(1)} %bitcast.230), channel_id=1, source_target_pairs={{0,4},{1,5},{2,6},{3,7},{4,0},{5,1},{6,2},{7,3},{8,12},{9,13},{10,... | collective-permute-start | bytes 442376 | tf_op jit(solution)/shard_map/ppermute | solution.py:51
  325.1 24.7 %collective-permute-start.26 = (bf16[2,32,768]{2,1,0:T(8,128)(2,1)S(1)}, bf16[2,32,768]{2,1,0:T(8,128)(2,1)S(1)}, u32[]{:S(2)}, u32[]{:S(2)}) collective-permute-start(bf16[2,32,768]{2,1,0:T(8,128)(2,1)S(1)} %bitcast.234), channel_id=1, source_target_pairs={{0,4},{1,5},{2,6},{3,7},{4,0},{5,1},{6,2},{7,3},{8,12},{9,13},{10,... | collective-permute-start | bytes 294920 | tf_op jit(solution)/shard_map/ppermute | solution.py:51
  349.8 6.8 %collective-permute-start.30 = (bf16[1,24,1536]{2,1,0:T(8,128)(2,1)S(1)}, bf16[1,24,1536]{2,1,0:T(8,128)(2,1)S(1)}, u32[]{:S(2)}, u32[]{:S(2)}) collective-permute-start(bf16[1,24,1536]{2,1,0:T(8,128)(2,1)S(1)} %add_convert_fusion.7), channel_id=1, source_target_pairs={{0,2},{1,3},{2,0},{3,1},{4,6},{5,7},{6,4},{7,5},{8,10},{9,11},{10,... | collective-permute-start | bytes 221192 | tf_op jit(solution)/shard_map/ppermute | solution.py:51
  350.0 4.8 %collective-permute-start.29 = (bf16[1,32,768]{2,1,0:T(8,128)(2,1)S(1)}, bf16[1,32,768]{2,1,0:T(8,128)(2,1)S(1)}, u32[]{:S(2)}, u32[]{:S(2)}) collective-permute-start(bf16[1,32,768]{2,1,0:T(8,128)(2,1)S(1)} %add_convert_fusion.8), channel_id=1, source_target_pairs={{0,2},{1,3},{2,0},{3,1},{4,6},{5,7},{6,4},{7,5},{8,10},{9,11},{10,... | collective-permute-start | bytes 147464 | tf_op jit(solution)/shard_map/ppermute | solution.py:51
  (6 other events, 11.9 us)
Sparse Core Ops, SparseCore 0:
  11.5 124.3 all-gather.1
  161.0 40.4 reduce-scatter.3
  204.8 94.0 reduce-scatter.5
  301.9 51.2 reduce-scatter.7

commit v10 on v9

--- a/solution.py
+++ b/solution.py
@@ -227,10 +227,9 @@
 def attention_kernel(blocks, first, rows, places, *refs):
     spots = refs[:blocks]
     (near_ref, me_ref, own_ref, a0_ref, a1_ref, b0_ref, b1_ref, segq_ref, segk_ref,
-     w_ref, q_ref, kp_ref, vp_ref, kn_ref, vn_ref, ctx_ref, lse_ref,
-     x_ref, s_ref, line_ref, bias_ref, sems, w_sems) = refs[blocks:]
+     w_out, q_ref, kp_ref, vp_ref, kn_ref, vn_ref, ctx_ref, lse_ref,
+     x_ref, w_ref, s_ref, vt_ref, out_ref, line_ref, bias_ref, sems, w_sems, o_sem) = refs[blocks:]
     near = near_ref[0]
-    at = lambda b: pl.ds(pl.multiple_of(b * rows, rows), rows)
     depth = own_ref.shape[1]
     owners = w_ref.shape[0]
     each = depth // owners
@@ -267,6 +266,7 @@
         weights(lambda c: c.wait())
         for copy in copies:
             copy.wait()
+        pltpu.make_async_copy(w_ref, w_out, o_sem).start()
         line = line_ref[:, 0, :128]
         place = lax.broadcasted_iota(jnp.int32, (128, depth), 0)
         lane = lax.broadcasted_iota(jnp.int32, (128, depth), 1)
@@ -283,59 +283,49 @@
     queries = (mm(own_ref[...], wq) + bias_ref[0:1, lanes]) * (HDIM**-0.5)
     q_ref[...] = queries.astype(BF)
 
-    def project(b, k_ref, v_ref, side):
-        x = x_ref[at(b), :]
-        k_ref[at(side), :] = mm(x, wk).astype(BF)
-        v_ref[at(side), :] = (mm(x, wv) + bias_ref[1:2, lanes]).astype(BF)
-
-    @pl.loop(0, first)
-    def _(b):
-        project(b, kp_ref, vp_ref, b)
-
-    @pl.loop(0, near)
-    def _(b):
-        project(first + b, kn_ref, vn_ref, b)
-
-    width = q_ref.shape[1]
-    heads = width // HDIM
+    heads = part // HDIM
     q = q_ref[...]
-    parts = [jnp.where(heads_mask(q.shape, h), q, 0) for h in range(heads)]
-
-    def scores(b, peaks, k_ref, base):
-        k = k_ref[at(b), :]
-        out = []
+    tall = x_ref.shape[0]
+
+    def body(sets):
+        for k_ref, v_ref, base, size, _ in sets:
+            x = x_ref[base : base + size, :]
+            k_ref[...] = mm(x, wk).astype(BF)
+            v = (mm(x, wv) + bias_ref[1:2, lanes]).astype(BF)
+            v_ref[...] = v
+            vt_ref[:, base : base + size] = v.T
         for h in range(heads):
-            s = nt(k, parts[h])
-            if base:
-                s = jnp.where(segk_ref[at(b), :] == segq_ref[...], s, MASK_FILL)
-            s_ref[h, at(base + b), :] = s
-            out.append(jnp.maximum(peaks[h], jnp.max(s, axis=0, keepdims=True)))
-        return tuple(out)
-
-    peaks = tuple(jnp.full((1, rows), MASK_FILL, F32) for _ in range(heads))
-    peaks = lax.fori_loop(0, first, lambda b, c: scores(b, c, kp_ref, 0), peaks)
-    peaks = lax.fori_loop(0, near, lambda b, c: scores(b, c, kn_ref, first), peaks)
-
-    def mix(b, carry, v_ref, base):
-        totals, mixed = carry
-        vt = v_ref[at(b), :].T
-        new_totals, new_mixed = [], []
-        for h in range(heads):
-            p = jnp.exp(s_ref[h, at(base + b), :] - peaks[h])
-            new_totals.append(totals[h] + jnp.sum(p, axis=0, keepdims=True))
-            new_mixed.append(mixed[h] + mm(vt[h * HDIM : (h + 1) * HDIM], p.astype(BF)))
-        return tuple(new_totals), tuple(new_mixed)
-
-    zero = (
-        tuple(jnp.zeros((1, rows), F32) for _ in range(heads)),
-        tuple(jnp.zeros((HDIM, rows), F32) for _ in range(heads)),
-    )
-    carry = lax.fori_loop(0, first, lambda b, c: mix(b, c, vp_ref, 0), zero)
-    totals, mixed = lax.fori_loop(0, near, lambda b, c: mix(b, c, vn_ref, first), carry)
-    whole = jnp.concatenate([mixed[h] / totals[h] for h in range(heads)], 0)
-    ctx_ref[...] = whole.T.astype(BF)
-    for h in range(heads):
-        lse_ref[0, h : h + 1, :] = peaks[h] + jnp.log(totals[h])
+            q_h = jnp.where(heads_mask(q.shape, h), q, 0)
+            peak = jnp.full((1, rows), MASK_FILL, F32)
+            for k_ref, _, base, size, masked in sets:
+                s = nt(k_ref[...], q_h)
+                if masked:
+                    s = jnp.where(segk_ref[...] == segq_ref[...], s, MASK_FILL)
+                s_ref[h % 2, base : base + size, :] = s
+                peak = jnp.maximum(peak, jnp.max(s, axis=0, keepdims=True))
+            total, mixed = jnp.zeros((1, rows), F32), jnp.zeros((HDIM, rows), F32)
+            for _, _, base, size, _ in sets:
+                p = jnp.exp(s_ref[h % 2, base : base + size, :] - peak)
+                total = total + jnp.sum(p, axis=0, keepdims=True)
+                mixed = mixed + mm(vt_ref[h * HDIM : (h + 1) * HDIM, base : base + size], p.astype(BF))
+            out_ref[h * HDIM : (h + 1) * HDIM, :] = mixed / total
+            lse_ref[0, h : h + 1, :] = peak + jnp.log(total)
+
+    prompt = (kp_ref, vp_ref, 0, PROMPT, False)
+
+    @pl.when(near == 0)
+    def _():
+        body([prompt])
+
+    @pl.when(near > 0)
+    def _():
+        body([prompt, (kn_ref, vn_ref, PROMPT, tall - PROMPT, True)])
+
+    ctx_ref[...] = out_ref[...].T.astype(BF)
+
+    @pl.when(pl.program_id(0) == pl.num_programs(0) - 1)
+    def _():
+        pltpu.make_async_copy(w_ref, w_out, o_sem).wait()
 
 
 def attention_call(spots, first, near, me, own, pieces, places, segq, segk):
@@ -362,7 +352,7 @@
             pl.BlockSpec(segk.shape, lambda g: (0, 0)),
         ],
         out_specs=[
-            pl.BlockSpec((owners, 3 * each, width), lambda g: (0, 0, 0)),
+            pl.BlockSpec(memory_space=pl.ANY),
             cols(rows), cols(PROMPT), cols(PROMPT), cols(tall - PROMPT), cols(tall - PROMPT),
             cols(rows), pl.BlockSpec((1, 8, rows), lambda g: (g, 0, 0)),
         ],
@@ -378,11 +368,15 @@
         ],
         scratch_shapes=[
             pltpu.VMEM((tall, width), BF),
-            pltpu.VMEM((heads, tall, rows), F32),
+            pltpu.VMEM((owners, 3 * each, width), BF),
+            pltpu.VMEM((2, tall, rows), F32),
+            pltpu.VMEM((part, tall), BF),
+            pltpu.VMEM((part, rows), F32),
             pltpu.VMEM((owners, 8, width), BF),
             pltpu.VMEM((8, width), F32),
             pltpu.SemaphoreType.DMA((blocks,)),
             pltpu.SemaphoreType.DMA((3, owners)),
+            pltpu.SemaphoreType.DMA,
         ],
         compiler_params=pltpu.CompilerParams(vmem_limit_bytes=60 * 2**20),
         cost_estimate=pl.CostEstimate(
@@ -401,19 +395,32 @@
     return jnp.where(core == 0, odd, even), jnp.where(core == 0, even, odd)
 
 
-def middle_kernel(wide, mapped, ctx_ref, own_ref, cot_ref, wo_ref, wi_ref, wu_ref, vec_ref, bin_ref,
+def middle_kernel(wide, mapped, ctx_ref, own_ref, cot_ref, got_ref, vec_ref, bin_ref,
                   out_ref, h1_ref, gctx_ref, grads, sums_ref, sbin_ref,
                   first_ref, n1_ref, inv_ref, low_ref, pre_ref, cdf_ref, act_ref, acc_ref,
-                  gffn_ref, glow_ref, out_buf, in_buf, wo_buf, sems):
+                  gffn_ref, glow_ref, lowt_ref, w_ref, out_buf, in_buf, wo_buf, sems, w_sems):
     step = pl.program_id(0)
     width = ctx_ref.shape[1]
-    square = lambda ref: ref[...].reshape(width, width)
     vec = lambda i: vec_ref[i : i + 1, :]
     mean = lambda v: jnp.sum(v, axis=-1, keepdims=True) * (1.0 / width)
     down = lambda v: jnp.sum(v, axis=0, keepdims=True)
-    owners = wi_ref.shape[0]
+    owners = got_ref.shape[0]
     each = width // owners
     some = owners // wide
+    square = lambda value: value.reshape(width, width)
+    rows_of = lambda place: pl.ds(pl.multiple_of(place * each, each), each)
+    w_output = lambda ref: ref.at[:, rows_of(WO)]
+    w_inner = lambda ref, at: ref.at[:, rows_of(WI + at)]
+    w_outer = lambda ref, at: ref.at[pl.ds(at * some, some), pl.ds(0, wide * each)]
+
+    def fetch_inner(at):
+        return pltpu.make_async_copy(w_inner(got_ref, at), w_inner(w_ref, at), w_sems.at[0, at])
+
+    def fetch_outer(at):
+        return pltpu.make_async_copy(w_outer(got_ref, at), w_outer(w_ref, at), w_sems.at[1, at])
+
+    def fetch_output():
+        return pltpu.make_async_copy(w_output(got_ref), w_output(w_ref), w_sems.at[0, wide])
 
     def slot(group, i):
         return group % 2 * 16 + group // 2 * 8 + i % 2 * 4 + i // 2 if mapped else group * 8 + i
@@ -455,7 +462,12 @@
 
     @pl.when(step == 0)
     def _():
-        hidden = own_ref[...].astype(F32) + mm(ctx_ref[...], square(wo_ref)) + vec(0)
+        fetch_output().start()
+        for at in range(wide):
+            fetch_inner(at).start()
+            fetch_outer(at).start()
+        fetch_output().wait()
+        hidden = own_ref[...].astype(F32) + mm(ctx_ref[...], square(w_output(w_ref)[...])) + vec(0)
         centred = hidden - mean(hidden)
         inverse = lax.rsqrt(mean(centred * centred) + NORM_EPS)
         normed = centred * inverse
@@ -464,17 +476,20 @@
         first = normed * vec(1) + vec(2)
         first_ref[...] = first
         low_ref[...] = first.astype(BF)
+        lowt_ref[...] = first.astype(BF).T
 
     @pl.when(step < wide)
     def _():
         chunk = pl.ds(pl.multiple_of(step * width, width), width)
-        pre = mm(low_ref[...], square(wi_ref)) + bin_ref[pl.ds(step, 1), :]
+        fetch_inner(step).wait()
+        fetch_outer(step).wait()
+        pre = mm(low_ref[...], square(w_inner(w_ref, step)[...])) + bin_ref[pl.ds(step, 1), :]
         cdf = 0.5 * (1.0 + lax.erf(pre * SQRT_HALF))
         act = (pre * cdf).astype(BF)
         pre_ref[:, chunk] = pre
         cdf_ref[:, chunk] = cdf
         act_ref[:, chunk] = act
-        more = mm(act, square(wu_ref))
+        more = mm(act, square(w_outer(w_ref, step)[...]))
 
         @pl.when(step == 0)
         def _():
@@ -508,7 +523,7 @@
         pre = pre_ref[:, chunk]
         slope = cdf_ref[:, chunk] + pre * jnp.exp(-0.5 * pre * pre) * INV_ROOT_TAU
         low = glow_ref[...]
-        grad = (nt(low, square(wu_ref)) * slope).astype(BF)
+        grad = (nt(low, square(w_outer(w_ref, at)[...])) * slope).astype(BF)
         sbin_ref[pl.ds(at, 1), :] = down(grad.astype(F32))
         turn = step % 2
 
@@ -518,9 +533,9 @@
 
         out_buf[turn] = tn(act_ref[:, chunk], low).astype(BF).reshape(some, wide * each, width)
         start(outer(at))
-        in_buf[turn] = tn(low_ref[...], grad).astype(BF).reshape(owners, each, width)
+        in_buf[turn] = mm(lowt_ref[...], grad).astype(BF).reshape(owners, each, width)
         start(inner(at))
-        gffn_ref[...] += nt(grad, square(wi_ref))
+        gffn_ref[...] += nt(grad, square(w_inner(w_ref, at)[...]))
 
     @pl.when(step == 2 * wide - 1)
     def _():
@@ -535,7 +550,7 @@
         sums_ref[5:6, :] = down(low.astype(F32))
         wo_buf[...] = tn(ctx_ref[...], low).astype(BF).reshape(owners, each, width)
         start(output())
-        gctx = nt(low, square(wo_ref)).astype(BF)
+        gctx = nt(low, square(w_output(w_ref)[...])).astype(BF)
         gctx_ref[...] = gctx
         sums_ref[6:7, :] = down(gctx.astype(F32))
         sums_ref[7:8, :] = jnp.zeros((1, width), F32)
@@ -548,16 +563,13 @@
     each = width // owners
     wide = WIDE
     whole = lambda shape: pl.BlockSpec(shape, lambda s: (0,) * len(shape))
-    at = lambda s: jnp.where(s < wide, s, 2 * wide - 1 - s)
     shape = jax.ShapeDtypeStruct
     return pl.pallas_call(
         functools.partial(middle_kernel, wide, mapped),
         grid=(2 * wide,),
         in_specs=[
             whole((rows, width)), whole((rows, width)), whole((rows, width)),
-            pl.BlockSpec((owners, each, width), lambda s: (0, WO, 0)),
-            pl.BlockSpec((owners, each, width), lambda s: (0, WI + at(s), 0)),
-            pl.BlockSpec((owners // wide, wide * each, width), lambda s: (at(s), 0, 0)),
+            pl.BlockSpec(memory_space=pl.ANY),
             whole((8, width)), whole((8, width)),
         ],
         out_specs=[
@@ -575,10 +587,12 @@
             pltpu.VMEM((rows, width), BF), pltpu.VMEM((rows, wide * width), F32),
             pltpu.VMEM((rows, wide * width), F32), pltpu.VMEM((rows, wide * width), BF),
             pltpu.VMEM((rows, width), F32), pltpu.VMEM((rows, width), F32),
-            pltpu.VMEM((rows, width), BF),
+            pltpu.VMEM((rows, width), BF), pltpu.VMEM((width, rows), BF),
+            pltpu.VMEM((owners, (2 * wide + 1) * each, width), BF),
             pltpu.VMEM((2, owners // wide, wide * each, width), BF),
             pltpu.VMEM((2, owners, each, width), BF),
             pltpu.VMEM((owners, each, width), BF), pltpu.SemaphoreType.DMA((5, owners)),
+            pltpu.SemaphoreType.DMA((2, wide + 1)),
         ],
         compiler_params=pltpu.CompilerParams(vmem_limit_bytes=60 * 2**20),
         cost_estimate=pl.CostEstimate(
@@ -586,12 +600,12 @@
             transcendentals=2 * rows * width * wide,
         ),
         name="middle",
-    )(ctx, own, cot, got, got, got, vec, b_inner)
+    )(ctx, own, cot, got, vec, b_inner)
 
 
 def back_kernel(rows, bound, started, *refs):
     near_ref, gctx_ref, ctx_ref, q_ref, k_ref, v_ref, lse_ref, segq_ref, segk_ref = refs[:9]
-    dk_ref, dv_ref, dq_ref = refs[-3:]
+    dk_ref, dv_ref, dq_ref, kt_ref, p_ref, ds_ref = refs[-6:]
     q, g = q_ref[...], gctx_ref[...]
     part = q.shape[1]
     heads = part // HDIM
@@ -603,35 +617,33 @@
         jnp.sum(product[h * HDIM : (h + 1) * HDIM], axis=0, keepdims=True) for h in range(heads)
     ]
 
-    def one(b, dq):
-        here = pl.ds(pl.multiple_of(b * rows, rows), rows)
-        k, v = k_ref[here, :], v_ref[here, :]
-        kt = k.T
-        if bound is None:
-            allowed = segk_ref[here, :] == segq_ref[...]
-        dk = jnp.zeros((rows, part), F32)
-        dv = jnp.zeros((rows, part), F32)
-        out = []
+    def body():
+        k, v = k_ref[...], v_ref[...]
+        kt_ref[...] = k.T
         for h in range(heads):
             s = nt(k, q_parts[h])
             if bound is None:
-                s = jnp.where(allowed, s, MASK_FILL)
+                s = jnp.where(segk_ref[...] == segq_ref[...], s, MASK_FILL)
             p = jnp.exp(s - lse_ref[0, h : h + 1, :])
-            dp = nt(v, g_parts[h])
-            ds = (p * (dp - inner[h])).astype(BF)
-            dv = dv + mm(p.astype(BF), g_parts[h])
-            dk = dk + mm(ds, q_parts[h])
-            out.append(dq[h] + mm(kt[h * HDIM : (h + 1) * HDIM], ds))
-        dk_ref[here, :] = dk.astype(BF)
-        dv_ref[here, :] = dv.astype(BF)
-        return tuple(out)
-
-    if started:
-        dq = tuple(refs[9][h * HDIM : (h + 1) * HDIM, :] for h in range(heads))
+            across = slice(h * rows, (h + 1) * rows)
+            ds = (p * (nt(v, g_parts[h]) - inner[h])).astype(BF)
+            p_ref[:, across] = p.astype(BF)
+            ds_ref[:, across] = ds
+            mine = slice(h * HDIM, (h + 1) * HDIM)
+            more = mm(kt_ref[mine, :], ds)
+            dq_ref[mine, :] = refs[9][mine, :] + more if started else more
+        dk_ref[...] = mm(ds_ref[...], jnp.concatenate(q_parts, 0)).astype(BF)
+        dv_ref[...] = mm(p_ref[...], jnp.concatenate(g_parts, 0)).astype(BF)
+
+    if bound is None:
+
+        @pl.when(near_ref[0] == 0)
+        def _():
+            dq_ref[...] = refs[9][...]
+
+        pl.when(near_ref[0] > 0)(body)
     else:
-        dq = tuple(jnp.zeros((HDIM, rows), F32) for _ in range(heads))
-    dq = lax.fori_loop(0, near_ref[0] if bound is None else bound, one, dq)
-    dq_ref[...] = jnp.concatenate(dq, 0)
+        body()
 
 
 def back_call(start, steps, bound, near, gctx, ctx, q, k, v, lse, segq, segk, dq0=None, into=None):
@@ -656,6 +668,11 @@
         out_specs=[cols(tall), cols(tall), down],
         out_shape=[shape((tall, width), BF), shape((tall, width), BF), shape((width, rows), F32)],
         input_output_aliases={9 + i: i for i in range(3)} if into else {},
+        scratch_shapes=[
+            pltpu.VMEM((part, tall), BF),
+            pltpu.VMEM((tall, part // HDIM * rows), BF),
+            pltpu.VMEM((tall, part // HDIM * rows), BF),
+        ],
         compiler_params=pltpu.CompilerParams(vmem_limit_bytes=60 * 2**20),
         cost_estimate=pl.CostEstimate(
             flops=2 * 10 * 2 * tall * rows * part * steps * 2,
@@ -699,9 +716,8 @@
 def weight_kernel(blocks, first, rows, runs, *refs):
     spots = refs[:blocks]
     (near_ref, core_ref, own_ref, dq_ref, wq_ref, h1_ref, dkp_ref, dvp_ref, dkn_ref, dvn_ref,
-     q_send, q_keep, kv_send, kv_keep, gown_ref, sums_ref, x_ref, sems) = refs[blocks:]
+     q_send, q_keep, kv_send, kv_keep, gown_ref, sums_ref, x_ref, xt_ref, sems) = refs[blocks:]
     core = core_ref[0]
-    at = lambda b: pl.ds(pl.multiple_of(b * rows, rows), rows)
     step = pl.program_id(0)
 
     @pl.when(step == 0)
@@ -712,9 +728,10 @@
         ]
         for copy in copies:
             copy.start()
-        for copy in copies:
+        gown_ref[...] = h1_ref[...]
+        for i, copy in enumerate(copies):
             copy.wait()
-        gown_ref[...] = h1_ref[...]
+            xt_ref[:, i * rows : (i + 1) * rows] = x_ref[i * rows : (i + 1) * rows, :].T
 
     scale = HDIM**-0.5
     dq = dq_ref[...].T.astype(BF)
@@ -726,20 +743,18 @@
     q_keep[...] = here.reshape(q_send.shape)
     sums_ref[0:1, :] = jnp.sum(dq.astype(F32), axis=0, keepdims=True) * scale
 
-    def products(b, carry, dk_ref, dv_ref, base):
-        dk, dv, x = dk_ref[at(b), :], dv_ref[at(b), :], x_ref[at(base + b), :]
-        wk, wv = carry
-        return wk + tn(x, dk), wv + tn(x, dv)
-
-    zero = jnp.zeros((width, part), F32)
-    carry = (zero, zero)
-    carry = lax.fori_loop(0, first, lambda b, c: products(b, c, dkp_ref, dvp_ref, 0), carry)
-    carry = lax.fori_loop(0, near_ref[0], lambda b, c: products(b, c, dkn_ref, dvn_ref, first), carry)
-    for i, grad in enumerate(carry):
-        away, here = halves(grad.astype(BF), runs, core)
-        shape = kv_send.shape[:2] + (part,)
-        kv_send[:, :, i * part : (i + 1) * part] = away.reshape(shape)
-        kv_keep[:, :, i * part : (i + 1) * part] = here.reshape(shape)
+    def body(near):
+        for i, (p_ref, n_ref) in enumerate(((dkp_ref, dkn_ref), (dvp_ref, dvn_ref))):
+            grad = mm(xt_ref[:, :PROMPT], p_ref[...])
+            if near:
+                grad = grad + mm(xt_ref[:, PROMPT:], n_ref[...])
+            away, here = halves(grad.astype(BF), runs, core)
+            shape = kv_send.shape[:2] + (part,)
+            kv_send[:, :, i * part : (i + 1) * part] = away.reshape(shape)
+            kv_keep[:, :, i * part : (i + 1) * part] = here.reshape(shape)
+
+    pl.when(near_ref[0] == 0)(lambda: body(False))
+    pl.when(near_ref[0] > 0)(lambda: body(True))
     sums_ref[1:8, :] = jnp.zeros((7, part), F32)
 
 
@@ -774,7 +789,9 @@
             shape((half, each, 2 * width), BF), shape((half, each, 2 * width), BF),
             shape((rows, width), F32), shape((8, width), F32),
         ],
-        scratch_shapes=[pltpu.VMEM((tall, width), BF), pltpu.SemaphoreType.DMA((blocks,))],
+        scratch_shapes=[
+            pltpu.VMEM((tall, width), BF), pltpu.VMEM((width, tall), BF), pltpu.SemaphoreType.DMA((blocks,)),
+        ],
         compiler_params=pltpu.CompilerParams(vmem_limit_bytes=60 * 2**20),
         cost_estimate=pl.CostEstimate(
             flops=4 * tall * width * width, bytes_accessed=12 * tall * width, transcendentals=0

time: 370 us -> 358 us (0.968)
  Pallas kernels: 95.3 us -> 81.1 us
  waiting for transfers between devices: 157 us -> 162 us
    pallas_call x2, Pallas kernels: 24.1 us -> 18.1 us  [back_call(): pl.pallas_call(functools.partial(back_kernel, rows, bound, dq0 is not Non...]
    ppermute x27, waiting for transfers between devices: 122 us -> 127 us  [swap(): return lax.ppermute(value, AXES, [(i, i ^ mask) for i in range(self.count)])]
    pallas_call x1, Pallas kernels: 14.8 us -> 10.8 us  [weight_call(): pl.pallas_call(functools.partial(weight_kernel, blocks, first, rows, runs...]
  transfers between devices with their start and end apart: 35 -> 35, of which waited for: 18 -> 20; matrix products, arithmetic and copies ran while one was open for 7% -> 8% of each run, Pallas kernels for 19% -> 16%
where the time goes in v10:
time: 358 us; the launch traced here: 357 us
  waiting for transfers between devices  162 us (45%)
  Pallas kernels  81.1 us (23%)
  starting transfers between devices  62.2 us (17%)
  local copies, waits for them, and re-layouts  20.8 us (6%)
  other arithmetic  16.6 us (5%)
  between operations  14.4 us (4%)
    ppermute x27, waiting for transfers between devices, swap(): return lax.ppermute(value, AXES, [(i, i ^ mask) for i in range(self.count)])  127 us
    ppermute x27, starting transfers between devices, swap(): return lax.ppermute(value, AXES, [(i, i ^ mask) for i in range(self.count)])  55.6 us
    pallas_call x1, Pallas kernels, middle_call(): pl.pallas_call(functools.partial(middle_kernel, wide, mapped), grid=(2 *...  20.8 us
    reduce_scatter x3, waiting for transfers between devices, per_device(): lax.psum_scatter(value, axes, scatter_dimension=0, tiled=True)  20.2 us
    pallas_call x1, Pallas kernels, attention_call(): pl.pallas_call(functools.partial(attention_kernel, blocks, first, rows, p...  19 us
    pallas_call x2, Pallas kernels, back_call(): pl.pallas_call(functools.partial(back_kernel, rows, bound, dq0 is not Non...  18.1 us
    ppermute x4, waiting for transfers between devices, send(): return lax.ppermute(value, AXES, pairs)  12.6 us
    pallas_call x1, Pallas kernels, weight_call(): pl.pallas_call(functools.partial(weight_kernel, blocks, first, rows, runs...  10.8 us
  transfers between devices with their start and end apart: 35, of which 20 were waited for; matrix products, arithmetic and copies ran while one was open for 8% of the time, Pallas kernels for 16%

profile of v10, /device:TPU:0, one launch (start us, length us, event | category | flops | bytes accessed | tf_op | source)
XLA Modules:
  0.0 356.8 jit_solution(12380337906451759492)
XLA Ops:
  9.5 1.8 pack.1
  11.4 3.1 collective-permute-start
  14.5 2.6 collective-permute-start.1
  17.1 3.8 %collective-permute-start.3 = (bf16[256,768]{1,0:T(8,128)(2,1)}, bf16[256,768]{1,0:T(8,128)(2,1)S(1)}, u32[]{:S(2)}, u32[]{:S(2)}) collective-permute-start(bf16[256,768]{1,0:T(8,128)(2,1)} %bitcast.208), channel_id=1, source_target_pairs={{0,4},{1,5},{2,6},{3,7},{8,12},{9,13},{10,14},{11,15},{16,20},{17,... | collective-permute-start | bytes 1179656 | tf_op jit(solution)/shard_map/ppermute | solution.py:55
  20.9 1.6 collective-permute-start.4
  25.9 12.6 %collective-permute-done.3 = bf16[256,768]{1,0:T(8,128)(2,1)S(1)} collective-permute-done((bf16[256,768]{1,0:T(8,128)(2,1)}, bf16[256,768]{1,0:T(8,128)(2,1)S(1)}, u32[]{:S(2)}, u32[]{:S(2)}) %collective-permute-start.3) | collective-permute-done | bytes 393248 | tf_op jit(solution)/shard_map/ppermute | solution.py:55
  39.3 16.1 %collective-permute-start.7 = (bf16[256,768]{1,0:T(8,128)(2,1)S(1)}, bf16[256,768]{1,0:T(8,128)(2,1)S(1)}, u32[]{:S(2)}, u32[]{:S(2)}) collective-permute-start(bf16[256,768]{1,0:T(8,128)(2,1)S(1)} %broadcast_select_fusion.refs_0_), channel_id=1, source_target_pairs={{0,2},{1,3},{2,0},{3,1},{4,6},{5,7},{6,4},{7,5},{8,10},{9,11},{10,... | collective-permute-start | bytes 1179656 | tf_op jit(solution)/shard_map/ppermute | solution.py:51
  55.4 1.2 collective-permute-start.8
  57.6 1.2 collective-permute-start.5
  58.9 7.3 %collective-permute-done.5 = bf16[4,32,768]{2,1,0:T(8,128)(2,1)S(1)} collective-permute-done((bf16[4,32,768]{2,1,0:T(8,128)(2,1)S(1)}, bf16[4,32,768]{2,1,0:T(8,128)(2,1)S(1)}, u32[]{:S(2)}, u32[]{:S(2)}) %collective-permute-start.5) | collective-permute-done | bytes 196640 | tf_op jit(solution)/shard_map/ppermute | solution.py:51
  66.2 5.6 %collective-permute-done.6 = bf16[4,48,768]{2,1,0:T(8,128)(2,1)S(1)} collective-permute-done((bf16[4,48,768]{2,1,0:T(8,128)(2,1)S(1)}, bf16[4,48,768]{2,1,0:T(8,128)(2,1)S(1)}, u32[]{:S(2)}, u32[]{:S(2)}) %collective-permute-start.6) | collective-permute-done | bytes 294944 | tf_op jit(solution)/shard_map/ppermute | solution.py:51
  71.8 3.5 collective-permute-done.7.refs_1_
  76.2 1.5 collective-permute-start.11
  77.6 1.5 collective-permute-start.10
  79.7 14.8 %collective-permute-done.10 = bf16[8,32,768]{2,1,0:T(8,128)(2,1)S(1)} collective-permute-done((bf16[8,32,768]{2,1,0:T(8,128)(2,1)S(1)}, bf16[8,32,768]{2,1,0:T(8,128)(2,1)S(1)}, u32[]{:S(2)}, u32[]{:S(2)}) %collective-permute-start.10) | collective-permute-done | bytes 393248 | tf_op jit(solution)/shard_map/ppermute | solution.py:51
  94.6 3.9 %collective-permute-done.11 = bf16[8,48,768]{2,1,0:T(8,128)(2,1)S(1)} collective-permute-done((bf16[8,48,768]{2,1,0:T(8,128)(2,1)S(1)}, bf16[8,48,768]{2,1,0:T(8,128)(2,1)S(1)}, u32[]{:S(2)}, u32[]{:S(2)}) %collective-permute-start.11) | collective-permute-done | bytes 589856 | tf_op jit(solution)/shard_map/ppermute | solution.py:51
  98.6 10.9 %collective-permute-done.12.refs_3_ = bf16[256,768]{1,0:T(8,128)(2,1)S(1)} collective-permute-done((bf16[256,768]{1,0:T(8,128)(2,1)S(1)}, bf16[256,768]{1,0:T(8,128)(2,1)S(1)}, u32[]{:S(2)}, u32[]{:S(2)}) %collective-permute-start.12) | collective-permute-done | bytes 393248 | tf_op jit(solution)/shard_map/ppermute | solution.py:51
  111.9 1.3 collective-permute-done.13.refs_11_
  114.6 19.0 %attention.1 = (bf16[32,72,768]{2,1,0:T(8,128)(2,1)}, bf16[256,768]{1,0:T(8,128)(2,1)}, bf16[1024,768]{1,0:T(8,128)(2,1)}, bf16[1024,768]{1,0:T(8,128)(2,1)}, bf...) custom-call(bf16[256,768]{1,0:T(8,128)(2,1)} %copy-done.8, ...), custom_call_target="tpu_custom_call" | custom-call | flops 9865003008 | bytes 12582912 | tf_op jit(solution)/shard_map/attention/pallas_call | solution.py:342
  133.6 2.3 all-gather.2.cloned.1.call-done
  138.1 20.8 %middle.1 = (bf16[256,768]{1,0:T(8,128)(2,1)}, f32[256,768]{1,0:T(8,128)}, bf16[256,768]{1,0:T(8,128)(2,1)}, bf16[32,216,768]{2,1,0:T(8,128)(2,1)}, f32[8,768]{1,0:T(8,128)}, /*index=5*/f32[8,768]{1,0:T(8,128)}) custom-call(bf16[256,768]{1,0:T(8,128)(2,1)} %get-tuple-element.116.ctx_ref.refs_2_, bf16[256,768]{1,0:T(8,128)(2,1)} %bitcast.212, ...), custom_call_target="tpu_custom_call" | custom-call | flops 8153726976 | bytes 33554432 | tf_op jit(solution)/shard_map/middle/pallas_call | solution.py:567
  159.0 12.5 %attention_back.2 = (bf16[1024,768]{1,0:T(8,128)(2,1)}, bf16[1024,768]{1,0:T(8,128)(2,1)}, f32[768,256]{1,0:T(8,128)}) custom-call(s32[1]{0:T(128)} %bitcast.9.refs_7_.refs_0_.near_ref, bf16[256,768]{1,0:T(8,128)(2,1)} %get-tuple-element.119.refs_1_, bf16[256,768]{1,0:T(8,128)(2,1)} %get-tuple-element.116.ctx_ref.refs_2_, ...), custom_call_target="tpu_custom_call" | custom-call | flops 16106127360 | bytes 6291456 | tf_op jit(solution)/shard_map/attention_back/pallas_call | solution.py:659
  171.6 20.2 %reduce-scatter.4.cloned.1.call-done = bf16[16,216,768]{2,1,0:T(8,128)(2,1)} async-done(((bf16[32,216,768]{2,1,0:T(8,128)(2,1)}), bf16[16,216,768]{2,1,0:T(8,128)(2,1)}) %reduce-scatter.4.cloned.1.call-update) | async-done | bytes 5308432 | tf_op jit(solution)/shard_map/reduce_scatter | solution.py:919
  193.1 6.5 %token_product.2 = bf16[4,256,768]{2,1,0:T(8,128)(2,1)} custom-call(s32[1]{0:T(128)} %bitcast.9.refs_7_.refs_0_.near_ref, bf16[1024,768]{1,0:T(8,128)(2,1)} %get-tuple-element.134.refs_13_.dk_ref, bf16[1024,768]{1,0:T(8,128)(2,1)} %get-tuple-element.135.refs_14_.dv_ref, bf16[32,72,768]{2,1,0:T(8,128)(2,1)} %get-tuple-element.132.refs_11_.wk_ref.wv_ref, ...), custom_call_target="tpu_custom_call" | custom-call | flops 2415919104 | bytes 4718592 | tf_op jit(solution)/shard_map/token_product/pallas_call | solution.py:697
  199.5 1.2 slice_bitcast_fusion
  200.7 1.9 collective-permute-start.15
  202.8 5.5 %attention_back.3 = (bf16[768,768]{1,0:T(8,128)(2,1)}, bf16[768,768]{1,0:T(8,128)(2,1)}, f32[768,256]{1,0:T(8,128)}) custom-call(s32[1]{0:T(128)} %bitcast.9.refs_7_.refs_0_.near_ref, bf16[256,768]{1,0:T(8,128)(2,1)} %get-tuple-element.119.refs_1_, bf16[256,768]{1,0:T(8,128)(2,1)} %get-tuple-element.116.ctx_ref.refs_2_, ...), custom_call_target="tpu_custom_call" | custom-call | flops 12079595520 | bytes 4718592 | tf_op jit(solution)/shard_map/attention_back/pallas_call | solution.py:659
  208.3 10.8 %weight_product.1 = (bf16[16,24,768]{2,1,0:T(8,128)(2,1)}, bf16[16,24,768]{2,1,0:T(8,128)(2,1)}, bf16[16,24,1536]{2,1,0:T(8,128)(2,1)}, bf16[16,24,1536]{2,1,0:T...) custom-call(bf16[256,768]{1,0:T(8,128)(2,1)} %copy-done.8, bf16[256,768]{1,0:T(8,128)(2,1)} %copy-done.15, ...), custom_call_target="tpu_custom_call" | custom-call | flops 4227858432 | bytes 16515072 | tf_op jit(solution)/shard_map/weight_product/pallas_call | solution.py:773
  219.1 1.4 collective-permute-done.15
  220.6 16.2 %collective-permute-done.18 = bf16[256,768]{1,0:T(8,128)(2,1)S(1)} collective-permute-done((bf16[256,768]{1,0:T(8,128)(2,1)S(1)}, bf16[256,768]{1,0:T(8,128)(2,1)S(1)}, u32[]{:S(2)}, u32[]{:S(2)}) %collective-permute-start.18) | collective-permute-done | bytes 393248 | tf_op jit(solution)/shard_map/ppermute | solution.py:51
  241.5 2.1 collective-permute-start.19
  243.6 1.1 pad_maximum_fusion.2
  244.7 4.1 %token_product.3 = bf16[3,256,768]{2,1,0:T(8,128)(2,1)} custom-call(s32[1]{0:T(128)} %bitcast.9.refs_7_.refs_0_.near_ref, bf16[768,768]{1,0:T(8,128)(2,1)} %get-tuple-element.150.refs_15_.dk_ref, bf16[768,768]{1,0:T(8,128)(2,1)} %get-tuple-element.151.refs_16_.dv_ref, bf16[32,72,768]{2,1,0:T(8,128)(2,1)} %get-tuple-element.132.refs_11_.wk_ref.wv_ref, ...), custom_call_target="tpu_custom_call" | custom-call | flops 1811939328 | bytes 3538944 | tf_op jit(solution)/shard_map/token_product/pallas_call | solution.py:697
  248.8 4.4 %collective-permute-done.19 = bf16[256,768]{1,0:T(8,128)(2,1)} collective-permute-done((bf16[256,768]{1,0:T(8,128)(2,1)}, bf16[256,768]{1,0:T(8,128)(2,1)}, u32[]{:S(2)}, u32[]{:S(2)}) %collective-permute-start.19) | collective-permute-done | bytes 393248 | tf_op jit(solution)/shard_map/ppermute | solution.py:51
  254.4 2.1 collective-permute-start.22
  257.9 1.1 add_convert_fusion.2
  259.0 1.5 collective-permute-start.20
  262.3 1.3 collective-permute-start.28
  263.7 10.4 %collective-permute-done.22 = bf16[256,768]{1,0:T(8,128)(2,1)S(1)} collective-permute-done((bf16[256,768]{1,0:T(8,128)(2,1)S(1)}, bf16[256,768]{1,0:T(8,128)(2,1)S(1)}, u32[]{:S(2)}, u32[]{:S(2)}) %collective-permute-start.22) | collective-permute-done | bytes 393248 | tf_op jit(solution)/shard_map/ppermute | solution.py:51
  274.2 4.6 %collective-permute-done.20 = bf16[8,32,768]{2,1,0:T(8,128)(2,1)} collective-permute-done((bf16[8,32,768]{2,1,0:T(8,128)(2,1)S(1)}, bf16[8,32,768]{2,1,0:T(8,128)(2,1)}, u32[]{:S(2)}, u32[]{:S(2)}) %collective-permute-start.20) | collective-permute-done | bytes 393248 | tf_op jit(solution)/shard_map/ppermute | solution.py:51
  278.8 13.2 %collective-permute-done.21 = bf16[8,24,1536]{2,1,0:T(8,128)(2,1)} collective-permute-done((bf16[8,24,1536]{2,1,0:T(8,128)(2,1)S(1)}, bf16[8,24,1536]{2,1,0:T(8,128)(2,1)}, u32[]{:S(2)}, u32[]{:S(2)}) %collective-permute-start.21) | collective-permute-done | bytes 589856 | tf_op jit(solution)/shard_map/ppermute | solution.py:51
  293.2 1.5 collective-permute-start.25
  296.6 1.8 collective-permute-start.24
  299.5 2.9 collective-permute-done.24
  302.6 10.6 %collective-permute-start.27 = (bf16[2,24,1536]{2,1,0:T(8,128)(2,1)S(1)}, bf16[2,24,1536]{2,1,0:T(8,128)(2,1)S(1)}, u32[]{:S(2)}, u32[]{:S(2)}) collective-permute-start(bf16[2,24,1536]{2,1,0:T(8,128)(2,1)S(1)} %bitcast.225), channel_id=1, source_target_pairs={{0,4},{1,5},{2,6},{3,7},{4,0},{5,1},{6,2},{7,3},{8,12},{9,13},{10,... | collective-permute-start | bytes 442376 | tf_op jit(solution)/shard_map/ppermute | solution.py:51
  313.5 24.9 %collective-permute-done.26 = bf16[2,32,768]{2,1,0:T(8,128)(2,1)S(1)} collective-permute-done((bf16[2,32,768]{2,1,0:T(8,128)(2,1)S(1)}, bf16[2,32,768]{2,1,0:T(8,128)(2,1)S(1)}, u32[]{:S(2)}, u32[]{:S(2)}) %collective-permute-start.26) | collective-permute-done | bytes 98336 | tf_op jit(solution)/shard_map/ppermute | solution.py:51
  338.6 2.1 collective-permute-start.29
  340.6 1.9 fusion.3
  (176 shorter events, 38.2 us)
Async XLA Ops:
  7.2 31.3 %copy-start.7 = (bf16[1,256,768]{2,1,0:T(8,128)(2,1)S(1)}, bf16[1,256,768]{2,1,0:T(8,128)(2,1)}, u32[]{:S(2)}) copy-start(bf16[1,256,768]{2,1,0:T(8,128)(2,1)} %param.18) | copy-start | bytes 1179652
  7.2 128.7 %all-gather.2.cloned.1.call-start = ((), (), s32[]{:S(2)}) async-start(), calls=%async_computation.3 | async-start | bytes 11354112 | tf_op jit(solution)/shard_map/all_gather | solution.py:845
  11.3 180.4 %reduce-scatter.4.cloned.1.call-start = ((), (), s32[]{:S(2)}) async-start(), calls=%async_computation.4 | async-start | bytes 15925248 | tf_op jit(solution)/shard_map/reduce_scatter | solution.py:919
  11.4 27.9 %collective-permute-start = (bf16[80,768]{1,0:T(8,128)(2,1)}, bf16[80,768]{1,0:T(8,128)(2,1)S(1)}, u32[]{:S(2)}, u32[]{:S(2)}) collective-permute-start(bf16[80,768]{1,0:T(8,128)(2,1)} %get-tuple-element.102), channel_id=1, source_target_pairs={{0,2},{1,3},{2,0},{3,1},{4,6},{5,7},{6,4},{7,5},{8,10},{9,11},{10,... | collective-permute-start | bytes 368648 | tf_op jit(solution)/shard_map/ppermute | solution.py:51
  14.5 24.8 %collective-permute-start.1 = (bf16[80,768]{1,0:T(8,128)(2,1)}, bf16[80,768]{1,0:T(8,128)(2,1)S(1)}, u32[]{:S(2)}, u32[]{:S(2)}) collective-permute-start(bf16[80,768]{1,0:T(8,128)(2,1)} %get-tuple-element.102), channel_id=1, source_target_pairs={{0,4},{1,5},{2,6},{3,7},{4,0},{5,1},{6,2},{7,3},{8,12},{9,13},{10,... | collective-permute-start | bytes 368648 | tf_op jit(solution)/shard_map/ppermute | solution.py:51
  17.1 22.2 %collective-permute-start.2 = (bf16[80,768]{1,0:T(8,128)(2,1)}, bf16[80,768]{1,0:T(8,128)(2,1)S(1)}, u32[]{:S(2)}, u32[]{:S(2)}) collective-permute-start(bf16[80,768]{1,0:T(8,128)(2,1)} %get-tuple-element.102), channel_id=1, source_target_pairs={{0,6},{1,7},{2,4},{3,5},{4,2},{5,3},{6,0},{7,1},{8,14},{9,15},{10,... | collective-permute-start | bytes 368648 | tf_op jit(solution)/shard_map/ppermute | solution.py:51
  17.1 21.4 %collective-permute-start.3 = (bf16[256,768]{1,0:T(8,128)(2,1)}, bf16[256,768]{1,0:T(8,128)(2,1)S(1)}, u32[]{:S(2)}, u32[]{:S(2)}) collective-permute-start(bf16[256,768]{1,0:T(8,128)(2,1)} %bitcast.208), channel_id=1, source_target_pairs={{0,4},{1,5},{2,6},{3,7},{8,12},{9,13},{10,14},{11,15},{16,20},{17,... | collective-permute-start | bytes 1179656 | tf_op jit(solution)/shard_map/ppermute | solution.py:55
  20.9 18.4 %collective-permute-start.4 = (bf16[256,768]{1,0:T(8,128)(2,1)}, bf16[256,768]{1,0:T(8,128)(2,1)S(1)}, u32[]{:S(2)}, u32[]{:S(2)}) collective-permute-start(bf16[256,768]{1,0:T(8,128)(2,1)} %bitcast.209), channel_id=1, source_target_pairs={{0,1},{1,0},{2,3},{3,2},{4,5},{5,4},{6,7},{7,6},{8,9},{9,8},{10,11... | collective-permute-start | bytes 1179656 | tf_op jit(solution)/shard_map/ppermute | solution.py:51
  38.5 33.3 %collective-permute-start.9 = (bf16[256,768]{1,0:T(8,128)(2,1)S(1)}, bf16[256,768]{1,0:T(8,128)(2,1)S(1)}, u32[]{:S(2)}, u32[]{:S(2)}) collective-permute-start(bf16[256,768]{1,0:T(8,128)(2,1)S(1)} %bitcast.215), channel_id=1, source_target_pairs={{5,6},{6,5},{13,14},{14,13},{21,22},{22,21},{29,30},{30,29}} | collective-permute-start | bytes 1179656 | tf_op jit(solution)/shard_map/ppermute | solution.py:55
  39.2 19.6 %copy-start.8 = (bf16[256,768]{1,0:T(8,128)(2,1)}, bf16[256,768]{1,0:T(8,128)(2,1)S(1)}, u32[]{:S(2)}) copy-start(bf16[256,768]{1,0:T(8,128)(2,1)S(1)} %broadcast_select_fusion.refs_0_) | copy-start | bytes 1179652
  39.3 19.6 %copy-start.13 = (bf16[256,768]{1,0:T(8,128)(2,1)}, bf16[256,768]{1,0:T(8,128)(2,1)S(1)}, u32[]{:S(2)}) copy-start(bf16[256,768]{1,0:T(8,128)(2,1)S(1)} %collective-permute-done.4.refs_5_) | copy-start | bytes 1179652
  39.3 36.0 %collective-permute-start.7 = (bf16[256,768]{1,0:T(8,128)(2,1)S(1)}, bf16[256,768]{1,0:T(8,128)(2,1)S(1)}, u32[]{:S(2)}, u32[]{:S(2)}) collective-permute-start(bf16[256,768]{1,0:T(8,128)(2,1)S(1)} %broadcast_select_fusion.refs_0_), channel_id=1, source_target_pairs={{0,2},{1,3},{2,0},{3,1},{4,6},{5,7},{6,4},{7,5},{8,10},{9,11},{10,... | collective-permute-start | bytes 1179656 | tf_op jit(solution)/shard_map/ppermute | solution.py:51
  55.4 19.9 %collective-permute-start.8 = (bf16[256,768]{1,0:T(8,128)(2,1)S(1)}, bf16[256,768]{1,0:T(8,128)(2,1)S(1)}, u32[]{:S(2)}, u32[]{:S(2)}) collective-permute-start(bf16[256,768]{1,0:T(8,128)(2,1)S(1)} %broadcast_select_fusion.refs_0_), channel_id=1, source_target_pairs={{0,1},{1,0},{2,3},{3,2},{4,5},{5,4},{6,7},{7,6},{8,9},{9,8},{10,11... | collective-permute-start | bytes 1179656 | tf_op jit(solution)/shard_map/ppermute | solution.py:51
  56.7 15.1 %collective-permute-start.6 = (bf16[4,48,768]{2,1,0:T(8,128)(2,1)S(1)}, bf16[4,48,768]{2,1,0:T(8,128)(2,1)S(1)}, u32[]{:S(2)}, u32[]{:S(2)}) collective-permute-start(bf16[4,48,768]{2,1,0:T(8,128)(2,1)S(1)} %pad_maximum_fusion.4), channel_id=1, source_target_pairs={{0,1},{1,0},{2,3},{3,2},{4,5},{5,4},{6,7},{7,6},{8,9},{9,8},{10,11... | collective-permute-start | bytes 884744 | tf_op jit(solution)/shard_map/ppermute | solution.py:51
  57.6 8.6 %collective-permute-start.5 = (bf16[4,32,768]{2,1,0:T(8,128)(2,1)S(1)}, bf16[4,32,768]{2,1,0:T(8,128)(2,1)S(1)}, u32[]{:S(2)}, u32[]{:S(2)}) collective-permute-start(bf16[4,32,768]{2,1,0:T(8,128)(2,1)S(1)} %pad_maximum_fusion.6), channel_id=1, source_target_pairs={{0,16},{1,17},{2,18},{3,19},{4,20},{5,21},{6,22},{7,23},{8,24},{9,... | collective-permute-start | bytes 589832 | tf_op jit(solution)/shard_map/ppermute | solution.py:51
  71.8 7.9 %copy-start.14 = (bf16[256,768]{1,0:T(8,128)(2,1)}, bf16[256,768]{1,0:T(8,128)(2,1)S(1)}, u32[]{:S(2)}) copy-start(bf16[256,768]{1,0:T(8,128)(2,1)S(1)} %collective-permute-done.9.refs_6_) | copy-start | bytes 1179652
  75.3 23.2 %copy-start.15 = (bf16[256,768]{1,0:T(8,128)(2,1)}, bf16[256,768]{1,0:T(8,128)(2,1)S(1)}, u32[]{:S(2)}) copy-start(bf16[256,768]{1,0:T(8,128)(2,1)S(1)} %collective-permute-done.7.refs_1_) | copy-start | bytes 1179652
  76.2 22.3 %collective-permute-start.11 = (bf16[8,48,768]{2,1,0:T(8,128)(2,1)S(1)}, bf16[8,48,768]{2,1,0:T(8,128)(2,1)S(1)}, u32[]{:S(2)}, u32[]{:S(2)}) collective-permute-start(bf16[8,48,768]{2,1,0:T(8,128)(2,1)S(1)} %constant_dynamic-update-slice_fusion.5), channel_id=1, source_target_pairs={{0,16},{1,17},{2,18},{3,19},{4,20},{5,21},{6,22},{7,23},{8,24},{9,... | collective-permute-start | bytes 1769480 | tf_op jit(solution)/shard_map/ppermute | solution.py:51
  77.6 16.8 %collective-permute-start.10 = (bf16[8,32,768]{2,1,0:T(8,128)(2,1)S(1)}, bf16[8,32,768]{2,1,0:T(8,128)(2,1)S(1)}, u32[]{:S(2)}, u32[]{:S(2)}) collective-permute-start(bf16[8,32,768]{2,1,0:T(8,128)(2,1)S(1)} %constant_dynamic-update-slice_fusion), channel_id=1, source_target_pairs={{0,1},{1,0},{2,3},{3,2},{4,5},{5,4},{6,7},{7,6},{8,9},{9,8},{10,11... | collective-permute-start | bytes 1179656 | tf_op jit(solution)/shard_map/ppermute | solution.py:51
  79.1 30.4 %collective-permute-start.12 = (bf16[256,768]{1,0:T(8,128)(2,1)S(1)}, bf16[256,768]{1,0:T(8,128)(2,1)S(1)}, u32[]{:S(2)}, u32[]{:S(2)}) collective-permute-start(bf16[256,768]{1,0:T(8,128)(2,1)S(1)} %collective-permute-done.7.refs_1_), channel_id=1, source_target_pairs={{0,1},{1,0},{2,3},{3,2},{4,5},{5,4},{6,7},{7,6},{8,9},{9,8},{10,11... | collective-permute-start | bytes 1179656 | tf_op jit(solution)/shard_map/ppermute | solution.py:51
  94.5 15.4 %copy-start.4 = (bf16[16,32,768]{2,1,0:T(8,128)(2,1)}, bf16[16,32,768]{2,1,0:T(8,128)(2,1)S(1)}, u32[]{:S(2)}) copy-start(bf16[16,32,768]{2,1,0:T(8,128)(2,1)S(1)} %pad_maximum_fusion.1.refs_10_) | copy-start | bytes 2359300
  94.6 15.4 %copy-start.18 = (s32[1,8]{1,0:T(1,128)S(1)}, s32[1,8]{1,0:T(1,128)}, u32[]{:S(2)}) copy-start(s32[1,8]{1,0:T(1,128)} %param.19) | copy-start | bytes 100
  98.5 15.1 %copy-start.2 = (bf16[16,48,768]{2,1,0:T(8,128)(2,1)}, bf16[16,48,768]{2,1,0:T(8,128)(2,1)S(1)}, u32[]{:S(2)}) copy-start(bf16[16,48,768]{2,1,0:T(8,128)(2,1)S(1)} %pad_maximum_fusion.refs_12_) | copy-start | bytes 3538948
  109.5 4.1 %collective-permute-start.14 = (bf16[16,48,768]{2,1,0:T(8,128)(2,1)S(1)}, bf16[16,48,768]{2,1,0:T(8,128)(2,1)S(1)}, u32[]{:S(2)}, u32[]{:S(2)}) collective-permute-start(bf16[16,48,768]{2,1,0:T(8,128)(2,1)S(1)} %pad_maximum_fusion.refs_12_), channel_id=1, source_target_pairs={{0,8},{1,9},{2,10},{3,11},{4,12},{5,13},{6,14},{7,15},{8,0},{9,1},... | collective-permute-start | bytes 3538952 | tf_op jit(solution)/shard_map/ppermute | solution.py:51
  109.5 3.7 %collective-permute-start.13 = (bf16[16,32,768]{2,1,0:T(8,128)(2,1)S(1)}, bf16[16,32,768]{2,1,0:T(8,128)(2,1)}, u32[]{:S(2)}, u32[]{:S(2)}) collective-permute-start(bf16[16,32,768]{2,1,0:T(8,128)(2,1)S(1)} %pad_maximum_fusion.1.refs_10_), channel_id=1, source_target_pairs={{0,8},{1,9},{2,10},{3,11},{4,12},{5,13},{6,14},{7,15},{8,0},{9,1},... | collective-permute-start | bytes 2359304 | tf_op jit(solution)/shard_map/ppermute | solution.py:51
  159.0 133.0 %reduce-scatter.6.cloned.1.call-start = ((), (), s32[]{:S(2)}) async-start(), calls=%async_computation.5 | async-start | bytes 6635520 | tf_op jit(solution)/shard_map/reduce_scatter | solution.py:919
  191.8 155.4 %reduce-scatter.8.cloned.1.call-start = ((), (), s32[]{:S(2)}) async-start(), calls=%async_computation.6 | async-start | bytes 1658880 | tf_op jit(solution)/shard_map/reduce_scatter | solution.py:919
  200.7 19.8 %collective-permute-start.15 = (bf16[256,768]{1,0:T(8,128)(2,1)S(1)}, bf16[256,768]{1,0:T(8,128)(2,1)S(1)}, u32[]{:S(2)}, u32[]{:S(2)}) collective-permute-start(bf16[256,768]{1,0:T(8,128)(2,1)S(1)} %get-tuple-element.192), channel_id=1, source_target_pairs={{0,1},{1,0},{2,3},{3,2},{4,5},{5,4},{6,7},{7,6},{8,9},{9,8},{10,11... | collective-permute-start | bytes 1179656 | tf_op jit(solution)/shard_map/ppermute | solution.py:51
  202.6 34.2 %collective-permute-start.18 = (bf16[256,768]{1,0:T(8,128)(2,1)S(1)}, bf16[256,768]{1,0:T(8,128)(2,1)S(1)}, u32[]{:S(2)}, u32[]{:S(2)}) collective-permute-start(bf16[256,768]{1,0:T(8,128)(2,1)S(1)} %get-tuple-element.191), channel_id=1, source_target_pairs={{0,1},{1,0},{2,3},{3,2},{4,5},{5,4},{6,7},{7,6},{8,9},{9,8},{10,11... | collective-permute-start | bytes 1179656 | tf_op jit(solution)/shard_map/ppermute | solution.py:51
  208.3 28.5 %copy-start = (bf16[4,256,768]{2,1,0:T(8,128)(2,1)S(1)}, bf16[4,256,768]{2,1,0:T(8,128)(2,1)}, u32[]{:S(2)}) copy-start(bf16[4,256,768]{2,1,0:T(8,128)(2,1)} %token_product.2) | copy-start | bytes 4718596
  220.6 18.8 %copy-start.10 = (bf16[1,768]{1,0:T(2,128)(2,1)S(1)}, bf16[1,768]{1,0:T(2,128)(2,1)}, u32[]{:S(2)}) copy-start(bf16[1,768]{1,0:T(2,128)(2,1)} %get-tuple-element.213) | copy-start | bytes 4612
  220.6 18.8 %copy-start.11 = (bf16[1,768]{1,0:T(2,128)(2,1)S(1)}, bf16[1,768]{1,0:T(2,128)(2,1)}, u32[]{:S(2)}) copy-start(bf16[1,768]{1,0:T(2,128)(2,1)} %get-tuple-element.214) | copy-start | bytes 4612
  237.7 16.6 %collective-permute-start.17 = (bf16[16,24,1536]{2,1,0:T(8,128)(2,1)}, bf16[16,24,1536]{2,1,0:T(8,128)(2,1)S(1)}, u32[]{:S(2)}, u32[]{:S(2)}) collective-permute-start(bf16[16,24,1536]{2,1,0:T(8,128)(2,1)} %get-tuple-element.149), channel_id=1, source_target_pairs={{0,8},{1,9},{2,10},{3,11},{4,12},{5,13},{6,14},{7,15},{8,0},{9,1},... | collective-permute-start | bytes 3538952 | tf_op jit(solution)/shard_map/ppermute | solution.py:51
  241.0 13.3 %collective-permute-start.16 = (bf16[16,32,768]{2,1,0:T(8,128)(2,1)}, bf16[16,32,768]{2,1,0:T(8,128)(2,1)}, u32[]{:S(2)}, u32[]{:S(2)}) collective-permute-start(bf16[16,32,768]{2,1,0:T(8,128)(2,1)} %pad_maximum_fusion.3), channel_id=1, source_target_pairs={{0,8},{1,9},{2,10},{3,11},{4,12},{5,13},{6,14},{7,15},{8,0},{9,1},... | collective-permute-start | bytes 2359304 | tf_op jit(solution)/shard_map/ppermute | solution.py:51
  241.5 11.8 %collective-permute-start.19 = (bf16[256,768]{1,0:T(8,128)(2,1)}, bf16[256,768]{1,0:T(8,128)(2,1)}, u32[]{:S(2)}, u32[]{:S(2)}) collective-permute-start(bf16[256,768]{1,0:T(8,128)(2,1)} %get-tuple-element.189), channel_id=1, source_target_pairs={{0,2},{1,3},{2,0},{3,1},{4,6},{5,7},{6,4},{7,5},{8,10},{9,11},{10,... | collective-permute-start | bytes 1179656 | tf_op jit(solution)/shard_map/ppermute | solution.py:51
  248.8 5.5 %copy-start.1 = (bf16[3,256,768]{2,1,0:T(8,128)(2,1)S(1)}, bf16[3,256,768]{2,1,0:T(8,128)(2,1)}, u32[]{:S(2)}) copy-start(bf16[3,256,768]{2,1,0:T(8,128)(2,1)} %token_product.3) | copy-start | bytes 3538948
  254.4 19.6 %collective-permute-start.22 = (bf16[256,768]{1,0:T(8,128)(2,1)S(1)}, bf16[256,768]{1,0:T(8,128)(2,1)S(1)}, u32[]{:S(2)}, u32[]{:S(2)}) collective-permute-start(bf16[256,768]{1,0:T(8,128)(2,1)S(1)} %get-tuple-element.193), channel_id=1, source_target_pairs={{0,1},{1,0},{2,3},{3,2},{4,5},{5,4},{6,7},{7,6},{8,9},{9,8},{10,11... | collective-permute-start | bytes 1179656 | tf_op jit(solution)/shard_map/ppermute | solution.py:51
  256.5 17.5 %collective-permute-start.23 = (bf16[256,768]{1,0:T(8,128)(2,1)S(1)}, bf16[256,768]{1,0:T(8,128)(2,1)S(1)}, u32[]{:S(2)}, u32[]{:S(2)}) collective-permute-start(bf16[256,768]{1,0:T(8,128)(2,1)S(1)} %get-tuple-element.194), channel_id=1, source_target_pairs={{5,6},{6,5},{13,14},{14,13},{21,22},{22,21},{29,30},{30,29}} | collective-permute-start | bytes 1179656 | tf_op jit(solution)/shard_map/ppermute | solution.py:55
  257.4 34.6 %collective-permute-start.21 = (bf16[8,24,1536]{2,1,0:T(8,128)(2,1)S(1)}, bf16[8,24,1536]{2,1,0:T(8,128)(2,1)}, u32[]{:S(2)}, u32[]{:S(2)}) collective-permute-start(bf16[8,24,1536]{2,1,0:T(8,128)(2,1)S(1)} %fusion.2), channel_id=1, source_target_pairs={{0,1},{1,0},{2,3},{3,2},{4,5},{5,4},{6,7},{7,6},{8,9},{9,8},{10,11... | collective-permute-start | bytes 1769480 | tf_op jit(solution)/shard_map/ppermute | solution.py:51
  259.0 19.9 %collective-permute-start.20 = (bf16[8,32,768]{2,1,0:T(8,128)(2,1)S(1)}, bf16[8,32,768]{2,1,0:T(8,128)(2,1)}, u32[]{:S(2)}, u32[]{:S(2)}) collective-permute-start(bf16[8,32,768]{2,1,0:T(8,128)(2,1)S(1)} %bitcast.216), channel_id=1, source_target_pairs={{0,16},{1,17},{2,18},{3,19},{4,20},{5,21},{6,22},{7,23},{8,24},{9,... | collective-permute-start | bytes 1179656 | tf_op jit(solution)/shard_map/ppermute | solution.py:51
  262.3 51.2 %collective-permute-start.28 = (bf16[256,768]{1,0:T(8,128)(2,1)}, bf16[256,768]{1,0:T(8,128)(2,1)}, u32[]{:S(2)}, u32[]{:S(2)}) collective-permute-start(bf16[256,768]{1,0:T(8,128)(2,1)} %convert_element_type.353), channel_id=1, source_target_pairs={{4,0},{5,1},{6,2},{7,3},{12,8},{13,9},{14,10},{15,11},{20,16},{21,... | collective-permute-start | bytes 1179656 | tf_op jit(solution)/shard_map/ppermute | solution.py:55
  293.2 9.2 %collective-permute-start.25 = (bf16[4,24,1536]{2,1,0:T(8,128)(2,1)S(1)}, bf16[4,24,1536]{2,1,0:T(8,128)(2,1)S(1)}, u32[]{:S(2)}, u32[]{:S(2)}) collective-permute-start(bf16[4,24,1536]{2,1,0:T(8,128)(2,1)S(1)} %bitcast.221), channel_id=1, source_target_pairs={{0,16},{1,17},{2,18},{3,19},{4,20},{5,21},{6,22},{7,23},{8,24},{9,... | collective-permute-start | bytes 884744 | tf_op jit(solution)/shard_map/ppermute | solution.py:51
  296.6 5.7 %collective-permute-start.24 = (bf16[4,32,768]{2,1,0:T(8,128)(2,1)S(1)}, bf16[4,32,768]{2,1,0:T(8,128)(2,1)S(1)}, u32[]{:S(2)}, u32[]{:S(2)}) collective-permute-start(bf16[4,32,768]{2,1,0:T(8,128)(2,1)S(1)} %fusion.4), channel_id=1, source_target_pairs={{0,1},{1,0},{2,3},{3,2},{4,5},{5,4},{6,7},{7,6},{8,9},{9,8},{10,11... | collective-permute-start | bytes 589832 | tf_op jit(solution)/shard_map/ppermute | solution.py:51
  302.6 38.0 %copy-start.5 = (f32[256,768]{1,0:T(8,128)S(1)}, f32[256,768]{1,0:T(8,128)}, u32[]{:S(2)}) copy-start(f32[256,768]{1,0:T(8,128)} %get-tuple-element.138) | copy-start | bytes 2359300
  302.6 35.8 %collective-permute-start.27 = (bf16[2,24,1536]{2,1,0:T(8,128)(2,1)S(1)}, bf16[2,24,1536]{2,1,0:T(8,128)(2,1)S(1)}, u32[]{:S(2)}, u32[]{:S(2)}) collective-permute-start(bf16[2,24,1536]{2,1,0:T(8,128)(2,1)S(1)} %bitcast.225), channel_id=1, source_target_pairs={{0,4},{1,5},{2,6},{3,7},{4,0},{5,1},{6,2},{7,3},{8,12},{9,13},{10,... | collective-permute-start | bytes 442376 | tf_op jit(solution)/shard_map/ppermute | solution.py:51
  313.4 25.0 %collective-permute-start.26 = (bf16[2,32,768]{2,1,0:T(8,128)(2,1)S(1)}, bf16[2,32,768]{2,1,0:T(8,128)(2,1)S(1)}, u32[]{:S(2)}, u32[]{:S(2)}) collective-permute-start(bf16[2,32,768]{2,1,0:T(8,128)(2,1)S(1)} %bitcast.229), channel_id=1, source_target_pairs={{0,4},{1,5},{2,6},{3,7},{4,0},{5,1},{6,2},{7,3},{8,12},{9,13},{10,... | collective-permute-start | bytes 294920 | tf_op jit(solution)/shard_map/ppermute | solution.py:51
  338.4 6.8 %collective-permute-start.30 = (bf16[1,24,1536]{2,1,0:T(8,128)(2,1)S(1)}, bf16[1,24,1536]{2,1,0:T(8,128)(2,1)S(1)}, u32[]{:S(2)}, u32[]{:S(2)}) collective-permute-start(bf16[1,24,1536]{2,1,0:T(8,128)(2,1)S(1)} %add_convert_fusion.7), channel_id=1, source_target_pairs={{0,2},{1,3},{2,0},{3,1},{4,6},{5,7},{6,4},{7,5},{8,10},{9,11},{10,... | collective-permute-start | bytes 221192 | tf_op jit(solution)/shard_map/ppermute | solution.py:51
  338.6 4.8 %collective-permute-start.29 = (bf16[1,32,768]{2,1,0:T(8,128)(2,1)S(1)}, bf16[1,32,768]{2,1,0:T(8,128)(2,1)S(1)}, u32[]{:S(2)}, u32[]{:S(2)}) collective-permute-start(bf16[1,32,768]{2,1,0:T(8,128)(2,1)S(1)} %add_convert_fusion.8), channel_id=1, source_target_pairs={{0,2},{1,3},{2,0},{3,1},{4,6},{5,7},{6,4},{7,5},{8,10},{9,11},{10,... | collective-permute-start | bytes 147464 | tf_op jit(solution)/shard_map/ppermute | solution.py:51
  (6 other events, 11.9 us)
Sparse Core Ops, SparseCore 0:
  11.5 124.3 all-gather.1
  159.1 32.6 reduce-scatter.3
  195.0 94.0 reduce-scatter.5
  292.2 50.3 reduce-scatter.7

commit v11 on v10

--- a/solution.py
+++ b/solution.py
@@ -716,7 +716,7 @@
 def weight_kernel(blocks, first, rows, runs, *refs):
     spots = refs[:blocks]
     (near_ref, core_ref, own_ref, dq_ref, wq_ref, h1_ref, dkp_ref, dvp_ref, dkn_ref, dvn_ref,
-     q_send, q_keep, kv_send, kv_keep, gown_ref, sums_ref, x_ref, xt_ref, sems) = refs[blocks:]
+     send_ref, keep_ref, gown_ref, sums_ref, x_ref, xt_ref, sems) = refs[blocks:]
     core = core_ref[0]
     step = pl.program_id(0)
 
@@ -738,20 +738,23 @@
     part = dq.shape[1]
     width = x_ref.shape[1]
     gown_ref[...] += nt(dq, wq_ref[...].reshape(width, part)) * scale
-    away, here = halves((tn(own_ref[...], dq) * scale).astype(BF), runs, core)
-    q_send[...] = away.reshape(q_send.shape)
-    q_keep[...] = here.reshape(q_send.shape)
+    half = send_ref.shape[0]
+    each = width // (2 * half)
+
+    def put(i, grad):
+        away, here = halves(grad.astype(BF), runs, core)
+        send_ref[:, i * each : (i + 1) * each, :] = away.reshape(half, each, part)
+        keep_ref[:, i * each : (i + 1) * each, :] = here.reshape(half, each, part)
+
+    put(WQ, tn(own_ref[...], dq) * scale)
     sums_ref[0:1, :] = jnp.sum(dq.astype(F32), axis=0, keepdims=True) * scale
 
     def body(near):
-        for i, (p_ref, n_ref) in enumerate(((dkp_ref, dkn_ref), (dvp_ref, dvn_ref))):
+        for i, p_ref, n_ref in ((WK, dkp_ref, dkn_ref), (WV, dvp_ref, dvn_ref)):
             grad = mm(xt_ref[:, :PROMPT], p_ref[...])
             if near:
                 grad = grad + mm(xt_ref[:, PROMPT:], n_ref[...])
-            away, here = halves(grad.astype(BF), runs, core)
-            shape = kv_send.shape[:2] + (part,)
-            kv_send[:, :, i * part : (i + 1) * part] = away.reshape(shape)
-            kv_keep[:, :, i * part : (i + 1) * part] = here.reshape(shape)
+            put(i, grad)
 
     pl.when(near_ref[0] == 0)(lambda: body(False))
     pl.when(near_ref[0] > 0)(lambda: body(True))
@@ -769,7 +772,7 @@
     shape = jax.ShapeDtypeStruct
     owners, each = got.shape[0], width // got.shape[0]
     half = owners // 2
-    slab = lambda size: pl.BlockSpec((half, each, size), lambda g: (0, 0, g))
+    slab = pl.BlockSpec((half, 3 * each, part), lambda g: (0, 0, g))
     return pl.pallas_call(
         functools.partial(weight_kernel, blocks, first, rows, runs),
         grid=(steps,),
@@ -782,11 +785,10 @@
             whole((rows, width)), cols(PROMPT), cols(PROMPT), cols(tall - PROMPT), cols(tall - PROMPT),
         ],
         out_specs=[
-            slab(part), slab(part), slab(2 * part), slab(2 * part), whole((rows, width)), cols(8),
+            slab, slab, whole((rows, width)), cols(8),
         ],
         out_shape=[
-            shape((half, each, width), BF), shape((half, each, width), BF),
-            shape((half, each, 2 * width), BF), shape((half, each, 2 * width), BF),
+            shape((half, 3 * each, width), BF), shape((half, 3 * each, width), BF),
             shape((rows, width), F32), shape((8, width), F32),
         ],
         scratch_shapes=[
@@ -925,21 +927,19 @@
             0, parts, first_near, near, grad_context, context, queries, keys_p, values_p, log_total,
             seg_own, seg_near,
         )
-        grads, dkp, dvp, dqp = tie(grads, dkp, dvp, dqp)
+        shared_p = product_call(first_near, near, dkp, dvp, squares, rows)
+        grads, shared_p, dqp = tie(grads, shared_p, dqp)
         grads = level(grads, ("x", "y"))
-        shared_p = product_call(first_near, near, dkp, dvp, squares, rows)
         returned = Return(plan, rows)
         returned.prompt_one(shared_p)
         dkn, dvn, dq = back_call(
             0, parts, None, near, grad_context, context, queries, keys_n, values_n, log_total,
             seg_own, seg_near, dqp,
         )
-        q_send, q_keep, kv_send, kv_keep, grad_own, sums_qkv = weight_call(
+        send, keep, grad_own, sums_qkv = weight_call(
             spots, first_near, near, own, dq, squares, grad_h1, dkp, dvp, dkn, dvn, core, runs
         )
-        q_send, q_keep, kv_send, kv_keep, returned.same, dkn, dvn = tie(
-            q_send, q_keep, kv_send, kv_keep, returned.same, dkn, dvn
-        )
+        send, keep, returned.same, dkn, dvn = tie(send, keep, returned.same, dkn, dvn)
         returned.prompt_two()
         shared_n = product_call(None, near, dkn, dvn, squares, rows)
 
@@ -958,44 +958,38 @@
         place = core[0]
         pick = Reduce(plan, [])
         if step % 8:
-            q_send, q_keep, kv_send, kv_keep = [
-                v.reshape(count // 2, step, -1) for v in (q_send, q_keep, kv_send, kv_keep)
-            ]
-        q_send = jnp.concatenate([q_send, pick.cut(d_lines, core_bit, 1 - place)], 1)
-        q_keep = jnp.concatenate([q_keep, pick.cut(d_lines, core_bit, place)], 1)
-        r_q = Reduce(plan, [q_keep, plan.swap(q_send, core_bit)], left)
-        r_kv = Reduce(plan, [kv_keep, plan.swap(kv_send, core_bit)], left)
-        for one, two in zip(plan.x + plan.y + plan.z[::-1], plan.y + plan.x + plan.z[::-1]):
-            n = len(r_q.terms)
-            held = [*r_q.terms, *r_kv.terms]
-            if one == plan.x[0]:
-                *held, shared_n, returned.same = tie(*held, shared_n, returned.same)
+            real = lambda v: v.reshape(16, 3, count // 32, step, width).transpose(0, 2, 1, 3, 4)
+            send, keep = [real(v).reshape(count // 2, 3 * step, width) for v in (send, keep)]
+        send = jnp.concatenate([send, pick.cut(d_lines, core_bit, 1 - place)], 1)
+        keep = jnp.concatenate([keep, pick.cut(d_lines, core_bit, place)], 1)
+        reduce = Reduce(plan, [keep, plan.swap(send, core_bit)], left)
+        for bit in plan.x + plan.y + plan.z[::-1]:
+            held = reduce.terms
+            if bit == plan.x[0]:
+                *held, returned.same = tie(*held, returned.same)
+                returned.prompt_three()
+            elif bit == plan.y[0]:
+                *held, grads, shared_n = tie(*held, grads, shared_n)
+                grads = level(grads, "z")
                 returned.near(shared_n)
-                returned.prompt_three()
-            elif one == plan.y[0]:
-                *held, grads, returned.own = tie(*held, grads, returned.own)
-                grads = level(grads, "z")
-            elif one == plan.z[-1]:
-                held = tie(*held)
-            else:
+            elif bit == plan.z[-1]:
+                *held, returned.own = tie(*held, returned.own)
+            elif bit == plan.z[0]:
                 *held, returned.back = tie(*held, returned.back)
-            r_q.terms, r_kv.terms = held[:n], held[n:]
-            r_q.stage(one)
-            r_kv.stage(two)
+            reduce.terms = list(held)
+            reduce.stage(bit)
         o_ab = grads.reshape(-1, width).astype(F32)
         grad_tokens = grad_own + returned.total()
-        o_query = r_q.result()
-        o_line = o_query[step]
-        o_both = r_kv.result().reshape(step, parts, 2, width // parts)
-
+        o_first = reduce.result()
+        o_line = o_first[3 * step]
         o_small = [o_line[i * step : (i + 1) * step] for i in range(small)]
         o_bin = o_line[small * step : (small + wide) * step]
         return (
             layer_out[None],
             grad_tokens.astype(BF)[None],
-            o_query[:step],
-            o_both[:, :, 0].reshape(step, width),
-            o_both[:, :, 1].reshape(step, width),
+            o_first[:step],
+            o_first[step : 2 * step],
+            o_first[2 * step : 3 * step],
             o_ab[wide * step : (wide + 1) * step],
             jnp.concatenate([o_ab[i * step : (i + 1) * step] for i in range(wide + 1, 2 * wide + 1)], 1),
             o_ab[: wide * step],

time: 358 us -> 347 us (0.969)
  starting transfers between devices: 62.2 us -> 54.6 us
  waiting for transfers between devices: 162 us -> 155 us
    ppermute x27 -> x22, starting transfers between devices: 55.6 us -> 48 us  [swap(): return lax.ppermute(value, AXES, [(i, i ^ mask) for i in range(self.count)])]
    reduce_scatter x3, waiting for transfers between devices: 20.2 us -> 14.8 us  [per_device(): lax.psum_scatter(value, axes, scatter_dimension=0, tiled=True)]
    ppermute x27 -> x22, waiting for transfers between devices: 127 us -> 124 us  [swap(): return lax.ppermute(value, AXES, [(i, i ^ mask) for i in range(self.count)])]
  transfers between devices with their start and end apart: 35 -> 30, of which waited for: 20 -> 19; matrix products, arithmetic and copies ran while one was open for 8% -> 9% of each run, Pallas kernels for 16% -> 17%
where the time goes in v11:
time: 347 us; the launch traced here: 345 us
  waiting for transfers between devices  155 us (45%)
  Pallas kernels  81.5 us (23%)
  starting transfers between devices  54.6 us (16%)
  local copies, waits for them, and re-layouts  20.4 us (6%)
  other arithmetic  19.3 us (6%)
  between operations  14.3 us (4%)
    ppermute x22, waiting for transfers between devices, swap(): return lax.ppermute(value, AXES, [(i, i ^ mask) for i in range(self.count)])  124 us
    ppermute x22, starting transfers between devices, swap(): return lax.ppermute(value, AXES, [(i, i ^ mask) for i in range(self.count)])  48 us
    pallas_call x1, Pallas kernels, middle_call(): pl.pallas_call(functools.partial(middle_kernel, wide, mapped), grid=(2 *...  20.9 us
    pallas_call x1, Pallas kernels, attention_call(): pl.pallas_call(functools.partial(attention_kernel, blocks, first, rows, p...  19 us
    pallas_call x2, Pallas kernels, back_call(): pl.pallas_call(functools.partial(back_kernel, rows, bound, dq0 is not Non...  17.9 us
    reduce_scatter x3, waiting for transfers between devices, per_device(): lax.psum_scatter(value, axes, scatter_dimension=0, tiled=True)  14.8 us
    ppermute x4, waiting for transfers between devices, send(): return lax.ppermute(value, AXES, pairs)  12.6 us
    pallas_call x1, Pallas kernels, weight_call(): pl.pallas_call(functools.partial(weight_kernel, blocks, first, rows, runs...  11.4 us
  transfers between devices with their start and end apart: 30, of which 19 were waited for; matrix products, arithmetic and copies ran while one was open for 9% of the time, Pallas kernels for 17%

profile of v11, /device:TPU:0, one launch (start us, length us, event | category | flops | bytes accessed | tf_op | source)
XLA Modules:
  0.0 345.4 jit_solution(14262347586549733555)
XLA Ops:
  9.4 1.8 pack.1
  11.3 3.1 collective-permute-start
  14.4 2.6 collective-permute-start.1
  17.0 3.8 %collective-permute-start.3 = (bf16[256,768]{1,0:T(8,128)(2,1)}, bf16[256,768]{1,0:T(8,128)(2,1)S(1)}, u32[]{:S(2)}, u32[]{:S(2)}) collective-permute-start(bf16[256,768]{1,0:T(8,128)(2,1)} %bitcast.160), channel_id=1, source_target_pairs={{0,4},{1,5},{2,6},{3,7},{8,12},{9,13},{10,14},{11,15},{16,20},{17,... | collective-permute-start | bytes 1179656 | tf_op jit(solution)/shard_map/ppermute | solution.py:55
  20.9 1.6 collective-permute-start.4
  25.8 12.6 %collective-permute-done.3 = bf16[256,768]{1,0:T(8,128)(2,1)S(1)} collective-permute-done((bf16[256,768]{1,0:T(8,128)(2,1)}, bf16[256,768]{1,0:T(8,128)(2,1)S(1)}, u32[]{:S(2)}, u32[]{:S(2)}) %collective-permute-start.3) | collective-permute-done | bytes 393248 | tf_op jit(solution)/shard_map/ppermute | solution.py:55
  40.2 16.6 %collective-permute-start.7 = (bf16[256,768]{1,0:T(8,128)(2,1)S(1)}, bf16[256,768]{1,0:T(8,128)(2,1)S(1)}, u32[]{:S(2)}, u32[]{:S(2)}) collective-permute-start(bf16[256,768]{1,0:T(8,128)(2,1)S(1)} %broadcast_select_fusion.refs_0_), channel_id=1, source_target_pairs={{0,2},{1,3},{2,0},{3,1},{4,6},{5,7},{6,4},{7,5},{8,10},{9,11},{10,... | collective-permute-start | bytes 1179656 | tf_op jit(solution)/shard_map/ppermute | solution.py:51
  57.7 1.4 collective-permute-start.6
  59.8 6.3 %collective-permute-done.5 = bf16[4,32,768]{2,1,0:T(8,128)(2,1)S(1)} collective-permute-done((bf16[4,32,768]{2,1,0:T(8,128)(2,1)S(1)}, bf16[4,32,768]{2,1,0:T(8,128)(2,1)S(1)}, u32[]{:S(2)}, u32[]{:S(2)}) %collective-permute-start.5) | collective-permute-done | bytes 196640 | tf_op jit(solution)/shard_map/ppermute | solution.py:51
  66.2 5.6 %collective-permute-done.6 = bf16[4,48,768]{2,1,0:T(8,128)(2,1)S(1)} collective-permute-done((bf16[4,48,768]{2,1,0:T(8,128)(2,1)S(1)}, bf16[4,48,768]{2,1,0:T(8,128)(2,1)S(1)}, u32[]{:S(2)}, u32[]{:S(2)}) %collective-permute-start.6) | collective-permute-done | bytes 294944 | tf_op jit(solution)/shard_map/ppermute | solution.py:51
  71.8 3.5 %collective-permute-done.7.refs_1_ = bf16[256,768]{1,0:T(8,128)(2,1)S(1)} collective-permute-done((bf16[256,768]{1,0:T(8,128)(2,1)S(1)}, bf16[256,768]{1,0:T(8,128)(2,1)S(1)}, u32[]{:S(2)}, u32[]{:S(2)}) %collective-permute-start.7) | collective-permute-done | bytes 393248 | tf_op jit(solution)/shard_map/ppermute | solution.py:51
  75.3 1.5 collective-permute-start.11
  76.8 1.5 collective-permute-start.10
  78.8 14.4 %collective-permute-done.10 = bf16[8,32,768]{2,1,0:T(8,128)(2,1)S(1)} collective-permute-done((bf16[8,32,768]{2,1,0:T(8,128)(2,1)S(1)}, bf16[8,32,768]{2,1,0:T(8,128)(2,1)S(1)}, u32[]{:S(2)}, u32[]{:S(2)}) %collective-permute-start.10) | collective-permute-done | bytes 393248 | tf_op jit(solution)/shard_map/ppermute | solution.py:51
  93.3 3.9 %collective-permute-done.11 = bf16[8,48,768]{2,1,0:T(8,128)(2,1)S(1)} collective-permute-done((bf16[8,48,768]{2,1,0:T(8,128)(2,1)S(1)}, bf16[8,48,768]{2,1,0:T(8,128)(2,1)S(1)}, u32[]{:S(2)}, u32[]{:S(2)}) %collective-permute-start.11) | collective-permute-done | bytes 589856 | tf_op jit(solution)/shard_map/ppermute | solution.py:51
  97.3 10.9 %collective-permute-done.12.refs_3_ = bf16[256,768]{1,0:T(8,128)(2,1)} collective-permute-done((bf16[256,768]{1,0:T(8,128)(2,1)S(1)}, bf16[256,768]{1,0:T(8,128)(2,1)}, u32[]{:S(2)}, u32[]{:S(2)}) %collective-permute-start.12) | collective-permute-done | bytes 393248 | tf_op jit(solution)/shard_map/ppermute | solution.py:51
  110.6 1.3 collective-permute-done.13.refs_11_
  113.4 19.0 %attention.1 = (bf16[32,72,768]{2,1,0:T(8,128)(2,1)}, bf16[256,768]{1,0:T(8,128)(2,1)}, bf16[1024,768]{1,0:T(8,128)(2,1)}, bf16[1024,768]{1,0:T(8,128)(2,1)}, bf...) custom-call(bf16[256,768]{1,0:T(8,128)(2,1)} %copy-done.8, ...), custom_call_target="tpu_custom_call" | custom-call | flops 9865003008 | bytes 12582912 | tf_op jit(solution)/shard_map/attention/pallas_call | solution.py:342
  132.4 3.3 all-gather.2.cloned.1.call-done
  138.0 20.9 %middle.1 = (bf16[256,768]{1,0:T(8,128)(2,1)}, f32[256,768]{1,0:T(8,128)}, bf16[256,768]{1,0:T(8,128)(2,1)}, bf16[32,216,768]{2,1,0:T(8,128)(2,1)}, f32[8,768]{1,0:T(8,128)}, /*index=5*/f32[8,768]{1,0:T(8,128)}) custom-call(bf16[256,768]{1,0:T(8,128)(2,1)} %get-tuple-element.97.ctx_ref.refs_2_, bf16[256,768]{1,0:T(8,128)(2,1)} %bitcast.165, ...), custom_call_target="tpu_custom_call" | custom-call | flops 8153726976 | bytes 33554432 | tf_op jit(solution)/shard_map/middle/pallas_call | solution.py:567
  158.9 12.5 %attention_back.2 = (bf16[1024,768]{1,0:T(8,128)(2,1)}, bf16[1024,768]{1,0:T(8,128)(2,1)}, f32[768,256]{1,0:T(8,128)}) custom-call(s32[1]{0:T(128)} %bitcast.9.refs_7_.refs_0_.near_ref, bf16[256,768]{1,0:T(8,128)(2,1)} %get-tuple-element.100.refs_1_, bf16[256,768]{1,0:T(8,128)(2,1)} %get-tuple-element.97.ctx_ref.refs_2_, ...), custom_call_target="tpu_custom_call" | custom-call | flops 16106127360 | bytes 6291456 | tf_op jit(solution)/shard_map/attention_back/pallas_call | solution.py:659
  171.4 6.4 %token_product.2 = bf16[4,256,768]{2,1,0:T(8,128)(2,1)} custom-call(s32[1]{0:T(128)} %bitcast.9.refs_7_.refs_0_.near_ref, bf16[1024,768]{1,0:T(8,128)(2,1)} %get-tuple-element.108.dk_ref.refs_13_, bf16[1024,768]{1,0:T(8,128)(2,1)} %get-tuple-element.109.dv_ref.refs_14_, bf16[32,72,768]{2,1,0:T(8,128)(2,1)} %get-tuple-element.110.wk_ref.wv_ref.refs_11_, ...), custom_call_target="tpu_custom_call" | custom-call | flops 2415919104 | bytes 4718592 | tf_op jit(solution)/shard_map/token_product/pallas_call | solution.py:697
  177.8 13.5 %reduce-scatter.4.cloned.1.call-done = bf16[16,216,768]{2,1,0:T(8,128)(2,1)} async-done(((bf16[32,216,768]{2,1,0:T(8,128)(2,1)}), bf16[16,216,768]{2,1,0:T(8,128)(2,1)}) %reduce-scatter.4.cloned.1.call-update) | async-done | bytes 5308432 | tf_op jit(solution)/shard_map/reduce_scatter | solution.py:921
  193.0 1.8 collective-permute-start.15
  195.1 5.4 %attention_back.3 = (bf16[768,768]{1,0:T(8,128)(2,1)}, bf16[768,768]{1,0:T(8,128)(2,1)}, f32[768,256]{1,0:T(8,128)}) custom-call(s32[1]{0:T(128)} %bitcast.9.refs_7_.refs_0_.near_ref, bf16[256,768]{1,0:T(8,128)(2,1)} %get-tuple-element.100.refs_1_, bf16[256,768]{1,0:T(8,128)(2,1)} %get-tuple-element.97.ctx_ref.refs_2_, ...), custom_call_target="tpu_custom_call" | custom-call | flops 12079595520 | bytes 4718592 | tf_op jit(solution)/shard_map/attention_back/pallas_call | solution.py:659
  200.6 11.4 %weight_product.1 = (bf16[16,72,768]{2,1,0:T(8,128)(2,1)}, bf16[16,72,768]{2,1,0:T(8,128)(2,1)}, f32[256,768]{1,0:T(8,128)}, f32[8,768]{1,0:T(8,128)}) custom-call(bf16[256,768]{1,0:T(8,128)(2,1)} %copy-done.8, bf16[256,768]{1,0:T(8,128)(2,1)} %copy-done.14, bf16[256,768]{1,0:T(8,128)(2,1)} %copy-done.15, bf16[256,768]{1,0:T(8,128)(2,1)} %collective-permute-done.12.refs_3_, ...), custom_call_target="tpu_custom_call" | custom-call | flops 4227858432 | bytes 16515072 | tf_op jit(solution)/shard_map/weight_product/pallas_call | solution.py:776
  214.7 7.7 %collective-permute-done.17 = bf16[256,768]{1,0:T(8,128)(2,1)} collective-permute-done((bf16[256,768]{1,0:T(8,128)(2,1)S(1)}, bf16[256,768]{1,0:T(8,128)(2,1)}, u32[]{:S(2)}, u32[]{:S(2)}) %collective-permute-start.17) | collective-permute-done | bytes 393248 | tf_op jit(solution)/shard_map/ppermute | solution.py:51
  222.4 2.0 fusion.1
  224.5 1.5 pad_maximum_fusion.1
  226.0 1.5 collective-permute-start.18
  227.5 1.8 pad_maximum_fusion
  229.2 8.5 %collective-permute-done.18 = bf16[256,768]{1,0:T(8,128)(2,1)} collective-permute-done((bf16[256,768]{1,0:T(8,128)(2,1)}, bf16[256,768]{1,0:T(8,128)(2,1)}, u32[]{:S(2)}, u32[]{:S(2)}) %collective-permute-start.18) | collective-permute-done | bytes 393248 | tf_op jit(solution)/shard_map/ppermute | solution.py:51
  238.9 2.4 add_convert_fusion
  241.3 1.4 collective-permute-start.19
  242.7 4.1 %token_product.3 = bf16[3,256,768]{2,1,0:T(8,128)(2,1)} custom-call(s32[1]{0:T(128)} %bitcast.9.refs_7_.refs_0_.near_ref, bf16[768,768]{1,0:T(8,128)(2,1)} %get-tuple-element.131.refs_15_.dk_ref, bf16[768,768]{1,0:T(8,128)(2,1)} %get-tuple-element.132.refs_16_.dv_ref, bf16[32,72,768]{2,1,0:T(8,128)(2,1)} %get-tuple-element.110.wk_ref.wv_ref.refs_11_, ...), custom_call_target="tpu_custom_call" | custom-call | flops 1811939328 | bytes 3538944 | tf_op jit(solution)/shard_map/token_product/pallas_call | solution.py:697
  246.9 1.3 collective-permute-start.24
  248.2 2.3 constant_dynamic-slice_fusion.4
  251.5 27.7 %collective-permute-done.19 = bf16[8,80,768]{2,1,0:T(8,128)(2,1)} collective-permute-done((bf16[8,80,768]{2,1,0:T(8,128)(2,1)}, bf16[8,80,768]{2,1,0:T(8,128)(2,1)}, u32[]{:S(2)}, u32[]{:S(2)}) %collective-permute-start.19) | collective-permute-done | bytes 983072 | tf_op jit(solution)/shard_map/ppermute | solution.py:51
  279.2 1.3 reduce-scatter.6.cloned.1.call-done
  280.5 1.2 slice_bitcast_fusion.1
  281.7 2.1 collective-permute-start.21
  284.5 1.2 fusion.2
  286.9 6.7 %collective-permute-done.21 = bf16[256,768]{1,0:T(8,128)(2,1)S(1)} collective-permute-done((bf16[256,768]{1,0:T(8,128)(2,1)S(1)}, bf16[256,768]{1,0:T(8,128)(2,1)S(1)}, u32[]{:S(2)}, u32[]{:S(2)}) %collective-permute-start.21) | collective-permute-done | bytes 393248 | tf_op jit(solution)/shard_map/ppermute | solution.py:51
  293.7 1.1 fusion
  294.8 8.8 %collective-permute-done.20 = bf16[4,80,768]{2,1,0:T(8,128)(2,1)S(1)} collective-permute-done((bf16[4,80,768]{2,1,0:T(8,128)(2,1)S(1)}, bf16[4,80,768]{2,1,0:T(8,128)(2,1)S(1)}, u32[]{:S(2)}, u32[]{:S(2)}) %collective-permute-start.20) | collective-permute-done | bytes 491552 | tf_op jit(solution)/shard_map/ppermute | solution.py:51
  303.8 10.0 %collective-permute-start.23 = (bf16[2,80,768]{2,1,0:T(8,128)(2,1)S(1)}, bf16[2,80,768]{2,1,0:T(8,128)(2,1)S(1)}, u32[]{:S(2)}, u32[]{:S(2)}) collective-permute-start(bf16[2,80,768]{2,1,0:T(8,128)(2,1)S(1)} %bitcast.169), channel_id=1, source_target_pairs={{0,4},{1,5},{2,6},{3,7},{4,0},{5,1},{6,2},{7,3},{8,12},{9,13},{10,... | collective-permute-start | bytes 737288 | tf_op jit(solution)/shard_map/ppermute | solution.py:51
  313.9 14.5 %collective-permute-done.23 = bf16[2,80,768]{2,1,0:T(8,128)(2,1)S(1)} collective-permute-done((bf16[2,80,768]{2,1,0:T(8,128)(2,1)S(1)}, bf16[2,80,768]{2,1,0:T(8,128)(2,1)S(1)}, u32[]{:S(2)}, u32[]{:S(2)}) %collective-permute-start.23) | collective-permute-done | bytes 245792 | tf_op jit(solution)/shard_map/ppermute | solution.py:51
  329.5 4.2 %collective-permute-done.25 = bf16[1,80,768]{2,1,0:T(8,128)(2,1)S(1)} collective-permute-done((bf16[1,80,768]{2,1,0:T(8,128)(2,1)S(1)}, bf16[1,80,768]{2,1,0:T(8,128)(2,1)S(1)}, u32[]{:S(2)}, u32[]{:S(2)}) %collective-permute-start.25) | collective-permute-done | bytes 122912 | tf_op jit(solution)/shard_map/ppermute | solution.py:51
  (144 shorter events, 31.0 us)
Async XLA Ops:
  7.2 128.6 %all-gather.2.cloned.1.call-start = ((), (), s32[]{:S(2)}) async-start(), calls=%async_computation.3 | async-start | bytes 11354112 | tf_op jit(solution)/shard_map/all_gather | solution.py:847
  11.3 180.1 %reduce-scatter.4.cloned.1.call-start = ((), (), s32[]{:S(2)}) async-start(), calls=%async_computation.4 | async-start | bytes 15925248 | tf_op jit(solution)/shard_map/reduce_scatter | solution.py:921
  11.3 28.8 %collective-permute-start = (bf16[80,768]{1,0:T(8,128)(2,1)}, bf16[80,768]{1,0:T(8,128)(2,1)S(1)}, u32[]{:S(2)}, u32[]{:S(2)}) collective-permute-start(bf16[80,768]{1,0:T(8,128)(2,1)} %get-tuple-element.83), channel_id=1, source_target_pairs={{0,2},{1,3},{2,0},{3,1},{4,6},{5,7},{6,4},{7,5},{8,10},{9,11},{10,... | collective-permute-start | bytes 368648 | tf_op jit(solution)/shard_map/ppermute | solution.py:51
  14.4 25.8 %collective-permute-start.1 = (bf16[80,768]{1,0:T(8,128)(2,1)}, bf16[80,768]{1,0:T(8,128)(2,1)S(1)}, u32[]{:S(2)}, u32[]{:S(2)}) collective-permute-start(bf16[80,768]{1,0:T(8,128)(2,1)} %get-tuple-element.83), channel_id=1, source_target_pairs={{0,4},{1,5},{2,6},{3,7},{4,0},{5,1},{6,2},{7,3},{8,12},{9,13},{10,... | collective-permute-start | bytes 368648 | tf_op jit(solution)/shard_map/ppermute | solution.py:51
  17.0 23.2 %collective-permute-start.2 = (bf16[80,768]{1,0:T(8,128)(2,1)}, bf16[80,768]{1,0:T(8,128)(2,1)S(1)}, u32[]{:S(2)}, u32[]{:S(2)}) collective-permute-start(bf16[80,768]{1,0:T(8,128)(2,1)} %get-tuple-element.83), channel_id=1, source_target_pairs={{0,6},{1,7},{2,4},{3,5},{4,2},{5,3},{6,0},{7,1},{8,14},{9,15},{10,... | collective-permute-start | bytes 368648 | tf_op jit(solution)/shard_map/ppermute | solution.py:51
  17.0 21.4 %collective-permute-start.3 = (bf16[256,768]{1,0:T(8,128)(2,1)}, bf16[256,768]{1,0:T(8,128)(2,1)S(1)}, u32[]{:S(2)}, u32[]{:S(2)}) collective-permute-start(bf16[256,768]{1,0:T(8,128)(2,1)} %bitcast.160), channel_id=1, source_target_pairs={{0,4},{1,5},{2,6},{3,7},{8,12},{9,13},{10,14},{11,15},{16,20},{17,... | collective-permute-start | bytes 1179656 | tf_op jit(solution)/shard_map/ppermute | solution.py:55
  20.9 19.4 %collective-permute-start.4 = (bf16[256,768]{1,0:T(8,128)(2,1)}, bf16[256,768]{1,0:T(8,128)(2,1)S(1)}, u32[]{:S(2)}, u32[]{:S(2)}) collective-permute-start(bf16[256,768]{1,0:T(8,128)(2,1)} %bitcast.161), channel_id=1, source_target_pairs={{0,1},{1,0},{2,3},{3,2},{4,5},{5,4},{6,7},{7,6},{8,9},{9,8},{10,11... | collective-permute-start | bytes 1179656 | tf_op jit(solution)/shard_map/ppermute | solution.py:51
  38.4 33.3 %collective-permute-start.9 = (bf16[256,768]{1,0:T(8,128)(2,1)}, bf16[256,768]{1,0:T(8,128)(2,1)S(1)}, u32[]{:S(2)}, u32[]{:S(2)}) collective-permute-start(bf16[256,768]{1,0:T(8,128)(2,1)} %bitcast.162), channel_id=1, source_target_pairs={{5,6},{6,5},{13,14},{14,13},{21,22},{22,21},{29,30},{30,29}} | collective-permute-start | bytes 1179656 | tf_op jit(solution)/shard_map/ppermute | solution.py:55
  40.2 53.1 %copy-start.8 = (bf16[256,768]{1,0:T(8,128)(2,1)}, bf16[256,768]{1,0:T(8,128)(2,1)S(1)}, u32[]{:S(2)}) copy-start(bf16[256,768]{1,0:T(8,128)(2,1)S(1)} %broadcast_select_fusion.refs_0_) | copy-start | bytes 1179652
  40.2 53.1 %copy-start.12 = (bf16[256,768]{1,0:T(8,128)(2,1)}, bf16[256,768]{1,0:T(8,128)(2,1)S(1)}, u32[]{:S(2)}) copy-start(bf16[256,768]{1,0:T(8,128)(2,1)S(1)} %collective-permute-done.4.refs_5_) | copy-start | bytes 1179652
  40.2 35.0 %collective-permute-start.7 = (bf16[256,768]{1,0:T(8,128)(2,1)S(1)}, bf16[256,768]{1,0:T(8,128)(2,1)S(1)}, u32[]{:S(2)}, u32[]{:S(2)}) collective-permute-start(bf16[256,768]{1,0:T(8,128)(2,1)S(1)} %broadcast_select_fusion.refs_0_), channel_id=1, source_target_pairs={{0,2},{1,3},{2,0},{3,1},{4,6},{5,7},{6,4},{7,5},{8,10},{9,11},{10,... | collective-permute-start | bytes 1179656 | tf_op jit(solution)/shard_map/ppermute | solution.py:51
  56.9 18.4 %collective-permute-start.8 = (bf16[256,768]{1,0:T(8,128)(2,1)S(1)}, bf16[256,768]{1,0:T(8,128)(2,1)S(1)}, u32[]{:S(2)}, u32[]{:S(2)}) collective-permute-start(bf16[256,768]{1,0:T(8,128)(2,1)S(1)} %broadcast_select_fusion.refs_0_), channel_id=1, source_target_pairs={{0,1},{1,0},{2,3},{3,2},{4,5},{5,4},{6,7},{7,6},{8,9},{9,8},{10,11... | collective-permute-start | bytes 1179656 | tf_op jit(solution)/shard_map/ppermute | solution.py:51
  57.7 14.0 %collective-permute-start.6 = (bf16[4,48,768]{2,1,0:T(8,128)(2,1)S(1)}, bf16[4,48,768]{2,1,0:T(8,128)(2,1)S(1)}, u32[]{:S(2)}, u32[]{:S(2)}) collective-permute-start(bf16[4,48,768]{2,1,0:T(8,128)(2,1)S(1)} %pad_maximum_fusion.4), channel_id=1, source_target_pairs={{0,1},{1,0},{2,3},{3,2},{4,5},{5,4},{6,7},{7,6},{8,9},{9,8},{10,11... | collective-permute-start | bytes 884744 | tf_op jit(solution)/shard_map/ppermute | solution.py:51
  59.1 7.0 %collective-permute-start.5 = (bf16[4,32,768]{2,1,0:T(8,128)(2,1)S(1)}, bf16[4,32,768]{2,1,0:T(8,128)(2,1)S(1)}, u32[]{:S(2)}, u32[]{:S(2)}) collective-permute-start(bf16[4,32,768]{2,1,0:T(8,128)(2,1)S(1)} %pad_maximum_fusion.6), channel_id=1, source_target_pairs={{0,16},{1,17},{2,18},{3,19},{4,20},{5,21},{6,22},{7,23},{8,24},{9,... | collective-permute-start | bytes 589832 | tf_op jit(solution)/shard_map/ppermute | solution.py:51
  71.7 37.0 %copy-start.16 = (s32[1,8]{1,0:T(1,128)S(1)}, s32[1,8]{1,0:T(1,128)}, u32[]{:S(2)}) copy-start(s32[1,8]{1,0:T(1,128)} %param.19) | copy-start | bytes 100
  71.8 21.5 %copy-start.13 = (bf16[256,768]{1,0:T(8,128)(2,1)}, bf16[256,768]{1,0:T(8,128)(2,1)S(1)}, u32[]{:S(2)}) copy-start(bf16[256,768]{1,0:T(8,128)(2,1)S(1)} %collective-permute-done.9.refs_6_) | copy-start | bytes 1179652
  75.3 22.0 %copy-start.14 = (bf16[256,768]{1,0:T(8,128)(2,1)}, bf16[256,768]{1,0:T(8,128)(2,1)S(1)}, u32[]{:S(2)}) copy-start(bf16[256,768]{1,0:T(8,128)(2,1)S(1)} %collective-permute-done.7.refs_1_) | copy-start | bytes 1179652
  75.3 22.0 %copy-start.15 = (bf16[256,768]{1,0:T(8,128)(2,1)}, bf16[256,768]{1,0:T(8,128)(2,1)S(1)}, u32[]{:S(2)}) copy-start(bf16[256,768]{1,0:T(8,128)(2,1)S(1)} %collective-permute-done.8.refs_2_) | copy-start | bytes 1179652
  75.3 21.9 %collective-permute-start.11 = (bf16[8,48,768]{2,1,0:T(8,128)(2,1)S(1)}, bf16[8,48,768]{2,1,0:T(8,128)(2,1)S(1)}, u32[]{:S(2)}, u32[]{:S(2)}) collective-permute-start(bf16[8,48,768]{2,1,0:T(8,128)(2,1)S(1)} %constant_dynamic-update-slice_fusion.5), channel_id=1, source_target_pairs={{0,16},{1,17},{2,18},{3,19},{4,20},{5,21},{6,22},{7,23},{8,24},{9,... | collective-permute-start | bytes 1769480 | tf_op jit(solution)/shard_map/ppermute | solution.py:51
  76.8 16.4 %collective-permute-start.10 = (bf16[8,32,768]{2,1,0:T(8,128)(2,1)S(1)}, bf16[8,32,768]{2,1,0:T(8,128)(2,1)S(1)}, u32[]{:S(2)}, u32[]{:S(2)}) collective-permute-start(bf16[8,32,768]{2,1,0:T(8,128)(2,1)S(1)} %constant_dynamic-update-slice_fusion), channel_id=1, source_target_pairs={{0,1},{1,0},{2,3},{3,2},{4,5},{5,4},{6,7},{7,6},{8,9},{9,8},{10,11... | collective-permute-start | bytes 1179656 | tf_op jit(solution)/shard_map/ppermute | solution.py:51
  78.3 30.0 %collective-permute-start.12 = (bf16[256,768]{1,0:T(8,128)(2,1)S(1)}, bf16[256,768]{1,0:T(8,128)(2,1)}, u32[]{:S(2)}, u32[]{:S(2)}) collective-permute-start(bf16[256,768]{1,0:T(8,128)(2,1)S(1)} %collective-permute-done.7.refs_1_), channel_id=1, source_target_pairs={{0,1},{1,0},{2,3},{3,2},{4,5},{5,4},{6,7},{7,6},{8,9},{9,8},{10,11... | collective-permute-start | bytes 1179656 | tf_op jit(solution)/shard_map/ppermute | solution.py:51
  93.3 19.1 %copy-start.5 = (bf16[16,32,768]{2,1,0:T(8,128)(2,1)}, bf16[16,32,768]{2,1,0:T(8,128)(2,1)S(1)}, u32[]{:S(2)}) copy-start(bf16[16,32,768]{2,1,0:T(8,128)(2,1)S(1)} %pad_maximum_fusion.3.refs_10_) | copy-start | bytes 2359300
  97.3 15.1 %copy-start.4 = (bf16[16,48,768]{2,1,0:T(8,128)(2,1)}, bf16[16,48,768]{2,1,0:T(8,128)(2,1)S(1)}, u32[]{:S(2)}) copy-start(bf16[16,48,768]{2,1,0:T(8,128)(2,1)S(1)} %pad_maximum_fusion.2.refs_12_) | copy-start | bytes 3538948
  108.2 4.1 %collective-permute-start.14 = (bf16[16,48,768]{2,1,0:T(8,128)(2,1)S(1)}, bf16[16,48,768]{2,1,0:T(8,128)(2,1)S(1)}, u32[]{:S(2)}, u32[]{:S(2)}) collective-permute-start(bf16[16,48,768]{2,1,0:T(8,128)(2,1)S(1)} %pad_maximum_fusion.2.refs_12_), channel_id=1, source_target_pairs={{0,8},{1,9},{2,10},{3,11},{4,12},{5,13},{6,14},{7,15},{8,0},{9,1},... | collective-permute-start | bytes 3538952 | tf_op jit(solution)/shard_map/ppermute | solution.py:51
  108.2 3.7 %collective-permute-start.13 = (bf16[16,32,768]{2,1,0:T(8,128)(2,1)S(1)}, bf16[16,32,768]{2,1,0:T(8,128)(2,1)}, u32[]{:S(2)}, u32[]{:S(2)}) collective-permute-start(bf16[16,32,768]{2,1,0:T(8,128)(2,1)S(1)} %pad_maximum_fusion.3.refs_10_), channel_id=1, source_target_pairs={{0,8},{1,9},{2,10},{3,11},{4,12},{5,13},{6,14},{7,15},{8,0},{9,1},... | collective-permute-start | bytes 2359304 | tf_op jit(solution)/shard_map/ppermute | solution.py:51
  112.4 1.1 copy-start.11
  158.9 121.6 %reduce-scatter.6.cloned.1.call-start = ((), (), s32[]{:S(2)}) async-start(), calls=%async_computation.5 | async-start | bytes 6635520 | tf_op jit(solution)/shard_map/reduce_scatter | solution.py:921
  191.4 0.7 copy-start.10
  191.4 1.6 copy-start
  191.4 144.3 %reduce-scatter.8.cloned.1.call-start = ((), (), s32[]{:S(2)}) async-start(), calls=%async_computation.6 | async-start | bytes 1658880 | tf_op jit(solution)/shard_map/reduce_scatter | solution.py:921
  193.0 20.9 %collective-permute-start.15 = (bf16[256,768]{1,0:T(8,128)(2,1)S(1)}, bf16[256,768]{1,0:T(8,128)(2,1)S(1)}, u32[]{:S(2)}, u32[]{:S(2)}) collective-permute-start(bf16[256,768]{1,0:T(8,128)(2,1)S(1)} %get-tuple-element.152), channel_id=1, source_target_pairs={{0,1},{1,0},{2,3},{3,2},{4,5},{5,4},{6,7},{7,6},{8,9},{9,8},{10,11... | collective-permute-start | bytes 1179656 | tf_op jit(solution)/shard_map/ppermute | solution.py:51
  194.9 27.6 %collective-permute-start.17 = (bf16[256,768]{1,0:T(8,128)(2,1)S(1)}, bf16[256,768]{1,0:T(8,128)(2,1)}, u32[]{:S(2)}, u32[]{:S(2)}) collective-permute-start(bf16[256,768]{1,0:T(8,128)(2,1)S(1)} %get-tuple-element.151), channel_id=1, source_target_pairs={{0,1},{1,0},{2,3},{3,2},{4,5},{5,4},{6,7},{7,6},{8,9},{9,8},{10,11... | collective-permute-start | bytes 1179656 | tf_op jit(solution)/shard_map/ppermute | solution.py:51
  213.2 11.3 %copy-start.3 = (bf16[16,72,768]{2,1,0:T(8,128)(2,1)S(1)}, bf16[16,72,768]{2,1,0:T(8,128)(2,1)}, u32[]{:S(2)}) copy-start(bf16[16,72,768]{2,1,0:T(8,128)(2,1)} %get-tuple-element.125) | copy-start | bytes 5308420
  214.0 0.7 copy-start.9
  224.5 3.0 copy-start.7
  225.9 12.9 %collective-permute-start.16 = (bf16[16,80,768]{2,1,0:T(8,128)(2,1)}, bf16[16,80,768]{2,1,0:T(8,128)(2,1)}, u32[]{:S(2)}, u32[]{:S(2)}) collective-permute-start(bf16[16,80,768]{2,1,0:T(8,128)(2,1)} %pad_maximum_fusion.1), channel_id=1, source_target_pairs={{0,8},{1,9},{2,10},{3,11},{4,12},{5,13},{6,14},{7,15},{8,0},{9,1},... | collective-permute-start | bytes 5898248 | tf_op jit(solution)/shard_map/ppermute | solution.py:51
  226.0 11.8 %collective-permute-start.18 = (bf16[256,768]{1,0:T(8,128)(2,1)}, bf16[256,768]{1,0:T(8,128)(2,1)}, u32[]{:S(2)}, u32[]{:S(2)}) collective-permute-start(bf16[256,768]{1,0:T(8,128)(2,1)} %get-tuple-element.149), channel_id=1, source_target_pairs={{0,2},{1,3},{2,0},{3,1},{4,6},{5,7},{6,4},{7,5},{8,10},{9,11},{10,... | collective-permute-start | bytes 1179656 | tf_op jit(solution)/shard_map/ppermute | solution.py:51
  241.3 37.9 %collective-permute-start.19 = (bf16[8,80,768]{2,1,0:T(8,128)(2,1)}, bf16[8,80,768]{2,1,0:T(8,128)(2,1)}, u32[]{:S(2)}, u32[]{:S(2)}) collective-permute-start(bf16[8,80,768]{2,1,0:T(8,128)(2,1)} %bitcast.33), channel_id=1, source_target_pairs={{0,16},{1,17},{2,18},{3,19},{4,20},{5,21},{6,22},{7,23},{8,24},{9,... | collective-permute-start | bytes 2949128 | tf_op jit(solution)/shard_map/ppermute | solution.py:51
  246.9 67.0 %collective-permute-start.24 = (bf16[256,768]{1,0:T(8,128)(2,1)S(1)}, bf16[256,768]{1,0:T(8,128)(2,1)S(1)}, u32[]{:S(2)}, u32[]{:S(2)}) collective-permute-start(bf16[256,768]{1,0:T(8,128)(2,1)S(1)} %convert_element_type.233), channel_id=1, source_target_pairs={{4,0},{5,1},{6,2},{7,3},{12,8},{13,9},{14,10},{15,11},{20,16},{21,... | collective-permute-start | bytes 1179656 | tf_op jit(solution)/shard_map/ppermute | solution.py:55
  251.5 32.9 %copy-start.1 = (bf16[1,1,640,768]{3,2,1,0:T(8,128)(2,1)S(1)}, bf16[1,1,640,768]{3,2,1,0:T(8,128)(2,1)}, u32[]{:S(2)}) copy-start(bf16[1,1,640,768]{3,2,1,0:T(8,128)(2,1)} %constant_dynamic-slice_fusion.5) | copy-start | bytes 2949124
  251.5 32.9 %copy-start.2 = (bf16[1,1,640,768]{3,2,1,0:T(8,128)(2,1)S(1)}, bf16[1,1,640,768]{3,2,1,0:T(8,128)(2,1)}, u32[]{:S(2)}) copy-start(bf16[1,1,640,768]{3,2,1,0:T(8,128)(2,1)} %constant_dynamic-slice_fusion.4) | copy-start | bytes 2949124
  281.7 12.0 %collective-permute-start.21 = (bf16[256,768]{1,0:T(8,128)(2,1)S(1)}, bf16[256,768]{1,0:T(8,128)(2,1)S(1)}, u32[]{:S(2)}, u32[]{:S(2)}) collective-permute-start(bf16[256,768]{1,0:T(8,128)(2,1)S(1)} %get-tuple-element.153), channel_id=1, source_target_pairs={{0,1},{1,0},{2,3},{3,2},{4,5},{5,4},{6,7},{7,6},{8,9},{9,8},{10,11... | collective-permute-start | bytes 1179656 | tf_op jit(solution)/shard_map/ppermute | solution.py:51
  283.8 9.9 %collective-permute-start.22 = (bf16[256,768]{1,0:T(8,128)(2,1)S(1)}, bf16[256,768]{1,0:T(8,128)(2,1)S(1)}, u32[]{:S(2)}, u32[]{:S(2)}) collective-permute-start(bf16[256,768]{1,0:T(8,128)(2,1)S(1)} %get-tuple-element.154), channel_id=1, source_target_pairs={{5,6},{6,5},{13,14},{14,13},{21,22},{22,21},{29,30},{30,29}} | collective-permute-start | bytes 1179656 | tf_op jit(solution)/shard_map/ppermute | solution.py:55
  285.7 18.0 %collective-permute-start.20 = (bf16[4,80,768]{2,1,0:T(8,128)(2,1)S(1)}, bf16[4,80,768]{2,1,0:T(8,128)(2,1)S(1)}, u32[]{:S(2)}, u32[]{:S(2)}) collective-permute-start(bf16[4,80,768]{2,1,0:T(8,128)(2,1)S(1)} %fusion.2), channel_id=1, source_target_pairs={{0,1},{1,0},{2,3},{3,2},{4,5},{5,4},{6,7},{7,6},{8,9},{9,8},{10,11... | collective-permute-start | bytes 1474568 | tf_op jit(solution)/shard_map/ppermute | solution.py:51
  303.7 24.9 %copy-start.6 = (f32[256,768]{1,0:T(8,128)S(1)}, f32[256,768]{1,0:T(8,128)}, u32[]{:S(2)}) copy-start(f32[256,768]{1,0:T(8,128)} %get-tuple-element.117) | copy-start | bytes 2359300
  303.8 24.6 %collective-permute-start.23 = (bf16[2,80,768]{2,1,0:T(8,128)(2,1)S(1)}, bf16[2,80,768]{2,1,0:T(8,128)(2,1)S(1)}, u32[]{:S(2)}, u32[]{:S(2)}) collective-permute-start(bf16[2,80,768]{2,1,0:T(8,128)(2,1)S(1)} %bitcast.169), channel_id=1, source_target_pairs={{0,4},{1,5},{2,6},{3,7},{4,0},{5,1},{6,2},{7,3},{8,12},{9,13},{10,... | collective-permute-start | bytes 737288 | tf_op jit(solution)/shard_map/ppermute | solution.py:51
  328.5 5.2 %collective-permute-start.25 = (bf16[1,80,768]{2,1,0:T(8,128)(2,1)S(1)}, bf16[1,80,768]{2,1,0:T(8,128)(2,1)S(1)}, u32[]{:S(2)}, u32[]{:S(2)}) collective-permute-start(bf16[1,80,768]{2,1,0:T(8,128)(2,1)S(1)} %add_convert_fusion.4), channel_id=1, source_target_pairs={{0,2},{1,3},{2,0},{3,1},{4,6},{5,7},{6,4},{7,5},{8,10},{9,11},{10,... | collective-permute-start | bytes 368648 | tf_op jit(solution)/shard_map/ppermute | solution.py:51
Sparse Core Ops, SparseCore 0:
  11.5 124.1 all-gather.1
  159.0 32.3 reduce-scatter.3
  194.6 85.8 reduce-scatter.5
  282.8 38.8 reduce-scatter.7

commit v12 on v11

--- a/solution.py
+++ b/solution.py
@@ -867,7 +867,7 @@
             exchange.other, exchange.same_y, exchange.diagonal = seen
             one, two = stage(one, plan.y[0]), stage(two, plan.x[0])
             exchange.stage_three()
-            one, two, exchange.other_y = tie(one, two, exchange.other_y)
+            one, exchange.other_y = tie(one, exchange.other_y)
             pieces = [one, plan.swap(one, plan.core[0]), two, plan.swap(two, plan.core[0])]
             order = lambda *bits: ([(bit, 1 << i) for i, bit in enumerate(bits)], plan.core[0])
             places = (
@@ -969,13 +969,13 @@
                 *held, returned.same = tie(*held, returned.same)
                 returned.prompt_three()
             elif bit == plan.y[0]:
-                *held, grads, shared_n = tie(*held, grads, shared_n)
+                *held, grads, shared_n, returned.back = tie(*held, grads, shared_n, returned.back)
                 grads = level(grads, "z")
+            elif bit == plan.z[-1]:
+                *held, shared_n = tie(*held, shared_n)
                 returned.near(shared_n)
-            elif bit == plan.z[-1]:
+            elif bit == plan.z[0]:
                 *held, returned.own = tie(*held, returned.own)
-            elif bit == plan.z[0]:
-                *held, returned.back = tie(*held, returned.back)
             reduce.terms = list(held)
             reduce.stage(bit)
         o_ab = grads.reshape(-1, width).astype(F32)

time: 347 us -> 344 us (level)
  waiting for transfers between devices: 155 us -> 148 us
  starting transfers between devices: 54.6 us -> 60.7 us
    ppermute x22, waiting for transfers between devices: 124 us -> 105 us  [swap(): return lax.ppermute(value, AXES, [(i, i ^ mask) for i in range(self.count)])]
    ppermute x4, waiting for transfers between devices: 12.6 us -> 25.4 us  [send(): return lax.ppermute(value, AXES, pairs)]
    ppermute x22, starting transfers between devices: 48 us -> 54.1 us  [swap(): return lax.ppermute(value, AXES, [(i, i ^ mask) for i in range(self.count)])]
  transfers between devices with their start and end apart: 30 -> 30, of which waited for: 19 -> 18; matrix products, arithmetic and copies ran while one was open for 9% -> 8% of each run, Pallas kernels for 17% -> 17%
where the time goes in v12:
time: 344 us; the launch traced here: 343 us
  waiting for transfers between devices  148 us (43%)
  Pallas kernels  81.5 us (24%)
  starting transfers between devices  60.7 us (18%)
  other arithmetic  19.3 us (6%)
  local copies, waits for them, and re-layouts  18.8 us (5%)
  between operations  14.3 us (4%)
    ppermute x22, waiting for transfers between devices, swap(): return lax.ppermute(value, AXES, [(i, i ^ mask) for i in range(self.count)])  105 us
    ppermute x22, starting transfers between devices, swap(): return lax.ppermute(value, AXES, [(i, i ^ mask) for i in range(self.count)])  54.1 us
    ppermute x4, waiting for transfers between devices, send(): return lax.ppermute(value, AXES, pairs)  25.4 us
    pallas_call x1, Pallas kernels, middle_call(): pl.pallas_call(functools.partial(middle_kernel, wide, mapped), grid=(2 *...  20.9 us
    pallas_call x1, Pallas kernels, attention_call(): pl.pallas_call(functools.partial(attention_kernel, blocks, first, rows, p...  18.8 us
    pallas_call x2, Pallas kernels, back_call(): pl.pallas_call(functools.partial(back_kernel, rows, bound, dq0 is not Non...  17.9 us
    reduce_scatter x3, waiting for transfers between devices, per_device(): lax.psum_scatter(value, axes, scatter_dimension=0, tiled=True)  12.6 us
    pallas_call x1, Pallas kernels, weight_call(): pl.pallas_call(functools.partial(weight_kernel, blocks, first, rows, runs...  11.4 us
  transfers between devices with their start and end apart: 30, of which 18 were waited for; matrix products, arithmetic and copies ran while one was open for 8% of the time, Pallas kernels for 17%

profile of v12, /device:TPU:0, one launch (start us, length us, event | category | flops | bytes accessed | tf_op | source)
XLA Modules:
  0.0 342.8 jit_solution(4857907629719515880)
XLA Ops:
  9.4 1.8 pack.1
  11.3 3.1 collective-permute-start
  14.4 2.6 collective-permute-start.1
  17.0 3.8 %collective-permute-start.3 = (bf16[256,768]{1,0:T(8,128)(2,1)}, bf16[256,768]{1,0:T(8,128)(2,1)S(1)}, u32[]{:S(2)}, u32[]{:S(2)}) collective-permute-start(bf16[256,768]{1,0:T(8,128)(2,1)} %bitcast.160), channel_id=1, source_target_pairs={{0,4},{1,5},{2,6},{3,7},{8,12},{9,13},{10,14},{11,15},{16,20},{17,... | collective-permute-start | bytes 1179656 | tf_op jit(solution)/shard_map/ppermute | solution.py:55
  20.9 1.6 collective-permute-start.4
  25.8 12.6 %collective-permute-done.3 = bf16[256,768]{1,0:T(8,128)(2,1)S(1)} collective-permute-done((bf16[256,768]{1,0:T(8,128)(2,1)}, bf16[256,768]{1,0:T(8,128)(2,1)S(1)}, u32[]{:S(2)}, u32[]{:S(2)}) %collective-permute-start.3) | collective-permute-done | bytes 393248 | tf_op jit(solution)/shard_map/ppermute | solution.py:55
  40.2 16.6 %collective-permute-start.7 = (bf16[256,768]{1,0:T(8,128)(2,1)S(1)}, bf16[256,768]{1,0:T(8,128)(2,1)S(1)}, u32[]{:S(2)}, u32[]{:S(2)}) collective-permute-start(bf16[256,768]{1,0:T(8,128)(2,1)S(1)} %broadcast_select_fusion.refs_0_), channel_id=1, source_target_pairs={{0,2},{1,3},{2,0},{3,1},{4,6},{5,7},{6,4},{7,5},{8,10},{9,11},{10,... | collective-permute-start | bytes 1179656 | tf_op jit(solution)/shard_map/ppermute | solution.py:51
  57.7 1.4 collective-permute-start.6
  59.8 6.3 %collective-permute-done.5 = bf16[4,32,768]{2,1,0:T(8,128)(2,1)S(1)} collective-permute-done((bf16[4,32,768]{2,1,0:T(8,128)(2,1)S(1)}, bf16[4,32,768]{2,1,0:T(8,128)(2,1)S(1)}, u32[]{:S(2)}, u32[]{:S(2)}) %collective-permute-start.5) | collective-permute-done | bytes 196640 | tf_op jit(solution)/shard_map/ppermute | solution.py:51
  66.2 5.6 %collective-permute-done.6 = bf16[4,48,768]{2,1,0:T(8,128)(2,1)S(1)} collective-permute-done((bf16[4,48,768]{2,1,0:T(8,128)(2,1)S(1)}, bf16[4,48,768]{2,1,0:T(8,128)(2,1)S(1)}, u32[]{:S(2)}, u32[]{:S(2)}) %collective-permute-start.6) | collective-permute-done | bytes 294944 | tf_op jit(solution)/shard_map/ppermute | solution.py:51
  71.8 3.5 %collective-permute-done.7.refs_1_ = bf16[256,768]{1,0:T(8,128)(2,1)S(1)} collective-permute-done((bf16[256,768]{1,0:T(8,128)(2,1)S(1)}, bf16[256,768]{1,0:T(8,128)(2,1)S(1)}, u32[]{:S(2)}, u32[]{:S(2)}) %collective-permute-start.7) | collective-permute-done | bytes 393248 | tf_op jit(solution)/shard_map/ppermute | solution.py:51
  75.3 1.5 collective-permute-start.13
  76.8 1.5 collective-permute-start.10
  79.0 18.3 %collective-permute-done.13 = bf16[8,48,768]{2,1,0:T(8,128)(2,1)S(1)} collective-permute-done((bf16[8,48,768]{2,1,0:T(8,128)(2,1)S(1)}, bf16[8,48,768]{2,1,0:T(8,128)(2,1)S(1)}, u32[]{:S(2)}, u32[]{:S(2)}) %collective-permute-start.13) | collective-permute-done | bytes 589856 | tf_op jit(solution)/shard_map/ppermute | solution.py:51
  97.5 10.8 %collective-permute-done.11.refs_3_ = bf16[256,768]{1,0:T(8,128)(2,1)} collective-permute-done((bf16[256,768]{1,0:T(8,128)(2,1)S(1)}, bf16[256,768]{1,0:T(8,128)(2,1)}, u32[]{:S(2)}, u32[]{:S(2)}) %collective-permute-start.11) | collective-permute-done | bytes 393248 | tf_op jit(solution)/shard_map/ppermute | solution.py:51
  111.4 18.8 %attention.1 = (bf16[32,72,768]{2,1,0:T(8,128)(2,1)}, bf16[256,768]{1,0:T(8,128)(2,1)}, bf16[1024,768]{1,0:T(8,128)(2,1)}, bf16[1024,768]{1,0:T(8,128)(2,1)}, bf...) custom-call(bf16[256,768]{1,0:T(8,128)(2,1)} %copy-done.8, ...), custom_call_target="tpu_custom_call" | custom-call | flops 9865003008 | bytes 12582912 | tf_op jit(solution)/shard_map/attention/pallas_call | solution.py:342
  130.2 5.6 %all-gather.2.cloned.1.call-done = bf16[7168,768]{1,0:T(8,128)(2,1)} async-done(((bf16[224,768]{1,0:T(8,128)(2,1)}), bf16[7168,768]{1,0:T(8,128)(2,1)}) %all-gather.2.cloned.1.call-update) | async-done | bytes 11010064 | tf_op jit(solution)/shard_map/all_gather | solution.py:847
  138.0 20.9 %middle.1 = (bf16[256,768]{1,0:T(8,128)(2,1)}, f32[256,768]{1,0:T(8,128)}, bf16[256,768]{1,0:T(8,128)(2,1)}, bf16[32,216,768]{2,1,0:T(8,128)(2,1)}, f32[8,768]{1,0:T(8,128)}, /*index=5*/f32[8,768]{1,0:T(8,128)}) custom-call(bf16[256,768]{1,0:T(8,128)(2,1)} %get-tuple-element.96.ctx_ref.refs_2_, bf16[256,768]{1,0:T(8,128)(2,1)} %bitcast.165, ...), custom_call_target="tpu_custom_call" | custom-call | flops 8153726976 | bytes 33554432 | tf_op jit(solution)/shard_map/middle/pallas_call | solution.py:567
  158.9 12.5 %attention_back.2 = (bf16[1024,768]{1,0:T(8,128)(2,1)}, bf16[1024,768]{1,0:T(8,128)(2,1)}, f32[768,256]{1,0:T(8,128)}) custom-call(s32[1]{0:T(128)} %bitcast.9.refs_7_.refs_0_.near_ref, bf16[256,768]{1,0:T(8,128)(2,1)} %get-tuple-element.99.refs_1_, bf16[256,768]{1,0:T(8,128)(2,1)} %get-tuple-element.96.ctx_ref.refs_2_, ...), custom_call_target="tpu_custom_call" | custom-call | flops 16106127360 | bytes 6291456 | tf_op jit(solution)/shard_map/attention_back/pallas_call | solution.py:659
  171.4 6.6 %token_product.2 = bf16[4,256,768]{2,1,0:T(8,128)(2,1)} custom-call(s32[1]{0:T(128)} %bitcast.9.refs_7_.refs_0_.near_ref, bf16[1024,768]{1,0:T(8,128)(2,1)} %get-tuple-element.107.dk_ref.refs_13_, bf16[1024,768]{1,0:T(8,128)(2,1)} %get-tuple-element.108.dv_ref.refs_14_, bf16[32,72,768]{2,1,0:T(8,128)(2,1)} %get-tuple-element.109.wk_ref.wv_ref.refs_11_, ...), custom_call_target="tpu_custom_call" | custom-call | flops 2415919104 | bytes 4718592 | tf_op jit(solution)/shard_map/token_product/pallas_call | solution.py:697
  178.0 11.3 %reduce-scatter.4.cloned.1.call-done = bf16[16,216,768]{2,1,0:T(8,128)(2,1)} async-done(((bf16[32,216,768]{2,1,0:T(8,128)(2,1)}), bf16[16,216,768]{2,1,0:T(8,128)(2,1)}) %reduce-scatter.4.cloned.1.call-update) | async-done | bytes 5308432 | tf_op jit(solution)/shard_map/reduce_scatter | solution.py:921
  191.0 1.9 collective-permute-start.15
  193.1 5.4 %attention_back.3 = (bf16[768,768]{1,0:T(8,128)(2,1)}, bf16[768,768]{1,0:T(8,128)(2,1)}, f32[768,256]{1,0:T(8,128)}) custom-call(s32[1]{0:T(128)} %bitcast.9.refs_7_.refs_0_.near_ref, bf16[256,768]{1,0:T(8,128)(2,1)} %get-tuple-element.99.refs_1_, bf16[256,768]{1,0:T(8,128)(2,1)} %get-tuple-element.96.ctx_ref.refs_2_, ...), custom_call_target="tpu_custom_call" | custom-call | flops 12079595520 | bytes 4718592 | tf_op jit(solution)/shard_map/attention_back/pallas_call | solution.py:659
  198.5 11.4 %weight_product.1 = (bf16[16,72,768]{2,1,0:T(8,128)(2,1)}, bf16[16,72,768]{2,1,0:T(8,128)(2,1)}, f32[256,768]{1,0:T(8,128)}, f32[8,768]{1,0:T(8,128)}) custom-call(bf16[256,768]{1,0:T(8,128)(2,1)} %copy-done.8, bf16[256,768]{1,0:T(8,128)(2,1)} %copy-done.16, bf16[256,768]{1,0:T(8,128)(2,1)} %collective-permute-done.8.refs_2_, ...), custom_call_target="tpu_custom_call" | custom-call | flops 4227858432 | bytes 16515072 | tf_op jit(solution)/shard_map/weight_product/pallas_call | solution.py:776
  212.0 8.5 %collective-permute-done.17 = bf16[256,768]{1,0:T(8,128)(2,1)} collective-permute-done((bf16[256,768]{1,0:T(8,128)(2,1)S(1)}, bf16[256,768]{1,0:T(8,128)(2,1)}, u32[]{:S(2)}, u32[]{:S(2)}) %collective-permute-start.17) | collective-permute-done | bytes 393248 | tf_op jit(solution)/shard_map/ppermute | solution.py:51
  220.4 2.0 fusion.1
  222.5 1.5 pad_maximum_fusion.1
  223.9 1.4 collective-permute-start.18
  225.4 1.7 pad_maximum_fusion
  227.1 8.6 %collective-permute-done.18 = bf16[256,768]{1,0:T(8,128)(2,1)} collective-permute-done((bf16[256,768]{1,0:T(8,128)(2,1)}, bf16[256,768]{1,0:T(8,128)(2,1)}, u32[]{:S(2)}, u32[]{:S(2)}) %collective-permute-start.18) | collective-permute-done | bytes 393248 | tf_op jit(solution)/shard_map/ppermute | solution.py:51
  236.9 2.4 add_convert_fusion
  239.3 1.5 collective-permute-start.19
  240.8 1.3 collective-permute-start.20
  242.1 4.1 %token_product.3 = bf16[3,256,768]{2,1,0:T(8,128)(2,1)} custom-call(s32[1]{0:T(128)} %bitcast.9.refs_7_.refs_0_.near_ref, bf16[768,768]{1,0:T(8,128)(2,1)} %get-tuple-element.130.refs_15_.dk_ref, bf16[768,768]{1,0:T(8,128)(2,1)} %get-tuple-element.131.refs_16_.dv_ref, bf16[32,72,768]{2,1,0:T(8,128)(2,1)} %get-tuple-element.109.wk_ref.wv_ref.refs_11_, ...), custom_call_target="tpu_custom_call" | custom-call | flops 1811939328 | bytes 3538944 | tf_op jit(solution)/shard_map/token_product/pallas_call | solution.py:697
  246.3 2.4 constant_dynamic-slice_fusion.4
  249.7 12.8 %collective-permute-done.20 = bf16[256,768]{1,0:T(8,128)(2,1)S(1)} collective-permute-done((bf16[256,768]{1,0:T(8,128)(2,1)S(1)}, bf16[256,768]{1,0:T(8,128)(2,1)S(1)}, u32[]{:S(2)}, u32[]{:S(2)}) %collective-permute-start.20) | collective-permute-done | bytes 393248 | tf_op jit(solution)/shard_map/ppermute | solution.py:55
  262.5 14.7 %collective-permute-done.19 = bf16[8,80,768]{2,1,0:T(8,128)(2,1)} collective-permute-done((bf16[8,80,768]{2,1,0:T(8,128)(2,1)}, bf16[8,80,768]{2,1,0:T(8,128)(2,1)}, u32[]{:S(2)}, u32[]{:S(2)}) %collective-permute-start.19) | collective-permute-done | bytes 983072 | tf_op jit(solution)/shard_map/ppermute | solution.py:51
  277.2 1.3 reduce-scatter.6.cloned.1.call-done
  278.5 2.4 fusion.2
  280.9 2.0 collective-permute-start.21
  283.0 1.2 dynamic-slice_bitcast_fusion
  284.4 10.1 %collective-permute-done.21 = bf16[4,80,768]{2,1,0:T(8,128)(2,1)S(1)} collective-permute-done((bf16[4,80,768]{2,1,0:T(8,128)(2,1)}, bf16[4,80,768]{2,1,0:T(8,128)(2,1)S(1)}, u32[]{:S(2)}, u32[]{:S(2)}) %collective-permute-start.21) | collective-permute-done | bytes 491552 | tf_op jit(solution)/shard_map/ppermute | solution.py:51
  294.6 1.8 collective-permute-start.23
  297.3 2.3 collective-permute-start.22
  299.7 5.6 %collective-permute-done.23 = bf16[256,768]{1,0:T(8,128)(2,1)S(1)} collective-permute-done((bf16[256,768]{1,0:T(8,128)(2,1)S(1)}, bf16[256,768]{1,0:T(8,128)(2,1)S(1)}, u32[]{:S(2)}, u32[]{:S(2)}) %collective-permute-start.23) | collective-permute-done | bytes 393248 | tf_op jit(solution)/shard_map/ppermute | solution.py:51
  305.5 10.1 %collective-permute-done.22 = bf16[2,80,768]{2,1,0:T(8,128)(2,1)S(1)} collective-permute-done((bf16[2,80,768]{2,1,0:T(8,128)(2,1)S(1)}, bf16[2,80,768]{2,1,0:T(8,128)(2,1)S(1)}, u32[]{:S(2)}, u32[]{:S(2)}) %collective-permute-start.22) | collective-permute-done | bytes 245792 | tf_op jit(solution)/shard_map/ppermute | solution.py:51
  315.7 12.5 %collective-permute-start.25 = (bf16[1,80,768]{2,1,0:T(8,128)(2,1)S(1)}, bf16[1,80,768]{2,1,0:T(8,128)(2,1)S(1)}, u32[]{:S(2)}, u32[]{:S(2)}) collective-permute-start(bf16[1,80,768]{2,1,0:T(8,128)(2,1)S(1)} %add_convert_fusion.4), channel_id=1, source_target_pairs={{0,2},{1,3},{2,0},{3,1},{4,6},{5,7},{6,4},{7,5},{8,10},{9,11},{10,... | collective-permute-start | bytes 368648 | tf_op jit(solution)/shard_map/ppermute | solution.py:51
  329.2 2.0 collective-permute-done.25
  (147 shorter events, 28.8 us)
Async XLA Ops:
  7.2 128.6 %all-gather.2.cloned.1.call-start = ((), (), s32[]{:S(2)}) async-start(), calls=%async_computation.3 | async-start | bytes 11354112 | tf_op jit(solution)/shard_map/all_gather | solution.py:847
  11.3 178.0 %reduce-scatter.4.cloned.1.call-start = ((), (), s32[]{:S(2)}) async-start(), calls=%async_computation.4 | async-start | bytes 15925248 | tf_op jit(solution)/shard_map/reduce_scatter | solution.py:921
  11.3 28.8 %collective-permute-start = (bf16[80,768]{1,0:T(8,128)(2,1)}, bf16[80,768]{1,0:T(8,128)(2,1)S(1)}, u32[]{:S(2)}, u32[]{:S(2)}) collective-permute-start(bf16[80,768]{1,0:T(8,128)(2,1)} %get-tuple-element.83), channel_id=1, source_target_pairs={{0,2},{1,3},{2,0},{3,1},{4,6},{5,7},{6,4},{7,5},{8,10},{9,11},{10,... | collective-permute-start | bytes 368648 | tf_op jit(solution)/shard_map/ppermute | solution.py:51
  14.4 25.8 %collective-permute-start.1 = (bf16[80,768]{1,0:T(8,128)(2,1)}, bf16[80,768]{1,0:T(8,128)(2,1)S(1)}, u32[]{:S(2)}, u32[]{:S(2)}) collective-permute-start(bf16[80,768]{1,0:T(8,128)(2,1)} %get-tuple-element.83), channel_id=1, source_target_pairs={{0,4},{1,5},{2,6},{3,7},{4,0},{5,1},{6,2},{7,3},{8,12},{9,13},{10,... | collective-permute-start | bytes 368648 | tf_op jit(solution)/shard_map/ppermute | solution.py:51
  17.0 23.2 %collective-permute-start.2 = (bf16[80,768]{1,0:T(8,128)(2,1)}, bf16[80,768]{1,0:T(8,128)(2,1)S(1)}, u32[]{:S(2)}, u32[]{:S(2)}) collective-permute-start(bf16[80,768]{1,0:T(8,128)(2,1)} %get-tuple-element.83), channel_id=1, source_target_pairs={{0,6},{1,7},{2,4},{3,5},{4,2},{5,3},{6,0},{7,1},{8,14},{9,15},{10,... | collective-permute-start | bytes 368648 | tf_op jit(solution)/shard_map/ppermute | solution.py:51
  17.0 21.4 %collective-permute-start.3 = (bf16[256,768]{1,0:T(8,128)(2,1)}, bf16[256,768]{1,0:T(8,128)(2,1)S(1)}, u32[]{:S(2)}, u32[]{:S(2)}) collective-permute-start(bf16[256,768]{1,0:T(8,128)(2,1)} %bitcast.160), channel_id=1, source_target_pairs={{0,4},{1,5},{2,6},{3,7},{8,12},{9,13},{10,14},{11,15},{16,20},{17,... | collective-permute-start | bytes 1179656 | tf_op jit(solution)/shard_map/ppermute | solution.py:55
  20.9 19.4 %collective-permute-start.4 = (bf16[256,768]{1,0:T(8,128)(2,1)}, bf16[256,768]{1,0:T(8,128)(2,1)S(1)}, u32[]{:S(2)}, u32[]{:S(2)}) collective-permute-start(bf16[256,768]{1,0:T(8,128)(2,1)} %bitcast.161), channel_id=1, source_target_pairs={{0,1},{1,0},{2,3},{3,2},{4,5},{5,4},{6,7},{7,6},{8,9},{9,8},{10,11... | collective-permute-start | bytes 1179656 | tf_op jit(solution)/shard_map/ppermute | solution.py:51
  38.4 33.3 %collective-permute-start.9 = (bf16[256,768]{1,0:T(8,128)(2,1)}, bf16[256,768]{1,0:T(8,128)(2,1)S(1)}, u32[]{:S(2)}, u32[]{:S(2)}) collective-permute-start(bf16[256,768]{1,0:T(8,128)(2,1)} %bitcast.162), channel_id=1, source_target_pairs={{5,6},{6,5},{13,14},{14,13},{21,22},{22,21},{29,30},{30,29}} | collective-permute-start | bytes 1179656 | tf_op jit(solution)/shard_map/ppermute | solution.py:55
  40.2 38.1 %copy-start.8 = (bf16[256,768]{1,0:T(8,128)(2,1)}, bf16[256,768]{1,0:T(8,128)(2,1)S(1)}, u32[]{:S(2)}) copy-start(bf16[256,768]{1,0:T(8,128)(2,1)S(1)} %broadcast_select_fusion.refs_0_) | copy-start | bytes 1179652
  40.2 38.1 %copy-start.14 = (bf16[256,768]{1,0:T(8,128)(2,1)}, bf16[256,768]{1,0:T(8,128)(2,1)S(1)}, u32[]{:S(2)}) copy-start(bf16[256,768]{1,0:T(8,128)(2,1)S(1)} %collective-permute-done.4.refs_5_) | copy-start | bytes 1179652
  40.2 35.0 %collective-permute-start.7 = (bf16[256,768]{1,0:T(8,128)(2,1)S(1)}, bf16[256,768]{1,0:T(8,128)(2,1)S(1)}, u32[]{:S(2)}, u32[]{:S(2)}) collective-permute-start(bf16[256,768]{1,0:T(8,128)(2,1)S(1)} %broadcast_select_fusion.refs_0_), channel_id=1, source_target_pairs={{0,2},{1,3},{2,0},{3,1},{4,6},{5,7},{6,4},{7,5},{8,10},{9,11},{10,... | collective-permute-start | bytes 1179656 | tf_op jit(solution)/shard_map/ppermute | solution.py:51
  56.9 18.4 %collective-permute-start.8 = (bf16[256,768]{1,0:T(8,128)(2,1)S(1)}, bf16[256,768]{1,0:T(8,128)(2,1)}, u32[]{:S(2)}, u32[]{:S(2)}) collective-permute-start(bf16[256,768]{1,0:T(8,128)(2,1)S(1)} %broadcast_select_fusion.refs_0_), channel_id=1, source_target_pairs={{0,1},{1,0},{2,3},{3,2},{4,5},{5,4},{6,7},{7,6},{8,9},{9,8},{10,11... | collective-permute-start | bytes 1179656 | tf_op jit(solution)/shard_map/ppermute | solution.py:51
  57.7 14.0 %collective-permute-start.6 = (bf16[4,48,768]{2,1,0:T(8,128)(2,1)S(1)}, bf16[4,48,768]{2,1,0:T(8,128)(2,1)S(1)}, u32[]{:S(2)}, u32[]{:S(2)}) collective-permute-start(bf16[4,48,768]{2,1,0:T(8,128)(2,1)S(1)} %pad_maximum_fusion.3), channel_id=1, source_target_pairs={{0,1},{1,0},{2,3},{3,2},{4,5},{5,4},{6,7},{7,6},{8,9},{9,8},{10,11... | collective-permute-start | bytes 884744 | tf_op jit(solution)/shard_map/ppermute | solution.py:51
  59.1 7.0 %collective-permute-start.5 = (bf16[4,32,768]{2,1,0:T(8,128)(2,1)S(1)}, bf16[4,32,768]{2,1,0:T(8,128)(2,1)S(1)}, u32[]{:S(2)}, u32[]{:S(2)}) collective-permute-start(bf16[4,32,768]{2,1,0:T(8,128)(2,1)S(1)} %pad_maximum_fusion.5), channel_id=1, source_target_pairs={{0,16},{1,17},{2,18},{3,19},{4,20},{5,21},{6,22},{7,23},{8,24},{9,... | collective-permute-start | bytes 589832 | tf_op jit(solution)/shard_map/ppermute | solution.py:51
  71.7 36.5 %copy-start.17 = (s32[1,8]{1,0:T(1,128)S(1)}, s32[1,8]{1,0:T(1,128)}, u32[]{:S(2)}) copy-start(s32[1,8]{1,0:T(1,128)} %param.19) | copy-start | bytes 100
  71.8 3.5 %copy-start.15 = (bf16[256,768]{1,0:T(8,128)(2,1)}, bf16[256,768]{1,0:T(8,128)(2,1)S(1)}, u32[]{:S(2)}) copy-start(bf16[256,768]{1,0:T(8,128)(2,1)S(1)} %collective-permute-done.9.refs_6_) | copy-start | bytes 1179652
  75.3 22.2 %copy-start.16 = (bf16[256,768]{1,0:T(8,128)(2,1)}, bf16[256,768]{1,0:T(8,128)(2,1)S(1)}, u32[]{:S(2)}) copy-start(bf16[256,768]{1,0:T(8,128)(2,1)S(1)} %collective-permute-done.7.refs_1_) | copy-start | bytes 1179652
  75.3 21.9 %collective-permute-start.13 = (bf16[8,48,768]{2,1,0:T(8,128)(2,1)S(1)}, bf16[8,48,768]{2,1,0:T(8,128)(2,1)S(1)}, u32[]{:S(2)}, u32[]{:S(2)}) collective-permute-start(bf16[8,48,768]{2,1,0:T(8,128)(2,1)S(1)} %constant_dynamic-update-slice_fusion.5), channel_id=1, source_target_pairs={{0,16},{1,17},{2,18},{3,19},{4,20},{5,21},{6,22},{7,23},{8,24},{9,... | collective-permute-start | bytes 1769480 | tf_op jit(solution)/shard_map/ppermute | solution.py:51
  76.8 20.5 %collective-permute-start.10 = (bf16[8,32,768]{2,1,0:T(8,128)(2,1)S(1)}, bf16[8,32,768]{2,1,0:T(8,128)(2,1)S(1)}, u32[]{:S(2)}, u32[]{:S(2)}) collective-permute-start(bf16[8,32,768]{2,1,0:T(8,128)(2,1)S(1)} %constant_dynamic-update-slice_fusion), channel_id=1, source_target_pairs={{0,1},{1,0},{2,3},{3,2},{4,5},{5,4},{6,7},{7,6},{8,9},{9,8},{10,11... | collective-permute-start | bytes 1179656 | tf_op jit(solution)/shard_map/ppermute | solution.py:51
  78.3 29.9 %collective-permute-start.11 = (bf16[256,768]{1,0:T(8,128)(2,1)S(1)}, bf16[256,768]{1,0:T(8,128)(2,1)}, u32[]{:S(2)}, u32[]{:S(2)}) collective-permute-start(bf16[256,768]{1,0:T(8,128)(2,1)S(1)} %collective-permute-done.7.refs_1_), channel_id=1, source_target_pairs={{0,1},{1,0},{2,3},{3,2},{4,5},{5,4},{6,7},{7,6},{8,9},{9,8},{10,11... | collective-permute-start | bytes 1179656 | tf_op jit(solution)/shard_map/ppermute | solution.py:51
  97.3 13.3 %copy-start.11 = (bf16[16,48,768]{2,1,0:T(8,128)(2,1)}, bf16[16,48,768]{2,1,0:T(8,128)(2,1)S(1)}, u32[]{:S(2)}) copy-start(bf16[16,48,768]{2,1,0:T(8,128)(2,1)S(1)} %constant_dynamic-update-slice_fusion.10.refs_12_) | copy-start | bytes 3538948
  97.3 13.3 %collective-permute-start.14 = (bf16[16,48,768]{2,1,0:T(8,128)(2,1)S(1)}, bf16[16,48,768]{2,1,0:T(8,128)(2,1)}, u32[]{:S(2)}, u32[]{:S(2)}) collective-permute-start(bf16[16,48,768]{2,1,0:T(8,128)(2,1)S(1)} %constant_dynamic-update-slice_fusion.10.refs_12_), channel_id=1, source_target_pairs={{0,8},{1,9},{2,10},{3,11},{4,12},{5,13},{6,14},{7,15},{8,0},{9,1},... | collective-permute-start | bytes 3538952 | tf_op jit(solution)/shard_map/ppermute | solution.py:51
  97.4 13.1 %copy-start.5 = (bf16[16,32,768]{2,1,0:T(8,128)(2,1)}, bf16[16,32,768]{2,1,0:T(8,128)(2,1)S(1)}, u32[]{:S(2)}) copy-start(bf16[16,32,768]{2,1,0:T(8,128)(2,1)S(1)} %pad_maximum_fusion.2.refs_10_) | copy-start | bytes 2359300
  108.2 2.3 collective-permute-start.12
  110.5 0.9 copy-start.13
  158.9 119.7 %reduce-scatter.6.cloned.1.call-start = ((), (), s32[]{:S(2)}) async-start(), calls=%async_computation.5 | async-start | bytes 6635520 | tf_op jit(solution)/shard_map/reduce_scatter | solution.py:921
  189.3 0.7 copy-start.12
  189.3 1.6 copy-start
  189.4 143.8 %reduce-scatter.8.cloned.1.call-start = ((), (), s32[]{:S(2)}) async-start(), calls=%async_computation.6 | async-start | bytes 1658880 | tf_op jit(solution)/shard_map/reduce_scatter | solution.py:921
  191.0 20.9 %collective-permute-start.15 = (bf16[256,768]{1,0:T(8,128)(2,1)S(1)}, bf16[256,768]{1,0:T(8,128)(2,1)}, u32[]{:S(2)}, u32[]{:S(2)}) collective-permute-start(bf16[256,768]{1,0:T(8,128)(2,1)S(1)} %get-tuple-element.152), channel_id=1, source_target_pairs={{0,1},{1,0},{2,3},{3,2},{4,5},{5,4},{6,7},{7,6},{8,9},{9,8},{10,11... | collective-permute-start | bytes 1179656 | tf_op jit(solution)/shard_map/ppermute | solution.py:51
  192.9 27.6 %collective-permute-start.17 = (bf16[256,768]{1,0:T(8,128)(2,1)S(1)}, bf16[256,768]{1,0:T(8,128)(2,1)}, u32[]{:S(2)}, u32[]{:S(2)}) collective-permute-start(bf16[256,768]{1,0:T(8,128)(2,1)S(1)} %get-tuple-element.151), channel_id=1, source_target_pairs={{0,1},{1,0},{2,3},{3,2},{4,5},{5,4},{6,7},{7,6},{8,9},{9,8},{10,11... | collective-permute-start | bytes 1179656 | tf_op jit(solution)/shard_map/ppermute | solution.py:51
  211.1 11.3 %copy-start.4 = (bf16[16,72,768]{2,1,0:T(8,128)(2,1)S(1)}, bf16[16,72,768]{2,1,0:T(8,128)(2,1)}, u32[]{:S(2)}) copy-start(bf16[16,72,768]{2,1,0:T(8,128)(2,1)} %get-tuple-element.124) | copy-start | bytes 5308420
  222.5 2.9 copy-start.7
  223.9 12.9 %collective-permute-start.16 = (bf16[16,80,768]{2,1,0:T(8,128)(2,1)}, bf16[16,80,768]{2,1,0:T(8,128)(2,1)}, u32[]{:S(2)}, u32[]{:S(2)}) collective-permute-start(bf16[16,80,768]{2,1,0:T(8,128)(2,1)} %pad_maximum_fusion.1), channel_id=1, source_target_pairs={{0,8},{1,9},{2,10},{3,11},{4,12},{5,13},{6,14},{7,15},{8,0},{9,1},... | collective-permute-start | bytes 5898248 | tf_op jit(solution)/shard_map/ppermute | solution.py:51
  223.9 11.8 %collective-permute-start.18 = (bf16[256,768]{1,0:T(8,128)(2,1)}, bf16[256,768]{1,0:T(8,128)(2,1)}, u32[]{:S(2)}, u32[]{:S(2)}) collective-permute-start(bf16[256,768]{1,0:T(8,128)(2,1)} %get-tuple-element.149), channel_id=1, source_target_pairs={{0,2},{1,3},{2,0},{3,1},{4,6},{5,7},{6,4},{7,5},{8,10},{9,11},{10,... | collective-permute-start | bytes 1179656 | tf_op jit(solution)/shard_map/ppermute | solution.py:51
  239.3 37.9 %collective-permute-start.19 = (bf16[8,80,768]{2,1,0:T(8,128)(2,1)}, bf16[8,80,768]{2,1,0:T(8,128)(2,1)}, u32[]{:S(2)}, u32[]{:S(2)}) collective-permute-start(bf16[8,80,768]{2,1,0:T(8,128)(2,1)} %bitcast.33), channel_id=1, source_target_pairs={{0,16},{1,17},{2,18},{3,19},{4,20},{5,21},{6,22},{7,23},{8,24},{9,... | collective-permute-start | bytes 2949128 | tf_op jit(solution)/shard_map/ppermute | solution.py:51
  240.8 21.7 %collective-permute-start.20 = (bf16[256,768]{1,0:T(8,128)(2,1)S(1)}, bf16[256,768]{1,0:T(8,128)(2,1)S(1)}, u32[]{:S(2)}, u32[]{:S(2)}) collective-permute-start(bf16[256,768]{1,0:T(8,128)(2,1)S(1)} %convert_element_type.220), channel_id=1, source_target_pairs={{4,0},{5,1},{6,2},{7,3},{12,8},{13,9},{14,10},{15,11},{20,16},{21,... | collective-permute-start | bytes 1179656 | tf_op jit(solution)/shard_map/ppermute | solution.py:55
  262.5 16.0 %copy-start.9 = (bf16[256,768]{1,0:T(8,128)(2,1)}, bf16[256,768]{1,0:T(8,128)(2,1)S(1)}, u32[]{:S(2)}) copy-start(bf16[256,768]{1,0:T(8,128)(2,1)S(1)} %collective-permute-done.20) | copy-start | bytes 1179652
  278.5 5.7 %copy-start.2 = (bf16[1,1,640,768]{3,2,1,0:T(8,128)(2,1)S(1)}, bf16[1,1,640,768]{3,2,1,0:T(8,128)(2,1)}, u32[]{:S(2)}) copy-start(bf16[1,1,640,768]{3,2,1,0:T(8,128)(2,1)} %constant_dynamic-slice_fusion.4) | copy-start | bytes 2949124
  280.9 13.7 %collective-permute-start.21 = (bf16[4,80,768]{2,1,0:T(8,128)(2,1)}, bf16[4,80,768]{2,1,0:T(8,128)(2,1)S(1)}, u32[]{:S(2)}, u32[]{:S(2)}) collective-permute-start(bf16[4,80,768]{2,1,0:T(8,128)(2,1)} %fusion.2), channel_id=1, source_target_pairs={{0,1},{1,0},{2,3},{3,2},{4,5},{5,4},{6,7},{7,6},{8,9},{9,8},{10,11... | collective-permute-start | bytes 1474568 | tf_op jit(solution)/shard_map/ppermute | solution.py:51
  282.9 11.6 %copy-start.1 = (bf16[3,256,768]{2,1,0:T(8,128)(2,1)S(1)}, bf16[3,256,768]{2,1,0:T(8,128)(2,1)}, u32[]{:S(2)}) copy-start(bf16[3,256,768]{2,1,0:T(8,128)(2,1)} %token_product.3) | copy-start | bytes 3538948
  282.9 1.4 copy-start.3
  294.6 10.7 %collective-permute-start.23 = (bf16[256,768]{1,0:T(8,128)(2,1)S(1)}, bf16[256,768]{1,0:T(8,128)(2,1)S(1)}, u32[]{:S(2)}, u32[]{:S(2)}) collective-permute-start(bf16[256,768]{1,0:T(8,128)(2,1)S(1)} %get-tuple-element.153), channel_id=1, source_target_pairs={{0,1},{1,0},{2,3},{3,2},{4,5},{5,4},{6,7},{7,6},{8,9},{9,8},{10,11... | collective-permute-start | bytes 1179656 | tf_op jit(solution)/shard_map/ppermute | solution.py:51
  296.4 8.9 %collective-permute-start.24 = (bf16[256,768]{1,0:T(8,128)(2,1)S(1)}, bf16[256,768]{1,0:T(8,128)(2,1)S(1)}, u32[]{:S(2)}, u32[]{:S(2)}) collective-permute-start(bf16[256,768]{1,0:T(8,128)(2,1)S(1)} %get-tuple-element.154), channel_id=1, source_target_pairs={{5,6},{6,5},{13,14},{14,13},{21,22},{22,21},{29,30},{30,29}} | collective-permute-start | bytes 1179656 | tf_op jit(solution)/shard_map/ppermute | solution.py:55
  297.3 18.4 %collective-permute-start.22 = (bf16[2,80,768]{2,1,0:T(8,128)(2,1)S(1)}, bf16[2,80,768]{2,1,0:T(8,128)(2,1)S(1)}, u32[]{:S(2)}, u32[]{:S(2)}) collective-permute-start(bf16[2,80,768]{2,1,0:T(8,128)(2,1)S(1)} %bitcast.169), channel_id=1, source_target_pairs={{0,4},{1,5},{2,6},{3,7},{4,0},{5,1},{6,2},{7,3},{8,12},{9,13},{10,... | collective-permute-start | bytes 737288 | tf_op jit(solution)/shard_map/ppermute | solution.py:51
  299.6 28.6 %copy-start.6 = (f32[256,768]{1,0:T(8,128)S(1)}, f32[256,768]{1,0:T(8,128)}, u32[]{:S(2)}) copy-start(f32[256,768]{1,0:T(8,128)} %get-tuple-element.116) | copy-start | bytes 2359300
  299.7 28.6 %copy-start.10 = (bf16[256,768]{1,0:T(8,128)(2,1)S(1)}, bf16[256,768]{1,0:T(8,128)(2,1)}, u32[]{:S(2)}) copy-start(bf16[256,768]{1,0:T(8,128)(2,1)} %copy-done.9) | copy-start | bytes 1179652
  315.7 15.5 %collective-permute-start.25 = (bf16[1,80,768]{2,1,0:T(8,128)(2,1)S(1)}, bf16[1,80,768]{2,1,0:T(8,128)(2,1)S(1)}, u32[]{:S(2)}, u32[]{:S(2)}) collective-permute-start(bf16[1,80,768]{2,1,0:T(8,128)(2,1)S(1)} %add_convert_fusion.4), channel_id=1, source_target_pairs={{0,2},{1,3},{2,0},{3,1},{4,6},{5,7},{6,4},{7,5},{8,10},{9,11},{10,... | collective-permute-start | bytes 368648 | tf_op jit(solution)/shard_map/ppermute | solution.py:51
Sparse Core Ops, SparseCore 0:
  11.5 124.1 all-gather.1
  159.0 30.3 reduce-scatter.3
  192.6 85.8 reduce-scatter.5
  283.1 41.6 reduce-scatter.7

commit v13 on v12

--- a/solution.py
+++ b/solution.py
@@ -114,7 +114,7 @@
 
     def stage_three(self):
         if self.ready:
-            self.other_y = self.plan.swap(self.other, 1)
+            self.other_y = self.plan.swap(self.same_y, 2)
 
     def spots(self):
         row, rows, own = lax.axis_index(ROW), self.rows, self.own
@@ -156,15 +156,15 @@
         self.plan, self.rows = plan, rows
 
     def prompt_one(self, parts):
-        self.prompt = self.same = self.own = self.back = parts
+        self.prompt = self.same = self.same_y = self.own = self.back = parts
         if self.plan.row == 8:
-            same, other, same_y, other_y = [parts[i].astype(F32) for i in range(4)]
-            self.other = (other + self.plan.swap(parts[3], 1).astype(F32)).astype(BF)
-            self.same = same + self.plan.swap(parts[2], 1).astype(F32)
+            same, same_y = parts[0].astype(F32), parts[2].astype(F32)
+            self.same_y = (same_y + self.plan.swap(parts[3], 2).astype(F32)).astype(BF)
+            self.same = same + self.plan.swap(parts[1], 2).astype(F32)
 
     def prompt_two(self):
         if self.plan.row == 8:
-            self.same = self.same + self.plan.swap(self.other, 2).astype(F32)
+            self.same = self.same + self.plan.swap(self.same_y, 1).astype(F32)
 
     def prompt_three(self):
         if self.plan.row == 8:
@@ -939,7 +939,9 @@
         send, keep, grad_own, sums_qkv = weight_call(
             spots, first_near, near, own, dq, squares, grad_h1, dkp, dvp, dkn, dvn, core, runs
         )
-        send, keep, returned.same, dkn, dvn = tie(send, keep, returned.same, dkn, dvn)
+        send, keep, returned.same, returned.same_y, dkn, dvn = tie(
+            send, keep, returned.same, returned.same_y, dkn, dvn
+        )
         returned.prompt_two()
         shared_n = product_call(None, near, dkn, dvn, squares, rows)
 

time: 344 us -> 340 us (0.988)
  waiting for transfers between devices: 148 us -> 139 us
  starting transfers between devices: 60.7 us -> 65.1 us
    ppermute x22, waiting for transfers between devices: 105 us -> 95.3 us  [swap(): return lax.ppermute(value, AXES, [(i, i ^ mask) for i in range(self.count)])]
    reduce_scatter x3, waiting for transfers between devices: 12.6 us -> 7.75 us  [per_device(): lax.psum_scatter(value, axes, scatter_dimension=0, tiled=True)]
    ppermute x22, starting transfers between devices: 54.1 us -> 58.5 us  [swap(): return lax.ppermute(value, AXES, [(i, i ^ mask) for i in range(self.count)])]
  transfers between devices with their start and end apart: 30 -> 30, of which waited for: 18 -> 16; matrix products, arithmetic and copies ran while one was open for 8% -> 8% of each run, Pallas kernels for 17% -> 18%
where the time goes in v13:
time: 340 us; the launch traced here: 339 us
  waiting for transfers between devices  139 us (41%)
  Pallas kernels  82.1 us (24%)
  starting transfers between devices  65.1 us (19%)
  local copies, waits for them, and re-layouts  19.4 us (6%)
  other arithmetic  19.2 us (6%)
  between operations  14.3 us (4%)
    ppermute x22, waiting for transfers between devices, swap(): return lax.ppermute(value, AXES, [(i, i ^ mask) for i in range(self.count)])  95.3 us
    ppermute x22, starting transfers between devices, swap(): return lax.ppermute(value, AXES, [(i, i ^ mask) for i in range(self.count)])  58.5 us
    ppermute x4, waiting for transfers between devices, send(): return lax.ppermute(value, AXES, pairs)  28.2 us
    pallas_call x1, Pallas kernels, middle_call(): pl.pallas_call(functools.partial(middle_kernel, wide, mapped), grid=(2 *...  20.9 us
    pallas_call x1, Pallas kernels, attention_call(): pl.pallas_call(functools.partial(attention_kernel, blocks, first, rows, p...  18.8 us
    pallas_call x2, Pallas kernels, back_call(): pl.pallas_call(functools.partial(back_kernel, rows, bound, dq0 is not Non...  18 us
    pallas_call x1, Pallas kernels, weight_call(): pl.pallas_call(functools.partial(weight_kernel, blocks, first, rows, runs...  11.4 us
    pallas_call x2, Pallas kernels, product_call(): pl.pallas_call(functools.partial(product_kernel, rows, bound), grid=(tall...  11.2 us
  transfers between devices with their start and end apart: 30, of which 16 were waited for; matrix products, arithmetic and copies ran while one was open for 8% of the time, Pallas kernels for 18%

profile of v13, /device:TPU:0, one launch (start us, length us, event | category | flops | bytes accessed | tf_op | source)
XLA Modules:
  0.0 338.9 jit_solution(8542057463288447689)
XLA Ops:
  9.4 1.8 pack.1
  11.3 3.1 collective-permute-start
  14.4 2.6 collective-permute-start.1
  17.0 3.8 %collective-permute-start.3 = (bf16[256,768]{1,0:T(8,128)(2,1)}, bf16[256,768]{1,0:T(8,128)(2,1)S(1)}, u32[]{:S(2)}, u32[]{:S(2)}) collective-permute-start(bf16[256,768]{1,0:T(8,128)(2,1)} %bitcast.160), channel_id=1, source_target_pairs={{0,4},{1,5},{2,6},{3,7},{8,12},{9,13},{10,14},{11,15},{16,20},{17,... | collective-permute-start | bytes 1179656 | tf_op jit(solution)/shard_map/ppermute | solution.py:55
  20.9 1.6 collective-permute-start.4
  25.8 12.6 %collective-permute-done.3 = bf16[256,768]{1,0:T(8,128)(2,1)S(1)} collective-permute-done((bf16[256,768]{1,0:T(8,128)(2,1)}, bf16[256,768]{1,0:T(8,128)(2,1)S(1)}, u32[]{:S(2)}, u32[]{:S(2)}) %collective-permute-start.3) | collective-permute-done | bytes 393248 | tf_op jit(solution)/shard_map/ppermute | solution.py:55
  39.1 1.1 broadcast_select_fusion.refs_0_
  40.2 16.6 %collective-permute-start.7 = (bf16[256,768]{1,0:T(8,128)(2,1)S(1)}, bf16[256,768]{1,0:T(8,128)(2,1)S(1)}, u32[]{:S(2)}, u32[]{:S(2)}) collective-permute-start(bf16[256,768]{1,0:T(8,128)(2,1)S(1)} %broadcast_select_fusion.refs_0_), channel_id=1, source_target_pairs={{0,2},{1,3},{2,0},{3,1},{4,6},{5,7},{6,4},{7,5},{8,10},{9,11},{10,... | collective-permute-start | bytes 1179656 | tf_op jit(solution)/shard_map/ppermute | solution.py:51
  57.7 1.4 collective-permute-start.6
  59.8 6.3 %collective-permute-done.5 = bf16[4,32,768]{2,1,0:T(8,128)(2,1)S(1)} collective-permute-done((bf16[4,32,768]{2,1,0:T(8,128)(2,1)S(1)}, bf16[4,32,768]{2,1,0:T(8,128)(2,1)S(1)}, u32[]{:S(2)}, u32[]{:S(2)}) %collective-permute-start.5) | collective-permute-done | bytes 196640 | tf_op jit(solution)/shard_map/ppermute | solution.py:51
  66.2 5.6 %collective-permute-done.6 = bf16[4,48,768]{2,1,0:T(8,128)(2,1)S(1)} collective-permute-done((bf16[4,48,768]{2,1,0:T(8,128)(2,1)S(1)}, bf16[4,48,768]{2,1,0:T(8,128)(2,1)S(1)}, u32[]{:S(2)}, u32[]{:S(2)}) %collective-permute-start.6) | collective-permute-done | bytes 294944 | tf_op jit(solution)/shard_map/ppermute | solution.py:51
  71.8 3.5 %collective-permute-done.7.refs_1_ = bf16[256,768]{1,0:T(8,128)(2,1)S(1)} collective-permute-done((bf16[256,768]{1,0:T(8,128)(2,1)S(1)}, bf16[256,768]{1,0:T(8,128)(2,1)S(1)}, u32[]{:S(2)}, u32[]{:S(2)}) %collective-permute-start.7) | collective-permute-done | bytes 393248 | tf_op jit(solution)/shard_map/ppermute | solution.py:51
  76.0 1.5 collective-permute-start.13
  77.5 1.5 collective-permute-start.10
  79.1 19.5 %collective-permute-done.13 = bf16[8,48,768]{2,1,0:T(8,128)(2,1)S(1)} collective-permute-done((bf16[8,48,768]{2,1,0:T(8,128)(2,1)S(1)}, bf16[8,48,768]{2,1,0:T(8,128)(2,1)S(1)}, u32[]{:S(2)}, u32[]{:S(2)}) %collective-permute-start.13) | collective-permute-done | bytes 589856 | tf_op jit(solution)/shard_map/ppermute | solution.py:51
  98.8 4.2 %collective-permute-done.11.refs_3_ = bf16[256,768]{1,0:T(8,128)(2,1)} collective-permute-done((bf16[256,768]{1,0:T(8,128)(2,1)S(1)}, bf16[256,768]{1,0:T(8,128)(2,1)}, u32[]{:S(2)}, u32[]{:S(2)}) %collective-permute-start.11) | collective-permute-done | bytes 393248 | tf_op jit(solution)/shard_map/ppermute | solution.py:51
  106.2 18.8 %attention.1 = (bf16[32,72,768]{2,1,0:T(8,128)(2,1)}, bf16[256,768]{1,0:T(8,128)(2,1)}, bf16[1024,768]{1,0:T(8,128)(2,1)}, bf16[1024,768]{1,0:T(8,128)(2,1)}, bf...) custom-call(bf16[256,768]{1,0:T(8,128)(2,1)} %copy-done.8, ...), custom_call_target="tpu_custom_call" | custom-call | flops 9865003008 | bytes 12582912 | tf_op jit(solution)/shard_map/attention/pallas_call | solution.py:342
  125.0 7.5 %all-gather.2.cloned.1.call-done = bf16[7168,768]{1,0:T(8,128)(2,1)} async-done(((bf16[224,768]{1,0:T(8,128)(2,1)}), bf16[7168,768]{1,0:T(8,128)(2,1)}) %all-gather.2.cloned.1.call-update) | async-done | bytes 11010064 | tf_op jit(solution)/shard_map/all_gather | solution.py:847
  134.8 20.9 %middle.1 = (bf16[256,768]{1,0:T(8,128)(2,1)}, f32[256,768]{1,0:T(8,128)}, bf16[256,768]{1,0:T(8,128)(2,1)}, bf16[32,216,768]{2,1,0:T(8,128)(2,1)}, f32[8,768]{1,0:T(8,128)}, /*index=5*/f32[8,768]{1,0:T(8,128)}) custom-call(bf16[256,768]{1,0:T(8,128)(2,1)} %get-tuple-element.97.ctx_ref.refs_2_, bf16[256,768]{1,0:T(8,128)(2,1)} %bitcast.165, ...), custom_call_target="tpu_custom_call" | custom-call | flops 8153726976 | bytes 33554432 | tf_op jit(solution)/shard_map/middle/pallas_call | solution.py:567
  155.7 12.5 %attention_back.2 = (bf16[1024,768]{1,0:T(8,128)(2,1)}, bf16[1024,768]{1,0:T(8,128)(2,1)}, f32[768,256]{1,0:T(8,128)}) custom-call(s32[1]{0:T(128)} %bitcast.9.refs_7_.refs_0_.near_ref, bf16[256,768]{1,0:T(8,128)(2,1)} %get-tuple-element.100.refs_1_, bf16[256,768]{1,0:T(8,128)(2,1)} %get-tuple-element.97.ctx_ref.refs_2_, ...), custom_call_target="tpu_custom_call" | custom-call | flops 16106127360 | bytes 6291456 | tf_op jit(solution)/shard_map/attention_back/pallas_call | solution.py:659
  168.2 7.1 %token_product.2 = bf16[4,256,768]{2,1,0:T(8,128)(2,1)} custom-call(s32[1]{0:T(128)} %bitcast.9.refs_7_.refs_0_.near_ref, bf16[1024,768]{1,0:T(8,128)(2,1)} %get-tuple-element.108.dk_ref.refs_13_, bf16[1024,768]{1,0:T(8,128)(2,1)} %get-tuple-element.109.dv_ref.refs_14_, bf16[32,72,768]{2,1,0:T(8,128)(2,1)} %get-tuple-element.110.wk_ref.wv_ref.refs_11_, ...), custom_call_target="tpu_custom_call" | custom-call | flops 2415919104 | bytes 4718592 | tf_op jit(solution)/shard_map/token_product/pallas_call | solution.py:697
  175.3 7.7 %reduce-scatter.4.cloned.1.call-done = bf16[16,216,768]{2,1,0:T(8,128)(2,1)} async-done(((bf16[32,216,768]{2,1,0:T(8,128)(2,1)}), bf16[16,216,768]{2,1,0:T(8,128)(2,1)}) %reduce-scatter.4.cloned.1.call-update) | async-done | bytes 5308432 | tf_op jit(solution)/shard_map/reduce_scatter | solution.py:921
  184.8 1.8 collective-permute-start.15
  186.8 5.5 %attention_back.3 = (bf16[768,768]{1,0:T(8,128)(2,1)}, bf16[768,768]{1,0:T(8,128)(2,1)}, f32[768,256]{1,0:T(8,128)}) custom-call(s32[1]{0:T(128)} %bitcast.9.refs_7_.refs_0_.near_ref, bf16[256,768]{1,0:T(8,128)(2,1)} %get-tuple-element.100.refs_1_, bf16[256,768]{1,0:T(8,128)(2,1)} %get-tuple-element.97.ctx_ref.refs_2_, ...), custom_call_target="tpu_custom_call" | custom-call | flops 12079595520 | bytes 4718592 | tf_op jit(solution)/shard_map/attention_back/pallas_call | solution.py:659
  192.3 11.4 %weight_product.1 = (bf16[16,72,768]{2,1,0:T(8,128)(2,1)}, bf16[16,72,768]{2,1,0:T(8,128)(2,1)}, f32[256,768]{1,0:T(8,128)}, f32[8,768]{1,0:T(8,128)}) custom-call(bf16[256,768]{1,0:T(8,128)(2,1)} %copy-done.8, bf16[256,768]{1,0:T(8,128)(2,1)} %copy-done.16, bf16[256,768]{1,0:T(8,128)(2,1)} %copy-done.17, bf16[256,768]{1,0:T(8,128)(2,1)} %collective-permute-done.11.refs_3_, ...), custom_call_target="tpu_custom_call" | custom-call | flops 4227858432 | bytes 16515072 | tf_op jit(solution)/shard_map/weight_product/pallas_call | solution.py:776
  205.7 2.0 fusion.1
  207.8 1.5 pad_maximum_fusion.1
  209.2 1.6 collective-permute-start.18
  210.9 1.7 pad_maximum_fusion
  212.5 17.2 %collective-permute-done.18 = bf16[256,768]{1,0:T(8,128)(2,1)} collective-permute-done((bf16[256,768]{1,0:T(8,128)(2,1)}, bf16[256,768]{1,0:T(8,128)(2,1)}, u32[]{:S(2)}, u32[]{:S(2)}) %collective-permute-start.18) | collective-permute-done | bytes 393248 | tf_op jit(solution)/shard_map/ppermute | solution.py:51
  229.8 1.1 convert_add_fusion.3
  230.9 2.4 add_convert_fusion
  233.3 1.6 collective-permute-start.19
  234.9 1.3 collective-permute-start.20
  236.2 4.1 %token_product.3 = bf16[3,256,768]{2,1,0:T(8,128)(2,1)} custom-call(s32[1]{0:T(128)} %bitcast.9.refs_7_.refs_0_.near_ref, bf16[768,768]{1,0:T(8,128)(2,1)} %get-tuple-element.132.refs_15_.dk_ref, bf16[768,768]{1,0:T(8,128)(2,1)} %get-tuple-element.133.refs_16_.dv_ref, bf16[32,72,768]{2,1,0:T(8,128)(2,1)} %get-tuple-element.110.wk_ref.wv_ref.refs_11_, ...), custom_call_target="tpu_custom_call" | custom-call | flops 1811939328 | bytes 3538944 | tf_op jit(solution)/shard_map/token_product/pallas_call | solution.py:697
  240.3 2.2 constant_dynamic-slice_fusion.4
  243.6 15.6 %collective-permute-done.20 = bf16[256,768]{1,0:T(8,128)(2,1)S(1)} collective-permute-done((bf16[256,768]{1,0:T(8,128)(2,1)S(1)}, bf16[256,768]{1,0:T(8,128)(2,1)S(1)}, u32[]{:S(2)}, u32[]{:S(2)}) %collective-permute-start.20) | collective-permute-done | bytes 393248 | tf_op jit(solution)/shard_map/ppermute | solution.py:55
  259.1 12.0 %collective-permute-done.19 = bf16[8,80,768]{2,1,0:T(8,128)(2,1)} collective-permute-done((bf16[8,80,768]{2,1,0:T(8,128)(2,1)}, bf16[8,80,768]{2,1,0:T(8,128)(2,1)}, u32[]{:S(2)}, u32[]{:S(2)}) %collective-permute-start.19) | collective-permute-done | bytes 983072 | tf_op jit(solution)/shard_map/ppermute | solution.py:51
  271.1 2.4 fusion.2
  273.5 1.6 collective-permute-start.21
  275.2 1.2 dynamic-slice_bitcast_fusion
  276.6 9.4 %collective-permute-done.21 = bf16[4,80,768]{2,1,0:T(8,128)(2,1)S(1)} collective-permute-done((bf16[4,80,768]{2,1,0:T(8,128)(2,1)}, bf16[4,80,768]{2,1,0:T(8,128)(2,1)S(1)}, u32[]{:S(2)}, u32[]{:S(2)}) %collective-permute-start.21) | collective-permute-done | bytes 491552 | tf_op jit(solution)/shard_map/ppermute | solution.py:51
  286.1 1.5 collective-permute-start.23
  288.5 5.1 %collective-permute-start.22 = (bf16[2,80,768]{2,1,0:T(8,128)(2,1)S(1)}, bf16[2,80,768]{2,1,0:T(8,128)(2,1)S(1)}, u32[]{:S(2)}, u32[]{:S(2)}) collective-permute-start(bf16[2,80,768]{2,1,0:T(8,128)(2,1)S(1)} %bitcast.169), channel_id=1, source_target_pairs={{0,4},{1,5},{2,6},{3,7},{4,0},{5,1},{6,2},{7,3},{8,12},{9,13},{10,... | collective-permute-start | bytes 737288 | tf_op jit(solution)/shard_map/ppermute | solution.py:51
  293.7 1.8 collective-permute-done.23
  295.6 13.5 %collective-permute-done.22 = bf16[2,80,768]{2,1,0:T(8,128)(2,1)S(1)} collective-permute-done((bf16[2,80,768]{2,1,0:T(8,128)(2,1)S(1)}, bf16[2,80,768]{2,1,0:T(8,128)(2,1)S(1)}, u32[]{:S(2)}, u32[]{:S(2)}) %collective-permute-start.22) | collective-permute-done | bytes 245792 | tf_op jit(solution)/shard_map/ppermute | solution.py:51
  309.2 15.2 %collective-permute-start.25 = (bf16[1,80,768]{2,1,0:T(8,128)(2,1)S(1)}, bf16[1,80,768]{2,1,0:T(8,128)(2,1)S(1)}, u32[]{:S(2)}, u32[]{:S(2)}) collective-permute-start(bf16[1,80,768]{2,1,0:T(8,128)(2,1)S(1)} %add_convert_fusion.4), channel_id=1, source_target_pairs={{0,2},{1,3},{2,0},{3,1},{4,6},{5,7},{6,4},{7,5},{8,10},{9,11},{10,... | collective-permute-start | bytes 368648 | tf_op jit(solution)/shard_map/ppermute | solution.py:51
  325.3 1.9 collective-permute-done.25
  (149 shorter events, 26.9 us)
Async XLA Ops:
  7.2 125.4 %all-gather.2.cloned.1.call-start = ((), (), s32[]{:S(2)}) async-start(), calls=%async_computation.3 | async-start | bytes 11354112 | tf_op jit(solution)/shard_map/all_gather | solution.py:847
  11.3 171.8 %reduce-scatter.4.cloned.1.call-start = ((), (), s32[]{:S(2)}) async-start(), calls=%async_computation.4 | async-start | bytes 15925248 | tf_op jit(solution)/shard_map/reduce_scatter | solution.py:921
  11.3 28.8 %collective-permute-start = (bf16[80,768]{1,0:T(8,128)(2,1)}, bf16[80,768]{1,0:T(8,128)(2,1)S(1)}, u32[]{:S(2)}, u32[]{:S(2)}) collective-permute-start(bf16[80,768]{1,0:T(8,128)(2,1)} %get-tuple-element.84), channel_id=1, source_target_pairs={{0,2},{1,3},{2,0},{3,1},{4,6},{5,7},{6,4},{7,5},{8,10},{9,11},{10,... | collective-permute-start | bytes 368648 | tf_op jit(solution)/shard_map/ppermute | solution.py:51
  14.4 25.8 %collective-permute-start.1 = (bf16[80,768]{1,0:T(8,128)(2,1)}, bf16[80,768]{1,0:T(8,128)(2,1)S(1)}, u32[]{:S(2)}, u32[]{:S(2)}) collective-permute-start(bf16[80,768]{1,0:T(8,128)(2,1)} %get-tuple-element.84), channel_id=1, source_target_pairs={{0,4},{1,5},{2,6},{3,7},{4,0},{5,1},{6,2},{7,3},{8,12},{9,13},{10,... | collective-permute-start | bytes 368648 | tf_op jit(solution)/shard_map/ppermute | solution.py:51
  17.0 23.2 %collective-permute-start.2 = (bf16[80,768]{1,0:T(8,128)(2,1)}, bf16[80,768]{1,0:T(8,128)(2,1)S(1)}, u32[]{:S(2)}, u32[]{:S(2)}) collective-permute-start(bf16[80,768]{1,0:T(8,128)(2,1)} %get-tuple-element.84), channel_id=1, source_target_pairs={{0,6},{1,7},{2,4},{3,5},{4,2},{5,3},{6,0},{7,1},{8,14},{9,15},{10,... | collective-permute-start | bytes 368648 | tf_op jit(solution)/shard_map/ppermute | solution.py:51
  17.0 21.4 %collective-permute-start.3 = (bf16[256,768]{1,0:T(8,128)(2,1)}, bf16[256,768]{1,0:T(8,128)(2,1)S(1)}, u32[]{:S(2)}, u32[]{:S(2)}) collective-permute-start(bf16[256,768]{1,0:T(8,128)(2,1)} %bitcast.160), channel_id=1, source_target_pairs={{0,4},{1,5},{2,6},{3,7},{8,12},{9,13},{10,14},{11,15},{16,20},{17,... | collective-permute-start | bytes 1179656 | tf_op jit(solution)/shard_map/ppermute | solution.py:55
  20.9 19.4 %collective-permute-start.4 = (bf16[256,768]{1,0:T(8,128)(2,1)}, bf16[256,768]{1,0:T(8,128)(2,1)S(1)}, u32[]{:S(2)}, u32[]{:S(2)}) collective-permute-start(bf16[256,768]{1,0:T(8,128)(2,1)} %bitcast.161), channel_id=1, source_target_pairs={{0,1},{1,0},{2,3},{3,2},{4,5},{5,4},{6,7},{7,6},{8,9},{9,8},{10,11... | collective-permute-start | bytes 1179656 | tf_op jit(solution)/shard_map/ppermute | solution.py:51
  38.4 33.3 %collective-permute-start.9 = (bf16[256,768]{1,0:T(8,128)(2,1)}, bf16[256,768]{1,0:T(8,128)(2,1)S(1)}, u32[]{:S(2)}, u32[]{:S(2)}) collective-permute-start(bf16[256,768]{1,0:T(8,128)(2,1)} %bitcast.162), channel_id=1, source_target_pairs={{5,6},{6,5},{13,14},{14,13},{21,22},{22,21},{29,30},{30,29}} | collective-permute-start | bytes 1179656 | tf_op jit(solution)/shard_map/ppermute | solution.py:55
  40.2 38.8 %copy-start.8 = (bf16[256,768]{1,0:T(8,128)(2,1)}, bf16[256,768]{1,0:T(8,128)(2,1)S(1)}, u32[]{:S(2)}) copy-start(bf16[256,768]{1,0:T(8,128)(2,1)S(1)} %broadcast_select_fusion.refs_0_) | copy-start | bytes 1179652
  40.2 38.8 %copy-start.14 = (bf16[256,768]{1,0:T(8,128)(2,1)}, bf16[256,768]{1,0:T(8,128)(2,1)S(1)}, u32[]{:S(2)}) copy-start(bf16[256,768]{1,0:T(8,128)(2,1)S(1)} %collective-permute-done.4.refs_5_) | copy-start | bytes 1179652
  40.2 35.0 %collective-permute-start.7 = (bf16[256,768]{1,0:T(8,128)(2,1)S(1)}, bf16[256,768]{1,0:T(8,128)(2,1)S(1)}, u32[]{:S(2)}, u32[]{:S(2)}) collective-permute-start(bf16[256,768]{1,0:T(8,128)(2,1)S(1)} %broadcast_select_fusion.refs_0_), channel_id=1, source_target_pairs={{0,2},{1,3},{2,0},{3,1},{4,6},{5,7},{6,4},{7,5},{8,10},{9,11},{10,... | collective-permute-start | bytes 1179656 | tf_op jit(solution)/shard_map/ppermute | solution.py:51
  56.9 19.1 %collective-permute-start.8 = (bf16[256,768]{1,0:T(8,128)(2,1)S(1)}, bf16[256,768]{1,0:T(8,128)(2,1)S(1)}, u32[]{:S(2)}, u32[]{:S(2)}) collective-permute-start(bf16[256,768]{1,0:T(8,128)(2,1)S(1)} %broadcast_select_fusion.refs_0_), channel_id=1, source_target_pairs={{0,1},{1,0},{2,3},{3,2},{4,5},{5,4},{6,7},{7,6},{8,9},{9,8},{10,11... | collective-permute-start | bytes 1179656 | tf_op jit(solution)/shard_map/ppermute | solution.py:51
  57.7 14.0 %collective-permute-start.6 = (bf16[4,48,768]{2,1,0:T(8,128)(2,1)S(1)}, bf16[4,48,768]{2,1,0:T(8,128)(2,1)S(1)}, u32[]{:S(2)}, u32[]{:S(2)}) collective-permute-start(bf16[4,48,768]{2,1,0:T(8,128)(2,1)S(1)} %pad_maximum_fusion.3), channel_id=1, source_target_pairs={{0,1},{1,0},{2,3},{3,2},{4,5},{5,4},{6,7},{7,6},{8,9},{9,8},{10,11... | collective-permute-start | bytes 884744 | tf_op jit(solution)/shard_map/ppermute | solution.py:51
  59.1 7.0 %collective-permute-start.5 = (bf16[4,32,768]{2,1,0:T(8,128)(2,1)S(1)}, bf16[4,32,768]{2,1,0:T(8,128)(2,1)S(1)}, u32[]{:S(2)}, u32[]{:S(2)}) collective-permute-start(bf16[4,32,768]{2,1,0:T(8,128)(2,1)S(1)} %pad_maximum_fusion.5), channel_id=1, source_target_pairs={{0,16},{1,17},{2,18},{3,19},{4,20},{5,21},{6,22},{7,23},{8,24},{9,... | collective-permute-start | bytes 589832 | tf_op jit(solution)/shard_map/ppermute | solution.py:51
  71.7 31.3 %copy-start.18 = (s32[1,8]{1,0:T(1,128)S(1)}, s32[1,8]{1,0:T(1,128)}, u32[]{:S(2)}) copy-start(s32[1,8]{1,0:T(1,128)} %param.19) | copy-start | bytes 100
  71.8 3.5 %copy-start.15 = (bf16[256,768]{1,0:T(8,128)(2,1)}, bf16[256,768]{1,0:T(8,128)(2,1)S(1)}, u32[]{:S(2)}) copy-start(bf16[256,768]{1,0:T(8,128)(2,1)S(1)} %collective-permute-done.9.refs_6_) | copy-start | bytes 1179652
  75.3 0.7 copy-start.16
  76.0 22.8 %copy-start.17 = (bf16[256,768]{1,0:T(8,128)(2,1)}, bf16[256,768]{1,0:T(8,128)(2,1)S(1)}, u32[]{:S(2)}) copy-start(bf16[256,768]{1,0:T(8,128)(2,1)S(1)} %collective-permute-done.8.refs_2_) | copy-start | bytes 1179652
  76.0 22.5 %collective-permute-start.13 = (bf16[8,48,768]{2,1,0:T(8,128)(2,1)S(1)}, bf16[8,48,768]{2,1,0:T(8,128)(2,1)S(1)}, u32[]{:S(2)}, u32[]{:S(2)}) collective-permute-start(bf16[8,48,768]{2,1,0:T(8,128)(2,1)S(1)} %constant_dynamic-update-slice_fusion.5), channel_id=1, source_target_pairs={{0,16},{1,17},{2,18},{3,19},{4,20},{5,21},{6,22},{7,23},{8,24},{9,... | collective-permute-start | bytes 1769480 | tf_op jit(solution)/shard_map/ppermute | solution.py:51
  77.5 21.2 %collective-permute-start.10 = (bf16[8,32,768]{2,1,0:T(8,128)(2,1)S(1)}, bf16[8,32,768]{2,1,0:T(8,128)(2,1)S(1)}, u32[]{:S(2)}, u32[]{:S(2)}) collective-permute-start(bf16[8,32,768]{2,1,0:T(8,128)(2,1)S(1)} %constant_dynamic-update-slice_fusion), channel_id=1, source_target_pairs={{0,1},{1,0},{2,3},{3,2},{4,5},{5,4},{6,7},{7,6},{8,9},{9,8},{10,11... | collective-permute-start | bytes 1179656 | tf_op jit(solution)/shard_map/ppermute | solution.py:51
  79.0 24.0 %collective-permute-start.11 = (bf16[256,768]{1,0:T(8,128)(2,1)S(1)}, bf16[256,768]{1,0:T(8,128)(2,1)}, u32[]{:S(2)}, u32[]{:S(2)}) collective-permute-start(bf16[256,768]{1,0:T(8,128)(2,1)S(1)} %collective-permute-done.8.refs_2_), channel_id=1, source_target_pairs={{0,2},{1,3},{2,0},{3,1},{4,6},{5,7},{6,4},{7,5},{8,10},{9,11},{10,... | collective-permute-start | bytes 1179656 | tf_op jit(solution)/shard_map/ppermute | solution.py:51
  98.6 6.7 %copy-start.11 = (bf16[16,48,768]{2,1,0:T(8,128)(2,1)}, bf16[16,48,768]{2,1,0:T(8,128)(2,1)S(1)}, u32[]{:S(2)}) copy-start(bf16[16,48,768]{2,1,0:T(8,128)(2,1)S(1)} %constant_dynamic-update-slice_fusion.10.refs_12_) | copy-start | bytes 3538948
  98.6 6.7 %collective-permute-start.14 = (bf16[16,48,768]{2,1,0:T(8,128)(2,1)S(1)}, bf16[16,48,768]{2,1,0:T(8,128)(2,1)}, u32[]{:S(2)}, u32[]{:S(2)}) collective-permute-start(bf16[16,48,768]{2,1,0:T(8,128)(2,1)S(1)} %constant_dynamic-update-slice_fusion.10.refs_12_), channel_id=1, source_target_pairs={{0,8},{1,9},{2,10},{3,11},{4,12},{5,13},{6,14},{7,15},{8,0},{9,1},... | collective-permute-start | bytes 3538952 | tf_op jit(solution)/shard_map/ppermute | solution.py:51
  98.8 6.5 %copy-start.5 = (bf16[16,32,768]{2,1,0:T(8,128)(2,1)}, bf16[16,32,768]{2,1,0:T(8,128)(2,1)S(1)}, u32[]{:S(2)}) copy-start(bf16[16,32,768]{2,1,0:T(8,128)(2,1)S(1)} %pad_maximum_fusion.2.refs_10_) | copy-start | bytes 2359300
  103.0 2.3 collective-permute-start.12
  105.3 0.9 copy-start.13
  155.7 115.4 %reduce-scatter.6.cloned.1.call-start = ((), (), s32[]{:S(2)}) async-start(), calls=%async_computation.5 | async-start | bytes 6635520 | tf_op jit(solution)/shard_map/reduce_scatter | solution.py:921
  183.1 1.6 copy-start
  183.1 146.1 %reduce-scatter.8.cloned.1.call-start = ((), (), s32[]{:S(2)}) async-start(), calls=%async_computation.6 | async-start | bytes 1658880 | tf_op jit(solution)/shard_map/reduce_scatter | solution.py:921
  184.8 21.0 %collective-permute-start.15 = (bf16[256,768]{1,0:T(8,128)(2,1)S(1)}, bf16[256,768]{1,0:T(8,128)(2,1)}, u32[]{:S(2)}, u32[]{:S(2)}) collective-permute-start(bf16[256,768]{1,0:T(8,128)(2,1)S(1)} %get-tuple-element.154), channel_id=1, source_target_pairs={{0,2},{1,3},{2,0},{3,1},{4,6},{5,7},{6,4},{7,5},{8,10},{9,11},{10,... | collective-permute-start | bytes 1179656 | tf_op jit(solution)/shard_map/ppermute | solution.py:51
  186.6 19.2 %collective-permute-start.16 = (bf16[256,768]{1,0:T(8,128)(2,1)S(1)}, bf16[256,768]{1,0:T(8,128)(2,1)}, u32[]{:S(2)}, u32[]{:S(2)}) collective-permute-start(bf16[256,768]{1,0:T(8,128)(2,1)S(1)} %get-tuple-element.153), channel_id=1, source_target_pairs={{0,2},{1,3},{2,0},{3,1},{4,6},{5,7},{6,4},{7,5},{8,10},{9,11},{10,... | collective-permute-start | bytes 1179656 | tf_op jit(solution)/shard_map/ppermute | solution.py:51
  204.9 2.8 copy-start.4
  207.8 3.1 copy-start.7
  209.2 21.6 %collective-permute-start.17 = (bf16[16,80,768]{2,1,0:T(8,128)(2,1)}, bf16[16,80,768]{2,1,0:T(8,128)(2,1)}, u32[]{:S(2)}, u32[]{:S(2)}) collective-permute-start(bf16[16,80,768]{2,1,0:T(8,128)(2,1)} %pad_maximum_fusion.1), channel_id=1, source_target_pairs={{0,8},{1,9},{2,10},{3,11},{4,12},{5,13},{6,14},{7,15},{8,0},{9,1},... | collective-permute-start | bytes 5898248 | tf_op jit(solution)/shard_map/ppermute | solution.py:51
  209.2 20.5 %collective-permute-start.18 = (bf16[256,768]{1,0:T(8,128)(2,1)}, bf16[256,768]{1,0:T(8,128)(2,1)}, u32[]{:S(2)}, u32[]{:S(2)}) collective-permute-start(bf16[256,768]{1,0:T(8,128)(2,1)} %get-tuple-element.127), channel_id=1, source_target_pairs={{0,1},{1,0},{2,3},{3,2},{4,5},{5,4},{6,7},{7,6},{8,9},{9,8},{10,11... | collective-permute-start | bytes 1179656 | tf_op jit(solution)/shard_map/ppermute | solution.py:51
  233.3 37.8 %collective-permute-start.19 = (bf16[8,80,768]{2,1,0:T(8,128)(2,1)}, bf16[8,80,768]{2,1,0:T(8,128)(2,1)}, u32[]{:S(2)}, u32[]{:S(2)}) collective-permute-start(bf16[8,80,768]{2,1,0:T(8,128)(2,1)} %bitcast.33), channel_id=1, source_target_pairs={{0,16},{1,17},{2,18},{3,19},{4,20},{5,21},{6,22},{7,23},{8,24},{9,... | collective-permute-start | bytes 2949128 | tf_op jit(solution)/shard_map/ppermute | solution.py:51
  234.9 24.2 %collective-permute-start.20 = (bf16[256,768]{1,0:T(8,128)(2,1)S(1)}, bf16[256,768]{1,0:T(8,128)(2,1)S(1)}, u32[]{:S(2)}, u32[]{:S(2)}) collective-permute-start(bf16[256,768]{1,0:T(8,128)(2,1)S(1)} %convert_element_type.220), channel_id=1, source_target_pairs={{4,0},{5,1},{6,2},{7,3},{12,8},{13,9},{14,10},{15,11},{20,16},{21,... | collective-permute-start | bytes 1179656 | tf_op jit(solution)/shard_map/ppermute | solution.py:55
  259.1 12.0 %copy-start.9 = (bf16[256,768]{1,0:T(8,128)(2,1)}, bf16[256,768]{1,0:T(8,128)(2,1)S(1)}, u32[]{:S(2)}) copy-start(bf16[256,768]{1,0:T(8,128)(2,1)S(1)} %collective-permute-done.20) | copy-start | bytes 1179652
  271.1 5.3 %copy-start.2 = (bf16[1,1,640,768]{3,2,1,0:T(8,128)(2,1)S(1)}, bf16[1,1,640,768]{3,2,1,0:T(8,128)(2,1)}, u32[]{:S(2)}) copy-start(bf16[1,1,640,768]{3,2,1,0:T(8,128)(2,1)} %constant_dynamic-slice_fusion.4) | copy-start | bytes 2949124
  273.5 12.5 %collective-permute-start.21 = (bf16[4,80,768]{2,1,0:T(8,128)(2,1)}, bf16[4,80,768]{2,1,0:T(8,128)(2,1)S(1)}, u32[]{:S(2)}, u32[]{:S(2)}) collective-permute-start(bf16[4,80,768]{2,1,0:T(8,128)(2,1)} %fusion.2), channel_id=1, source_target_pairs={{0,1},{1,0},{2,3},{3,2},{4,5},{5,4},{6,7},{7,6},{8,9},{9,8},{10,11... | collective-permute-start | bytes 1474568 | tf_op jit(solution)/shard_map/ppermute | solution.py:51
  275.1 10.9 %copy-start.1 = (bf16[3,256,768]{2,1,0:T(8,128)(2,1)S(1)}, bf16[3,256,768]{2,1,0:T(8,128)(2,1)}, u32[]{:S(2)}) copy-start(bf16[3,256,768]{2,1,0:T(8,128)(2,1)} %token_product.3) | copy-start | bytes 3538948
  275.1 1.4 copy-start.3
  286.1 9.4 %collective-permute-start.23 = (bf16[256,768]{1,0:T(8,128)(2,1)S(1)}, bf16[256,768]{1,0:T(8,128)(2,1)S(1)}, u32[]{:S(2)}, u32[]{:S(2)}) collective-permute-start(bf16[256,768]{1,0:T(8,128)(2,1)S(1)} %get-tuple-element.155), channel_id=1, source_target_pairs={{0,1},{1,0},{2,3},{3,2},{4,5},{5,4},{6,7},{7,6},{8,9},{9,8},{10,11... | collective-permute-start | bytes 1179656 | tf_op jit(solution)/shard_map/ppermute | solution.py:51
  287.6 7.8 %collective-permute-start.24 = (bf16[256,768]{1,0:T(8,128)(2,1)S(1)}, bf16[256,768]{1,0:T(8,128)(2,1)S(1)}, u32[]{:S(2)}, u32[]{:S(2)}) collective-permute-start(bf16[256,768]{1,0:T(8,128)(2,1)S(1)} %get-tuple-element.156), channel_id=1, source_target_pairs={{5,6},{6,5},{13,14},{14,13},{21,22},{22,21},{29,30},{30,29}} | collective-permute-start | bytes 1179656 | tf_op jit(solution)/shard_map/ppermute | solution.py:55
  288.5 20.6 %collective-permute-start.22 = (bf16[2,80,768]{2,1,0:T(8,128)(2,1)S(1)}, bf16[2,80,768]{2,1,0:T(8,128)(2,1)S(1)}, u32[]{:S(2)}, u32[]{:S(2)}) collective-permute-start(bf16[2,80,768]{2,1,0:T(8,128)(2,1)S(1)} %bitcast.169), channel_id=1, source_target_pairs={{0,4},{1,5},{2,6},{3,7},{4,0},{5,1},{6,2},{7,3},{8,12},{9,13},{10,... | collective-permute-start | bytes 737288 | tf_op jit(solution)/shard_map/ppermute | solution.py:51
  293.6 30.8 %copy-start.6 = (f32[256,768]{1,0:T(8,128)S(1)}, f32[256,768]{1,0:T(8,128)}, u32[]{:S(2)}) copy-start(f32[256,768]{1,0:T(8,128)} %get-tuple-element.117) | copy-start | bytes 2359300
  293.6 30.8 %copy-start.10 = (bf16[256,768]{1,0:T(8,128)(2,1)S(1)}, bf16[256,768]{1,0:T(8,128)(2,1)}, u32[]{:S(2)}) copy-start(bf16[256,768]{1,0:T(8,128)(2,1)} %copy-done.9) | copy-start | bytes 1179652
  309.2 18.0 %collective-permute-start.25 = (bf16[1,80,768]{2,1,0:T(8,128)(2,1)S(1)}, bf16[1,80,768]{2,1,0:T(8,128)(2,1)S(1)}, u32[]{:S(2)}, u32[]{:S(2)}) collective-permute-start(bf16[1,80,768]{2,1,0:T(8,128)(2,1)S(1)} %add_convert_fusion.4), channel_id=1, source_target_pairs={{0,2},{1,3},{2,0},{3,1},{4,6},{5,7},{6,4},{7,5},{8,10},{9,11},{10,... | collective-permute-start | bytes 368648 | tf_op jit(solution)/shard_map/ppermute | solution.py:51
  (1 other events, 0.7 us)
Sparse Core Ops, SparseCore 0:
  11.5 121.0 all-gather.1
  155.8 27.2 reduce-scatter.3
  186.4 83.8 reduce-scatter.5
  275.3 47.1 reduce-scatter.7

commit v14 on v13

--- a/solution.py
+++ b/solution.py
@@ -240,8 +240,8 @@
         def _(e):
             away = e ^ me_ref[0]
             for (bits, half), (zero, one), parts in (
-                (places[0], (a0_ref, a1_ref), ((0, each, w_ref, 0), (each, 8, line_ref, 0))),
-                (places[1], (b0_ref, b1_ref), ((0, 2 * each, w_ref, each),)),
+                (places[0], (a0_ref, a1_ref), ((0, each, w_ref, 0), (each, 8, line_ref, 0), (each + 8, 8, w_ref, each))),
+                (places[1], (b0_ref, b1_ref), ((0, 2 * each - 8, w_ref, each + 8),)),
             ):
                 j = sum([((away // bit) & 1) * weight for bit, weight in bits])
                 for which, source in enumerate((zero, one)):
@@ -251,7 +251,7 @@
                         for k, (top, size, target, base) in enumerate(parts):
                             act(pltpu.make_async_copy(
                                 source.at[j, pl.ds(top, size)], target.at[e, pl.ds(base, size)],
-                                w_sems.at[2 * k if zero is a0_ref else 1, e],
+                                w_sems.at[k if zero is a0_ref else 3, e],
                             ))
 
     @pl.when(pl.program_id(0) == 0)
@@ -375,7 +375,7 @@
             pltpu.VMEM((owners, 8, width), BF),
             pltpu.VMEM((8, width), F32),
             pltpu.SemaphoreType.DMA((blocks,)),
-            pltpu.SemaphoreType.DMA((3, owners)),
+            pltpu.SemaphoreType.DMA((4, owners)),
             pltpu.SemaphoreType.DMA,
         ],
         compiler_params=pltpu.CompilerParams(vmem_limit_bytes=60 * 2**20),
@@ -859,7 +859,7 @@
             away = swaps(first_pack, plan.z)
             *away, same, beside = tie(*away, *exchange.stage_one())
             exchange.same, exchange.beside = same, beside
-            cut = step + 8
+            cut = step + 16
             one = jnp.stack([v[:cut] for v in (first_pack, *away)])
             two = jnp.stack([v[cut:] for v in (first_pack, *away)])
             one, two = stage(one, plan.x[0]), stage(two, plan.y[0])
@@ -890,8 +890,8 @@
             got = jnp.concatenate([v.reshape(32, -1, width) for v in (outer, output, inner)], 1)
             pairs = marks[:, 0, : 2 * step].reshape(32, count // 32, 2, step).transpose(0, 2, 1, 3)
             pairs = jnp.pad(pairs.reshape(32, 1, -1), ((0, 0), (0, 7), (0, width - 2 * width // 32)))
-            one = jnp.concatenate([rest[:, 0], pairs], 1)
-            two = rest[:, 1:].reshape(32, -1, width)
+            one = jnp.concatenate([rest[:, 0], pairs, rest[:, 1, :8]], 1)
+            two = jnp.concatenate([rest[:, 1, 8:], rest[:, 2]], 1)
             pieces = [one[:16], one[16:], two[:16], two[16:]]
             places = (([(1, 1), (2, 2), (4, 4), (8, 8)], 16),) * 2
             me = jnp.zeros((1,), jnp.int32)
@@ -968,7 +968,7 @@
         for bit in plan.x + plan.y + plan.z[::-1]:
             held = reduce.terms
             if bit == plan.x[0]:
-                *held, returned.same = tie(*held, returned.same)
+                held = tie(*held)
                 returned.prompt_three()
             elif bit == plan.y[0]:
                 *held, grads, shared_n, returned.back = tie(*held, grads, shared_n, returned.back)

time: 340 us -> 330 us (0.971)
  starting transfers between devices: 65.1 us -> 60.5 us
  waiting for transfers between devices: 139 us -> 135 us
    ppermute x22, waiting for transfers between devices: 95.3 us -> 77.6 us  [swap(): return lax.ppermute(value, AXES, [(i, i ^ mask) for i in range(self.count)])]
    reduce_scatter x3, waiting for transfers between devices: 7.75 us -> 19.7 us  [per_device(): lax.psum_scatter(value, axes, scatter_dimension=0, tiled=True)]
    ppermute x22, starting transfers between devices: 58.5 us -> 53.9 us  [swap(): return lax.ppermute(value, AXES, [(i, i ^ mask) for i in range(self.count)])]
  transfers between devices with their start and end apart: 30 -> 30, of which waited for: 16 -> 17; matrix products, arithmetic and copies ran while one was open for 8% -> 8% of each run, Pallas kernels for 18% -> 18%
where the time goes in v14:
time: 330 us; the launch traced here: 329 us
  waiting for transfers between devices  135 us (41%)
  Pallas kernels  81.7 us (25%)
  starting transfers between devices  60.5 us (18%)
  other arithmetic  20.2 us (6%)
  local copies, waits for them, and re-layouts  17.3 us (5%)
  between operations  14.3 us (4%)
    ppermute x22, waiting for transfers between devices, swap(): return lax.ppermute(value, AXES, [(i, i ^ mask) for i in range(self.count)])  77.6 us
    ppermute x22, starting transfers between devices, swap(): return lax.ppermute(value, AXES, [(i, i ^ mask) for i in range(self.count)])  53.9 us
    ppermute x4, waiting for transfers between devices, send(): return lax.ppermute(value, AXES, pairs)  31 us
    pallas_call x1, Pallas kernels, middle_call(): pl.pallas_call(functools.partial(middle_kernel, wide, mapped), grid=(2 *...  20.9 us
    reduce_scatter x3, waiting for transfers between devices, per_device(): lax.psum_scatter(value, axes, scatter_dimension=0, tiled=True)  19.7 us
    pallas_call x1, Pallas kernels, attention_call(): pl.pallas_call(functools.partial(attention_kernel, blocks, first, rows, p...  19.1 us
    pallas_call x2, Pallas kernels, back_call(): pl.pallas_call(functools.partial(back_kernel, rows, bound, dq0 is not Non...  18 us
    pallas_call x1, Pallas kernels, weight_call(): pl.pallas_call(functools.partial(weight_kernel, blocks, first, rows, runs...  11.4 us
  transfers between devices with their start and end apart: 30, of which 17 were waited for; matrix products, arithmetic and copies ran while one was open for 8% of the time, Pallas kernels for 18%

profile of v14, /device:TPU:0, one launch (start us, length us, event | category | flops | bytes accessed | tf_op | source)
XLA Modules:
  0.0 328.8 jit_solution(976486644622494565)
XLA Ops:
  9.4 1.8 pack.1
  11.3 3.1 collective-permute-start
  14.4 2.6 collective-permute-start.1
  17.0 3.8 %collective-permute-start.3 = (bf16[256,768]{1,0:T(8,128)(2,1)}, bf16[256,768]{1,0:T(8,128)(2,1)S(1)}, u32[]{:S(2)}, u32[]{:S(2)}) collective-permute-start(bf16[256,768]{1,0:T(8,128)(2,1)} %bitcast.158), channel_id=1, source_target_pairs={{0,4},{1,5},{2,6},{3,7},{8,12},{9,13},{10,14},{11,15},{16,20},{17,... | collective-permute-start | bytes 1179656 | tf_op jit(solution)/shard_map/ppermute | solution.py:55
  20.9 1.6 collective-permute-start.4
  24.2 14.2 %collective-permute-done.3 = bf16[256,768]{1,0:T(8,128)(2,1)S(1)} collective-permute-done((bf16[256,768]{1,0:T(8,128)(2,1)}, bf16[256,768]{1,0:T(8,128)(2,1)S(1)}, u32[]{:S(2)}, u32[]{:S(2)}) %collective-permute-start.3) | collective-permute-done | bytes 393248 | tf_op jit(solution)/shard_map/ppermute | solution.py:55
  40.2 16.6 %collective-permute-start.7 = (bf16[256,768]{1,0:T(8,128)(2,1)S(1)}, bf16[256,768]{1,0:T(8,128)(2,1)S(1)}, u32[]{:S(2)}, u32[]{:S(2)}) collective-permute-start(bf16[256,768]{1,0:T(8,128)(2,1)S(1)} %broadcast_select_fusion.refs_0_), channel_id=1, source_target_pairs={{0,2},{1,3},{2,0},{3,1},{4,6},{5,7},{6,4},{7,5},{8,10},{9,11},{10,... | collective-permute-start | bytes 1179656 | tf_op jit(solution)/shard_map/ppermute | solution.py:51
  57.7 1.4 collective-permute-start.6
  59.8 10.9 %collective-permute-done.6 = bf16[4,40,768]{2,1,0:T(8,128)(2,1)S(1)} collective-permute-done((bf16[4,40,768]{2,1,0:T(8,128)(2,1)S(1)}, bf16[4,40,768]{2,1,0:T(8,128)(2,1)S(1)}, u32[]{:S(2)}, u32[]{:S(2)}) %collective-permute-start.6) | collective-permute-done | bytes 245792 | tf_op jit(solution)/shard_map/ppermute | solution.py:51
  70.8 4.5 %collective-permute-done.7.refs_1_ = bf16[256,768]{1,0:T(8,128)(2,1)S(1)} collective-permute-done((bf16[256,768]{1,0:T(8,128)(2,1)S(1)}, bf16[256,768]{1,0:T(8,128)(2,1)S(1)}, u32[]{:S(2)}, u32[]{:S(2)}) %collective-permute-start.7) | collective-permute-done | bytes 393248 | tf_op jit(solution)/shard_map/ppermute | solution.py:51
  75.3 1.5 collective-permute-start.13
  76.8 1.5 collective-permute-start.10
  78.3 14.6 %collective-permute-done.13 = bf16[8,40,768]{2,1,0:T(8,128)(2,1)S(1)} collective-permute-done((bf16[8,40,768]{2,1,0:T(8,128)(2,1)S(1)}, bf16[8,40,768]{2,1,0:T(8,128)(2,1)S(1)}, u32[]{:S(2)}, u32[]{:S(2)}) %collective-permute-start.13) | collective-permute-done | bytes 491552 | tf_op jit(solution)/shard_map/ppermute | solution.py:51
  93.1 2.5 collective-permute-done.10
  95.7 5.6 %collective-permute-done.11.refs_3_ = bf16[256,768]{1,0:T(8,128)(2,1)S(1)} collective-permute-done((bf16[256,768]{1,0:T(8,128)(2,1)S(1)}, bf16[256,768]{1,0:T(8,128)(2,1)S(1)}, u32[]{:S(2)}, u32[]{:S(2)}) %collective-permute-start.11) | collective-permute-done | bytes 393248 | tf_op jit(solution)/shard_map/ppermute | solution.py:51
  104.9 19.1 %attention.1 = (bf16[32,72,768]{2,1,0:T(8,128)(2,1)}, bf16[256,768]{1,0:T(8,128)(2,1)}, bf16[1024,768]{1,0:T(8,128)(2,1)}, bf16[1024,768]{1,0:T(8,128)(2,1)}, bf...) custom-call(bf16[256,768]{1,0:T(8,128)(2,1)} %copy-done.7, ...), custom_call_target="tpu_custom_call" | custom-call | flops 9865003008 | bytes 12582912 | tf_op jit(solution)/shard_map/attention/pallas_call | solution.py:342
  124.0 6.3 %all-gather.2.cloned.1.call-done = bf16[7168,768]{1,0:T(8,128)(2,1)} async-done(((bf16[224,768]{1,0:T(8,128)(2,1)}), bf16[7168,768]{1,0:T(8,128)(2,1)}) %all-gather.2.cloned.1.call-update) | async-done | bytes 11010064 | tf_op jit(solution)/shard_map/all_gather | solution.py:847
  132.6 20.9 %middle.1 = (bf16[256,768]{1,0:T(8,128)(2,1)}, f32[256,768]{1,0:T(8,128)}, bf16[256,768]{1,0:T(8,128)(2,1)}, bf16[32,216,768]{2,1,0:T(8,128)(2,1)}, f32[8,768]{1,0:T(8,128)}, /*index=5*/f32[8,768]{1,0:T(8,128)}) custom-call(bf16[256,768]{1,0:T(8,128)(2,1)} %get-tuple-element.96.ctx_ref.refs_2_, bf16[256,768]{1,0:T(8,128)(2,1)} %bitcast.163, ...), custom_call_target="tpu_custom_call" | custom-call | flops 8153726976 | bytes 33554432 | tf_op jit(solution)/shard_map/middle/pallas_call | solution.py:567
  153.5 12.5 %attention_back.2 = (bf16[1024,768]{1,0:T(8,128)(2,1)}, bf16[1024,768]{1,0:T(8,128)(2,1)}, f32[768,256]{1,0:T(8,128)}) custom-call(s32[1]{0:T(128)} %bitcast.9.refs_7_.refs_0_.near_ref, bf16[256,768]{1,0:T(8,128)(2,1)} %get-tuple-element.99.refs_1_, bf16[256,768]{1,0:T(8,128)(2,1)} %get-tuple-element.96.ctx_ref.refs_2_, ...), custom_call_target="tpu_custom_call" | custom-call | flops 16106127360 | bytes 6291456 | tf_op jit(solution)/shard_map/attention_back/pallas_call | solution.py:659
  166.0 6.4 %token_product.2 = bf16[4,256,768]{2,1,0:T(8,128)(2,1)} custom-call(s32[1]{0:T(128)} %bitcast.9.refs_7_.refs_0_.near_ref, bf16[1024,768]{1,0:T(8,128)(2,1)} %get-tuple-element.107.dk_ref.refs_13_, bf16[1024,768]{1,0:T(8,128)(2,1)} %get-tuple-element.108.dv_ref.refs_14_, bf16[32,72,768]{2,1,0:T(8,128)(2,1)} %get-tuple-element.109.wk_ref.wv_ref.refs_11_, ...), custom_call_target="tpu_custom_call" | custom-call | flops 2415919104 | bytes 4718592 | tf_op jit(solution)/shard_map/token_product/pallas_call | solution.py:697
  172.5 12.9 %reduce-scatter.4.cloned.1.call-done = bf16[16,216,768]{2,1,0:T(8,128)(2,1)} async-done(((bf16[32,216,768]{2,1,0:T(8,128)(2,1)}), bf16[16,216,768]{2,1,0:T(8,128)(2,1)}) %reduce-scatter.4.cloned.1.call-update) | async-done | bytes 5308432 | tf_op jit(solution)/shard_map/reduce_scatter | solution.py:921
  187.0 1.9 collective-permute-start.15
  189.1 5.5 %attention_back.3 = (bf16[768,768]{1,0:T(8,128)(2,1)}, bf16[768,768]{1,0:T(8,128)(2,1)}, f32[768,256]{1,0:T(8,128)}) custom-call(s32[1]{0:T(128)} %bitcast.9.refs_7_.refs_0_.near_ref, bf16[256,768]{1,0:T(8,128)(2,1)} %get-tuple-element.99.refs_1_, bf16[256,768]{1,0:T(8,128)(2,1)} %get-tuple-element.96.ctx_ref.refs_2_, ...), custom_call_target="tpu_custom_call" | custom-call | flops 12079595520 | bytes 4718592 | tf_op jit(solution)/shard_map/attention_back/pallas_call | solution.py:659
  194.6 11.4 %weight_product.1 = (bf16[16,72,768]{2,1,0:T(8,128)(2,1)}, bf16[16,72,768]{2,1,0:T(8,128)(2,1)}, f32[256,768]{1,0:T(8,128)}, f32[8,768]{1,0:T(8,128)}) custom-call(bf16[256,768]{1,0:T(8,128)(2,1)} %copy-done.7, bf16[256,768]{1,0:T(8,128)(2,1)} %copy-done.13, bf16[256,768]{1,0:T(8,128)(2,1)} %copy-done.14, bf16[256,768]{1,0:T(8,128)(2,1)} %copy-done.15, ...), custom_call_target="tpu_custom_call" | custom-call | flops 4227858432 | bytes 16515072 | tf_op jit(solution)/shard_map/weight_product/pallas_call | solution.py:776
  207.3 2.1 fusion.1
  209.4 1.5 pad_maximum_fusion.1
  210.9 1.6 collective-permute-start.17
  212.6 1.6 pad_maximum_fusion
  214.2 1.1 collective-permute-done.18
  215.2 2.4 add_convert_fusion
  217.6 1.6 collective-permute-start.19
  219.2 12.1 %collective-permute-done.17 = bf16[256,768]{1,0:T(8,128)(2,1)S(1)} collective-permute-done((bf16[256,768]{1,0:T(8,128)(2,1)}, bf16[256,768]{1,0:T(8,128)(2,1)S(1)}, u32[]{:S(2)}, u32[]{:S(2)}) %collective-permute-start.17) | collective-permute-done | bytes 393248 | tf_op jit(solution)/shard_map/ppermute | solution.py:51
  231.4 1.3 collective-permute-start.20
  232.7 4.2 %token_product.3 = bf16[3,256,768]{2,1,0:T(8,128)(2,1)} custom-call(s32[1]{0:T(128)} %bitcast.9.refs_7_.refs_0_.near_ref, bf16[768,768]{1,0:T(8,128)(2,1)} %get-tuple-element.130.refs_15_.dk_ref, bf16[768,768]{1,0:T(8,128)(2,1)} %get-tuple-element.131.refs_16_.dv_ref, bf16[32,72,768]{2,1,0:T(8,128)(2,1)} %get-tuple-element.109.wk_ref.wv_ref.refs_11_, ...), custom_call_target="tpu_custom_call" | custom-call | flops 1811939328 | bytes 3538944 | tf_op jit(solution)/shard_map/token_product/pallas_call | solution.py:697
  236.9 2.2 constant_dynamic-slice_fusion.4
  240.2 16.8 %collective-permute-done.20 = bf16[256,768]{1,0:T(8,128)(2,1)} collective-permute-done((bf16[256,768]{1,0:T(8,128)(2,1)S(1)}, bf16[256,768]{1,0:T(8,128)(2,1)}, u32[]{:S(2)}, u32[]{:S(2)}) %collective-permute-start.20) | collective-permute-done | bytes 393248 | tf_op jit(solution)/shard_map/ppermute | solution.py:55
  257.0 6.8 %reduce-scatter.6.cloned.1.call-done = bf16[4,216,768]{2,1,0:T(8,128)(2,1)} async-done(((bf16[16,216,768]{2,1,0:T(8,128)(2,1)}), bf16[4,216,768]{2,1,0:T(8,128)(2,1)}) %reduce-scatter.6.cloned.1.call-update) | async-done | bytes 1327120 | tf_op jit(solution)/shard_map/reduce_scatter | solution.py:921
  263.8 2.4 fusion.3
  266.2 1.5 collective-permute-start.21
  267.7 1.2 dynamic-slice_bitcast_fusion
  269.2 10.5 %collective-permute-done.21 = bf16[4,80,768]{2,1,0:T(8,128)(2,1)} collective-permute-done((bf16[4,80,768]{2,1,0:T(8,128)(2,1)}, bf16[4,80,768]{2,1,0:T(8,128)(2,1)}, u32[]{:S(2)}, u32[]{:S(2)}) %collective-permute-start.21) | collective-permute-done | bytes 491552 | tf_op jit(solution)/shard_map/ppermute | solution.py:51
  279.7 1.6 collective-permute-start.23
  282.0 1.1 add_convert_fusion.3
  283.1 3.1 collective-permute-start.22
  287.3 2.8 collective-permute-done.23
  290.2 11.3 %collective-permute-done.22 = bf16[2,80,768]{2,1,0:T(8,128)(2,1)S(1)} collective-permute-done((bf16[2,80,768]{2,1,0:T(8,128)(2,1)S(1)}, bf16[2,80,768]{2,1,0:T(8,128)(2,1)S(1)}, u32[]{:S(2)}, u32[]{:S(2)}) %collective-permute-start.22) | collective-permute-done | bytes 245792 | tf_op jit(solution)/shard_map/ppermute | solution.py:51
  301.6 12.6 %collective-permute-start.25 = (bf16[1,80,768]{2,1,0:T(8,128)(2,1)S(1)}, bf16[1,80,768]{2,1,0:T(8,128)(2,1)S(1)}, u32[]{:S(2)}, u32[]{:S(2)}) collective-permute-start(bf16[1,80,768]{2,1,0:T(8,128)(2,1)S(1)} %add_convert_fusion.4), channel_id=1, source_target_pairs={{0,2},{1,3},{2,0},{3,1},{4,6},{5,7},{6,4},{7,5},{8,10},{9,11},{10,... | collective-permute-start | bytes 368648 | tf_op jit(solution)/shard_map/ppermute | solution.py:51
  314.2 2.0 fusion.4
  (137 shorter events, 26.0 us)
Async XLA Ops:
  7.2 123.2 %all-gather.2.cloned.1.call-start = ((), (), s32[]{:S(2)}) async-start(), calls=%async_computation.3 | async-start | bytes 11354112 | tf_op jit(solution)/shard_map/all_gather | solution.py:847
  11.3 174.1 %reduce-scatter.4.cloned.1.call-start = ((), (), s32[]{:S(2)}) async-start(), calls=%async_computation.4 | async-start | bytes 15925248 | tf_op jit(solution)/shard_map/reduce_scatter | solution.py:921
  11.3 28.8 %collective-permute-start = (bf16[80,768]{1,0:T(8,128)(2,1)}, bf16[80,768]{1,0:T(8,128)(2,1)S(1)}, u32[]{:S(2)}, u32[]{:S(2)}) collective-permute-start(bf16[80,768]{1,0:T(8,128)(2,1)} %get-tuple-element.83), channel_id=1, source_target_pairs={{0,2},{1,3},{2,0},{3,1},{4,6},{5,7},{6,4},{7,5},{8,10},{9,11},{10,... | collective-permute-start | bytes 368648 | tf_op jit(solution)/shard_map/ppermute | solution.py:51
  14.4 25.8 %collective-permute-start.1 = (bf16[80,768]{1,0:T(8,128)(2,1)}, bf16[80,768]{1,0:T(8,128)(2,1)S(1)}, u32[]{:S(2)}, u32[]{:S(2)}) collective-permute-start(bf16[80,768]{1,0:T(8,128)(2,1)} %get-tuple-element.83), channel_id=1, source_target_pairs={{0,4},{1,5},{2,6},{3,7},{4,0},{5,1},{6,2},{7,3},{8,12},{9,13},{10,... | collective-permute-start | bytes 368648 | tf_op jit(solution)/shard_map/ppermute | solution.py:51
  17.0 23.2 %collective-permute-start.2 = (bf16[80,768]{1,0:T(8,128)(2,1)}, bf16[80,768]{1,0:T(8,128)(2,1)S(1)}, u32[]{:S(2)}, u32[]{:S(2)}) collective-permute-start(bf16[80,768]{1,0:T(8,128)(2,1)} %get-tuple-element.83), channel_id=1, source_target_pairs={{0,6},{1,7},{2,4},{3,5},{4,2},{5,3},{6,0},{7,1},{8,14},{9,15},{10,... | collective-permute-start | bytes 368648 | tf_op jit(solution)/shard_map/ppermute | solution.py:51
  17.0 21.4 %collective-permute-start.3 = (bf16[256,768]{1,0:T(8,128)(2,1)}, bf16[256,768]{1,0:T(8,128)(2,1)S(1)}, u32[]{:S(2)}, u32[]{:S(2)}) collective-permute-start(bf16[256,768]{1,0:T(8,128)(2,1)} %bitcast.158), channel_id=1, source_target_pairs={{0,4},{1,5},{2,6},{3,7},{8,12},{9,13},{10,14},{11,15},{16,20},{17,... | collective-permute-start | bytes 1179656 | tf_op jit(solution)/shard_map/ppermute | solution.py:55
  20.9 19.4 %collective-permute-start.4 = (bf16[256,768]{1,0:T(8,128)(2,1)}, bf16[256,768]{1,0:T(8,128)(2,1)S(1)}, u32[]{:S(2)}, u32[]{:S(2)}) collective-permute-start(bf16[256,768]{1,0:T(8,128)(2,1)} %bitcast.159), channel_id=1, source_target_pairs={{0,1},{1,0},{2,3},{3,2},{4,5},{5,4},{6,7},{7,6},{8,9},{9,8},{10,11... | collective-permute-start | bytes 1179656 | tf_op jit(solution)/shard_map/ppermute | solution.py:51
  38.4 32.3 %collective-permute-start.9 = (bf16[256,768]{1,0:T(8,128)(2,1)}, bf16[256,768]{1,0:T(8,128)(2,1)S(1)}, u32[]{:S(2)}, u32[]{:S(2)}) collective-permute-start(bf16[256,768]{1,0:T(8,128)(2,1)} %bitcast.160), channel_id=1, source_target_pairs={{5,6},{6,5},{13,14},{14,13},{21,22},{22,21},{29,30},{30,29}} | collective-permute-start | bytes 1179656 | tf_op jit(solution)/shard_map/ppermute | solution.py:55
  40.2 38.1 %copy-start.7 = (bf16[256,768]{1,0:T(8,128)(2,1)}, bf16[256,768]{1,0:T(8,128)(2,1)S(1)}, u32[]{:S(2)}) copy-start(bf16[256,768]{1,0:T(8,128)(2,1)S(1)} %broadcast_select_fusion.refs_0_) | copy-start | bytes 1179652
  40.2 38.1 %copy-start.11 = (bf16[256,768]{1,0:T(8,128)(2,1)}, bf16[256,768]{1,0:T(8,128)(2,1)S(1)}, u32[]{:S(2)}) copy-start(bf16[256,768]{1,0:T(8,128)(2,1)S(1)} %collective-permute-done.4.refs_5_) | copy-start | bytes 1179652
  40.2 35.0 %collective-permute-start.7 = (bf16[256,768]{1,0:T(8,128)(2,1)S(1)}, bf16[256,768]{1,0:T(8,128)(2,1)S(1)}, u32[]{:S(2)}, u32[]{:S(2)}) collective-permute-start(bf16[256,768]{1,0:T(8,128)(2,1)S(1)} %broadcast_select_fusion.refs_0_), channel_id=1, source_target_pairs={{0,2},{1,3},{2,0},{3,1},{4,6},{5,7},{6,4},{7,5},{8,10},{9,11},{10,... | collective-permute-start | bytes 1179656 | tf_op jit(solution)/shard_map/ppermute | solution.py:51
  56.9 18.4 %collective-permute-start.8 = (bf16[256,768]{1,0:T(8,128)(2,1)S(1)}, bf16[256,768]{1,0:T(8,128)(2,1)S(1)}, u32[]{:S(2)}, u32[]{:S(2)}) collective-permute-start(bf16[256,768]{1,0:T(8,128)(2,1)S(1)} %broadcast_select_fusion.refs_0_), channel_id=1, source_target_pairs={{0,1},{1,0},{2,3},{3,2},{4,5},{5,4},{6,7},{7,6},{8,9},{9,8},{10,11... | collective-permute-start | bytes 1179656 | tf_op jit(solution)/shard_map/ppermute | solution.py:51
  57.7 13.0 %collective-permute-start.6 = (bf16[4,40,768]{2,1,0:T(8,128)(2,1)S(1)}, bf16[4,40,768]{2,1,0:T(8,128)(2,1)S(1)}, u32[]{:S(2)}, u32[]{:S(2)}) collective-permute-start(bf16[4,40,768]{2,1,0:T(8,128)(2,1)S(1)} %pad_maximum_fusion.5), channel_id=1, source_target_pairs={{0,1},{1,0},{2,3},{3,2},{4,5},{5,4},{6,7},{7,6},{8,9},{9,8},{10,11... | collective-permute-start | bytes 737288 | tf_op jit(solution)/shard_map/ppermute | solution.py:51
  59.1 11.6 %collective-permute-start.5 = (bf16[4,40,768]{2,1,0:T(8,128)(2,1)S(1)}, bf16[4,40,768]{2,1,0:T(8,128)(2,1)S(1)}, u32[]{:S(2)}, u32[]{:S(2)}) collective-permute-start(bf16[4,40,768]{2,1,0:T(8,128)(2,1)S(1)} %pad_maximum_fusion.4), channel_id=1, source_target_pairs={{0,16},{1,17},{2,18},{3,19},{4,20},{5,21},{6,22},{7,23},{8,24},{9,... | collective-permute-start | bytes 737288 | tf_op jit(solution)/shard_map/ppermute | solution.py:51
  70.7 31.3 %copy-start.16 = (s32[1,8]{1,0:T(1,128)S(1)}, s32[1,8]{1,0:T(1,128)}, u32[]{:S(2)}) copy-start(s32[1,8]{1,0:T(1,128)} %param.19) | copy-start | bytes 100
  70.8 7.5 %copy-start.12 = (bf16[256,768]{1,0:T(8,128)(2,1)}, bf16[256,768]{1,0:T(8,128)(2,1)S(1)}, u32[]{:S(2)}) copy-start(bf16[256,768]{1,0:T(8,128)(2,1)S(1)} %collective-permute-done.9.refs_6_) | copy-start | bytes 1179652
  75.3 3.0 copy-start.13
  75.3 20.4 %copy-start.14 = (bf16[256,768]{1,0:T(8,128)(2,1)}, bf16[256,768]{1,0:T(8,128)(2,1)S(1)}, u32[]{:S(2)}) copy-start(bf16[256,768]{1,0:T(8,128)(2,1)S(1)} %collective-permute-done.8.refs_2_) | copy-start | bytes 1179652
  75.3 17.7 %collective-permute-start.13 = (bf16[8,40,768]{2,1,0:T(8,128)(2,1)S(1)}, bf16[8,40,768]{2,1,0:T(8,128)(2,1)S(1)}, u32[]{:S(2)}, u32[]{:S(2)}) collective-permute-start(bf16[8,40,768]{2,1,0:T(8,128)(2,1)S(1)} %constant_dynamic-update-slice_fusion.5), channel_id=1, source_target_pairs={{0,16},{1,17},{2,18},{3,19},{4,20},{5,21},{6,22},{7,23},{8,24},{9,... | collective-permute-start | bytes 1474568 | tf_op jit(solution)/shard_map/ppermute | solution.py:51
  76.8 18.8 %collective-permute-start.10 = (bf16[8,40,768]{2,1,0:T(8,128)(2,1)S(1)}, bf16[8,40,768]{2,1,0:T(8,128)(2,1)S(1)}, u32[]{:S(2)}, u32[]{:S(2)}) collective-permute-start(bf16[8,40,768]{2,1,0:T(8,128)(2,1)S(1)} %constant_dynamic-update-slice_fusion), channel_id=1, source_target_pairs={{0,1},{1,0},{2,3},{3,2},{4,5},{5,4},{6,7},{7,6},{8,9},{9,8},{10,11... | collective-permute-start | bytes 1474568 | tf_op jit(solution)/shard_map/ppermute | solution.py:51
  78.3 23.0 %collective-permute-start.11 = (bf16[256,768]{1,0:T(8,128)(2,1)S(1)}, bf16[256,768]{1,0:T(8,128)(2,1)S(1)}, u32[]{:S(2)}, u32[]{:S(2)}) collective-permute-start(bf16[256,768]{1,0:T(8,128)(2,1)S(1)} %collective-permute-done.8.refs_2_), channel_id=1, source_target_pairs={{0,2},{1,3},{2,0},{3,1},{4,6},{5,7},{6,4},{7,5},{8,10},{9,11},{10,... | collective-permute-start | bytes 1179656 | tf_op jit(solution)/shard_map/ppermute | solution.py:51
  93.0 11.8 %copy-start.8 = (bf16[16,40,768]{2,1,0:T(8,128)(2,1)}, bf16[16,40,768]{2,1,0:T(8,128)(2,1)S(1)}, u32[]{:S(2)}) copy-start(bf16[16,40,768]{2,1,0:T(8,128)(2,1)S(1)} %constant_dynamic-update-slice_fusion.10.refs_12_) | copy-start | bytes 2949124
  93.0 10.9 %collective-permute-start.14 = (bf16[16,40,768]{2,1,0:T(8,128)(2,1)S(1)}, bf16[16,40,768]{2,1,0:T(8,128)(2,1)S(1)}, u32[]{:S(2)}, u32[]{:S(2)}) collective-permute-start(bf16[16,40,768]{2,1,0:T(8,128)(2,1)S(1)} %constant_dynamic-update-slice_fusion.10.refs_12_), channel_id=1, source_target_pairs={{0,8},{1,9},{2,10},{3,11},{4,12},{5,13},{6,14},{7,15},{8,0},{9,1},... | collective-permute-start | bytes 2949128 | tf_op jit(solution)/shard_map/ppermute | solution.py:51
  95.7 9.1 %copy-start.5 = (bf16[16,40,768]{2,1,0:T(8,128)(2,1)}, bf16[16,40,768]{2,1,0:T(8,128)(2,1)S(1)}, u32[]{:S(2)}) copy-start(bf16[16,40,768]{2,1,0:T(8,128)(2,1)S(1)} %pad_maximum_fusion.2.refs_10_) | copy-start | bytes 2949124
  101.3 0.8 copy-start.15
  102.1 2.7 collective-permute-start.12
  104.0 1.0 copy-start.10
  153.5 110.3 %reduce-scatter.6.cloned.1.call-start = ((), (), s32[]{:S(2)}) async-start(), calls=%async_computation.5 | async-start | bytes 6635520 | tf_op jit(solution)/shard_map/reduce_scatter | solution.py:921
  185.4 0.7 copy-start.9
  185.4 1.6 copy-start
  185.4 133.7 %reduce-scatter.8.cloned.1.call-start = ((), (), s32[]{:S(2)}) async-start(), calls=%async_computation.6 | async-start | bytes 1658880 | tf_op jit(solution)/shard_map/reduce_scatter | solution.py:921
  187.0 20.3 %collective-permute-start.15 = (bf16[256,768]{1,0:T(8,128)(2,1)S(1)}, bf16[256,768]{1,0:T(8,128)(2,1)S(1)}, u32[]{:S(2)}, u32[]{:S(2)}) collective-permute-start(bf16[256,768]{1,0:T(8,128)(2,1)S(1)} %get-tuple-element.152), channel_id=1, source_target_pairs={{0,2},{1,3},{2,0},{3,1},{4,6},{5,7},{6,4},{7,5},{8,10},{9,11},{10,... | collective-permute-start | bytes 1179656 | tf_op jit(solution)/shard_map/ppermute | solution.py:51
  188.9 18.4 %collective-permute-start.16 = (bf16[256,768]{1,0:T(8,128)(2,1)S(1)}, bf16[256,768]{1,0:T(8,128)(2,1)}, u32[]{:S(2)}, u32[]{:S(2)}) collective-permute-start(bf16[256,768]{1,0:T(8,128)(2,1)S(1)} %get-tuple-element.151), channel_id=1, source_target_pairs={{0,2},{1,3},{2,0},{3,1},{4,6},{5,7},{6,4},{7,5},{8,10},{9,11},{10,... | collective-permute-start | bytes 1179656 | tf_op jit(solution)/shard_map/ppermute | solution.py:51
  207.2 2.3 copy-start.4
  210.9 4.3 %collective-permute-start.18 = (bf16[16,80,768]{2,1,0:T(8,128)(2,1)}, bf16[16,80,768]{2,1,0:T(8,128)(2,1)}, u32[]{:S(2)}, u32[]{:S(2)}) collective-permute-start(bf16[16,80,768]{2,1,0:T(8,128)(2,1)} %pad_maximum_fusion.1), channel_id=1, source_target_pairs={{0,8},{1,9},{2,10},{3,11},{4,12},{5,13},{6,14},{7,15},{8,0},{9,1},... | collective-permute-start | bytes 5898248 | tf_op jit(solution)/shard_map/ppermute | solution.py:51
  210.9 20.4 %collective-permute-start.17 = (bf16[256,768]{1,0:T(8,128)(2,1)}, bf16[256,768]{1,0:T(8,128)(2,1)S(1)}, u32[]{:S(2)}, u32[]{:S(2)}) collective-permute-start(bf16[256,768]{1,0:T(8,128)(2,1)} %get-tuple-element.121), channel_id=1, source_target_pairs={{0,1},{1,0},{2,3},{3,2},{4,5},{5,4},{6,7},{7,6},{8,9},{9,8},{10,11... | collective-permute-start | bytes 1179656 | tf_op jit(solution)/shard_map/ppermute | solution.py:51
  217.6 39.4 %collective-permute-start.19 = (bf16[8,80,768]{2,1,0:T(8,128)(2,1)}, bf16[8,80,768]{2,1,0:T(8,128)(2,1)}, u32[]{:S(2)}, u32[]{:S(2)}) collective-permute-start(bf16[8,80,768]{2,1,0:T(8,128)(2,1)} %bitcast.33), channel_id=1, source_target_pairs={{0,16},{1,17},{2,18},{3,19},{4,20},{5,21},{6,22},{7,23},{8,24},{9,... | collective-permute-start | bytes 2949128 | tf_op jit(solution)/shard_map/ppermute | solution.py:51
  231.4 25.6 %collective-permute-start.20 = (bf16[256,768]{1,0:T(8,128)(2,1)S(1)}, bf16[256,768]{1,0:T(8,128)(2,1)}, u32[]{:S(2)}, u32[]{:S(2)}) collective-permute-start(bf16[256,768]{1,0:T(8,128)(2,1)S(1)} %fusion.2), channel_id=1, source_target_pairs={{4,0},{5,1},{6,2},{7,3},{12,8},{13,9},{14,10},{15,11},{20,16},{21,... | collective-permute-start | bytes 1179656 | tf_op jit(solution)/shard_map/ppermute | solution.py:55
  263.8 5.1 %copy-start.2 = (bf16[1,1,640,768]{3,2,1,0:T(8,128)(2,1)S(1)}, bf16[1,1,640,768]{3,2,1,0:T(8,128)(2,1)}, u32[]{:S(2)}) copy-start(bf16[1,1,640,768]{3,2,1,0:T(8,128)(2,1)} %constant_dynamic-slice_fusion.4) | copy-start | bytes 2949124
  266.2 13.5 %collective-permute-start.21 = (bf16[4,80,768]{2,1,0:T(8,128)(2,1)}, bf16[4,80,768]{2,1,0:T(8,128)(2,1)}, u32[]{:S(2)}, u32[]{:S(2)}) collective-permute-start(bf16[4,80,768]{2,1,0:T(8,128)(2,1)} %fusion.3), channel_id=1, source_target_pairs={{0,1},{1,0},{2,3},{3,2},{4,5},{5,4},{6,7},{7,6},{8,9},{9,8},{10,11... | collective-permute-start | bytes 1474568 | tf_op jit(solution)/shard_map/ppermute | solution.py:51
  267.7 12.0 %copy-start.1 = (bf16[3,256,768]{2,1,0:T(8,128)(2,1)S(1)}, bf16[3,256,768]{2,1,0:T(8,128)(2,1)}, u32[]{:S(2)}) copy-start(bf16[3,256,768]{2,1,0:T(8,128)(2,1)} %token_product.3) | copy-start | bytes 3538948
  267.7 1.4 copy-start.3
  279.7 10.3 %collective-permute-start.23 = (bf16[256,768]{1,0:T(8,128)(2,1)S(1)}, bf16[256,768]{1,0:T(8,128)(2,1)S(1)}, u32[]{:S(2)}, u32[]{:S(2)}) collective-permute-start(bf16[256,768]{1,0:T(8,128)(2,1)S(1)} %get-tuple-element.153), channel_id=1, source_target_pairs={{0,1},{1,0},{2,3},{3,2},{4,5},{5,4},{6,7},{7,6},{8,9},{9,8},{10,11... | collective-permute-start | bytes 1179656 | tf_op jit(solution)/shard_map/ppermute | solution.py:51
  281.3 8.7 %collective-permute-start.24 = (bf16[256,768]{1,0:T(8,128)(2,1)S(1)}, bf16[256,768]{1,0:T(8,128)(2,1)S(1)}, u32[]{:S(2)}, u32[]{:S(2)}) collective-permute-start(bf16[256,768]{1,0:T(8,128)(2,1)S(1)} %get-tuple-element.154), channel_id=1, source_target_pairs={{5,6},{6,5},{13,14},{14,13},{21,22},{22,21},{29,30},{30,29}} | collective-permute-start | bytes 1179656 | tf_op jit(solution)/shard_map/ppermute | solution.py:55
  283.1 18.4 %collective-permute-start.22 = (bf16[2,80,768]{2,1,0:T(8,128)(2,1)S(1)}, bf16[2,80,768]{2,1,0:T(8,128)(2,1)S(1)}, u32[]{:S(2)}, u32[]{:S(2)}) collective-permute-start(bf16[2,80,768]{2,1,0:T(8,128)(2,1)S(1)} %bitcast.167), channel_id=1, source_target_pairs={{0,4},{1,5},{2,6},{3,7},{4,0},{5,1},{6,2},{7,3},{8,12},{9,13},{10,... | collective-permute-start | bytes 737288 | tf_op jit(solution)/shard_map/ppermute | solution.py:51
  287.2 27.0 %copy-start.6 = (f32[256,768]{1,0:T(8,128)S(1)}, f32[256,768]{1,0:T(8,128)}, u32[]{:S(2)}) copy-start(f32[256,768]{1,0:T(8,128)} %get-tuple-element.116) | copy-start | bytes 2359300
  301.6 15.6 %collective-permute-start.25 = (bf16[1,80,768]{2,1,0:T(8,128)(2,1)S(1)}, bf16[1,80,768]{2,1,0:T(8,128)(2,1)S(1)}, u32[]{:S(2)}, u32[]{:S(2)}) collective-permute-start(bf16[1,80,768]{2,1,0:T(8,128)(2,1)S(1)} %add_convert_fusion.4), channel_id=1, source_target_pairs={{0,2},{1,3},{2,0},{3,1},{4,6},{5,7},{6,4},{7,5},{8,10},{9,11},{10,... | collective-permute-start | bytes 368648 | tf_op jit(solution)/shard_map/ppermute | solution.py:51
Sparse Core Ops, SparseCore 0:
  11.5 118.8 all-gather.1
  153.6 31.6 reduce-scatter.3
  188.6 75.1 reduce-scatter.5
  267.8 43.3 reduce-scatter.7

commit v15 on v14

--- a/solution.py
+++ b/solution.py
@@ -395,8 +395,8 @@
     return jnp.where(core == 0, odd, even), jnp.where(core == 0, even, odd)
 
 
-def middle_kernel(wide, mapped, ctx_ref, own_ref, cot_ref, got_ref, vec_ref, bin_ref,
-                  out_ref, h1_ref, gctx_ref, grads, sums_ref, sbin_ref,
+def middle_kernel(wide, mapped, core_ref, ctx_ref, own_ref, cot_ref, got_ref, vec_ref, bin_ref,
+                  out_ref, h1_ref, gctx_ref, send, keep, sums_ref, sbin_ref,
                   first_ref, n1_ref, inv_ref, low_ref, pre_ref, cdf_ref, act_ref, acc_ref,
                   gffn_ref, glow_ref, lowt_ref, w_ref, out_buf, in_buf, wo_buf, sems, w_sems):
     step = pl.program_id(0)
@@ -422,43 +422,44 @@
     def fetch_output():
         return pltpu.make_async_copy(w_output(got_ref), w_output(w_ref), w_sems.at[0, wide])
 
-    def slot(group, i):
-        return group % 2 * 16 + group // 2 * 8 + i % 2 * 4 + i // 2 if mapped else group * 8 + i
-
-    def outer(at):
+    def home(core, group, i):
+        half = keep if group % 2 == core else send
+        return half.at[group // 2 * 8 + (i % 2 * 4 + i // 2 if mapped else i)]
+
+    def outer(at, core, act):
         turn = (2 * wide - 1 - at) % 2
-        return [
-            pltpu.make_async_copy(
-                out_buf.at[turn, i], grads.at[slot(at, i), pl.ds(0, wide * each)], sems.at[turn, i]
-            )
-            for i in range(some)
-        ]
-
-    def inner(at):
+        for i in range(some):
+            for parity in range(2):
+
+                @pl.when(at % 2 == parity)
+                def _():
+                    half = keep if parity == core else send
+                    place = half.at[at // 2 * 8 + (i % 2 * 4 + i // 2 if mapped else i)]
+                    act(pltpu.make_async_copy(
+                        out_buf.at[turn, i], place.at[pl.ds(0, wide * each)], sems.at[turn, i]
+                    ))
+
+    def inner(at, core, act):
         turn = (2 * wide - 1 - at) % 2
         top = pl.multiple_of((wide + 1 + at) * each, each)
-        return [
-            pltpu.make_async_copy(
-                in_buf.at[turn, e], grads.at[slot(e // 8, e % 8), pl.ds(top, each)], sems.at[2 + turn, e]
-            )
-            for e in range(owners)
-        ]
-
-    def output():
-        return [
-            pltpu.make_async_copy(
-                wo_buf.at[e], grads.at[slot(e // 8, e % 8), pl.ds(wide * each, each)], sems.at[4, e]
-            )
-            for e in range(owners)
-        ]
-
-    def start(copies):
-        for copy in copies:
-            copy.start()
-
-    def wait(copies):
-        for copy in copies:
-            copy.wait()
+        for e in range(owners):
+            place = home(core, e // 8, e % 8).at[pl.ds(top, each)]
+            act(pltpu.make_async_copy(in_buf.at[turn, e], place, sems.at[2 + turn, e]))
+
+    def output(at, core, act):
+        for e in range(owners):
+            place = home(core, e // 8, e % 8).at[pl.ds(wide * each, each)]
+            act(pltpu.make_async_copy(wo_buf.at[e], place, sems.at[4, e]))
+
+    def on_core(*calls):
+        for core in range(2):
+
+            @pl.when(core_ref[0] == core)
+            def _():
+                for call, at, act in calls:
+                    call(at, core, act)
+
+    go, end = lambda copy: copy.start(), lambda copy: copy.wait()
 
     @pl.when(step == 0)
     def _():
@@ -529,12 +530,12 @@
 
         @pl.when(step >= wide + 2)
         def _():
-            wait(outer(at + 2) + inner(at + 2))
+            on_core((outer, at + 2, end), (inner, at + 2, end))
 
         out_buf[turn] = tn(act_ref[:, chunk], low).astype(BF).reshape(some, wide * each, width)
-        start(outer(at))
+        on_core((outer, at, go))
         in_buf[turn] = mm(lowt_ref[...], grad).astype(BF).reshape(owners, each, width)
-        start(inner(at))
+        on_core((inner, at, go))
         gffn_ref[...] += nt(grad, square(w_inner(w_ref, at)[...]))
 
     @pl.when(step == 2 * wide - 1)
@@ -549,15 +550,15 @@
         low = back.astype(BF)
         sums_ref[5:6, :] = down(low.astype(F32))
         wo_buf[...] = tn(ctx_ref[...], low).astype(BF).reshape(owners, each, width)
-        start(output())
+        on_core((output, 0, go))
         gctx = nt(low, square(w_output(w_ref)[...])).astype(BF)
         gctx_ref[...] = gctx
         sums_ref[6:7, :] = down(gctx.astype(F32))
         sums_ref[7:8, :] = jnp.zeros((1, width), F32)
-        wait(outer(1) + inner(1) + outer(0) + inner(0) + output())
-
-
-def middle_call(ctx, own, cot, got, vec, b_inner, mapped):
+        on_core(*[(call, at, end) for at in (1, 0) for call in (outer, inner)], (output, 0, end))
+
+
+def middle_call(core, ctx, own, cot, got, vec, b_inner, mapped):
     rows, width = own.shape
     owners = got.shape[0]
     each = width // owners
@@ -568,18 +569,20 @@
         functools.partial(middle_kernel, wide, mapped),
         grid=(2 * wide,),
         in_specs=[
+            pl.BlockSpec(memory_space=pltpu.SMEM),
             whole((rows, width)), whole((rows, width)), whole((rows, width)),
             pl.BlockSpec(memory_space=pl.ANY),
             whole((8, width)), whole((8, width)),
         ],
         out_specs=[
             whole((rows, width)), whole((rows, width)), whole((rows, width)),
-            pl.BlockSpec(memory_space=pl.ANY),
+            pl.BlockSpec(memory_space=pl.ANY), pl.BlockSpec(memory_space=pl.ANY),
             whole((8, width)), whole((8, width)),
         ],
         out_shape=[
             shape((rows, width), BF), shape((rows, width), F32), shape((rows, width), BF),
-            shape((owners, (2 * wide + 1) * each, width), BF),
+            shape((owners // 2, (2 * wide + 1) * each, width), BF),
+            shape((owners // 2, (2 * wide + 1) * each, width), BF),
             shape((8, width), F32), shape((8, width), F32),
         ],
         scratch_shapes=[
@@ -600,7 +603,7 @@
             transcendentals=2 * rows * width * wide,
         ),
         name="middle",
-    )(ctx, own, cot, got, vec, b_inner)
+    )(core, ctx, own, cot, got, vec, b_inner)
 
 
 def back_kernel(rows, bound, started, *refs):
@@ -911,15 +914,19 @@
             spots, first_near, near, me, own, pieces, places, seg_own, seg_near
         )
         vec = jnp.concatenate([table, jnp.zeros((2, width), F32)], 0)
-        layer_out, grad_h1, grad_context, grads, sums, sums_bin = middle_call(
-            context, own, cotangent[0], got, vec, v_bin, step % 8 == 0
+        layer_out, grad_h1, grad_context, g_send, g_keep, sums, sums_bin = middle_call(
+            core if step % 8 == 0 else jnp.zeros_like(core), context, own, cotangent[0], got, vec, v_bin, step % 8 == 0
         )
+        level = lambda value, axes: lax.psum_scatter(value, axes, scatter_dimension=0, tiled=True)
         if step % 8:
-            grads = real_owners(grads, count, step, width)
+            pair = [v.reshape(2, 8, -1, width) for v in (g_keep, g_send)]
+            grads = real_owners(jnp.stack(pair, 1).reshape(32, -1, width), count, step, width)
             grads = grads.reshape(plan.grp // 2, 2, 4, plan.row // 4, -1, width)
             grads = grads.transpose(1, 0, 3, 2, 4, 5).reshape(count, -1, width)
-        level = lambda value, axes: lax.psum_scatter(value, axes, scatter_dimension=0, tiled=True)
-        grads = level(grads, "core")
+            g_got = level(grads, "core")
+            g_keep = jnp.zeros_like(g_got)
+        else:
+            g_got = plan.swap(g_send, plan.core[0])
         core_bit = plan.core[0]
         left = [1 << i for i in reversed(range(plan.bits)) if 1 << i != core_bit]
         parts = width // 256
@@ -927,9 +934,9 @@
             0, parts, first_near, near, grad_context, context, queries, keys_p, values_p, log_total,
             seg_own, seg_near,
         )
+        g_keep, g_got, dkp, dvp, dqp = tie(g_keep, g_got, dkp, dvp, dqp)
+        grads = level((g_keep.astype(F32) + g_got.astype(F32)).astype(BF), ("x", "y"))
         shared_p = product_call(first_near, near, dkp, dvp, squares, rows)
-        grads, shared_p, dqp = tie(grads, shared_p, dqp)
-        grads = level(grads, ("x", "y"))
         returned = Return(plan, rows)
         returned.prompt_one(shared_p)
         dkn, dvn, dq = back_call(

time: 330 us -> 339 us (1.027)
  waiting for transfers between devices: 135 us -> 123 us
  starting transfers between devices: 60.5 us -> 69.2 us
  other arithmetic: 20.2 us -> 28.1 us
    reduce_scatter x3 -> x2, waiting for transfers between devices: 19.7 us -> 2.64 us  [per_device(): lax.psum_scatter(value, axes, scatter_dimension=0, tiled=True)]
    ppermute x22 -> x23, starting transfers between devices: 53.9 us -> 62.6 us  [swap(): return lax.ppermute(value, AXES, [(i, i ^ mask) for i in range(self.count)])]
    convert_element_type x0 -> x1, other arithmetic: none -> 7.79 us  [per_device(): (g_keep.astype(F32) + g_got.astype(F32)).astype(BF)]
    ppermute x4, waiting for transfers between devices: 31 us -> 35.5 us  [send(): return lax.ppermute(value, AXES, pairs)]
    ppermute x22 -> x23, waiting for transfers between devices: 77.6 us -> 78.7 us  [swap(): return lax.ppermute(value, AXES, [(i, i ^ mask) for i in range(self.count)])]
  transfers between devices with their start and end apart: 30 -> 30, of which waited for: 17 -> 15; matrix products, arithmetic and copies ran while one was open for 8% -> 8% of each run, Pallas kernels for 18% -> 17%
where the time goes in v15:
time: 339 us; the launch traced here: 338 us
  waiting for transfers between devices  123 us (36%)
  Pallas kernels  84.1 us (25%)
  starting transfers between devices  69.2 us (20%)
  other arithmetic  28.1 us (8%)
  local copies, waits for them, and re-layouts  18.5 us (5%)
  between operations  14.3 us (4%)
    ppermute x23, waiting for transfers between devices, swap(): return lax.ppermute(value, AXES, [(i, i ^ mask) for i in range(self.count)])  78.7 us
    ppermute x23, starting transfers between devices, swap(): return lax.ppermute(value, AXES, [(i, i ^ mask) for i in range(self.count)])  62.6 us
    ppermute x4, waiting for transfers between devices, send(): return lax.ppermute(value, AXES, pairs)  35.5 us
    pallas_call x1, Pallas kernels, middle_call(): pl.pallas_call(functools.partial(middle_kernel, wide, mapped), grid=(2 *...  23.3 us
    pallas_call x1, Pallas kernels, attention_call(): pl.pallas_call(functools.partial(attention_kernel, blocks, first, rows, p...  19 us
    pallas_call x2, Pallas kernels, back_call(): pl.pallas_call(functools.partial(back_kernel, rows, bound, dq0 is not Non...  17.8 us
    pallas_call x1, Pallas kernels, weight_call(): pl.pallas_call(functools.partial(weight_kernel, blocks, first, rows, runs...  11.3 us
    pallas_call x2, Pallas kernels, product_call(): pl.pallas_call(functools.partial(product_kernel, rows, bound), grid=(tall...  10.9 us
  transfers between devices with their start and end apart: 30, of which 15 were waited for; matrix products, arithmetic and copies ran while one was open for 8% of the time, Pallas kernels for 17%

profile of v15, /device:TPU:0, one launch (start us, length us, event | category | flops | bytes accessed | tf_op | source)
XLA Modules:
  0.0 337.5 jit_solution(10640142037766223938)
XLA Ops:
  9.4 1.8 pack.1
  11.3 3.1 collective-permute-start
  14.4 2.6 collective-permute-start.1
  17.0 3.8 %collective-permute-start.3 = (bf16[256,768]{1,0:T(8,128)(2,1)}, bf16[256,768]{1,0:T(8,128)(2,1)S(1)}, u32[]{:S(2)}, u32[]{:S(2)}) collective-permute-start(bf16[256,768]{1,0:T(8,128)(2,1)} %bitcast.162), channel_id=1, source_target_pairs={{0,4},{1,5},{2,6},{3,7},{8,12},{9,13},{10,14},{11,15},{16,20},{17,... | collective-permute-start | bytes 1179656 | tf_op jit(solution)/shard_map/ppermute | solution.py:55
  20.9 1.6 collective-permute-start.4
  24.2 14.2 %collective-permute-done.3 = bf16[256,768]{1,0:T(8,128)(2,1)S(1)} collective-permute-done((bf16[256,768]{1,0:T(8,128)(2,1)}, bf16[256,768]{1,0:T(8,128)(2,1)S(1)}, u32[]{:S(2)}, u32[]{:S(2)}) %collective-permute-start.3) | collective-permute-done | bytes 393248 | tf_op jit(solution)/shard_map/ppermute | solution.py:55
  39.1 1.1 broadcast_select_fusion.refs_0_
  40.2 16.6 %collective-permute-start.7 = (bf16[256,768]{1,0:T(8,128)(2,1)S(1)}, bf16[256,768]{1,0:T(8,128)(2,1)S(1)}, u32[]{:S(2)}, u32[]{:S(2)}) collective-permute-start(bf16[256,768]{1,0:T(8,128)(2,1)S(1)} %broadcast_select_fusion.refs_0_), channel_id=1, source_target_pairs={{0,2},{1,3},{2,0},{3,1},{4,6},{5,7},{6,4},{7,5},{8,10},{9,11},{10,... | collective-permute-start | bytes 1179656 | tf_op jit(solution)/shard_map/ppermute | solution.py:51
  57.7 1.4 collective-permute-start.6
  59.8 10.9 %collective-permute-done.6 = bf16[4,40,768]{2,1,0:T(8,128)(2,1)S(1)} collective-permute-done((bf16[4,40,768]{2,1,0:T(8,128)(2,1)S(1)}, bf16[4,40,768]{2,1,0:T(8,128)(2,1)S(1)}, u32[]{:S(2)}, u32[]{:S(2)}) %collective-permute-start.6) | collective-permute-done | bytes 245792 | tf_op jit(solution)/shard_map/ppermute | solution.py:51
  70.8 4.5 %collective-permute-done.7.refs_1_ = bf16[256,768]{1,0:T(8,128)(2,1)S(1)} collective-permute-done((bf16[256,768]{1,0:T(8,128)(2,1)S(1)}, bf16[256,768]{1,0:T(8,128)(2,1)S(1)}, u32[]{:S(2)}, u32[]{:S(2)}) %collective-permute-start.7) | collective-permute-done | bytes 393248 | tf_op jit(solution)/shard_map/ppermute | solution.py:51
  75.3 1.5 collective-permute-start.13
  76.8 1.5 collective-permute-start.10
  78.4 14.7 %collective-permute-done.13 = bf16[8,40,768]{2,1,0:T(8,128)(2,1)S(1)} collective-permute-done((bf16[8,40,768]{2,1,0:T(8,128)(2,1)S(1)}, bf16[8,40,768]{2,1,0:T(8,128)(2,1)S(1)}, u32[]{:S(2)}, u32[]{:S(2)}) %collective-permute-start.13) | collective-permute-done | bytes 491552 | tf_op jit(solution)/shard_map/ppermute | solution.py:51
  93.1 2.5 collective-permute-done.10
  95.7 5.6 %collective-permute-done.11.refs_3_ = bf16[256,768]{1,0:T(8,128)(2,1)S(1)} collective-permute-done((bf16[256,768]{1,0:T(8,128)(2,1)S(1)}, bf16[256,768]{1,0:T(8,128)(2,1)S(1)}, u32[]{:S(2)}, u32[]{:S(2)}) %collective-permute-start.11) | collective-permute-done | bytes 393248 | tf_op jit(solution)/shard_map/ppermute | solution.py:51
  105.0 19.0 %attention.1 = (bf16[32,72,768]{2,1,0:T(8,128)(2,1)}, bf16[256,768]{1,0:T(8,128)(2,1)}, bf16[1024,768]{1,0:T(8,128)(2,1)}, bf16[1024,768]{1,0:T(8,128)(2,1)}, bf...) custom-call(bf16[256,768]{1,0:T(8,128)(2,1)} %copy-done.7, ...), custom_call_target="tpu_custom_call" | custom-call | flops 9865003008 | bytes 12582912 | tf_op jit(solution)/shard_map/attention/pallas_call | solution.py:342
  124.0 6.4 %all-gather.2.cloned.1.call-done = bf16[7168,768]{1,0:T(8,128)(2,1)} async-done(((bf16[224,768]{1,0:T(8,128)(2,1)}), bf16[7168,768]{1,0:T(8,128)(2,1)}) %all-gather.2.cloned.1.call-update) | async-done | bytes 11010064 | tf_op jit(solution)/shard_map/all_gather | solution.py:850
  132.6 23.3 %middle.1 = (bf16[256,768]{1,0:T(8,128)(2,1)}, f32[256,768]{1,0:T(8,128)}, bf16[256,768]{1,0:T(8,128)(2,1)}, bf16[16,216,768]{2,1,0:T(8,128)(2,1)}, bf16[16,216,...) custom-call(s32[1]{0:T(128)} %bitcast.core_ref.refs_8_, ...), custom_call_target="tpu_custom_call" | custom-call | flops 8153726976 | bytes 33554432 | tf_op jit(solution)/shard_map/middle/pallas_call | solution.py:568
  156.2 12.5 %attention_back.2 = (bf16[1024,768]{1,0:T(8,128)(2,1)}, bf16[1024,768]{1,0:T(8,128)(2,1)}, f32[768,256]{1,0:T(8,128)}) custom-call(s32[1]{0:T(128)} %bitcast.10.refs_7_.refs_0_.near_ref, bf16[256,768]{1,0:T(8,128)(2,1)} %get-tuple-element.102.refs_1_, bf16[256,768]{1,0:T(8,128)(2,1)} %get-tuple-element.99.ctx_ref.refs_2_, ...), custom_call_target="tpu_custom_call" | custom-call | flops 16106127360 | bytes 6291456 | tf_op jit(solution)/shard_map/attention_back/pallas_call | solution.py:662
  168.7 7.8 %add_convert_fusion = bf16[16,216,768]{2,1,0:T(8,128)(2,1)} fusion(bf16[16,216,768]{2,1,0:T(8,128)(2,1)} %collective-permute-done.15, bf16[16,216,768]{2,1,0:T(8,128)(2,1)} %get-tuple-element.134), kind=kLoop, calls=%fused_computation | loop fusion | flops 10616832 | bytes 15925248 | tf_op jit(solution)/shard_map/convert_element_type | solution.py:938
  178.1 6.7 %token_product.2 = bf16[4,256,768]{2,1,0:T(8,128)(2,1)} custom-call(s32[1]{0:T(128)} %bitcast.10.refs_7_.refs_0_.near_ref, bf16[1024,768]{1,0:T(8,128)(2,1)} %get-tuple-element.118.refs_13_.dk_ref, bf16[1024,768]{1,0:T(8,128)(2,1)} %get-tuple-element.119.refs_14_.dv_ref, bf16[32,72,768]{2,1,0:T(8,128)(2,1)} %get-tuple-element.116.refs_11_.wk_ref.wv_ref, ...), custom_call_target="tpu_custom_call" | custom-call | flops 2415919104 | bytes 4718592 | tf_op jit(solution)/shard_map/token_product/pallas_call | solution.py:700
  184.8 1.2 slice_bitcast_fusion
  187.0 1.1 collective-permute-start.17
  188.1 5.3 %attention_back.3 = (bf16[768,768]{1,0:T(8,128)(2,1)}, bf16[768,768]{1,0:T(8,128)(2,1)}, f32[768,256]{1,0:T(8,128)}) custom-call(s32[1]{0:T(128)} %bitcast.10.refs_7_.refs_0_.near_ref, bf16[256,768]{1,0:T(8,128)(2,1)} %get-tuple-element.102.refs_1_, bf16[256,768]{1,0:T(8,128)(2,1)} %get-tuple-element.99.ctx_ref.refs_2_, ...), custom_call_target="tpu_custom_call" | custom-call | flops 12079595520 | bytes 4718592 | tf_op jit(solution)/shard_map/attention_back/pallas_call | solution.py:662
  193.3 11.3 %weight_product.1 = (bf16[16,72,768]{2,1,0:T(8,128)(2,1)}, bf16[16,72,768]{2,1,0:T(8,128)(2,1)}, f32[256,768]{1,0:T(8,128)}, f32[8,768]{1,0:T(8,128)}) custom-call(bf16[256,768]{1,0:T(8,128)(2,1)} %copy-done.7, bf16[256,768]{1,0:T(8,128)(2,1)} %copy-done.13, bf16[256,768]{1,0:T(8,128)(2,1)} %copy-done.14, bf16[256,768]{1,0:T(8,128)(2,1)} %copy-done.15, ...), custom_call_target="tpu_custom_call" | custom-call | flops 4227858432 | bytes 16515072 | tf_op jit(solution)/shard_map/weight_product/pallas_call | solution.py:779
  206.2 2.2 fusion.1
  208.4 1.5 pad_maximum_fusion.1
  210.6 1.6 pad_maximum_fusion
  212.2 2.0 collective-permute-done.19
  214.2 2.4 add_convert_fusion.1
  216.6 1.2 collective-permute-start.20
  217.7 12.5 %collective-permute-done.18 = bf16[256,768]{1,0:T(8,128)(2,1)S(1)} collective-permute-done((bf16[256,768]{1,0:T(8,128)(2,1)}, bf16[256,768]{1,0:T(8,128)(2,1)S(1)}, u32[]{:S(2)}, u32[]{:S(2)}) %collective-permute-start.18) | collective-permute-done | bytes 393248 | tf_op jit(solution)/shard_map/ppermute | solution.py:51
  230.4 1.3 collective-permute-start.21
  231.7 4.2 %token_product.3 = bf16[3,256,768]{2,1,0:T(8,128)(2,1)} custom-call(s32[1]{0:T(128)} %bitcast.10.refs_7_.refs_0_.near_ref, bf16[768,768]{1,0:T(8,128)(2,1)} %get-tuple-element.136.refs_15_.dk_ref, bf16[768,768]{1,0:T(8,128)(2,1)} %get-tuple-element.137.refs_16_.dv_ref, bf16[32,72,768]{2,1,0:T(8,128)(2,1)} %get-tuple-element.116.refs_11_.wk_ref.wv_ref, ...), custom_call_target="tpu_custom_call" | custom-call | flops 1811939328 | bytes 3538944 | tf_op jit(solution)/shard_map/token_product/pallas_call | solution.py:700
  235.9 2.2 constant_dynamic-slice_fusion.4
  239.2 21.3 %collective-permute-done.21 = bf16[256,768]{1,0:T(8,128)(2,1)} collective-permute-done((bf16[256,768]{1,0:T(8,128)(2,1)S(1)}, bf16[256,768]{1,0:T(8,128)(2,1)}, u32[]{:S(2)}, u32[]{:S(2)}) %collective-permute-start.21) | collective-permute-done | bytes 393248 | tf_op jit(solution)/shard_map/ppermute | solution.py:55
  260.4 2.6 reduce-scatter.3.cloned.1.call-done
  263.1 2.4 fusion.3
  265.4 1.5 collective-permute-start.22
  266.9 1.2 dynamic-slice_bitcast_fusion
  268.4 10.5 %collective-permute-done.22 = bf16[4,80,768]{2,1,0:T(8,128)(2,1)} collective-permute-done((bf16[4,80,768]{2,1,0:T(8,128)(2,1)}, bf16[4,80,768]{2,1,0:T(8,128)(2,1)}, u32[]{:S(2)}, u32[]{:S(2)}) %collective-permute-start.22) | collective-permute-done | bytes 491552 | tf_op jit(solution)/shard_map/ppermute | solution.py:51
  279.0 1.5 collective-permute-start.24
  281.2 1.1 add_convert_fusion.4
  282.3 11.3 %collective-permute-start.23 = (bf16[2,80,768]{2,1,0:T(8,128)(2,1)S(1)}, bf16[2,80,768]{2,1,0:T(8,128)(2,1)S(1)}, u32[]{:S(2)}, u32[]{:S(2)}) collective-permute-start(bf16[2,80,768]{2,1,0:T(8,128)(2,1)S(1)} %bitcast.171), channel_id=1, source_target_pairs={{0,4},{1,5},{2,6},{3,7},{4,0},{5,1},{6,2},{7,3},{8,12},{9,13},{10,... | collective-permute-start | bytes 737288 | tf_op jit(solution)/shard_map/ppermute | solution.py:51
  294.8 13.8 %collective-permute-done.23 = bf16[2,80,768]{2,1,0:T(8,128)(2,1)S(1)} collective-permute-done((bf16[2,80,768]{2,1,0:T(8,128)(2,1)S(1)}, bf16[2,80,768]{2,1,0:T(8,128)(2,1)S(1)}, u32[]{:S(2)}, u32[]{:S(2)}) %collective-permute-start.23) | collective-permute-done | bytes 245792 | tf_op jit(solution)/shard_map/ppermute | solution.py:51
  308.8 14.2 %collective-permute-start.26 = (bf16[1,80,768]{2,1,0:T(8,128)(2,1)S(1)}, bf16[1,80,768]{2,1,0:T(8,128)(2,1)S(1)}, u32[]{:S(2)}, u32[]{:S(2)}) collective-permute-start(bf16[1,80,768]{2,1,0:T(8,128)(2,1)S(1)} %add_convert_fusion.5), channel_id=1, source_target_pairs={{0,2},{1,3},{2,0},{3,1},{4,6},{5,7},{6,4},{7,5},{8,10},{9,11},{10,... | collective-permute-start | bytes 368648 | tf_op jit(solution)/shard_map/ppermute | solution.py:51
  323.0 2.0 fusion.4
  (137 shorter events, 26.9 us)
Async XLA Ops:
  7.2 123.2 %all-gather.2.cloned.1.call-start = ((), (), s32[]{:S(2)}) async-start(), calls=%async_computation.2 | async-start | bytes 11354112 | tf_op jit(solution)/shard_map/all_gather | solution.py:850
  11.3 251.8 %reduce-scatter.3.cloned.1.call-start = ((), (), s32[]{:S(2)}) async-start(), calls=%async_computation.3 | async-start | bytes 6635520 | tf_op jit(solution)/shard_map/reduce_scatter | solution.py:920
  11.3 28.8 %collective-permute-start = (bf16[80,768]{1,0:T(8,128)(2,1)}, bf16[80,768]{1,0:T(8,128)(2,1)S(1)}, u32[]{:S(2)}, u32[]{:S(2)}) collective-permute-start(bf16[80,768]{1,0:T(8,128)(2,1)} %get-tuple-element.86), channel_id=1, source_target_pairs={{0,2},{1,3},{2,0},{3,1},{4,6},{5,7},{6,4},{7,5},{8,10},{9,11},{10,... | collective-permute-start | bytes 368648 | tf_op jit(solution)/shard_map/ppermute | solution.py:51
  14.4 25.8 %collective-permute-start.1 = (bf16[80,768]{1,0:T(8,128)(2,1)}, bf16[80,768]{1,0:T(8,128)(2,1)S(1)}, u32[]{:S(2)}, u32[]{:S(2)}) collective-permute-start(bf16[80,768]{1,0:T(8,128)(2,1)} %get-tuple-element.86), channel_id=1, source_target_pairs={{0,4},{1,5},{2,6},{3,7},{4,0},{5,1},{6,2},{7,3},{8,12},{9,13},{10,... | collective-permute-start | bytes 368648 | tf_op jit(solution)/shard_map/ppermute | solution.py:51
  17.0 23.2 %collective-permute-start.2 = (bf16[80,768]{1,0:T(8,128)(2,1)}, bf16[80,768]{1,0:T(8,128)(2,1)S(1)}, u32[]{:S(2)}, u32[]{:S(2)}) collective-permute-start(bf16[80,768]{1,0:T(8,128)(2,1)} %get-tuple-element.86), channel_id=1, source_target_pairs={{0,6},{1,7},{2,4},{3,5},{4,2},{5,3},{6,0},{7,1},{8,14},{9,15},{10,... | collective-permute-start | bytes 368648 | tf_op jit(solution)/shard_map/ppermute | solution.py:51
  17.0 21.4 %collective-permute-start.3 = (bf16[256,768]{1,0:T(8,128)(2,1)}, bf16[256,768]{1,0:T(8,128)(2,1)S(1)}, u32[]{:S(2)}, u32[]{:S(2)}) collective-permute-start(bf16[256,768]{1,0:T(8,128)(2,1)} %bitcast.162), channel_id=1, source_target_pairs={{0,4},{1,5},{2,6},{3,7},{8,12},{9,13},{10,14},{11,15},{16,20},{17,... | collective-permute-start | bytes 1179656 | tf_op jit(solution)/shard_map/ppermute | solution.py:55
  20.9 19.4 %collective-permute-start.4 = (bf16[256,768]{1,0:T(8,128)(2,1)}, bf16[256,768]{1,0:T(8,128)(2,1)S(1)}, u32[]{:S(2)}, u32[]{:S(2)}) collective-permute-start(bf16[256,768]{1,0:T(8,128)(2,1)} %bitcast.163), channel_id=1, source_target_pairs={{0,1},{1,0},{2,3},{3,2},{4,5},{5,4},{6,7},{7,6},{8,9},{9,8},{10,11... | collective-permute-start | bytes 1179656 | tf_op jit(solution)/shard_map/ppermute | solution.py:51
  38.4 32.3 %collective-permute-start.9 = (bf16[256,768]{1,0:T(8,128)(2,1)}, bf16[256,768]{1,0:T(8,128)(2,1)S(1)}, u32[]{:S(2)}, u32[]{:S(2)}) collective-permute-start(bf16[256,768]{1,0:T(8,128)(2,1)} %bitcast.164), channel_id=1, source_target_pairs={{5,6},{6,5},{13,14},{14,13},{21,22},{22,21},{29,30},{30,29}} | collective-permute-start | bytes 1179656 | tf_op jit(solution)/shard_map/ppermute | solution.py:55
  40.2 38.2 %copy-start.7 = (bf16[256,768]{1,0:T(8,128)(2,1)}, bf16[256,768]{1,0:T(8,128)(2,1)S(1)}, u32[]{:S(2)}) copy-start(bf16[256,768]{1,0:T(8,128)(2,1)S(1)} %broadcast_select_fusion.refs_0_) | copy-start | bytes 1179652
  40.2 38.1 %copy-start.11 = (bf16[256,768]{1,0:T(8,128)(2,1)}, bf16[256,768]{1,0:T(8,128)(2,1)S(1)}, u32[]{:S(2)}) copy-start(bf16[256,768]{1,0:T(8,128)(2,1)S(1)} %collective-permute-done.4.refs_5_) | copy-start | bytes 1179652
  40.2 35.0 %collective-permute-start.7 = (bf16[256,768]{1,0:T(8,128)(2,1)S(1)}, bf16[256,768]{1,0:T(8,128)(2,1)S(1)}, u32[]{:S(2)}, u32[]{:S(2)}) collective-permute-start(bf16[256,768]{1,0:T(8,128)(2,1)S(1)} %broadcast_select_fusion.refs_0_), channel_id=1, source_target_pairs={{0,2},{1,3},{2,0},{3,1},{4,6},{5,7},{6,4},{7,5},{8,10},{9,11},{10,... | collective-permute-start | bytes 1179656 | tf_op jit(solution)/shard_map/ppermute | solution.py:51
  56.9 18.4 %collective-permute-start.8 = (bf16[256,768]{1,0:T(8,128)(2,1)S(1)}, bf16[256,768]{1,0:T(8,128)(2,1)S(1)}, u32[]{:S(2)}, u32[]{:S(2)}) collective-permute-start(bf16[256,768]{1,0:T(8,128)(2,1)S(1)} %broadcast_select_fusion.refs_0_), channel_id=1, source_target_pairs={{0,1},{1,0},{2,3},{3,2},{4,5},{5,4},{6,7},{7,6},{8,9},{9,8},{10,11... | collective-permute-start | bytes 1179656 | tf_op jit(solution)/shard_map/ppermute | solution.py:51
  57.7 13.0 %collective-permute-start.6 = (bf16[4,40,768]{2,1,0:T(8,128)(2,1)S(1)}, bf16[4,40,768]{2,1,0:T(8,128)(2,1)S(1)}, u32[]{:S(2)}, u32[]{:S(2)}) collective-permute-start(bf16[4,40,768]{2,1,0:T(8,128)(2,1)S(1)} %pad_maximum_fusion.5), channel_id=1, source_target_pairs={{0,1},{1,0},{2,3},{3,2},{4,5},{5,4},{6,7},{7,6},{8,9},{9,8},{10,11... | collective-permute-start | bytes 737288 | tf_op jit(solution)/shard_map/ppermute | solution.py:51
  59.1 11.6 %collective-permute-start.5 = (bf16[4,40,768]{2,1,0:T(8,128)(2,1)S(1)}, bf16[4,40,768]{2,1,0:T(8,128)(2,1)S(1)}, u32[]{:S(2)}, u32[]{:S(2)}) collective-permute-start(bf16[4,40,768]{2,1,0:T(8,128)(2,1)S(1)} %pad_maximum_fusion.4), channel_id=1, source_target_pairs={{0,16},{1,17},{2,18},{3,19},{4,20},{5,21},{6,22},{7,23},{8,24},{9,... | collective-permute-start | bytes 737288 | tf_op jit(solution)/shard_map/ppermute | solution.py:51
  70.7 31.4 %copy-start.16 = (s32[1,8]{1,0:T(1,128)S(1)}, s32[1,8]{1,0:T(1,128)}, u32[]{:S(2)}) copy-start(s32[1,8]{1,0:T(1,128)} %param.19) | copy-start | bytes 100
  70.8 4.5 %copy-start.12 = (bf16[256,768]{1,0:T(8,128)(2,1)}, bf16[256,768]{1,0:T(8,128)(2,1)S(1)}, u32[]{:S(2)}) copy-start(bf16[256,768]{1,0:T(8,128)(2,1)S(1)} %collective-permute-done.9.refs_6_) | copy-start | bytes 1179652
  75.3 3.0 copy-start.13
  75.3 20.4 %copy-start.14 = (bf16[256,768]{1,0:T(8,128)(2,1)}, bf16[256,768]{1,0:T(8,128)(2,1)S(1)}, u32[]{:S(2)}) copy-start(bf16[256,768]{1,0:T(8,128)(2,1)S(1)} %collective-permute-done.8.refs_2_) | copy-start | bytes 1179652
  75.3 17.7 %collective-permute-start.13 = (bf16[8,40,768]{2,1,0:T(8,128)(2,1)S(1)}, bf16[8,40,768]{2,1,0:T(8,128)(2,1)S(1)}, u32[]{:S(2)}, u32[]{:S(2)}) collective-permute-start(bf16[8,40,768]{2,1,0:T(8,128)(2,1)S(1)} %constant_dynamic-update-slice_fusion.5), channel_id=1, source_target_pairs={{0,16},{1,17},{2,18},{3,19},{4,20},{5,21},{6,22},{7,23},{8,24},{9,... | collective-permute-start | bytes 1474568 | tf_op jit(solution)/shard_map/ppermute | solution.py:51
  76.8 18.8 %collective-permute-start.10 = (bf16[8,40,768]{2,1,0:T(8,128)(2,1)S(1)}, bf16[8,40,768]{2,1,0:T(8,128)(2,1)S(1)}, u32[]{:S(2)}, u32[]{:S(2)}) collective-permute-start(bf16[8,40,768]{2,1,0:T(8,128)(2,1)S(1)} %constant_dynamic-update-slice_fusion), channel_id=1, source_target_pairs={{0,1},{1,0},{2,3},{3,2},{4,5},{5,4},{6,7},{7,6},{8,9},{9,8},{10,11... | collective-permute-start | bytes 1474568 | tf_op jit(solution)/shard_map/ppermute | solution.py:51
  78.3 23.0 %collective-permute-start.11 = (bf16[256,768]{1,0:T(8,128)(2,1)S(1)}, bf16[256,768]{1,0:T(8,128)(2,1)S(1)}, u32[]{:S(2)}, u32[]{:S(2)}) collective-permute-start(bf16[256,768]{1,0:T(8,128)(2,1)S(1)} %collective-permute-done.8.refs_2_), channel_id=1, source_target_pairs={{0,2},{1,3},{2,0},{3,1},{4,6},{5,7},{6,4},{7,5},{8,10},{9,11},{10,... | collective-permute-start | bytes 1179656 | tf_op jit(solution)/shard_map/ppermute | solution.py:51
  93.0 11.7 %copy-start.8 = (bf16[16,40,768]{2,1,0:T(8,128)(2,1)}, bf16[16,40,768]{2,1,0:T(8,128)(2,1)S(1)}, u32[]{:S(2)}) copy-start(bf16[16,40,768]{2,1,0:T(8,128)(2,1)S(1)} %constant_dynamic-update-slice_fusion.10.refs_12_) | copy-start | bytes 2949124
  93.1 10.9 %collective-permute-start.14 = (bf16[16,40,768]{2,1,0:T(8,128)(2,1)S(1)}, bf16[16,40,768]{2,1,0:T(8,128)(2,1)S(1)}, u32[]{:S(2)}, u32[]{:S(2)}) collective-permute-start(bf16[16,40,768]{2,1,0:T(8,128)(2,1)S(1)} %constant_dynamic-update-slice_fusion.10.refs_12_), channel_id=1, source_target_pairs={{0,8},{1,9},{2,10},{3,11},{4,12},{5,13},{6,14},{7,15},{8,0},{9,1},... | collective-permute-start | bytes 2949128 | tf_op jit(solution)/shard_map/ppermute | solution.py:51
  95.7 9.1 %copy-start.5 = (bf16[16,40,768]{2,1,0:T(8,128)(2,1)}, bf16[16,40,768]{2,1,0:T(8,128)(2,1)S(1)}, u32[]{:S(2)}) copy-start(bf16[16,40,768]{2,1,0:T(8,128)(2,1)S(1)} %pad_maximum_fusion.2.refs_10_) | copy-start | bytes 2949124
  101.3 0.8 copy-start.15
  102.1 2.7 collective-permute-start.12
  104.0 1.0 copy-start.10
  155.9 12.9 %collective-permute-start.15 = (bf16[16,216,768]{2,1,0:T(8,128)(2,1)}, bf16[16,216,768]{2,1,0:T(8,128)(2,1)}, u32[]{:S(2)}, u32[]{:S(2)}) collective-permute-start(bf16[16,216,768]{2,1,0:T(8,128)(2,1)} %get-tuple-element.108), channel_id=1, source_target_pairs={{0,8},{1,9},{2,10},{3,11},{4,12},{5,13},{6,14},{7,15},{8,0},{9,1},... | collective-permute-start | bytes 15925256 | tf_op jit(solution)/shard_map/ppermute | solution.py:51
  176.5 0.7 copy-start.9
  176.6 151.3 %reduce-scatter.5.cloned.1.call-start = ((), (), s32[]{:S(2)}) async-start(), calls=%async_computation.4 | async-start | bytes 1658880 | tf_op jit(solution)/shard_map/reduce_scatter | solution.py:920
  186.0 20.1 %collective-permute-start.16 = (bf16[256,768]{1,0:T(8,128)(2,1)S(1)}, bf16[256,768]{1,0:T(8,128)(2,1)S(1)}, u32[]{:S(2)}, u32[]{:S(2)}) collective-permute-start(bf16[256,768]{1,0:T(8,128)(2,1)S(1)} %get-tuple-element.158), channel_id=1, source_target_pairs={{0,2},{1,3},{2,0},{3,1},{4,6},{5,7},{6,4},{7,5},{8,10},{9,11},{10,... | collective-permute-start | bytes 1179656 | tf_op jit(solution)/shard_map/ppermute | solution.py:51
  187.0 19.1 %collective-permute-start.17 = (bf16[256,768]{1,0:T(8,128)(2,1)S(1)}, bf16[256,768]{1,0:T(8,128)(2,1)}, u32[]{:S(2)}, u32[]{:S(2)}) collective-permute-start(bf16[256,768]{1,0:T(8,128)(2,1)S(1)} %get-tuple-element.157), channel_id=1, source_target_pairs={{0,2},{1,3},{2,0},{3,1},{4,6},{5,7},{6,4},{7,5},{8,10},{9,11},{10,... | collective-permute-start | bytes 1179656 | tf_op jit(solution)/shard_map/ppermute | solution.py:51
  204.6 1.5 copy-start
  206.0 2.4 copy-start.4
  209.8 4.3 %collective-permute-start.19 = (bf16[16,80,768]{2,1,0:T(8,128)(2,1)}, bf16[16,80,768]{2,1,0:T(8,128)(2,1)}, u32[]{:S(2)}, u32[]{:S(2)}) collective-permute-start(bf16[16,80,768]{2,1,0:T(8,128)(2,1)} %pad_maximum_fusion.1), channel_id=1, source_target_pairs={{0,8},{1,9},{2,10},{3,11},{4,12},{5,13},{6,14},{7,15},{8,0},{9,1},... | collective-permute-start | bytes 5898248 | tf_op jit(solution)/shard_map/ppermute | solution.py:51
  209.8 20.4 %collective-permute-start.18 = (bf16[256,768]{1,0:T(8,128)(2,1)}, bf16[256,768]{1,0:T(8,128)(2,1)S(1)}, u32[]{:S(2)}, u32[]{:S(2)}) collective-permute-start(bf16[256,768]{1,0:T(8,128)(2,1)} %get-tuple-element.126), channel_id=1, source_target_pairs={{0,1},{1,0},{2,3},{3,2},{4,5},{5,4},{6,7},{7,6},{8,9},{9,8},{10,11... | collective-permute-start | bytes 1179656 | tf_op jit(solution)/shard_map/ppermute | solution.py:51
  216.6 43.9 %collective-permute-start.20 = (bf16[8,80,768]{2,1,0:T(8,128)(2,1)}, bf16[8,80,768]{2,1,0:T(8,128)(2,1)}, u32[]{:S(2)}, u32[]{:S(2)}) collective-permute-start(bf16[8,80,768]{2,1,0:T(8,128)(2,1)} %bitcast.33), channel_id=1, source_target_pairs={{0,16},{1,17},{2,18},{3,19},{4,20},{5,21},{6,22},{7,23},{8,24},{9,... | collective-permute-start | bytes 2949128 | tf_op jit(solution)/shard_map/ppermute | solution.py:51
  230.4 30.1 %collective-permute-start.21 = (bf16[256,768]{1,0:T(8,128)(2,1)S(1)}, bf16[256,768]{1,0:T(8,128)(2,1)}, u32[]{:S(2)}, u32[]{:S(2)}) collective-permute-start(bf16[256,768]{1,0:T(8,128)(2,1)S(1)} %fusion.2), channel_id=1, source_target_pairs={{4,0},{5,1},{6,2},{7,3},{12,8},{13,9},{14,10},{15,11},{20,16},{21,... | collective-permute-start | bytes 1179656 | tf_op jit(solution)/shard_map/ppermute | solution.py:55
  263.1 5.1 %copy-start.2 = (bf16[1,1,640,768]{3,2,1,0:T(8,128)(2,1)S(1)}, bf16[1,1,640,768]{3,2,1,0:T(8,128)(2,1)}, u32[]{:S(2)}) copy-start(bf16[1,1,640,768]{3,2,1,0:T(8,128)(2,1)} %constant_dynamic-slice_fusion.4) | copy-start | bytes 2949124
  265.4 13.5 %collective-permute-start.22 = (bf16[4,80,768]{2,1,0:T(8,128)(2,1)}, bf16[4,80,768]{2,1,0:T(8,128)(2,1)}, u32[]{:S(2)}, u32[]{:S(2)}) collective-permute-start(bf16[4,80,768]{2,1,0:T(8,128)(2,1)} %fusion.3), channel_id=1, source_target_pairs={{0,1},{1,0},{2,3},{3,2},{4,5},{5,4},{6,7},{7,6},{8,9},{9,8},{10,11... | collective-permute-start | bytes 1474568 | tf_op jit(solution)/shard_map/ppermute | solution.py:51
  266.9 12.0 %copy-start.1 = (bf16[3,256,768]{2,1,0:T(8,128)(2,1)S(1)}, bf16[3,256,768]{2,1,0:T(8,128)(2,1)}, u32[]{:S(2)}) copy-start(bf16[3,256,768]{2,1,0:T(8,128)(2,1)} %token_product.3) | copy-start | bytes 3538948
  266.9 1.4 copy-start.3
  279.0 15.7 %collective-permute-start.24 = (bf16[256,768]{1,0:T(8,128)(2,1)S(1)}, bf16[256,768]{1,0:T(8,128)(2,1)S(1)}, u32[]{:S(2)}, u32[]{:S(2)}) collective-permute-start(bf16[256,768]{1,0:T(8,128)(2,1)S(1)} %get-tuple-element.159), channel_id=1, source_target_pairs={{0,1},{1,0},{2,3},{3,2},{4,5},{5,4},{6,7},{7,6},{8,9},{9,8},{10,11... | collective-permute-start | bytes 1179656 | tf_op jit(solution)/shard_map/ppermute | solution.py:51
  280.5 14.2 %collective-permute-start.25 = (bf16[256,768]{1,0:T(8,128)(2,1)S(1)}, bf16[256,768]{1,0:T(8,128)(2,1)S(1)}, u32[]{:S(2)}, u32[]{:S(2)}) collective-permute-start(bf16[256,768]{1,0:T(8,128)(2,1)S(1)} %get-tuple-element.160), channel_id=1, source_target_pairs={{5,6},{6,5},{13,14},{14,13},{21,22},{22,21},{29,30},{30,29}} | collective-permute-start | bytes 1179656 | tf_op jit(solution)/shard_map/ppermute | solution.py:55
  282.3 26.4 %collective-permute-start.23 = (bf16[2,80,768]{2,1,0:T(8,128)(2,1)S(1)}, bf16[2,80,768]{2,1,0:T(8,128)(2,1)S(1)}, u32[]{:S(2)}, u32[]{:S(2)}) collective-permute-start(bf16[2,80,768]{2,1,0:T(8,128)(2,1)S(1)} %bitcast.171), channel_id=1, source_target_pairs={{0,4},{1,5},{2,6},{3,7},{4,0},{5,1},{6,2},{7,3},{8,12},{9,13},{10,... | collective-permute-start | bytes 737288 | tf_op jit(solution)/shard_map/ppermute | solution.py:51
  294.6 28.4 %copy-start.6 = (f32[256,768]{1,0:T(8,128)S(1)}, f32[256,768]{1,0:T(8,128)}, u32[]{:S(2)}) copy-start(f32[256,768]{1,0:T(8,128)} %get-tuple-element.122) | copy-start | bytes 2359300
  308.8 17.1 %collective-permute-start.26 = (bf16[1,80,768]{2,1,0:T(8,128)(2,1)S(1)}, bf16[1,80,768]{2,1,0:T(8,128)(2,1)S(1)}, u32[]{:S(2)}, u32[]{:S(2)}) collective-permute-start(bf16[1,80,768]{2,1,0:T(8,128)(2,1)S(1)} %add_convert_fusion.5), channel_id=1, source_target_pairs={{0,2},{1,3},{2,0},{3,1},{4,6},{5,7},{6,4},{7,5},{8,10},{9,11},{10,... | collective-permute-start | bytes 368648 | tf_op jit(solution)/shard_map/ppermute | solution.py:51
Sparse Core Ops, SparseCore 0:
  11.5 118.8 all-gather.1
  176.7 86.3 reduce-scatter.2
  267.1 54.6 reduce-scatter.4

commit v16 on v14

--- a/solution.py
+++ b/solution.py
@@ -79,6 +79,22 @@
         here = [self.cut(t, bit, place) for t in self.terms]
         self.left = [b for b in self.left if b != bit]
         self.terms = here + [self.plan.swap(away, bit)]
+
+    def stage_direct(self, bits):
+        masks = [0]
+        for bit in bits:
+            masks = masks + [m ^ bit for m in masks]
+        me, left = self.plan.me(), self.left
+        parts = []
+        for mask in masks:
+            terms, self.left = self.terms, left
+            for bit in bits:
+                place = ((me ^ mask) // bit) & 1
+                terms = [self.cut(t, bit, place) for t in terms]
+                self.left = [b for b in self.left if b != bit]
+            parts.append(terms)
+        away = [self.total(p).astype(BF) for p in parts[1:]]
+        self.terms = parts[0] + [self.plan.swap(v, m) for v, m in zip(away, masks[1:])]
 
     def result(self):
         return self.total(self.terms)[0]
@@ -965,7 +981,7 @@
         send = jnp.concatenate([send, pick.cut(d_lines, core_bit, 1 - place)], 1)
         keep = jnp.concatenate([keep, pick.cut(d_lines, core_bit, place)], 1)
         reduce = Reduce(plan, [keep, plan.swap(send, core_bit)], left)
-        for bit in plan.x + plan.y + plan.z[::-1]:
+        for bit in plan.x + plan.y:
             held = reduce.terms
             if bit == plan.x[0]:
                 held = tie(*held)
@@ -973,13 +989,12 @@
             elif bit == plan.y[0]:
                 *held, grads, shared_n, returned.back = tie(*held, grads, shared_n, returned.back)
                 grads = level(grads, "z")
-            elif bit == plan.z[-1]:
-                *held, shared_n = tie(*held, shared_n)
-                returned.near(shared_n)
-            elif bit == plan.z[0]:
-                *held, returned.own = tie(*held, returned.own)
             reduce.terms = list(held)
             reduce.stage(bit)
+        *held, shared_n = tie(*reduce.terms, shared_n)
+        reduce.terms = list(held)
+        returned.near(shared_n)
+        reduce.stage_direct(plan.z)
         o_ab = grads.reshape(-1, width).astype(F32)
         grad_tokens = grad_own + returned.total()
         o_first = reduce.result()

time: 330 us -> 324 us (0.982)
  starting transfers between devices: 60.5 us -> 49.4 us
  waiting for transfers between devices: 135 us -> 139 us
    ppermute x22 -> x23, starting transfers between devices: 53.9 us -> 42.8 us  [swap(): return lax.ppermute(value, AXES, [(i, i ^ mask) for i in range(self.count)])]
    reduce_scatter x3, waiting for transfers between devices: 19.7 us -> 23.7 us  [per_device(): lax.psum_scatter(value, axes, scatter_dimension=0, tiled=True)]
    ppermute x22 -> x23, waiting for transfers between devices: 77.6 us -> 78.3 us  [swap(): return lax.ppermute(value, AXES, [(i, i ^ mask) for i in range(self.count)])]
  transfers between devices with their start and end apart: 30 -> 31, of which waited for: 17 -> 18; matrix products, arithmetic and copies ran while one was open for 8% -> 8% of each run, Pallas kernels for 18% -> 18%
where the time goes in v16:
time: 324 us; the launch traced here: 321 us
  waiting for transfers between devices  139 us (43%)
  Pallas kernels  81.7 us (25%)
  starting transfers between devices  49.4 us (15%)
  other arithmetic  20.4 us (6%)
  local copies, waits for them, and re-layouts  15.9 us (5%)
  between operations  14.3 us (4%)
    ppermute x23, waiting for transfers between devices, swap(): return lax.ppermute(value, AXES, [(i, i ^ mask) for i in range(self.count)])  78.3 us
    ppermute x23, starting transfers between devices, swap(): return lax.ppermute(value, AXES, [(i, i ^ mask) for i in range(self.count)])  42.8 us
    ppermute x4, waiting for transfers between devices, send(): return lax.ppermute(value, AXES, pairs)  30.8 us
    reduce_scatter x3, waiting for transfers between devices, per_device(): lax.psum_scatter(value, axes, scatter_dimension=0, tiled=True)  23.7 us
    pallas_call x1, Pallas kernels, middle_call(): pl.pallas_call(functools.partial(middle_kernel, wide, mapped), grid=(2 *...  20.8 us
    pallas_call x1, Pallas kernels, attention_call(): pl.pallas_call(functools.partial(attention_kernel, blocks, first, rows, p...  19.1 us
    pallas_call x2, Pallas kernels, back_call(): pl.pallas_call(functools.partial(back_kernel, rows, bound, dq0 is not Non...  17.9 us
    pallas_call x1, Pallas kernels, weight_call(): pl.pallas_call(functools.partial(weight_kernel, blocks, first, rows, runs...  11.4 us
  transfers between devices with their start and end apart: 31, of which 18 were waited for; matrix products, arithmetic and copies ran while one was open for 8% of the time, Pallas kernels for 18%

profile of v16, /device:TPU:0, one launch (start us, length us, event | category | flops | bytes accessed | tf_op | source)
XLA Modules:
  0.0 320.9 jit_solution(610631789388821633)
XLA Ops:
  9.4 1.8 pack.1
  11.3 3.1 collective-permute-start
  14.4 2.6 collective-permute-start.1
  17.0 3.8 %collective-permute-start.3 = (bf16[256,768]{1,0:T(8,128)(2,1)}, bf16[256,768]{1,0:T(8,128)(2,1)S(1)}, u32[]{:S(2)}, u32[]{:S(2)}) collective-permute-start(bf16[256,768]{1,0:T(8,128)(2,1)} %bitcast.157), channel_id=1, source_target_pairs={{0,4},{1,5},{2,6},{3,7},{8,12},{9,13},{10,14},{11,15},{16,20},{17,... | collective-permute-start | bytes 1179656 | tf_op jit(solution)/shard_map/ppermute | solution.py:55
  20.9 1.6 collective-permute-start.4
  24.2 14.2 %collective-permute-done.3 = bf16[256,768]{1,0:T(8,128)(2,1)S(1)} collective-permute-done((bf16[256,768]{1,0:T(8,128)(2,1)}, bf16[256,768]{1,0:T(8,128)(2,1)S(1)}, u32[]{:S(2)}, u32[]{:S(2)}) %collective-permute-start.3) | collective-permute-done | bytes 393248 | tf_op jit(solution)/shard_map/ppermute | solution.py:55
  40.2 16.6 %collective-permute-start.7 = (bf16[256,768]{1,0:T(8,128)(2,1)S(1)}, bf16[256,768]{1,0:T(8,128)(2,1)S(1)}, u32[]{:S(2)}, u32[]{:S(2)}) collective-permute-start(bf16[256,768]{1,0:T(8,128)(2,1)S(1)} %broadcast_select_fusion.refs_0_), channel_id=1, source_target_pairs={{0,2},{1,3},{2,0},{3,1},{4,6},{5,7},{6,4},{7,5},{8,10},{9,11},{10,... | collective-permute-start | bytes 1179656 | tf_op jit(solution)/shard_map/ppermute | solution.py:51
  57.7 1.4 collective-permute-start.6
  59.8 10.9 %collective-permute-done.6 = bf16[4,40,768]{2,1,0:T(8,128)(2,1)S(1)} collective-permute-done((bf16[4,40,768]{2,1,0:T(8,128)(2,1)S(1)}, bf16[4,40,768]{2,1,0:T(8,128)(2,1)S(1)}, u32[]{:S(2)}, u32[]{:S(2)}) %collective-permute-start.6) | collective-permute-done | bytes 245792 | tf_op jit(solution)/shard_map/ppermute | solution.py:51
  70.8 4.5 %collective-permute-done.7.refs_1_ = bf16[256,768]{1,0:T(8,128)(2,1)S(1)} collective-permute-done((bf16[256,768]{1,0:T(8,128)(2,1)S(1)}, bf16[256,768]{1,0:T(8,128)(2,1)S(1)}, u32[]{:S(2)}, u32[]{:S(2)}) %collective-permute-start.7) | collective-permute-done | bytes 393248 | tf_op jit(solution)/shard_map/ppermute | solution.py:51
  75.3 1.5 collective-permute-start.13
  76.8 1.5 collective-permute-start.10
  78.3 14.6 %collective-permute-done.13 = bf16[8,40,768]{2,1,0:T(8,128)(2,1)S(1)} collective-permute-done((bf16[8,40,768]{2,1,0:T(8,128)(2,1)S(1)}, bf16[8,40,768]{2,1,0:T(8,128)(2,1)S(1)}, u32[]{:S(2)}, u32[]{:S(2)}) %collective-permute-start.13) | collective-permute-done | bytes 491552 | tf_op jit(solution)/shard_map/ppermute | solution.py:51
  93.1 2.5 collective-permute-done.10
  95.7 5.6 %collective-permute-done.11.refs_3_ = bf16[256,768]{1,0:T(8,128)(2,1)S(1)} collective-permute-done((bf16[256,768]{1,0:T(8,128)(2,1)S(1)}, bf16[256,768]{1,0:T(8,128)(2,1)S(1)}, u32[]{:S(2)}, u32[]{:S(2)}) %collective-permute-start.11) | collective-permute-done | bytes 393248 | tf_op jit(solution)/shard_map/ppermute | solution.py:51
  104.9 19.1 %attention.1 = (bf16[32,72,768]{2,1,0:T(8,128)(2,1)}, bf16[256,768]{1,0:T(8,128)(2,1)}, bf16[1024,768]{1,0:T(8,128)(2,1)}, bf16[1024,768]{1,0:T(8,128)(2,1)}, bf...) custom-call(bf16[256,768]{1,0:T(8,128)(2,1)} %copy-done.7, ...), custom_call_target="tpu_custom_call" | custom-call | flops 9865003008 | bytes 12582912 | tf_op jit(solution)/shard_map/attention/pallas_call | solution.py:358
  124.0 6.4 %all-gather.2.cloned.1.call-done = bf16[7168,768]{1,0:T(8,128)(2,1)} async-done(((bf16[224,768]{1,0:T(8,128)(2,1)}), bf16[7168,768]{1,0:T(8,128)(2,1)}) %all-gather.2.cloned.1.call-update) | async-done | bytes 11010064 | tf_op jit(solution)/shard_map/all_gather | solution.py:863
  132.6 20.8 %middle.1 = (bf16[256,768]{1,0:T(8,128)(2,1)}, f32[256,768]{1,0:T(8,128)}, bf16[256,768]{1,0:T(8,128)(2,1)}, bf16[32,216,768]{2,1,0:T(8,128)(2,1)}, f32[8,768]{1,0:T(8,128)}, /*index=5*/f32[8,768]{1,0:T(8,128)}) custom-call(bf16[256,768]{1,0:T(8,128)(2,1)} %get-tuple-element.90.ctx_ref.refs_2_, bf16[256,768]{1,0:T(8,128)(2,1)} %bitcast.162, ...), custom_call_target="tpu_custom_call" | custom-call | flops 8153726976 | bytes 33554432 | tf_op jit(solution)/shard_map/middle/pallas_call | solution.py:583
  153.5 12.5 %attention_back.2 = (bf16[1024,768]{1,0:T(8,128)(2,1)}, bf16[1024,768]{1,0:T(8,128)(2,1)}, f32[768,256]{1,0:T(8,128)}) custom-call(s32[1]{0:T(128)} %bitcast.9.refs_7_.refs_0_.near_ref, bf16[256,768]{1,0:T(8,128)(2,1)} %get-tuple-element.93.refs_1_, bf16[256,768]{1,0:T(8,128)(2,1)} %get-tuple-element.90.ctx_ref.refs_2_, ...), custom_call_target="tpu_custom_call" | custom-call | flops 16106127360 | bytes 6291456 | tf_op jit(solution)/shard_map/attention_back/pallas_call | solution.py:675
  166.0 6.4 %token_product.2 = bf16[4,256,768]{2,1,0:T(8,128)(2,1)} custom-call(s32[1]{0:T(128)} %bitcast.9.refs_7_.refs_0_.near_ref, bf16[1024,768]{1,0:T(8,128)(2,1)} %get-tuple-element.101.dk_ref.refs_13_, bf16[1024,768]{1,0:T(8,128)(2,1)} %get-tuple-element.102.dv_ref.refs_14_, bf16[32,72,768]{2,1,0:T(8,128)(2,1)} %get-tuple-element.103.wk_ref.wv_ref.refs_11_, ...), custom_call_target="tpu_custom_call" | custom-call | flops 2415919104 | bytes 4718592 | tf_op jit(solution)/shard_map/token_product/pallas_call | solution.py:713
  172.5 12.8 %reduce-scatter.4.cloned.1.call-done = bf16[16,216,768]{2,1,0:T(8,128)(2,1)} async-done(((bf16[32,216,768]{2,1,0:T(8,128)(2,1)}), bf16[16,216,768]{2,1,0:T(8,128)(2,1)}) %reduce-scatter.4.cloned.1.call-update) | async-done | bytes 5308432 | tf_op jit(solution)/shard_map/reduce_scatter | solution.py:937
  186.9 1.9 collective-permute-start.15
  189.0 5.4 %attention_back.3 = (bf16[768,768]{1,0:T(8,128)(2,1)}, bf16[768,768]{1,0:T(8,128)(2,1)}, f32[768,256]{1,0:T(8,128)}) custom-call(s32[1]{0:T(128)} %bitcast.9.refs_7_.refs_0_.near_ref, bf16[256,768]{1,0:T(8,128)(2,1)} %get-tuple-element.93.refs_1_, bf16[256,768]{1,0:T(8,128)(2,1)} %get-tuple-element.90.ctx_ref.refs_2_, ...), custom_call_target="tpu_custom_call" | custom-call | flops 12079595520 | bytes 4718592 | tf_op jit(solution)/shard_map/attention_back/pallas_call | solution.py:675
  194.5 11.4 %weight_product.1 = (bf16[16,72,768]{2,1,0:T(8,128)(2,1)}, bf16[16,72,768]{2,1,0:T(8,128)(2,1)}, f32[256,768]{1,0:T(8,128)}, f32[8,768]{1,0:T(8,128)}) custom-call(bf16[256,768]{1,0:T(8,128)(2,1)} %copy-done.7, bf16[256,768]{1,0:T(8,128)(2,1)} %copy-done.13, bf16[256,768]{1,0:T(8,128)(2,1)} %copy-done.14, bf16[256,768]{1,0:T(8,128)(2,1)} %copy-done.15, ...), custom_call_target="tpu_custom_call" | custom-call | flops 4227858432 | bytes 16515072 | tf_op jit(solution)/shard_map/weight_product/pallas_call | solution.py:792
  207.2 2.2 fusion.4
  209.5 1.5 pad_maximum_fusion.1
  211.0 1.6 collective-permute-start.17
  212.5 1.6 pad_maximum_fusion
  214.2 1.1 collective-permute-done.18
  215.3 2.4 add_convert_fusion
  217.7 1.6 collective-permute-start.19
  219.3 12.1 %collective-permute-done.17 = bf16[256,768]{1,0:T(8,128)(2,1)S(1)} collective-permute-done((bf16[256,768]{1,0:T(8,128)(2,1)}, bf16[256,768]{1,0:T(8,128)(2,1)S(1)}, u32[]{:S(2)}, u32[]{:S(2)}) %collective-permute-start.17) | collective-permute-done | bytes 393248 | tf_op jit(solution)/shard_map/ppermute | solution.py:51
  231.5 1.3 collective-permute-start.20
  232.8 4.2 %token_product.3 = bf16[3,256,768]{2,1,0:T(8,128)(2,1)} custom-call(s32[1]{0:T(128)} %bitcast.9.refs_7_.refs_0_.near_ref, bf16[768,768]{1,0:T(8,128)(2,1)} %get-tuple-element.124.refs_15_.dk_ref, bf16[768,768]{1,0:T(8,128)(2,1)} %get-tuple-element.125.refs_16_.dv_ref, bf16[32,72,768]{2,1,0:T(8,128)(2,1)} %get-tuple-element.103.wk_ref.wv_ref.refs_11_, ...), custom_call_target="tpu_custom_call" | custom-call | flops 1811939328 | bytes 3538944 | tf_op jit(solution)/shard_map/token_product/pallas_call | solution.py:713
  237.0 2.2 constant_dynamic-slice_fusion
  240.2 16.6 %collective-permute-done.20 = bf16[256,768]{1,0:T(8,128)(2,1)S(1)} collective-permute-done((bf16[256,768]{1,0:T(8,128)(2,1)S(1)}, bf16[256,768]{1,0:T(8,128)(2,1)S(1)}, u32[]{:S(2)}, u32[]{:S(2)}) %collective-permute-start.20) | collective-permute-done | bytes 393248 | tf_op jit(solution)/shard_map/ppermute | solution.py:55
  256.8 6.9 %reduce-scatter.6.cloned.1.call-done = bf16[4,216,768]{2,1,0:T(8,128)(2,1)} async-done(((bf16[16,216,768]{2,1,0:T(8,128)(2,1)}), bf16[4,216,768]{2,1,0:T(8,128)(2,1)}) %reduce-scatter.6.cloned.1.call-update) | async-done | bytes 1327120 | tf_op jit(solution)/shard_map/reduce_scatter | solution.py:937
  263.8 2.5 fusion.6
  266.2 1.5 collective-permute-start.21
  268.9 10.8 %collective-permute-done.21 = bf16[4,80,768]{2,1,0:T(8,128)(2,1)} collective-permute-done((bf16[4,80,768]{2,1,0:T(8,128)(2,1)}, bf16[4,80,768]{2,1,0:T(8,128)(2,1)}, u32[]{:S(2)}, u32[]{:S(2)}) %collective-permute-start.21) | collective-permute-done | bytes 491552 | tf_op jit(solution)/shard_map/ppermute | solution.py:51
  279.7 1.2 fusion.10
  280.9 1.6 collective-permute-start.24
  282.5 3.2 collective-permute-start.25
  285.8 1.5 collective-permute-start.22
  288.0 7.2 %collective-permute-done.24 = bf16[1,80,768]{2,1,0:T(8,128)(2,1)S(1)} collective-permute-done((bf16[1,80,768]{2,1,0:T(8,128)(2,1)S(1)}, bf16[1,80,768]{2,1,0:T(8,128)(2,1)S(1)}, u32[]{:S(2)}, u32[]{:S(2)}) %collective-permute-start.24) | collective-permute-done | bytes 122912 | tf_op jit(solution)/shard_map/ppermute | solution.py:51
  295.1 5.2 %collective-permute-done.25 = bf16[1,80,768]{2,1,0:T(8,128)(2,1)S(1)} collective-permute-done((bf16[1,80,768]{2,1,0:T(8,128)(2,1)S(1)}, bf16[1,80,768]{2,1,0:T(8,128)(2,1)S(1)}, u32[]{:S(2)}, u32[]{:S(2)}) %collective-permute-start.25) | collective-permute-done | bytes 122912 | tf_op jit(solution)/shard_map/ppermute | solution.py:51
  300.4 2.9 collective-permute-done.26
  307.3 4.0 %reduce-scatter.8.cloned.1.call-done = bf16[1,216,768]{2,1,0:T(8,128)(2,1)} async-done(((bf16[4,216,768]{2,1,0:T(8,128)(2,1)}), bf16[1,216,768]{2,1,0:T(8,128)(2,1)}) %reduce-scatter.8.cloned.1.call-update) | async-done | bytes 331792 | tf_op jit(solution)/shard_map/reduce_scatter | solution.py:937
  (133 shorter events, 26.8 us)
Async XLA Ops:
  7.2 123.2 %all-gather.2.cloned.1.call-start = ((), (), s32[]{:S(2)}) async-start(), calls=%async_computation.3 | async-start | bytes 11354112 | tf_op jit(solution)/shard_map/all_gather | solution.py:863
  11.3 174.0 %reduce-scatter.4.cloned.1.call-start = ((), (), s32[]{:S(2)}) async-start(), calls=%async_computation.4 | async-start | bytes 15925248 | tf_op jit(solution)/shard_map/reduce_scatter | solution.py:937
  11.3 28.8 %collective-permute-start = (bf16[80,768]{1,0:T(8,128)(2,1)}, bf16[80,768]{1,0:T(8,128)(2,1)S(1)}, u32[]{:S(2)}, u32[]{:S(2)}) collective-permute-start(bf16[80,768]{1,0:T(8,128)(2,1)} %get-tuple-element.77), channel_id=1, source_target_pairs={{0,2},{1,3},{2,0},{3,1},{4,6},{5,7},{6,4},{7,5},{8,10},{9,11},{10,... | collective-permute-start | bytes 368648 | tf_op jit(solution)/shard_map/ppermute | solution.py:51
  14.4 25.8 %collective-permute-start.1 = (bf16[80,768]{1,0:T(8,128)(2,1)}, bf16[80,768]{1,0:T(8,128)(2,1)S(1)}, u32[]{:S(2)}, u32[]{:S(2)}) collective-permute-start(bf16[80,768]{1,0:T(8,128)(2,1)} %get-tuple-element.77), channel_id=1, source_target_pairs={{0,4},{1,5},{2,6},{3,7},{4,0},{5,1},{6,2},{7,3},{8,12},{9,13},{10,... | collective-permute-start | bytes 368648 | tf_op jit(solution)/shard_map/ppermute | solution.py:51
  17.0 23.2 %collective-permute-start.2 = (bf16[80,768]{1,0:T(8,128)(2,1)}, bf16[80,768]{1,0:T(8,128)(2,1)S(1)}, u32[]{:S(2)}, u32[]{:S(2)}) collective-permute-start(bf16[80,768]{1,0:T(8,128)(2,1)} %get-tuple-element.77), channel_id=1, source_target_pairs={{0,6},{1,7},{2,4},{3,5},{4,2},{5,3},{6,0},{7,1},{8,14},{9,15},{10,... | collective-permute-start | bytes 368648 | tf_op jit(solution)/shard_map/ppermute | solution.py:51
  17.0 21.4 %collective-permute-start.3 = (bf16[256,768]{1,0:T(8,128)(2,1)}, bf16[256,768]{1,0:T(8,128)(2,1)S(1)}, u32[]{:S(2)}, u32[]{:S(2)}) collective-permute-start(bf16[256,768]{1,0:T(8,128)(2,1)} %bitcast.157), channel_id=1, source_target_pairs={{0,4},{1,5},{2,6},{3,7},{8,12},{9,13},{10,14},{11,15},{16,20},{17,... | collective-permute-start | bytes 1179656 | tf_op jit(solution)/shard_map/ppermute | solution.py:55
  20.9 19.4 %collective-permute-start.4 = (bf16[256,768]{1,0:T(8,128)(2,1)}, bf16[256,768]{1,0:T(8,128)(2,1)S(1)}, u32[]{:S(2)}, u32[]{:S(2)}) collective-permute-start(bf16[256,768]{1,0:T(8,128)(2,1)} %bitcast.158), channel_id=1, source_target_pairs={{0,1},{1,0},{2,3},{3,2},{4,5},{5,4},{6,7},{7,6},{8,9},{9,8},{10,11... | collective-permute-start | bytes 1179656 | tf_op jit(solution)/shard_map/ppermute | solution.py:51
  38.4 32.3 %collective-permute-start.9 = (bf16[256,768]{1,0:T(8,128)(2,1)}, bf16[256,768]{1,0:T(8,128)(2,1)S(1)}, u32[]{:S(2)}, u32[]{:S(2)}) collective-permute-start(bf16[256,768]{1,0:T(8,128)(2,1)} %bitcast.159), channel_id=1, source_target_pairs={{5,6},{6,5},{13,14},{14,13},{21,22},{22,21},{29,30},{30,29}} | collective-permute-start | bytes 1179656 | tf_op jit(solution)/shard_map/ppermute | solution.py:55
  40.2 38.1 %copy-start.7 = (bf16[256,768]{1,0:T(8,128)(2,1)}, bf16[256,768]{1,0:T(8,128)(2,1)S(1)}, u32[]{:S(2)}) copy-start(bf16[256,768]{1,0:T(8,128)(2,1)S(1)} %broadcast_select_fusion.refs_0_) | copy-start | bytes 1179652
  40.2 38.1 %copy-start.11 = (bf16[256,768]{1,0:T(8,128)(2,1)}, bf16[256,768]{1,0:T(8,128)(2,1)S(1)}, u32[]{:S(2)}) copy-start(bf16[256,768]{1,0:T(8,128)(2,1)S(1)} %collective-permute-done.4.refs_5_) | copy-start | bytes 1179652
  40.2 35.0 %collective-permute-start.7 = (bf16[256,768]{1,0:T(8,128)(2,1)S(1)}, bf16[256,768]{1,0:T(8,128)(2,1)S(1)}, u32[]{:S(2)}, u32[]{:S(2)}) collective-permute-start(bf16[256,768]{1,0:T(8,128)(2,1)S(1)} %broadcast_select_fusion.refs_0_), channel_id=1, source_target_pairs={{0,2},{1,3},{2,0},{3,1},{4,6},{5,7},{6,4},{7,5},{8,10},{9,11},{10,... | collective-permute-start | bytes 1179656 | tf_op jit(solution)/shard_map/ppermute | solution.py:51
  56.9 18.4 %collective-permute-start.8 = (bf16[256,768]{1,0:T(8,128)(2,1)S(1)}, bf16[256,768]{1,0:T(8,128)(2,1)S(1)}, u32[]{:S(2)}, u32[]{:S(2)}) collective-permute-start(bf16[256,768]{1,0:T(8,128)(2,1)S(1)} %broadcast_select_fusion.refs_0_), channel_id=1, source_target_pairs={{0,1},{1,0},{2,3},{3,2},{4,5},{5,4},{6,7},{7,6},{8,9},{9,8},{10,11... | collective-permute-start | bytes 1179656 | tf_op jit(solution)/shard_map/ppermute | solution.py:51
  57.7 13.0 %collective-permute-start.6 = (bf16[4,40,768]{2,1,0:T(8,128)(2,1)S(1)}, bf16[4,40,768]{2,1,0:T(8,128)(2,1)S(1)}, u32[]{:S(2)}, u32[]{:S(2)}) collective-permute-start(bf16[4,40,768]{2,1,0:T(8,128)(2,1)S(1)} %pad_maximum_fusion.5), channel_id=1, source_target_pairs={{0,1},{1,0},{2,3},{3,2},{4,5},{5,4},{6,7},{7,6},{8,9},{9,8},{10,11... | collective-permute-start | bytes 737288 | tf_op jit(solution)/shard_map/ppermute | solution.py:51
  59.1 11.6 %collective-permute-start.5 = (bf16[4,40,768]{2,1,0:T(8,128)(2,1)S(1)}, bf16[4,40,768]{2,1,0:T(8,128)(2,1)S(1)}, u32[]{:S(2)}, u32[]{:S(2)}) collective-permute-start(bf16[4,40,768]{2,1,0:T(8,128)(2,1)S(1)} %pad_maximum_fusion.4), channel_id=1, source_target_pairs={{0,16},{1,17},{2,18},{3,19},{4,20},{5,21},{6,22},{7,23},{8,24},{9,... | collective-permute-start | bytes 737288 | tf_op jit(solution)/shard_map/ppermute | solution.py:51
  70.7 31.4 %copy-start.16 = (s32[1,8]{1,0:T(1,128)S(1)}, s32[1,8]{1,0:T(1,128)}, u32[]{:S(2)}) copy-start(s32[1,8]{1,0:T(1,128)} %param.19) | copy-start | bytes 100
  70.8 7.5 %copy-start.12 = (bf16[256,768]{1,0:T(8,128)(2,1)}, bf16[256,768]{1,0:T(8,128)(2,1)S(1)}, u32[]{:S(2)}) copy-start(bf16[256,768]{1,0:T(8,128)(2,1)S(1)} %collective-permute-done.9.refs_6_) | copy-start | bytes 1179652
  75.3 3.0 copy-start.13
  75.3 20.4 %copy-start.14 = (bf16[256,768]{1,0:T(8,128)(2,1)}, bf16[256,768]{1,0:T(8,128)(2,1)S(1)}, u32[]{:S(2)}) copy-start(bf16[256,768]{1,0:T(8,128)(2,1)S(1)} %collective-permute-done.8.refs_2_) | copy-start | bytes 1179652
  75.3 17.7 %collective-permute-start.13 = (bf16[8,40,768]{2,1,0:T(8,128)(2,1)S(1)}, bf16[8,40,768]{2,1,0:T(8,128)(2,1)S(1)}, u32[]{:S(2)}, u32[]{:S(2)}) collective-permute-start(bf16[8,40,768]{2,1,0:T(8,128)(2,1)S(1)} %constant_dynamic-update-slice_fusion.5), channel_id=1, source_target_pairs={{0,16},{1,17},{2,18},{3,19},{4,20},{5,21},{6,22},{7,23},{8,24},{9,... | collective-permute-start | bytes 1474568 | tf_op jit(solution)/shard_map/ppermute | solution.py:51
  76.8 18.8 %collective-permute-start.10 = (bf16[8,40,768]{2,1,0:T(8,128)(2,1)S(1)}, bf16[8,40,768]{2,1,0:T(8,128)(2,1)S(1)}, u32[]{:S(2)}, u32[]{:S(2)}) collective-permute-start(bf16[8,40,768]{2,1,0:T(8,128)(2,1)S(1)} %constant_dynamic-update-slice_fusion), channel_id=1, source_target_pairs={{0,1},{1,0},{2,3},{3,2},{4,5},{5,4},{6,7},{7,6},{8,9},{9,8},{10,11... | collective-permute-start | bytes 1474568 | tf_op jit(solution)/shard_map/ppermute | solution.py:51
  78.3 23.0 %collective-permute-start.11 = (bf16[256,768]{1,0:T(8,128)(2,1)S(1)}, bf16[256,768]{1,0:T(8,128)(2,1)S(1)}, u32[]{:S(2)}, u32[]{:S(2)}) collective-permute-start(bf16[256,768]{1,0:T(8,128)(2,1)S(1)} %collective-permute-done.8.refs_2_), channel_id=1, source_target_pairs={{0,2},{1,3},{2,0},{3,1},{4,6},{5,7},{6,4},{7,5},{8,10},{9,11},{10,... | collective-permute-start | bytes 1179656 | tf_op jit(solution)/shard_map/ppermute | solution.py:51
  93.0 11.8 %copy-start.8 = (bf16[16,40,768]{2,1,0:T(8,128)(2,1)}, bf16[16,40,768]{2,1,0:T(8,128)(2,1)S(1)}, u32[]{:S(2)}) copy-start(bf16[16,40,768]{2,1,0:T(8,128)(2,1)S(1)} %constant_dynamic-update-slice_fusion.10.refs_12_) | copy-start | bytes 2949124
  93.0 10.9 %collective-permute-start.14 = (bf16[16,40,768]{2,1,0:T(8,128)(2,1)S(1)}, bf16[16,40,768]{2,1,0:T(8,128)(2,1)S(1)}, u32[]{:S(2)}, u32[]{:S(2)}) collective-permute-start(bf16[16,40,768]{2,1,0:T(8,128)(2,1)S(1)} %constant_dynamic-update-slice_fusion.10.refs_12_), channel_id=1, source_target_pairs={{0,8},{1,9},{2,10},{3,11},{4,12},{5,13},{6,14},{7,15},{8,0},{9,1},... | collective-permute-start | bytes 2949128 | tf_op jit(solution)/shard_map/ppermute | solution.py:51
  95.7 9.1 %copy-start.5 = (bf16[16,40,768]{2,1,0:T(8,128)(2,1)}, bf16[16,40,768]{2,1,0:T(8,128)(2,1)S(1)}, u32[]{:S(2)}) copy-start(bf16[16,40,768]{2,1,0:T(8,128)(2,1)S(1)} %pad_maximum_fusion.2.refs_10_) | copy-start | bytes 2949124
  101.3 0.8 copy-start.15
  102.1 2.7 collective-permute-start.12
  104.0 1.0 copy-start.10
  153.5 110.2 %reduce-scatter.6.cloned.1.call-start = ((), (), s32[]{:S(2)}) async-start(), calls=%async_computation.5 | async-start | bytes 6635520 | tf_op jit(solution)/shard_map/reduce_scatter | solution.py:937
  185.3 0.7 copy-start.9
  185.3 1.6 copy-start
  185.3 126.0 %reduce-scatter.8.cloned.1.call-start = ((), (), s32[]{:S(2)}) async-start(), calls=%async_computation.6 | async-start | bytes 1658880 | tf_op jit(solution)/shard_map/reduce_scatter | solution.py:937
  186.9 20.3 %collective-permute-start.15 = (bf16[256,768]{1,0:T(8,128)(2,1)S(1)}, bf16[256,768]{1,0:T(8,128)(2,1)}, u32[]{:S(2)}, u32[]{:S(2)}) collective-permute-start(bf16[256,768]{1,0:T(8,128)(2,1)S(1)} %get-tuple-element.143), channel_id=1, source_target_pairs={{0,2},{1,3},{2,0},{3,1},{4,6},{5,7},{6,4},{7,5},{8,10},{9,11},{10,... | collective-permute-start | bytes 1179656 | tf_op jit(solution)/shard_map/ppermute | solution.py:51
  188.8 18.4 %collective-permute-start.16 = (bf16[256,768]{1,0:T(8,128)(2,1)S(1)}, bf16[256,768]{1,0:T(8,128)(2,1)}, u32[]{:S(2)}, u32[]{:S(2)}) collective-permute-start(bf16[256,768]{1,0:T(8,128)(2,1)S(1)} %get-tuple-element.142), channel_id=1, source_target_pairs={{0,2},{1,3},{2,0},{3,1},{4,6},{5,7},{6,4},{7,5},{8,10},{9,11},{10,... | collective-permute-start | bytes 1179656 | tf_op jit(solution)/shard_map/ppermute | solution.py:51
  207.1 2.4 copy-start.4
  211.0 4.3 %collective-permute-start.18 = (bf16[16,80,768]{2,1,0:T(8,128)(2,1)}, bf16[16,80,768]{2,1,0:T(8,128)(2,1)}, u32[]{:S(2)}, u32[]{:S(2)}) collective-permute-start(bf16[16,80,768]{2,1,0:T(8,128)(2,1)} %pad_maximum_fusion.1), channel_id=1, source_target_pairs={{0,8},{1,9},{2,10},{3,11},{4,12},{5,13},{6,14},{7,15},{8,0},{9,1},... | collective-permute-start | bytes 5898248 | tf_op jit(solution)/shard_map/ppermute | solution.py:51
  211.0 20.4 %collective-permute-start.17 = (bf16[256,768]{1,0:T(8,128)(2,1)}, bf16[256,768]{1,0:T(8,128)(2,1)S(1)}, u32[]{:S(2)}, u32[]{:S(2)}) collective-permute-start(bf16[256,768]{1,0:T(8,128)(2,1)} %get-tuple-element.115), channel_id=1, source_target_pairs={{0,1},{1,0},{2,3},{3,2},{4,5},{5,4},{6,7},{7,6},{8,9},{9,8},{10,11... | collective-permute-start | bytes 1179656 | tf_op jit(solution)/shard_map/ppermute | solution.py:51
  217.7 39.1 %collective-permute-start.19 = (bf16[8,80,768]{2,1,0:T(8,128)(2,1)}, bf16[8,80,768]{2,1,0:T(8,128)(2,1)}, u32[]{:S(2)}, u32[]{:S(2)}) collective-permute-start(bf16[8,80,768]{2,1,0:T(8,128)(2,1)} %bitcast.33), channel_id=1, source_target_pairs={{0,16},{1,17},{2,18},{3,19},{4,20},{5,21},{6,22},{7,23},{8,24},{9,... | collective-permute-start | bytes 2949128 | tf_op jit(solution)/shard_map/ppermute | solution.py:51
  231.5 25.3 %collective-permute-start.20 = (bf16[256,768]{1,0:T(8,128)(2,1)S(1)}, bf16[256,768]{1,0:T(8,128)(2,1)S(1)}, u32[]{:S(2)}, u32[]{:S(2)}) collective-permute-start(bf16[256,768]{1,0:T(8,128)(2,1)S(1)} %fusion.5), channel_id=1, source_target_pairs={{4,0},{5,1},{6,2},{7,3},{12,8},{13,9},{14,10},{15,11},{20,16},{21,... | collective-permute-start | bytes 1179656 | tf_op jit(solution)/shard_map/ppermute | solution.py:55
  263.7 5.1 %copy-start.2 = (bf16[1,1,640,768]{3,2,1,0:T(8,128)(2,1)S(1)}, bf16[1,1,640,768]{3,2,1,0:T(8,128)(2,1)}, u32[]{:S(2)}) copy-start(bf16[1,1,640,768]{3,2,1,0:T(8,128)(2,1)} %constant_dynamic-slice_fusion) | copy-start | bytes 2949124
  263.7 5.1 %copy-start.3 = (bf16[1,1,640,768]{3,2,1,0:T(8,128)(2,1)S(1)}, bf16[1,1,640,768]{3,2,1,0:T(8,128)(2,1)}, u32[]{:S(2)}) copy-start(bf16[1,1,640,768]{3,2,1,0:T(8,128)(2,1)} %constant_dynamic-slice_fusion.1) | copy-start | bytes 2949124
  266.2 13.5 %collective-permute-start.21 = (bf16[4,80,768]{2,1,0:T(8,128)(2,1)}, bf16[4,80,768]{2,1,0:T(8,128)(2,1)}, u32[]{:S(2)}, u32[]{:S(2)}) collective-permute-start(bf16[4,80,768]{2,1,0:T(8,128)(2,1)} %fusion.6), channel_id=1, source_target_pairs={{0,1},{1,0},{2,3},{3,2},{4,5},{5,4},{6,7},{7,6},{8,9},{9,8},{10,11... | collective-permute-start | bytes 1474568 | tf_op jit(solution)/shard_map/ppermute | solution.py:51
  268.8 17.0 %copy-start.1 = (bf16[3,256,768]{2,1,0:T(8,128)(2,1)S(1)}, bf16[3,256,768]{2,1,0:T(8,128)(2,1)}, u32[]{:S(2)}) copy-start(bf16[3,256,768]{2,1,0:T(8,128)(2,1)} %token_product.3) | copy-start | bytes 3538948
  280.9 25.2 %copy-start.6 = (f32[256,768]{1,0:T(8,128)S(1)}, f32[256,768]{1,0:T(8,128)}, u32[]{:S(2)}) copy-start(f32[256,768]{1,0:T(8,128)} %get-tuple-element.110) | copy-start | bytes 2359300
  280.9 14.2 %collective-permute-start.24 = (bf16[1,80,768]{2,1,0:T(8,128)(2,1)S(1)}, bf16[1,80,768]{2,1,0:T(8,128)(2,1)S(1)}, u32[]{:S(2)}, u32[]{:S(2)}) collective-permute-start(bf16[1,80,768]{2,1,0:T(8,128)(2,1)S(1)} %get-tuple-element.137), channel_id=1, source_target_pairs={{0,2},{1,3},{2,0},{3,1},{4,6},{5,7},{6,4},{7,5},{8,10},{9,11},{10,... | collective-permute-start | bytes 368648 | tf_op jit(solution)/shard_map/ppermute | solution.py:51
  282.5 17.9 %collective-permute-start.25 = (bf16[1,80,768]{2,1,0:T(8,128)(2,1)S(1)}, bf16[1,80,768]{2,1,0:T(8,128)(2,1)S(1)}, u32[]{:S(2)}, u32[]{:S(2)}) collective-permute-start(bf16[1,80,768]{2,1,0:T(8,128)(2,1)S(1)} %get-tuple-element.139), channel_id=1, source_target_pairs={{0,4},{1,5},{2,6},{3,7},{4,0},{5,1},{6,2},{7,3},{8,12},{9,13},{10,... | collective-permute-start | bytes 368648 | tf_op jit(solution)/shard_map/ppermute | solution.py:51
  285.7 17.5 %collective-permute-start.26 = (bf16[1,80,768]{2,1,0:T(8,128)(2,1)S(1)}, bf16[1,80,768]{2,1,0:T(8,128)(2,1)S(1)}, u32[]{:S(2)}, u32[]{:S(2)}) collective-permute-start(bf16[1,80,768]{2,1,0:T(8,128)(2,1)S(1)} %get-tuple-element.138), channel_id=1, source_target_pairs={{0,6},{1,7},{2,4},{3,5},{4,2},{5,3},{6,0},{7,1},{8,14},{9,15},{10,... | collective-permute-start | bytes 368648 | tf_op jit(solution)/shard_map/ppermute | solution.py:51
  285.8 20.4 %collective-permute-start.22 = (bf16[256,768]{1,0:T(8,128)(2,1)S(1)}, bf16[256,768]{1,0:T(8,128)(2,1)S(1)}, u32[]{:S(2)}, u32[]{:S(2)}) collective-permute-start(bf16[256,768]{1,0:T(8,128)(2,1)S(1)} %get-tuple-element.144), channel_id=1, source_target_pairs={{0,1},{1,0},{2,3},{3,2},{4,5},{5,4},{6,7},{7,6},{8,9},{9,8},{10,11... | collective-permute-start | bytes 1179656 | tf_op jit(solution)/shard_map/ppermute | solution.py:51
  287.3 18.9 %collective-permute-start.23 = (bf16[256,768]{1,0:T(8,128)(2,1)S(1)}, bf16[256,768]{1,0:T(8,128)(2,1)S(1)}, u32[]{:S(2)}, u32[]{:S(2)}) collective-permute-start(bf16[256,768]{1,0:T(8,128)(2,1)S(1)} %get-tuple-element.145), channel_id=1, source_target_pairs={{5,6},{6,5},{13,14},{14,13},{21,22},{22,21},{29,30},{30,29}} | collective-permute-start | bytes 1179656 | tf_op jit(solution)/shard_map/ppermute | solution.py:55
Sparse Core Ops, SparseCore 0:
  11.5 118.8 all-gather.1
  153.6 31.6 reduce-scatter.3
  188.6 75.1 reduce-scatter.5
  266.0 45.2 reduce-scatter.7

commit v17 on v16

--- a/solution.py
+++ b/solution.py
@@ -981,16 +981,13 @@
         send = jnp.concatenate([send, pick.cut(d_lines, core_bit, 1 - place)], 1)
         keep = jnp.concatenate([keep, pick.cut(d_lines, core_bit, place)], 1)
         reduce = Reduce(plan, [keep, plan.swap(send, core_bit)], left)
-        for bit in plan.x + plan.y:
-            held = reduce.terms
-            if bit == plan.x[0]:
-                held = tie(*held)
-                returned.prompt_three()
-            elif bit == plan.y[0]:
-                *held, grads, shared_n, returned.back = tie(*held, grads, shared_n, returned.back)
-                grads = level(grads, "z")
-            reduce.terms = list(held)
-            reduce.stage(bit)
+        returned.prompt_three()
+        reduce.stage_direct(plan.x + plan.y)
+        *held, grads, shared_n, returned.back = tie(
+            *reduce.terms, grads, shared_n, returned.back
+        )
+        reduce.terms = list(held)
+        grads = level(grads, "z")
         *held, shared_n = tie(*reduce.terms, shared_n)
         reduce.terms = list(held)
         returned.near(shared_n)

time: 324 us -> 327 us (level)
  waiting for transfers between devices: 139 us -> 146 us
    reduce_scatter x3, waiting for transfers between devices: 23.7 us -> 36.7 us  [per_device(): lax.psum_scatter(value, axes, scatter_dimension=0, tiled=True)]
    ppermute x23 -> x24, waiting for transfers between devices: 78.3 us -> 69.1 us  [swap(): return lax.ppermute(value, AXES, [(i, i ^ mask) for i in range(self.count)])]
    ppermute x23 -> x24, starting transfers between devices: 42.8 us -> 42.9 us  [swap(): return lax.ppermute(value, AXES, [(i, i ^ mask) for i in range(self.count)])]
  transfers between devices with their start and end apart: 31 -> 32, of which waited for: 18 -> 15; matrix products, arithmetic and copies ran while one was open for 8% -> 8% of each run, Pallas kernels for 18% -> 18%
where the time goes in v17:
time: 327 us; the launch traced here: 326 us
  waiting for transfers between devices  146 us (45%)
  Pallas kernels  82.1 us (25%)
  starting transfers between devices  49.5 us (15%)
  other arithmetic  20.5 us (6%)
  between operations  14.4 us (4%)
  local copies, waits for them, and re-layouts  13.7 us (4%)
    ppermute x24, waiting for transfers between devices, swap(): return lax.ppermute(value, AXES, [(i, i ^ mask) for i in range(self.count)])  69.1 us
    ppermute x24, starting transfers between devices, swap(): return lax.ppermute(value, AXES, [(i, i ^ mask) for i in range(self.count)])  42.9 us
    reduce_scatter x3, waiting for transfers between devices, per_device(): lax.psum_scatter(value, axes, scatter_dimension=0, tiled=True)  36.7 us
    ppermute x4, waiting for transfers between devices, send(): return lax.ppermute(value, AXES, pairs)  33.3 us
    pallas_call x1, Pallas kernels, middle_call(): pl.pallas_call(functools.partial(middle_kernel, wide, mapped), grid=(2 *...  20.8 us
    pallas_call x1, Pallas kernels, attention_call(): pl.pallas_call(functools.partial(attention_kernel, blocks, first, rows, p...  19.2 us
    pallas_call x2, Pallas kernels, back_call(): pl.pallas_call(functools.partial(back_kernel, rows, bound, dq0 is not Non...  17.9 us
    pallas_call x1, Pallas kernels, weight_call(): pl.pallas_call(functools.partial(weight_kernel, blocks, first, rows, runs...  11.7 us
  transfers between devices with their start and end apart: 32, of which 15 were waited for; matrix products, arithmetic and copies ran while one was open for 8% of the time, Pallas kernels for 18%

profile of v17, /device:TPU:0, one launch (start us, length us, event | category | flops | bytes accessed | tf_op | source)
XLA Modules:
  0.0 326.0 jit_solution(3348490195349105802)
XLA Ops:
  9.4 1.8 pack.1
  11.3 3.1 collective-permute-start
  14.4 2.6 collective-permute-start.1
  17.0 3.8 %collective-permute-start.3 = (bf16[256,768]{1,0:T(8,128)(2,1)}, bf16[256,768]{1,0:T(8,128)(2,1)S(1)}, u32[]{:S(2)}, u32[]{:S(2)}) collective-permute-start(bf16[256,768]{1,0:T(8,128)(2,1)} %bitcast.164), channel_id=1, source_target_pairs={{0,4},{1,5},{2,6},{3,7},{8,12},{9,13},{10,14},{11,15},{16,20},{17,... | collective-permute-start | bytes 1179656 | tf_op jit(solution)/shard_map/ppermute | solution.py:55
  20.9 1.6 collective-permute-start.4
  24.2 14.2 %collective-permute-done.3 = bf16[256,768]{1,0:T(8,128)(2,1)S(1)} collective-permute-done((bf16[256,768]{1,0:T(8,128)(2,1)}, bf16[256,768]{1,0:T(8,128)(2,1)S(1)}, u32[]{:S(2)}, u32[]{:S(2)}) %collective-permute-start.3) | collective-permute-done | bytes 393248 | tf_op jit(solution)/shard_map/ppermute | solution.py:55
  39.1 1.1 broadcast_select_fusion.refs_0_
  40.2 16.6 %collective-permute-start.7 = (bf16[256,768]{1,0:T(8,128)(2,1)S(1)}, bf16[256,768]{1,0:T(8,128)(2,1)S(1)}, u32[]{:S(2)}, u32[]{:S(2)}) collective-permute-start(bf16[256,768]{1,0:T(8,128)(2,1)S(1)} %broadcast_select_fusion.refs_0_), channel_id=1, source_target_pairs={{0,2},{1,3},{2,0},{3,1},{4,6},{5,7},{6,4},{7,5},{8,10},{9,11},{10,... | collective-permute-start | bytes 1179656 | tf_op jit(solution)/shard_map/ppermute | solution.py:51
  57.7 1.4 collective-permute-start.6
  59.8 10.9 %collective-permute-done.6 = bf16[4,40,768]{2,1,0:T(8,128)(2,1)S(1)} collective-permute-done((bf16[4,40,768]{2,1,0:T(8,128)(2,1)S(1)}, bf16[4,40,768]{2,1,0:T(8,128)(2,1)S(1)}, u32[]{:S(2)}, u32[]{:S(2)}) %collective-permute-start.6) | collective-permute-done | bytes 245792 | tf_op jit(solution)/shard_map/ppermute | solution.py:51
  70.8 4.5 %collective-permute-done.7.refs_1_ = bf16[256,768]{1,0:T(8,128)(2,1)S(1)} collective-permute-done((bf16[256,768]{1,0:T(8,128)(2,1)S(1)}, bf16[256,768]{1,0:T(8,128)(2,1)S(1)}, u32[]{:S(2)}, u32[]{:S(2)}) %collective-permute-start.7) | collective-permute-done | bytes 393248 | tf_op jit(solution)/shard_map/ppermute | solution.py:51
  75.3 1.5 collective-permute-start.13
  76.8 1.5 collective-permute-start.10
  78.3 14.6 %collective-permute-done.13 = bf16[8,40,768]{2,1,0:T(8,128)(2,1)S(1)} collective-permute-done((bf16[8,40,768]{2,1,0:T(8,128)(2,1)S(1)}, bf16[8,40,768]{2,1,0:T(8,128)(2,1)S(1)}, u32[]{:S(2)}, u32[]{:S(2)}) %collective-permute-start.13) | collective-permute-done | bytes 491552 | tf_op jit(solution)/shard_map/ppermute | solution.py:51
  93.1 2.5 collective-permute-done.10
  95.7 5.6 %collective-permute-done.11.refs_3_ = bf16[256,768]{1,0:T(8,128)(2,1)S(1)} collective-permute-done((bf16[256,768]{1,0:T(8,128)(2,1)S(1)}, bf16[256,768]{1,0:T(8,128)(2,1)S(1)}, u32[]{:S(2)}, u32[]{:S(2)}) %collective-permute-start.11) | collective-permute-done | bytes 393248 | tf_op jit(solution)/shard_map/ppermute | solution.py:51
  103.0 0.9 broadcast_in_dim.40.refs_15_.refs_8_
  104.8 19.2 %attention.1 = (bf16[32,72,768]{2,1,0:T(8,128)(2,1)}, bf16[256,768]{1,0:T(8,128)(2,1)}, bf16[1024,768]{1,0:T(8,128)(2,1)}, bf16[1024,768]{1,0:T(8,128)(2,1)}, bf...) custom-call(bf16[256,768]{1,0:T(8,128)(2,1)} %copy-done.6, ...), custom_call_target="tpu_custom_call" | custom-call | flops 9865003008 | bytes 12582912 | tf_op jit(solution)/shard_map/attention/pallas_call | solution.py:358
  123.9 6.5 %all-gather.2.cloned.1.call-done = bf16[7168,768]{1,0:T(8,128)(2,1)} async-done(((bf16[224,768]{1,0:T(8,128)(2,1)}), bf16[7168,768]{1,0:T(8,128)(2,1)}) %all-gather.2.cloned.1.call-update) | async-done | bytes 11010064 | tf_op jit(solution)/shard_map/all_gather | solution.py:863
  130.5 1.0 slice.266
  132.7 20.8 %middle.1 = (bf16[256,768]{1,0:T(8,128)(2,1)}, f32[256,768]{1,0:T(8,128)}, bf16[256,768]{1,0:T(8,128)(2,1)}, bf16[32,216,768]{2,1,0:T(8,128)(2,1)}, f32[8,768]{1,0:T(8,128)}, /*index=5*/f32[8,768]{1,0:T(8,128)}) custom-call(bf16[256,768]{1,0:T(8,128)(2,1)} %get-tuple-element.91.ctx_ref.refs_2_, bf16[256,768]{1,0:T(8,128)(2,1)} %bitcast.169, ...), custom_call_target="tpu_custom_call" | custom-call | flops 8153726976 | bytes 33554432 | tf_op jit(solution)/shard_map/middle/pallas_call | solution.py:583
  153.6 12.5 %attention_back.2 = (bf16[1024,768]{1,0:T(8,128)(2,1)}, bf16[1024,768]{1,0:T(8,128)(2,1)}, f32[768,256]{1,0:T(8,128)}) custom-call(s32[1]{0:T(128)} %bitcast.9.refs_7_.refs_0_.near_ref, bf16[256,768]{1,0:T(8,128)(2,1)} %get-tuple-element.94.refs_1_, bf16[256,768]{1,0:T(8,128)(2,1)} %get-tuple-element.91.ctx_ref.refs_2_, ...), custom_call_target="tpu_custom_call" | custom-call | flops 16106127360 | bytes 6291456 | tf_op jit(solution)/shard_map/attention_back/pallas_call | solution.py:675
  166.1 6.4 %token_product.2 = bf16[4,256,768]{2,1,0:T(8,128)(2,1)} custom-call(s32[1]{0:T(128)} %bitcast.9.refs_7_.refs_0_.near_ref, bf16[1024,768]{1,0:T(8,128)(2,1)} %get-tuple-element.102.dk_ref.refs_13_, bf16[1024,768]{1,0:T(8,128)(2,1)} %get-tuple-element.103.dv_ref.refs_14_, bf16[32,72,768]{2,1,0:T(8,128)(2,1)} %get-tuple-element.104.wk_ref.wv_ref.refs_11_, ...), custom_call_target="tpu_custom_call" | custom-call | flops 2415919104 | bytes 4718592 | tf_op jit(solution)/shard_map/token_product/pallas_call | solution.py:713
  172.5 12.8 %reduce-scatter.4.cloned.1.call-done = bf16[16,216,768]{2,1,0:T(8,128)(2,1)} async-done(((bf16[32,216,768]{2,1,0:T(8,128)(2,1)}), bf16[16,216,768]{2,1,0:T(8,128)(2,1)}) %reduce-scatter.4.cloned.1.call-update) | async-done | bytes 5308432 | tf_op jit(solution)/shard_map/reduce_scatter | solution.py:937
  187.7 1.8 collective-permute-start.15
  189.7 5.5 %attention_back.3 = (bf16[768,768]{1,0:T(8,128)(2,1)}, bf16[768,768]{1,0:T(8,128)(2,1)}, f32[768,256]{1,0:T(8,128)}) custom-call(s32[1]{0:T(128)} %bitcast.9.refs_7_.refs_0_.near_ref, bf16[256,768]{1,0:T(8,128)(2,1)} %get-tuple-element.94.refs_1_, bf16[256,768]{1,0:T(8,128)(2,1)} %get-tuple-element.91.ctx_ref.refs_2_, ...), custom_call_target="tpu_custom_call" | custom-call | flops 12079595520 | bytes 4718592 | tf_op jit(solution)/shard_map/attention_back/pallas_call | solution.py:675
  195.2 11.7 %weight_product.1 = (bf16[16,72,768]{2,1,0:T(8,128)(2,1)}, bf16[16,72,768]{2,1,0:T(8,128)(2,1)}, f32[256,768]{1,0:T(8,128)}, f32[8,768]{1,0:T(8,128)}) custom-call(bf16[256,768]{1,0:T(8,128)(2,1)} %copy-done.6, bf16[256,768]{1,0:T(8,128)(2,1)} %copy-done.11, bf16[256,768]{1,0:T(8,128)(2,1)} %copy-done.12, bf16[256,768]{1,0:T(8,128)(2,1)} %copy-done.13, ...), custom_call_target="tpu_custom_call" | custom-call | flops 4227858432 | bytes 16515072 | tf_op jit(solution)/shard_map/weight_product/pallas_call | solution.py:792
  208.3 2.0 fusion.4
  210.3 1.4 pad_maximum_fusion.1
  211.7 1.8 collective-permute-start.17
  213.5 1.9 pad_maximum_fusion
  215.9 1.3 constant_dynamic-slice_fusion
  218.1 2.6 collective-permute-start.21
  220.6 0.9 fusion.7
  223.4 19.5 %collective-permute-done.17 = bf16[256,768]{1,0:T(8,128)(2,1)S(1)} collective-permute-done((bf16[256,768]{1,0:T(8,128)(2,1)}, bf16[256,768]{1,0:T(8,128)(2,1)S(1)}, u32[]{:S(2)}, u32[]{:S(2)}) %collective-permute-start.17) | collective-permute-done | bytes 393248 | tf_op jit(solution)/shard_map/ppermute | solution.py:51
  243.7 1.3 collective-permute-start.22
  245.0 4.2 %token_product.3 = bf16[3,256,768]{2,1,0:T(8,128)(2,1)} custom-call(s32[1]{0:T(128)} %bitcast.9.refs_7_.refs_0_.near_ref, bf16[768,768]{1,0:T(8,128)(2,1)} %get-tuple-element.123.refs_15_.dk_ref, bf16[768,768]{1,0:T(8,128)(2,1)} %get-tuple-element.124.refs_16_.dv_ref, bf16[32,72,768]{2,1,0:T(8,128)(2,1)} %get-tuple-element.104.wk_ref.wv_ref.refs_11_, ...), custom_call_target="tpu_custom_call" | custom-call | flops 1811939328 | bytes 3538944 | tf_op jit(solution)/shard_map/token_product/pallas_call | solution.py:713
  249.2 19.1 %collective-permute-done.22 = bf16[256,768]{1,0:T(8,128)(2,1)} collective-permute-done((bf16[256,768]{1,0:T(8,128)(2,1)}, bf16[256,768]{1,0:T(8,128)(2,1)}, u32[]{:S(2)}, u32[]{:S(2)}) %collective-permute-start.22) | collective-permute-done | bytes 393248 | tf_op jit(solution)/shard_map/ppermute | solution.py:55
  268.4 3.8 %reduce-scatter.6.cloned.1.call-done = bf16[4,216,768]{2,1,0:T(8,128)(2,1)} async-done(((bf16[16,216,768]{2,1,0:T(8,128)(2,1)}), bf16[4,216,768]{2,1,0:T(8,128)(2,1)}) %reduce-scatter.6.cloned.1.call-update) | async-done | bytes 1327120 | tf_op jit(solution)/shard_map/reduce_scatter | solution.py:937
  272.4 1.6 fusion.12
  273.9 1.6 collective-permute-start.25
  275.5 2.4 collective-permute-start.26
  278.5 1.4 collective-permute-start.23
  280.6 10.5 %collective-permute-done.26 = bf16[1,80,768]{2,1,0:T(8,128)(2,1)S(1)} collective-permute-done((bf16[1,80,768]{2,1,0:T(8,128)(2,1)S(1)}, bf16[1,80,768]{2,1,0:T(8,128)(2,1)S(1)}, u32[]{:S(2)}, u32[]{:S(2)}) %collective-permute-start.26) | collective-permute-done | bytes 122912 | tf_op jit(solution)/shard_map/ppermute | solution.py:51
  291.0 1.1 fusion.11
  294.1 2.1 fusion.9
  296.2 20.1 %reduce-scatter.8.cloned.1.call-done = bf16[1,216,768]{2,1,0:T(8,128)(2,1)} async-done(((bf16[4,216,768]{2,1,0:T(8,128)(2,1)}), bf16[1,216,768]{2,1,0:T(8,128)(2,1)}) %reduce-scatter.8.cloned.1.call-update) | async-done | bytes 331792 | tf_op jit(solution)/shard_map/reduce_scatter | solution.py:937
  316.3 1.0 convert_element_type.490
  (131 shorter events, 23.7 us)
Async XLA Ops:
  7.2 123.3 %all-gather.2.cloned.1.call-start = ((), (), s32[]{:S(2)}) async-start(), calls=%async_computation.3 | async-start | bytes 11354112 | tf_op jit(solution)/shard_map/all_gather | solution.py:863
  11.3 174.0 %reduce-scatter.4.cloned.1.call-start = ((), (), s32[]{:S(2)}) async-start(), calls=%async_computation.4 | async-start | bytes 15925248 | tf_op jit(solution)/shard_map/reduce_scatter | solution.py:937
  11.3 28.8 %collective-permute-start = (bf16[80,768]{1,0:T(8,128)(2,1)}, bf16[80,768]{1,0:T(8,128)(2,1)S(1)}, u32[]{:S(2)}, u32[]{:S(2)}) collective-permute-start(bf16[80,768]{1,0:T(8,128)(2,1)} %get-tuple-element.78), channel_id=1, source_target_pairs={{0,2},{1,3},{2,0},{3,1},{4,6},{5,7},{6,4},{7,5},{8,10},{9,11},{10,... | collective-permute-start | bytes 368648 | tf_op jit(solution)/shard_map/ppermute | solution.py:51
  14.4 25.8 %collective-permute-start.1 = (bf16[80,768]{1,0:T(8,128)(2,1)}, bf16[80,768]{1,0:T(8,128)(2,1)S(1)}, u32[]{:S(2)}, u32[]{:S(2)}) collective-permute-start(bf16[80,768]{1,0:T(8,128)(2,1)} %get-tuple-element.78), channel_id=1, source_target_pairs={{0,4},{1,5},{2,6},{3,7},{4,0},{5,1},{6,2},{7,3},{8,12},{9,13},{10,... | collective-permute-start | bytes 368648 | tf_op jit(solution)/shard_map/ppermute | solution.py:51
  17.0 23.2 %collective-permute-start.2 = (bf16[80,768]{1,0:T(8,128)(2,1)}, bf16[80,768]{1,0:T(8,128)(2,1)S(1)}, u32[]{:S(2)}, u32[]{:S(2)}) collective-permute-start(bf16[80,768]{1,0:T(8,128)(2,1)} %get-tuple-element.78), channel_id=1, source_target_pairs={{0,6},{1,7},{2,4},{3,5},{4,2},{5,3},{6,0},{7,1},{8,14},{9,15},{10,... | collective-permute-start | bytes 368648 | tf_op jit(solution)/shard_map/ppermute | solution.py:51
  17.0 21.4 %collective-permute-start.3 = (bf16[256,768]{1,0:T(8,128)(2,1)}, bf16[256,768]{1,0:T(8,128)(2,1)S(1)}, u32[]{:S(2)}, u32[]{:S(2)}) collective-permute-start(bf16[256,768]{1,0:T(8,128)(2,1)} %bitcast.164), channel_id=1, source_target_pairs={{0,4},{1,5},{2,6},{3,7},{8,12},{9,13},{10,14},{11,15},{16,20},{17,... | collective-permute-start | bytes 1179656 | tf_op jit(solution)/shard_map/ppermute | solution.py:55
  20.9 19.4 %collective-permute-start.4 = (bf16[256,768]{1,0:T(8,128)(2,1)}, bf16[256,768]{1,0:T(8,128)(2,1)S(1)}, u32[]{:S(2)}, u32[]{:S(2)}) collective-permute-start(bf16[256,768]{1,0:T(8,128)(2,1)} %bitcast.165), channel_id=1, source_target_pairs={{0,1},{1,0},{2,3},{3,2},{4,5},{5,4},{6,7},{7,6},{8,9},{9,8},{10,11... | collective-permute-start | bytes 1179656 | tf_op jit(solution)/shard_map/ppermute | solution.py:51
  38.4 32.3 %collective-permute-start.9 = (bf16[256,768]{1,0:T(8,128)(2,1)}, bf16[256,768]{1,0:T(8,128)(2,1)S(1)}, u32[]{:S(2)}, u32[]{:S(2)}) collective-permute-start(bf16[256,768]{1,0:T(8,128)(2,1)} %bitcast.166), channel_id=1, source_target_pairs={{5,6},{6,5},{13,14},{14,13},{21,22},{22,21},{29,30},{30,29}} | collective-permute-start | bytes 1179656 | tf_op jit(solution)/shard_map/ppermute | solution.py:55
  40.2 38.1 %copy-start.6 = (bf16[256,768]{1,0:T(8,128)(2,1)}, bf16[256,768]{1,0:T(8,128)(2,1)S(1)}, u32[]{:S(2)}) copy-start(bf16[256,768]{1,0:T(8,128)(2,1)S(1)} %broadcast_select_fusion.refs_0_) | copy-start | bytes 1179652
  40.2 38.1 %copy-start.9 = (bf16[256,768]{1,0:T(8,128)(2,1)}, bf16[256,768]{1,0:T(8,128)(2,1)S(1)}, u32[]{:S(2)}) copy-start(bf16[256,768]{1,0:T(8,128)(2,1)S(1)} %collective-permute-done.4.refs_5_) | copy-start | bytes 1179652
  40.2 35.0 %collective-permute-start.7 = (bf16[256,768]{1,0:T(8,128)(2,1)S(1)}, bf16[256,768]{1,0:T(8,128)(2,1)S(1)}, u32[]{:S(2)}, u32[]{:S(2)}) collective-permute-start(bf16[256,768]{1,0:T(8,128)(2,1)S(1)} %broadcast_select_fusion.refs_0_), channel_id=1, source_target_pairs={{0,2},{1,3},{2,0},{3,1},{4,6},{5,7},{6,4},{7,5},{8,10},{9,11},{10,... | collective-permute-start | bytes 1179656 | tf_op jit(solution)/shard_map/ppermute | solution.py:51
  56.9 18.4 %collective-permute-start.8 = (bf16[256,768]{1,0:T(8,128)(2,1)S(1)}, bf16[256,768]{1,0:T(8,128)(2,1)S(1)}, u32[]{:S(2)}, u32[]{:S(2)}) collective-permute-start(bf16[256,768]{1,0:T(8,128)(2,1)S(1)} %broadcast_select_fusion.refs_0_), channel_id=1, source_target_pairs={{0,1},{1,0},{2,3},{3,2},{4,5},{5,4},{6,7},{7,6},{8,9},{9,8},{10,11... | collective-permute-start | bytes 1179656 | tf_op jit(solution)/shard_map/ppermute | solution.py:51
  57.7 13.0 %collective-permute-start.6 = (bf16[4,40,768]{2,1,0:T(8,128)(2,1)S(1)}, bf16[4,40,768]{2,1,0:T(8,128)(2,1)S(1)}, u32[]{:S(2)}, u32[]{:S(2)}) collective-permute-start(bf16[4,40,768]{2,1,0:T(8,128)(2,1)S(1)} %pad_maximum_fusion.5), channel_id=1, source_target_pairs={{0,1},{1,0},{2,3},{3,2},{4,5},{5,4},{6,7},{7,6},{8,9},{9,8},{10,11... | collective-permute-start | bytes 737288 | tf_op jit(solution)/shard_map/ppermute | solution.py:51
  59.1 11.6 %collective-permute-start.5 = (bf16[4,40,768]{2,1,0:T(8,128)(2,1)S(1)}, bf16[4,40,768]{2,1,0:T(8,128)(2,1)S(1)}, u32[]{:S(2)}, u32[]{:S(2)}) collective-permute-start(bf16[4,40,768]{2,1,0:T(8,128)(2,1)S(1)} %pad_maximum_fusion.4), channel_id=1, source_target_pairs={{0,16},{1,17},{2,18},{3,19},{4,20},{5,21},{6,22},{7,23},{8,24},{9,... | collective-permute-start | bytes 737288 | tf_op jit(solution)/shard_map/ppermute | solution.py:51
  70.7 31.3 %copy-start.14 = (s32[1,8]{1,0:T(1,128)S(1)}, s32[1,8]{1,0:T(1,128)}, u32[]{:S(2)}) copy-start(s32[1,8]{1,0:T(1,128)} %param.19) | copy-start | bytes 100
  70.8 24.9 %copy-start.10 = (bf16[256,768]{1,0:T(8,128)(2,1)}, bf16[256,768]{1,0:T(8,128)(2,1)S(1)}, u32[]{:S(2)}) copy-start(bf16[256,768]{1,0:T(8,128)(2,1)S(1)} %collective-permute-done.9.refs_6_) | copy-start | bytes 1179652
  75.3 3.0 copy-start.11
  75.3 20.4 %copy-start.12 = (bf16[256,768]{1,0:T(8,128)(2,1)}, bf16[256,768]{1,0:T(8,128)(2,1)S(1)}, u32[]{:S(2)}) copy-start(bf16[256,768]{1,0:T(8,128)(2,1)S(1)} %collective-permute-done.8.refs_2_) | copy-start | bytes 1179652
  75.3 17.7 %collective-permute-start.13 = (bf16[8,40,768]{2,1,0:T(8,128)(2,1)S(1)}, bf16[8,40,768]{2,1,0:T(8,128)(2,1)S(1)}, u32[]{:S(2)}, u32[]{:S(2)}) collective-permute-start(bf16[8,40,768]{2,1,0:T(8,128)(2,1)S(1)} %constant_dynamic-update-slice_fusion.5), channel_id=1, source_target_pairs={{0,16},{1,17},{2,18},{3,19},{4,20},{5,21},{6,22},{7,23},{8,24},{9,... | collective-permute-start | bytes 1474568 | tf_op jit(solution)/shard_map/ppermute | solution.py:51
  76.8 18.8 %collective-permute-start.10 = (bf16[8,40,768]{2,1,0:T(8,128)(2,1)S(1)}, bf16[8,40,768]{2,1,0:T(8,128)(2,1)S(1)}, u32[]{:S(2)}, u32[]{:S(2)}) collective-permute-start(bf16[8,40,768]{2,1,0:T(8,128)(2,1)S(1)} %constant_dynamic-update-slice_fusion), channel_id=1, source_target_pairs={{0,1},{1,0},{2,3},{3,2},{4,5},{5,4},{6,7},{7,6},{8,9},{9,8},{10,11... | collective-permute-start | bytes 1474568 | tf_op jit(solution)/shard_map/ppermute | solution.py:51
  78.3 23.0 %collective-permute-start.11 = (bf16[256,768]{1,0:T(8,128)(2,1)S(1)}, bf16[256,768]{1,0:T(8,128)(2,1)S(1)}, u32[]{:S(2)}, u32[]{:S(2)}) collective-permute-start(bf16[256,768]{1,0:T(8,128)(2,1)S(1)} %collective-permute-done.8.refs_2_), channel_id=1, source_target_pairs={{0,2},{1,3},{2,0},{3,1},{4,6},{5,7},{6,4},{7,5},{8,10},{9,11},{10,... | collective-permute-start | bytes 1179656 | tf_op jit(solution)/shard_map/ppermute | solution.py:51
  93.0 11.7 %copy-start.7 = (bf16[16,40,768]{2,1,0:T(8,128)(2,1)}, bf16[16,40,768]{2,1,0:T(8,128)(2,1)S(1)}, u32[]{:S(2)}) copy-start(bf16[16,40,768]{2,1,0:T(8,128)(2,1)S(1)} %constant_dynamic-update-slice_fusion.10.refs_12_) | copy-start | bytes 2949124
  93.0 10.9 %collective-permute-start.14 = (bf16[16,40,768]{2,1,0:T(8,128)(2,1)S(1)}, bf16[16,40,768]{2,1,0:T(8,128)(2,1)}, u32[]{:S(2)}, u32[]{:S(2)}) collective-permute-start(bf16[16,40,768]{2,1,0:T(8,128)(2,1)S(1)} %constant_dynamic-update-slice_fusion.10.refs_12_), channel_id=1, source_target_pairs={{0,8},{1,9},{2,10},{3,11},{4,12},{5,13},{6,14},{7,15},{8,0},{9,1},... | collective-permute-start | bytes 2949128 | tf_op jit(solution)/shard_map/ppermute | solution.py:51
  95.7 9.1 %copy-start.4 = (bf16[16,40,768]{2,1,0:T(8,128)(2,1)}, bf16[16,40,768]{2,1,0:T(8,128)(2,1)S(1)}, u32[]{:S(2)}) copy-start(bf16[16,40,768]{2,1,0:T(8,128)(2,1)S(1)} %pad_maximum_fusion.2.refs_10_) | copy-start | bytes 2949124
  101.3 0.8 copy-start.13
  102.1 2.7 collective-permute-start.12
  153.5 118.6 %reduce-scatter.6.cloned.1.call-start = ((), (), s32[]{:S(2)}) async-start(), calls=%async_computation.5 | async-start | bytes 6635520 | tf_op jit(solution)/shard_map/reduce_scatter | solution.py:937
  185.3 0.7 copy-start.8
  185.3 1.6 copy-start
  185.3 131.0 %reduce-scatter.8.cloned.1.call-start = ((), (), s32[]{:S(2)}) async-start(), calls=%async_computation.6 | async-start | bytes 1658880 | tf_op jit(solution)/shard_map/reduce_scatter | solution.py:937
  187.7 20.6 %collective-permute-start.15 = (bf16[256,768]{1,0:T(8,128)(2,1)}, bf16[256,768]{1,0:T(8,128)(2,1)S(1)}, u32[]{:S(2)}, u32[]{:S(2)}) collective-permute-start(bf16[256,768]{1,0:T(8,128)(2,1)} %get-tuple-element.153), channel_id=1, source_target_pairs={{0,2},{1,3},{2,0},{3,1},{4,6},{5,7},{6,4},{7,5},{8,10},{9,11},{10,... | collective-permute-start | bytes 1179656 | tf_op jit(solution)/shard_map/ppermute | solution.py:51
  189.5 18.8 %collective-permute-start.16 = (bf16[256,768]{1,0:T(8,128)(2,1)S(1)}, bf16[256,768]{1,0:T(8,128)(2,1)}, u32[]{:S(2)}, u32[]{:S(2)}) collective-permute-start(bf16[256,768]{1,0:T(8,128)(2,1)S(1)} %get-tuple-element.152), channel_id=1, source_target_pairs={{0,2},{1,3},{2,0},{3,1},{4,6},{5,7},{6,4},{7,5},{8,10},{9,11},{10,... | collective-permute-start | bytes 1179656 | tf_op jit(solution)/shard_map/ppermute | solution.py:51
  208.1 2.2 copy-start.3
  211.7 4.2 %collective-permute-start.18 = (bf16[16,80,768]{2,1,0:T(8,128)(2,1)}, bf16[16,80,768]{2,1,0:T(8,128)(2,1)S(1)}, u32[]{:S(2)}, u32[]{:S(2)}) collective-permute-start(bf16[16,80,768]{2,1,0:T(8,128)(2,1)} %pad_maximum_fusion.1), channel_id=1, source_target_pairs={{0,8},{1,9},{2,10},{3,11},{4,12},{5,13},{6,14},{7,15},{8,0},{9,1},... | collective-permute-start | bytes 5898248 | tf_op jit(solution)/shard_map/ppermute | solution.py:51
  211.7 31.1 %collective-permute-start.17 = (bf16[256,768]{1,0:T(8,128)(2,1)}, bf16[256,768]{1,0:T(8,128)(2,1)S(1)}, u32[]{:S(2)}, u32[]{:S(2)}) collective-permute-start(bf16[256,768]{1,0:T(8,128)(2,1)} %get-tuple-element.116), channel_id=1, source_target_pairs={{0,1},{1,0},{2,3},{3,2},{4,5},{5,4},{6,7},{7,6},{8,9},{9,8},{10,11... | collective-permute-start | bytes 1179656 | tf_op jit(solution)/shard_map/ppermute | solution.py:51
  218.1 50.3 %collective-permute-start.21 = (bf16[4,80,768]{2,1,0:T(8,128)(2,1)}, bf16[4,80,768]{2,1,0:T(8,128)(2,1)}, u32[]{:S(2)}, u32[]{:S(2)}) collective-permute-start(bf16[4,80,768]{2,1,0:T(8,128)(2,1)} %fusion.8), channel_id=1, source_target_pairs={{0,17},{1,16},{2,19},{3,18},{4,21},{5,20},{6,23},{7,22},{8,25},{9,... | collective-permute-start | bytes 1474568 | tf_op jit(solution)/shard_map/ppermute | solution.py:51
  221.6 46.8 %collective-permute-start.20 = (bf16[4,80,768]{2,1,0:T(8,128)(2,1)}, bf16[4,80,768]{2,1,0:T(8,128)(2,1)}, u32[]{:S(2)}, u32[]{:S(2)}) collective-permute-start(bf16[4,80,768]{2,1,0:T(8,128)(2,1)} %fusion.7), channel_id=1, source_target_pairs={{0,1},{1,0},{2,3},{3,2},{4,5},{5,4},{6,7},{7,6},{8,9},{9,8},{10,11... | collective-permute-start | bytes 1474568 | tf_op jit(solution)/shard_map/ppermute | solution.py:51
  223.1 45.2 %collective-permute-start.19 = (bf16[4,80,768]{2,1,0:T(8,128)(2,1)}, bf16[4,80,768]{2,1,0:T(8,128)(2,1)}, u32[]{:S(2)}, u32[]{:S(2)}) collective-permute-start(bf16[4,80,768]{2,1,0:T(8,128)(2,1)} %fusion.6), channel_id=1, source_target_pairs={{0,16},{1,17},{2,18},{3,19},{4,20},{5,21},{6,22},{7,23},{8,24},{9,... | collective-permute-start | bytes 1474568 | tf_op jit(solution)/shard_map/ppermute | solution.py:51
  243.7 24.7 %collective-permute-start.22 = (bf16[256,768]{1,0:T(8,128)(2,1)}, bf16[256,768]{1,0:T(8,128)(2,1)}, u32[]{:S(2)}, u32[]{:S(2)}) collective-permute-start(bf16[256,768]{1,0:T(8,128)(2,1)} %fusion.5), channel_id=1, source_target_pairs={{4,0},{5,1},{6,2},{7,3},{12,8},{13,9},{14,10},{15,11},{20,16},{21,... | collective-permute-start | bytes 1179656 | tf_op jit(solution)/shard_map/ppermute | solution.py:55
  245.0 4.2 %copy-start.2 = (bf16[1,1,640,768]{3,2,1,0:T(8,128)(2,1)S(1)}, bf16[1,1,640,768]{3,2,1,0:T(8,128)(2,1)}, u32[]{:S(2)}) copy-start(bf16[1,1,640,768]{3,2,1,0:T(8,128)(2,1)} %get-tuple-element.149) | copy-start | bytes 2949124
  249.2 29.2 %copy-start.1 = (bf16[3,256,768]{2,1,0:T(8,128)(2,1)S(1)}, bf16[3,256,768]{2,1,0:T(8,128)(2,1)}, u32[]{:S(2)}) copy-start(bf16[3,256,768]{2,1,0:T(8,128)(2,1)} %token_product.3) | copy-start | bytes 3538948
  273.9 20.1 %copy-start.5 = (f32[256,768]{1,0:T(8,128)S(1)}, f32[256,768]{1,0:T(8,128)}, u32[]{:S(2)}) copy-start(f32[256,768]{1,0:T(8,128)} %get-tuple-element.111) | copy-start | bytes 2359300
  273.9 6.6 %collective-permute-start.25 = (bf16[1,80,768]{2,1,0:T(8,128)(2,1)S(1)}, bf16[1,80,768]{2,1,0:T(8,128)(2,1)S(1)}, u32[]{:S(2)}, u32[]{:S(2)}) collective-permute-start(bf16[1,80,768]{2,1,0:T(8,128)(2,1)S(1)} %get-tuple-element.139), channel_id=1, source_target_pairs={{0,2},{1,3},{2,0},{3,1},{4,6},{5,7},{6,4},{7,5},{8,10},{9,11},{10,... | collective-permute-start | bytes 368648 | tf_op jit(solution)/shard_map/ppermute | solution.py:51
  275.5 15.5 %collective-permute-start.26 = (bf16[1,80,768]{2,1,0:T(8,128)(2,1)S(1)}, bf16[1,80,768]{2,1,0:T(8,128)(2,1)S(1)}, u32[]{:S(2)}, u32[]{:S(2)}) collective-permute-start(bf16[1,80,768]{2,1,0:T(8,128)(2,1)S(1)} %get-tuple-element.141), channel_id=1, source_target_pairs={{0,4},{1,5},{2,6},{3,7},{4,0},{5,1},{6,2},{7,3},{8,12},{9,13},{10,... | collective-permute-start | bytes 368648 | tf_op jit(solution)/shard_map/ppermute | solution.py:51
  277.9 13.1 %collective-permute-start.27 = (bf16[1,80,768]{2,1,0:T(8,128)(2,1)S(1)}, bf16[1,80,768]{2,1,0:T(8,128)(2,1)S(1)}, u32[]{:S(2)}, u32[]{:S(2)}) collective-permute-start(bf16[1,80,768]{2,1,0:T(8,128)(2,1)S(1)} %get-tuple-element.140), channel_id=1, source_target_pairs={{0,6},{1,7},{2,4},{3,5},{4,2},{5,3},{6,0},{7,1},{8,14},{9,15},{10,... | collective-permute-start | bytes 368648 | tf_op jit(solution)/shard_map/ppermute | solution.py:51
  278.5 15.6 %collective-permute-start.23 = (bf16[256,768]{1,0:T(8,128)(2,1)S(1)}, bf16[256,768]{1,0:T(8,128)(2,1)S(1)}, u32[]{:S(2)}, u32[]{:S(2)}) collective-permute-start(bf16[256,768]{1,0:T(8,128)(2,1)S(1)} %get-tuple-element.154), channel_id=1, source_target_pairs={{0,1},{1,0},{2,3},{3,2},{4,5},{5,4},{6,7},{7,6},{8,9},{9,8},{10,11... | collective-permute-start | bytes 1179656 | tf_op jit(solution)/shard_map/ppermute | solution.py:51
  279.8 14.2 %collective-permute-start.24 = (bf16[256,768]{1,0:T(8,128)(2,1)S(1)}, bf16[256,768]{1,0:T(8,128)(2,1)S(1)}, u32[]{:S(2)}, u32[]{:S(2)}) collective-permute-start(bf16[256,768]{1,0:T(8,128)(2,1)S(1)} %get-tuple-element.155), channel_id=1, source_target_pairs={{5,6},{6,5},{13,14},{14,13},{21,22},{22,21},{29,30},{30,29}} | collective-permute-start | bytes 1179656 | tf_op jit(solution)/shard_map/ppermute | solution.py:55
Sparse Core Ops, SparseCore 0:
  11.5 118.9 all-gather.1
  153.7 31.5 reduce-scatter.3
  188.5 83.5 reduce-scatter.5
  274.5 41.7 reduce-scatter.7
